TPU v7x, 32 devices: a whole 2x2x4 slice. The times are simulated.
32 devices in a mesh: groups: 2 (over y), chan: 4 (over z), space: 4 (over x, core).
Axes of the slice: x: 2, y: 2, z: 4, core: 2. Of those that a mesh axis runs over, the one named last changes fastest.
Arguments:
- volume: bfloat16 [2048, 16, 512], P(('groups', 'chan'), 'space'), parts along dimension 0, may hold values from -6 to 6
- out_grad: bfloat16 [2048, 16, 512], P(('groups', 'chan'), 'space'), parts along dimension 0, may hold values from -6 to 6
- weight_in: bfloat16 [1024, 1024], P('chan'), may hold values from -0.1875 to 0.1875
- weight_out: bfloat16 [1024, 1024], P('chan'), may hold values from -0.1875 to 0.1875
- filter_taps: float32 [1024, 27], P('chan'), may hold values from -1.25 to 1.25
- filter_bias: float32 [1024], P('chan'), may hold values from -3 to 3
Outputs:
- block_out: bfloat16 [2048, 16, 512], P(('groups', 'chan'), 'space'), parts along dimension 0
- volume_grad: bfloat16 [2048, 16, 512], P(('groups', 'chan'), 'space'), parts along dimension 0
There are 2 independent parts, one for each index of `groups`. A program takes and returns all parts, laid end to end along the dimension named above; an argument that names none is the same for every part. Nothing has to cross between parts.
All inputs are finite; a program needn't handle non-finite values.
Results may differ from a plain program's by a relative error of at most 0.0085.
Values may be sent and summed in bfloat16 or wider, within the bound.
No kernel may reach another device: no remote copies, remote signals or barrier semaphores. Data moves between devices by JAX's collectives and lax.ppermute only.
A program may use at most 64 MiB of HBM per device.

v0:
```python
import jax
import jax.numpy as jnp
from jax import lax
from jax.sharding import PartitionSpec as P

CX = 32
CY = 16


root_half = 0.7071067811865476
inv_root_two_pi = 0.3989422804014327


def with_halo(block, sides, width):
    for axis, dim in sides:
        count = lax.axis_size(axis)
        forward = [(i, i + 1) for i in range(count - 1)]
        backward = [(target, source) for source, target in forward]
        low = lax.ppermute(
            lax.slice_in_dim(block, block.shape[dim] - width, None, axis=dim), axis, forward
        )
        high = lax.ppermute(lax.slice_in_dim(block, 0, width, axis=dim), axis, backward)
        block = jnp.concatenate([low, block, high], axis=dim)
    return block


def gelu_value(field):
    return 0.5 * field * (1.0 + lax.erf(field * root_half))


def gelu_slope(field):
    return (
        0.5 * (1.0 + lax.erf(field * root_half))
        + field * jnp.exp(-0.5 * field * field) * inv_root_two_pi
    )


def core(padded, filter_taps, direction):
    extent_z = padded.shape[1] - 2
    extent_y = padded.shape[2] - 2
    extent_x = padded.shape[3] - 2
    summed = jnp.zeros((padded.shape[0], extent_z, extent_y, extent_x), jnp.float32)
    for shift_z in range(3):
        for shift_y in range(3):
            for shift_x in range(3):
                tap_index = (shift_z * 3 + shift_y) * 3 + shift_x
                begin_z = 1 + direction * (shift_z - 1)
                begin_y = 1 + direction * (shift_y - 1)
                begin_x = 1 + direction * (shift_x - 1)
                window = padded[
                    :,
                    begin_z : begin_z + extent_z,
                    begin_y : begin_y + extent_y,
                    begin_x : begin_x + extent_x,
                ]
                summed = summed + filter_taps[:, tap_index][:, None, None, None] * window
    return summed


def lift(field_z):
    extended = field_z.astype(jnp.float32).reshape(field_z.shape[0], field_z.shape[1], CY, CX)
    return jnp.pad(extended, ((0, 0), (0, 0), (1, 1), (1, 1)))


def to_cells(field):
    return lax.all_to_all(
        field.reshape(field.shape[0], -1), "chan", split_axis=1, concat_axis=0, tiled=True
    )


def to_channels(field, slab_shape):
    return lax.all_to_all(field, "chan", split_axis=0, concat_axis=1, tiled=True).reshape(
        slab_shape
    )


def body(volume, out_grad, weight_in, weight_out, filter_taps, filter_bias):
    slab_shape = volume.shape
    contract_first = (((0,), (0,)), ((), ()))
    full_in, full_out = (
        lax.all_gather(weight_in, "chan", axis=0, tiled=True),
        lax.all_gather(weight_out, "chan", axis=0, tiled=True),
    )
    vol_cells = to_cells(volume)
    hidden = to_channels(
        jnp.dot(full_in, vol_cells, preferred_element_type=jnp.float32).astype(jnp.bfloat16),
        slab_shape,
    )
    padded = lift(with_halo(hidden, (("space", 1),), 1))
    mixed = core(padded, filter_taps, 1) + filter_bias[:, None, None, None]
    active = gelu_value(mixed).astype(jnp.bfloat16).reshape(slab_shape)
    act_cells = to_cells(active)
    out_cells = vol_cells.astype(jnp.float32) + jnp.dot(
        full_out, act_cells, preferred_element_type=jnp.float32
    )
    block_out = to_channels(out_cells.astype(jnp.bfloat16), slab_shape)
    grad_cells = to_cells(out_grad)
    act_part = lax.dot_general(
        full_out, grad_cells, contract_first, preferred_element_type=jnp.float32
    )
    act_grad = to_channels(act_part.astype(jnp.bfloat16), slab_shape)
    slope = gelu_slope(mixed)
    mix_grad = (
        (act_grad.astype(jnp.float32).reshape(slope.shape) * slope)
        .astype(jnp.bfloat16)
        .reshape(slab_shape)
    )
    padded_grad = lift(with_halo(mix_grad, (("space", 1),), 1))
    hid_grad = core(padded_grad, filter_taps, -1).astype(jnp.bfloat16).reshape(slab_shape)
    hid_cells = to_cells(hid_grad)
    back_part = lax.dot_general(
        full_in, hid_cells, contract_first, preferred_element_type=jnp.float32
    )
    volume_grad = to_channels(
        (grad_cells.astype(jnp.float32) + back_part).astype(jnp.bfloat16), slab_shape
    )
    return (block_out, volume_grad)


def solution(mesh):
    placed = (
        P(("groups", "chan"), "space", None),
        P(("groups", "chan"), "space", None),
        P("chan", None),
        P("chan", None),
        P("chan", None),
        P("chan"),
    )
    return jax.shard_map(
        body,
        mesh=mesh,
        in_specs=placed,
        out_specs=(P(("groups", "chan"), "space", None), P(("groups", "chan"), "space", None)),
        check_vma=False,
    )
```

profile of v0, /device:TPU:0, one launch (start us, length us, event | category | flops | bytes accessed | tf_op | source)
XLA Modules:
  0.0 338.6 jit_solution(1226160043802990815)
XLA Ops:
  7.2 0.0 all-gather.3.cloned.1.call-start
  7.2 0.7 all-gather.3.cloned.1.call-update
  7.9 0.0 copy-start.2
  7.9 2.5 copy.26
  10.4 6.3 %all-to-all-start = ((bf16[256,4,512]{2,0,1:T(8,128)(2,1)}), bf16[256,4,512]{2,0,1:T(8,128)(2,1)S(1)}, u32[]{:S(2)}, u32[]{:S(2)}) async-start(bf16[256,4,512]{2,0,1:T(8,128)(2,1)} %copy.26), calls=%async_computation | async-start | bytes 2097152 | tf_op jit(solution)/shard_map/all_to_all | solution.py:66
  16.7 0.0 all-gather.5.cloned.1.call-start
  16.7 0.7 all-gather.5.cloned.1.call-update
  17.5 0.0 copy-done.2
  17.5 1.2 copy.31
  18.6 49.2 %all-to-all-done = bf16[256,4,512]{2,0,1:T(8,128)(2,1)S(1)} async-done(((bf16[256,4,512]{2,0,1:T(8,128)(2,1)}), bf16[256,4,512]{2,0,1:T(8,128)(2,1)S(1)}, u32[]{:S(2)}, u32[]{:S(2)}) %all-to-all-start) | async-done | bytes 1048608 | tf_op jit(solution)/shard_map/all_to_all | solution.py:66
  67.8 0.0 copy-start
  67.8 3.5 %all-to-all-start.4 = ((bf16[256,4,512]{2,0,1:T(8,128)(2,1)}), bf16[256,4,512]{2,0,1:T(8,128)(2,1)S(1)}, u32[]{:S(2)}, u32[]{:S(2)}) async-start(bf16[256,4,512]{2,0,1:T(8,128)(2,1)} %copy.31), calls=%async_computation.4 | async-start | bytes 2097152 | tf_op jit(solution)/shard_map/all_to_all | solution.py:66
  71.3 15.1 %all-gather.3.cloned.1.call-done = bf16[1024,1024]{1,0:T(8,128)(2,1)} async-done(((bf16[256,1024]{1,0:T(8,128)(2,1)}), bf16[1024,1024]{1,0:T(8,128)(2,1)}) %all-gather.3.cloned.1.call-update) | async-done | bytes 2097168 | tf_op jit(solution)/shard_map/all_gather | solution.py:81
  86.5 2.8 convolution_convert_fusion.1
  89.3 0.0 copy-done
  89.3 1.3 copy.28
  90.7 8.0 %all-to-all-done.4 = bf16[256,4,512]{2,0,1:T(8,128)(2,1)S(1)} async-done(((bf16[256,4,512]{2,0,1:T(8,128)(2,1)}), bf16[256,4,512]{2,0,1:T(8,128)(2,1)S(1)}, u32[]{:S(2)}, u32[]{:S(2)}) %all-to-all-start.4) | async-done | bytes 1048608 | tf_op jit(solution)/shard_map/all_to_all | solution.py:66
  98.7 3.5 %all-to-all-start.1 = ((bf16[4,256,512]{1,2,0:T(8,128)(2,1)}), bf16[4,256,512]{1,2,0:T(8,128)(2,1)S(1)}, u32[]{:S(2)}, u32[]{:S(2)}) async-start(bf16[4,256,512]{1,2,0:T(8,128)(2,1)} %copy.28), calls=%async_computation.1 | async-start | bytes 2097152 | tf_op jit(solution)/shard_map/all_to_all | solution.py:72
  102.3 58.4 %all-gather.5.cloned.1.call-done = bf16[1024,1024]{1,0:T(8,128)(2,1)} async-done(((bf16[256,1024]{1,0:T(8,128)(2,1)}), bf16[1024,1024]{1,0:T(8,128)(2,1)}) %all-gather.5.cloned.1.call-update) | async-done | bytes 2097168 | tf_op jit(solution)/shard_map/all_gather | solution.py:82
  160.6 2.9 convolution_convert_fusion
  163.5 1.3 copy.33
  164.8 0.0 copy-start.4
  164.8 0.0 all-to-all-done.1
  164.8 3.6 %all-to-all-start.5 = ((bf16[4,256,512]{1,2,0:T(8,128)(2,1)}), bf16[4,256,512]{1,2,0:T(8,128)(2,1)S(1)}, u32[]{:S(2)}, u32[]{:S(2)}) async-start(bf16[4,256,512]{1,2,0:T(8,128)(2,1)} %copy.33), calls=%async_computation.5 | async-start | bytes 2097152 | tf_op jit(solution)/shard_map/all_to_all | solution.py:72
  168.5 0.8 fusion.112
  169.3 1.6 collective-permute-start
  170.9 1.3 collective-permute-start.1
  172.2 0.0 copy-done.4
  172.3 22.0 %all-to-all-done.5 = bf16[4,256,512]{1,2,0:T(8,128)(2,1)S(1)} async-done(((bf16[4,256,512]{1,2,0:T(8,128)(2,1)}), bf16[4,256,512]{1,2,0:T(8,128)(2,1)S(1)}, u32[]{:S(2)}, u32[]{:S(2)}) %all-to-all-start.5) | async-done | bytes 1048608 | tf_op jit(solution)/shard_map/all_to_all | solution.py:72
  194.3 0.2 convert_element_type.63
  194.5 0.0 collective-permute-done
  194.5 0.0 collective-permute-done.1
  194.5 0.0 copy-start.5
  194.5 1.2 maximum_convert_fusion
  195.7 0.0 copy-done.5
  195.7 10.0 %fusion.5 = (bf16[256,4,16,32]{0,3,2,1:T(8,128)(2,1)S(1)}, f32[256,4,16,32]{0,3,2,1:T(8,128)S(1)}) fusion(f32[256,4,16,32]{0,3,2,1:T(8,128)S(1)} %bitcast.72, f32[256]{0:T(256)S(1)} %copy-done.5, f32[256]{0:T(256)S(1)} %bitcast.102, f32[256]{0:T(256)S(1)} %bitcast.104, f32[256]{0:T(256)S(1)} %bitcast.108, f32[256]{0:T(256)S(1)} %bitcast.110, ...), kind=kLoop, calls=%fused_computation.54 | loop fusion | flops 33554432 | bytes 14708736 | tf_op jit(solution)/shard_map/convert_element_type | solution.py:105
  205.8 0.8 fusion.111
  206.6 1.3 collective-permute-start.2
  207.9 1.3 collective-permute-start.3
  209.2 1.4 multiply_convert_fusion
  210.6 3.5 %all-to-all-start.2 = ((bf16[256,4,512]{0,2,1:T(8,128)(2,1)}), bf16[256,4,512]{0,2,1:T(8,128)(2,1)S(1)}, u32[]{:S(2)}, u32[]{:S(2)}) async-start(bf16[256,4,512]{0,2,1:T(8,128)(2,1)} %bitcast.35), calls=%async_computation.2 | async-start | bytes 2097152 | tf_op jit(solution)/shard_map/all_to_all | solution.py:66
  214.1 0.0 collective-permute-done.2
  214.1 0.0 collective-permute-done.3
  214.1 1.2 maximum_convert_fusion.1
  215.3 10.0 %fusion.104 = bf16[256,4,16,32]{0,3,2,1:T(8,128)(2,1)} fusion(f32[256,6,16,32]{0,3,2,1:T(8,128)S(1)} %maximum_convert_fusion.1, f32[256]{0:T(256)S(1)} %bitcast.103, f32[256]{0:T(256)S(1)} %bitcast.105, f32[256]{0:T(256)S(1)} %bitcast.109, f32[256]{0:T(256)S(1)} %bitcast.111, f32[256]{0:T(256)S(1)} %bitcast.113, f32[256]{0:T(256)S(1)} %bitcast.115, ...), kind=kLoop, calls=%fused_computation.153 | loop fusion | flops 28311552 | bytes 10513408 | tf_op jit(solution)/shard_map/convert_element_type | solution.py:109
  225.4 14.8 %all-to-all-done.2 = bf16[256,4,512]{0,2,1:T(8,128)(2,1)S(1)} async-done(((bf16[256,4,512]{0,2,1:T(8,128)(2,1)}), bf16[256,4,512]{0,2,1:T(8,128)(2,1)S(1)}, u32[]{:S(2)}, u32[]{:S(2)}) %all-to-all-start.2) | async-done | bytes 1048608 | tf_op jit(solution)/shard_map/all_to_all | solution.py:66
  240.2 4.3 %all-to-all-start.6 = ((bf16[256,4,512]{0,2,1:T(8,128)(2,1)}), bf16[256,4,512]{0,2,1:T(8,128)(2,1)}, u32[]{:S(2)}, u32[]{:S(2)}) async-start(bf16[256,4,512]{0,2,1:T(8,128)(2,1)} %bitcast.83), calls=%async_computation.6 | async-start | bytes 2097152 | tf_op jit(solution)/shard_map/all_to_all | solution.py:66
  244.5 0.0 copy-done.1
  244.5 1.3 copy.38
  245.8 1.3 copy.29
  247.1 0.0 copy-done.3
  247.1 3.2 fusion.109
  250.3 1.3 copy.39
  251.7 19.9 %all-to-all-done.6 = bf16[256,4,512]{0,2,1:T(8,128)(2,1)} async-done(((bf16[256,4,512]{0,2,1:T(8,128)(2,1)}), bf16[256,4,512]{0,2,1:T(8,128)(2,1)}, u32[]{:S(2)}, u32[]{:S(2)}) %all-to-all-start.6) | async-done | bytes 1048608 | tf_op jit(solution)/shard_map/all_to_all | solution.py:66
  271.5 3.7 %all-to-all-start.3 = ((bf16[4,256,512]{2,1,0:T(8,128)(2,1)}), bf16[4,256,512]{2,1,0:T(8,128)(2,1)S(1)}, u32[]{:S(2)}, u32[]{:S(2)}) async-start(bf16[4,256,512]{2,1,0:T(8,128)(2,1)} %bitcast.39), calls=%async_computation.3 | async-start | bytes 2097152 | tf_op jit(solution)/shard_map/all_to_all | solution.py:72
  275.2 0.5 copy.40
  275.8 1.5 copy.34
  277.3 3.8 %fusion.108 = bf16[1024,512]{0,1:T(8,128)(2,1)} fusion(bf16[1024,512]{0,1:T(8,128)(2,1)S(1)} %copy.40, bf16[1024,512]{1,0:T(8,128)(2,1)S(1)} %bitcast.85, bf16[1024,1024]{1,0:T(8,128)(2,1)} %all-gather.3.cloned.1.call-done), kind=kOutput, calls=%fused_computation.164 | convolution fusion | flops 1075314688 | bytes 5242880 | tf_op jit(solution)/shard_map/dot_general | solution.py:111
  281.1 2.3 copy.41
  283.4 17.8 %all-to-all-done.3 = bf16[4,256,512]{2,1,0:T(8,128)(2,1)S(1)} async-done(((bf16[4,256,512]{2,1,0:T(8,128)(2,1)}), bf16[4,256,512]{2,1,0:T(8,128)(2,1)S(1)}, u32[]{:S(2)}, u32[]{:S(2)}) %all-to-all-start.3) | async-done | bytes 1048608 | tf_op jit(solution)/shard_map/all_to_all | solution.py:72
  301.2 3.5 %all-to-all-start.7 = ((bf16[4,256,512]{2,1,0:T(8,128)(2,1)}), bf16[4,256,512]{2,1,0:T(8,128)(2,1)S(1)}, u32[]{:S(2)}, u32[]{:S(2)}) async-start(bf16[4,256,512]{2,1,0:T(8,128)(2,1)} %bitcast.54), calls=%async_computation.7 | async-start | bytes 2097152 | tf_op jit(solution)/shard_map/all_to_all | solution.py:72
  304.7 1.8 copy.36
  306.5 23.5 %all-to-all-done.7 = bf16[4,256,512]{2,1,0:T(8,128)(2,1)S(1)} async-done(((bf16[4,256,512]{2,1,0:T(8,128)(2,1)}), bf16[4,256,512]{2,1,0:T(8,128)(2,1)S(1)}, u32[]{:S(2)}, u32[]{:S(2)}) %all-to-all-start.7) | async-done | bytes 1048608 | tf_op jit(solution)/shard_map/all_to_all | solution.py:72
  329.9 1.8 copy.37
  (4 shorter events, 0.0 us)
Async XLA Ops:
  7.2 79.3 %all-gather.3.cloned.1.call-start = ((), (), s32[]{:S(2)}) async-start(), calls=%async_computation.8 | async-start | bytes 2621440 | tf_op jit(solution)/shard_map/all_gather | solution.py:81
  7.9 9.6 %copy-start.2 = (bf16[256,4,512]{2,1,0:T(4,128)(2,1)S(1)}, bf16[256,4,512]{2,1,0:T(4,128)(2,1)}, u32[]{:S(2)}) copy-start(bf16[256,4,512]{2,1,0:T(4,128)(2,1)} %param.7) | copy-start | bytes 3145732
  10.4 57.4 %all-to-all-start = ((bf16[256,4,512]{2,0,1:T(8,128)(2,1)}), bf16[256,4,512]{2,0,1:T(8,128)(2,1)S(1)}, u32[]{:S(2)}, u32[]{:S(2)}) async-start(bf16[256,4,512]{2,0,1:T(8,128)(2,1)} %copy.26), calls=%async_computation | async-start | bytes 2097152 | tf_op jit(solution)/shard_map/all_to_all | solution.py:66
  16.7 143.9 %all-gather.5.cloned.1.call-start = ((), (), s32[]{:S(2)}) async-start(), calls=%async_computation.9 | async-start | bytes 2621440 | tf_op jit(solution)/shard_map/all_gather | solution.py:82
  67.8 21.5 %copy-start = (bf16[256,4,512]{2,0,1:T(8,128)(2,1)}, bf16[256,4,512]{2,0,1:T(8,128)(2,1)S(1)}, u32[]{:S(2)}) copy-start(bf16[256,4,512]{2,0,1:T(8,128)(2,1)S(1)} %all-to-all-done) | copy-start | bytes 3145732
  67.8 30.9 %all-to-all-start.4 = ((bf16[256,4,512]{2,0,1:T(8,128)(2,1)}), bf16[256,4,512]{2,0,1:T(8,128)(2,1)S(1)}, u32[]{:S(2)}, u32[]{:S(2)}) async-start(bf16[256,4,512]{2,0,1:T(8,128)(2,1)} %copy.31), calls=%async_computation.4 | async-start | bytes 2097152 | tf_op jit(solution)/shard_map/all_to_all | solution.py:66
  98.7 66.1 %all-to-all-start.1 = ((bf16[4,256,512]{1,2,0:T(8,128)(2,1)}), bf16[4,256,512]{1,2,0:T(8,128)(2,1)S(1)}, u32[]{:S(2)}, u32[]{:S(2)}) async-start(bf16[4,256,512]{1,2,0:T(8,128)(2,1)} %copy.28), calls=%async_computation.1 | async-start | bytes 2097152 | tf_op jit(solution)/shard_map/all_to_all | solution.py:72
  164.8 7.4 %copy-start.4 = (f32[256,27]{0,1:T(8,128)S(1)}, f32[256,27]{0,1:T(8,128)}, u32[]{:S(2)}) copy-start(f32[256,27]{0,1:T(8,128)} %param.10) | copy-start | bytes 82948
  164.8 29.5 %all-to-all-start.5 = ((bf16[4,256,512]{1,2,0:T(8,128)(2,1)}), bf16[4,256,512]{1,2,0:T(8,128)(2,1)S(1)}, u32[]{:S(2)}, u32[]{:S(2)}) async-start(bf16[4,256,512]{1,2,0:T(8,128)(2,1)} %copy.33), calls=%async_computation.5 | async-start | bytes 2097152 | tf_op jit(solution)/shard_map/all_to_all | solution.py:72
  169.3 25.2 %collective-permute-start = (bf16[256,1,512]{0,2,1:T(8,128)(2,1)}, bf16[256,1,512]{0,2,1:T(8,128)(2,1)S(1)}, u32[]{:S(2)}, u32[]{:S(2)}) collective-permute-start(bf16[256,1,512]{0,2,1:T(8,128)(2,1)} %get-tuple-element.8), channel_id=1, source_target_pairs={{0,1},{1,2},{2,3},{4,5},{5,6},{6,7},{8,9},{9,10},{10,11},{12,13},{... | collective-permute-start | bytes 786440 | tf_op jit(solution)/shard_map/ppermute | solution.py:19
  170.9 23.6 %collective-permute-start.1 = (bf16[256,1,512]{0,2,1:T(8,128)(2,1)}, bf16[256,1,512]{0,2,1:T(8,128)(2,1)}, u32[]{:S(2)}, u32[]{:S(2)}) collective-permute-start(bf16[256,1,512]{0,2,1:T(8,128)(2,1)} %get-tuple-element.9), channel_id=1, source_target_pairs={{1,0},{2,1},{3,2},{5,4},{6,5},{7,6},{9,8},{10,9},{11,10},{13,12},{... | collective-permute-start | bytes 786440 | tf_op jit(solution)/shard_map/ppermute | solution.py:22
  194.5 1.2 copy-start.5
  206.6 7.5 %collective-permute-start.2 = (bf16[256,1,512]{0,2,1:T(8,128)(2,1)}, bf16[256,1,512]{0,2,1:T(8,128)(2,1)S(1)}, u32[]{:S(2)}, u32[]{:S(2)}) collective-permute-start(bf16[256,1,512]{0,2,1:T(8,128)(2,1)} %get-tuple-element.6), channel_id=1, source_target_pairs={{0,1},{1,2},{2,3},{4,5},{5,6},{6,7},{8,9},{9,10},{10,11},{12,13},{... | collective-permute-start | bytes 786440 | tf_op jit(solution)/shard_map/ppermute | solution.py:19
  207.9 6.2 %collective-permute-start.3 = (bf16[256,1,512]{0,2,1:T(8,128)(2,1)}, bf16[256,1,512]{0,2,1:T(8,128)(2,1)}, u32[]{:S(2)}, u32[]{:S(2)}) collective-permute-start(bf16[256,1,512]{0,2,1:T(8,128)(2,1)} %get-tuple-element.7), channel_id=1, source_target_pairs={{1,0},{2,1},{3,2},{5,4},{6,5},{7,6},{9,8},{10,9},{11,10},{13,12},{... | collective-permute-start | bytes 786440 | tf_op jit(solution)/shard_map/ppermute | solution.py:22
  210.6 29.6 %all-to-all-start.2 = ((bf16[256,4,512]{0,2,1:T(8,128)(2,1)}), bf16[256,4,512]{0,2,1:T(8,128)(2,1)S(1)}, u32[]{:S(2)}, u32[]{:S(2)}) async-start(bf16[256,4,512]{0,2,1:T(8,128)(2,1)} %bitcast.35), calls=%async_computation.2 | async-start | bytes 2097152 | tf_op jit(solution)/shard_map/all_to_all | solution.py:66
  225.4 19.1 %copy-start.1 = (bf16[256,4,512]{2,0,1:T(8,128)(2,1)S(1)}, bf16[256,4,512]{2,0,1:T(8,128)(2,1)}, u32[]{:S(2)}) copy-start(bf16[256,4,512]{2,0,1:T(8,128)(2,1)} %copy-done) | copy-start | bytes 3145732
  240.2 31.3 %all-to-all-start.6 = ((bf16[256,4,512]{0,2,1:T(8,128)(2,1)}), bf16[256,4,512]{0,2,1:T(8,128)(2,1)}, u32[]{:S(2)}, u32[]{:S(2)}) async-start(bf16[256,4,512]{0,2,1:T(8,128)(2,1)} %bitcast.83), calls=%async_computation.6 | async-start | bytes 2097152 | tf_op jit(solution)/shard_map/all_to_all | solution.py:66
  245.8 1.3 copy-start.3
  271.5 29.6 %all-to-all-start.3 = ((bf16[4,256,512]{2,1,0:T(8,128)(2,1)}), bf16[4,256,512]{2,1,0:T(8,128)(2,1)S(1)}, u32[]{:S(2)}, u32[]{:S(2)}) async-start(bf16[4,256,512]{2,1,0:T(8,128)(2,1)} %bitcast.39), calls=%async_computation.3 | async-start | bytes 2097152 | tf_op jit(solution)/shard_map/all_to_all | solution.py:72
  301.2 28.8 %all-to-all-start.7 = ((bf16[4,256,512]{2,1,0:T(8,128)(2,1)}), bf16[4,256,512]{2,1,0:T(8,128)(2,1)S(1)}, u32[]{:S(2)}, u32[]{:S(2)}) async-start(bf16[4,256,512]{2,1,0:T(8,128)(2,1)} %bitcast.54), calls=%async_computation.7 | async-start | bytes 2097152 | tf_op jit(solution)/shard_map/all_to_all | solution.py:72
Sparse Core Ops, SparseCore 0:
  9.5 76.9 all-gather.2
  88.1 72.5 all-gather.4
where the time goes:
time: 340 us; the launch traced here: 339 us
  waiting for transfers between devices  230 us (68%)
  starting transfers between devices  37.6 us (11%)
  other arithmetic  24 us (7%)
  local copies, waits for them, and re-layouts  19.9 us (6%)
  between operations  14.3 us (4%)
  matrix products  12.7 us (4%)
    all_to_all x4, waiting for transfers between devices, to_cells(): lax.all_to_all(field.reshape(field.shape[0], -1), 'chan', split_axis=1, c...  91.9 us
    all_to_all x4, waiting for transfers between devices, to_channels(): lax.all_to_all(field, 'chan', split_axis=0, concat_axis=1, tiled=True)  63.2 us
    all_gather x1, waiting for transfers between devices, body(): lax.all_gather(weight_out, 'chan', axis=0, tiled=True)  58.4 us
    all_to_all x4, starting transfers between devices, to_cells(): lax.all_to_all(field.reshape(field.shape[0], -1), 'chan', split_axis=1, c...  17.6 us
    all_gather x1, waiting for transfers between devices, body(): lax.all_gather(weight_in, 'chan', axis=0, tiled=True)  15.1 us
    all_to_all x4, starting transfers between devices, to_channels(): lax.all_to_all(field, 'chan', split_axis=0, concat_axis=1, tiled=True)  14.4 us
    convert_element_type x1, other arithmetic, body(): core(padded_grad, filter_taps, -1).astype(jnp.bfloat16).reshape(slab_shape)  10 us
    convert_element_type x1, other arithmetic, body(): mix_grad = (act_grad.astype(jnp.float32).reshape(slope.shape) * slope).as...  10 us
  transfers between devices with their start and end apart: 14, of which 9 were waited for; matrix products, arithmetic and copies ran while one was open for 13% of the time, Pallas kernels for 0%

commit v1 on v0

v1 whole, which is shorter than its diff:
```python
import jax
import jax.numpy as jnp
from jax import lax
from jax.experimental import pallas as pl
from jax.experimental.pallas import tpu as pltpu
from jax.sharding import PartitionSpec as P

CX = 32
CY = 16
LANES = 128


root_half = 0.7071067811865476
inv_root_two_pi = 0.3989422804014327


def gelu_value(field):
    return 0.5 * field * (1.0 + lax.erf(field * root_half))


def gelu_slope(field):
    return (
        0.5 * (1.0 + lax.erf(field * root_half))
        + field * jnp.exp(-0.5 * field * field) * inv_root_two_pi
    )


def fill_padded(padded, own, row_low, row_high, plane_low, plane_high):
    planes, rows = own.shape[0], own.shape[1]
    for z in range(planes):
        padded[z + 1, 0] = row_low[z].astype(jnp.float32)
        padded[z + 1, rows + 1] = row_high[z].astype(jnp.float32)
        for y in range(rows):
            padded[z + 1, y + 1] = own[z, y].astype(jnp.float32)
    for y in range(rows + 2):
        padded[0, y] = plane_low[y].astype(jnp.float32)
        padded[planes + 1, y] = plane_high[y].astype(jnp.float32)


def stencil_row(padded, taps, z, y, flip):
    sums = [None, None, None]
    for a in range(3):
        for b in range(3):
            row = padded[z + a, y + b]
            for e in range(3):
                index = (a * 3 + b) * 3 + e
                tap = taps[26 - index if flip else index]
                term = row * tap[None, :]
                sums[e] = term if sums[e] is None else sums[e] + term
    x = lax.broadcasted_iota(jnp.int32, sums[0].shape, 0)
    extent = sums[0].shape[0]
    before = jnp.where(x == 0, 0.0, pltpu.roll(sums[0], 1, 0))
    after = jnp.where(x == extent - 1, 0.0, pltpu.roll(sums[2], extent - 1, 0))
    return sums[1] + (before + after)


def forward_kernel(own, row_low, row_high, plane_low, plane_high, taps, bias, active, slope, padded):
    fill_padded(padded, own, row_low, row_high, plane_low, plane_high)
    for z in range(own.shape[0]):
        for y in range(own.shape[1]):
            mixed = stencil_row(padded, taps, z, y, False) + bias[0][None, :]
            half = 0.5 * (1.0 + lax.erf(mixed * root_half))
            active[z, y] = (mixed * half).astype(active.dtype)
            slope[z, y] = half + mixed * jnp.exp(-0.5 * mixed * mixed) * inv_root_two_pi


def backward_kernel(own, row_low, row_high, plane_low, plane_high, taps, out, padded):
    fill_padded(padded, own, row_low, row_high, plane_low, plane_high)
    for z in range(own.shape[0]):
        for y in range(own.shape[1]):
            out[z, y] = stencil_row(padded, taps, z, y, True).astype(out.dtype)


def stencil(own, halo, taps, bias=None):
    planes, rows, extent, channels = own.shape

    def block(*lead):
        zeros = (0,) * len(lead)
        return pl.BlockSpec(lead + (LANES,), lambda c: zeros + (c,))

    in_specs = [
        block(planes, rows, extent),
        block(planes, extent),
        block(planes, extent),
        block(rows + 2, extent),
        block(rows + 2, extent),
        block(27),
    ]
    args = (own,) + halo + (taps,)
    scratch = [pltpu.VMEM((planes + 2, rows + 2, extent, LANES), jnp.float32)]
    shape = jax.ShapeDtypeStruct(own.shape, own.dtype)
    if bias is None:
        return pl.pallas_call(
            backward_kernel,
            grid=(channels // LANES,),
            in_specs=in_specs,
            out_specs=block(planes, rows, extent),
            out_shape=shape,
            scratch_shapes=scratch,
        )(*args)
    return pl.pallas_call(
        forward_kernel,
        grid=(channels // LANES,),
        in_specs=in_specs + [block(1)],
        out_specs=[block(planes, rows, extent)] * 2,
        out_shape=[shape, jax.ShapeDtypeStruct(own.shape, jnp.float32)],
        scratch_shapes=scratch,
    )(*args, bias)


def shift_pairs(axis):
    count = lax.axis_size(axis)
    forward = [(i, i + 1) for i in range(count - 1)]
    return forward, [(target, source) for source, target in forward]


def halo_of(field):
    forward, backward = shift_pairs("chan")
    row_low = lax.ppermute(field[:, -1], "chan", forward)
    row_high = lax.ppermute(field[:, 0], "chan", backward)
    forward, backward = shift_pairs("space")

    def plane(z):
        return jnp.concatenate([row_low[z][None], field[z], row_high[z][None]], axis=0)

    plane_low = lax.ppermute(plane(-1), "space", forward)
    plane_high = lax.ppermute(plane(0), "space", backward)
    return row_low, row_high, plane_low, plane_high


def split_cells_body(volume, out_grad, weight_in, weight_out, filter_taps, filter_bias):
    own, planes, cells = volume.shape
    parts = lax.axis_size("chan")
    rows = CY // parts
    channels = own * parts

    def to_cells(field):
        blocks = field.reshape(own, planes, parts, rows * CX).transpose(2, 1, 0, 3)
        return lax.all_to_all(blocks, "chan", split_axis=0, concat_axis=0, tiled=True)

    def to_channels(blocks):
        back = lax.all_to_all(blocks, "chan", split_axis=0, concat_axis=0, tiled=True)
        return back.transpose(2, 1, 0, 3).reshape(own, planes, cells)

    def gather(part):
        return lax.all_gather(part, "chan", axis=0, tiled=True)

    full_in, full_out = gather(weight_in), gather(weight_out)
    taps = gather(filter_taps).T
    bias = gather(filter_bias)[None, :]
    grid = (planes, rows, CX, channels)

    vol_cells = to_cells(volume)
    hidden = jnp.einsum(
        "kzcl,okc->zlo",
        vol_cells,
        full_in.reshape(channels, parts, own),
        preferred_element_type=jnp.float32,
    ).astype(jnp.bfloat16)
    hidden = hidden.reshape(grid)
    active, slope = stencil(hidden, halo_of(hidden), taps, bias)
    out_cells = jnp.einsum(
        "kcd,zld->kzcl",
        full_out.reshape(parts, own, channels),
        active.reshape(planes, rows * CX, channels),
        preferred_element_type=jnp.float32,
    )
    block_out = to_channels((vol_cells.astype(jnp.float32) + out_cells).astype(jnp.bfloat16))

    grad_cells = to_cells(out_grad)
    act_grad = jnp.einsum(
        "kzcl,kcd->zld",
        grad_cells,
        full_out.reshape(parts, own, channels),
        preferred_element_type=jnp.float32,
    ).astype(jnp.bfloat16)
    mix_grad = (act_grad.reshape(grid).astype(jnp.float32) * slope).astype(jnp.bfloat16)
    hid_grad = stencil(mix_grad, halo_of(mix_grad), taps)
    back_cells = jnp.einsum(
        "dkc,zld->kzcl",
        full_in.reshape(channels, parts, own),
        hid_grad.reshape(planes, rows * CX, channels),
        preferred_element_type=jnp.float32,
    )
    volume_grad = to_channels((grad_cells.astype(jnp.float32) + back_cells).astype(jnp.bfloat16))
    return block_out, volume_grad


def with_halo(block, axis, dim):
    forward, backward = shift_pairs(axis)
    low = lax.ppermute(lax.slice_in_dim(block, block.shape[dim] - 1, None, axis=dim), axis, forward)
    high = lax.ppermute(lax.slice_in_dim(block, 0, 1, axis=dim), axis, backward)
    return jnp.concatenate([low, block, high], axis=dim)


def core(padded, filter_taps, direction):
    extent_z = padded.shape[1] - 2
    extent_y = padded.shape[2] - 2
    extent_x = padded.shape[3] - 2
    summed = jnp.zeros((padded.shape[0], extent_z, extent_y, extent_x), jnp.float32)
    for shift_z in range(3):
        for shift_y in range(3):
            for shift_x in range(3):
                tap_index = (shift_z * 3 + shift_y) * 3 + shift_x
                begin_z = 1 + direction * (shift_z - 1)
                begin_y = 1 + direction * (shift_y - 1)
                begin_x = 1 + direction * (shift_x - 1)
                window = padded[
                    :,
                    begin_z : begin_z + extent_z,
                    begin_y : begin_y + extent_y,
                    begin_x : begin_x + extent_x,
                ]
                summed = summed + filter_taps[:, tap_index][:, None, None, None] * window
    return summed


def lift(field_z):
    extended = field_z.astype(jnp.float32).reshape(field_z.shape[0], field_z.shape[1], CY, CX)
    return jnp.pad(extended, ((0, 0), (0, 0), (1, 1), (1, 1)))


def exchange_body(volume, out_grad, weight_in, weight_out, filter_taps, filter_bias):
    slab_shape = volume.shape
    contract_first = (((0,), (0,)), ((), ()))

    def to_cells(field):
        return lax.all_to_all(
            field.reshape(field.shape[0], -1), "chan", split_axis=1, concat_axis=0, tiled=True
        )

    def to_channels(field):
        return lax.all_to_all(field, "chan", split_axis=0, concat_axis=1, tiled=True).reshape(
            slab_shape
        )

    full_in = lax.all_gather(weight_in, "chan", axis=0, tiled=True)
    full_out = lax.all_gather(weight_out, "chan", axis=0, tiled=True)
    vol_cells = to_cells(volume)
    hidden = to_channels(
        jnp.dot(full_in, vol_cells, preferred_element_type=jnp.float32).astype(jnp.bfloat16)
    )
    padded = lift(with_halo(hidden, "space", 1))
    mixed = core(padded, filter_taps, 1) + filter_bias[:, None, None, None]
    active = gelu_value(mixed).astype(jnp.bfloat16).reshape(slab_shape)
    out_cells = vol_cells.astype(jnp.float32) + jnp.dot(
        full_out, to_cells(active), preferred_element_type=jnp.float32
    )
    block_out = to_channels(out_cells.astype(jnp.bfloat16))
    grad_cells = to_cells(out_grad)
    act_part = lax.dot_general(
        full_out, grad_cells, contract_first, preferred_element_type=jnp.float32
    )
    act_grad = to_channels(act_part.astype(jnp.bfloat16))
    slope = gelu_slope(mixed)
    mix_grad = (
        (act_grad.astype(jnp.float32).reshape(slope.shape) * slope)
        .astype(jnp.bfloat16)
        .reshape(slab_shape)
    )
    padded_grad = lift(with_halo(mix_grad, "space", 1))
    hid_grad = core(padded_grad, filter_taps, -1).astype(jnp.bfloat16).reshape(slab_shape)
    back_part = lax.dot_general(
        full_in, to_cells(hid_grad), contract_first, preferred_element_type=jnp.float32
    )
    volume_grad = to_channels((grad_cells.astype(jnp.float32) + back_part).astype(jnp.bfloat16))
    return block_out, volume_grad


def solution(mesh):
    field = P(("groups", "chan"), "space", None)
    placed = (field, field, P("chan", None), P("chan", None), P("chan", None), P("chan"))
    parts = mesh.shape["chan"]
    whole_rows = CY % parts == 0 and (CY // parts * CX) % LANES == 0
    return jax.shard_map(
        split_cells_body if whole_rows else exchange_body,
        mesh=mesh,
        in_specs=placed,
        out_specs=(field, field),
        check_vma=False,
    )
```

time: 340 us -> 270 us (0.79)
  waiting for transfers between devices: 230 us -> 112 us
  blocking collectives: 0 us -> 36.2 us
  starting transfers between devices: 37.6 us -> 58.1 us
  other arithmetic: 24 us -> 4.13 us
  Pallas kernels: 0 us -> 16 us
  local copies, waits for them, and re-layouts: 19.9 us -> 15.5 us
    all_to_all x8 -> x4, waiting for transfers between devices: 155 us -> 74.7 us  [the longest x2 51.4 us: to_cells(): lax.all_to_all(blocks, 'chan', split_axis=0, concat_axis=0, tiled=True)]
    all_gather x2, waiting for transfers between devices: 73.5 us -> 9.43 us  [gather(): return lax.all_gather(part, 'chan', axis=0, tiled=True)]
    all_gather x0 -> x2, blocking collectives: none -> 36.2 us  [gather(): return lax.all_gather(part, 'chan', axis=0, tiled=True)]
    ppermute x4 -> x8, waiting for transfers between devices: 0.01 us -> 27.4 us  [the longest x2 26.3 us: halo_of(): row_low = lax.ppermute(field[:, -1], 'chan', forward)]
    ppermute x4 -> x8, starting transfers between devices: 5.46 us -> 32.6 us  [the longest x2 23.7 us: halo_of(): row_low = lax.ppermute(field[:, -1], 'chan', forward)]
    convert_element_type x6 -> x1, other arithmetic: 24 us -> 2.36 us  [split_cells_body(): (act_grad.reshape(grid).astype(jnp.float32) * slope).astype(jnp.bfloat16)]
    pallas_call x0 -> x2, Pallas kernels: none -> 16 us  [the longest x1 8.49 us: stencil(): pl.pallas_call(forward_kernel, grid=(channels // LANES,), in_specs=in_spe...]
    all_to_all x8 -> x2, local copies, waits for them, and re-layouts: 10.9 us -> 0.18 us  [to_channels(): lax.all_to_all(blocks, 'chan', split_axis=0, concat_axis=0, tiled=True)]
  transfers between devices with their start and end apart: 14 -> 14, of which waited for: 9 -> 6; matrix products, arithmetic and copies ran while one was open for 13% -> 8% of each run, Pallas kernels for 0% -> 3%
where the time goes in v1:
time: 270 us; the launch traced here: 268 us
  waiting for transfers between devices  112 us (41%)
  starting transfers between devices  58.1 us (22%)
  blocking collectives  36.2 us (13%)
  Pallas kernels  16 us (6%)
  local copies, waits for them, and re-layouts  15.5 us (6%)
  between operations  14.4 us (5%)
  matrix products  11.2 us (4%)
  other arithmetic  4.13 us (2%)
    all_to_all x2, waiting for transfers between devices, to_cells(): lax.all_to_all(blocks, 'chan', split_axis=0, concat_axis=0, tiled=True)  51.4 us
    all_gather x2, blocking collectives, gather(): return lax.all_gather(part, 'chan', axis=0, tiled=True)  36.2 us
    ppermute x2, waiting for transfers between devices, halo_of(): row_low = lax.ppermute(field[:, -1], 'chan', forward)  26.3 us
    ppermute x2, starting transfers between devices, halo_of(): row_low = lax.ppermute(field[:, -1], 'chan', forward)  23.7 us
    all_to_all x2, waiting for transfers between devices, to_channels(): lax.all_to_all(blocks, 'chan', split_axis=0, concat_axis=0, tiled=True)  23.3 us
    all_to_all x2, starting transfers between devices, to_channels(): lax.all_to_all(blocks, 'chan', split_axis=0, concat_axis=0, tiled=True)  15.6 us
    all_to_all x2, starting transfers between devices, to_cells(): lax.all_to_all(blocks, 'chan', split_axis=0, concat_axis=0, tiled=True)  9.87 us
    all_gather x2, waiting for transfers between devices, gather(): return lax.all_gather(part, 'chan', axis=0, tiled=True)  9.43 us
  transfers between devices with their start and end apart: 14, of which 6 were waited for; matrix products, arithmetic and copies ran while one was open for 8% of the time, Pallas kernels for 3%

profile of v1, /device:TPU:0, one launch (start us, length us, event | category | flops | bytes accessed | tf_op | source)
XLA Modules:
  0.0 267.7 jit_solution(15587860053863714169)
XLA Ops:
  7.2 0.0 all-gather.4.cloned.1.call-start
  7.2 2.1 copy.44
  9.3 0.0 all-gather.4.cloned.1.call-update
  9.4 0.8 copy.41
  10.2 0.0 copy-start.2
  10.2 1.0 copy.42
  11.2 6.3 %all-to-all-start = ((bf16[4,4,256,128]{2,3,1,0:T(8,128)(2,1)}), bf16[4,4,256,128]{2,3,1,0:T(8,128)(2,1)S(1)}, u32[]{:S(2)}, u32[]{:S(2)}) async-start(bf16[4,4,256,128]{2,3,1,0:T(8,128)(2,1)} %copy.42), calls=%async_computation | async-start | bytes 2097152 | tf_op jit(solution)/shard_map/all_to_all | solution.py:139
  17.6 0.7 all-gather.6.cloned.1.call-update
  18.3 0.0 copy-done.2
  18.3 0.8 copy.50
  19.1 1.0 copy.51
  20.2 51.4 %all-to-all-done = bf16[4,4,256,128]{2,3,1,0:T(8,128)(2,1)S(1)} async-done(((bf16[4,4,256,128]{2,3,1,0:T(8,128)(2,1)}), bf16[4,4,256,128]{2,3,1,0:T(8,128)(2,1)S(1)}, u32[]{:S(2)}, u32[]{:S(2)}) %all-to-all-start) | async-done | bytes 1048608 | tf_op jit(solution)/shard_map/all_to_all | solution.py:139
  71.5 3.5 %all-to-all-start.2 = ((bf16[4,4,256,128]{2,3,1,0:T(8,128)(2,1)}), bf16[4,4,256,128]{2,3,1,0:T(8,128)(2,1)S(1)}, u32[]{:S(2)}, u32[]{:S(2)}) async-start(bf16[4,4,256,128]{2,3,1,0:T(8,128)(2,1)} %copy.51), calls=%async_computation.2 | async-start | bytes 2097152 | tf_op jit(solution)/shard_map/all_to_all | solution.py:139
  75.1 9.4 %all-gather.4.cloned.1.call-done = bf16[1024,1024]{0,1:T(8,128)(2,1)} async-done(((bf16[256,1024]{0,1:T(8,128)(2,1)}), bf16[1024,1024]{0,1:T(8,128)(2,1)}) %all-gather.4.cloned.1.call-update) | async-done | bytes 2097168 | tf_op jit(solution)/shard_map/all_gather | solution.py:146
  84.5 2.9 %bitcast_convert_fusion.1 = bf16[4,128,1024]{2,1,0:T(8,128)(2,1)S(1)} fusion(bf16[4,4,256,128]{2,3,1,0:T(8,128)(2,1)S(1)} %all-to-all-done, bf16[1024,4,256,1]{0,2,3,1:T(8,128)(2,1)} %bitcast.91), kind=kOutput, calls=%fused_computation.5 | convolution fusion | flops 1074266112 | bytes 4194304 | tf_op jit(solution)/shard_map/kzcl,okc->zlo/dot_general | solution.py:154
  87.4 0.0 copy-start
  87.4 0.0 copy-start.12
  87.4 1.3 collective-permute-start.1
  88.7 0.0 copy-done.13
  88.7 21.6 %all-gather = f32[4,1,256]{2,1,0:T(1,128)} all-gather(f32[1,1,256]{2,1,0:T(1,128)S(1)} %bitcast.90), channel_id=1, replica_groups=mesh['groups'=2,'chan'=4,'space'=4] {'chan'}, dimensions={0}, use_global_device_ids=true | all-gather | bytes 5120 | tf_op jit(solution)/shard_map/all_gather | solution.py:146
  110.4 19.7 %collective-permute-start = (bf16[4,32,1024]{2,1,0:T(8,128)(2,1)S(1)}, bf16[4,32,1024]{2,1,0:T(8,128)(2,1)S(1)}, u32[]{:S(2)}, u32[]{:S(2)}) collective-permute-start(bf16[4,32,1024]{2,1,0:T(8,128)(2,1)S(1)} %get-tuple-element.19), channel_id=1, source_target_pairs={{0,4},{4,8},{8,12},{1,5},{5,9},{9,13},{2,6},{6,10},{10,14},{3,7},{... | collective-permute-start | bytes 786440 | tf_op jit(solution)/shard_map/ppermute | solution.py:119
  130.2 0.0 collective-permute-done.1.row_high
  130.2 6.9 %collective-permute-done.row_low = bf16[4,32,1024]{2,1,0:T(8,128)(2,1)S(1)} collective-permute-done((bf16[4,32,1024]{2,1,0:T(8,128)(2,1)S(1)}, bf16[4,32,1024]{2,1,0:T(8,128)(2,1)S(1)}, u32[]{:S(2)}, u32[]{:S(2)}) %collective-permute-start) | collective-permute-done | bytes 262176 | tf_op jit(solution)/shard_map/ppermute | solution.py:119
  137.1 0.9 pad_maximum_fusion
  138.0 1.3 collective-permute-start.2
  139.3 0.8 pad_maximum_fusion.1
  140.1 1.3 collective-permute-start.3
  141.4 14.5 %all_gather.13 = f32[1024,27]{0,1:T(8,128)} all-gather(f32[256,27]{0,1:T(8,128)S(1)} %copy-done.12), channel_id=1, replica_groups=mesh['groups'=2,'chan'=4,'space'=4] {'chan'}, dimensions={0}, use_global_device_ids=true | all-gather | bytes 138240 | tf_op jit(solution)/shard_map/all_gather | solution.py:146
  155.9 0.0 all-to-all-done.2
  155.9 3.9 %bitcast_convert_fusion = bf16[4,128,1024]{2,1,0:T(8,128)(2,1)} fusion(bf16[4,4,256,128]{2,3,1,0:T(8,128)(2,1)S(1)} %all-to-all-done.2, bf16[4,256,1024,1]{2,1,3,0:T(8,128)(2,1)} %bitcast.93), kind=kOutput, calls=%fused_computation.2 | convolution fusion | flops 1074266112 | bytes 4194304 | tf_op jit(solution)/shard_map/kzcl,kcd->zld/dot_general | solution.py:171
  159.8 0.0 collective-permute-done.2.plane_low
  159.8 0.0 collective-permute-done.3.plane_high
  159.8 0.8 copy-done.9
  160.6 0.1 copy-done.10
  160.7 8.5 %shard_map.77 = (bf16[4,4,32,1024]{3,2,1,0:T(8,128)(2,1)}, f32[4,4,32,1024]{3,2,1,0:T(8,128)}) custom-call(bf16[4,4,32,1024]{3,2,1,0:T(8,128)(2,1)} %bitcast.78, bf16[4,32,1024]{2,1,0:T(8,128)(2,1)} %copy-done.7, bf16[4,32,1024]{2,1,0:T(8,128)(2,1)} %copy-done.6, bf16[6,32,1024]{2,1,0:T(8,128)(2,1)} %copy-done.9, bf16[6,32,1024]{2,1,0:T(8,128)(2,1)} %copy-done.10, ...), custom_call_target="tpu_custom_call" | custom-call | tf_op jit(solution)/shard_map/pallas_call | solution.py:101
  169.2 0.0 copy-start.15
  169.2 2.4 fusion.2
  171.6 0.9 slice_bitcast_fusion.2
  172.4 1.3 collective-permute-start.5
  173.8 1.3 fusion.1
  175.1 1.0 copy.48
  176.1 4.6 %all-to-all-start.1 = ((bf16[4,4,256,128]{2,3,1,0:T(8,128)(2,1)}), bf16[4,4,256,128]{2,3,1,0:T(8,128)(2,1)S(1)}, u32[]{:S(2)}, u32[]{:S(2)}) async-start(bf16[4,4,256,128]{2,3,1,0:T(8,128)(2,1)} %copy.48), calls=%async_computation.1 | async-start | bytes 2097152 | tf_op jit(solution)/shard_map/all_to_all | solution.py:142
  180.7 3.9 %collective-permute-start.4 = (bf16[4,32,1024]{2,1,0:T(8,128)(2,1)}, bf16[4,32,1024]{2,1,0:T(8,128)(2,1)S(1)}, u32[]{:S(2)}, u32[]{:S(2)}) collective-permute-start(bf16[4,32,1024]{2,1,0:T(8,128)(2,1)} %get-tuple-element.15), channel_id=1, source_target_pairs={{0,4},{4,8},{8,12},{1,5},{5,9},{9,13},{2,6},{6,10},{10,14},{3,7},{... | collective-permute-start | bytes 786440 | tf_op jit(solution)/shard_map/ppermute | solution.py:119
  184.7 0.0 collective-permute-done.5.row_high
  184.7 19.5 %collective-permute-done.4.row_low = bf16[4,32,1024]{2,1,0:T(8,128)(2,1)S(1)} collective-permute-done((bf16[4,32,1024]{2,1,0:T(8,128)(2,1)}, bf16[4,32,1024]{2,1,0:T(8,128)(2,1)S(1)}, u32[]{:S(2)}, u32[]{:S(2)}) %collective-permute-start.4) | collective-permute-done | bytes 262176 | tf_op jit(solution)/shard_map/ppermute | solution.py:119
  204.2 0.1 pad_maximum_fusion.2
  204.2 2.5 collective-permute-start.6
  206.7 0.1 pad_maximum_fusion.3
  206.8 1.3 collective-permute-start.7
  208.1 1.1 copy.55.own
  209.2 0.0 copy-done.5
  209.2 0.0 collective-permute-done.6.plane_low
  209.2 0.8 copy-done.11
  209.9 1.0 collective-permute-done.7.plane_high
  211.0 7.5 %shard_map.78 = bf16[4,4,32,1024]{3,2,1,0:T(8,128)(2,1)} custom-call(bf16[4,4,32,1024]{3,2,1,0:T(8,128)(2,1)} %copy.55.own, bf16[4,32,1024]{2,1,0:T(8,128)(2,1)} %copy-done.8, bf16[4,32,1024]{2,1,0:T(8,128)(2,1)} %copy-done.5, bf16[6,32,1024]{2,1,0:T(8,128)(2,1)} %copy-done.11, bf16[6,32,1024]{2,1,0:T(8,128)(2,1)} %collective-permute-done.7.plane_high, ...), custom_call_target="tpu_custom_call" | custom-call | tf_op jit(solution)/shard_map/pallas_call | solution.py:93
  218.5 3.2 %fusion = bf16[4,4,256,128]{2,3,0,1:T(8,128)(2,1)S(1)} fusion(bf16[4,128,1024,1]{2,1,3,0:T(8,128)(2,1)} %bitcast.85, bf16[1024,4,256,1]{0,2,1,3:T(8,128)(2,1)} %bitcast.92, bf16[4,4,256,128]{2,3,1,0:T(8,128)(2,1)S(1)} %all-to-all-done.2), kind=kOutput, calls=%fused_computation.1 | convolution fusion | flops 1075314688 | bytes 5242880 | tf_op jit(solution)/shard_map/dkc,zld->kzcl/dot_general | solution.py:179
  221.7 1.1 copy.57
  222.8 0.0 all-to-all-done.1
  222.8 11.0 %all-to-all-start.3 = ((bf16[4,4,256,128]{2,3,1,0:T(8,128)(2,1)}), bf16[4,4,256,128]{2,3,1,0:T(8,128)(2,1)S(1)}, u32[]{:S(2)}, u32[]{:S(2)}) async-start(bf16[4,4,256,128]{2,3,1,0:T(8,128)(2,1)} %copy.57), calls=%async_computation.3 | async-start | bytes 2097152 | tf_op jit(solution)/shard_map/all_to_all | solution.py:142
  233.8 0.1 copy.49
  233.9 1.8 copy.59
  235.7 23.3 %all-to-all-done.3 = bf16[4,4,256,128]{2,3,1,0:T(8,128)(2,1)S(1)} async-done(((bf16[4,4,256,128]{2,3,1,0:T(8,128)(2,1)}), bf16[4,4,256,128]{2,3,1,0:T(8,128)(2,1)S(1)}, u32[]{:S(2)}, u32[]{:S(2)}) %all-to-all-start.3) | async-done | bytes 1048608 | tf_op jit(solution)/shard_map/all_to_all | solution.py:142
  259.0 0.1 copy.58
  259.1 1.8 copy.60
  (31 shorter events, 0.2 us)
Async XLA Ops:
  7.2 2.2 copy-start.1
  7.2 77.3 %all-gather.4.cloned.1.call-start = ((), (), s32[]{:S(2)}) async-start(), calls=%async_computation.4 | async-start | bytes 2621440 | tf_op jit(solution)/shard_map/all_gather | solution.py:146
  10.2 8.1 %copy-start.2 = (bf16[256,4,512]{2,1,0:T(4,128)(2,1)S(1)}, bf16[256,4,512]{2,1,0:T(4,128)(2,1)}, u32[]{:S(2)}) copy-start(bf16[256,4,512]{2,1,0:T(4,128)(2,1)} %param.7) | copy-start | bytes 3145732
  11.2 60.3 %all-to-all-start = ((bf16[4,4,256,128]{2,3,1,0:T(8,128)(2,1)}), bf16[4,4,256,128]{2,3,1,0:T(8,128)(2,1)S(1)}, u32[]{:S(2)}, u32[]{:S(2)}) async-start(bf16[4,4,256,128]{2,3,1,0:T(8,128)(2,1)} %copy.42), calls=%async_computation | async-start | bytes 2097152 | tf_op jit(solution)/shard_map/all_to_all | solution.py:139
  17.6 138.3 %all-gather.6.cloned.1.call-start = ((), (), s32[]{:S(2)}) async-start(), calls=%async_computation.5 | async-start | bytes 2621440 | tf_op jit(solution)/shard_map/all_gather | solution.py:146
  71.5 68.5 %copy-start.3 = (bf16[4,4,256,128]{2,3,1,0:T(8,128)(2,1)}, bf16[4,4,256,128]{2,3,1,0:T(8,128)(2,1)S(1)}, u32[]{:S(2)}) copy-start(bf16[4,4,256,128]{2,3,1,0:T(8,128)(2,1)S(1)} %all-to-all-done) | copy-start | bytes 3145732
  71.5 84.4 %all-to-all-start.2 = ((bf16[4,4,256,128]{2,3,1,0:T(8,128)(2,1)}), bf16[4,4,256,128]{2,3,1,0:T(8,128)(2,1)S(1)}, u32[]{:S(2)}, u32[]{:S(2)}) async-start(bf16[4,4,256,128]{2,3,1,0:T(8,128)(2,1)} %copy.51), calls=%async_computation.2 | async-start | bytes 2097152 | tf_op jit(solution)/shard_map/all_to_all | solution.py:139
  84.5 4.2 %copy-start.13 = (f32[256]{0:T(256)S(1)}, f32[256]{0:T(256)}, u32[]{:S(2)}) copy-start(f32[256]{0:T(256)} %param.11) | copy-start | bytes 3076
  87.4 52.7 %copy-start = (bf16[4,128,1024]{2,1,0:T(8,128)(2,1)}, bf16[4,128,1024]{2,1,0:T(8,128)(2,1)S(1)}, u32[]{:S(2)}) copy-start(bf16[4,128,1024]{2,1,0:T(8,128)(2,1)S(1)} %bitcast_convert_fusion.1) | copy-start | bytes 3145732
  87.4 54.0 %copy-start.12 = (f32[256,27]{0,1:T(8,128)S(1)}, f32[256,27]{0,1:T(8,128)}, u32[]{:S(2)}) copy-start(f32[256,27]{0,1:T(8,128)} %param.10) | copy-start | bytes 82948
  87.4 42.7 %collective-permute-start.1 = (bf16[4,32,1024]{2,1,0:T(8,128)(2,1)S(1)}, bf16[4,32,1024]{2,1,0:T(8,128)(2,1)S(1)}, u32[]{:S(2)}, u32[]{:S(2)}) collective-permute-start(bf16[4,32,1024]{2,1,0:T(8,128)(2,1)S(1)} %get-tuple-element.18), channel_id=1, source_target_pairs={{4,0},{8,4},{12,8},{5,1},{9,5},{13,9},{6,2},{10,6},{14,10},{7,3},{... | collective-permute-start | bytes 786440 | tf_op jit(solution)/shard_map/ppermute | solution.py:120
  110.4 26.7 %collective-permute-start = (bf16[4,32,1024]{2,1,0:T(8,128)(2,1)S(1)}, bf16[4,32,1024]{2,1,0:T(8,128)(2,1)S(1)}, u32[]{:S(2)}, u32[]{:S(2)}) collective-permute-start(bf16[4,32,1024]{2,1,0:T(8,128)(2,1)S(1)} %get-tuple-element.19), channel_id=1, source_target_pairs={{0,4},{4,8},{8,12},{1,5},{5,9},{9,13},{2,6},{6,10},{10,14},{3,7},{... | collective-permute-start | bytes 786440 | tf_op jit(solution)/shard_map/ppermute | solution.py:119
  130.2 29.6 %copy-start.6 = (bf16[4,32,1024]{2,1,0:T(8,128)(2,1)}, bf16[4,32,1024]{2,1,0:T(8,128)(2,1)S(1)}, u32[]{:S(2)}) copy-start(bf16[4,32,1024]{2,1,0:T(8,128)(2,1)S(1)} %collective-permute-done.1.row_high) | copy-start | bytes 786436
  137.1 22.7 %copy-start.7 = (bf16[4,32,1024]{2,1,0:T(8,128)(2,1)}, bf16[4,32,1024]{2,1,0:T(8,128)(2,1)S(1)}, u32[]{:S(2)}) copy-start(bf16[4,32,1024]{2,1,0:T(8,128)(2,1)S(1)} %collective-permute-done.row_low) | copy-start | bytes 786436
  138.0 21.8 %collective-permute-start.2 = (bf16[6,32,1024]{2,1,0:T(8,128)(2,1)}, bf16[6,32,1024]{2,1,0:T(8,128)(2,1)S(1)}, u32[]{:S(2)}, u32[]{:S(2)}) collective-permute-start(bf16[6,32,1024]{2,1,0:T(8,128)(2,1)} %pad_maximum_fusion), channel_id=1, source_target_pairs={{0,1},{1,2},{2,3},{4,5},{5,6},{6,7},{8,9},{9,10},{10,11},{12,13},{... | collective-permute-start | bytes 1179656 | tf_op jit(solution)/shard_map/ppermute | solution.py:126
  140.1 19.7 %collective-permute-start.3 = (bf16[6,32,1024]{2,1,0:T(8,128)(2,1)}, bf16[6,32,1024]{2,1,0:T(8,128)(2,1)S(1)}, u32[]{:S(2)}, u32[]{:S(2)}) collective-permute-start(bf16[6,32,1024]{2,1,0:T(8,128)(2,1)} %pad_maximum_fusion.1), channel_id=1, source_target_pairs={{1,0},{2,1},{3,2},{5,4},{6,5},{7,6},{9,8},{10,9},{11,10},{13,12},{... | collective-permute-start | bytes 1179656 | tf_op jit(solution)/shard_map/ppermute | solution.py:127
  159.8 0.8 copy-start.9
  159.8 0.9 copy-start.10
  169.2 4.6 %copy-start.4 = (bf16[4,4,256,128]{2,3,1,0:T(8,128)(2,1)S(1)}, bf16[4,4,256,128]{2,3,1,0:T(8,128)(2,1)}, u32[]{:S(2)}) copy-start(bf16[4,4,256,128]{2,3,1,0:T(8,128)(2,1)} %copy-done.3) | copy-start | bytes 3145732
  169.2 4.6 %copy-start.14 = (bf16[1024,1024]{1,0:T(8,128)(2,1)S(1)}, bf16[1024,1024]{1,0:T(8,128)(2,1)}, u32[]{:S(2)}) copy-start(bf16[1024,1024]{1,0:T(8,128)(2,1)} %all-gather.6.cloned.1.call-done) | copy-start | bytes 6291460
  169.2 4.6 %copy-start.15 = (bf16[4,4,32,1024]{3,2,1,0:T(8,128)(2,1)S(1)}, bf16[4,4,32,1024]{3,2,1,0:T(8,128)(2,1)}, u32[]{:S(2)}) copy-start(bf16[4,4,32,1024]{3,2,1,0:T(8,128)(2,1)} %get-tuple-element.4) | copy-start | bytes 3145732
  172.4 12.2 %collective-permute-start.5 = (bf16[4,32,1024]{2,1,0:T(8,128)(2,1)}, bf16[4,32,1024]{2,1,0:T(8,128)(2,1)S(1)}, u32[]{:S(2)}, u32[]{:S(2)}) collective-permute-start(bf16[4,32,1024]{2,1,0:T(8,128)(2,1)} %get-tuple-element.14), channel_id=1, source_target_pairs={{4,0},{8,4},{12,8},{5,1},{9,5},{13,9},{6,2},{10,6},{14,10},{7,3},{... | collective-permute-start | bytes 786440 | tf_op jit(solution)/shard_map/ppermute | solution.py:120
  176.1 46.6 %all-to-all-start.1 = ((bf16[4,4,256,128]{2,3,1,0:T(8,128)(2,1)}), bf16[4,4,256,128]{2,3,1,0:T(8,128)(2,1)S(1)}, u32[]{:S(2)}, u32[]{:S(2)}) async-start(bf16[4,4,256,128]{2,3,1,0:T(8,128)(2,1)} %copy.48), calls=%async_computation.1 | async-start | bytes 2097152 | tf_op jit(solution)/shard_map/all_to_all | solution.py:142
  180.7 23.5 %collective-permute-start.4 = (bf16[4,32,1024]{2,1,0:T(8,128)(2,1)}, bf16[4,32,1024]{2,1,0:T(8,128)(2,1)S(1)}, u32[]{:S(2)}, u32[]{:S(2)}) collective-permute-start(bf16[4,32,1024]{2,1,0:T(8,128)(2,1)} %get-tuple-element.15), channel_id=1, source_target_pairs={{0,4},{4,8},{8,12},{1,5},{5,9},{9,13},{2,6},{6,10},{10,14},{3,7},{... | collective-permute-start | bytes 786440 | tf_op jit(solution)/shard_map/ppermute | solution.py:119
  184.7 24.5 %copy-start.5 = (bf16[4,32,1024]{2,1,0:T(8,128)(2,1)}, bf16[4,32,1024]{2,1,0:T(8,128)(2,1)S(1)}, u32[]{:S(2)}) copy-start(bf16[4,32,1024]{2,1,0:T(8,128)(2,1)S(1)} %collective-permute-done.5.row_high) | copy-start | bytes 786436
  204.2 2.6 copy-start.8
  204.2 4.9 %collective-permute-start.6 = (bf16[6,32,1024]{2,1,0:T(8,128)(2,1)S(1)}, bf16[6,32,1024]{2,1,0:T(8,128)(2,1)S(1)}, u32[]{:S(2)}, u32[]{:S(2)}) collective-permute-start(bf16[6,32,1024]{2,1,0:T(8,128)(2,1)S(1)} %pad_maximum_fusion.2), channel_id=1, source_target_pairs={{0,1},{1,2},{2,3},{4,5},{5,6},{6,7},{8,9},{9,10},{10,11},{12,13},{... | collective-permute-start | bytes 1179656 | tf_op jit(solution)/shard_map/ppermute | solution.py:126
  206.8 4.2 %collective-permute-start.7 = (bf16[6,32,1024]{2,1,0:T(8,128)(2,1)S(1)}, bf16[6,32,1024]{2,1,0:T(8,128)(2,1)}, u32[]{:S(2)}, u32[]{:S(2)}) collective-permute-start(bf16[6,32,1024]{2,1,0:T(8,128)(2,1)S(1)} %pad_maximum_fusion.3), channel_id=1, source_target_pairs={{1,0},{2,1},{3,2},{5,4},{6,5},{7,6},{9,8},{10,9},{11,10},{13,12},{... | collective-permute-start | bytes 1179656 | tf_op jit(solution)/shard_map/ppermute | solution.py:127
  209.2 0.8 copy-start.11
  222.8 36.2 %all-to-all-start.3 = ((bf16[4,4,256,128]{2,3,1,0:T(8,128)(2,1)}), bf16[4,4,256,128]{2,3,1,0:T(8,128)(2,1)S(1)}, u32[]{:S(2)}, u32[]{:S(2)}) async-start(bf16[4,4,256,128]{2,3,1,0:T(8,128)(2,1)} %copy.57), calls=%async_computation.3 | async-start | bytes 2097152 | tf_op jit(solution)/shard_map/all_to_all | solution.py:142
Sparse Core Ops, SparseCore 0:
  9.5 74.9 all-gather.3
  86.1 53.1 all-gather.5

commit v2 on v1

--- a/solution.py
+++ b/solution.py
@@ -54,29 +54,77 @@
     return sums[1] + (before + after)
 
 
-def forward_kernel(own, row_low, row_high, plane_low, plane_high, taps, bias, active, slope, padded):
+def forward_kernel(
+    here, own, row_low, row_high, plane_low, plane_high, taps, bias, weight, *rest
+):
+    count = (len(rest) - 3) // 2
+    inputs, outputs = rest[:count], rest[count : 2 * count]
+    slope, padded, active = rest[2 * count :]
+    step = pl.program_id(0)
+    planes, rows, extent = own.shape[:3]
     fill_padded(padded, own, row_low, row_high, plane_low, plane_high)
-    for z in range(own.shape[0]):
-        for y in range(own.shape[1]):
+    lanes = pl.ds(pl.multiple_of(step * LANES, LANES), LANES)
+    for z in range(planes):
+        for y in range(rows):
             mixed = stencil_row(padded, taps, z, y, False) + bias[0][None, :]
             half = 0.5 * (1.0 + lax.erf(mixed * root_half))
-            active[z, y] = (mixed * half).astype(active.dtype)
+            at = (z * rows + y) * extent
+            active[at : at + extent, lanes] = (mixed * half).astype(active.dtype)
             slope[z, y] = half + mixed * jnp.exp(-0.5 * mixed * mixed) * inv_root_two_pi
 
-
-def backward_kernel(own, row_low, row_high, plane_low, plane_high, taps, out, padded):
+    @pl.when(step == pl.num_programs(0) - 1)
+    def _():
+        own_channels = inputs[0].shape[0]
+        for shift in range(count):
+            start = pl.multiple_of((here[0] ^ shift) * own_channels, own_channels)
+            product = lax.dot_general(
+                weight[pl.ds(start, own_channels), :],
+                active[...],
+                (((1,), (1,)), ((), ())),
+                preferred_element_type=jnp.float32,
+            )
+            total = inputs[shift][...].astype(jnp.float32) + product
+            outputs[shift][...] = total.astype(outputs[shift].dtype)
+
+
+def backward_kernel(here, own, row_low, row_high, plane_low, plane_high, taps, weight, *rest):
+    count = (len(rest) - 2) // 2
+    inputs, outputs = rest[:count], rest[count : 2 * count]
+    padded, grads = rest[2 * count :]
+    step = pl.program_id(0)
+    planes, rows, extent = own.shape[:3]
     fill_padded(padded, own, row_low, row_high, plane_low, plane_high)
-    for z in range(own.shape[0]):
-        for y in range(own.shape[1]):
-            out[z, y] = stencil_row(padded, taps, z, y, True).astype(out.dtype)
-
-
-def stencil(own, halo, taps, bias=None):
+    lanes = pl.ds(pl.multiple_of(step * LANES, LANES), LANES)
+    for z in range(planes):
+        for y in range(rows):
+            at = (z * rows + y) * extent
+            total = stencil_row(padded, taps, z, y, True)
+            grads[at : at + extent, lanes] = total.astype(grads.dtype)
+
+    @pl.when(step == pl.num_programs(0) - 1)
+    def _():
+        own_channels = inputs[0].shape[0]
+        for shift in range(count):
+            start = pl.multiple_of((here[0] ^ shift) * own_channels, own_channels)
+            product = jnp.dot(
+                grads[...],
+                weight[:, pl.ds(start, own_channels)],
+                preferred_element_type=jnp.float32,
+            )
+            total = inputs[shift][...].astype(jnp.float32) + product.T
+            outputs[shift][...] = total.astype(outputs[shift].dtype)
+
+
+def stencil(here, own, halo, taps, bias, weight, blocks):
     planes, rows, extent, channels = own.shape
+    cells = planes * rows * extent
 
     def block(*lead):
         zeros = (0,) * len(lead)
-        return pl.BlockSpec(lead + (LANES,), lambda c: zeros + (c,))
+        return pl.BlockSpec(lead + (LANES,), lambda c, here: zeros + (c,))
+
+    def resident(shape):
+        return pl.BlockSpec(shape, lambda c, here: (0,) * len(shape), pipeline_mode=pl.Buffered(1))
 
     in_specs = [
         block(planes, rows, extent),
@@ -86,26 +134,119 @@
         block(rows + 2, extent),
         block(27),
     ]
-    args = (own,) + halo + (taps,)
-    scratch = [pltpu.VMEM((planes + 2, rows + 2, extent, LANES), jnp.float32)]
-    shape = jax.ShapeDtypeStruct(own.shape, own.dtype)
-    if bias is None:
-        return pl.pallas_call(
-            backward_kernel,
+    args = [own, *halo, taps]
+    out_specs = [resident(piece.shape) for piece in blocks]
+    out_shape = [jax.ShapeDtypeStruct(piece.shape, piece.dtype) for piece in blocks]
+    if bias is not None:
+        in_specs.append(block(1))
+        args.append(bias)
+        out_specs.append(block(planes, rows, extent))
+        out_shape.append(jax.ShapeDtypeStruct(own.shape, jnp.float32))
+    in_specs += [resident(weight.shape)] + [resident(piece.shape) for piece in blocks]
+    return pl.pallas_call(
+        backward_kernel if bias is None else forward_kernel,
+        grid_spec=pltpu.PrefetchScalarGridSpec(
+            num_scalar_prefetch=1,
             grid=(channels // LANES,),
             in_specs=in_specs,
-            out_specs=block(planes, rows, extent),
-            out_shape=shape,
-            scratch_shapes=scratch,
-        )(*args)
+            out_specs=out_specs,
+            scratch_shapes=[
+                pltpu.VMEM((planes + 2, rows + 2, extent, LANES), jnp.float32),
+                pltpu.VMEM((cells, channels), own.dtype),
+            ],
+        ),
+        out_shape=out_shape,
+    )(here, *args, weight, *blocks)
+
+
+def turn_kernel(here, *refs, count):
+    inputs, turned = refs[:count], refs[-1]
+
+    @pl.when(pl.program_id(0) == 0)
+    def _():
+        own = inputs[0].shape[0]
+        for shift in range(count):
+            start = pl.multiple_of((here[0] ^ shift) * own, own)
+            turned[:, pl.ds(start, own)] = inputs[shift][...].T
+
+
+def hidden_kernel(here, *refs, count):
+    turn_kernel(here, *refs, count=count)
+    weight, out, turned = refs[count:]
+    out[...] = lax.dot_general(
+        turned[...],
+        weight[...],
+        (((1,), (1,)), ((), ())),
+        preferred_element_type=jnp.float32,
+    ).astype(out.dtype)
+
+
+def mix_kernel(here, *refs, count):
+    turn_kernel(here, *refs, count=count)
+    weight, slope, out, turned = refs[count:]
+    grad = jnp.dot(turned[...], weight[...], preferred_element_type=jnp.float32)
+    grad = grad.astype(out.dtype).astype(jnp.float32)
+    out[...] = (grad * slope[...]).astype(out.dtype)
+
+
+def product_call(here, blocks, weight, slope=None):
+    own, cells = blocks[0].shape
+    channels = weight.shape[0]
+    count = len(blocks)
+    width = 2 * LANES
+    columns = pl.BlockSpec((cells, width), lambda c, here: (0, c))
+    whole = pl.BlockSpec((own, cells), lambda c, here: (0, 0), pipeline_mode=pl.Buffered(1))
+    if slope is None:
+        kernel, extra = hidden_kernel, []
+        weight_spec = pl.BlockSpec((width, channels), lambda c, here: (c, 0))
+    else:
+        kernel, extra = mix_kernel, [slope]
+        weight_spec = pl.BlockSpec((channels, width), lambda c, here: (0, c))
     return pl.pallas_call(
-        forward_kernel,
-        grid=(channels // LANES,),
-        in_specs=in_specs + [block(1)],
-        out_specs=[block(planes, rows, extent)] * 2,
-        out_shape=[shape, jax.ShapeDtypeStruct(own.shape, jnp.float32)],
-        scratch_shapes=scratch,
-    )(*args, bias)
+        lambda *refs: kernel(*refs, count=count),
+        grid_spec=pltpu.PrefetchScalarGridSpec(
+            num_scalar_prefetch=1,
+            grid=(channels // width,),
+            in_specs=[whole] * count + [weight_spec] + [columns] * len(extra),
+            out_specs=columns,
+            scratch_shapes=[pltpu.VMEM((cells, channels), blocks[0].dtype)],
+        ),
+        out_shape=jax.ShapeDtypeStruct((cells, channels), blocks[0].dtype),
+    )(here, *blocks, weight, *extra)
+
+
+def place_kernel(here, mine, other, full_in, full_out, sems):
+    chan, seat = here[0], here[1]
+    copies = []
+    for side, pieces in enumerate((mine, other)):
+        for turn in range(pieces.shape[0]):
+            for shift in range(pieces.shape[1]):
+                for which, full in enumerate((full_in, full_out)):
+                    copies.append(
+                        pltpu.make_async_copy(
+                            pieces.at[turn, shift, which],
+                            full.at[chan ^ shift, seat ^ side ^ (2 * turn)],
+                            sems.at[len(copies)],
+                        )
+                    )
+    for copy in copies:
+        copy.start()
+    for copy in copies:
+        copy.wait()
+
+
+def place(here, mine, other):
+    turns, parts, _, share, channels = mine.shape
+    full = jax.ShapeDtypeStruct((parts, 2 * turns, share, channels), mine.dtype)
+    anywhere = pl.BlockSpec(memory_space=pl.ANY)
+    found = pl.pallas_call(
+        place_kernel,
+        in_specs=[pl.BlockSpec(memory_space=pltpu.SMEM), anywhere, anywhere],
+        out_specs=[anywhere] * 2,
+        out_shape=[full] * 2,
+        scratch_shapes=[pltpu.SemaphoreType.DMA((4 * turns * parts,))],
+    )(here, mine, other)
+    return [weight.reshape(channels, channels) for weight in found]
 
 
 def shift_pairs(axis):
@@ -114,76 +255,99 @@
     return forward, [(target, source) for source, target in forward]
 
 
-def halo_of(field):
-    forward, backward = shift_pairs("chan")
-    row_low = lax.ppermute(field[:, -1], "chan", forward)
-    row_high = lax.ppermute(field[:, 0], "chan", backward)
-    forward, backward = shift_pairs("space")
-
-    def plane(z):
-        return jnp.concatenate([row_low[z][None], field[z], row_high[z][None]], axis=0)
-
-    plane_low = lax.ppermute(plane(-1), "space", forward)
-    plane_high = lax.ppermute(plane(0), "space", backward)
-    return row_low, row_high, plane_low, plane_high
-
-
 def split_cells_body(volume, out_grad, weight_in, weight_out, filter_taps, filter_bias):
     own, planes, cells = volume.shape
     parts = lax.axis_size("chan")
     rows = CY // parts
+    width = rows * CX
     channels = own * parts
-
-    def to_cells(field):
-        blocks = field.reshape(own, planes, parts, rows * CX).transpose(2, 1, 0, 3)
-        return lax.all_to_all(blocks, "chan", split_axis=0, concat_axis=0, tiled=True)
-
-    def to_channels(blocks):
-        back = lax.all_to_all(blocks, "chan", split_axis=0, concat_axis=0, tiled=True)
-        return back.transpose(2, 1, 0, 3).reshape(own, planes, cells)
-
-    def gather(part):
-        return lax.all_gather(part, "chan", axis=0, tiled=True)
-
-    full_in, full_out = gather(weight_in), gather(weight_out)
-    taps = gather(filter_taps).T
-    bias = gather(filter_bias)[None, :]
+    others = ("groups", "space")
+    seat = lax.axis_index(others)
+    chan = lax.axis_index("chan")
+    share = own // lax.axis_size(others)
+    here = jnp.stack([chan, seat]).astype(jnp.int32)
+    shifts = sorted(range(1, parts), key=lambda shift: (shift & (parts // 2) == 0, shift))
+
+    def swap(part, axes, partner):
+        count = lax.axis_size(axes)
+        return lax.ppermute(part, axes, [(i, partner(i)) for i in range(count)])
+
+    def exchange(blocks):
+        got = {0: blocks(0)}
+        for shift in shifts:
+            got[shift] = swap(blocks(shift), "chan", lambda i: i ^ shift)
+        return [got[shift] for shift in range(parts)]
+
+    def cut(field):
+        def blocks(shift):
+            start = (chan ^ shift) * width
+            piece = lax.dynamic_slice_in_dim(field, start, width, axis=2)
+            return piece.reshape(own, planes * width)
+
+        return blocks
+
+    def paste(pieces):
+        field = jnp.zeros((own, planes, cells), pieces[0].dtype)
+        for shift in [0] + shifts:
+            piece = pieces[shift].reshape(own, planes, width)
+            field = lax.dynamic_update_slice_in_dim(field, piece, (chan ^ shift) * width, axis=2)
+        return field
+
+    def gather_weights():
+        begin = seat * share
+        pair = jnp.stack(
+            [
+                lax.dynamic_slice_in_dim(weight, begin, share, axis=0)
+                for weight in (weight_in, weight_out)
+            ]
+        )
+        column = jnp.stack(exchange(lambda shift: pair))
+        over_x = swap(column, others, lambda i: i ^ 2)
+        over_y = swap(column, others, lambda i: i ^ 4)
+        mixed = jnp.where(seat & 1 == 0, over_y, over_x)
+        far = swap(mixed, others, lambda i: i ^ (4 if i & 1 else 2))
+        mine = jnp.stack([column, over_x, over_y, far])
+        other = swap(mine, others, lambda i: i ^ 1)
+        return place(here, mine, other)
+
+    def gather_taps():
+        table = jnp.concatenate([filter_taps, filter_bias[:, None]], axis=1).T
+        found = exchange(lambda shift: table)
+        full = jnp.zeros((28, channels), jnp.float32)
+        for shift in range(parts):
+            full = lax.dynamic_update_slice_in_dim(full, found[shift], (chan ^ shift) * own, axis=1)
+        return full[:27], full[27:]
+
+    def halo_of(field):
+        forward, backward = shift_pairs("chan")
+        row_low = lax.ppermute(field[:, -1], "chan", forward)
+        row_high = lax.ppermute(field[:, 0], "chan", backward)
+        forward, backward = shift_pairs("space")
+
+        def plane(z):
+            return jnp.concatenate([row_low[z][None], field[z], row_high[z][None]], axis=0)
+
+        plane_low = lax.ppermute(plane(-1), "space", forward)
+        plane_high = lax.ppermute(plane(0), "space", backward)
+        return row_low, row_high, plane_low, plane_high
+
     grid = (planes, rows, CX, channels)
-
-    vol_cells = to_cells(volume)
-    hidden = jnp.einsum(
-        "kzcl,okc->zlo",
-        vol_cells,
-        full_in.reshape(channels, parts, own),
-        preferred_element_type=jnp.float32,
-    ).astype(jnp.bfloat16)
-    hidden = hidden.reshape(grid)
-    active, slope = stencil(hidden, halo_of(hidden), taps, bias)
-    out_cells = jnp.einsum(
-        "kcd,zld->kzcl",
-        full_out.reshape(parts, own, channels),
-        active.reshape(planes, rows * CX, channels),
-        preferred_element_type=jnp.float32,
-    )
-    block_out = to_channels((vol_cells.astype(jnp.float32) + out_cells).astype(jnp.bfloat16))
-
-    grad_cells = to_cells(out_grad)
-    act_grad = jnp.einsum(
-        "kzcl,kcd->zld",
-        grad_cells,
-        full_out.reshape(parts, own, channels),
-        preferred_element_type=jnp.float32,
-    ).astype(jnp.bfloat16)
-    mix_grad = (act_grad.reshape(grid).astype(jnp.float32) * slope).astype(jnp.bfloat16)
-    hid_grad = stencil(mix_grad, halo_of(mix_grad), taps)
-    back_cells = jnp.einsum(
-        "dkc,zld->kzcl",
-        full_in.reshape(channels, parts, own),
-        hid_grad.reshape(planes, rows * CX, channels),
-        preferred_element_type=jnp.float32,
-    )
-    volume_grad = to_channels((grad_cells.astype(jnp.float32) + back_cells).astype(jnp.bfloat16))
+    full_in, full_out = gather_weights()
+    taps, bias = gather_taps()
+    vol_blocks = exchange(cut(volume))
+    grad_blocks = exchange(cut(out_grad))
+    hidden = in_grid(product_call(here, vol_blocks, full_in), grid)
+    *out_blocks, slope = stencil(here, hidden, halo_of(hidden), taps, bias, full_out, vol_blocks)
+    block_out = paste(exchange(lambda shift: out_blocks[shift]))
+    mix_grad = product_call(here, grad_blocks, full_out, slope.reshape(planes * width, channels))
+    mix_grad = in_grid(mix_grad, grid)
+    back_blocks = stencil(here, mix_grad, halo_of(mix_grad), taps, None, full_in, grad_blocks)
+    volume_grad = paste(exchange(lambda shift: back_blocks[shift]))
     return block_out, volume_grad
+
+
+def in_grid(field, grid):
+    return field.reshape(grid)
 
 
 def with_halo(block, axis, dim):
@@ -267,13 +431,22 @@
     return block_out, volume_grad
 
 
+def body(volume, out_grad, weight_in, weight_out, filter_taps, filter_bias):
+    own = volume.shape[0]
+    parts = lax.axis_size("chan")
+    groups, space = lax.axis_size("groups"), lax.axis_size("space")
+    whole_rows = CY % parts == 0 and (CY // parts * CX) % LANES == 0 and parts & (parts - 1) == 0
+    whole_shares = own % LANES == 0 and own % (16 * groups * space) == 0
+    split = whole_rows and whole_shares and (groups, space) == (2, 4)
+    chosen = split_cells_body if split else exchange_body
+    return chosen(volume, out_grad, weight_in, weight_out, filter_taps, filter_bias)
+
+
 def solution(mesh):
     field = P(("groups", "chan"), "space", None)
     placed = (field, field, P("chan", None), P("chan", None), P("chan", None), P("chan"))
-    parts = mesh.shape["chan"]
-    whole_rows = CY % parts == 0 and (CY // parts * CX) % LANES == 0
     return jax.shard_map(
-        split_cells_body if whole_rows else exchange_body,
+        body,
         mesh=mesh,
         in_specs=placed,
         out_specs=(field, field),

time: 270 us -> 329 us (1.22)
  Pallas kernels: 16 us -> 164 us
  blocking collectives: 36.2 us -> 0 us
  waiting for transfers between devices: 112 us -> 78.3 us
  between operations: 14.4 us -> 1.23 us
  matrix products: 11.2 us -> 0 us
  local copies, waits for them, and re-layouts: 15.5 us -> 25.4 us
  starting transfers between devices: 58.1 us -> 54.3 us
    pallas_call x2 -> x5, Pallas kernels: 16 us -> 164 us  [the longest x1 129 us: place(): pl.pallas_call(place_kernel, in_specs=[pl.BlockSpec(memory_space=pltpu.SM...]
    all_to_all x4 -> x0, waiting for transfers between devices: 74.7 us -> none  [the longest x2 51.4 us: to_cells(): lax.all_to_all(blocks, 'chan', split_axis=0, concat_axis=0, tiled=True)]
    ppermute x0 -> x22, waiting for transfers between devices: none -> 66 us  [swap(): return lax.ppermute(part, axes, [(i, partner(i)) for i in range(count)])]
    all_gather x2 -> x0, blocking collectives: 36.2 us -> none  [gather(): return lax.all_gather(part, 'chan', axis=0, tiled=True)]
    ppermute x0 -> x22, starting transfers between devices: none -> 33.9 us  [swap(): return lax.ppermute(part, axes, [(i, partner(i)) for i in range(count)])]
    all_to_all x4 -> x0, starting transfers between devices: 25.4 us -> none  [the longest x2 15.6 us: to_channels(): lax.all_to_all(blocks, 'chan', split_axis=0, concat_axis=0, tiled=True)]
    ppermute x2, waiting for transfers between devices: 26.3 us -> 3.87 us  [halo_of(): row_low = lax.ppermute(field[:, -1], 'chan', forward)]
    ppermute x2, starting transfers between devices: 23.7 us -> 8.98 us  [halo_of(): row_low = lax.ppermute(field[:, -1], 'chan', forward)]
  transfers between devices with their start and end apart: 14 -> 30, of which waited for: 6 -> 13; matrix products, arithmetic and copies ran while one was open for 8% -> 6% of each run, Pallas kernels for 3% -> 47%
where the time goes in v2:
time: 329 us; the launch traced here: 327 us
  Pallas kernels  164 us (50%)
  waiting for transfers between devices  78.3 us (24%)
  starting transfers between devices  54.3 us (17%)
  local copies, waits for them, and re-layouts  25.4 us (8%)
  other arithmetic  3.82 us (1%)
    pallas_call x1, Pallas kernels, place(): pl.pallas_call(place_kernel, in_specs=[pl.BlockSpec(memory_space=pltpu.SM...  129 us
    ppermute x22, waiting for transfers between devices, swap(): return lax.ppermute(part, axes, [(i, partner(i)) for i in range(count)])  66 us
    ppermute x22, starting transfers between devices, swap(): return lax.ppermute(part, axes, [(i, partner(i)) for i in range(count)])  33.9 us
    pallas_call x2, Pallas kernels, stencil(): pl.pallas_call(backward_kernel if bias is None else forward_kernel, grid_...  22.8 us
    pallas_call x2, Pallas kernels, product_call(): pl.pallas_call(lambda *refs: kernel(*refs, count=count), grid_spec=pltpu....  11.9 us
    unnamed x56, local copies, waits for them, and re-layouts  10.2 us
    ppermute x2, starting transfers between devices, halo_of(): row_low = lax.ppermute(field[:, -1], 'chan', forward)  8.98 us
    ppermute x2, waiting for transfers between devices, halo_of(): row_high = lax.ppermute(field[:, 0], 'chan', backward)  8.46 us
  transfers between devices with their start and end apart: 30, of which 13 were waited for; matrix products, arithmetic and copies ran while one was open for 6% of the time, Pallas kernels for 47%

profile of v2, /device:TPU:0, one launch (start us, length us, event | category | flops | bytes accessed | tf_op | source)
XLA Modules:
  0.0 327.2 jit_solution(14621740872002448174)
XLA Ops:
  0.6 0.9 dynamic-slice_bitcast_fusion
  1.6 3.1 collective-permute-start.3
  4.7 2.6 collective-permute-start.4
  7.3 2.5 collective-permute-done.3
  9.7 7.8 %collective-permute-done.4 = bf16[2,32,1024]{2,1,0:T(8,128)(2,1)S(1)} collective-permute-done((bf16[2,32,1024]{2,1,0:T(8,128)(2,1)S(1)}, bf16[2,32,1024]{2,1,0:T(8,128)(2,1)S(1)}, u32[]{:S(2)}, u32[]{:S(2)}) %collective-permute-start.4) | collective-permute-done | bytes 131104 | tf_op jit(solution)/shard_map/ppermute | solution.py:273
  17.7 1.6 collective-permute-start.6
  19.2 1.5 collective-permute-start.7
  20.7 8.3 %collective-permute-done.6 = bf16[4,2,32,1024]{3,2,1,0:T(8,128)(2,1)S(1)} collective-permute-done((bf16[4,2,32,1024]{3,2,1,0:T(8,128)(2,1)S(1)}, bf16[4,2,32,1024]{3,2,1,0:T(8,128)(2,1)S(1)}, u32[]{:S(2)}, u32[]{:S(2)}) %collective-permute-start.6) | collective-permute-done | bytes 524320 | tf_op jit(solution)/shard_map/ppermute | solution.py:273
  29.0 2.2 collective-permute-done.7
  31.8 8.7 %collective-permute-done.8 = bf16[4,2,32,1024]{3,2,1,0:T(8,128)(2,1)S(1)} collective-permute-done((bf16[4,2,32,1024]{3,2,1,0:T(8,128)(2,1)S(1)}, bf16[4,2,32,1024]{3,2,1,0:T(8,128)(2,1)S(1)}, u32[]{:S(2)}, u32[]{:S(2)}) %collective-permute-start.8) | collective-permute-done | bytes 524320 | tf_op jit(solution)/shard_map/ppermute | solution.py:273
  40.5 1.3 pad_maximum_fusion.mine
  41.9 3.7 %constant_dynamic-slice_fusion = (bf16[256,4,128]{2,1,0:T(4,128)(2,1)S(1)}, bf16[256,4,128]{2,1,0:T(4,128)(2,1)}, bf16[256,4,128]{2,1,0:T(4,128)(2,1)S(1)}, bf16...) fusion(bf16[256,4,512]{2,1,0:T(4,128)(2,1)} %param.7, ...), kind=kLoop, calls=%fused_computation.27 | loop fusion | bytes 4194320 | tf_op jit(solution)/shard_map/dynamic_slice | solution.py:284
  45.6 0.7 copy.40
  46.3 2.3 collective-permute-start
  48.6 0.7 copy.39
  49.4 1.2 collective-permute-start.1
  50.6 0.8 copy.38
  51.3 1.5 collective-permute-start.2
  52.8 0.8 copy.41
  54.2 129.4 %shard_map.77 = (bf16[4,8,32,1024]{3,2,1,0:T(8,128)(2,1)}, bf16[4,8,32,1024]{3,2,1,0:T(8,128)(2,1)}) custom-call(s32[2]{0:T(128)} %pad_add_fusion.here.refs_0_, bf16[4,4,2,32,1024]{4,3,2,1,0:T(8,128)(2,1)} %copy-done, bf16[4,4,2,32,1024]{4,3,2,1,0:T(8,128)(2,1)} %collective-permute-done.9.other), custom_call_target="tpu_custom_call" | custom-call | tf_op jit(solution)/shard_map/pallas_call | solution.py:242
  184.5 5.8 %shard_map.78 = bf16[512,1024]{1,0:T(8,128)(2,1)} custom-call(s32[2]{0:T(128)} %pad_add_fusion.here.refs_0_, bf16[256,512]{1,0:T(8,128)(2,1)} %bitcast.86, bf16[256,512]{1,0:T(8,128)(2,1)} %copy-done.3, bf16[256,512]{1,0:T(8,128)(2,1)} %copy-done.4, bf16[256,512]{1,0:T(8,128)(2,1)} %copy-done.5, bf16[1024,1024]{1,0:T(8,128)(2,1)} %bitcast.82), custom_call_target="tpu_custom_call" | custom-call | tf_op jit(solution)/shard_map/pallas_call | solution.py:205
  190.3 1.1 slice_bitcast_fusion.2
  191.5 2.9 collective-permute-start.10
  194.3 1.3 collective-permute-start.11
  195.6 1.1 fusion.3
  196.7 2.3 collective-permute-done.10.row_low
  199.1 4.1 %collective-permute-done.11.row_high = bf16[4,32,1024]{2,1,0:T(8,128)(2,1)S(1)} collective-permute-done((bf16[4,32,1024]{2,1,0:T(8,128)(2,1)S(1)}, bf16[4,32,1024]{2,1,0:T(8,128)(2,1)S(1)}, u32[]{:S(2)}, u32[]{:S(2)}) %collective-permute-start.11) | collective-permute-done | bytes 262176 | tf_op jit(solution)/shard_map/ppermute | solution.py:324
  203.2 1.3 collective-permute-start.13
  204.5 0.8 pad_maximum_fusion.2
  205.3 3.0 collective-permute-start.12
  208.4 1.8 collective-permute-start.14
  210.9 2.0 collective-permute-start.16
  212.9 0.7 copy.36
  213.6 0.8 copy.35
  214.4 0.7 copy.37
  215.2 0.9 collective-permute-start.20
  216.1 1.6 collective-permute-start.21
  217.7 2.0 collective-permute-start.22
  220.4 0.7 copy-done.17
  221.2 11.8 %shard_map.79 = (bf16[256,512]{1,0:T(8,128)(2,1)}, bf16[256,512]{1,0:T(8,128)(2,1)}, bf16[256,512]{1,0:T(8,128)(2,1)}, bf16[256,512]{1,0:T(8,128)(2,1)}, f32[4,4,32,1024]{3,2,1,0:T(8,128)}) custom-call(s32[2]{0:T(128)} %pad_add_fusion.here.refs_0_, bf16[4,4,32,1024]{3,2,1,0:T(8,128)(2,1)} %bitcast.79, bf16[4,32,1024]{2,1,0:T(8,128)(2,1)} %copy-done.13, ...), custom_call_target="tpu_custom_call" | custom-call | tf_op jit(solution)/shard_map/pallas_call | solution.py:146
  233.0 4.6 %collective-permute-done.21.refs_3_.rest_2_ = bf16[256,512]{1,0:T(8,128)(2,1)S(1)} collective-permute-done((bf16[256,512]{1,0:T(8,128)(2,1)}, bf16[256,512]{1,0:T(8,128)(2,1)S(1)}, u32[]{:S(2)}, u32[]{:S(2)}) %collective-permute-start.21) | collective-permute-done | bytes 262176 | tf_op jit(solution)/shard_map/ppermute | solution.py:273
  238.4 6.1 %shard_map.80 = bf16[512,1024]{1,0:T(8,128)(2,1)} custom-call(s32[2]{0:T(128)} %pad_add_fusion.here.refs_0_, bf16[256,512]{1,0:T(8,128)(2,1)} %bitcast.88, bf16[256,512]{1,0:T(8,128)(2,1)} %copy-done.6, bf16[256,512]{1,0:T(8,128)(2,1)} %copy-done.7, bf16[256,512]{1,0:T(8,128)(2,1)} %copy-done.8, bf16[1024,1024]{1,0:T(8,128)(2,1)} %bitcast.85, ...), custom_call_target="tpu_custom_call" | custom-call | tf_op jit(solution)/shard_map/pallas_call | solution.py:205
  244.5 1.1 slice_bitcast_fusion
  245.6 6.1 %collective-permute-start.23 = (bf16[4,32,1024]{2,1,0:T(8,128)(2,1)S(1)}, bf16[4,32,1024]{2,1,0:T(8,128)(2,1)S(1)}, u32[]{:S(2)}, u32[]{:S(2)}) collective-permute-start(bf16[4,32,1024]{2,1,0:T(8,128)(2,1)S(1)} %get-tuple-element.29), channel_id=1, source_target_pairs={{0,4},{4,8},{8,12},{1,5},{5,9},{9,13},{2,6},{6,10},{10,14},{3,7},{... | collective-permute-start | bytes 786440 | tf_op jit(solution)/shard_map/ppermute | solution.py:323
  251.8 1.3 collective-permute-start.24
  253.1 1.1 fusion.2
  254.1 1.5 collective-permute-done.23.row_low
  255.7 4.3 %collective-permute-done.24.row_high = bf16[4,32,1024]{2,1,0:T(8,128)(2,1)S(1)} collective-permute-done((bf16[4,32,1024]{2,1,0:T(8,128)(2,1)S(1)}, bf16[4,32,1024]{2,1,0:T(8,128)(2,1)S(1)}, u32[]{:S(2)}, u32[]{:S(2)}) %collective-permute-start.24) | collective-permute-done | bytes 262176 | tf_op jit(solution)/shard_map/ppermute | solution.py:324
  260.1 1.3 collective-permute-start.26
  261.4 0.8 pad_maximum_fusion.4
  262.2 3.2 collective-permute-start.25
  266.1 2.9 collective-permute-start.18
  269.7 17.2 %collective-permute-done.17 = bf16[256,512]{1,0:T(8,128)(2,1)} collective-permute-done((bf16[256,512]{1,0:T(8,128)(2,1)}, bf16[256,512]{1,0:T(8,128)(2,1)}, u32[]{:S(2)}, u32[]{:S(2)}) %collective-permute-start.17) | collective-permute-done | bytes 262176 | tf_op jit(solution)/shard_map/ppermute | solution.py:273
  286.9 1.0 reshape.83
  287.9 1.0 reshape.84
  289.2 0.8 copy-done.19
  289.9 0.7 copy-done.20
  290.7 11.0 %shard_map.81 = (bf16[256,512]{1,0:T(8,128)(2,1)}, bf16[256,512]{1,0:T(8,128)(2,1)}, bf16[256,512]{1,0:T(8,128)(2,1)}, bf16[256,512]{1,0:T(8,128)(2,1)}) custom-call(s32[2]{0:T(128)} %pad_add_fusion.here.refs_0_, bf16[4,4,32,1024]{3,2,1,0:T(8,128)(2,1)} %bitcast.81, bf16[4,32,1024]{2,1,0:T(8,128)(2,1)} %copy-done.15, bf16[4,32,1024]{2,1,0:T(8,128)(2,1)} %copy-done.16, ...), custom_call_target="tpu_custom_call" | custom-call | tf_op jit(solution)/shard_map/pallas_call | solution.py:146
  301.6 3.9 %collective-permute-start.27 = (bf16[256,512]{1,0:T(8,128)(2,1)}, bf16[256,512]{1,0:T(8,128)(2,1)S(1)}, u32[]{:S(2)}, u32[]{:S(2)}) collective-permute-start(bf16[256,512]{1,0:T(8,128)(2,1)} %get-tuple-element.21), channel_id=1, source_target_pairs={{0,8},{4,12},{8,0},{12,4},{1,9},{5,13},{9,1},{13,5},{2,10},{6,14},... | collective-permute-start | bytes 786440 | tf_op jit(solution)/shard_map/ppermute | solution.py:273
  305.5 3.0 collective-permute-start.28
  309.0 1.2 reshape.92
  310.7 13.5 %collective-permute-done.27 = bf16[256,512]{1,0:T(8,128)(2,1)S(1)} collective-permute-done((bf16[256,512]{1,0:T(8,128)(2,1)}, bf16[256,512]{1,0:T(8,128)(2,1)S(1)}, u32[]{:S(2)}, u32[]{:S(2)}) %collective-permute-start.27) | collective-permute-done | bytes 262176 | tf_op jit(solution)/shard_map/ppermute | solution.py:273
  324.7 1.3 collective-permute-done.29
  326.3 1.0 copy-done.9
  (100 shorter events, 8.1 us)
Async XLA Ops:
  1.6 8.2 %collective-permute-start.3 = (bf16[2,32,1024]{2,1,0:T(8,128)(2,1)S(1)}, bf16[2,32,1024]{2,1,0:T(8,128)(2,1)S(1)}, u32[]{:S(2)}, u32[]{:S(2)}) collective-permute-start(bf16[2,32,1024]{2,1,0:T(8,128)(2,1)S(1)} %get-tuple-element.53), channel_id=1, source_target_pairs={{0,4},{4,0},{8,12},{12,8},{1,5},{5,1},{9,13},{13,9},{2,6},{6,2},{1... | collective-permute-start | bytes 393224 | tf_op jit(solution)/shard_map/ppermute | solution.py:273
  4.7 12.9 %collective-permute-start.4 = (bf16[2,32,1024]{2,1,0:T(8,128)(2,1)S(1)}, bf16[2,32,1024]{2,1,0:T(8,128)(2,1)S(1)}, u32[]{:S(2)}, u32[]{:S(2)}) collective-permute-start(bf16[2,32,1024]{2,1,0:T(8,128)(2,1)S(1)} %get-tuple-element.53), channel_id=1, source_target_pairs={{0,8},{4,12},{8,0},{12,4},{1,9},{5,13},{9,1},{13,5},{2,10},{6,14},... | collective-permute-start | bytes 393224 | tf_op jit(solution)/shard_map/ppermute | solution.py:273
  7.3 10.3 %collective-permute-start.5 = (bf16[2,32,1024]{2,1,0:T(8,128)(2,1)S(1)}, bf16[2,32,1024]{2,1,0:T(8,128)(2,1)S(1)}, u32[]{:S(2)}, u32[]{:S(2)}) collective-permute-start(bf16[2,32,1024]{2,1,0:T(8,128)(2,1)S(1)} %get-tuple-element.53), channel_id=1, source_target_pairs={{0,12},{4,8},{8,4},{12,0},{1,13},{5,9},{9,5},{13,1},{2,14},{6,10},... | collective-permute-start | bytes 393224 | tf_op jit(solution)/shard_map/ppermute | solution.py:273
  17.7 11.3 %collective-permute-start.6 = (bf16[4,2,32,1024]{3,2,1,0:T(8,128)(2,1)S(1)}, bf16[4,2,32,1024]{3,2,1,0:T(8,128)(2,1)S(1)}, u32[]{:S(2)}, u32[]{:S(2)}) collective-permute-start(bf16[4,2,32,1024]{3,2,1,0:T(8,128)(2,1)S(1)} %get-tuple-element.43), channel_id=1, source_target_pairs={{0,2},{1,3},{2,0},{3,1},{16,18},{17,19},{18,16},{19,17},{4,6},{5,7... | collective-permute-start | bytes 1572872 | tf_op jit(solution)/shard_map/ppermute | solution.py:273
  19.2 12.0 %collective-permute-start.7 = (bf16[4,2,32,1024]{3,2,1,0:T(8,128)(2,1)S(1)}, bf16[4,2,32,1024]{3,2,1,0:T(8,128)(2,1)S(1)}, u32[]{:S(2)}, u32[]{:S(2)}) collective-permute-start(bf16[4,2,32,1024]{3,2,1,0:T(8,128)(2,1)S(1)} %get-tuple-element.43), channel_id=1, source_target_pairs={{0,16},{1,17},{2,18},{3,19},{16,0},{17,1},{18,2},{19,3},{4,20},{5,... | collective-permute-start | bytes 1572872 | tf_op jit(solution)/shard_map/ppermute | solution.py:273
  31.2 9.3 %copy-start.1 = (bf16[4,2,32,1024]{3,2,1,0:T(8,128)(2,1)}, bf16[4,2,32,1024]{3,2,1,0:T(8,128)(2,1)S(1)}, u32[]{:S(2)}) copy-start(bf16[4,2,32,1024]{3,2,1,0:T(8,128)(2,1)S(1)} %collective-permute-done.7) | copy-start | bytes 1572868
  31.2 9.2 %collective-permute-start.8 = (bf16[4,2,32,1024]{3,2,1,0:T(8,128)(2,1)S(1)}, bf16[4,2,32,1024]{3,2,1,0:T(8,128)(2,1)S(1)}, u32[]{:S(2)}, u32[]{:S(2)}) collective-permute-start(bf16[4,2,32,1024]{3,2,1,0:T(8,128)(2,1)S(1)} %broadcast_select_fusion), channel_id=1, source_target_pairs={{0,2},{1,17},{2,0},{3,19},{16,18},{17,1},{18,16},{19,3},{4,6},{5,2... | collective-permute-start | bytes 1572872 | tf_op jit(solution)/shard_map/ppermute | solution.py:273
  41.8 3.8 %copy-start = (bf16[4,4,2,32,1024]{4,3,2,1,0:T(8,128)(2,1)}, bf16[4,4,2,32,1024]{4,3,2,1,0:T(8,128)(2,1)S(1)}, u32[]{:S(2)}) copy-start(bf16[4,4,2,32,1024]{4,3,2,1,0:T(8,128)(2,1)S(1)} %pad_maximum_fusion.mine) | copy-start | bytes 6291460
  41.8 12.4 %collective-permute-start.9 = (bf16[4,4,2,32,1024]{4,3,2,1,0:T(8,128)(2,1)S(1)}, bf16[4,4,2,32,1024]{4,3,2,1,0:T(8,128)(2,1)}, u32[]{:S(2)}, u32[]{:S(2)}) collective-permute-start(bf16[4,4,2,32,1024]{4,3,2,1,0:T(8,128)(2,1)S(1)} %pad_maximum_fusion.mine), channel_id=1, source_target_pairs={{0,1},{1,0},{2,3},{3,2},{16,17},{17,16},{18,19},{19,18},{4,5},{5,4... | collective-permute-start | bytes 6291464 | tf_op jit(solution)/shard_map/ppermute | solution.py:273
  46.3 137.3 %collective-permute-start = (bf16[256,512]{1,0:T(8,128)(2,1)}, bf16[256,512]{1,0:T(8,128)(2,1)S(1)}, u32[]{:S(2)}, u32[]{:S(2)}) collective-permute-start(bf16[256,512]{1,0:T(8,128)(2,1)} %bitcast.75), channel_id=1, source_target_pairs={{0,4},{4,0},{8,12},{12,8},{1,5},{5,1},{9,13},{13,9},{2,6},{6,2},{1... | collective-permute-start | bytes 786440 | tf_op jit(solution)/shard_map/ppermute | solution.py:273
  49.4 134.3 %collective-permute-start.1 = (bf16[256,512]{1,0:T(8,128)(2,1)}, bf16[256,512]{1,0:T(8,128)(2,1)S(1)}, u32[]{:S(2)}, u32[]{:S(2)}) collective-permute-start(bf16[256,512]{1,0:T(8,128)(2,1)} %bitcast.74), channel_id=1, source_target_pairs={{0,8},{4,12},{8,0},{12,4},{1,9},{5,13},{9,1},{13,5},{2,10},{6,14},... | collective-permute-start | bytes 786440 | tf_op jit(solution)/shard_map/ppermute | solution.py:273
  51.3 132.3 %collective-permute-start.2 = (bf16[256,512]{1,0:T(8,128)(2,1)}, bf16[256,512]{1,0:T(8,128)(2,1)S(1)}, u32[]{:S(2)}, u32[]{:S(2)}) collective-permute-start(bf16[256,512]{1,0:T(8,128)(2,1)} %bitcast.73), channel_id=1, source_target_pairs={{0,12},{4,8},{8,4},{12,0},{1,13},{5,9},{9,5},{13,1},{2,14},{6,10},... | collective-permute-start | bytes 786440 | tf_op jit(solution)/shard_map/ppermute | solution.py:273
  183.6 0.7 copy-start.3
  183.6 0.8 copy-start.4
  183.7 0.8 copy-start.5
  190.3 18.1 %copy-start.22 = (f32[256,27]{0,1:T(8,128)S(1)}, f32[256,27]{0,1:T(8,128)}, u32[]{:S(2)}) copy-start(f32[256,27]{0,1:T(8,128)} %param.10) | copy-start | bytes 82948
  190.3 18.1 %copy-start.23 = (f32[256]{0:T(256)S(1)}, f32[256]{0:T(256)}, u32[]{:S(2)}) copy-start(f32[256]{0:T(256)} %param.11) | copy-start | bytes 3076
  190.3 22.6 %copy-start.12 = (bf16[256,4,128]{2,1,0:T(4,128)(2,1)S(1)}, bf16[256,4,128]{2,1,0:T(4,128)(2,1)}, u32[]{:S(2)}) copy-start(bf16[256,4,128]{2,1,0:T(4,128)(2,1)} %get-tuple-element.31) | copy-start | bytes 786436
  191.4 22.2 %copy-start.11 = (bf16[256,4,128]{2,1,0:T(4,128)(2,1)S(1)}, bf16[256,4,128]{2,1,0:T(4,128)(2,1)}, u32[]{:S(2)}) copy-start(bf16[256,4,128]{2,1,0:T(4,128)(2,1)} %get-tuple-element.33) | copy-start | bytes 786436
  191.5 7.6 %collective-permute-start.10 = (bf16[4,32,1024]{2,1,0:T(8,128)(2,1)S(1)}, bf16[4,32,1024]{2,1,0:T(8,128)(2,1)S(1)}, u32[]{:S(2)}, u32[]{:S(2)}) collective-permute-start(bf16[4,32,1024]{2,1,0:T(8,128)(2,1)S(1)} %get-tuple-element.37), channel_id=1, source_target_pairs={{0,4},{4,8},{8,12},{1,5},{5,9},{9,13},{2,6},{6,10},{10,14},{3,7},{... | collective-permute-start | bytes 786440 | tf_op jit(solution)/shard_map/ppermute | solution.py:323
  194.3 8.8 %collective-permute-start.11 = (bf16[4,32,1024]{2,1,0:T(8,128)(2,1)S(1)}, bf16[4,32,1024]{2,1,0:T(8,128)(2,1)S(1)}, u32[]{:S(2)}, u32[]{:S(2)}) collective-permute-start(bf16[4,32,1024]{2,1,0:T(8,128)(2,1)S(1)} %get-tuple-element.36), channel_id=1, source_target_pairs={{4,0},{8,4},{12,8},{5,1},{9,5},{13,9},{6,2},{10,6},{14,10},{7,3},{... | collective-permute-start | bytes 786440 | tf_op jit(solution)/shard_map/ppermute | solution.py:324
  199.0 16.1 %copy-start.13 = (bf16[4,32,1024]{2,1,0:T(8,128)(2,1)}, bf16[4,32,1024]{2,1,0:T(8,128)(2,1)S(1)}, u32[]{:S(2)}) copy-start(bf16[4,32,1024]{2,1,0:T(8,128)(2,1)S(1)} %collective-permute-done.10.row_low) | copy-start | bytes 786436
  203.2 12.0 %copy-start.14 = (bf16[4,32,1024]{2,1,0:T(8,128)(2,1)}, bf16[4,32,1024]{2,1,0:T(8,128)(2,1)S(1)}, u32[]{:S(2)}) copy-start(bf16[4,32,1024]{2,1,0:T(8,128)(2,1)S(1)} %collective-permute-done.11.row_high) | copy-start | bytes 786436
  203.2 17.1 %collective-permute-start.13 = (bf16[6,32,1024]{2,1,0:T(8,128)(2,1)S(1)}, bf16[6,32,1024]{2,1,0:T(8,128)(2,1)S(1)}, u32[]{:S(2)}, u32[]{:S(2)}) collective-permute-start(bf16[6,32,1024]{2,1,0:T(8,128)(2,1)S(1)} %pad_maximum_fusion.3), channel_id=1, source_target_pairs={{1,0},{2,1},{3,2},{5,4},{6,5},{7,6},{9,8},{10,9},{11,10},{13,12},{... | collective-permute-start | bytes 1179656 | tf_op jit(solution)/shard_map/ppermute | solution.py:331
  205.3 15.0 %collective-permute-start.12 = (bf16[6,32,1024]{2,1,0:T(8,128)(2,1)}, bf16[6,32,1024]{2,1,0:T(8,128)(2,1)S(1)}, u32[]{:S(2)}, u32[]{:S(2)}) collective-permute-start(bf16[6,32,1024]{2,1,0:T(8,128)(2,1)} %pad_maximum_fusion.2), channel_id=1, source_target_pairs={{0,1},{1,2},{2,3},{4,5},{5,6},{6,7},{8,9},{9,10},{10,11},{12,13},{... | collective-permute-start | bytes 1179656 | tf_op jit(solution)/shard_map/ppermute | solution.py:330
  208.4 6.7 %collective-permute-start.14 = (f32[28,256]{1,0:T(8,128)S(1)}, f32[28,256]{1,0:T(8,128)S(1)}, u32[]{:S(2)}, u32[]{:S(2)}) collective-permute-start(f32[28,256]{1,0:T(8,128)S(1)} %get-tuple-element.25), channel_id=1, source_target_pairs={{0,4},{4,0},{8,12},{12,8},{1,5},{5,1},{9,13},{13,9},{2,6},{6,2},{1... | collective-permute-start | bytes 86024 | tf_op jit(solution)/shard_map/ppermute | solution.py:273
  210.2 5.8 %collective-permute-start.15 = (f32[28,256]{1,0:T(8,128)S(1)}, f32[28,256]{1,0:T(8,128)S(1)}, u32[]{:S(2)}, u32[]{:S(2)}) collective-permute-start(f32[28,256]{1,0:T(8,128)S(1)} %get-tuple-element.25), channel_id=1, source_target_pairs={{0,8},{4,12},{8,0},{12,4},{1,9},{5,13},{9,1},{13,5},{2,10},{6,14},... | collective-permute-start | bytes 86024 | tf_op jit(solution)/shard_map/ppermute | solution.py:273
  210.9 6.7 %collective-permute-start.16 = (f32[28,256]{1,0:T(8,128)S(1)}, f32[28,256]{1,0:T(8,128)S(1)}, u32[]{:S(2)}, u32[]{:S(2)}) collective-permute-start(f32[28,256]{1,0:T(8,128)S(1)} %get-tuple-element.25), channel_id=1, source_target_pairs={{0,12},{4,8},{8,4},{12,0},{1,13},{5,9},{9,5},{13,1},{2,14},{6,10},... | collective-permute-start | bytes 86024 | tf_op jit(solution)/shard_map/ppermute | solution.py:273
  215.2 17.8 %collective-permute-start.20 = (bf16[256,512]{1,0:T(8,128)(2,1)}, bf16[256,512]{1,0:T(8,128)(2,1)S(1)}, u32[]{:S(2)}, u32[]{:S(2)}) collective-permute-start(bf16[256,512]{1,0:T(8,128)(2,1)} %bitcast.71), channel_id=1, source_target_pairs={{0,4},{4,0},{8,12},{12,8},{1,5},{5,1},{9,13},{13,9},{2,6},{6,2},{1... | collective-permute-start | bytes 786440 | tf_op jit(solution)/shard_map/ppermute | solution.py:273
  216.1 21.5 %collective-permute-start.21 = (bf16[256,512]{1,0:T(8,128)(2,1)}, bf16[256,512]{1,0:T(8,128)(2,1)S(1)}, u32[]{:S(2)}, u32[]{:S(2)}) collective-permute-start(bf16[256,512]{1,0:T(8,128)(2,1)} %bitcast.70), channel_id=1, source_target_pairs={{0,8},{4,12},{8,0},{12,4},{1,9},{5,13},{9,1},{13,5},{2,10},{6,14},... | collective-permute-start | bytes 786440 | tf_op jit(solution)/shard_map/ppermute | solution.py:273
  217.7 19.9 %collective-permute-start.22 = (bf16[256,512]{1,0:T(8,128)(2,1)S(1)}, bf16[256,512]{1,0:T(8,128)(2,1)S(1)}, u32[]{:S(2)}, u32[]{:S(2)}) collective-permute-start(bf16[256,512]{1,0:T(8,128)(2,1)S(1)} %bitcast.108), channel_id=1, source_target_pairs={{0,12},{4,8},{8,4},{12,0},{1,13},{5,9},{9,5},{13,1},{2,14},{6,10},... | collective-permute-start | bytes 786440 | tf_op jit(solution)/shard_map/ppermute | solution.py:273
  219.7 0.7 copy-start.2
  220.3 0.8 copy-start.17
  220.3 0.9 copy-start.18
  233.0 4.6 %copy-start.6 = (bf16[256,512]{1,0:T(8,128)(2,1)}, bf16[256,512]{1,0:T(8,128)(2,1)S(1)}, u32[]{:S(2)}) copy-start(bf16[256,512]{1,0:T(8,128)(2,1)S(1)} %collective-permute-done.20.refs_2_.rest_1_) | copy-start | bytes 786436
  237.6 0.7 copy-start.7
  237.6 0.8 copy-start.8
  244.5 24.5 %copy-start.21 = (bf16[256,512]{1,0:T(8,128)(2,1)S(1)}, bf16[256,512]{1,0:T(8,128)(2,1)}, u32[]{:S(2)}) copy-start(bf16[256,512]{1,0:T(8,128)(2,1)} %get-tuple-element.15) | copy-start | bytes 786436
  245.6 10.0 %collective-permute-start.23 = (bf16[4,32,1024]{2,1,0:T(8,128)(2,1)S(1)}, bf16[4,32,1024]{2,1,0:T(8,128)(2,1)S(1)}, u32[]{:S(2)}, u32[]{:S(2)}) collective-permute-start(bf16[4,32,1024]{2,1,0:T(8,128)(2,1)S(1)} %get-tuple-element.29), channel_id=1, source_target_pairs={{0,4},{4,8},{8,12},{1,5},{5,9},{9,13},{2,6},{6,10},{10,14},{3,7},{... | collective-permute-start | bytes 786440 | tf_op jit(solution)/shard_map/ppermute | solution.py:323
  251.8 8.3 %collective-permute-start.24 = (bf16[4,32,1024]{2,1,0:T(8,128)(2,1)S(1)}, bf16[4,32,1024]{2,1,0:T(8,128)(2,1)S(1)}, u32[]{:S(2)}, u32[]{:S(2)}) collective-permute-start(bf16[4,32,1024]{2,1,0:T(8,128)(2,1)S(1)} %get-tuple-element.28), channel_id=1, source_target_pairs={{4,0},{8,4},{12,8},{5,1},{9,5},{13,9},{6,2},{10,6},{14,10},{7,3},{... | collective-permute-start | bytes 786440 | tf_op jit(solution)/shard_map/ppermute | solution.py:324
  255.7 14.0 %copy-start.15 = (bf16[4,32,1024]{2,1,0:T(8,128)(2,1)}, bf16[4,32,1024]{2,1,0:T(8,128)(2,1)S(1)}, u32[]{:S(2)}) copy-start(bf16[4,32,1024]{2,1,0:T(8,128)(2,1)S(1)} %collective-permute-done.23.row_low) | copy-start | bytes 786436
  260.0 27.9 %copy-start.16 = (bf16[4,32,1024]{2,1,0:T(8,128)(2,1)}, bf16[4,32,1024]{2,1,0:T(8,128)(2,1)S(1)}, u32[]{:S(2)}) copy-start(bf16[4,32,1024]{2,1,0:T(8,128)(2,1)S(1)} %collective-permute-done.24.row_high) | copy-start | bytes 786436
  260.1 29.0 %collective-permute-start.26 = (bf16[6,32,1024]{2,1,0:T(8,128)(2,1)S(1)}, bf16[6,32,1024]{2,1,0:T(8,128)(2,1)S(1)}, u32[]{:S(2)}, u32[]{:S(2)}) collective-permute-start(bf16[6,32,1024]{2,1,0:T(8,128)(2,1)S(1)} %pad_maximum_fusion.5), channel_id=1, source_target_pairs={{1,0},{2,1},{3,2},{5,4},{6,5},{7,6},{9,8},{10,9},{11,10},{13,12},{... | collective-permute-start | bytes 1179656 | tf_op jit(solution)/shard_map/ppermute | solution.py:331
  262.2 27.0 %collective-permute-start.25 = (bf16[6,32,1024]{2,1,0:T(8,128)(2,1)}, bf16[6,32,1024]{2,1,0:T(8,128)(2,1)S(1)}, u32[]{:S(2)}, u32[]{:S(2)}) collective-permute-start(bf16[6,32,1024]{2,1,0:T(8,128)(2,1)} %pad_maximum_fusion.4), channel_id=1, source_target_pairs={{0,1},{1,2},{2,3},{4,5},{5,6},{6,7},{8,9},{9,10},{10,11},{12,13},{... | collective-permute-start | bytes 1179656 | tf_op jit(solution)/shard_map/ppermute | solution.py:330
  265.4 21.5 %collective-permute-start.17 = (bf16[256,512]{1,0:T(8,128)(2,1)}, bf16[256,512]{1,0:T(8,128)(2,1)}, u32[]{:S(2)}, u32[]{:S(2)}) collective-permute-start(bf16[256,512]{1,0:T(8,128)(2,1)} %get-tuple-element.16), channel_id=1, source_target_pairs={{0,8},{4,12},{8,0},{12,4},{1,9},{5,13},{9,1},{13,5},{2,10},{6,14},... | collective-permute-start | bytes 786440 | tf_op jit(solution)/shard_map/ppermute | solution.py:273
  266.1 21.8 %collective-permute-start.18 = (bf16[256,512]{1,0:T(8,128)(2,1)}, bf16[256,512]{1,0:T(8,128)(2,1)}, u32[]{:S(2)}, u32[]{:S(2)}) collective-permute-start(bf16[256,512]{1,0:T(8,128)(2,1)} %get-tuple-element.17), channel_id=1, source_target_pairs={{0,12},{4,8},{8,4},{12,0},{1,13},{5,9},{9,5},{13,1},{2,14},{6,10},... | collective-permute-start | bytes 786440 | tf_op jit(solution)/shard_map/ppermute | solution.py:273
  269.1 39.6 %collective-permute-start.19 = (bf16[256,512]{1,0:T(8,128)(2,1)}, bf16[256,512]{1,0:T(8,128)(2,1)S(1)}, u32[]{:S(2)}, u32[]{:S(2)}) collective-permute-start(bf16[256,512]{1,0:T(8,128)(2,1)} %get-tuple-element.18), channel_id=1, source_target_pairs={{0,4},{4,0},{8,12},{12,8},{1,5},{5,1},{9,13},{13,9},{2,6},{6,2},{1... | collective-permute-start | bytes 786440 | tf_op jit(solution)/shard_map/ppermute | solution.py:273
  289.2 0.8 copy-start.19
  289.9 0.7 copy-start.20
  301.6 22.5 %collective-permute-start.27 = (bf16[256,512]{1,0:T(8,128)(2,1)}, bf16[256,512]{1,0:T(8,128)(2,1)S(1)}, u32[]{:S(2)}, u32[]{:S(2)}) collective-permute-start(bf16[256,512]{1,0:T(8,128)(2,1)} %get-tuple-element.21), channel_id=1, source_target_pairs={{0,8},{4,12},{8,0},{12,4},{1,9},{5,13},{9,1},{13,5},{2,10},{6,14},... | collective-permute-start | bytes 786440 | tf_op jit(solution)/shard_map/ppermute | solution.py:273
  305.5 18.7 %collective-permute-start.28 = (bf16[256,512]{1,0:T(8,128)(2,1)}, bf16[256,512]{1,0:T(8,128)(2,1)S(1)}, u32[]{:S(2)}, u32[]{:S(2)}) collective-permute-start(bf16[256,512]{1,0:T(8,128)(2,1)} %get-tuple-element.22), channel_id=1, source_target_pairs={{0,12},{4,8},{8,4},{12,0},{1,13},{5,9},{9,5},{13,1},{2,14},{6,10},... | collective-permute-start | bytes 786440 | tf_op jit(solution)/shard_map/ppermute | solution.py:273
  308.9 15.8 %copy-start.10 = (bf16[256,4,512]{2,1,0:T(4,128)(2,1)}, bf16[256,4,512]{2,1,0:T(4,128)(2,1)S(1)}, u32[]{:S(2)}) copy-start(bf16[256,4,512]{2,1,0:T(4,128)(2,1)S(1)} %constant_dynamic-update-slice_fusion.4) | copy-start | bytes 3145732
  310.2 15.8 %collective-permute-start.29 = (bf16[256,512]{1,0:T(8,128)(2,1)}, bf16[256,512]{1,0:T(8,128)(2,1)S(1)}, u32[]{:S(2)}, u32[]{:S(2)}) collective-permute-start(bf16[256,512]{1,0:T(8,128)(2,1)} %get-tuple-element.23), channel_id=1, source_target_pairs={{0,4},{4,0},{8,12},{12,8},{1,5},{5,1},{9,13},{13,9},{2,6},{6,2},{1... | collective-permute-start | bytes 786440 | tf_op jit(solution)/shard_map/ppermute | solution.py:273
  326.2 1.0 copy-start.9

commit v3 on v2

--- a/solution.py
+++ b/solution.py
@@ -215,36 +215,30 @@
     )(here, *blocks, weight, *extra)
 
 
-def place_kernel(here, mine, other, full_in, full_out, sems):
-    chan, seat = here[0], here[1]
-    copies = []
-    for side, pieces in enumerate((mine, other)):
-        for turn in range(pieces.shape[0]):
-            for shift in range(pieces.shape[1]):
-                for which, full in enumerate((full_in, full_out)):
-                    copies.append(
-                        pltpu.make_async_copy(
-                            pieces.at[turn, shift, which],
-                            full.at[chan ^ shift, seat ^ side ^ (2 * turn)],
-                            sems.at[len(copies)],
-                        )
-                    )
-    for copy in copies:
-        copy.start()
-    for copy in copies:
-        copy.wait()
+def place_kernel(here, mine, other, full_in, full_out):
+    chan, side = here[0], here[1] & 1
+    for shift in range(mine.shape[1]):
+        for which, full in enumerate((full_in, full_out)):
+            full[chan ^ shift, 0, side] = mine[0, shift, which]
+            full[chan ^ shift, 0, side ^ 1] = other[0, shift, which]
 
 
 def place(here, mine, other):
     turns, parts, _, share, channels = mine.shape
-    full = jax.ShapeDtypeStruct((parts, 2 * turns, share, channels), mine.dtype)
-    anywhere = pl.BlockSpec(memory_space=pl.ANY)
+    full = jax.ShapeDtypeStruct((parts, turns, 2, share, channels), mine.dtype)
+    pieces = pl.BlockSpec((1,) + mine.shape[1:], lambda turn, here: (turn, 0, 0, 0, 0))
+    placed = pl.BlockSpec(
+        (parts, 1, 2, share, channels), lambda turn, here: (0, (here[1] >> 1) ^ turn, 0, 0, 0)
+    )
     found = pl.pallas_call(
         place_kernel,
-        in_specs=[pl.BlockSpec(memory_space=pltpu.SMEM), anywhere, anywhere],
-        out_specs=[anywhere] * 2,
+        grid_spec=pltpu.PrefetchScalarGridSpec(
+            num_scalar_prefetch=1,
+            grid=(turns,),
+            in_specs=[pieces, pieces],
+            out_specs=[placed, placed],
+        ),
         out_shape=[full] * 2,
-        scratch_shapes=[pltpu.SemaphoreType.DMA((4 * turns * parts,))],
     )(here, mine, other)
     return [weight.reshape(channels, channels) for weight in found]
 
@@ -332,8 +326,8 @@
         return row_low, row_high, plane_low, plane_high
 
     grid = (planes, rows, CX, channels)
+    taps, bias = gather_taps()
     full_in, full_out = gather_weights()
-    taps, bias = gather_taps()
     vol_blocks = exchange(cut(volume))
     grad_blocks = exchange(cut(out_grad))
     hidden = in_grid(product_call(here, vol_blocks, full_in), grid)

time: 329 us -> 221 us (0.67)
  Pallas kernels: 164 us -> 40.1 us
  waiting for transfers between devices: 78.3 us -> 88.7 us
  starting transfers between devices: 54.3 us -> 58.8 us
    pallas_call x1, Pallas kernels: 129 us -> 5.41 us  [place(): pl.pallas_call(place_kernel, grid_spec=pltpu.PrefetchScalarGridSpec(num_s...]
    ppermute x22, waiting for transfers between devices: 66 us -> 76.6 us  [swap(): return lax.ppermute(part, axes, [(i, partner(i)) for i in range(count)])]
    ppermute x2, starting transfers between devices: 8.98 us -> 12.9 us  [halo_of(): row_low = lax.ppermute(field[:, -1], 'chan', forward)]
  transfers between devices with their start and end apart: 30 -> 30, of which waited for: 13 -> 15; matrix products, arithmetic and copies ran while one was open for 6% -> 9% of each run, Pallas kernels for 47% -> 13%
where the time goes in v3:
time: 221 us; the launch traced here: 218 us
  waiting for transfers between devices  88.7 us (40%)
  starting transfers between devices  58.8 us (27%)
  Pallas kernels  40.1 us (18%)
  local copies, waits for them, and re-layouts  25.4 us (11%)
  other arithmetic  3.82 us (2%)
    ppermute x22, waiting for transfers between devices, swap(): return lax.ppermute(part, axes, [(i, partner(i)) for i in range(count)])  76.6 us
    ppermute x22, starting transfers between devices, swap(): return lax.ppermute(part, axes, [(i, partner(i)) for i in range(count)])  34.5 us
    pallas_call x2, Pallas kernels, stencil(): pl.pallas_call(backward_kernel if bias is None else forward_kernel, grid_...  22.8 us
    ppermute x2, starting transfers between devices, halo_of(): row_low = lax.ppermute(field[:, -1], 'chan', forward)  12.9 us
    pallas_call x2, Pallas kernels, product_call(): pl.pallas_call(lambda *refs: kernel(*refs, count=count), grid_spec=pltpu....  11.9 us
    unnamed x56, local copies, waits for them, and re-layouts  10.2 us
    ppermute x2, waiting for transfers between devices, halo_of(): row_high = lax.ppermute(field[:, 0], 'chan', backward)  8.5 us
    ppermute x2, starting transfers between devices, halo_of(): plane_low = lax.ppermute(plane(-1), 'space', forward)  6.26 us
  transfers between devices with their start and end apart: 30, of which 15 were waited for; matrix products, arithmetic and copies ran while one was open for 9% of the time, Pallas kernels for 13%

profile of v3, /device:TPU:0, one launch (start us, length us, event | category | flops | bytes accessed | tf_op | source)
XLA Modules:
  0.0 217.9 jit_solution(2210433172524963737)
XLA Ops:
  0.6 0.9 dynamic-slice_bitcast_fusion
  1.6 3.1 %collective-permute-start.3 = (bf16[2,32,1024]{2,1,0:T(8,128)(2,1)S(1)}, bf16[2,32,1024]{2,1,0:T(8,128)(2,1)S(1)}, u32[]{:S(2)}, u32[]{:S(2)}) collective-permute-start(bf16[2,32,1024]{2,1,0:T(8,128)(2,1)S(1)} %get-tuple-element.53), channel_id=1, source_target_pairs={{0,4},{4,0},{8,12},{12,8},{1,5},{5,1},{9,13},{13,9},{2,6},{6,2},{1... | collective-permute-start | bytes 393224 | tf_op jit(solution)/shard_map/ppermute | solution.py:267
  4.7 2.6 %collective-permute-start.4 = (bf16[2,32,1024]{2,1,0:T(8,128)(2,1)S(1)}, bf16[2,32,1024]{2,1,0:T(8,128)(2,1)S(1)}, u32[]{:S(2)}, u32[]{:S(2)}) collective-permute-start(bf16[2,32,1024]{2,1,0:T(8,128)(2,1)S(1)} %get-tuple-element.53), channel_id=1, source_target_pairs={{0,8},{4,12},{8,0},{12,4},{1,9},{5,13},{9,1},{13,5},{2,10},{6,14},... | collective-permute-start | bytes 393224 | tf_op jit(solution)/shard_map/ppermute | solution.py:267
  7.3 2.5 %collective-permute-done.3 = bf16[2,32,1024]{2,1,0:T(8,128)(2,1)S(1)} collective-permute-done((bf16[2,32,1024]{2,1,0:T(8,128)(2,1)S(1)}, bf16[2,32,1024]{2,1,0:T(8,128)(2,1)S(1)}, u32[]{:S(2)}, u32[]{:S(2)}) %collective-permute-start.3) | collective-permute-done | bytes 131104 | tf_op jit(solution)/shard_map/ppermute | solution.py:267
  9.7 7.8 %collective-permute-done.4 = bf16[2,32,1024]{2,1,0:T(8,128)(2,1)S(1)} collective-permute-done((bf16[2,32,1024]{2,1,0:T(8,128)(2,1)S(1)}, bf16[2,32,1024]{2,1,0:T(8,128)(2,1)S(1)}, u32[]{:S(2)}, u32[]{:S(2)}) %collective-permute-start.4) | collective-permute-done | bytes 131104 | tf_op jit(solution)/shard_map/ppermute | solution.py:267
  17.7 1.6 collective-permute-start.6
  19.2 1.5 collective-permute-start.7
  20.7 8.3 %collective-permute-done.6 = bf16[4,2,32,1024]{3,2,1,0:T(8,128)(2,1)S(1)} collective-permute-done((bf16[4,2,32,1024]{3,2,1,0:T(8,128)(2,1)S(1)}, bf16[4,2,32,1024]{3,2,1,0:T(8,128)(2,1)S(1)}, u32[]{:S(2)}, u32[]{:S(2)}) %collective-permute-start.6) | collective-permute-done | bytes 524320 | tf_op jit(solution)/shard_map/ppermute | solution.py:267
  29.0 2.2 %collective-permute-done.7 = bf16[4,2,32,1024]{3,2,1,0:T(8,128)(2,1)S(1)} collective-permute-done((bf16[4,2,32,1024]{3,2,1,0:T(8,128)(2,1)S(1)}, bf16[4,2,32,1024]{3,2,1,0:T(8,128)(2,1)S(1)}, u32[]{:S(2)}, u32[]{:S(2)}) %collective-permute-start.7) | collective-permute-done | bytes 524320 | tf_op jit(solution)/shard_map/ppermute | solution.py:267
  31.8 8.7 %collective-permute-done.8 = bf16[4,2,32,1024]{3,2,1,0:T(8,128)(2,1)S(1)} collective-permute-done((bf16[4,2,32,1024]{3,2,1,0:T(8,128)(2,1)S(1)}, bf16[4,2,32,1024]{3,2,1,0:T(8,128)(2,1)S(1)}, u32[]{:S(2)}, u32[]{:S(2)}) %collective-permute-start.8) | collective-permute-done | bytes 524320 | tf_op jit(solution)/shard_map/ppermute | solution.py:267
  40.5 1.3 pad_maximum_fusion.mine
  41.9 3.7 %constant_dynamic-slice_fusion = (bf16[256,4,128]{2,1,0:T(4,128)(2,1)S(1)}, bf16[256,4,128]{2,1,0:T(4,128)(2,1)}, bf16[256,4,128]{2,1,0:T(4,128)(2,1)S(1)}, bf16...) fusion(bf16[256,4,512]{2,1,0:T(4,128)(2,1)} %param.7, ...), kind=kLoop, calls=%fused_computation.27 | loop fusion | bytes 4194320 | tf_op jit(solution)/shard_map/dynamic_slice | solution.py:278
  45.6 0.7 copy.40
  46.3 2.3 %collective-permute-start = (bf16[256,512]{1,0:T(8,128)(2,1)}, bf16[256,512]{1,0:T(8,128)(2,1)S(1)}, u32[]{:S(2)}, u32[]{:S(2)}) collective-permute-start(bf16[256,512]{1,0:T(8,128)(2,1)} %bitcast.75), channel_id=1, source_target_pairs={{0,4},{4,0},{8,12},{12,8},{1,5},{5,1},{9,13},{13,9},{2,6},{6,2},{1... | collective-permute-start | bytes 786440 | tf_op jit(solution)/shard_map/ppermute | solution.py:267
  48.6 0.7 copy.39
  49.4 1.2 collective-permute-start.1
  50.6 0.8 copy.38
  51.3 1.5 collective-permute-start.2
  52.8 0.8 copy.41
  54.2 5.4 %shard_map.77 = (bf16[4,4,2,32,1024]{4,3,2,1,0:T(8,128)(2,1)}, bf16[4,4,2,32,1024]{4,3,2,1,0:T(8,128)(2,1)}) custom-call(s32[2]{0:T(128)} %pad_add_fusion.here.refs_0_, bf16[4,4,2,32,1024]{4,3,2,1,0:T(8,128)(2,1)} %copy-done, bf16[4,4,2,32,1024]{4,3,2,1,0:T(8,128)(2,1)} %collective-permute-done.9.other), custom_call_target="tpu_custom_call" | custom-call | tf_op jit(solution)/shard_map/pallas_call | solution.py:233
  59.7 11.2 %collective-permute-done.1.refs_3_.rest_2_ = bf16[256,512]{1,0:T(8,128)(2,1)S(1)} collective-permute-done((bf16[256,512]{1,0:T(8,128)(2,1)}, bf16[256,512]{1,0:T(8,128)(2,1)S(1)}, u32[]{:S(2)}, u32[]{:S(2)}) %collective-permute-start.1) | collective-permute-done | bytes 262176 | tf_op jit(solution)/shard_map/ppermute | solution.py:267
  71.7 5.8 %shard_map.78 = bf16[512,1024]{1,0:T(8,128)(2,1)} custom-call(s32[2]{0:T(128)} %pad_add_fusion.here.refs_0_, bf16[256,512]{1,0:T(8,128)(2,1)} %bitcast.86, bf16[256,512]{1,0:T(8,128)(2,1)} %copy-done.3, bf16[256,512]{1,0:T(8,128)(2,1)} %copy-done.4, bf16[256,512]{1,0:T(8,128)(2,1)} %copy-done.5, bf16[1024,1024]{1,0:T(8,128)(2,1)} %bitcast.82), custom_call_target="tpu_custom_call" | custom-call | tf_op jit(solution)/shard_map/pallas_call | solution.py:205
  77.5 1.1 slice_bitcast_fusion.2
  78.7 6.8 %collective-permute-start.10 = (bf16[4,32,1024]{2,1,0:T(8,128)(2,1)S(1)}, bf16[4,32,1024]{2,1,0:T(8,128)(2,1)S(1)}, u32[]{:S(2)}, u32[]{:S(2)}) collective-permute-start(bf16[4,32,1024]{2,1,0:T(8,128)(2,1)S(1)} %get-tuple-element.37), channel_id=1, source_target_pairs={{0,4},{4,8},{8,12},{1,5},{5,9},{9,13},{2,6},{6,10},{10,14},{3,7},{... | collective-permute-start | bytes 786440 | tf_op jit(solution)/shard_map/ppermute | solution.py:317
  85.4 1.3 collective-permute-start.11
  86.7 1.1 fusion.3
  87.8 2.1 collective-permute-done.10.row_low
  89.9 4.1 %collective-permute-done.11.row_high = bf16[4,32,1024]{2,1,0:T(8,128)(2,1)S(1)} collective-permute-done((bf16[4,32,1024]{2,1,0:T(8,128)(2,1)S(1)}, bf16[4,32,1024]{2,1,0:T(8,128)(2,1)S(1)}, u32[]{:S(2)}, u32[]{:S(2)}) %collective-permute-start.11) | collective-permute-done | bytes 262176 | tf_op jit(solution)/shard_map/ppermute | solution.py:318
  94.1 1.3 collective-permute-start.13
  95.4 0.8 pad_maximum_fusion.2
  96.2 3.0 %collective-permute-start.12 = (bf16[6,32,1024]{2,1,0:T(8,128)(2,1)}, bf16[6,32,1024]{2,1,0:T(8,128)(2,1)S(1)}, u32[]{:S(2)}, u32[]{:S(2)}) collective-permute-start(bf16[6,32,1024]{2,1,0:T(8,128)(2,1)} %pad_maximum_fusion.2), channel_id=1, source_target_pairs={{0,1},{1,2},{2,3},{4,5},{5,6},{6,7},{8,9},{9,10},{10,11},{12,13},{... | collective-permute-start | bytes 1179656 | tf_op jit(solution)/shard_map/ppermute | solution.py:324
  99.3 1.8 collective-permute-start.14
  101.1 2.7 %collective-permute-start.16 = (f32[28,256]{1,0:T(8,128)S(1)}, f32[28,256]{1,0:T(8,128)S(1)}, u32[]{:S(2)}, u32[]{:S(2)}) collective-permute-start(f32[28,256]{1,0:T(8,128)S(1)} %get-tuple-element.25), channel_id=1, source_target_pairs={{0,12},{4,8},{8,4},{12,0},{1,13},{5,9},{9,5},{13,1},{2,14},{6,10},... | collective-permute-start | bytes 86024 | tf_op jit(solution)/shard_map/ppermute | solution.py:267
  103.7 0.7 copy.36
  104.5 0.8 copy.35
  106.0 0.9 collective-permute-start.20
  106.9 0.9 collective-permute-start.21
  107.8 2.7 %collective-permute-start.22 = (bf16[256,512]{1,0:T(8,128)(2,1)S(1)}, bf16[256,512]{1,0:T(8,128)(2,1)S(1)}, u32[]{:S(2)}, u32[]{:S(2)}) collective-permute-start(bf16[256,512]{1,0:T(8,128)(2,1)S(1)} %bitcast.108), channel_id=1, source_target_pairs={{0,12},{4,8},{8,4},{12,0},{1,13},{5,9},{9,5},{13,1},{2,14},{6,10},... | collective-permute-start | bytes 786440 | tf_op jit(solution)/shard_map/ppermute | solution.py:267
  112.0 11.8 %shard_map.79 = (bf16[256,512]{1,0:T(8,128)(2,1)}, bf16[256,512]{1,0:T(8,128)(2,1)}, bf16[256,512]{1,0:T(8,128)(2,1)}, bf16[256,512]{1,0:T(8,128)(2,1)}, f32[4,4,32,1024]{3,2,1,0:T(8,128)}) custom-call(s32[2]{0:T(128)} %pad_add_fusion.here.refs_0_, bf16[4,4,32,1024]{3,2,1,0:T(8,128)(2,1)} %bitcast.79, bf16[4,32,1024]{2,1,0:T(8,128)(2,1)} %copy-done.13, ...), custom_call_target="tpu_custom_call" | custom-call | tf_op jit(solution)/shard_map/pallas_call | solution.py:146
  123.9 4.6 %collective-permute-done.21.refs_3_.rest_2_ = bf16[256,512]{1,0:T(8,128)(2,1)S(1)} collective-permute-done((bf16[256,512]{1,0:T(8,128)(2,1)}, bf16[256,512]{1,0:T(8,128)(2,1)S(1)}, u32[]{:S(2)}, u32[]{:S(2)}) %collective-permute-start.21) | collective-permute-done | bytes 262176 | tf_op jit(solution)/shard_map/ppermute | solution.py:267
  129.2 6.1 %shard_map.80 = bf16[512,1024]{1,0:T(8,128)(2,1)} custom-call(s32[2]{0:T(128)} %pad_add_fusion.here.refs_0_, bf16[256,512]{1,0:T(8,128)(2,1)} %bitcast.88, bf16[256,512]{1,0:T(8,128)(2,1)} %copy-done.6, bf16[256,512]{1,0:T(8,128)(2,1)} %copy-done.7, bf16[256,512]{1,0:T(8,128)(2,1)} %copy-done.8, bf16[1024,1024]{1,0:T(8,128)(2,1)} %bitcast.85, ...), custom_call_target="tpu_custom_call" | custom-call | tf_op jit(solution)/shard_map/pallas_call | solution.py:205
  135.4 1.1 slice_bitcast_fusion
  136.5 6.1 %collective-permute-start.23 = (bf16[4,32,1024]{2,1,0:T(8,128)(2,1)S(1)}, bf16[4,32,1024]{2,1,0:T(8,128)(2,1)S(1)}, u32[]{:S(2)}, u32[]{:S(2)}) collective-permute-start(bf16[4,32,1024]{2,1,0:T(8,128)(2,1)S(1)} %get-tuple-element.29), channel_id=1, source_target_pairs={{0,4},{4,8},{8,12},{1,5},{5,9},{9,13},{2,6},{6,10},{10,14},{3,7},{... | collective-permute-start | bytes 786440 | tf_op jit(solution)/shard_map/ppermute | solution.py:317
  142.6 1.3 collective-permute-start.24
  143.9 1.1 fusion.2
  145.0 1.5 collective-permute-done.23.row_low
  146.5 4.4 %collective-permute-done.24.row_high = bf16[4,32,1024]{2,1,0:T(8,128)(2,1)S(1)} collective-permute-done((bf16[4,32,1024]{2,1,0:T(8,128)(2,1)S(1)}, bf16[4,32,1024]{2,1,0:T(8,128)(2,1)S(1)}, u32[]{:S(2)}, u32[]{:S(2)}) %collective-permute-start.24) | collective-permute-done | bytes 262176 | tf_op jit(solution)/shard_map/ppermute | solution.py:318
  151.0 1.3 collective-permute-start.26
  152.3 0.8 pad_maximum_fusion.4
  153.1 3.2 %collective-permute-start.25 = (bf16[6,32,1024]{2,1,0:T(8,128)(2,1)}, bf16[6,32,1024]{2,1,0:T(8,128)(2,1)S(1)}, u32[]{:S(2)}, u32[]{:S(2)}) collective-permute-start(bf16[6,32,1024]{2,1,0:T(8,128)(2,1)} %pad_maximum_fusion.4), channel_id=1, source_target_pairs={{0,1},{1,2},{2,3},{4,5},{5,6},{6,7},{8,9},{9,10},{10,11},{12,13},{... | collective-permute-start | bytes 1179656 | tf_op jit(solution)/shard_map/ppermute | solution.py:324
  156.4 2.6 %collective-permute-start.18 = (bf16[256,512]{1,0:T(8,128)(2,1)}, bf16[256,512]{1,0:T(8,128)(2,1)}, u32[]{:S(2)}, u32[]{:S(2)}) collective-permute-start(bf16[256,512]{1,0:T(8,128)(2,1)} %get-tuple-element.17), channel_id=1, source_target_pairs={{0,12},{4,8},{8,4},{12,0},{1,13},{5,9},{9,5},{13,1},{2,14},{6,10},... | collective-permute-start | bytes 786440 | tf_op jit(solution)/shard_map/ppermute | solution.py:267
  159.1 0.9 collective-permute-start.19
  160.5 16.4 %collective-permute-done.17 = bf16[256,512]{1,0:T(8,128)(2,1)} collective-permute-done((bf16[256,512]{1,0:T(8,128)(2,1)}, bf16[256,512]{1,0:T(8,128)(2,1)}, u32[]{:S(2)}, u32[]{:S(2)}) %collective-permute-start.17) | collective-permute-done | bytes 262176 | tf_op jit(solution)/shard_map/ppermute | solution.py:267
  176.9 1.0 reshape.83
  177.9 1.0 reshape.84
  179.1 0.8 copy-done.19
  179.9 0.7 copy-done.20
  180.6 11.0 %shard_map.81 = (bf16[256,512]{1,0:T(8,128)(2,1)}, bf16[256,512]{1,0:T(8,128)(2,1)}, bf16[256,512]{1,0:T(8,128)(2,1)}, bf16[256,512]{1,0:T(8,128)(2,1)}) custom-call(s32[2]{0:T(128)} %pad_add_fusion.here.refs_0_, bf16[4,4,32,1024]{3,2,1,0:T(8,128)(2,1)} %bitcast.81, bf16[4,32,1024]{2,1,0:T(8,128)(2,1)} %copy-done.15, bf16[4,32,1024]{2,1,0:T(8,128)(2,1)} %copy-done.16, ...), custom_call_target="tpu_custom_call" | custom-call | tf_op jit(solution)/shard_map/pallas_call | solution.py:146
  191.6 4.0 %collective-permute-start.27 = (bf16[256,512]{1,0:T(8,128)(2,1)}, bf16[256,512]{1,0:T(8,128)(2,1)S(1)}, u32[]{:S(2)}, u32[]{:S(2)}) collective-permute-start(bf16[256,512]{1,0:T(8,128)(2,1)} %get-tuple-element.21), channel_id=1, source_target_pairs={{0,8},{4,12},{8,0},{12,4},{1,9},{5,13},{9,1},{13,5},{2,10},{6,14},... | collective-permute-start | bytes 786440 | tf_op jit(solution)/shard_map/ppermute | solution.py:267
  195.6 3.4 %collective-permute-start.28 = (bf16[256,512]{1,0:T(8,128)(2,1)}, bf16[256,512]{1,0:T(8,128)(2,1)S(1)}, u32[]{:S(2)}, u32[]{:S(2)}) collective-permute-start(bf16[256,512]{1,0:T(8,128)(2,1)} %get-tuple-element.22), channel_id=1, source_target_pairs={{0,12},{4,8},{8,4},{12,0},{1,13},{5,9},{9,5},{13,1},{2,14},{6,10},... | collective-permute-start | bytes 786440 | tf_op jit(solution)/shard_map/ppermute | solution.py:267
  199.5 1.2 reshape.92
  201.3 13.0 %collective-permute-done.27 = bf16[256,512]{1,0:T(8,128)(2,1)S(1)} collective-permute-done((bf16[256,512]{1,0:T(8,128)(2,1)}, bf16[256,512]{1,0:T(8,128)(2,1)S(1)}, u32[]{:S(2)}, u32[]{:S(2)}) %collective-permute-start.27) | collective-permute-done | bytes 262176 | tf_op jit(solution)/shard_map/ppermute | solution.py:267
  214.8 1.9 collective-permute-done.29
  217.0 1.0 copy-done.9
  (100 shorter events, 8.2 us)
Async XLA Ops:
  1.6 8.2 %collective-permute-start.3 = (bf16[2,32,1024]{2,1,0:T(8,128)(2,1)S(1)}, bf16[2,32,1024]{2,1,0:T(8,128)(2,1)S(1)}, u32[]{:S(2)}, u32[]{:S(2)}) collective-permute-start(bf16[2,32,1024]{2,1,0:T(8,128)(2,1)S(1)} %get-tuple-element.53), channel_id=1, source_target_pairs={{0,4},{4,0},{8,12},{12,8},{1,5},{5,1},{9,13},{13,9},{2,6},{6,2},{1... | collective-permute-start | bytes 393224 | tf_op jit(solution)/shard_map/ppermute | solution.py:267
  4.7 12.9 %collective-permute-start.4 = (bf16[2,32,1024]{2,1,0:T(8,128)(2,1)S(1)}, bf16[2,32,1024]{2,1,0:T(8,128)(2,1)S(1)}, u32[]{:S(2)}, u32[]{:S(2)}) collective-permute-start(bf16[2,32,1024]{2,1,0:T(8,128)(2,1)S(1)} %get-tuple-element.53), channel_id=1, source_target_pairs={{0,8},{4,12},{8,0},{12,4},{1,9},{5,13},{9,1},{13,5},{2,10},{6,14},... | collective-permute-start | bytes 393224 | tf_op jit(solution)/shard_map/ppermute | solution.py:267
  7.3 10.3 %collective-permute-start.5 = (bf16[2,32,1024]{2,1,0:T(8,128)(2,1)S(1)}, bf16[2,32,1024]{2,1,0:T(8,128)(2,1)S(1)}, u32[]{:S(2)}, u32[]{:S(2)}) collective-permute-start(bf16[2,32,1024]{2,1,0:T(8,128)(2,1)S(1)} %get-tuple-element.53), channel_id=1, source_target_pairs={{0,12},{4,8},{8,4},{12,0},{1,13},{5,9},{9,5},{13,1},{2,14},{6,10},... | collective-permute-start | bytes 393224 | tf_op jit(solution)/shard_map/ppermute | solution.py:267
  17.7 11.3 %collective-permute-start.6 = (bf16[4,2,32,1024]{3,2,1,0:T(8,128)(2,1)S(1)}, bf16[4,2,32,1024]{3,2,1,0:T(8,128)(2,1)S(1)}, u32[]{:S(2)}, u32[]{:S(2)}) collective-permute-start(bf16[4,2,32,1024]{3,2,1,0:T(8,128)(2,1)S(1)} %get-tuple-element.43), channel_id=1, source_target_pairs={{0,2},{1,3},{2,0},{3,1},{16,18},{17,19},{18,16},{19,17},{4,6},{5,7... | collective-permute-start | bytes 1572872 | tf_op jit(solution)/shard_map/ppermute | solution.py:267
  19.2 12.0 %collective-permute-start.7 = (bf16[4,2,32,1024]{3,2,1,0:T(8,128)(2,1)S(1)}, bf16[4,2,32,1024]{3,2,1,0:T(8,128)(2,1)S(1)}, u32[]{:S(2)}, u32[]{:S(2)}) collective-permute-start(bf16[4,2,32,1024]{3,2,1,0:T(8,128)(2,1)S(1)} %get-tuple-element.43), channel_id=1, source_target_pairs={{0,16},{1,17},{2,18},{3,19},{16,0},{17,1},{18,2},{19,3},{4,20},{5,... | collective-permute-start | bytes 1572872 | tf_op jit(solution)/shard_map/ppermute | solution.py:267
  31.2 9.3 %copy-start.1 = (bf16[4,2,32,1024]{3,2,1,0:T(8,128)(2,1)}, bf16[4,2,32,1024]{3,2,1,0:T(8,128)(2,1)S(1)}, u32[]{:S(2)}) copy-start(bf16[4,2,32,1024]{3,2,1,0:T(8,128)(2,1)S(1)} %collective-permute-done.7) | copy-start | bytes 1572868
  31.2 9.2 %collective-permute-start.8 = (bf16[4,2,32,1024]{3,2,1,0:T(8,128)(2,1)S(1)}, bf16[4,2,32,1024]{3,2,1,0:T(8,128)(2,1)S(1)}, u32[]{:S(2)}, u32[]{:S(2)}) collective-permute-start(bf16[4,2,32,1024]{3,2,1,0:T(8,128)(2,1)S(1)} %broadcast_select_fusion), channel_id=1, source_target_pairs={{0,2},{1,17},{2,0},{3,19},{16,18},{17,1},{18,16},{19,3},{4,6},{5,2... | collective-permute-start | bytes 1572872 | tf_op jit(solution)/shard_map/ppermute | solution.py:267
  41.8 3.8 %copy-start = (bf16[4,4,2,32,1024]{4,3,2,1,0:T(8,128)(2,1)}, bf16[4,4,2,32,1024]{4,3,2,1,0:T(8,128)(2,1)S(1)}, u32[]{:S(2)}) copy-start(bf16[4,4,2,32,1024]{4,3,2,1,0:T(8,128)(2,1)S(1)} %pad_maximum_fusion.mine) | copy-start | bytes 6291460
  41.8 12.4 %collective-permute-start.9 = (bf16[4,4,2,32,1024]{4,3,2,1,0:T(8,128)(2,1)S(1)}, bf16[4,4,2,32,1024]{4,3,2,1,0:T(8,128)(2,1)}, u32[]{:S(2)}, u32[]{:S(2)}) collective-permute-start(bf16[4,4,2,32,1024]{4,3,2,1,0:T(8,128)(2,1)S(1)} %pad_maximum_fusion.mine), channel_id=1, source_target_pairs={{0,1},{1,0},{2,3},{3,2},{16,17},{17,16},{18,19},{19,18},{4,5},{5,4... | collective-permute-start | bytes 6291464 | tf_op jit(solution)/shard_map/ppermute | solution.py:267
  46.3 13.4 %collective-permute-start = (bf16[256,512]{1,0:T(8,128)(2,1)}, bf16[256,512]{1,0:T(8,128)(2,1)S(1)}, u32[]{:S(2)}, u32[]{:S(2)}) collective-permute-start(bf16[256,512]{1,0:T(8,128)(2,1)} %bitcast.75), channel_id=1, source_target_pairs={{0,4},{4,0},{8,12},{12,8},{1,5},{5,1},{9,13},{13,9},{2,6},{6,2},{1... | collective-permute-start | bytes 786440 | tf_op jit(solution)/shard_map/ppermute | solution.py:267
  49.4 21.5 %collective-permute-start.1 = (bf16[256,512]{1,0:T(8,128)(2,1)}, bf16[256,512]{1,0:T(8,128)(2,1)S(1)}, u32[]{:S(2)}, u32[]{:S(2)}) collective-permute-start(bf16[256,512]{1,0:T(8,128)(2,1)} %bitcast.74), channel_id=1, source_target_pairs={{0,8},{4,12},{8,0},{12,4},{1,9},{5,13},{9,1},{13,5},{2,10},{6,14},... | collective-permute-start | bytes 786440 | tf_op jit(solution)/shard_map/ppermute | solution.py:267
  51.3 19.6 %collective-permute-start.2 = (bf16[256,512]{1,0:T(8,128)(2,1)}, bf16[256,512]{1,0:T(8,128)(2,1)S(1)}, u32[]{:S(2)}, u32[]{:S(2)}) collective-permute-start(bf16[256,512]{1,0:T(8,128)(2,1)} %bitcast.73), channel_id=1, source_target_pairs={{0,12},{4,8},{8,4},{12,0},{1,13},{5,9},{9,5},{13,1},{2,14},{6,10},... | collective-permute-start | bytes 786440 | tf_op jit(solution)/shard_map/ppermute | solution.py:267
  59.7 11.2 %copy-start.3 = (bf16[256,512]{1,0:T(8,128)(2,1)}, bf16[256,512]{1,0:T(8,128)(2,1)S(1)}, u32[]{:S(2)}) copy-start(bf16[256,512]{1,0:T(8,128)(2,1)S(1)} %collective-permute-done.refs_2_.rest_1_) | copy-start | bytes 786436
  70.9 0.7 copy-start.4
  70.9 0.8 copy-start.5
  77.5 21.7 %copy-start.22 = (f32[256,27]{0,1:T(8,128)S(1)}, f32[256,27]{0,1:T(8,128)}, u32[]{:S(2)}) copy-start(f32[256,27]{0,1:T(8,128)} %param.10) | copy-start | bytes 82948
  77.5 21.7 %copy-start.23 = (f32[256]{0:T(256)S(1)}, f32[256]{0:T(256)}, u32[]{:S(2)}) copy-start(f32[256]{0:T(256)} %param.11) | copy-start | bytes 3076
  77.5 26.2 %copy-start.12 = (bf16[256,4,128]{2,1,0:T(4,128)(2,1)S(1)}, bf16[256,4,128]{2,1,0:T(4,128)(2,1)}, u32[]{:S(2)}) copy-start(bf16[256,4,128]{2,1,0:T(4,128)(2,1)} %get-tuple-element.31) | copy-start | bytes 786436
  78.6 25.8 %copy-start.11 = (bf16[256,4,128]{2,1,0:T(4,128)(2,1)S(1)}, bf16[256,4,128]{2,1,0:T(4,128)(2,1)}, u32[]{:S(2)}) copy-start(bf16[256,4,128]{2,1,0:T(4,128)(2,1)} %get-tuple-element.33) | copy-start | bytes 786436
  78.7 11.2 %collective-permute-start.10 = (bf16[4,32,1024]{2,1,0:T(8,128)(2,1)S(1)}, bf16[4,32,1024]{2,1,0:T(8,128)(2,1)S(1)}, u32[]{:S(2)}, u32[]{:S(2)}) collective-permute-start(bf16[4,32,1024]{2,1,0:T(8,128)(2,1)S(1)} %get-tuple-element.37), channel_id=1, source_target_pairs={{0,4},{4,8},{8,12},{1,5},{5,9},{9,13},{2,6},{6,10},{10,14},{3,7},{... | collective-permute-start | bytes 786440 | tf_op jit(solution)/shard_map/ppermute | solution.py:317
  85.4 8.6 %collective-permute-start.11 = (bf16[4,32,1024]{2,1,0:T(8,128)(2,1)S(1)}, bf16[4,32,1024]{2,1,0:T(8,128)(2,1)S(1)}, u32[]{:S(2)}, u32[]{:S(2)}) collective-permute-start(bf16[4,32,1024]{2,1,0:T(8,128)(2,1)S(1)} %get-tuple-element.36), channel_id=1, source_target_pairs={{4,0},{8,4},{12,8},{5,1},{9,5},{13,9},{6,2},{10,6},{14,10},{7,3},{... | collective-permute-start | bytes 786440 | tf_op jit(solution)/shard_map/ppermute | solution.py:318
  89.8 16.2 %copy-start.13 = (bf16[4,32,1024]{2,1,0:T(8,128)(2,1)}, bf16[4,32,1024]{2,1,0:T(8,128)(2,1)S(1)}, u32[]{:S(2)}) copy-start(bf16[4,32,1024]{2,1,0:T(8,128)(2,1)S(1)} %collective-permute-done.10.row_low) | copy-start | bytes 786436
  94.0 12.0 %copy-start.14 = (bf16[4,32,1024]{2,1,0:T(8,128)(2,1)}, bf16[4,32,1024]{2,1,0:T(8,128)(2,1)S(1)}, u32[]{:S(2)}) copy-start(bf16[4,32,1024]{2,1,0:T(8,128)(2,1)S(1)} %collective-permute-done.11.row_high) | copy-start | bytes 786436
  94.1 17.1 %collective-permute-start.13 = (bf16[6,32,1024]{2,1,0:T(8,128)(2,1)S(1)}, bf16[6,32,1024]{2,1,0:T(8,128)(2,1)S(1)}, u32[]{:S(2)}, u32[]{:S(2)}) collective-permute-start(bf16[6,32,1024]{2,1,0:T(8,128)(2,1)S(1)} %pad_maximum_fusion.3), channel_id=1, source_target_pairs={{1,0},{2,1},{3,2},{5,4},{6,5},{7,6},{9,8},{10,9},{11,10},{13,12},{... | collective-permute-start | bytes 1179656 | tf_op jit(solution)/shard_map/ppermute | solution.py:325
  96.2 15.0 %collective-permute-start.12 = (bf16[6,32,1024]{2,1,0:T(8,128)(2,1)}, bf16[6,32,1024]{2,1,0:T(8,128)(2,1)S(1)}, u32[]{:S(2)}, u32[]{:S(2)}) collective-permute-start(bf16[6,32,1024]{2,1,0:T(8,128)(2,1)} %pad_maximum_fusion.2), channel_id=1, source_target_pairs={{0,1},{1,2},{2,3},{4,5},{5,6},{6,7},{8,9},{9,10},{10,11},{12,13},{... | collective-permute-start | bytes 1179656 | tf_op jit(solution)/shard_map/ppermute | solution.py:324
  99.3 6.7 %collective-permute-start.14 = (f32[28,256]{1,0:T(8,128)S(1)}, f32[28,256]{1,0:T(8,128)S(1)}, u32[]{:S(2)}, u32[]{:S(2)}) collective-permute-start(f32[28,256]{1,0:T(8,128)S(1)} %get-tuple-element.25), channel_id=1, source_target_pairs={{0,4},{4,0},{8,12},{12,8},{1,5},{5,1},{9,13},{13,9},{2,6},{6,2},{1... | collective-permute-start | bytes 86024 | tf_op jit(solution)/shard_map/ppermute | solution.py:267
  101.1 5.8 %collective-permute-start.15 = (f32[28,256]{1,0:T(8,128)S(1)}, f32[28,256]{1,0:T(8,128)S(1)}, u32[]{:S(2)}, u32[]{:S(2)}) collective-permute-start(f32[28,256]{1,0:T(8,128)S(1)} %get-tuple-element.25), channel_id=1, source_target_pairs={{0,8},{4,12},{8,0},{12,4},{1,9},{5,13},{9,1},{13,5},{2,10},{6,14},... | collective-permute-start | bytes 86024 | tf_op jit(solution)/shard_map/ppermute | solution.py:267
  101.1 6.7 %collective-permute-start.16 = (f32[28,256]{1,0:T(8,128)S(1)}, f32[28,256]{1,0:T(8,128)S(1)}, u32[]{:S(2)}, u32[]{:S(2)}) collective-permute-start(f32[28,256]{1,0:T(8,128)S(1)} %get-tuple-element.25), channel_id=1, source_target_pairs={{0,12},{4,8},{8,4},{12,0},{1,13},{5,9},{9,5},{13,1},{2,14},{6,10},... | collective-permute-start | bytes 86024 | tf_op jit(solution)/shard_map/ppermute | solution.py:267
  106.0 17.8 %collective-permute-start.20 = (bf16[256,512]{1,0:T(8,128)(2,1)}, bf16[256,512]{1,0:T(8,128)(2,1)S(1)}, u32[]{:S(2)}, u32[]{:S(2)}) collective-permute-start(bf16[256,512]{1,0:T(8,128)(2,1)} %bitcast.71), channel_id=1, source_target_pairs={{0,4},{4,0},{8,12},{12,8},{1,5},{5,1},{9,13},{13,9},{2,6},{6,2},{1... | collective-permute-start | bytes 786440 | tf_op jit(solution)/shard_map/ppermute | solution.py:267
  106.9 21.5 %collective-permute-start.21 = (bf16[256,512]{1,0:T(8,128)(2,1)}, bf16[256,512]{1,0:T(8,128)(2,1)S(1)}, u32[]{:S(2)}, u32[]{:S(2)}) collective-permute-start(bf16[256,512]{1,0:T(8,128)(2,1)} %bitcast.70), channel_id=1, source_target_pairs={{0,8},{4,12},{8,0},{12,4},{1,9},{5,13},{9,1},{13,5},{2,10},{6,14},... | collective-permute-start | bytes 786440 | tf_op jit(solution)/shard_map/ppermute | solution.py:267
  107.8 20.6 %collective-permute-start.22 = (bf16[256,512]{1,0:T(8,128)(2,1)S(1)}, bf16[256,512]{1,0:T(8,128)(2,1)S(1)}, u32[]{:S(2)}, u32[]{:S(2)}) collective-permute-start(bf16[256,512]{1,0:T(8,128)(2,1)S(1)} %bitcast.108), channel_id=1, source_target_pairs={{0,12},{4,8},{8,4},{12,0},{1,13},{5,9},{9,5},{13,1},{2,14},{6,10},... | collective-permute-start | bytes 786440 | tf_op jit(solution)/shard_map/ppermute | solution.py:267
  110.5 0.7 copy-start.2
  111.2 0.8 copy-start.17
  111.2 0.9 copy-start.18
  123.9 4.6 %copy-start.6 = (bf16[256,512]{1,0:T(8,128)(2,1)}, bf16[256,512]{1,0:T(8,128)(2,1)S(1)}, u32[]{:S(2)}) copy-start(bf16[256,512]{1,0:T(8,128)(2,1)S(1)} %collective-permute-done.20.refs_2_.rest_1_) | copy-start | bytes 786436
  128.5 0.7 copy-start.7
  128.5 0.8 copy-start.8
  135.4 23.6 %copy-start.21 = (bf16[256,512]{1,0:T(8,128)(2,1)S(1)}, bf16[256,512]{1,0:T(8,128)(2,1)}, u32[]{:S(2)}) copy-start(bf16[256,512]{1,0:T(8,128)(2,1)} %get-tuple-element.15) | copy-start | bytes 786436
  136.5 10.0 %collective-permute-start.23 = (bf16[4,32,1024]{2,1,0:T(8,128)(2,1)S(1)}, bf16[4,32,1024]{2,1,0:T(8,128)(2,1)S(1)}, u32[]{:S(2)}, u32[]{:S(2)}) collective-permute-start(bf16[4,32,1024]{2,1,0:T(8,128)(2,1)S(1)} %get-tuple-element.29), channel_id=1, source_target_pairs={{0,4},{4,8},{8,12},{1,5},{5,9},{9,13},{2,6},{6,10},{10,14},{3,7},{... | collective-permute-start | bytes 786440 | tf_op jit(solution)/shard_map/ppermute | solution.py:317
  142.6 8.3 %collective-permute-start.24 = (bf16[4,32,1024]{2,1,0:T(8,128)(2,1)S(1)}, bf16[4,32,1024]{2,1,0:T(8,128)(2,1)S(1)}, u32[]{:S(2)}, u32[]{:S(2)}) collective-permute-start(bf16[4,32,1024]{2,1,0:T(8,128)(2,1)S(1)} %get-tuple-element.28), channel_id=1, source_target_pairs={{4,0},{8,4},{12,8},{5,1},{9,5},{13,9},{6,2},{10,6},{14,10},{7,3},{... | collective-permute-start | bytes 786440 | tf_op jit(solution)/shard_map/ppermute | solution.py:318
  146.5 13.9 %copy-start.15 = (bf16[4,32,1024]{2,1,0:T(8,128)(2,1)}, bf16[4,32,1024]{2,1,0:T(8,128)(2,1)S(1)}, u32[]{:S(2)}) copy-start(bf16[4,32,1024]{2,1,0:T(8,128)(2,1)S(1)} %collective-permute-done.23.row_low) | copy-start | bytes 786436
  150.9 27.0 %copy-start.16 = (bf16[4,32,1024]{2,1,0:T(8,128)(2,1)}, bf16[4,32,1024]{2,1,0:T(8,128)(2,1)S(1)}, u32[]{:S(2)}) copy-start(bf16[4,32,1024]{2,1,0:T(8,128)(2,1)S(1)} %collective-permute-done.24.row_high) | copy-start | bytes 786436
  151.0 28.1 %collective-permute-start.26 = (bf16[6,32,1024]{2,1,0:T(8,128)(2,1)S(1)}, bf16[6,32,1024]{2,1,0:T(8,128)(2,1)S(1)}, u32[]{:S(2)}, u32[]{:S(2)}) collective-permute-start(bf16[6,32,1024]{2,1,0:T(8,128)(2,1)S(1)} %pad_maximum_fusion.5), channel_id=1, source_target_pairs={{1,0},{2,1},{3,2},{5,4},{6,5},{7,6},{9,8},{10,9},{11,10},{13,12},{... | collective-permute-start | bytes 1179656 | tf_op jit(solution)/shard_map/ppermute | solution.py:325
  153.1 26.1 %collective-permute-start.25 = (bf16[6,32,1024]{2,1,0:T(8,128)(2,1)}, bf16[6,32,1024]{2,1,0:T(8,128)(2,1)S(1)}, u32[]{:S(2)}, u32[]{:S(2)}) collective-permute-start(bf16[6,32,1024]{2,1,0:T(8,128)(2,1)} %pad_maximum_fusion.4), channel_id=1, source_target_pairs={{0,1},{1,2},{2,3},{4,5},{5,6},{6,7},{8,9},{9,10},{10,11},{12,13},{... | collective-permute-start | bytes 1179656 | tf_op jit(solution)/shard_map/ppermute | solution.py:324
  156.3 20.6 %collective-permute-start.17 = (bf16[256,512]{1,0:T(8,128)(2,1)}, bf16[256,512]{1,0:T(8,128)(2,1)}, u32[]{:S(2)}, u32[]{:S(2)}) collective-permute-start(bf16[256,512]{1,0:T(8,128)(2,1)} %get-tuple-element.16), channel_id=1, source_target_pairs={{0,8},{4,12},{8,0},{12,4},{1,9},{5,13},{9,1},{13,5},{2,10},{6,14},... | collective-permute-start | bytes 786440 | tf_op jit(solution)/shard_map/ppermute | solution.py:267
  156.4 21.5 %collective-permute-start.18 = (bf16[256,512]{1,0:T(8,128)(2,1)}, bf16[256,512]{1,0:T(8,128)(2,1)}, u32[]{:S(2)}, u32[]{:S(2)}) collective-permute-start(bf16[256,512]{1,0:T(8,128)(2,1)} %get-tuple-element.17), channel_id=1, source_target_pairs={{0,12},{4,8},{8,4},{12,0},{1,13},{5,9},{9,5},{13,1},{2,14},{6,10},... | collective-permute-start | bytes 786440 | tf_op jit(solution)/shard_map/ppermute | solution.py:267
  159.1 40.2 %collective-permute-start.19 = (bf16[256,512]{1,0:T(8,128)(2,1)}, bf16[256,512]{1,0:T(8,128)(2,1)S(1)}, u32[]{:S(2)}, u32[]{:S(2)}) collective-permute-start(bf16[256,512]{1,0:T(8,128)(2,1)} %get-tuple-element.18), channel_id=1, source_target_pairs={{0,4},{4,0},{8,12},{12,8},{1,5},{5,1},{9,13},{13,9},{2,6},{6,2},{1... | collective-permute-start | bytes 786440 | tf_op jit(solution)/shard_map/ppermute | solution.py:267
  179.1 0.8 copy-start.19
  179.9 0.7 copy-start.20
  191.6 22.7 %collective-permute-start.27 = (bf16[256,512]{1,0:T(8,128)(2,1)}, bf16[256,512]{1,0:T(8,128)(2,1)S(1)}, u32[]{:S(2)}, u32[]{:S(2)}) collective-permute-start(bf16[256,512]{1,0:T(8,128)(2,1)} %get-tuple-element.21), channel_id=1, source_target_pairs={{0,8},{4,12},{8,0},{12,4},{1,9},{5,13},{9,1},{13,5},{2,10},{6,14},... | collective-permute-start | bytes 786440 | tf_op jit(solution)/shard_map/ppermute | solution.py:267
  195.6 18.7 %collective-permute-start.28 = (bf16[256,512]{1,0:T(8,128)(2,1)}, bf16[256,512]{1,0:T(8,128)(2,1)S(1)}, u32[]{:S(2)}, u32[]{:S(2)}) collective-permute-start(bf16[256,512]{1,0:T(8,128)(2,1)} %get-tuple-element.22), channel_id=1, source_target_pairs={{0,12},{4,8},{8,4},{12,0},{1,13},{5,9},{9,5},{13,1},{2,14},{6,10},... | collective-permute-start | bytes 786440 | tf_op jit(solution)/shard_map/ppermute | solution.py:267
  199.5 15.3 %copy-start.10 = (bf16[256,4,512]{2,1,0:T(4,128)(2,1)}, bf16[256,4,512]{2,1,0:T(4,128)(2,1)S(1)}, u32[]{:S(2)}) copy-start(bf16[256,4,512]{2,1,0:T(4,128)(2,1)S(1)} %constant_dynamic-update-slice_fusion.4) | copy-start | bytes 3145732
  200.7 16.0 %collective-permute-start.29 = (bf16[256,512]{1,0:T(8,128)(2,1)}, bf16[256,512]{1,0:T(8,128)(2,1)S(1)}, u32[]{:S(2)}, u32[]{:S(2)}) collective-permute-start(bf16[256,512]{1,0:T(8,128)(2,1)} %get-tuple-element.23), channel_id=1, source_target_pairs={{0,4},{4,0},{8,12},{12,8},{1,5},{5,1},{9,13},{13,9},{2,6},{6,2},{1... | collective-permute-start | bytes 786440 | tf_op jit(solution)/shard_map/ppermute | solution.py:267
  217.0 1.0 copy-start.9

commit v4 on v3

--- a/solution.py
+++ b/solution.py
@@ -44,7 +44,7 @@
             row = padded[z + a, y + b]
             for e in range(3):
                 index = (a * 3 + b) * 3 + e
-                tap = taps[26 - index if flip else index]
+                tap = taps[0, 26 - index if flip else index]
                 term = row * tap[None, :]
                 sums[e] = term if sums[e] is None else sums[e] + term
     x = lax.broadcasted_iota(jnp.int32, sums[0].shape, 0)
@@ -54,19 +54,51 @@
     return sums[1] + (before + after)
 
 
+def piece_copies(here, mine, other, full, sems):
+    chan, seat = here[0], here[1]
+    copies = []
+    for side, pieces in enumerate((mine, other)):
+        for turn in range(pieces.shape[0]):
+            for shift in range(pieces.shape[1]):
+                copies.append(
+                    pltpu.make_async_copy(
+                        pieces.at[turn, shift],
+                        full.at[chan ^ shift, seat ^ side ^ (2 * turn)],
+                        sems.at[len(copies)],
+                    )
+                )
+    return copies
+
+
+def start_all(copies):
+    for copy in copies:
+        copy.start()
+
+
+def wait_all(copies):
+    for copy in copies:
+        copy.wait()
+
+
 def forward_kernel(
-    here, own, row_low, row_high, plane_low, plane_high, taps, bias, weight, *rest
+    here, own, row_low, row_high, plane_low, plane_high, taps, mine, other, *rest
 ):
-    count = (len(rest) - 3) // 2
+    count = (len(rest) - 5) // 2
     inputs, outputs = rest[:count], rest[count : 2 * count]
-    slope, padded, active = rest[2 * count :]
+    slope, padded, active, weight, sems = rest[2 * count :]
     step = pl.program_id(0)
     planes, rows, extent = own.shape[:3]
+    copies = piece_copies(here, mine, other, weight, sems)
+
+    @pl.when(step == 0)
+    def _():
+        start_all(copies)
+
     fill_padded(padded, own, row_low, row_high, plane_low, plane_high)
     lanes = pl.ds(pl.multiple_of(step * LANES, LANES), LANES)
     for z in range(planes):
         for y in range(rows):
-            mixed = stencil_row(padded, taps, z, y, False) + bias[0][None, :]
+            mixed = stencil_row(padded, taps, z, y, False) + taps[0, 27][None, :]
             half = 0.5 * (1.0 + lax.erf(mixed * root_half))
             at = (z * rows + y) * extent
             active[at : at + extent, lanes] = (mixed * half).astype(active.dtype)
@@ -74,11 +106,11 @@
 
     @pl.when(step == pl.num_programs(0) - 1)
     def _():
-        own_channels = inputs[0].shape[0]
+        wait_all(copies)
         for shift in range(count):
-            start = pl.multiple_of((here[0] ^ shift) * own_channels, own_channels)
+            rows_of = weight[here[0] ^ shift]
             product = lax.dot_general(
-                weight[pl.ds(start, own_channels), :],
+                rows_of.reshape(-1, rows_of.shape[-1]),
                 active[...],
                 (((1,), (1,)), ((), ())),
                 preferred_element_type=jnp.float32,
@@ -87,12 +119,20 @@
             outputs[shift][...] = total.astype(outputs[shift].dtype)
 
 
-def backward_kernel(here, own, row_low, row_high, plane_low, plane_high, taps, weight, *rest):
-    count = (len(rest) - 2) // 2
+def backward_kernel(
+    here, own, row_low, row_high, plane_low, plane_high, taps, mine, other, *rest
+):
+    count = (len(rest) - 4) // 2
     inputs, outputs = rest[:count], rest[count : 2 * count]
-    padded, grads = rest[2 * count :]
+    padded, grads, weight, sems = rest[2 * count :]
     step = pl.program_id(0)
     planes, rows, extent = own.shape[:3]
+    copies = piece_copies(here, mine, other, weight, sems)
+
+    @pl.when(step == 0)
+    def _():
+        start_all(copies)
+
     fill_padded(padded, own, row_low, row_high, plane_low, plane_high)
     lanes = pl.ds(pl.multiple_of(step * LANES, LANES), LANES)
     for z in range(planes):
@@ -103,21 +143,29 @@
 
     @pl.when(step == pl.num_programs(0) - 1)
     def _():
-        own_channels = inputs[0].shape[0]
+        wait_all(copies)
+        channels = grads.shape[1]
+        width = inputs[0].shape[0]
         for shift in range(count):
-            start = pl.multiple_of((here[0] ^ shift) * own_channels, own_channels)
-            product = jnp.dot(
-                grads[...],
-                weight[:, pl.ds(start, own_channels)],
-                preferred_element_type=jnp.float32,
-            )
+            start = pl.multiple_of((here[0] ^ shift) * width, width)
+            columns = weight[:, :, :, pl.ds(start, width)].reshape(channels, width)
+            product = jnp.dot(grads[...], columns, preferred_element_type=jnp.float32)
             total = inputs[shift][...].astype(jnp.float32) + product.T
             outputs[shift][...] = total.astype(outputs[shift].dtype)
 
 
-def stencil(here, own, halo, taps, bias, weight, blocks):
+def weight_scratch(mine):
+    turns, parts, share, channels = mine.shape
+    return [
+        pltpu.VMEM((parts, 2 * turns, share, channels), mine.dtype),
+        pltpu.SemaphoreType.DMA((2 * turns * parts,)),
+    ]
+
+
+def stencil(here, own, halo, taps, weight, blocks, forward):
     planes, rows, extent, channels = own.shape
     cells = planes * rows * extent
+    per_table = taps.shape[2] // LANES
 
     def block(*lead):
         zeros = (0,) * len(lead)
@@ -126,25 +174,27 @@
     def resident(shape):
         return pl.BlockSpec(shape, lambda c, here: (0,) * len(shape), pipeline_mode=pl.Buffered(1))
 
+    anywhere = pl.BlockSpec(memory_space=pl.ANY)
     in_specs = [
         block(planes, rows, extent),
         block(planes, extent),
         block(planes, extent),
         block(rows + 2, extent),
         block(rows + 2, extent),
-        block(27),
+        pl.BlockSpec(
+            (1, 28, LANES), lambda c, here: ((c // per_table) ^ here[0], 0, c % per_table)
+        ),
+        anywhere,
+        anywhere,
     ]
-    args = [own, *halo, taps]
+    in_specs += [resident(piece.shape) for piece in blocks]
     out_specs = [resident(piece.shape) for piece in blocks]
     out_shape = [jax.ShapeDtypeStruct(piece.shape, piece.dtype) for piece in blocks]
-    if bias is not None:
-        in_specs.append(block(1))
-        args.append(bias)
+    if forward:
         out_specs.append(block(planes, rows, extent))
         out_shape.append(jax.ShapeDtypeStruct(own.shape, jnp.float32))
-    in_specs += [resident(weight.shape)] + [resident(piece.shape) for piece in blocks]
     return pl.pallas_call(
-        backward_kernel if bias is None else forward_kernel,
+        forward_kernel if forward else backward_kernel,
         grid_spec=pltpu.PrefetchScalarGridSpec(
             num_scalar_prefetch=1,
             grid=(channels // LANES,),
@@ -153,94 +203,89 @@
             scratch_shapes=[
                 pltpu.VMEM((planes + 2, rows + 2, extent, LANES), jnp.float32),
                 pltpu.VMEM((cells, channels), own.dtype),
+                *weight_scratch(weight[0]),
             ],
         ),
         out_shape=out_shape,
-    )(here, *args, weight, *blocks)
-
-
-def turn_kernel(here, *refs, count):
-    inputs, turned = refs[:count], refs[-1]
+    )(here, own, *halo, taps, *weight, *blocks)
+
+
+def turn_blocks(here, inputs, turned):
+    own = inputs[0].shape[0]
+    for shift, block in enumerate(inputs):
+        start = pl.multiple_of((here[0] ^ shift) * own, own)
+        turned[:, pl.ds(start, own)] = block[...].T
+
+
+def put_with_rows(value, out, first, last):
+    out[...] = value
+    planes, extent = first.shape[:2]
+    plane = value.shape[0] // planes
+    for z in range(planes):
+        first[z] = value[z * plane : z * plane + extent]
+        last[z] = value[(z + 1) * plane - extent : (z + 1) * plane]
+
+
+def hidden_kernel(here, mine, other, *rest, count):
+    inputs, (out, first, last, turned, weight, sems) = rest[:count], rest[count:]
 
     @pl.when(pl.program_id(0) == 0)
     def _():
-        own = inputs[0].shape[0]
-        for shift in range(count):
-            start = pl.multiple_of((here[0] ^ shift) * own, own)
-            turned[:, pl.ds(start, own)] = inputs[shift][...].T
-
-
-def hidden_kernel(here, *refs, count):
-    turn_kernel(here, *refs, count=count)
-    weight, out, turned = refs[count:]
-    out[...] = lax.dot_general(
+        copies = piece_copies(here, mine, other, weight, sems)
+        start_all(copies)
+        turn_blocks(here, inputs, turned)
+        wait_all(copies)
+
+    rows_of = weight[pl.program_id(0)]
+    value = lax.dot_general(
         turned[...],
-        weight[...],
+        rows_of.reshape(-1, rows_of.shape[-1]),
         (((1,), (1,)), ((), ())),
         preferred_element_type=jnp.float32,
-    ).astype(out.dtype)
-
-
-def mix_kernel(here, *refs, count):
-    turn_kernel(here, *refs, count=count)
-    weight, slope, out, turned = refs[count:]
-    grad = jnp.dot(turned[...], weight[...], preferred_element_type=jnp.float32)
+    )
+    put_with_rows(value.astype(out.dtype), out, first, last)
+
+
+def mix_kernel(here, mine, other, *rest, count):
+    inputs, (slope, out, first, last, turned, weight, sems) = rest[:count], rest[count:]
+
+    @pl.when(pl.program_id(0) == 0)
+    def _():
+        copies = piece_copies(here, mine, other, weight, sems)
+        start_all(copies)
+        turn_blocks(here, inputs, turned)
+        wait_all(copies)
+
+    channels, width = turned.shape[1], out.shape[1]
+    start = pl.multiple_of(pl.program_id(0) * width, width)
+    columns = weight[:, :, :, pl.ds(start, width)].reshape(channels, width)
+    grad = jnp.dot(turned[...], columns, preferred_element_type=jnp.float32)
     grad = grad.astype(out.dtype).astype(jnp.float32)
-    out[...] = (grad * slope[...]).astype(out.dtype)
-
-
-def product_call(here, blocks, weight, slope=None):
+    put_with_rows((grad * slope[...]).astype(out.dtype), out, first, last)
+
+
+def product_call(here, blocks, weight, planes, slope=None):
     own, cells = blocks[0].shape
-    channels = weight.shape[0]
     count = len(blocks)
-    width = 2 * LANES
-    columns = pl.BlockSpec((cells, width), lambda c, here: (0, c))
+    channels = own * count
+    dtype = blocks[0].dtype
+    columns = pl.BlockSpec((cells, own), lambda c, here: (0, c))
+    edge = pl.BlockSpec((planes, CX, own), lambda c, here: (0, 0, c))
     whole = pl.BlockSpec((own, cells), lambda c, here: (0, 0), pipeline_mode=pl.Buffered(1))
-    if slope is None:
-        kernel, extra = hidden_kernel, []
-        weight_spec = pl.BlockSpec((width, channels), lambda c, here: (c, 0))
-    else:
-        kernel, extra = mix_kernel, [slope]
-        weight_spec = pl.BlockSpec((channels, width), lambda c, here: (0, c))
+    anywhere = pl.BlockSpec(memory_space=pl.ANY)
+    kernel, extra = (hidden_kernel, []) if slope is None else (mix_kernel, [slope])
+    edge_shape = jax.ShapeDtypeStruct((planes, CX, channels), dtype)
     return pl.pallas_call(
         lambda *refs: kernel(*refs, count=count),
         grid_spec=pltpu.PrefetchScalarGridSpec(
             num_scalar_prefetch=1,
-            grid=(channels // width,),
-            in_specs=[whole] * count + [weight_spec] + [columns] * len(extra),
-            out_specs=columns,
-            scratch_shapes=[pltpu.VMEM((cells, channels), blocks[0].dtype)],
+            grid=(count,),
+            in_specs=[anywhere] * 2 + [whole] * count + [columns] * len(extra),
+            out_specs=[columns, edge, edge],
+            scratch_shapes=[pltpu.VMEM((cells, channels), dtype), *weight_scratch(weight[0])],
         ),
-        out_shape=jax.ShapeDtypeStruct((cells, channels), blocks[0].dtype),
-    )(here, *blocks, weight, *extra)
-
-
-def place_kernel(here, mine, other, full_in, full_out):
-    chan, side = here[0], here[1] & 1
-    for shift in range(mine.shape[1]):
-        for which, full in enumerate((full_in, full_out)):
-            full[chan ^ shift, 0, side] = mine[0, shift, which]
-            full[chan ^ shift, 0, side ^ 1] = other[0, shift, which]
-
-
-def place(here, mine, other):
-    turns, parts, _, share, channels = mine.shape
-    full = jax.ShapeDtypeStruct((parts, turns, 2, share, channels), mine.dtype)
-    pieces = pl.BlockSpec((1,) + mine.shape[1:], lambda turn, here: (turn, 0, 0, 0, 0))
-    placed = pl.BlockSpec(
-        (parts, 1, 2, share, channels), lambda turn, here: (0, (here[1] >> 1) ^ turn, 0, 0, 0)
-    )
-    found = pl.pallas_call(
-        place_kernel,
-        grid_spec=pltpu.PrefetchScalarGridSpec(
-            num_scalar_prefetch=1,
-            grid=(turns,),
-            in_specs=[pieces, pieces],
-            out_specs=[placed, placed],
-        ),
-        out_shape=[full] * 2,
-    )(here, mine, other)
-    return [weight.reshape(channels, channels) for weight in found]
+        out_shape=[jax.ShapeDtypeStruct((cells, channels), dtype), edge_shape, edge_shape],
+    )(here, *weight, *blocks, *extra)
 
 
 def shift_pairs(axis):
@@ -287,35 +332,20 @@
             field = lax.dynamic_update_slice_in_dim(field, piece, (chan ^ shift) * width, axis=2)
         return field
 
-    def gather_weights():
-        begin = seat * share
-        pair = jnp.stack(
-            [
-                lax.dynamic_slice_in_dim(weight, begin, share, axis=0)
-                for weight in (weight_in, weight_out)
-            ]
-        )
-        column = jnp.stack(exchange(lambda shift: pair))
+    def gather_weight(weight):
+        piece = lax.dynamic_slice_in_dim(weight, seat * share, share, axis=0)
+        column = jnp.stack(exchange(lambda shift: piece))
         over_x = swap(column, others, lambda i: i ^ 2)
         over_y = swap(column, others, lambda i: i ^ 4)
         mixed = jnp.where(seat & 1 == 0, over_y, over_x)
         far = swap(mixed, others, lambda i: i ^ (4 if i & 1 else 2))
         mine = jnp.stack([column, over_x, over_y, far])
-        other = swap(mine, others, lambda i: i ^ 1)
-        return place(here, mine, other)
-
-    def gather_taps():
-        table = jnp.concatenate([filter_taps, filter_bias[:, None]], axis=1).T
-        found = exchange(lambda shift: table)
-        full = jnp.zeros((28, channels), jnp.float32)
-        for shift in range(parts):
-            full = lax.dynamic_update_slice_in_dim(full, found[shift], (chan ^ shift) * own, axis=1)
-        return full[:27], full[27:]
-
-    def halo_of(field):
+        return mine, swap(mine, others, lambda i: i ^ 1)
+
+    def halo_of(field, first, last):
         forward, backward = shift_pairs("chan")
-        row_low = lax.ppermute(field[:, -1], "chan", forward)
-        row_high = lax.ppermute(field[:, 0], "chan", backward)
+        row_low = lax.ppermute(last, "chan", forward)
+        row_high = lax.ppermute(first, "chan", backward)
         forward, backward = shift_pairs("space")
 
         def plane(z):
@@ -326,22 +356,25 @@
         return row_low, row_high, plane_low, plane_high
 
     grid = (planes, rows, CX, channels)
-    taps, bias = gather_taps()
-    full_in, full_out = gather_weights()
+    full_in = gather_weight(weight_in)
+    full_out = gather_weight(weight_out)
+    table = jnp.concatenate([filter_taps, filter_bias[:, None]], axis=1).T
+    taps = jnp.stack(exchange(lambda shift: table))
     vol_blocks = exchange(cut(volume))
     grad_blocks = exchange(cut(out_grad))
-    hidden = in_grid(product_call(here, vol_blocks, full_in), grid)
-    *out_blocks, slope = stencil(here, hidden, halo_of(hidden), taps, bias, full_out, vol_blocks)
+    hidden, first, last = product_call(here, vol_blocks, full_in, planes)
+    hidden = hidden.reshape(grid)
+    halo = halo_of(hidden, first, last)
+    *out_blocks, slope = stencil(here, hidden, halo, taps, full_out, vol_blocks, True)
     block_out = paste(exchange(lambda shift: out_blocks[shift]))
-    mix_grad = product_call(here, grad_blocks, full_out, slope.reshape(planes * width, channels))
-    mix_grad = in_grid(mix_grad, grid)
-    back_blocks = stencil(here, mix_grad, halo_of(mix_grad), taps, None, full_in, grad_blocks)
+    mix_grad, first, last = product_call(
+        here, grad_blocks, full_out, planes, slope.reshape(planes * width, channels)
+    )
+    mix_grad = mix_grad.reshape(grid)
+    halo = halo_of(mix_grad, first, last)
+    back_blocks = stencil(here, mix_grad, halo, taps, full_in, grad_blocks, False)
     volume_grad = paste(exchange(lambda shift: back_blocks[shift]))
     return block_out, volume_grad
-
-
-def in_grid(field, grid):
-    return field.reshape(grid)
 
 
 def with_halo(block, axis, dim):

time: 221 us -> 223 us (level)
  waiting for transfers between devices: 88.7 us -> 92.4 us
  other arithmetic: 3.82 us -> 7.04 us
  Pallas kernels: 40.1 us -> 37.2 us
    pallas_call x3 -> x2, Pallas kernels: 28.2 us -> 22.7 us  [stencil(): pl.pallas_call(forward_kernel if forward else backward_kernel, grid_spec=...]
    ppermute x4, waiting for transfers between devices: 12.1 us -> 15.2 us  [the longest x2 12.1 us: halo_of(): row_high = lax.ppermute(first, 'chan', backward)]
    pallas_call x2, Pallas kernels: 11.9 us -> 14.6 us  [product_call(): pl.pallas_call(lambda *refs: kernel(*refs, count=count), grid_spec=pltpu....]
    squeeze x2 -> x0, local copies, waits for them, and re-layouts: 2.24 us -> none  [halo_of(): row_high = lax.ppermute(field[:, 0], 'chan', backward)]
    ppermute x22 -> x29, starting transfers between devices: 34.5 us -> 36.2 us  [swap(): return lax.ppermute(part, axes, [(i, partner(i)) for i in range(count)])]
    ppermute x22 -> x29, waiting for transfers between devices: 76.6 us -> 77.2 us  [swap(): return lax.ppermute(part, axes, [(i, partner(i)) for i in range(count)])]
    unnamed x56 -> x70, local copies, waits for them, and re-layouts: 10.2 us -> 10.2 us
  transfers between devices with their start and end apart: 30 -> 37, of which waited for: 15 -> 20; matrix products, arithmetic and copies ran while one was open for 9% -> 10% of each run, Pallas kernels for 13% -> 13%
where the time goes in v4:
time: 223 us; the launch traced here: 222 us
  waiting for transfers between devices  92.4 us (41%)
  starting transfers between devices  60 us (27%)
  Pallas kernels  37.2 us (17%)
  local copies, waits for them, and re-layouts  23.7 us (11%)
  other arithmetic  7.04 us (3%)
    ppermute x29, waiting for transfers between devices, swap(): return lax.ppermute(part, axes, [(i, partner(i)) for i in range(count)])  77.2 us
    ppermute x29, starting transfers between devices, swap(): return lax.ppermute(part, axes, [(i, partner(i)) for i in range(count)])  36.2 us
    pallas_call x2, Pallas kernels, stencil(): pl.pallas_call(forward_kernel if forward else backward_kernel, grid_spec=...  22.7 us
    pallas_call x2, Pallas kernels, product_call(): pl.pallas_call(lambda *refs: kernel(*refs, count=count), grid_spec=pltpu....  14.6 us
    ppermute x2, waiting for transfers between devices, halo_of(): row_high = lax.ppermute(first, 'chan', backward)  12.1 us
    ppermute x2, starting transfers between devices, halo_of(): row_low = lax.ppermute(last, 'chan', forward)  11.5 us
    unnamed x70, local copies, waits for them, and re-layouts  10.2 us
    ppermute x2, starting transfers between devices, halo_of(): plane_low = lax.ppermute(plane(-1), 'space', forward)  7.04 us
  transfers between devices with their start and end apart: 37, of which 20 were waited for; matrix products, arithmetic and copies ran while one was open for 10% of the time, Pallas kernels for 13%

profile of v4, /device:TPU:0, one launch (start us, length us, event | category | flops | bytes accessed | tf_op | source)
XLA Modules:
  0.0 221.7 jit_solution(1023308115849674595)
XLA Ops:
  0.7 1.0 copy-done
  1.7 3.1 %collective-permute-start = (bf16[32,1024]{1,0:T(8,128)(2,1)S(1)}, bf16[32,1024]{1,0:T(8,128)(2,1)S(1)}, u32[]{:S(2)}, u32[]{:S(2)}) collective-permute-start(bf16[32,1024]{1,0:T(8,128)(2,1)S(1)} %constant_dynamic-slice_fusion.9), channel_id=1, source_target_pairs={{0,4},{4,0},{8,12},{12,8},{1,5},{5,1},{9,13},{13,9},{2,6},{6,2},{1... | collective-permute-start | bytes 196616 | tf_op jit(solution)/shard_map/ppermute | solution.py:312
  4.7 2.6 %collective-permute-start.1 = (bf16[32,1024]{1,0:T(8,128)(2,1)S(1)}, bf16[32,1024]{1,0:T(8,128)(2,1)S(1)}, u32[]{:S(2)}, u32[]{:S(2)}) collective-permute-start(bf16[32,1024]{1,0:T(8,128)(2,1)S(1)} %constant_dynamic-slice_fusion.9), channel_id=1, source_target_pairs={{0,8},{4,12},{8,0},{12,4},{1,9},{5,13},{9,1},{13,5},{2,10},{6,14},... | collective-permute-start | bytes 196616 | tf_op jit(solution)/shard_map/ppermute | solution.py:312
  7.3 4.6 %collective-permute-done.1 = bf16[32,1024]{1,0:T(8,128)(2,1)S(1)} collective-permute-done((bf16[32,1024]{1,0:T(8,128)(2,1)S(1)}, bf16[32,1024]{1,0:T(8,128)(2,1)S(1)}, u32[]{:S(2)}, u32[]{:S(2)}) %collective-permute-start.1) | collective-permute-done | bytes 65568 | tf_op jit(solution)/shard_map/ppermute | solution.py:312
  12.0 1.4 collective-permute-done.2
  13.4 1.6 collective-permute-start.3
  15.0 1.5 collective-permute-start.4
  16.5 3.4 %collective-permute-done.3 = bf16[4,32,1024]{2,1,0:T(8,128)(2,1)S(1)} collective-permute-done((bf16[4,32,1024]{2,1,0:T(8,128)(2,1)S(1)}, bf16[4,32,1024]{2,1,0:T(8,128)(2,1)S(1)}, u32[]{:S(2)}, u32[]{:S(2)}) %collective-permute-start.3) | collective-permute-done | bytes 262176 | tf_op jit(solution)/shard_map/ppermute | solution.py:312
  19.9 1.7 collective-permute-done.4
  22.2 5.8 %collective-permute-done.5 = bf16[4,32,1024]{2,1,0:T(8,128)(2,1)S(1)} collective-permute-done((bf16[4,32,1024]{2,1,0:T(8,128)(2,1)S(1)}, bf16[4,32,1024]{2,1,0:T(8,128)(2,1)S(1)}, u32[]{:S(2)}, u32[]{:S(2)}) %collective-permute-start.5) | collective-permute-done | bytes 262176 | tf_op jit(solution)/shard_map/ppermute | solution.py:312
  28.3 0.9 constant_dynamic-slice_fusion.4
  29.5 2.8 %collective-permute-start.18 = (bf16[32,1024]{1,0:T(8,128)(2,1)S(1)}, bf16[32,1024]{1,0:T(8,128)(2,1)S(1)}, u32[]{:S(2)}, u32[]{:S(2)}) collective-permute-start(bf16[32,1024]{1,0:T(8,128)(2,1)S(1)} %constant_dynamic-slice_fusion.4), channel_id=1, source_target_pairs={{0,8},{4,12},{8,0},{12,4},{1,9},{5,13},{9,1},{13,5},{2,10},{6,14},... | collective-permute-start | bytes 196616 | tf_op jit(solution)/shard_map/ppermute | solution.py:312
  32.3 1.3 collective-permute-start.19
  33.6 0.8 fusion.10
  34.8 1.5 collective-permute-done.18
  36.4 2.0 collective-permute-done.19
  38.4 0.9 fusion.2
  39.3 0.8 collective-permute-start.20
  40.1 1.5 collective-permute-start.21
  41.6 3.1 %constant_dynamic-slice_fusion = (bf16[256,4,128]{2,1,0:T(4,128)(2,1)}, bf16[256,4,128]{2,1,0:T(4,128)(2,1)}, bf16[256,4,128]{2,1,0:T(4,128)(2,1)}, bf16[256,4,1...) fusion(bf16[256,4,512]{2,1,0:T(4,128)(2,1)} %param.7, ...), kind=kLoop, calls=%fused_computation.26 | loop fusion | bytes 4194320 | tf_op jit(solution)/shard_map/dynamic_slice | solution.py:323
  44.8 1.2 collective-permute-start.7
  46.0 1.7 collective-permute-start.8
  48.5 1.6 collective-permute-start.9
  50.1 1.7 broadcast_select_fusion
  51.8 1.2 collective-permute-start.22
  54.3 1.3 collective-permute-done.7.refs_4_.rest_1_
  55.6 11.7 %collective-permute-done.8.refs_5_.rest_2_ = bf16[256,512]{1,0:T(8,128)(2,1)S(1)} collective-permute-done((bf16[256,512]{1,0:T(8,128)(2,1)S(1)}, bf16[256,512]{1,0:T(8,128)(2,1)S(1)}, u32[]{:S(2)}, u32[]{:S(2)}) %collective-permute-start.8) | collective-permute-done | bytes 262176 | tf_op jit(solution)/shard_map/ppermute | solution.py:312
  68.4 7.0 %shard_map.77 = (bf16[512,1024]{1,0:T(8,128)(2,1)}, bf16[4,32,1024]{2,1,0:T(8,128)(2,1)}, bf16[4,32,1024]{2,1,0:T(8,128)(2,1)}) custom-call(s32[2]{0:T(128)} %pad_add_fusion.refs_0_.here, bf16[4,4,32,1024]{3,2,1,0:T(8,128)(2,1)} %copy-done.1, bf16[4,4,32,1024]{3,2,1,0:T(8,128)(2,1)} %copy-done.3, bf16[256,512]{1,0:T(8,128)(2,1)} %bitcast.72, ...), custom_call_target="tpu_custom_call" | custom-call | tf_op jit(solution)/shard_map/pallas_call | solution.py:278
  75.5 6.1 %collective-permute-start.10 = (bf16[4,32,1024]{2,1,0:T(8,128)(2,1)}, bf16[4,32,1024]{2,1,0:T(8,128)(2,1)S(1)}, u32[]{:S(2)}, u32[]{:S(2)}) collective-permute-start(bf16[4,32,1024]{2,1,0:T(8,128)(2,1)} %get-tuple-element.18), channel_id=1, source_target_pairs={{0,4},{4,8},{8,12},{1,5},{5,9},{9,13},{2,6},{6,10},{10,14},{3,7},{... | collective-permute-start | bytes 786440 | tf_op jit(solution)/shard_map/ppermute | solution.py:347
  81.6 1.2 pad_maximum_fusion.1.mine.refs_1_
  83.0 1.4 collective-permute-start.11
  84.5 1.3 collective-permute-done.10.row_low
  85.7 7.8 %collective-permute-done.11.row_high = bf16[4,32,1024]{2,1,0:T(8,128)(2,1)S(1)} collective-permute-done((bf16[4,32,1024]{2,1,0:T(8,128)(2,1)S(1)}, bf16[4,32,1024]{2,1,0:T(8,128)(2,1)S(1)}, u32[]{:S(2)}, u32[]{:S(2)}) %collective-permute-start.11) | collective-permute-done | bytes 262176 | tf_op jit(solution)/shard_map/ppermute | solution.py:348
  93.6 1.3 collective-permute-start.13
  95.0 3.8 %collective-permute-start.12 = (bf16[6,32,1024]{2,1,0:T(8,128)(2,1)S(1)}, bf16[6,32,1024]{2,1,0:T(8,128)(2,1)}, u32[]{:S(2)}, u32[]{:S(2)}) collective-permute-start(bf16[6,32,1024]{2,1,0:T(8,128)(2,1)S(1)} %pad_maximum_fusion.2), channel_id=1, source_target_pairs={{0,1},{1,2},{2,3},{4,5},{5,6},{6,7},{8,9},{9,10},{10,11},{12,13},{... | collective-permute-start | bytes 1179656 | tf_op jit(solution)/shard_map/ppermute | solution.py:354
  98.8 0.9 collective-permute-start.14
  99.7 3.1 %collective-permute-done.14 = f32[28,256]{1,0:T(8,128)S(1)} collective-permute-done((f32[28,256]{1,0:T(8,128)S(1)}, f32[28,256]{1,0:T(8,128)S(1)}, u32[]{:S(2)}, u32[]{:S(2)}) %collective-permute-start.14) | collective-permute-done | bytes 28704 | tf_op jit(solution)/shard_map/ppermute | solution.py:312
  105.9 2.7 %collective-permute-done.16 = f32[28,256]{1,0:T(8,128)S(1)} collective-permute-done((f32[28,256]{1,0:T(8,128)S(1)}, f32[28,256]{1,0:T(8,128)S(1)}, u32[]{:S(2)}, u32[]{:S(2)}) %collective-permute-start.16) | collective-permute-done | bytes 28704 | tf_op jit(solution)/shard_map/ppermute | solution.py:312
  108.6 0.9 collective-permute-start.28
  112.2 11.6 %shard_map.78 = (bf16[256,512]{1,0:T(8,128)(2,1)}, bf16[256,512]{1,0:T(8,128)(2,1)}, bf16[256,512]{1,0:T(8,128)(2,1)}, bf16[256,512]{1,0:T(8,128)(2,1)}, f32[4,4,32,1024]{3,2,1,0:T(8,128)}) custom-call(s32[2]{0:T(128)} %pad_add_fusion.refs_0_.here, bf16[4,4,32,1024]{3,2,1,0:T(8,128)(2,1)} %bitcast.70, bf16[4,32,1024]{2,1,0:T(8,128)(2,1)} %copy-done.20, ...), custom_call_target="tpu_custom_call" | custom-call | tf_op jit(solution)/shard_map/pallas_call | solution.py:196
  123.8 6.0 %collective-permute-done.28.refs_5_.rest_2_ = bf16[256,512]{1,0:T(8,128)(2,1)S(1)} collective-permute-done((bf16[256,512]{1,0:T(8,128)(2,1)}, bf16[256,512]{1,0:T(8,128)(2,1)S(1)}, u32[]{:S(2)}, u32[]{:S(2)}) %collective-permute-start.28) | collective-permute-done | bytes 262176 | tf_op jit(solution)/shard_map/ppermute | solution.py:312
  130.7 7.6 %shard_map.79 = (bf16[512,1024]{1,0:T(8,128)(2,1)}, bf16[4,32,1024]{2,1,0:T(8,128)(2,1)}, bf16[4,32,1024]{2,1,0:T(8,128)(2,1)}) custom-call(s32[2]{0:T(128)} %pad_add_fusion.refs_0_.here, bf16[4,4,32,1024]{3,2,1,0:T(8,128)(2,1)} %copy-done.2, bf16[4,4,32,1024]{3,2,1,0:T(8,128)(2,1)} %copy-done.4, bf16[256,512]{1,0:T(8,128)(2,1)} %bitcast.74, ...), custom_call_target="tpu_custom_call" | custom-call | tf_op jit(solution)/shard_map/pallas_call | solution.py:278
  138.3 5.4 %collective-permute-start.30 = (bf16[4,32,1024]{2,1,0:T(8,128)(2,1)}, bf16[4,32,1024]{2,1,0:T(8,128)(2,1)S(1)}, u32[]{:S(2)}, u32[]{:S(2)}) collective-permute-start(bf16[4,32,1024]{2,1,0:T(8,128)(2,1)} %get-tuple-element.26), channel_id=1, source_target_pairs={{0,4},{4,8},{8,12},{1,5},{5,9},{9,13},{2,6},{6,10},{10,14},{3,7},{... | collective-permute-start | bytes 786440 | tf_op jit(solution)/shard_map/ppermute | solution.py:347
  143.7 1.3 collective-permute-start.31
  145.0 1.1 fusion.4
  146.1 1.8 collective-permute-done.30.row_low
  147.9 4.3 %collective-permute-done.31.row_high = bf16[4,32,1024]{2,1,0:T(8,128)(2,1)S(1)} collective-permute-done((bf16[4,32,1024]{2,1,0:T(8,128)(2,1)}, bf16[4,32,1024]{2,1,0:T(8,128)(2,1)S(1)}, u32[]{:S(2)}, u32[]{:S(2)}) %collective-permute-start.31) | collective-permute-done | bytes 262176 | tf_op jit(solution)/shard_map/ppermute | solution.py:348
  152.2 0.9 pad_maximum_fusion.5
  153.1 1.3 collective-permute-start.33
  154.4 0.8 pad_maximum_fusion.4
  155.2 3.2 %collective-permute-start.32 = (bf16[6,32,1024]{2,1,0:T(8,128)(2,1)}, bf16[6,32,1024]{2,1,0:T(8,128)(2,1)S(1)}, u32[]{:S(2)}, u32[]{:S(2)}) collective-permute-start(bf16[6,32,1024]{2,1,0:T(8,128)(2,1)} %pad_maximum_fusion.4), channel_id=1, source_target_pairs={{0,1},{1,2},{2,3},{4,5},{5,6},{6,7},{8,9},{9,10},{10,11},{12,13},{... | collective-permute-start | bytes 1179656 | tf_op jit(solution)/shard_map/ppermute | solution.py:354
  158.5 2.8 %collective-permute-start.25 = (bf16[256,512]{1,0:T(8,128)(2,1)}, bf16[256,512]{1,0:T(8,128)(2,1)}, u32[]{:S(2)}, u32[]{:S(2)}) collective-permute-start(bf16[256,512]{1,0:T(8,128)(2,1)} %get-tuple-element.22), channel_id=1, source_target_pairs={{0,12},{4,8},{8,4},{12,0},{1,13},{5,9},{9,5},{13,1},{2,14},{6,10},... | collective-permute-start | bytes 786440 | tf_op jit(solution)/shard_map/ppermute | solution.py:312
  162.6 16.5 %collective-permute-done.24 = bf16[256,512]{1,0:T(8,128)(2,1)} collective-permute-done((bf16[256,512]{1,0:T(8,128)(2,1)}, bf16[256,512]{1,0:T(8,128)(2,1)}, u32[]{:S(2)}, u32[]{:S(2)}) %collective-permute-start.24) | collective-permute-done | bytes 262176 | tf_op jit(solution)/shard_map/ppermute | solution.py:312
  179.1 1.0 reshape.75
  180.1 1.0 reshape.76
  182.3 11.0 %shard_map.80 = (bf16[256,512]{1,0:T(8,128)(2,1)}, bf16[256,512]{1,0:T(8,128)(2,1)}, bf16[256,512]{1,0:T(8,128)(2,1)}, bf16[256,512]{1,0:T(8,128)(2,1)}) custom-call(s32[2]{0:T(128)} %pad_add_fusion.refs_0_.here, bf16[4,4,32,1024]{3,2,1,0:T(8,128)(2,1)} %bitcast.71, bf16[4,32,1024]{2,1,0:T(8,128)(2,1)} %copy-done.22, bf16[4,32,1024]{2,1,0:T(8,128)(2,1)} %copy-done.23, ...), custom_call_target="tpu_custom_call" | custom-call | tf_op jit(solution)/shard_map/pallas_call | solution.py:196
  193.3 4.1 %collective-permute-start.34 = (bf16[256,512]{1,0:T(8,128)(2,1)}, bf16[256,512]{1,0:T(8,128)(2,1)S(1)}, u32[]{:S(2)}, u32[]{:S(2)}) collective-permute-start(bf16[256,512]{1,0:T(8,128)(2,1)} %get-tuple-element.29), channel_id=1, source_target_pairs={{0,8},{4,12},{8,0},{12,4},{1,9},{5,13},{9,1},{13,5},{2,10},{6,14},... | collective-permute-start | bytes 786440 | tf_op jit(solution)/shard_map/ppermute | solution.py:312
  197.4 3.4 %collective-permute-start.35 = (bf16[256,512]{1,0:T(8,128)(2,1)}, bf16[256,512]{1,0:T(8,128)(2,1)S(1)}, u32[]{:S(2)}, u32[]{:S(2)}) collective-permute-start(bf16[256,512]{1,0:T(8,128)(2,1)} %get-tuple-element.30), channel_id=1, source_target_pairs={{0,12},{4,8},{8,4},{12,0},{1,13},{5,9},{9,5},{13,1},{2,14},{6,10},... | collective-permute-start | bytes 786440 | tf_op jit(solution)/shard_map/ppermute | solution.py:312
  201.0 1.0 reshape.77
  202.2 1.2 reshape.84
  204.0 12.1 %collective-permute-done.34 = bf16[256,512]{1,0:T(8,128)(2,1)S(1)} collective-permute-done((bf16[256,512]{1,0:T(8,128)(2,1)}, bf16[256,512]{1,0:T(8,128)(2,1)S(1)}, u32[]{:S(2)}, u32[]{:S(2)}) %collective-permute-start.34) | collective-permute-done | bytes 262176 | tf_op jit(solution)/shard_map/ppermute | solution.py:312
  216.6 2.9 %collective-permute-done.36 = bf16[256,512]{1,0:T(8,128)(2,1)} collective-permute-done((bf16[256,512]{1,0:T(8,128)(2,1)}, bf16[256,512]{1,0:T(8,128)(2,1)}, u32[]{:S(2)}, u32[]{:S(2)}) %collective-permute-start.36) | collective-permute-done | bytes 262176 | tf_op jit(solution)/shard_map/ppermute | solution.py:312
  219.5 1.0 reshape.87
  220.8 1.0 copy-done.6
  (126 shorter events, 15.8 us)
Async XLA Ops:
  0.6 1.0 copy-start
  1.7 5.7 %collective-permute-start = (bf16[32,1024]{1,0:T(8,128)(2,1)S(1)}, bf16[32,1024]{1,0:T(8,128)(2,1)S(1)}, u32[]{:S(2)}, u32[]{:S(2)}) collective-permute-start(bf16[32,1024]{1,0:T(8,128)(2,1)S(1)} %constant_dynamic-slice_fusion.9), channel_id=1, source_target_pairs={{0,4},{4,0},{8,12},{12,8},{1,5},{5,1},{9,13},{13,9},{2,6},{6,2},{1... | collective-permute-start | bytes 196616 | tf_op jit(solution)/shard_map/ppermute | solution.py:312
  4.7 7.3 %collective-permute-start.1 = (bf16[32,1024]{1,0:T(8,128)(2,1)S(1)}, bf16[32,1024]{1,0:T(8,128)(2,1)S(1)}, u32[]{:S(2)}, u32[]{:S(2)}) collective-permute-start(bf16[32,1024]{1,0:T(8,128)(2,1)S(1)} %constant_dynamic-slice_fusion.9), channel_id=1, source_target_pairs={{0,8},{4,12},{8,0},{12,4},{1,9},{5,13},{9,1},{13,5},{2,10},{6,14},... | collective-permute-start | bytes 196616 | tf_op jit(solution)/shard_map/ppermute | solution.py:312
  7.3 6.1 %collective-permute-start.2 = (bf16[32,1024]{1,0:T(8,128)(2,1)S(1)}, bf16[32,1024]{1,0:T(8,128)(2,1)S(1)}, u32[]{:S(2)}, u32[]{:S(2)}) collective-permute-start(bf16[32,1024]{1,0:T(8,128)(2,1)S(1)} %constant_dynamic-slice_fusion.9), channel_id=1, source_target_pairs={{0,12},{4,8},{8,4},{12,0},{1,13},{5,9},{9,5},{13,1},{2,14},{6,10},... | collective-permute-start | bytes 196616 | tf_op jit(solution)/shard_map/ppermute | solution.py:312
  13.4 6.5 %collective-permute-start.3 = (bf16[4,32,1024]{2,1,0:T(8,128)(2,1)S(1)}, bf16[4,32,1024]{2,1,0:T(8,128)(2,1)S(1)}, u32[]{:S(2)}, u32[]{:S(2)}) collective-permute-start(bf16[4,32,1024]{2,1,0:T(8,128)(2,1)S(1)} %get-tuple-element.55), channel_id=1, source_target_pairs={{0,2},{1,3},{2,0},{3,1},{16,18},{17,19},{18,16},{19,17},{4,6},{5,7... | collective-permute-start | bytes 786440 | tf_op jit(solution)/shard_map/ppermute | solution.py:312
  15.0 6.6 %collective-permute-start.4 = (bf16[4,32,1024]{2,1,0:T(8,128)(2,1)S(1)}, bf16[4,32,1024]{2,1,0:T(8,128)(2,1)S(1)}, u32[]{:S(2)}, u32[]{:S(2)}) collective-permute-start(bf16[4,32,1024]{2,1,0:T(8,128)(2,1)S(1)} %get-tuple-element.55), channel_id=1, source_target_pairs={{0,16},{1,17},{2,18},{3,19},{16,0},{17,1},{18,2},{19,3},{4,20},{5,... | collective-permute-start | bytes 786440 | tf_op jit(solution)/shard_map/ppermute | solution.py:312
  21.6 6.4 %collective-permute-start.5 = (bf16[4,32,1024]{2,1,0:T(8,128)(2,1)S(1)}, bf16[4,32,1024]{2,1,0:T(8,128)(2,1)S(1)}, u32[]{:S(2)}, u32[]{:S(2)}) collective-permute-start(bf16[4,32,1024]{2,1,0:T(8,128)(2,1)S(1)} %broadcast_select_fusion.1), channel_id=1, source_target_pairs={{0,2},{1,17},{2,0},{3,19},{16,18},{17,1},{18,16},{19,3},{4,6},{5,2... | collective-permute-start | bytes 786440 | tf_op jit(solution)/shard_map/ppermute | solution.py:312
  28.2 16.5 %copy-start.1 = (bf16[4,4,32,1024]{3,2,1,0:T(8,128)(2,1)}, bf16[4,4,32,1024]{3,2,1,0:T(8,128)(2,1)S(1)}, u32[]{:S(2)}) copy-start(bf16[4,4,32,1024]{3,2,1,0:T(8,128)(2,1)S(1)} %pad_maximum_fusion.refs_1_.mine) | copy-start | bytes 3145732
  28.2 39.1 %collective-permute-start.6 = (bf16[4,4,32,1024]{3,2,1,0:T(8,128)(2,1)S(1)}, bf16[4,4,32,1024]{3,2,1,0:T(8,128)(2,1)S(1)}, u32[]{:S(2)}, u32[]{:S(2)}) collective-permute-start(bf16[4,4,32,1024]{3,2,1,0:T(8,128)(2,1)S(1)} %pad_maximum_fusion.refs_1_.mine), channel_id=1, source_target_pairs={{0,1},{1,0},{2,3},{3,2},{16,17},{17,16},{18,19},{19,18},{4,5},{5,4... | collective-permute-start | bytes 3145736 | tf_op jit(solution)/shard_map/ppermute | solution.py:312
  29.2 5.6 %collective-permute-start.17 = (bf16[32,1024]{1,0:T(8,128)(2,1)S(1)}, bf16[32,1024]{1,0:T(8,128)(2,1)S(1)}, u32[]{:S(2)}, u32[]{:S(2)}) collective-permute-start(bf16[32,1024]{1,0:T(8,128)(2,1)S(1)} %constant_dynamic-slice_fusion.4), channel_id=1, source_target_pairs={{0,4},{4,0},{8,12},{12,8},{1,5},{5,1},{9,13},{13,9},{2,6},{6,2},{1... | collective-permute-start | bytes 196616 | tf_op jit(solution)/shard_map/ppermute | solution.py:312
  29.5 6.9 %collective-permute-start.18 = (bf16[32,1024]{1,0:T(8,128)(2,1)S(1)}, bf16[32,1024]{1,0:T(8,128)(2,1)S(1)}, u32[]{:S(2)}, u32[]{:S(2)}) collective-permute-start(bf16[32,1024]{1,0:T(8,128)(2,1)S(1)} %constant_dynamic-slice_fusion.4), channel_id=1, source_target_pairs={{0,8},{4,12},{8,0},{12,4},{1,9},{5,13},{9,1},{13,5},{2,10},{6,14},... | collective-permute-start | bytes 196616 | tf_op jit(solution)/shard_map/ppermute | solution.py:312
  32.3 6.1 %collective-permute-start.19 = (bf16[32,1024]{1,0:T(8,128)(2,1)S(1)}, bf16[32,1024]{1,0:T(8,128)(2,1)S(1)}, u32[]{:S(2)}, u32[]{:S(2)}) collective-permute-start(bf16[32,1024]{1,0:T(8,128)(2,1)S(1)} %constant_dynamic-slice_fusion.4), channel_id=1, source_target_pairs={{0,12},{4,8},{8,4},{12,0},{1,13},{5,9},{9,5},{13,1},{2,14},{6,10},... | collective-permute-start | bytes 196616 | tf_op jit(solution)/shard_map/ppermute | solution.py:312
  39.3 8.5 %collective-permute-start.20 = (bf16[4,32,1024]{2,1,0:T(8,128)(2,1)}, bf16[4,32,1024]{2,1,0:T(8,128)(2,1)S(1)}, u32[]{:S(2)}, u32[]{:S(2)}) collective-permute-start(bf16[4,32,1024]{2,1,0:T(8,128)(2,1)} %get-tuple-element.49), channel_id=1, source_target_pairs={{0,2},{1,3},{2,0},{3,1},{16,18},{17,19},{18,16},{19,17},{4,6},{5,7... | collective-permute-start | bytes 786440 | tf_op jit(solution)/shard_map/ppermute | solution.py:312
  40.1 10.0 %collective-permute-start.21 = (bf16[4,32,1024]{2,1,0:T(8,128)(2,1)}, bf16[4,32,1024]{2,1,0:T(8,128)(2,1)}, u32[]{:S(2)}, u32[]{:S(2)}) collective-permute-start(bf16[4,32,1024]{2,1,0:T(8,128)(2,1)} %get-tuple-element.49), channel_id=1, source_target_pairs={{0,16},{1,17},{2,18},{3,19},{16,0},{17,1},{18,2},{19,3},{4,20},{5,... | collective-permute-start | bytes 786440 | tf_op jit(solution)/shard_map/ppermute | solution.py:312
  44.8 10.8 %collective-permute-start.7 = (bf16[256,512]{1,0:T(8,128)(2,1)S(1)}, bf16[256,512]{1,0:T(8,128)(2,1)S(1)}, u32[]{:S(2)}, u32[]{:S(2)}) collective-permute-start(bf16[256,512]{1,0:T(8,128)(2,1)S(1)} %bitcast.92), channel_id=1, source_target_pairs={{0,4},{4,0},{8,12},{12,8},{1,5},{5,1},{9,13},{13,9},{2,6},{6,2},{1... | collective-permute-start | bytes 786440 | tf_op jit(solution)/shard_map/ppermute | solution.py:312
  46.0 21.3 %collective-permute-start.8 = (bf16[256,512]{1,0:T(8,128)(2,1)S(1)}, bf16[256,512]{1,0:T(8,128)(2,1)S(1)}, u32[]{:S(2)}, u32[]{:S(2)}) collective-permute-start(bf16[256,512]{1,0:T(8,128)(2,1)S(1)} %bitcast.93), channel_id=1, source_target_pairs={{0,8},{4,12},{8,0},{12,4},{1,9},{5,13},{9,1},{13,5},{2,10},{6,14},... | collective-permute-start | bytes 786440 | tf_op jit(solution)/shard_map/ppermute | solution.py:312
  48.5 18.8 %collective-permute-start.9 = (bf16[256,512]{1,0:T(8,128)(2,1)S(1)}, bf16[256,512]{1,0:T(8,128)(2,1)S(1)}, u32[]{:S(2)}, u32[]{:S(2)}) collective-permute-start(bf16[256,512]{1,0:T(8,128)(2,1)S(1)} %bitcast.94), channel_id=1, source_target_pairs={{0,12},{4,8},{8,4},{12,0},{1,13},{5,9},{9,5},{13,1},{2,14},{6,10},... | collective-permute-start | bytes 786440 | tf_op jit(solution)/shard_map/ppermute | solution.py:312
  51.8 29.8 %collective-permute-start.22 = (bf16[4,32,1024]{2,1,0:T(8,128)(2,1)}, bf16[4,32,1024]{2,1,0:T(8,128)(2,1)}, u32[]{:S(2)}, u32[]{:S(2)}) collective-permute-start(bf16[4,32,1024]{2,1,0:T(8,128)(2,1)} %broadcast_select_fusion), channel_id=1, source_target_pairs={{0,2},{1,17},{2,0},{3,19},{16,18},{17,1},{18,16},{19,3},{4,6},{5,2... | collective-permute-start | bytes 786440 | tf_op jit(solution)/shard_map/ppermute | solution.py:312
  55.6 11.8 %copy-start.8 = (bf16[256,512]{1,0:T(8,128)(2,1)}, bf16[256,512]{1,0:T(8,128)(2,1)S(1)}, u32[]{:S(2)}) copy-start(bf16[256,512]{1,0:T(8,128)(2,1)S(1)} %collective-permute-done.7.refs_4_.rest_1_) | copy-start | bytes 786436
  67.3 0.8 copy-start.10
  67.3 1.1 copy-start.3
  67.3 14.2 %copy-start.12 = (bf16[4,32,1024]{2,1,0:T(8,128)(2,1)S(1)}, bf16[4,32,1024]{2,1,0:T(8,128)(2,1)}, u32[]{:S(2)}) copy-start(bf16[4,32,1024]{2,1,0:T(8,128)(2,1)} %copy-done.11) | copy-start | bytes 786436
  75.4 7.5 %copy-start.30 = (bf16[4,32,1024]{2,1,0:T(8,128)(2,1)S(1)}, bf16[4,32,1024]{2,1,0:T(8,128)(2,1)}, u32[]{:S(2)}) copy-start(bf16[4,32,1024]{2,1,0:T(8,128)(2,1)} %get-tuple-element.19) | copy-start | bytes 786436
  75.4 8.9 %copy-start.5 = (bf16[512,1024]{1,0:T(8,128)(2,1)S(1)}, bf16[512,1024]{1,0:T(8,128)(2,1)}, u32[]{:S(2)}) copy-start(bf16[512,1024]{1,0:T(8,128)(2,1)} %get-tuple-element.17) | copy-start | bytes 3145732
  75.5 10.3 %collective-permute-start.10 = (bf16[4,32,1024]{2,1,0:T(8,128)(2,1)}, bf16[4,32,1024]{2,1,0:T(8,128)(2,1)S(1)}, u32[]{:S(2)}, u32[]{:S(2)}) collective-permute-start(bf16[4,32,1024]{2,1,0:T(8,128)(2,1)} %get-tuple-element.18), channel_id=1, source_target_pairs={{0,4},{4,8},{8,12},{1,5},{5,9},{9,13},{2,6},{6,10},{10,14},{3,7},{... | collective-permute-start | bytes 786440 | tf_op jit(solution)/shard_map/ppermute | solution.py:347
  82.8 22.0 %copy-start.2 = (bf16[4,4,32,1024]{3,2,1,0:T(8,128)(2,1)}, bf16[4,4,32,1024]{3,2,1,0:T(8,128)(2,1)S(1)}, u32[]{:S(2)}) copy-start(bf16[4,4,32,1024]{3,2,1,0:T(8,128)(2,1)S(1)} %pad_maximum_fusion.1.mine.refs_1_) | copy-start | bytes 3145732
  82.8 16.0 %copy-start.28 = (f32[256,27]{0,1:T(8,128)S(1)}, f32[256,27]{0,1:T(8,128)}, u32[]{:S(2)}) copy-start(f32[256,27]{0,1:T(8,128)} %param.10) | copy-start | bytes 82948
  82.8 16.0 %copy-start.29 = (f32[256]{0:T(256)S(1)}, f32[256]{0:T(256)}, u32[]{:S(2)}) copy-start(f32[256]{0:T(256)} %param.11) | copy-start | bytes 3076
  82.8 20.4 %copy-start.19 = (bf16[256,4,128]{2,1,0:T(4,128)(2,1)S(1)}, bf16[256,4,128]{2,1,0:T(4,128)(2,1)}, u32[]{:S(2)}) copy-start(bf16[256,4,128]{2,1,0:T(4,128)(2,1)} %get-tuple-element.35) | copy-start | bytes 786436
  82.9 21.2 %copy-start.18 = (bf16[256,4,128]{2,1,0:T(4,128)(2,1)S(1)}, bf16[256,4,128]{2,1,0:T(4,128)(2,1)}, u32[]{:S(2)}) copy-start(bf16[256,4,128]{2,1,0:T(4,128)(2,1)} %get-tuple-element.37) | copy-start | bytes 786436
  82.9 26.6 %collective-permute-start.23 = (bf16[4,4,32,1024]{3,2,1,0:T(8,128)(2,1)S(1)}, bf16[4,4,32,1024]{3,2,1,0:T(8,128)(2,1)S(1)}, u32[]{:S(2)}, u32[]{:S(2)}) collective-permute-start(bf16[4,4,32,1024]{3,2,1,0:T(8,128)(2,1)S(1)} %pad_maximum_fusion.1.mine.refs_1_), channel_id=1, source_target_pairs={{0,1},{1,0},{2,3},{3,2},{16,17},{17,16},{18,19},{19,18},{4,5},{5,4... | collective-permute-start | bytes 3145736 | tf_op jit(solution)/shard_map/ppermute | solution.py:312
  83.0 10.6 %collective-permute-start.11 = (bf16[4,32,1024]{2,1,0:T(8,128)(2,1)S(1)}, bf16[4,32,1024]{2,1,0:T(8,128)(2,1)S(1)}, u32[]{:S(2)}, u32[]{:S(2)}) collective-permute-start(bf16[4,32,1024]{2,1,0:T(8,128)(2,1)S(1)} %copy-done.30), channel_id=1, source_target_pairs={{4,0},{8,4},{12,8},{5,1},{9,5},{13,9},{6,2},{10,6},{14,10},{7,3},{... | collective-permute-start | bytes 786440 | tf_op jit(solution)/shard_map/ppermute | solution.py:348
  84.4 20.4 %copy-start.17 = (bf16[256,4,128]{2,1,0:T(4,128)(2,1)S(1)}, bf16[256,4,128]{2,1,0:T(4,128)(2,1)}, u32[]{:S(2)}) copy-start(bf16[256,4,128]{2,1,0:T(4,128)(2,1)} %get-tuple-element.34) | copy-start | bytes 786436
  84.4 25.5 %copy-start.16 = (bf16[256,4,128]{2,1,0:T(4,128)(2,1)S(1)}, bf16[256,4,128]{2,1,0:T(4,128)(2,1)}, u32[]{:S(2)}) copy-start(bf16[256,4,128]{2,1,0:T(4,128)(2,1)} %get-tuple-element.36) | copy-start | bytes 786436
  85.7 25.0 %copy-start.20 = (bf16[4,32,1024]{2,1,0:T(8,128)(2,1)}, bf16[4,32,1024]{2,1,0:T(8,128)(2,1)S(1)}, u32[]{:S(2)}) copy-start(bf16[4,32,1024]{2,1,0:T(8,128)(2,1)S(1)} %collective-permute-done.10.row_low) | copy-start | bytes 786436
  93.5 17.9 %copy-start.21 = (bf16[4,32,1024]{2,1,0:T(8,128)(2,1)}, bf16[4,32,1024]{2,1,0:T(8,128)(2,1)S(1)}, u32[]{:S(2)}) copy-start(bf16[4,32,1024]{2,1,0:T(8,128)(2,1)S(1)} %collective-permute-done.11.row_high) | copy-start | bytes 786436
  93.6 17.8 %collective-permute-start.13 = (bf16[6,32,1024]{2,1,0:T(8,128)(2,1)S(1)}, bf16[6,32,1024]{2,1,0:T(8,128)(2,1)S(1)}, u32[]{:S(2)}, u32[]{:S(2)}) collective-permute-start(bf16[6,32,1024]{2,1,0:T(8,128)(2,1)S(1)} %pad_maximum_fusion.3), channel_id=1, source_target_pairs={{1,0},{2,1},{3,2},{5,4},{6,5},{7,6},{9,8},{10,9},{11,10},{13,12},{... | collective-permute-start | bytes 1179656 | tf_op jit(solution)/shard_map/ppermute | solution.py:355
  95.0 16.5 %collective-permute-start.12 = (bf16[6,32,1024]{2,1,0:T(8,128)(2,1)S(1)}, bf16[6,32,1024]{2,1,0:T(8,128)(2,1)}, u32[]{:S(2)}, u32[]{:S(2)}) collective-permute-start(bf16[6,32,1024]{2,1,0:T(8,128)(2,1)S(1)} %pad_maximum_fusion.2), channel_id=1, source_target_pairs={{0,1},{1,2},{2,3},{4,5},{5,6},{6,7},{8,9},{9,10},{10,11},{12,13},{... | collective-permute-start | bytes 1179656 | tf_op jit(solution)/shard_map/ppermute | solution.py:354
  98.8 4.0 %collective-permute-start.14 = (f32[28,256]{1,0:T(8,128)S(1)}, f32[28,256]{1,0:T(8,128)S(1)}, u32[]{:S(2)}, u32[]{:S(2)}) collective-permute-start(f32[28,256]{1,0:T(8,128)S(1)} %get-tuple-element.57), channel_id=1, source_target_pairs={{0,4},{4,0},{8,12},{12,8},{1,5},{5,1},{9,13},{13,9},{2,6},{6,2},{1... | collective-permute-start | bytes 86024 | tf_op jit(solution)/shard_map/ppermute | solution.py:312
  99.7 5.9 %collective-permute-start.15 = (f32[28,256]{1,0:T(8,128)S(1)}, f32[28,256]{1,0:T(8,128)S(1)}, u32[]{:S(2)}, u32[]{:S(2)}) collective-permute-start(f32[28,256]{1,0:T(8,128)S(1)} %get-tuple-element.57), channel_id=1, source_target_pairs={{0,8},{4,12},{8,0},{12,4},{1,9},{5,13},{9,1},{13,5},{2,10},{6,14},... | collective-permute-start | bytes 86024 | tf_op jit(solution)/shard_map/ppermute | solution.py:312
  102.8 5.8 %collective-permute-start.16 = (f32[28,256]{1,0:T(8,128)S(1)}, f32[28,256]{1,0:T(8,128)S(1)}, u32[]{:S(2)}, u32[]{:S(2)}) collective-permute-start(f32[28,256]{1,0:T(8,128)S(1)} %get-tuple-element.57), channel_id=1, source_target_pairs={{0,12},{4,8},{8,4},{12,0},{1,13},{5,9},{9,5},{13,1},{2,14},{6,10},... | collective-permute-start | bytes 86024 | tf_op jit(solution)/shard_map/ppermute | solution.py:312
  105.5 18.3 %collective-permute-start.27 = (bf16[256,512]{1,0:T(8,128)(2,1)}, bf16[256,512]{1,0:T(8,128)(2,1)S(1)}, u32[]{:S(2)}, u32[]{:S(2)}) collective-permute-start(bf16[256,512]{1,0:T(8,128)(2,1)} %bitcast.64), channel_id=1, source_target_pairs={{0,4},{4,0},{8,12},{12,8},{1,5},{5,1},{9,13},{13,9},{2,6},{6,2},{1... | collective-permute-start | bytes 786440 | tf_op jit(solution)/shard_map/ppermute | solution.py:312
  108.6 21.2 %collective-permute-start.28 = (bf16[256,512]{1,0:T(8,128)(2,1)}, bf16[256,512]{1,0:T(8,128)(2,1)S(1)}, u32[]{:S(2)}, u32[]{:S(2)}) collective-permute-start(bf16[256,512]{1,0:T(8,128)(2,1)} %bitcast.63), channel_id=1, source_target_pairs={{0,8},{4,12},{8,0},{12,4},{1,9},{5,13},{9,1},{13,5},{2,10},{6,14},... | collective-permute-start | bytes 786440 | tf_op jit(solution)/shard_map/ppermute | solution.py:312
  109.4 2.0 copy-start.4
  109.5 20.4 %collective-permute-start.29 = (bf16[256,512]{1,0:T(8,128)(2,1)}, bf16[256,512]{1,0:T(8,128)(2,1)S(1)}, u32[]{:S(2)}, u32[]{:S(2)}) collective-permute-start(bf16[256,512]{1,0:T(8,128)(2,1)} %bitcast.62), channel_id=1, source_target_pairs={{0,12},{4,8},{8,4},{12,0},{1,13},{5,9},{9,5},{13,1},{2,14},{6,10},... | collective-permute-start | bytes 786440 | tf_op jit(solution)/shard_map/ppermute | solution.py:312
  123.8 6.0 %copy-start.13 = (bf16[256,512]{1,0:T(8,128)(2,1)}, bf16[256,512]{1,0:T(8,128)(2,1)S(1)}, u32[]{:S(2)}) copy-start(bf16[256,512]{1,0:T(8,128)(2,1)S(1)} %collective-permute-done.27.refs_4_.rest_1_) | copy-start | bytes 786436
  129.8 0.8 copy-start.15
  138.3 23.0 %copy-start.27 = (bf16[256,512]{1,0:T(8,128)(2,1)S(1)}, bf16[256,512]{1,0:T(8,128)(2,1)}, u32[]{:S(2)}) copy-start(bf16[256,512]{1,0:T(8,128)(2,1)} %get-tuple-element.20) | copy-start | bytes 786436
  138.3 9.6 %collective-permute-start.30 = (bf16[4,32,1024]{2,1,0:T(8,128)(2,1)}, bf16[4,32,1024]{2,1,0:T(8,128)(2,1)S(1)}, u32[]{:S(2)}, u32[]{:S(2)}) collective-permute-start(bf16[4,32,1024]{2,1,0:T(8,128)(2,1)} %get-tuple-element.26), channel_id=1, source_target_pairs={{0,4},{4,8},{8,12},{1,5},{5,9},{9,13},{2,6},{6,10},{10,14},{3,7},{... | collective-permute-start | bytes 786440 | tf_op jit(solution)/shard_map/ppermute | solution.py:347
  143.7 8.5 %collective-permute-start.31 = (bf16[4,32,1024]{2,1,0:T(8,128)(2,1)}, bf16[4,32,1024]{2,1,0:T(8,128)(2,1)S(1)}, u32[]{:S(2)}, u32[]{:S(2)}) collective-permute-start(bf16[4,32,1024]{2,1,0:T(8,128)(2,1)} %get-tuple-element.27), channel_id=1, source_target_pairs={{4,0},{8,4},{12,8},{5,1},{9,5},{13,9},{6,2},{10,6},{14,10},{7,3},{... | collective-permute-start | bytes 786440 | tf_op jit(solution)/shard_map/ppermute | solution.py:348
  147.9 14.7 %copy-start.22 = (bf16[4,32,1024]{2,1,0:T(8,128)(2,1)}, bf16[4,32,1024]{2,1,0:T(8,128)(2,1)S(1)}, u32[]{:S(2)}) copy-start(bf16[4,32,1024]{2,1,0:T(8,128)(2,1)S(1)} %collective-permute-done.30.row_low) | copy-start | bytes 786436
  152.2 27.9 %copy-start.23 = (bf16[4,32,1024]{2,1,0:T(8,128)(2,1)}, bf16[4,32,1024]{2,1,0:T(8,128)(2,1)S(1)}, u32[]{:S(2)}) copy-start(bf16[4,32,1024]{2,1,0:T(8,128)(2,1)S(1)} %collective-permute-done.31.row_high) | copy-start | bytes 786436
  153.1 28.3 %collective-permute-start.33 = (bf16[6,32,1024]{2,1,0:T(8,128)(2,1)}, bf16[6,32,1024]{2,1,0:T(8,128)(2,1)S(1)}, u32[]{:S(2)}, u32[]{:S(2)}) collective-permute-start(bf16[6,32,1024]{2,1,0:T(8,128)(2,1)} %pad_maximum_fusion.5), channel_id=1, source_target_pairs={{1,0},{2,1},{3,2},{5,4},{6,5},{7,6},{9,8},{10,9},{11,10},{13,12},{... | collective-permute-start | bytes 1179656 | tf_op jit(solution)/shard_map/ppermute | solution.py:355
  155.2 26.2 %collective-permute-start.32 = (bf16[6,32,1024]{2,1,0:T(8,128)(2,1)}, bf16[6,32,1024]{2,1,0:T(8,128)(2,1)S(1)}, u32[]{:S(2)}, u32[]{:S(2)}) collective-permute-start(bf16[6,32,1024]{2,1,0:T(8,128)(2,1)} %pad_maximum_fusion.4), channel_id=1, source_target_pairs={{0,1},{1,2},{2,3},{4,5},{5,6},{6,7},{8,9},{9,10},{10,11},{12,13},{... | collective-permute-start | bytes 1179656 | tf_op jit(solution)/shard_map/ppermute | solution.py:354
  158.4 20.7 %collective-permute-start.24 = (bf16[256,512]{1,0:T(8,128)(2,1)}, bf16[256,512]{1,0:T(8,128)(2,1)}, u32[]{:S(2)}, u32[]{:S(2)}) collective-permute-start(bf16[256,512]{1,0:T(8,128)(2,1)} %get-tuple-element.21), channel_id=1, source_target_pairs={{0,8},{4,12},{8,0},{12,4},{1,9},{5,13},{9,1},{13,5},{2,10},{6,14},... | collective-permute-start | bytes 786440 | tf_op jit(solution)/shard_map/ppermute | solution.py:312
  158.5 21.7 %collective-permute-start.25 = (bf16[256,512]{1,0:T(8,128)(2,1)}, bf16[256,512]{1,0:T(8,128)(2,1)}, u32[]{:S(2)}, u32[]{:S(2)}) collective-permute-start(bf16[256,512]{1,0:T(8,128)(2,1)} %get-tuple-element.22), channel_id=1, source_target_pairs={{0,12},{4,8},{8,4},{12,0},{1,13},{5,9},{9,5},{13,1},{2,14},{6,10},... | collective-permute-start | bytes 786440 | tf_op jit(solution)/shard_map/ppermute | solution.py:312
  161.3 39.7 %collective-permute-start.26 = (bf16[256,512]{1,0:T(8,128)(2,1)}, bf16[256,512]{1,0:T(8,128)(2,1)}, u32[]{:S(2)}, u32[]{:S(2)}) collective-permute-start(bf16[256,512]{1,0:T(8,128)(2,1)} %get-tuple-element.23), channel_id=1, source_target_pairs={{0,4},{4,0},{8,12},{12,8},{1,5},{5,1},{9,13},{13,9},{2,6},{6,2},{1... | collective-permute-start | bytes 786440 | tf_op jit(solution)/shard_map/ppermute | solution.py:312
  181.4 0.8 copy-start.25
  181.4 0.9 copy-start.26
  193.3 22.7 %collective-permute-start.34 = (bf16[256,512]{1,0:T(8,128)(2,1)}, bf16[256,512]{1,0:T(8,128)(2,1)S(1)}, u32[]{:S(2)}, u32[]{:S(2)}) collective-permute-start(bf16[256,512]{1,0:T(8,128)(2,1)} %get-tuple-element.29), channel_id=1, source_target_pairs={{0,8},{4,12},{8,0},{12,4},{1,9},{5,13},{9,1},{13,5},{2,10},{6,14},... | collective-permute-start | bytes 786440 | tf_op jit(solution)/shard_map/ppermute | solution.py:312
  197.4 18.7 %collective-permute-start.35 = (bf16[256,512]{1,0:T(8,128)(2,1)}, bf16[256,512]{1,0:T(8,128)(2,1)S(1)}, u32[]{:S(2)}, u32[]{:S(2)}) collective-permute-start(bf16[256,512]{1,0:T(8,128)(2,1)} %get-tuple-element.30), channel_id=1, source_target_pairs={{0,12},{4,8},{8,4},{12,0},{1,13},{5,9},{9,5},{13,1},{2,14},{6,10},... | collective-permute-start | bytes 786440 | tf_op jit(solution)/shard_map/ppermute | solution.py:312
  202.2 14.4 %copy-start.7 = (bf16[256,4,512]{2,1,0:T(4,128)(2,1)}, bf16[256,4,512]{2,1,0:T(4,128)(2,1)S(1)}, u32[]{:S(2)}) copy-start(bf16[256,4,512]{2,1,0:T(4,128)(2,1)S(1)} %constant_dynamic-update-slice_fusion.4) | copy-start | bytes 3145732
  203.4 16.1 %collective-permute-start.36 = (bf16[256,512]{1,0:T(8,128)(2,1)}, bf16[256,512]{1,0:T(8,128)(2,1)}, u32[]{:S(2)}, u32[]{:S(2)}) collective-permute-start(bf16[256,512]{1,0:T(8,128)(2,1)} %get-tuple-element.31), channel_id=1, source_target_pairs={{0,4},{4,0},{8,12},{12,8},{1,5},{5,1},{9,13},{13,9},{2,6},{6,2},{1... | collective-permute-start | bytes 786440 | tf_op jit(solution)/shard_map/ppermute | solution.py:312
  220.7 1.0 copy-start.6
  (4 other events, 2.9 us)

commit v5 on v4

--- a/solution.py
+++ b/solution.py
@@ -54,22 +54,45 @@
     return sums[1] + (before + after)
 
 
+def doubling(count):
+    masks = []
+    while count > 1:
+        masks.append(count - 1)
+        count //= 2
+    return masks
+
+
+def distances(count):
+    found = [0]
+    for mask in doubling(count):
+        found += [mask ^ distance for distance in found]
+    return found
+
+
 def piece_copies(here, mine, other, full, sems):
     chan, seat = here[0], here[1]
     copies = []
-    for side, pieces in enumerate((mine, other)):
-        for turn in range(pieces.shape[0]):
-            for shift in range(pieces.shape[1]):
+    for slot, distance in enumerate(distances(mine.shape[1])):
+        for side, pieces in enumerate((mine, other)):
+            for turn in range(pieces.shape[0]):
                 copies.append(
                     pltpu.make_async_copy(
-                        pieces.at[turn, shift],
-                        full.at[chan ^ shift, seat ^ side ^ (2 * turn)],
-                        sems.at[len(copies)],
+                        pieces.at[turn, slot],
+                        full.at[chan ^ distance, seat ^ side ^ (2 * turn)],
+                        sems.at[chan ^ distance, 2 * turn + side],
                     )
                 )
     return copies
 
 
+def wait_block(block, mine, other, full, sems):
+    for side, pieces in enumerate((mine, other)):
+        for turn in range(pieces.shape[0]):
+            pltpu.make_async_copy(
+                pieces.at[turn, 0], full.at[block, 2 * turn + side], sems.at[block, 2 * turn + side]
+            ).wait()
+
+
 def start_all(copies):
     for copy in copies:
         copy.start()
@@ -78,6 +101,13 @@
 def wait_all(copies):
     for copy in copies:
         copy.wait()
+
+
+def add_planes(base, product, out):
+    planes, _, width = base.shape
+    for z in range(planes):
+        total = base[z].astype(jnp.float32) + product[:, z * width : (z + 1) * width]
+        out[z] = total.astype(out.dtype)
 
 
 def forward_kernel(
@@ -115,8 +145,7 @@
                 (((1,), (1,)), ((), ())),
                 preferred_element_type=jnp.float32,
             )
-            total = inputs[shift][...].astype(jnp.float32) + product
-            outputs[shift][...] = total.astype(outputs[shift].dtype)
+            add_planes(inputs[shift], product, outputs[shift])
 
 
 def backward_kernel(
@@ -145,20 +174,19 @@
     def _():
         wait_all(copies)
         channels = grads.shape[1]
-        width = inputs[0].shape[0]
+        width = inputs[0].shape[1]
         for shift in range(count):
             start = pl.multiple_of((here[0] ^ shift) * width, width)
             columns = weight[:, :, :, pl.ds(start, width)].reshape(channels, width)
             product = jnp.dot(grads[...], columns, preferred_element_type=jnp.float32)
-            total = inputs[shift][...].astype(jnp.float32) + product.T
-            outputs[shift][...] = total.astype(outputs[shift].dtype)
+            add_planes(inputs[shift], product.T, outputs[shift])
 
 
 def weight_scratch(mine):
     turns, parts, share, channels = mine.shape
     return [
         pltpu.VMEM((parts, 2 * turns, share, channels), mine.dtype),
-        pltpu.SemaphoreType.DMA((2 * turns * parts,)),
+        pltpu.SemaphoreType.DMA((parts, 2 * turns)),
     ]
 
 
@@ -173,6 +201,13 @@
 
     def resident(shape):
         return pl.BlockSpec(shape, lambda c, here: (0,) * len(shape), pipeline_mode=pl.Buffered(1))
+
+    def table_at(c, here):
+        away = (c // per_table) ^ here[0]
+        slot = 0
+        for place, distance in enumerate(distances(taps.shape[0])):
+            slot = jnp.where(away == distance, place, slot)
+        return slot, 0, c % per_table
 
     anywhere = pl.BlockSpec(memory_space=pl.ANY)
     in_specs = [
@@ -181,9 +216,7 @@
         block(planes, extent),
         block(rows + 2, extent),
         block(rows + 2, extent),
-        pl.BlockSpec(
-            (1, 28, LANES), lambda c, here: ((c // per_table) ^ here[0], 0, c % per_table)
-        ),
+        pl.BlockSpec((1, 28, LANES), table_at),
         anywhere,
         anywhere,
     ]
@@ -211,10 +244,11 @@
 
 
 def turn_blocks(here, inputs, turned):
-    own = inputs[0].shape[0]
+    planes, own, width = inputs[0].shape
     for shift, block in enumerate(inputs):
         start = pl.multiple_of((here[0] ^ shift) * own, own)
-        turned[:, pl.ds(start, own)] = block[...].T
+        for z in range(planes):
+            turned[z * width : (z + 1) * width, pl.ds(start, own)] = block[z].T
 
 
 def put_with_rows(value, out, first, last):
@@ -231,11 +265,10 @@
 
     @pl.when(pl.program_id(0) == 0)
     def _():
-        copies = piece_copies(here, mine, other, weight, sems)
-        start_all(copies)
+        start_all(piece_copies(here, mine, other, weight, sems))
         turn_blocks(here, inputs, turned)
-        wait_all(copies)
-
+
+    wait_block(pl.program_id(0), mine, other, weight, sems)
     rows_of = weight[pl.program_id(0)]
     value = lax.dot_general(
         turned[...],
@@ -264,14 +297,17 @@
     put_with_rows((grad * slope[...]).astype(out.dtype), out, first, last)
 
 
-def product_call(here, blocks, weight, planes, slope=None):
-    own, cells = blocks[0].shape
+def product_call(here, blocks, weight, slope=None):
+    planes, own, width = blocks[0].shape
+    cells = planes * width
     count = len(blocks)
     channels = own * count
     dtype = blocks[0].dtype
     columns = pl.BlockSpec((cells, own), lambda c, here: (0, c))
     edge = pl.BlockSpec((planes, CX, own), lambda c, here: (0, 0, c))
-    whole = pl.BlockSpec((own, cells), lambda c, here: (0, 0), pipeline_mode=pl.Buffered(1))
+    whole = pl.BlockSpec(
+        blocks[0].shape, lambda c, here: (0, 0, 0), pipeline_mode=pl.Buffered(1)
+    )
     anywhere = pl.BlockSpec(memory_space=pl.ANY)
     kernel, extra = (hidden_kernel, []) if slope is None else (mix_kernel, [slope])
     edge_shape = jax.ShapeDtypeStruct((planes, CX, channels), dtype)
@@ -321,20 +357,27 @@
         def blocks(shift):
             start = (chan ^ shift) * width
             piece = lax.dynamic_slice_in_dim(field, start, width, axis=2)
-            return piece.reshape(own, planes * width)
+            return lax.optimization_barrier(piece.transpose(1, 0, 2))
 
         return blocks
 
     def paste(pieces):
         field = jnp.zeros((own, planes, cells), pieces[0].dtype)
         for shift in [0] + shifts:
-            piece = pieces[shift].reshape(own, planes, width)
+            piece = pieces[shift].transpose(1, 0, 2)
             field = lax.dynamic_update_slice_in_dim(field, piece, (chan ^ shift) * width, axis=2)
         return field
 
+    def gather_column(piece):
+        column = piece[None]
+        for mask in doubling(parts):
+            got = swap(column, "chan", lambda i: i ^ mask)
+            column = jnp.concatenate([column, got])
+        return column
+
     def gather_weight(weight):
         piece = lax.dynamic_slice_in_dim(weight, seat * share, share, axis=0)
-        column = jnp.stack(exchange(lambda shift: piece))
+        column = gather_column(piece)
         over_x = swap(column, others, lambda i: i ^ 2)
         over_y = swap(column, others, lambda i: i ^ 4)
         mixed = jnp.where(seat & 1 == 0, over_y, over_x)
@@ -359,16 +402,16 @@
     full_in = gather_weight(weight_in)
     full_out = gather_weight(weight_out)
     table = jnp.concatenate([filter_taps, filter_bias[:, None]], axis=1).T
-    taps = jnp.stack(exchange(lambda shift: table))
+    taps = gather_column(table)
     vol_blocks = exchange(cut(volume))
     grad_blocks = exchange(cut(out_grad))
-    hidden, first, last = product_call(here, vol_blocks, full_in, planes)
+    hidden, first, last = product_call(here, vol_blocks, full_in)
     hidden = hidden.reshape(grid)
     halo = halo_of(hidden, first, last)
     *out_blocks, slope = stencil(here, hidden, halo, taps, full_out, vol_blocks, True)
     block_out = paste(exchange(lambda shift: out_blocks[shift]))
     mix_grad, first, last = product_call(
-        here, grad_blocks, full_out, planes, slope.reshape(planes * width, channels)
+        here, grad_blocks, full_out, slope.reshape(planes * width, channels)
     )
     mix_grad = mix_grad.reshape(grid)
     halo = halo_of(mix_grad, first, last)

time: 223 us -> 208 us (0.933); the launches traced: 222 us -> 204 us
  waiting for transfers between devices: 92.4 us -> 73.4 us
  starting transfers between devices: 60 us -> 67.8 us
  local copies, waits for them, and re-layouts: 23.7 us -> 19.1 us
    ppermute x29 -> x26, waiting for transfers between devices: 77.2 us -> 59.2 us  [swap(): return lax.ppermute(part, axes, [(i, partner(i)) for i in range(count)])]
    ppermute x29 -> x26, starting transfers between devices: 36.2 us -> 41.7 us  [swap(): return lax.ppermute(part, axes, [(i, partner(i)) for i in range(count)])]
    reshape x8 -> x0, local copies, waits for them, and re-layouts: 5.46 us -> none  [paste(): piece = pieces[shift].reshape(own, planes, width)]
    ppermute x2, starting transfers between devices: 11.5 us -> 13.8 us  [halo_of(): row_low = lax.ppermute(last, 'chan', forward)]
    unnamed x70 -> x68, local copies, waits for them, and re-layouts: 10.2 us -> 10.1 us
  transfers between devices with their start and end apart: 37 -> 34, of which waited for: 20 -> 15; matrix products, arithmetic and copies ran while one was open for 10% -> 9% of each run, Pallas kernels for 13% -> 14%
where the time goes in v5:
time: 208 us; the launch traced here: 204 us
  waiting for transfers between devices  73.4 us (35%)
  starting transfers between devices  67.8 us (33%)
  Pallas kernels  36.9 us (18%)
  local copies, waits for them, and re-layouts  19.1 us (9%)
  other arithmetic  5.56 us (3%)
    ppermute x26, waiting for transfers between devices, swap(): return lax.ppermute(part, axes, [(i, partner(i)) for i in range(count)])  59.2 us
    ppermute x26, starting transfers between devices, swap(): return lax.ppermute(part, axes, [(i, partner(i)) for i in range(count)])  41.7 us
    pallas_call x2, Pallas kernels, stencil(): pl.pallas_call(forward_kernel if forward else backward_kernel, grid_spec=...  22.7 us
    pallas_call x2, Pallas kernels, product_call(): pl.pallas_call(lambda *refs: kernel(*refs, count=count), grid_spec=pltpu....  14.2 us
    ppermute x2, starting transfers between devices, halo_of(): row_low = lax.ppermute(last, 'chan', forward)  13.8 us
    ppermute x2, waiting for transfers between devices, halo_of(): row_high = lax.ppermute(first, 'chan', backward)  12.9 us
    unnamed x68, local copies, waits for them, and re-layouts  10.1 us
    ppermute x2, starting transfers between devices, halo_of(): plane_low = lax.ppermute(plane(-1), 'space', forward)  7.04 us
  transfers between devices with their start and end apart: 34, of which 15 were waited for; matrix products, arithmetic and copies ran while one was open for 9% of the time, Pallas kernels for 14%

profile of v5, /device:TPU:0, one launch (start us, length us, event | category | flops | bytes accessed | tf_op | source)
XLA Modules:
  0.0 204.0 jit_solution(2336289414696062656)
XLA Ops:
  0.7 1.0 copy-done
  1.7 5.1 %collective-permute-start = (bf16[1,32,1024]{2,1,0:T(8,128)(2,1)S(1)}, bf16[1,32,1024]{2,1,0:T(8,128)(2,1)S(1)}, u32[]{:S(2)}, u32[]{:S(2)}) collective-permute-start(bf16[1,32,1024]{2,1,0:T(8,128)(2,1)S(1)} %dynamic-slice_bitcast_fusion.1), channel_id=1, source_target_pairs={{0,12},{4,8},{8,4},{12,0},{1,13},{5,9},{9,5},{13,1},{2,14},{6,10},... | collective-permute-start | bytes 196616 | tf_op jit(solution)/shard_map/ppermute | solution.py:348
  6.8 2.2 %collective-permute-done = bf16[1,32,1024]{2,1,0:T(8,128)(2,1)S(1)} collective-permute-done((bf16[1,32,1024]{2,1,0:T(8,128)(2,1)S(1)}, bf16[1,32,1024]{2,1,0:T(8,128)(2,1)S(1)}, u32[]{:S(2)}, u32[]{:S(2)}) %collective-permute-start) | collective-permute-done | bytes 65568 | tf_op jit(solution)/shard_map/ppermute | solution.py:348
  9.0 1.2 collective-permute-start.1
  10.2 3.9 %collective-permute-done.1 = bf16[2,32,1024]{2,1,0:T(8,128)(2,1)S(1)} collective-permute-done((bf16[2,32,1024]{2,1,0:T(8,128)(2,1)S(1)}, bf16[2,32,1024]{2,1,0:T(8,128)(2,1)S(1)}, u32[]{:S(2)}, u32[]{:S(2)}) %collective-permute-start.1) | collective-permute-done | bytes 131104 | tf_op jit(solution)/shard_map/ppermute | solution.py:348
  14.1 1.8 collective-permute-start.2
  15.9 1.5 collective-permute-start.3
  17.4 3.1 %collective-permute-done.2 = bf16[4,32,1024]{2,1,0:T(8,128)(2,1)S(1)} collective-permute-done((bf16[4,32,1024]{2,1,0:T(8,128)(2,1)S(1)}, bf16[4,32,1024]{2,1,0:T(8,128)(2,1)S(1)}, u32[]{:S(2)}, u32[]{:S(2)}) %collective-permute-start.2) | collective-permute-done | bytes 262176 | tf_op jit(solution)/shard_map/ppermute | solution.py:348
  20.5 2.5 %collective-permute-done.3 = bf16[4,32,1024]{2,1,0:T(8,128)(2,1)S(1)} collective-permute-done((bf16[4,32,1024]{2,1,0:T(8,128)(2,1)S(1)}, bf16[4,32,1024]{2,1,0:T(8,128)(2,1)S(1)}, u32[]{:S(2)}, u32[]{:S(2)}) %collective-permute-start.3) | collective-permute-done | bytes 262176 | tf_op jit(solution)/shard_map/ppermute | solution.py:348
  23.5 0.8 dynamic-slice_bitcast_fusion
  24.4 4.2 %collective-permute-start.15 = (bf16[1,32,1024]{2,1,0:T(8,128)(2,1)S(1)}, bf16[1,32,1024]{2,1,0:T(8,128)(2,1)S(1)}, u32[]{:S(2)}, u32[]{:S(2)}) collective-permute-start(bf16[1,32,1024]{2,1,0:T(8,128)(2,1)S(1)} %dynamic-slice_bitcast_fusion), channel_id=1, source_target_pairs={{0,12},{4,8},{8,4},{12,0},{1,13},{5,9},{9,5},{13,1},{2,14},{6,10},... | collective-permute-start | bytes 196616 | tf_op jit(solution)/shard_map/ppermute | solution.py:348
  28.6 0.9 collective-permute-done.4
  29.7 1.1 collective-permute-done.15
  31.3 4.6 %collective-permute-done.16 = bf16[2,32,1024]{2,1,0:T(8,128)(2,1)S(1)} collective-permute-done((bf16[2,32,1024]{2,1,0:T(8,128)(2,1)S(1)}, bf16[2,32,1024]{2,1,0:T(8,128)(2,1)S(1)}, u32[]{:S(2)}, u32[]{:S(2)}) %collective-permute-start.16) | collective-permute-done | bytes 131104 | tf_op jit(solution)/shard_map/ppermute | solution.py:348
  35.9 0.8 fusion
  36.8 1.2 collective-permute-start.17
  38.0 1.5 collective-permute-start.18
  39.5 3.1 %constant_dynamic-slice_fusion = (bf16[256,4,128]{2,1,0:T(4,128)(2,1)}, bf16[256,4,128]{2,1,0:T(4,128)(2,1)}, bf16[256,4,128]{2,1,0:T(4,128)(2,1)}, bf16[256,4,1...) fusion(bf16[256,4,512]{2,1,0:T(4,128)(2,1)} %param.7, ...), kind=kLoop, calls=%fused_computation.33 | loop fusion | bytes 4194320 | tf_op jit(solution)/shard_map/dynamic_slice | solution.py:359
  42.7 0.9 collective-permute-start.6
  43.7 3.6 %collective-permute-start.7 = (bf16[4,256,128]{2,1,0:T(8,128)(2,1)S(1)}, bf16[4,256,128]{2,1,0:T(8,128)(2,1)S(1)}, u32[]{:S(2)}, u32[]{:S(2)}) collective-permute-start(bf16[4,256,128]{2,1,0:T(8,128)(2,1)S(1)} %bitcast.81), channel_id=1, source_target_pairs={{0,8},{4,12},{8,0},{12,4},{1,9},{5,13},{9,1},{13,5},{2,10},{6,14},... | collective-permute-start | bytes 786440 | tf_op jit(solution)/shard_map/ppermute | solution.py:348
  47.4 1.7 broadcast_select_fusion
  49.0 1.1 collective-permute-start.19
  50.1 0.7 copy.55
  51.5 2.3 %collective-permute-done.6.refs_4_.rest_1_ = bf16[4,256,128]{2,1,0:T(8,128)(2,1)S(1)} collective-permute-done((bf16[4,256,128]{2,1,0:T(8,128)(2,1)S(1)}, bf16[4,256,128]{2,1,0:T(8,128)(2,1)S(1)}, u32[]{:S(2)}, u32[]{:S(2)}) %collective-permute-start.6) | collective-permute-done | bytes 262176 | tf_op jit(solution)/shard_map/ppermute | solution.py:348
  53.8 2.0 collective-permute-start.13
  55.8 9.6 %collective-permute-done.7.refs_5_.rest_2_ = bf16[4,256,128]{2,1,0:T(8,128)(2,1)S(1)} collective-permute-done((bf16[4,256,128]{2,1,0:T(8,128)(2,1)S(1)}, bf16[4,256,128]{2,1,0:T(8,128)(2,1)S(1)}, u32[]{:S(2)}, u32[]{:S(2)}) %collective-permute-start.7) | collective-permute-done | bytes 262176 | tf_op jit(solution)/shard_map/ppermute | solution.py:348
  65.4 0.7 copy-done.9
  66.2 1.0 copy-done.3
  67.2 6.5 %shard_map.77 = (bf16[512,1024]{1,0:T(8,128)(2,1)}, bf16[4,32,1024]{2,1,0:T(8,128)(2,1)}, bf16[4,32,1024]{2,1,0:T(8,128)(2,1)}) custom-call(s32[2]{0:T(128)} %pad_add_fusion.refs_0_.here, bf16[4,4,32,1024]{3,2,1,0:T(8,128)(2,1)} %copy-done.1, bf16[4,4,32,1024]{3,2,1,0:T(8,128)(2,1)} %copy-done.3, bf16[4,256,128]{2,1,0:T(8,128)(2,1)} %bitcast.62, ...), custom_call_target="tpu_custom_call" | custom-call | tf_op jit(solution)/shard_map/pallas_call | solution.py:314
  73.7 7.0 %collective-permute-start.9 = (bf16[4,32,1024]{2,1,0:T(8,128)(2,1)}, bf16[4,32,1024]{2,1,0:T(8,128)(2,1)S(1)}, u32[]{:S(2)}, u32[]{:S(2)}) collective-permute-start(bf16[4,32,1024]{2,1,0:T(8,128)(2,1)} %get-tuple-element.18), channel_id=1, source_target_pairs={{0,4},{4,8},{8,12},{1,5},{5,9},{9,13},{2,6},{6,10},{10,14},{3,7},{... | collective-permute-start | bytes 786440 | tf_op jit(solution)/shard_map/ppermute | solution.py:390
  80.7 1.3 pad_maximum_fusion.1.mine.refs_1_
  82.2 1.4 collective-permute-start.10
  83.7 1.2 collective-permute-done.9.row_low
  84.9 7.8 %collective-permute-done.10.row_high = bf16[4,32,1024]{2,1,0:T(8,128)(2,1)S(1)} collective-permute-done((bf16[4,32,1024]{2,1,0:T(8,128)(2,1)S(1)}, bf16[4,32,1024]{2,1,0:T(8,128)(2,1)S(1)}, u32[]{:S(2)}, u32[]{:S(2)}) %collective-permute-start.10) | collective-permute-done | bytes 262176 | tf_op jit(solution)/shard_map/ppermute | solution.py:391
  92.8 1.3 collective-permute-start.12
  94.2 3.8 %collective-permute-start.11 = (bf16[6,32,1024]{2,1,0:T(8,128)(2,1)S(1)}, bf16[6,32,1024]{2,1,0:T(8,128)(2,1)}, u32[]{:S(2)}, u32[]{:S(2)}) collective-permute-start(bf16[6,32,1024]{2,1,0:T(8,128)(2,1)S(1)} %pad_maximum_fusion.2), channel_id=1, source_target_pairs={{0,1},{1,2},{2,3},{4,5},{5,6},{6,7},{8,9},{9,10},{10,11},{12,13},{... | collective-permute-start | bytes 1179656 | tf_op jit(solution)/shard_map/ppermute | solution.py:397
  98.0 0.8 collective-permute-start.14
  98.8 0.7 copy.50
  99.5 1.3 collective-permute-start.24
  100.8 0.8 copy.49
  101.6 0.8 copy.48
  102.4 0.7 collective-permute-start.25
  103.1 2.5 %collective-permute-start.26 = (bf16[4,256,128]{2,1,0:T(8,128)(2,1)}, bf16[4,256,128]{2,1,0:T(8,128)(2,1)S(1)}, u32[]{:S(2)}, u32[]{:S(2)}) collective-permute-start(bf16[4,256,128]{2,1,0:T(8,128)(2,1)} %bitcast.52), channel_id=1, source_target_pairs={{0,12},{4,8},{8,4},{12,0},{1,13},{5,9},{9,5},{13,1},{2,14},{6,10},... | collective-permute-start | bytes 786440 | tf_op jit(solution)/shard_map/ppermute | solution.py:348
  105.6 0.7 copy.51
  107.0 0.7 copy-done.22
  107.8 11.7 %shard_map.78 = (bf16[4,256,128]{2,1,0:T(8,128)(2,1)}, bf16[4,256,128]{2,1,0:T(8,128)(2,1)}, bf16[4,256,128]{2,1,0:T(8,128)(2,1)}, bf16[4,256,128]{2,1,0:T(8,128)(2,1)}, f32[4,4,32,1024]{3,2,1,0:T(8,128)}) custom-call(s32[2]{0:T(128)} %pad_add_fusion.refs_0_.here, bf16[4,4,32,1024]{3,2,1,0:T(8,128)(2,1)} %bitcast.60, bf16[4,32,1024]{2,1,0:T(8,128)(2,1)} %copy-done.18, ...), custom_call_target="tpu_custom_call" | custom-call | tf_op jit(solution)/shard_map/pallas_call | solution.py:229
  119.5 4.4 %collective-permute-done.25.refs_5_.rest_2_ = bf16[4,256,128]{2,1,0:T(8,128)(2,1)S(1)} collective-permute-done((bf16[4,256,128]{2,1,0:T(8,128)(2,1)}, bf16[4,256,128]{2,1,0:T(8,128)(2,1)S(1)}, u32[]{:S(2)}, u32[]{:S(2)}) %collective-permute-start.25) | collective-permute-done | bytes 262176 | tf_op jit(solution)/shard_map/ppermute | solution.py:348
  124.7 7.7 %shard_map.79 = (bf16[512,1024]{1,0:T(8,128)(2,1)}, bf16[4,32,1024]{2,1,0:T(8,128)(2,1)}, bf16[4,32,1024]{2,1,0:T(8,128)(2,1)}) custom-call(s32[2]{0:T(128)} %pad_add_fusion.refs_0_.here, bf16[4,4,32,1024]{3,2,1,0:T(8,128)(2,1)} %copy-done.2, bf16[4,4,32,1024]{3,2,1,0:T(8,128)(2,1)} %copy-done.4, bf16[4,256,128]{2,1,0:T(8,128)(2,1)} %bitcast.64, ...), custom_call_target="tpu_custom_call" | custom-call | tf_op jit(solution)/shard_map/pallas_call | solution.py:314
  132.4 6.8 %collective-permute-start.27 = (bf16[4,32,1024]{2,1,0:T(8,128)(2,1)}, bf16[4,32,1024]{2,1,0:T(8,128)(2,1)S(1)}, u32[]{:S(2)}, u32[]{:S(2)}) collective-permute-start(bf16[4,32,1024]{2,1,0:T(8,128)(2,1)} %get-tuple-element.26), channel_id=1, source_target_pairs={{0,4},{4,8},{8,12},{1,5},{5,9},{9,13},{2,6},{6,10},{10,14},{3,7},{... | collective-permute-start | bytes 786440 | tf_op jit(solution)/shard_map/ppermute | solution.py:390
  139.2 1.1 fusion.2
  140.3 1.3 collective-permute-start.28
  141.6 2.1 %collective-permute-start.21 = (bf16[4,256,128]{2,1,0:T(8,128)(2,1)}, bf16[4,256,128]{2,1,0:T(8,128)(2,1)S(1)}, u32[]{:S(2)}, u32[]{:S(2)}) collective-permute-start(bf16[4,256,128]{2,1,0:T(8,128)(2,1)} %get-tuple-element.21), channel_id=1, source_target_pairs={{0,8},{4,12},{8,0},{12,4},{1,9},{5,13},{9,1},{13,5},{2,10},{6,14},... | collective-permute-start | bytes 786440 | tf_op jit(solution)/shard_map/ppermute | solution.py:348
  143.7 2.9 %collective-permute-start.22 = (bf16[4,256,128]{2,1,0:T(8,128)(2,1)}, bf16[4,256,128]{2,1,0:T(8,128)(2,1)S(1)}, u32[]{:S(2)}, u32[]{:S(2)}) collective-permute-start(bf16[4,256,128]{2,1,0:T(8,128)(2,1)} %get-tuple-element.22), channel_id=1, source_target_pairs={{0,12},{4,8},{8,4},{12,0},{1,13},{5,9},{9,5},{13,1},{2,14},{6,10},... | collective-permute-start | bytes 786440 | tf_op jit(solution)/shard_map/ppermute | solution.py:348
  147.3 5.1 %collective-permute-done.28.row_high = bf16[4,32,1024]{2,1,0:T(8,128)(2,1)S(1)} collective-permute-done((bf16[4,32,1024]{2,1,0:T(8,128)(2,1)}, bf16[4,32,1024]{2,1,0:T(8,128)(2,1)S(1)}, u32[]{:S(2)}, u32[]{:S(2)}) %collective-permute-start.28) | collective-permute-done | bytes 262176 | tf_op jit(solution)/shard_map/ppermute | solution.py:391
  152.5 1.3 collective-permute-start.30
  153.8 3.2 %collective-permute-start.29 = (bf16[6,32,1024]{2,1,0:T(8,128)(2,1)S(1)}, bf16[6,32,1024]{2,1,0:T(8,128)(2,1)S(1)}, u32[]{:S(2)}, u32[]{:S(2)}) collective-permute-start(bf16[6,32,1024]{2,1,0:T(8,128)(2,1)S(1)} %pad_maximum_fusion.4), channel_id=1, source_target_pairs={{0,1},{1,2},{2,3},{4,5},{5,6},{6,7},{8,9},{9,10},{10,11},{12,13},{... | collective-permute-start | bytes 1179656 | tf_op jit(solution)/shard_map/ppermute | solution.py:397
  157.1 10.8 %collective-permute-done.21 = bf16[4,256,128]{2,1,0:T(8,128)(2,1)S(1)} collective-permute-done((bf16[4,256,128]{2,1,0:T(8,128)(2,1)}, bf16[4,256,128]{2,1,0:T(8,128)(2,1)S(1)}, u32[]{:S(2)}, u32[]{:S(2)}) %collective-permute-start.21) | collective-permute-done | bytes 262176 | tf_op jit(solution)/shard_map/ppermute | solution.py:348
  168.6 0.7 copy-done.23
  169.4 11.0 %shard_map.80 = (bf16[4,256,128]{2,1,0:T(8,128)(2,1)}, bf16[4,256,128]{2,1,0:T(8,128)(2,1)}, bf16[4,256,128]{2,1,0:T(8,128)(2,1)}, bf16[4,256,128]{2,1,0:T(8,128)(2,1)}) custom-call(s32[2]{0:T(128)} %pad_add_fusion.refs_0_.here, bf16[4,4,32,1024]{3,2,1,0:T(8,128)(2,1)} %bitcast.61, bf16[4,32,1024]{2,1,0:T(8,128)(2,1)} %copy-done.20, ...), custom_call_target="tpu_custom_call" | custom-call | tf_op jit(solution)/shard_map/pallas_call | solution.py:229
  180.4 2.8 %collective-permute-start.31 = (bf16[4,256,128]{2,1,0:T(8,128)(2,1)}, bf16[4,256,128]{2,1,0:T(8,128)(2,1)S(1)}, u32[]{:S(2)}, u32[]{:S(2)}) collective-permute-start(bf16[4,256,128]{2,1,0:T(8,128)(2,1)} %get-tuple-element.29), channel_id=1, source_target_pairs={{0,8},{4,12},{8,0},{12,4},{1,9},{5,13},{9,1},{13,5},{2,10},{6,14},... | collective-permute-start | bytes 786440 | tf_op jit(solution)/shard_map/ppermute | solution.py:348
  183.5 3.3 %collective-permute-start.32 = (bf16[4,256,128]{2,1,0:T(8,128)(2,1)}, bf16[4,256,128]{2,1,0:T(8,128)(2,1)S(1)}, u32[]{:S(2)}, u32[]{:S(2)}) collective-permute-start(bf16[4,256,128]{2,1,0:T(8,128)(2,1)} %get-tuple-element.30), channel_id=1, source_target_pairs={{0,12},{4,8},{8,4},{12,0},{1,13},{5,9},{9,5},{13,1},{2,14},{6,10},... | collective-permute-start | bytes 786440 | tf_op jit(solution)/shard_map/ppermute | solution.py:348
  187.1 1.2 copy_dynamic-update-slice_fusion.3
  188.4 13.7 %collective-permute-done.31 = bf16[4,256,128]{2,1,0:T(8,128)(2,1)S(1)} collective-permute-done((bf16[4,256,128]{2,1,0:T(8,128)(2,1)}, bf16[4,256,128]{2,1,0:T(8,128)(2,1)S(1)}, u32[]{:S(2)}, u32[]{:S(2)}) %collective-permute-start.31) | collective-permute-done | bytes 262176 | tf_op jit(solution)/shard_map/ppermute | solution.py:348
  203.0 1.0 copy-done.6
  (111 shorter events, 6.9 us)
Async XLA Ops:
  0.6 1.0 copy-start
  1.7 7.3 %collective-permute-start = (bf16[1,32,1024]{2,1,0:T(8,128)(2,1)S(1)}, bf16[1,32,1024]{2,1,0:T(8,128)(2,1)S(1)}, u32[]{:S(2)}, u32[]{:S(2)}) collective-permute-start(bf16[1,32,1024]{2,1,0:T(8,128)(2,1)S(1)} %dynamic-slice_bitcast_fusion.1), channel_id=1, source_target_pairs={{0,12},{4,8},{8,4},{12,0},{1,13},{5,9},{9,5},{13,1},{2,14},{6,10},... | collective-permute-start | bytes 196616 | tf_op jit(solution)/shard_map/ppermute | solution.py:348
  9.0 5.0 %collective-permute-start.1 = (bf16[2,32,1024]{2,1,0:T(8,128)(2,1)S(1)}, bf16[2,32,1024]{2,1,0:T(8,128)(2,1)S(1)}, u32[]{:S(2)}, u32[]{:S(2)}) collective-permute-start(bf16[2,32,1024]{2,1,0:T(8,128)(2,1)S(1)} %pad_maximum_fusion.8), channel_id=1, source_target_pairs={{0,4},{4,0},{8,12},{12,8},{1,5},{5,1},{9,13},{13,9},{2,6},{6,2},{1... | collective-permute-start | bytes 393224 | tf_op jit(solution)/shard_map/ppermute | solution.py:348
  14.1 6.4 %collective-permute-start.2 = (bf16[4,32,1024]{2,1,0:T(8,128)(2,1)S(1)}, bf16[4,32,1024]{2,1,0:T(8,128)(2,1)S(1)}, u32[]{:S(2)}, u32[]{:S(2)}) collective-permute-start(bf16[4,32,1024]{2,1,0:T(8,128)(2,1)S(1)} %get-tuple-element.55), channel_id=1, source_target_pairs={{0,2},{1,3},{2,0},{3,1},{16,18},{17,19},{18,16},{19,17},{4,6},{5,7... | collective-permute-start | bytes 786440 | tf_op jit(solution)/shard_map/ppermute | solution.py:348
  15.9 7.2 %collective-permute-start.3 = (bf16[4,32,1024]{2,1,0:T(8,128)(2,1)S(1)}, bf16[4,32,1024]{2,1,0:T(8,128)(2,1)S(1)}, u32[]{:S(2)}, u32[]{:S(2)}) collective-permute-start(bf16[4,32,1024]{2,1,0:T(8,128)(2,1)S(1)} %get-tuple-element.55), channel_id=1, source_target_pairs={{0,16},{1,17},{2,18},{3,19},{16,0},{17,1},{18,2},{19,3},{4,20},{5,... | collective-permute-start | bytes 786440 | tf_op jit(solution)/shard_map/ppermute | solution.py:348
  23.1 6.4 %collective-permute-start.4 = (bf16[4,32,1024]{2,1,0:T(8,128)(2,1)S(1)}, bf16[4,32,1024]{2,1,0:T(8,128)(2,1)S(1)}, u32[]{:S(2)}, u32[]{:S(2)}) collective-permute-start(bf16[4,32,1024]{2,1,0:T(8,128)(2,1)S(1)} %broadcast_select_fusion.1), channel_id=1, source_target_pairs={{0,2},{1,17},{2,0},{3,19},{16,18},{17,1},{18,16},{19,3},{4,6},{5,2... | collective-permute-start | bytes 786440 | tf_op jit(solution)/shard_map/ppermute | solution.py:348
  24.4 6.5 %collective-permute-start.15 = (bf16[1,32,1024]{2,1,0:T(8,128)(2,1)S(1)}, bf16[1,32,1024]{2,1,0:T(8,128)(2,1)S(1)}, u32[]{:S(2)}, u32[]{:S(2)}) collective-permute-start(bf16[1,32,1024]{2,1,0:T(8,128)(2,1)S(1)} %dynamic-slice_bitcast_fusion), channel_id=1, source_target_pairs={{0,12},{4,8},{8,4},{12,0},{1,13},{5,9},{9,5},{13,1},{2,14},{6,10},... | collective-permute-start | bytes 196616 | tf_op jit(solution)/shard_map/ppermute | solution.py:348
  29.7 13.0 %copy-start.1 = (bf16[4,4,32,1024]{3,2,1,0:T(8,128)(2,1)}, bf16[4,4,32,1024]{3,2,1,0:T(8,128)(2,1)S(1)}, u32[]{:S(2)}) copy-start(bf16[4,4,32,1024]{3,2,1,0:T(8,128)(2,1)S(1)} %pad_maximum_fusion.refs_1_.mine) | copy-start | bytes 3145732
  29.7 35.7 %collective-permute-start.5 = (bf16[4,4,32,1024]{3,2,1,0:T(8,128)(2,1)S(1)}, bf16[4,4,32,1024]{3,2,1,0:T(8,128)(2,1)S(1)}, u32[]{:S(2)}, u32[]{:S(2)}) collective-permute-start(bf16[4,4,32,1024]{3,2,1,0:T(8,128)(2,1)S(1)} %pad_maximum_fusion.refs_1_.mine), channel_id=1, source_target_pairs={{0,1},{1,0},{2,3},{3,2},{16,17},{17,16},{18,19},{19,18},{4,5},{5,4... | collective-permute-start | bytes 3145736 | tf_op jit(solution)/shard_map/ppermute | solution.py:348
  30.9 5.0 %collective-permute-start.16 = (bf16[2,32,1024]{2,1,0:T(8,128)(2,1)S(1)}, bf16[2,32,1024]{2,1,0:T(8,128)(2,1)S(1)}, u32[]{:S(2)}, u32[]{:S(2)}) collective-permute-start(bf16[2,32,1024]{2,1,0:T(8,128)(2,1)S(1)} %pad_maximum_fusion.10), channel_id=1, source_target_pairs={{0,4},{4,0},{8,12},{12,8},{1,5},{5,1},{9,13},{13,9},{2,6},{6,2},{1... | collective-permute-start | bytes 393224 | tf_op jit(solution)/shard_map/ppermute | solution.py:348
  36.8 10.5 %collective-permute-start.17 = (bf16[4,32,1024]{2,1,0:T(8,128)(2,1)}, bf16[4,32,1024]{2,1,0:T(8,128)(2,1)}, u32[]{:S(2)}, u32[]{:S(2)}) collective-permute-start(bf16[4,32,1024]{2,1,0:T(8,128)(2,1)} %get-tuple-element.49), channel_id=1, source_target_pairs={{0,2},{1,3},{2,0},{3,1},{16,18},{17,19},{18,16},{19,17},{4,6},{5,7... | collective-permute-start | bytes 786440 | tf_op jit(solution)/shard_map/ppermute | solution.py:348
  38.0 9.4 %collective-permute-start.18 = (bf16[4,32,1024]{2,1,0:T(8,128)(2,1)}, bf16[4,32,1024]{2,1,0:T(8,128)(2,1)}, u32[]{:S(2)}, u32[]{:S(2)}) collective-permute-start(bf16[4,32,1024]{2,1,0:T(8,128)(2,1)} %get-tuple-element.49), channel_id=1, source_target_pairs={{0,16},{1,17},{2,18},{3,19},{16,0},{17,1},{18,2},{19,3},{4,20},{5,... | collective-permute-start | bytes 786440 | tf_op jit(solution)/shard_map/ppermute | solution.py:348
  42.6 8.9 %copy-start.26 = (f32[256,27]{0,1:T(8,128)S(1)}, f32[256,27]{0,1:T(8,128)}, u32[]{:S(2)}) copy-start(f32[256,27]{0,1:T(8,128)} %param.10) | copy-start | bytes 82948
  42.6 8.9 %copy-start.27 = (f32[256]{0:T(256)S(1)}, f32[256]{0:T(256)}, u32[]{:S(2)}) copy-start(f32[256]{0:T(256)} %param.11) | copy-start | bytes 3076
  42.7 11.1 %collective-permute-start.6 = (bf16[4,256,128]{2,1,0:T(8,128)(2,1)S(1)}, bf16[4,256,128]{2,1,0:T(8,128)(2,1)S(1)}, u32[]{:S(2)}, u32[]{:S(2)}) collective-permute-start(bf16[4,256,128]{2,1,0:T(8,128)(2,1)S(1)} %bitcast.82), channel_id=1, source_target_pairs={{0,4},{4,0},{8,12},{12,8},{1,5},{5,1},{9,13},{13,9},{2,6},{6,2},{1... | collective-permute-start | bytes 786440 | tf_op jit(solution)/shard_map/ppermute | solution.py:348
  43.7 21.7 %collective-permute-start.7 = (bf16[4,256,128]{2,1,0:T(8,128)(2,1)S(1)}, bf16[4,256,128]{2,1,0:T(8,128)(2,1)S(1)}, u32[]{:S(2)}, u32[]{:S(2)}) collective-permute-start(bf16[4,256,128]{2,1,0:T(8,128)(2,1)S(1)} %bitcast.81), channel_id=1, source_target_pairs={{0,8},{4,12},{8,0},{12,4},{1,9},{5,13},{9,1},{13,5},{2,10},{6,14},... | collective-permute-start | bytes 786440 | tf_op jit(solution)/shard_map/ppermute | solution.py:348
  47.3 18.1 %collective-permute-start.8 = (bf16[4,256,128]{2,1,0:T(8,128)(2,1)S(1)}, bf16[4,256,128]{2,1,0:T(8,128)(2,1)S(1)}, u32[]{:S(2)}, u32[]{:S(2)}) collective-permute-start(bf16[4,256,128]{2,1,0:T(8,128)(2,1)S(1)} %bitcast.83), channel_id=1, source_target_pairs={{0,12},{4,8},{8,4},{12,0},{1,13},{5,9},{9,5},{13,1},{2,14},{6,10},... | collective-permute-start | bytes 786440 | tf_op jit(solution)/shard_map/ppermute | solution.py:348
  49.0 31.7 %collective-permute-start.19 = (bf16[4,32,1024]{2,1,0:T(8,128)(2,1)}, bf16[4,32,1024]{2,1,0:T(8,128)(2,1)}, u32[]{:S(2)}, u32[]{:S(2)}) collective-permute-start(bf16[4,32,1024]{2,1,0:T(8,128)(2,1)} %broadcast_select_fusion), channel_id=1, source_target_pairs={{0,2},{1,17},{2,0},{3,19},{16,18},{17,1},{18,16},{19,3},{4,6},{5,2... | collective-permute-start | bytes 786440 | tf_op jit(solution)/shard_map/ppermute | solution.py:348
  53.8 11.6 %copy-start.8 = (bf16[4,256,128]{2,1,0:T(8,128)(2,1)}, bf16[4,256,128]{2,1,0:T(8,128)(2,1)S(1)}, u32[]{:S(2)}) copy-start(bf16[4,256,128]{2,1,0:T(8,128)(2,1)S(1)} %collective-permute-done.6.refs_4_.rest_1_) | copy-start | bytes 786436
  53.8 44.2 %collective-permute-start.13 = (f32[1,28,256]{2,1,0:T(8,128)S(1)}, f32[1,28,256]{2,1,0:T(8,128)S(1)}, u32[]{:S(2)}, u32[]{:S(2)}) collective-permute-start(f32[1,28,256]{2,1,0:T(8,128)S(1)} %maximum_bitcast_fusion), channel_id=1, source_target_pairs={{0,12},{4,8},{8,4},{12,0},{1,13},{5,9},{9,5},{13,1},{2,14},{6,10},... | collective-permute-start | bytes 86024 | tf_op jit(solution)/shard_map/ppermute | solution.py:348
  65.4 0.7 copy-start.9
  65.4 0.8 copy-start.10
  66.2 1.0 copy-start.3
  73.7 8.5 %copy-start.29 = (bf16[4,32,1024]{2,1,0:T(8,128)(2,1)S(1)}, bf16[4,32,1024]{2,1,0:T(8,128)(2,1)}, u32[]{:S(2)}) copy-start(bf16[4,32,1024]{2,1,0:T(8,128)(2,1)} %get-tuple-element.19) | copy-start | bytes 786436
  73.7 9.9 %copy-start.5 = (bf16[512,1024]{1,0:T(8,128)(2,1)S(1)}, bf16[512,1024]{1,0:T(8,128)(2,1)}, u32[]{:S(2)}) copy-start(bf16[512,1024]{1,0:T(8,128)(2,1)} %get-tuple-element.17) | copy-start | bytes 3145732
  73.7 11.2 %collective-permute-start.9 = (bf16[4,32,1024]{2,1,0:T(8,128)(2,1)}, bf16[4,32,1024]{2,1,0:T(8,128)(2,1)S(1)}, u32[]{:S(2)}, u32[]{:S(2)}) collective-permute-start(bf16[4,32,1024]{2,1,0:T(8,128)(2,1)} %get-tuple-element.18), channel_id=1, source_target_pairs={{0,4},{4,8},{8,12},{1,5},{5,9},{9,13},{2,6},{6,10},{10,14},{3,7},{... | collective-permute-start | bytes 786440 | tf_op jit(solution)/shard_map/ppermute | solution.py:390
  82.0 19.6 %copy-start.2 = (bf16[4,4,32,1024]{3,2,1,0:T(8,128)(2,1)}, bf16[4,4,32,1024]{3,2,1,0:T(8,128)(2,1)S(1)}, u32[]{:S(2)}) copy-start(bf16[4,4,32,1024]{3,2,1,0:T(8,128)(2,1)S(1)} %pad_maximum_fusion.1.mine.refs_1_) | copy-start | bytes 3145732
  82.1 16.7 %copy-start.17 = (bf16[256,4,128]{2,1,0:T(4,128)(2,1)S(1)}, bf16[256,4,128]{2,1,0:T(4,128)(2,1)}, u32[]{:S(2)}) copy-start(bf16[256,4,128]{2,1,0:T(4,128)(2,1)} %get-tuple-element.36) | copy-start | bytes 786436
  82.1 18.8 %copy-start.16 = (bf16[256,4,128]{2,1,0:T(4,128)(2,1)S(1)}, bf16[256,4,128]{2,1,0:T(4,128)(2,1)}, u32[]{:S(2)}) copy-start(bf16[256,4,128]{2,1,0:T(4,128)(2,1)} %get-tuple-element.35) | copy-start | bytes 786436
  82.1 21.0 %collective-permute-start.20 = (bf16[4,4,32,1024]{3,2,1,0:T(8,128)(2,1)S(1)}, bf16[4,4,32,1024]{3,2,1,0:T(8,128)(2,1)S(1)}, u32[]{:S(2)}, u32[]{:S(2)}) collective-permute-start(bf16[4,4,32,1024]{3,2,1,0:T(8,128)(2,1)S(1)} %pad_maximum_fusion.1.mine.refs_1_), channel_id=1, source_target_pairs={{0,1},{1,0},{2,3},{3,2},{16,17},{17,16},{18,19},{19,18},{4,5},{5,4... | collective-permute-start | bytes 3145736 | tf_op jit(solution)/shard_map/ppermute | solution.py:348
  82.2 10.6 %collective-permute-start.10 = (bf16[4,32,1024]{2,1,0:T(8,128)(2,1)S(1)}, bf16[4,32,1024]{2,1,0:T(8,128)(2,1)S(1)}, u32[]{:S(2)}, u32[]{:S(2)}) collective-permute-start(bf16[4,32,1024]{2,1,0:T(8,128)(2,1)S(1)} %copy-done.29), channel_id=1, source_target_pairs={{4,0},{8,4},{12,8},{5,1},{9,5},{13,9},{6,2},{10,6},{14,10},{7,3},{... | collective-permute-start | bytes 786440 | tf_op jit(solution)/shard_map/ppermute | solution.py:391
  83.6 18.0 %copy-start.15 = (bf16[256,4,128]{2,1,0:T(4,128)(2,1)S(1)}, bf16[256,4,128]{2,1,0:T(4,128)(2,1)}, u32[]{:S(2)}) copy-start(bf16[256,4,128]{2,1,0:T(4,128)(2,1)} %get-tuple-element.34) | copy-start | bytes 786436
  83.7 21.9 %copy-start.14 = (bf16[256,4,128]{2,1,0:T(4,128)(2,1)S(1)}, bf16[256,4,128]{2,1,0:T(4,128)(2,1)}, u32[]{:S(2)}) copy-start(bf16[256,4,128]{2,1,0:T(4,128)(2,1)} %get-tuple-element.37) | copy-start | bytes 786436
  84.9 21.5 %copy-start.18 = (bf16[4,32,1024]{2,1,0:T(8,128)(2,1)}, bf16[4,32,1024]{2,1,0:T(8,128)(2,1)S(1)}, u32[]{:S(2)}) copy-start(bf16[4,32,1024]{2,1,0:T(8,128)(2,1)S(1)} %collective-permute-done.9.row_low) | copy-start | bytes 786436
  92.7 14.2 %copy-start.19 = (bf16[4,32,1024]{2,1,0:T(8,128)(2,1)}, bf16[4,32,1024]{2,1,0:T(8,128)(2,1)S(1)}, u32[]{:S(2)}) copy-start(bf16[4,32,1024]{2,1,0:T(8,128)(2,1)S(1)} %collective-permute-done.10.row_high) | copy-start | bytes 786436
  92.8 14.2 %collective-permute-start.12 = (bf16[6,32,1024]{2,1,0:T(8,128)(2,1)S(1)}, bf16[6,32,1024]{2,1,0:T(8,128)(2,1)S(1)}, u32[]{:S(2)}, u32[]{:S(2)}) collective-permute-start(bf16[6,32,1024]{2,1,0:T(8,128)(2,1)S(1)} %pad_maximum_fusion.3), channel_id=1, source_target_pairs={{1,0},{2,1},{3,2},{5,4},{6,5},{7,6},{9,8},{10,9},{11,10},{13,12},{... | collective-permute-start | bytes 1179656 | tf_op jit(solution)/shard_map/ppermute | solution.py:398
  94.2 12.8 %collective-permute-start.11 = (bf16[6,32,1024]{2,1,0:T(8,128)(2,1)S(1)}, bf16[6,32,1024]{2,1,0:T(8,128)(2,1)}, u32[]{:S(2)}, u32[]{:S(2)}) collective-permute-start(bf16[6,32,1024]{2,1,0:T(8,128)(2,1)S(1)} %pad_maximum_fusion.2), channel_id=1, source_target_pairs={{0,1},{1,2},{2,3},{4,5},{5,6},{6,7},{8,9},{9,10},{10,11},{12,13},{... | collective-permute-start | bytes 1179656 | tf_op jit(solution)/shard_map/ppermute | solution.py:397
  98.0 4.4 %collective-permute-start.14 = (f32[2,28,256]{2,1,0:T(8,128)S(1)}, f32[2,28,256]{2,1,0:T(8,128)S(1)}, u32[]{:S(2)}, u32[]{:S(2)}) collective-permute-start(f32[2,28,256]{2,1,0:T(8,128)S(1)} %pad_maximum_fusion.11), channel_id=1, source_target_pairs={{0,4},{4,0},{8,12},{12,8},{1,5},{5,1},{9,13},{13,9},{2,6},{6,2},{1... | collective-permute-start | bytes 172040 | tf_op jit(solution)/shard_map/ppermute | solution.py:348
  99.5 20.0 %collective-permute-start.24 = (bf16[4,256,128]{2,1,0:T(8,128)(2,1)}, bf16[4,256,128]{2,1,0:T(8,128)(2,1)S(1)}, u32[]{:S(2)}, u32[]{:S(2)}) collective-permute-start(bf16[4,256,128]{2,1,0:T(8,128)(2,1)} %bitcast.54), channel_id=1, source_target_pairs={{0,4},{4,0},{8,12},{12,8},{1,5},{5,1},{9,13},{13,9},{2,6},{6,2},{1... | collective-permute-start | bytes 786440 | tf_op jit(solution)/shard_map/ppermute | solution.py:348
  102.4 21.5 %collective-permute-start.25 = (bf16[4,256,128]{2,1,0:T(8,128)(2,1)}, bf16[4,256,128]{2,1,0:T(8,128)(2,1)S(1)}, u32[]{:S(2)}, u32[]{:S(2)}) collective-permute-start(bf16[4,256,128]{2,1,0:T(8,128)(2,1)} %bitcast.53), channel_id=1, source_target_pairs={{0,8},{4,12},{8,0},{12,4},{1,9},{5,13},{9,1},{13,5},{2,10},{6,14},... | collective-permute-start | bytes 786440 | tf_op jit(solution)/shard_map/ppermute | solution.py:348
  103.1 3.9 %copy-start.4 = (bf16[4,4,32,1024]{3,2,1,0:T(8,128)(2,1)}, bf16[4,4,32,1024]{3,2,1,0:T(8,128)(2,1)S(1)}, u32[]{:S(2)}) copy-start(bf16[4,4,32,1024]{3,2,1,0:T(8,128)(2,1)S(1)} %collective-permute-done.20.other.refs_2_) | copy-start | bytes 3145732
  103.1 20.8 %collective-permute-start.26 = (bf16[4,256,128]{2,1,0:T(8,128)(2,1)}, bf16[4,256,128]{2,1,0:T(8,128)(2,1)S(1)}, u32[]{:S(2)}, u32[]{:S(2)}) collective-permute-start(bf16[4,256,128]{2,1,0:T(8,128)(2,1)} %bitcast.52), channel_id=1, source_target_pairs={{0,12},{4,8},{8,4},{12,0},{1,13},{5,9},{9,5},{13,1},{2,14},{6,10},... | collective-permute-start | bytes 786440 | tf_op jit(solution)/shard_map/ppermute | solution.py:348
  107.0 0.8 copy-start.22
  119.5 4.4 %copy-start.11 = (bf16[4,256,128]{2,1,0:T(8,128)(2,1)}, bf16[4,256,128]{2,1,0:T(8,128)(2,1)S(1)}, u32[]{:S(2)}) copy-start(bf16[4,256,128]{2,1,0:T(8,128)(2,1)S(1)} %collective-permute-done.24.refs_4_.rest_1_) | copy-start | bytes 786436
  123.9 0.7 copy-start.12
  123.9 0.8 copy-start.13
  124.7 22.0 %copy-start.28 = (bf16[4,256,128]{2,1,0:T(8,128)(2,1)S(1)}, bf16[4,256,128]{2,1,0:T(8,128)(2,1)}, u32[]{:S(2)}) copy-start(bf16[4,256,128]{2,1,0:T(8,128)(2,1)} %get-tuple-element.23) | copy-start | bytes 786436
  132.4 14.5 %copy-start.25 = (bf16[4,256,128]{2,1,0:T(8,128)(2,1)S(1)}, bf16[4,256,128]{2,1,0:T(8,128)(2,1)}, u32[]{:S(2)}) copy-start(bf16[4,256,128]{2,1,0:T(8,128)(2,1)} %get-tuple-element.20) | copy-start | bytes 786436
  132.4 14.8 %collective-permute-start.27 = (bf16[4,32,1024]{2,1,0:T(8,128)(2,1)}, bf16[4,32,1024]{2,1,0:T(8,128)(2,1)S(1)}, u32[]{:S(2)}, u32[]{:S(2)}) collective-permute-start(bf16[4,32,1024]{2,1,0:T(8,128)(2,1)} %get-tuple-element.26), channel_id=1, source_target_pairs={{0,4},{4,8},{8,12},{1,5},{5,9},{9,13},{2,6},{6,10},{10,14},{3,7},{... | collective-permute-start | bytes 786440 | tf_op jit(solution)/shard_map/ppermute | solution.py:390
  140.3 12.1 %collective-permute-start.28 = (bf16[4,32,1024]{2,1,0:T(8,128)(2,1)}, bf16[4,32,1024]{2,1,0:T(8,128)(2,1)S(1)}, u32[]{:S(2)}, u32[]{:S(2)}) collective-permute-start(bf16[4,32,1024]{2,1,0:T(8,128)(2,1)} %get-tuple-element.27), channel_id=1, source_target_pairs={{4,0},{8,4},{12,8},{5,1},{9,5},{13,9},{6,2},{10,6},{14,10},{7,3},{... | collective-permute-start | bytes 786440 | tf_op jit(solution)/shard_map/ppermute | solution.py:391
  141.6 26.3 %collective-permute-start.21 = (bf16[4,256,128]{2,1,0:T(8,128)(2,1)}, bf16[4,256,128]{2,1,0:T(8,128)(2,1)S(1)}, u32[]{:S(2)}, u32[]{:S(2)}) collective-permute-start(bf16[4,256,128]{2,1,0:T(8,128)(2,1)} %get-tuple-element.21), channel_id=1, source_target_pairs={{0,8},{4,12},{8,0},{12,4},{1,9},{5,13},{9,1},{13,5},{2,10},{6,14},... | collective-permute-start | bytes 786440 | tf_op jit(solution)/shard_map/ppermute | solution.py:348
  143.7 24.5 %collective-permute-start.22 = (bf16[4,256,128]{2,1,0:T(8,128)(2,1)}, bf16[4,256,128]{2,1,0:T(8,128)(2,1)S(1)}, u32[]{:S(2)}, u32[]{:S(2)}) collective-permute-start(bf16[4,256,128]{2,1,0:T(8,128)(2,1)} %get-tuple-element.22), channel_id=1, source_target_pairs={{0,12},{4,8},{8,4},{12,0},{1,13},{5,9},{9,5},{13,1},{2,14},{6,10},... | collective-permute-start | bytes 786440 | tf_op jit(solution)/shard_map/ppermute | solution.py:348
  146.7 36.6 %collective-permute-start.23 = (bf16[4,256,128]{2,1,0:T(8,128)(2,1)S(1)}, bf16[4,256,128]{2,1,0:T(8,128)(2,1)S(1)}, u32[]{:S(2)}, u32[]{:S(2)}) collective-permute-start(bf16[4,256,128]{2,1,0:T(8,128)(2,1)S(1)} %copy-done.28), channel_id=1, source_target_pairs={{0,4},{4,0},{8,12},{12,8},{1,5},{5,1},{9,13},{13,9},{2,6},{6,2},{1... | collective-permute-start | bytes 786440 | tf_op jit(solution)/shard_map/ppermute | solution.py:348
  147.3 21.3 %copy-start.20 = (bf16[4,32,1024]{2,1,0:T(8,128)(2,1)}, bf16[4,32,1024]{2,1,0:T(8,128)(2,1)S(1)}, u32[]{:S(2)}) copy-start(bf16[4,32,1024]{2,1,0:T(8,128)(2,1)S(1)} %collective-permute-done.27.row_low) | copy-start | bytes 786436
  152.4 16.2 %copy-start.21 = (bf16[4,32,1024]{2,1,0:T(8,128)(2,1)}, bf16[4,32,1024]{2,1,0:T(8,128)(2,1)S(1)}, u32[]{:S(2)}) copy-start(bf16[4,32,1024]{2,1,0:T(8,128)(2,1)S(1)} %collective-permute-done.28.row_high) | copy-start | bytes 786436
  152.5 16.1 %collective-permute-start.30 = (bf16[6,32,1024]{2,1,0:T(8,128)(2,1)S(1)}, bf16[6,32,1024]{2,1,0:T(8,128)(2,1)S(1)}, u32[]{:S(2)}, u32[]{:S(2)}) collective-permute-start(bf16[6,32,1024]{2,1,0:T(8,128)(2,1)S(1)} %pad_maximum_fusion.5), channel_id=1, source_target_pairs={{1,0},{2,1},{3,2},{5,4},{6,5},{7,6},{9,8},{10,9},{11,10},{13,12},{... | collective-permute-start | bytes 1179656 | tf_op jit(solution)/shard_map/ppermute | solution.py:398
  153.8 14.7 %collective-permute-start.29 = (bf16[6,32,1024]{2,1,0:T(8,128)(2,1)S(1)}, bf16[6,32,1024]{2,1,0:T(8,128)(2,1)S(1)}, u32[]{:S(2)}, u32[]{:S(2)}) collective-permute-start(bf16[6,32,1024]{2,1,0:T(8,128)(2,1)S(1)} %pad_maximum_fusion.4), channel_id=1, source_target_pairs={{0,1},{1,2},{2,3},{4,5},{5,6},{6,7},{8,9},{9,10},{10,11},{12,13},{... | collective-permute-start | bytes 1179656 | tf_op jit(solution)/shard_map/ppermute | solution.py:397
  168.5 0.7 copy-start.23
  168.5 0.9 copy-start.24
  180.4 21.6 %collective-permute-start.31 = (bf16[4,256,128]{2,1,0:T(8,128)(2,1)}, bf16[4,256,128]{2,1,0:T(8,128)(2,1)S(1)}, u32[]{:S(2)}, u32[]{:S(2)}) collective-permute-start(bf16[4,256,128]{2,1,0:T(8,128)(2,1)} %get-tuple-element.29), channel_id=1, source_target_pairs={{0,8},{4,12},{8,0},{12,4},{1,9},{5,13},{9,1},{13,5},{2,10},{6,14},... | collective-permute-start | bytes 786440 | tf_op jit(solution)/shard_map/ppermute | solution.py:348
  183.5 19.5 %copy-start.7 = (bf16[256,4,512]{2,1,0:T(4,128)(2,1)}, bf16[256,4,512]{2,1,0:T(4,128)(2,1)S(1)}, u32[]{:S(2)}) copy-start(bf16[256,4,512]{2,1,0:T(4,128)(2,1)S(1)} %copy_dynamic-update-slice_fusion.4) | copy-start | bytes 3145732
  183.5 18.8 %collective-permute-start.32 = (bf16[4,256,128]{2,1,0:T(8,128)(2,1)}, bf16[4,256,128]{2,1,0:T(8,128)(2,1)S(1)}, u32[]{:S(2)}, u32[]{:S(2)}) collective-permute-start(bf16[4,256,128]{2,1,0:T(8,128)(2,1)} %get-tuple-element.30), channel_id=1, source_target_pairs={{0,12},{4,8},{8,4},{12,0},{1,13},{5,9},{9,5},{13,1},{2,14},{6,10},... | collective-permute-start | bytes 786440 | tf_op jit(solution)/shard_map/ppermute | solution.py:348
  186.9 15.8 %collective-permute-start.33 = (bf16[4,256,128]{2,1,0:T(8,128)(2,1)}, bf16[4,256,128]{2,1,0:T(8,128)(2,1)S(1)}, u32[]{:S(2)}, u32[]{:S(2)}) collective-permute-start(bf16[4,256,128]{2,1,0:T(8,128)(2,1)} %get-tuple-element.31), channel_id=1, source_target_pairs={{0,4},{4,0},{8,12},{12,8},{1,5},{5,1},{9,13},{13,9},{2,6},{6,2},{1... | collective-permute-start | bytes 786440 | tf_op jit(solution)/shard_map/ppermute | solution.py:348
  203.0 1.0 copy-start.6

commit v6 on v5

--- a/solution.py
+++ b/solution.py
@@ -209,7 +209,7 @@
             slot = jnp.where(away == distance, place, slot)
         return slot, 0, c % per_table
 
-    anywhere = pl.BlockSpec(memory_space=pl.ANY)
+    anywhere = pl.BlockSpec(memory_space=pltpu.HBM)
     in_specs = [
         block(planes, rows, extent),
         block(planes, extent),
@@ -308,7 +308,7 @@
     whole = pl.BlockSpec(
         blocks[0].shape, lambda c, here: (0, 0, 0), pipeline_mode=pl.Buffered(1)
     )
-    anywhere = pl.BlockSpec(memory_space=pl.ANY)
+    anywhere = pl.BlockSpec(memory_space=pltpu.HBM)
     kernel, extra = (hidden_kernel, []) if slope is None else (mix_kernel, [slope])
     edge_shape = jax.ShapeDtypeStruct((planes, CX, channels), dtype)
     return pl.pallas_call(
@@ -354,12 +354,12 @@
         return [got[shift] for shift in range(parts)]
 
     def cut(field):
-        def blocks(shift):
-            start = (chan ^ shift) * width
-            piece = lax.dynamic_slice_in_dim(field, start, width, axis=2)
-            return lax.optimization_barrier(piece.transpose(1, 0, 2))
-
-        return blocks
+        pieces, place = {}, chan
+        for shift in shifts + [0]:
+            start = (place ^ shift) * width
+            piece = lax.dynamic_slice_in_dim(field, start, width, axis=2).transpose(1, 0, 2)
+            pieces[shift], place = lax.optimization_barrier((piece, place))
+        return lambda shift: pieces[shift]
 
     def paste(pieces):
         field = jnp.zeros((own, planes, cells), pieces[0].dtype)
@@ -375,9 +375,7 @@
             column = jnp.concatenate([column, got])
         return column
 
-    def gather_weight(weight):
-        piece = lax.dynamic_slice_in_dim(weight, seat * share, share, axis=0)
-        column = gather_column(piece)
+    def gather_weight(column):
         over_x = swap(column, others, lambda i: i ^ 2)
         over_y = swap(column, others, lambda i: i ^ 4)
         mixed = jnp.where(seat & 1 == 0, over_y, over_x)
@@ -399,8 +397,13 @@
         return row_low, row_high, plane_low, plane_high
 
     grid = (planes, rows, CX, channels)
-    full_in = gather_weight(weight_in)
-    full_out = gather_weight(weight_out)
+    pieces = [
+        lax.dynamic_slice_in_dim(weight, seat * share, share, axis=0)
+        for weight in (weight_in, weight_out)
+    ]
+    column = gather_column(jnp.concatenate(pieces))
+    full_in = gather_weight(column[:, :share])
+    full_out = gather_weight(column[:, share:])
     table = jnp.concatenate([filter_taps, filter_bias[:, None]], axis=1).T
     taps = gather_column(table)
     vol_blocks = exchange(cut(volume))

time: 208 us -> 206 us (level)
  starting transfers between devices: 67.8 us -> 55.2 us
  waiting for transfers between devices: 73.4 us -> 84.8 us
    ppermute x26 -> x24, waiting for transfers between devices: 59.2 us -> 72.5 us  [swap(): return lax.ppermute(part, axes, [(i, partner(i)) for i in range(count)])]
    ppermute x2, starting transfers between devices: 13.8 us -> 4.19 us  [halo_of(): row_low = lax.ppermute(last, 'chan', forward)]
    ppermute x26 -> x24, starting transfers between devices: 41.7 us -> 38.7 us  [swap(): return lax.ppermute(part, axes, [(i, partner(i)) for i in range(count)])]
    ppermute x2, waiting for transfers between devices: 12.9 us -> 10.7 us  [halo_of(): row_high = lax.ppermute(first, 'chan', backward)]
    unnamed x68 -> x54, local copies, waits for them, and re-layouts: 10.1 us -> 9.53 us
  transfers between devices with their start and end apart: 34 -> 32, of which waited for: 15 -> 14; matrix products, arithmetic and copies ran while one was open for 9% -> 10% of each run, Pallas kernels for 14% -> 14%
where the time goes in v6:
time: 206 us; the launch traced here: 203 us
  waiting for transfers between devices  84.8 us (41%)
  starting transfers between devices  55.2 us (27%)
  Pallas kernels  36.7 us (18%)
  local copies, waits for them, and re-layouts  19.2 us (9%)
  other arithmetic  6.16 us (3%)
    ppermute x24, waiting for transfers between devices, swap(): return lax.ppermute(part, axes, [(i, partner(i)) for i in range(count)])  72.5 us
    ppermute x24, starting transfers between devices, swap(): return lax.ppermute(part, axes, [(i, partner(i)) for i in range(count)])  38.7 us
    pallas_call x2, Pallas kernels, stencil(): pl.pallas_call(forward_kernel if forward else backward_kernel, grid_spec=...  22.6 us
    pallas_call x2, Pallas kernels, product_call(): pl.pallas_call(lambda *refs: kernel(*refs, count=count), grid_spec=pltpu....  14.1 us
    ppermute x2, waiting for transfers between devices, halo_of(): row_high = lax.ppermute(first, 'chan', backward)  10.7 us
    unnamed x54, local copies, waits for them, and re-layouts  9.53 us
    ppermute x2, starting transfers between devices, halo_of(): plane_low = lax.ppermute(plane(-1), 'space', forward)  7.02 us
    ppermute x2, starting transfers between devices, halo_of(): row_low = lax.ppermute(last, 'chan', forward)  4.19 us
  transfers between devices with their start and end apart: 32, of which 14 were waited for; matrix products, arithmetic and copies ran while one was open for 10% of the time, Pallas kernels for 14%

profile of v6, /device:TPU:0, one launch (start us, length us, event | category | flops | bytes accessed | tf_op | source)
XLA Modules:
  0.0 203.3 jit_solution(5839488597100258818)
XLA Ops:
  0.6 0.9 constant_dynamic-slice_fusion.8
  1.5 5.1 %collective-permute-start = (bf16[1,64,1024]{2,1,0:T(8,128)(2,1)S(1)}, bf16[1,64,1024]{2,1,0:T(8,128)(2,1)S(1)}, u32[]{:S(2)}, u32[]{:S(2)}) collective-permute-start(bf16[1,64,1024]{2,1,0:T(8,128)(2,1)S(1)} %maximum_bitcast_fusion), channel_id=1, source_target_pairs={{0,12},{4,8},{8,4},{12,0},{1,13},{5,9},{9,5},{13,1},{2,14},{6,10},... | collective-permute-start | bytes 393224 | tf_op jit(solution)/shard_map/ppermute | solution.py:348
  6.7 3.6 %collective-permute-done = bf16[1,64,1024]{2,1,0:T(8,128)(2,1)S(1)} collective-permute-done((bf16[1,64,1024]{2,1,0:T(8,128)(2,1)S(1)}, bf16[1,64,1024]{2,1,0:T(8,128)(2,1)S(1)}, u32[]{:S(2)}, u32[]{:S(2)}) %collective-permute-start) | collective-permute-done | bytes 131104 | tf_op jit(solution)/shard_map/ppermute | solution.py:348
  10.3 2.5 %collective-permute-start.1 = (bf16[2,64,1024]{2,1,0:T(8,128)(2,1)S(1)}, bf16[2,64,1024]{2,1,0:T(8,128)(2,1)S(1)}, u32[]{:S(2)}, u32[]{:S(2)}) collective-permute-start(bf16[2,64,1024]{2,1,0:T(8,128)(2,1)S(1)} %pad_maximum_fusion.7), channel_id=1, source_target_pairs={{0,4},{4,0},{8,12},{12,8},{1,5},{5,1},{9,13},{13,9},{2,6},{6,2},{1... | collective-permute-start | bytes 786440 | tf_op jit(solution)/shard_map/ppermute | solution.py:348
  12.8 5.6 %collective-permute-done.1 = bf16[2,64,1024]{2,1,0:T(8,128)(2,1)S(1)} collective-permute-done((bf16[2,64,1024]{2,1,0:T(8,128)(2,1)S(1)}, bf16[2,64,1024]{2,1,0:T(8,128)(2,1)S(1)}, u32[]{:S(2)}, u32[]{:S(2)}) %collective-permute-start.1) | collective-permute-done | bytes 262176 | tf_op jit(solution)/shard_map/ppermute | solution.py:348
  18.5 0.9 slice_bitcast_fusion
  19.4 1.5 collective-permute-start.2
  20.9 1.5 collective-permute-start.3
  22.4 3.8 %collective-permute-done.2 = bf16[4,32,1024]{2,1,0:T(8,128)(2,1)S(1)} collective-permute-done((bf16[4,32,1024]{2,1,0:T(8,128)(2,1)S(1)}, bf16[4,32,1024]{2,1,0:T(8,128)(2,1)S(1)}, u32[]{:S(2)}, u32[]{:S(2)}) %collective-permute-start.2) | collective-permute-done | bytes 262176 | tf_op jit(solution)/shard_map/ppermute | solution.py:348
  26.2 1.2 collective-permute-done.3
  28.1 5.8 %collective-permute-done.4 = bf16[4,32,1024]{2,1,0:T(8,128)(2,1)S(1)} collective-permute-done((bf16[4,32,1024]{2,1,0:T(8,128)(2,1)S(1)}, bf16[4,32,1024]{2,1,0:T(8,128)(2,1)S(1)}, u32[]{:S(2)}, u32[]{:S(2)}) %collective-permute-start.4) | collective-permute-done | bytes 262176 | tf_op jit(solution)/shard_map/ppermute | solution.py:348
  34.2 1.3 constant_dynamic-slice_fusion.3
  35.5 0.8 copy.55
  36.8 1.5 collective-permute-start.16
  38.4 0.7 copy.54
  39.3 0.7 copy.53
  40.0 1.7 collective-permute-start.6
  41.7 3.0 %collective-permute-start.8 = (bf16[4,256,128]{2,1,0:T(8,128)(2,1)}, bf16[4,256,128]{2,1,0:T(8,128)(2,1)}, u32[]{:S(2)}, u32[]{:S(2)}) collective-permute-start(bf16[4,256,128]{2,1,0:T(8,128)(2,1)} %bitcast.80), channel_id=1, source_target_pairs={{0,12},{4,8},{8,4},{12,0},{1,13},{5,9},{9,5},{13,1},{2,14},{6,10},... | collective-permute-start | bytes 786440 | tf_op jit(solution)/shard_map/ppermute | solution.py:348
  44.7 0.8 copy.51
  45.4 1.0 constant_dynamic-slice_fusion.2
  46.5 1.5 collective-permute-start.7
  48.0 1.7 broadcast_select_fusion
  49.7 0.8 collective-permute-start.17
  50.6 0.7 copy.50
  51.4 0.8 copy.52
  52.7 0.9 collective-permute-start.13
  53.7 4.2 %collective-permute-done.8.refs_6_.rest_3_ = bf16[4,256,128]{2,1,0:T(8,128)(2,1)} collective-permute-done((bf16[4,256,128]{2,1,0:T(8,128)(2,1)}, bf16[4,256,128]{2,1,0:T(8,128)(2,1)}, u32[]{:S(2)}, u32[]{:S(2)}) %collective-permute-start.8) | collective-permute-done | bytes 262176 | tf_op jit(solution)/shard_map/ppermute | solution.py:348
  57.9 9.8 %collective-permute-done.7.refs_5_.rest_2_ = bf16[4,256,128]{2,1,0:T(8,128)(2,1)} collective-permute-done((bf16[4,256,128]{2,1,0:T(8,128)(2,1)}, bf16[4,256,128]{2,1,0:T(8,128)(2,1)}, u32[]{:S(2)}, u32[]{:S(2)}) %collective-permute-start.7) | collective-permute-done | bytes 262176 | tf_op jit(solution)/shard_map/ppermute | solution.py:348
  67.7 1.0 copy-done.2
  68.6 6.5 %shard_map.77 = (bf16[512,1024]{1,0:T(8,128)(2,1)}, bf16[4,32,1024]{2,1,0:T(8,128)(2,1)}, bf16[4,32,1024]{2,1,0:T(8,128)(2,1)}) custom-call(s32[2]{0:T(128)} %pad_add_fusion.refs_0_.here, bf16[4,4,32,1024]{3,2,1,0:T(8,128)(2,1)} %copy-done, bf16[4,4,32,1024]{3,2,1,0:T(8,128)(2,1)} %copy-done.2, bf16[4,256,128]{2,1,0:T(8,128)(2,1)} %bitcast.60, ...), custom_call_target="tpu_custom_call" | custom-call | tf_op jit(solution)/shard_map/pallas_call | solution.py:314
  75.2 2.2 %collective-permute-start.9 = (bf16[4,32,1024]{2,1,0:T(8,128)(2,1)}, bf16[4,32,1024]{2,1,0:T(8,128)(2,1)S(1)}, u32[]{:S(2)}, u32[]{:S(2)}) collective-permute-start(bf16[4,32,1024]{2,1,0:T(8,128)(2,1)} %get-tuple-element.39), channel_id=1, source_target_pairs={{0,4},{4,8},{8,12},{1,5},{5,9},{9,13},{2,6},{6,10},{10,14},{3,7},{... | collective-permute-start | bytes 786440 | tf_op jit(solution)/shard_map/ppermute | solution.py:388
  77.4 1.2 pad_maximum_fusion.1.mine.refs_1_
  78.8 1.4 collective-permute-start.10
  80.3 1.6 collective-permute-done.9.row_low
  81.9 7.5 %collective-permute-done.10.row_high = bf16[4,32,1024]{2,1,0:T(8,128)(2,1)S(1)} collective-permute-done((bf16[4,32,1024]{2,1,0:T(8,128)(2,1)S(1)}, bf16[4,32,1024]{2,1,0:T(8,128)(2,1)S(1)}, u32[]{:S(2)}, u32[]{:S(2)}) %collective-permute-start.10) | collective-permute-done | bytes 262176 | tf_op jit(solution)/shard_map/ppermute | solution.py:389
  89.4 0.8 pad_maximum_fusion.4
  90.2 1.3 collective-permute-start.12
  91.5 0.8 pad_maximum_fusion.3
  92.3 3.8 %collective-permute-start.11 = (bf16[6,32,1024]{2,1,0:T(8,128)(2,1)}, bf16[6,32,1024]{2,1,0:T(8,128)(2,1)}, u32[]{:S(2)}, u32[]{:S(2)}) collective-permute-start(bf16[6,32,1024]{2,1,0:T(8,128)(2,1)} %pad_maximum_fusion.3), channel_id=1, source_target_pairs={{0,1},{1,2},{2,3},{4,5},{5,6},{6,7},{8,9},{9,10},{10,11},{12,13},{... | collective-permute-start | bytes 1179656 | tf_op jit(solution)/shard_map/ppermute | solution.py:395
  96.1 2.1 %collective-permute-start.14 = (f32[2,28,256]{2,1,0:T(8,128)S(1)}, f32[2,28,256]{2,1,0:T(8,128)S(1)}, u32[]{:S(2)}, u32[]{:S(2)}) collective-permute-start(f32[2,28,256]{2,1,0:T(8,128)S(1)} %pad_maximum_fusion.9), channel_id=1, source_target_pairs={{0,4},{4,0},{8,12},{12,8},{1,5},{5,1},{9,13},{13,9},{2,6},{6,2},{1... | collective-permute-start | bytes 172040 | tf_op jit(solution)/shard_map/ppermute | solution.py:348
  98.3 0.7 copy.49
  99.1 1.7 collective-permute-done.14
  100.7 2.6 %collective-permute-start.24 = (bf16[4,256,128]{2,1,0:T(8,128)(2,1)}, bf16[4,256,128]{2,1,0:T(8,128)(2,1)S(1)}, u32[]{:S(2)}, u32[]{:S(2)}) collective-permute-start(bf16[4,256,128]{2,1,0:T(8,128)(2,1)} %bitcast.52), channel_id=1, source_target_pairs={{0,12},{4,8},{8,4},{12,0},{1,13},{5,9},{9,5},{13,1},{2,14},{6,10},... | collective-permute-start | bytes 786440 | tf_op jit(solution)/shard_map/ppermute | solution.py:348
  103.4 0.9 collective-permute-start.23
  104.3 0.7 copy.48
  105.8 11.7 %shard_map.78 = (bf16[4,256,128]{2,1,0:T(8,128)(2,1)}, bf16[4,256,128]{2,1,0:T(8,128)(2,1)}, bf16[4,256,128]{2,1,0:T(8,128)(2,1)}, bf16[4,256,128]{2,1,0:T(8,128)(2,1)}, f32[4,4,32,1024]{3,2,1,0:T(8,128)}) custom-call(s32[2]{0:T(128)} %pad_add_fusion.refs_0_.here, bf16[4,4,32,1024]{3,2,1,0:T(8,128)(2,1)} %bitcast.58, bf16[4,32,1024]{2,1,0:T(8,128)(2,1)} %copy-done.13, ...), custom_call_target="tpu_custom_call" | custom-call | tf_op jit(solution)/shard_map/pallas_call | solution.py:229
  117.5 9.1 %collective-permute-done.23.refs_5_.rest_2_ = bf16[4,256,128]{2,1,0:T(8,128)(2,1)S(1)} collective-permute-done((bf16[4,256,128]{2,1,0:T(8,128)(2,1)}, bf16[4,256,128]{2,1,0:T(8,128)(2,1)S(1)}, u32[]{:S(2)}, u32[]{:S(2)}) %collective-permute-start.23) | collective-permute-done | bytes 262176 | tf_op jit(solution)/shard_map/ppermute | solution.py:348
  126.6 0.7 copy-done.12
  127.3 7.5 %shard_map.79 = (bf16[512,1024]{1,0:T(8,128)(2,1)}, bf16[4,32,1024]{2,1,0:T(8,128)(2,1)}, bf16[4,32,1024]{2,1,0:T(8,128)(2,1)}) custom-call(s32[2]{0:T(128)} %pad_add_fusion.refs_0_.here, bf16[4,4,32,1024]{3,2,1,0:T(8,128)(2,1)} %copy-done.1, bf16[4,4,32,1024]{3,2,1,0:T(8,128)(2,1)} %copy-done.3, bf16[4,256,128]{2,1,0:T(8,128)(2,1)} %bitcast.62, ...), custom_call_target="tpu_custom_call" | custom-call | tf_op jit(solution)/shard_map/pallas_call | solution.py:314
  134.8 2.0 collective-permute-start.25
  136.8 1.1 fusion
  137.9 1.3 collective-permute-start.26
  139.2 4.0 %collective-permute-start.19 = (bf16[4,256,128]{2,1,0:T(8,128)(2,1)}, bf16[4,256,128]{2,1,0:T(8,128)(2,1)S(1)}, u32[]{:S(2)}, u32[]{:S(2)}) collective-permute-start(bf16[4,256,128]{2,1,0:T(8,128)(2,1)} %get-tuple-element.42), channel_id=1, source_target_pairs={{0,8},{4,12},{8,0},{12,4},{1,9},{5,13},{9,1},{13,5},{2,10},{6,14},... | collective-permute-start | bytes 786440 | tf_op jit(solution)/shard_map/ppermute | solution.py:348
  143.2 1.5 collective-permute-start.20
  145.8 3.2 %collective-permute-done.26.row_high = bf16[4,32,1024]{2,1,0:T(8,128)(2,1)S(1)} collective-permute-done((bf16[4,32,1024]{2,1,0:T(8,128)(2,1)}, bf16[4,32,1024]{2,1,0:T(8,128)(2,1)S(1)}, u32[]{:S(2)}, u32[]{:S(2)}) %collective-permute-start.26) | collective-permute-done | bytes 262176 | tf_op jit(solution)/shard_map/ppermute | solution.py:389
  149.1 1.3 collective-permute-start.28
  150.5 3.2 %collective-permute-start.27 = (bf16[6,32,1024]{2,1,0:T(8,128)(2,1)S(1)}, bf16[6,32,1024]{2,1,0:T(8,128)(2,1)S(1)}, u32[]{:S(2)}, u32[]{:S(2)}) collective-permute-start(bf16[6,32,1024]{2,1,0:T(8,128)(2,1)S(1)} %pad_maximum_fusion.5), channel_id=1, source_target_pairs={{0,1},{1,2},{2,3},{4,5},{5,6},{6,7},{8,9},{9,10},{10,11},{12,13},{... | collective-permute-start | bytes 1179656 | tf_op jit(solution)/shard_map/ppermute | solution.py:395
  153.7 13.5 %collective-permute-done.19 = bf16[4,256,128]{2,1,0:T(8,128)(2,1)S(1)} collective-permute-done((bf16[4,256,128]{2,1,0:T(8,128)(2,1)}, bf16[4,256,128]{2,1,0:T(8,128)(2,1)S(1)}, u32[]{:S(2)}, u32[]{:S(2)}) %collective-permute-start.19) | collective-permute-done | bytes 262176 | tf_op jit(solution)/shard_map/ppermute | solution.py:348
  168.8 11.0 %shard_map.80 = (bf16[4,256,128]{2,1,0:T(8,128)(2,1)}, bf16[4,256,128]{2,1,0:T(8,128)(2,1)}, bf16[4,256,128]{2,1,0:T(8,128)(2,1)}, bf16[4,256,128]{2,1,0:T(8,128)(2,1)}) custom-call(s32[2]{0:T(128)} %pad_add_fusion.refs_0_.here, bf16[4,4,32,1024]{3,2,1,0:T(8,128)(2,1)} %bitcast.59, bf16[4,32,1024]{2,1,0:T(8,128)(2,1)} %copy-done.15, ...), custom_call_target="tpu_custom_call" | custom-call | tf_op jit(solution)/shard_map/pallas_call | solution.py:229
  179.8 2.3 %collective-permute-start.29 = (bf16[4,256,128]{2,1,0:T(8,128)(2,1)}, bf16[4,256,128]{2,1,0:T(8,128)(2,1)S(1)}, u32[]{:S(2)}, u32[]{:S(2)}) collective-permute-start(bf16[4,256,128]{2,1,0:T(8,128)(2,1)} %get-tuple-element.57), channel_id=1, source_target_pairs={{0,8},{4,12},{8,0},{12,4},{1,9},{5,13},{9,1},{13,5},{2,10},{6,14},... | collective-permute-start | bytes 786440 | tf_op jit(solution)/shard_map/ppermute | solution.py:348
  182.4 3.3 %collective-permute-start.30 = (bf16[4,256,128]{2,1,0:T(8,128)(2,1)}, bf16[4,256,128]{2,1,0:T(8,128)(2,1)S(1)}, u32[]{:S(2)}, u32[]{:S(2)}) collective-permute-start(bf16[4,256,128]{2,1,0:T(8,128)(2,1)} %get-tuple-element.58), channel_id=1, source_target_pairs={{0,12},{4,8},{8,4},{12,0},{1,13},{5,9},{9,5},{13,1},{2,14},{6,10},... | collective-permute-start | bytes 786440 | tf_op jit(solution)/shard_map/ppermute | solution.py:348
  186.0 1.2 copy_dynamic-update-slice_fusion.3
  187.3 14.1 %collective-permute-done.29 = bf16[4,256,128]{2,1,0:T(8,128)(2,1)S(1)} collective-permute-done((bf16[4,256,128]{2,1,0:T(8,128)(2,1)}, bf16[4,256,128]{2,1,0:T(8,128)(2,1)S(1)}, u32[]{:S(2)}, u32[]{:S(2)}) %collective-permute-start.29) | collective-permute-done | bytes 262176 | tf_op jit(solution)/shard_map/ppermute | solution.py:348
  202.3 1.0 copy-done.7
  (98 shorter events, 7.6 us)
Async XLA Ops:
  1.5 8.7 %collective-permute-start = (bf16[1,64,1024]{2,1,0:T(8,128)(2,1)S(1)}, bf16[1,64,1024]{2,1,0:T(8,128)(2,1)S(1)}, u32[]{:S(2)}, u32[]{:S(2)}) collective-permute-start(bf16[1,64,1024]{2,1,0:T(8,128)(2,1)S(1)} %maximum_bitcast_fusion), channel_id=1, source_target_pairs={{0,12},{4,8},{8,4},{12,0},{1,13},{5,9},{9,5},{13,1},{2,14},{6,10},... | collective-permute-start | bytes 393224 | tf_op jit(solution)/shard_map/ppermute | solution.py:348
  10.3 8.1 %collective-permute-start.1 = (bf16[2,64,1024]{2,1,0:T(8,128)(2,1)S(1)}, bf16[2,64,1024]{2,1,0:T(8,128)(2,1)S(1)}, u32[]{:S(2)}, u32[]{:S(2)}) collective-permute-start(bf16[2,64,1024]{2,1,0:T(8,128)(2,1)S(1)} %pad_maximum_fusion.7), channel_id=1, source_target_pairs={{0,4},{4,0},{8,12},{12,8},{1,5},{5,1},{9,13},{13,9},{2,6},{6,2},{1... | collective-permute-start | bytes 786440 | tf_op jit(solution)/shard_map/ppermute | solution.py:348
  18.5 15.6 %copy-start.5 = (bf16[256,4,512]{2,1,0:T(4,128)(2,1)S(1)}, bf16[256,4,512]{2,1,0:T(4,128)(2,1)}, u32[]{:S(2)}) copy-start(bf16[256,4,512]{2,1,0:T(4,128)(2,1)} %param.6) | copy-start | bytes 3145732
  19.4 6.8 %collective-permute-start.2 = (bf16[4,32,1024]{2,1,0:T(8,128)(2,1)S(1)}, bf16[4,32,1024]{2,1,0:T(8,128)(2,1)S(1)}, u32[]{:S(2)}, u32[]{:S(2)}) collective-permute-start(bf16[4,32,1024]{2,1,0:T(8,128)(2,1)S(1)} %get-tuple-element.67), channel_id=1, source_target_pairs={{0,2},{1,3},{2,0},{3,1},{16,18},{17,19},{18,16},{19,17},{4,6},{5,7... | collective-permute-start | bytes 786440 | tf_op jit(solution)/shard_map/ppermute | solution.py:348
  20.9 6.5 %collective-permute-start.3 = (bf16[4,32,1024]{2,1,0:T(8,128)(2,1)S(1)}, bf16[4,32,1024]{2,1,0:T(8,128)(2,1)S(1)}, u32[]{:S(2)}, u32[]{:S(2)}) collective-permute-start(bf16[4,32,1024]{2,1,0:T(8,128)(2,1)S(1)} %get-tuple-element.67), channel_id=1, source_target_pairs={{0,16},{1,17},{2,18},{3,19},{16,0},{17,1},{18,2},{19,3},{4,20},{5,... | collective-permute-start | bytes 786440 | tf_op jit(solution)/shard_map/ppermute | solution.py:348
  27.5 6.4 %collective-permute-start.4 = (bf16[4,32,1024]{2,1,0:T(8,128)(2,1)S(1)}, bf16[4,32,1024]{2,1,0:T(8,128)(2,1)S(1)}, u32[]{:S(2)}, u32[]{:S(2)}) collective-permute-start(bf16[4,32,1024]{2,1,0:T(8,128)(2,1)S(1)} %broadcast_select_fusion.1), channel_id=1, source_target_pairs={{0,2},{1,17},{2,0},{3,19},{16,18},{17,1},{18,16},{19,3},{4,6},{5,2... | collective-permute-start | bytes 786440 | tf_op jit(solution)/shard_map/ppermute | solution.py:348
  34.1 11.4 %copy-start = (bf16[4,4,32,1024]{3,2,1,0:T(8,128)(2,1)}, bf16[4,4,32,1024]{3,2,1,0:T(8,128)(2,1)S(1)}, u32[]{:S(2)}) copy-start(bf16[4,4,32,1024]{3,2,1,0:T(8,128)(2,1)S(1)} %pad_maximum_fusion.refs_1_.mine) | copy-start | bytes 3145732
  34.1 33.6 %collective-permute-start.5 = (bf16[4,4,32,1024]{3,2,1,0:T(8,128)(2,1)S(1)}, bf16[4,4,32,1024]{3,2,1,0:T(8,128)(2,1)S(1)}, u32[]{:S(2)}, u32[]{:S(2)}) collective-permute-start(bf16[4,4,32,1024]{3,2,1,0:T(8,128)(2,1)S(1)} %pad_maximum_fusion.refs_1_.mine), channel_id=1, source_target_pairs={{0,1},{1,0},{2,3},{3,2},{16,17},{17,16},{18,19},{19,18},{4,5},{5,4... | collective-permute-start | bytes 3145736 | tf_op jit(solution)/shard_map/ppermute | solution.py:348
  36.3 10.2 %collective-permute-start.15 = (bf16[4,32,1024]{2,1,0:T(8,128)(2,1)}, bf16[4,32,1024]{2,1,0:T(8,128)(2,1)}, u32[]{:S(2)}, u32[]{:S(2)}) collective-permute-start(bf16[4,32,1024]{2,1,0:T(8,128)(2,1)} %get-tuple-element.66), channel_id=1, source_target_pairs={{0,2},{1,3},{2,0},{3,1},{16,18},{17,19},{18,16},{19,17},{4,6},{5,7... | collective-permute-start | bytes 786440 | tf_op jit(solution)/shard_map/ppermute | solution.py:348
  36.8 11.2 %collective-permute-start.16 = (bf16[4,32,1024]{2,1,0:T(8,128)(2,1)}, bf16[4,32,1024]{2,1,0:T(8,128)(2,1)}, u32[]{:S(2)}, u32[]{:S(2)}) collective-permute-start(bf16[4,32,1024]{2,1,0:T(8,128)(2,1)} %get-tuple-element.66), channel_id=1, source_target_pairs={{0,16},{1,17},{2,18},{3,19},{16,0},{17,1},{18,2},{19,3},{4,20},{5,... | collective-permute-start | bytes 786440 | tf_op jit(solution)/shard_map/ppermute | solution.py:348
  39.2 13.5 %copy-start.20 = (f32[256,27]{0,1:T(8,128)S(1)}, f32[256,27]{0,1:T(8,128)}, u32[]{:S(2)}) copy-start(f32[256,27]{0,1:T(8,128)} %param.10) | copy-start | bytes 82948
  39.3 13.5 %copy-start.21 = (f32[256]{0:T(256)S(1)}, f32[256]{0:T(256)}, u32[]{:S(2)}) copy-start(f32[256]{0:T(256)} %param.11) | copy-start | bytes 3076
  40.0 12.7 %collective-permute-start.6 = (bf16[4,256,128]{2,1,0:T(8,128)(2,1)}, bf16[4,256,128]{2,1,0:T(8,128)(2,1)}, u32[]{:S(2)}, u32[]{:S(2)}) collective-permute-start(bf16[4,256,128]{2,1,0:T(8,128)(2,1)} %bitcast.55), channel_id=1, source_target_pairs={{0,4},{4,0},{8,12},{12,8},{1,5},{5,1},{9,13},{13,9},{2,6},{6,2},{1... | collective-permute-start | bytes 786440 | tf_op jit(solution)/shard_map/ppermute | solution.py:348
  41.7 16.2 %collective-permute-start.8 = (bf16[4,256,128]{2,1,0:T(8,128)(2,1)}, bf16[4,256,128]{2,1,0:T(8,128)(2,1)}, u32[]{:S(2)}, u32[]{:S(2)}) collective-permute-start(bf16[4,256,128]{2,1,0:T(8,128)(2,1)} %bitcast.80), channel_id=1, source_target_pairs={{0,12},{4,8},{8,4},{12,0},{1,13},{5,9},{9,5},{13,1},{2,14},{6,10},... | collective-permute-start | bytes 786440 | tf_op jit(solution)/shard_map/ppermute | solution.py:348
  46.5 21.1 %collective-permute-start.7 = (bf16[4,256,128]{2,1,0:T(8,128)(2,1)}, bf16[4,256,128]{2,1,0:T(8,128)(2,1)}, u32[]{:S(2)}, u32[]{:S(2)}) collective-permute-start(bf16[4,256,128]{2,1,0:T(8,128)(2,1)} %bitcast.79), channel_id=1, source_target_pairs={{0,8},{4,12},{8,0},{12,4},{1,9},{5,13},{9,1},{13,5},{2,10},{6,14},... | collective-permute-start | bytes 786440 | tf_op jit(solution)/shard_map/ppermute | solution.py:348
  49.7 27.7 %collective-permute-start.17 = (bf16[4,32,1024]{2,1,0:T(8,128)(2,1)}, bf16[4,32,1024]{2,1,0:T(8,128)(2,1)}, u32[]{:S(2)}, u32[]{:S(2)}) collective-permute-start(bf16[4,32,1024]{2,1,0:T(8,128)(2,1)} %broadcast_select_fusion), channel_id=1, source_target_pairs={{0,2},{1,17},{2,0},{3,19},{16,18},{17,1},{18,16},{19,3},{4,6},{5,2... | collective-permute-start | bytes 786440 | tf_op jit(solution)/shard_map/ppermute | solution.py:348
  50.6 26.8 %copy-start.9 = (bf16[1,4,32,1024]{3,2,1,0:T(8,128)(2,1)S(1)}, bf16[1,4,32,1024]{3,2,1,0:T(8,128)(2,1)}, u32[]{:S(2)}) copy-start(bf16[1,4,32,1024]{3,2,1,0:T(8,128)(2,1)} %get-tuple-element.64) | copy-start | bytes 786436
  52.7 43.3 %collective-permute-start.13 = (f32[1,28,256]{2,1,0:T(8,128)S(1)}, f32[1,28,256]{2,1,0:T(8,128)S(1)}, u32[]{:S(2)}, u32[]{:S(2)}) collective-permute-start(f32[1,28,256]{2,1,0:T(8,128)S(1)} %maximum_bitcast_fusion.1), channel_id=1, source_target_pairs={{0,12},{4,8},{8,4},{12,0},{1,13},{5,9},{9,5},{13,1},{2,14},{6,10},... | collective-permute-start | bytes 86024 | tf_op jit(solution)/shard_map/ppermute | solution.py:348
  67.7 1.0 copy-start.2
  75.2 3.6 %copy-start.22 = (bf16[4,32,1024]{2,1,0:T(8,128)(2,1)S(1)}, bf16[4,32,1024]{2,1,0:T(8,128)(2,1)}, u32[]{:S(2)}) copy-start(bf16[4,32,1024]{2,1,0:T(8,128)(2,1)} %get-tuple-element.40) | copy-start | bytes 786436
  75.2 5.0 %copy-start.4 = (bf16[512,1024]{1,0:T(8,128)(2,1)S(1)}, bf16[512,1024]{1,0:T(8,128)(2,1)}, u32[]{:S(2)}) copy-start(bf16[512,1024]{1,0:T(8,128)(2,1)} %get-tuple-element.38) | copy-start | bytes 3145732
  75.2 6.7 %collective-permute-start.9 = (bf16[4,32,1024]{2,1,0:T(8,128)(2,1)}, bf16[4,32,1024]{2,1,0:T(8,128)(2,1)S(1)}, u32[]{:S(2)}, u32[]{:S(2)}) collective-permute-start(bf16[4,32,1024]{2,1,0:T(8,128)(2,1)} %get-tuple-element.39), channel_id=1, source_target_pairs={{0,4},{4,8},{8,12},{1,5},{5,9},{9,13},{2,6},{6,10},{10,14},{3,7},{... | collective-permute-start | bytes 786440 | tf_op jit(solution)/shard_map/ppermute | solution.py:388
  78.7 20.4 %copy-start.1 = (bf16[4,4,32,1024]{3,2,1,0:T(8,128)(2,1)}, bf16[4,4,32,1024]{3,2,1,0:T(8,128)(2,1)S(1)}, u32[]{:S(2)}) copy-start(bf16[4,4,32,1024]{3,2,1,0:T(8,128)(2,1)S(1)} %pad_maximum_fusion.1.mine.refs_1_) | copy-start | bytes 3145732
  78.7 19.5 %copy-start.6 = (bf16[256,4,512]{2,1,0:T(4,128)(2,1)S(1)}, bf16[256,4,512]{2,1,0:T(4,128)(2,1)}, u32[]{:S(2)}) copy-start(bf16[256,4,512]{2,1,0:T(4,128)(2,1)} %param.7) | copy-start | bytes 3145732
  78.7 24.7 %collective-permute-start.18 = (bf16[4,4,32,1024]{3,2,1,0:T(8,128)(2,1)S(1)}, bf16[4,4,32,1024]{3,2,1,0:T(8,128)(2,1)S(1)}, u32[]{:S(2)}, u32[]{:S(2)}) collective-permute-start(bf16[4,4,32,1024]{3,2,1,0:T(8,128)(2,1)S(1)} %pad_maximum_fusion.1.mine.refs_1_), channel_id=1, source_target_pairs={{0,1},{1,0},{2,3},{3,2},{16,17},{17,16},{18,19},{19,18},{4,5},{5,4... | collective-permute-start | bytes 3145736 | tf_op jit(solution)/shard_map/ppermute | solution.py:348
  78.8 10.6 %collective-permute-start.10 = (bf16[4,32,1024]{2,1,0:T(8,128)(2,1)S(1)}, bf16[4,32,1024]{2,1,0:T(8,128)(2,1)S(1)}, u32[]{:S(2)}, u32[]{:S(2)}) collective-permute-start(bf16[4,32,1024]{2,1,0:T(8,128)(2,1)S(1)} %copy-done.22), channel_id=1, source_target_pairs={{4,0},{8,4},{12,8},{5,1},{9,5},{13,9},{6,2},{10,6},{14,10},{7,3},{... | collective-permute-start | bytes 786440 | tf_op jit(solution)/shard_map/ppermute | solution.py:389
  81.9 23.2 %copy-start.13 = (bf16[4,32,1024]{2,1,0:T(8,128)(2,1)}, bf16[4,32,1024]{2,1,0:T(8,128)(2,1)S(1)}, u32[]{:S(2)}) copy-start(bf16[4,32,1024]{2,1,0:T(8,128)(2,1)S(1)} %collective-permute-done.9.row_low) | copy-start | bytes 786436
  89.4 16.4 %copy-start.14 = (bf16[4,32,1024]{2,1,0:T(8,128)(2,1)}, bf16[4,32,1024]{2,1,0:T(8,128)(2,1)S(1)}, u32[]{:S(2)}) copy-start(bf16[4,32,1024]{2,1,0:T(8,128)(2,1)S(1)} %collective-permute-done.10.row_high) | copy-start | bytes 786436
  90.2 15.5 %collective-permute-start.12 = (bf16[6,32,1024]{2,1,0:T(8,128)(2,1)}, bf16[6,32,1024]{2,1,0:T(8,128)(2,1)}, u32[]{:S(2)}, u32[]{:S(2)}) collective-permute-start(bf16[6,32,1024]{2,1,0:T(8,128)(2,1)} %pad_maximum_fusion.4), channel_id=1, source_target_pairs={{1,0},{2,1},{3,2},{5,4},{6,5},{7,6},{9,8},{10,9},{11,10},{13,12},{... | collective-permute-start | bytes 1179656 | tf_op jit(solution)/shard_map/ppermute | solution.py:396
  92.3 13.5 %collective-permute-start.11 = (bf16[6,32,1024]{2,1,0:T(8,128)(2,1)}, bf16[6,32,1024]{2,1,0:T(8,128)(2,1)}, u32[]{:S(2)}, u32[]{:S(2)}) collective-permute-start(bf16[6,32,1024]{2,1,0:T(8,128)(2,1)} %pad_maximum_fusion.3), channel_id=1, source_target_pairs={{0,1},{1,2},{2,3},{4,5},{5,6},{6,7},{8,9},{9,10},{10,11},{12,13},{... | collective-permute-start | bytes 1179656 | tf_op jit(solution)/shard_map/ppermute | solution.py:395
  96.1 4.6 %collective-permute-start.14 = (f32[2,28,256]{2,1,0:T(8,128)S(1)}, f32[2,28,256]{2,1,0:T(8,128)S(1)}, u32[]{:S(2)}, u32[]{:S(2)}) collective-permute-start(f32[2,28,256]{2,1,0:T(8,128)S(1)} %pad_maximum_fusion.9), channel_id=1, source_target_pairs={{0,4},{4,0},{8,12},{12,8},{1,5},{5,1},{9,13},{13,9},{2,6},{6,2},{1... | collective-permute-start | bytes 172040 | tf_op jit(solution)/shard_map/ppermute | solution.py:348
  99.0 18.4 %collective-permute-start.22 = (bf16[4,256,128]{2,1,0:T(8,128)(2,1)}, bf16[4,256,128]{2,1,0:T(8,128)(2,1)S(1)}, u32[]{:S(2)}, u32[]{:S(2)}) collective-permute-start(bf16[4,256,128]{2,1,0:T(8,128)(2,1)} %bitcast.51), channel_id=1, source_target_pairs={{0,4},{4,0},{8,12},{12,8},{1,5},{5,1},{9,13},{13,9},{2,6},{6,2},{1... | collective-permute-start | bytes 786440 | tf_op jit(solution)/shard_map/ppermute | solution.py:348
  100.7 16.7 %collective-permute-start.24 = (bf16[4,256,128]{2,1,0:T(8,128)(2,1)}, bf16[4,256,128]{2,1,0:T(8,128)(2,1)S(1)}, u32[]{:S(2)}, u32[]{:S(2)}) collective-permute-start(bf16[4,256,128]{2,1,0:T(8,128)(2,1)} %bitcast.52), channel_id=1, source_target_pairs={{0,12},{4,8},{8,4},{12,0},{1,13},{5,9},{9,5},{13,1},{2,14},{6,10},... | collective-permute-start | bytes 786440 | tf_op jit(solution)/shard_map/ppermute | solution.py:348
  103.3 2.4 %copy-start.3 = (bf16[4,4,32,1024]{3,2,1,0:T(8,128)(2,1)}, bf16[4,4,32,1024]{3,2,1,0:T(8,128)(2,1)S(1)}, u32[]{:S(2)}) copy-start(bf16[4,4,32,1024]{3,2,1,0:T(8,128)(2,1)S(1)} %collective-permute-done.18.other.refs_2_) | copy-start | bytes 3145732
  103.4 23.2 %collective-permute-start.23 = (bf16[4,256,128]{2,1,0:T(8,128)(2,1)}, bf16[4,256,128]{2,1,0:T(8,128)(2,1)S(1)}, u32[]{:S(2)}, u32[]{:S(2)}) collective-permute-start(bf16[4,256,128]{2,1,0:T(8,128)(2,1)} %bitcast.53), channel_id=1, source_target_pairs={{0,8},{4,12},{8,0},{12,4},{1,9},{5,13},{9,1},{13,5},{2,10},{6,14},... | collective-permute-start | bytes 786440 | tf_op jit(solution)/shard_map/ppermute | solution.py:348
  117.4 9.1 %copy-start.10 = (bf16[4,256,128]{2,1,0:T(8,128)(2,1)}, bf16[4,256,128]{2,1,0:T(8,128)(2,1)S(1)}, u32[]{:S(2)}) copy-start(bf16[4,256,128]{2,1,0:T(8,128)(2,1)S(1)} %collective-permute-done.22.refs_4_.rest_1_) | copy-start | bytes 786436
  117.5 9.1 %copy-start.11 = (bf16[4,256,128]{2,1,0:T(8,128)(2,1)}, bf16[4,256,128]{2,1,0:T(8,128)(2,1)S(1)}, u32[]{:S(2)}) copy-start(bf16[4,256,128]{2,1,0:T(8,128)(2,1)S(1)} %collective-permute-done.24.refs_6_.rest_3_) | copy-start | bytes 786436
  126.6 0.7 copy-start.12
  134.8 10.6 %copy-start.19 = (bf16[4,256,128]{2,1,0:T(8,128)(2,1)S(1)}, bf16[4,256,128]{2,1,0:T(8,128)(2,1)}, u32[]{:S(2)}) copy-start(bf16[4,256,128]{2,1,0:T(8,128)(2,1)} %get-tuple-element.41) | copy-start | bytes 786436
  134.8 10.9 %collective-permute-start.25 = (bf16[4,32,1024]{2,1,0:T(8,128)(2,1)}, bf16[4,32,1024]{2,1,0:T(8,128)(2,1)S(1)}, u32[]{:S(2)}, u32[]{:S(2)}) collective-permute-start(bf16[4,32,1024]{2,1,0:T(8,128)(2,1)} %get-tuple-element.54), channel_id=1, source_target_pairs={{0,4},{4,8},{8,12},{1,5},{5,9},{9,13},{2,6},{6,10},{10,14},{3,7},{... | collective-permute-start | bytes 786440 | tf_op jit(solution)/shard_map/ppermute | solution.py:388
  137.9 11.2 %collective-permute-start.26 = (bf16[4,32,1024]{2,1,0:T(8,128)(2,1)}, bf16[4,32,1024]{2,1,0:T(8,128)(2,1)S(1)}, u32[]{:S(2)}, u32[]{:S(2)}) collective-permute-start(bf16[4,32,1024]{2,1,0:T(8,128)(2,1)} %get-tuple-element.55), channel_id=1, source_target_pairs={{4,0},{8,4},{12,8},{5,1},{9,5},{13,9},{6,2},{10,6},{14,10},{7,3},{... | collective-permute-start | bytes 786440 | tf_op jit(solution)/shard_map/ppermute | solution.py:389
  139.2 28.1 %collective-permute-start.19 = (bf16[4,256,128]{2,1,0:T(8,128)(2,1)}, bf16[4,256,128]{2,1,0:T(8,128)(2,1)S(1)}, u32[]{:S(2)}, u32[]{:S(2)}) collective-permute-start(bf16[4,256,128]{2,1,0:T(8,128)(2,1)} %get-tuple-element.42), channel_id=1, source_target_pairs={{0,8},{4,12},{8,0},{12,4},{1,9},{5,13},{9,1},{13,5},{2,10},{6,14},... | collective-permute-start | bytes 786440 | tf_op jit(solution)/shard_map/ppermute | solution.py:348
  143.2 24.4 %collective-permute-start.20 = (bf16[4,256,128]{2,1,0:T(8,128)(2,1)}, bf16[4,256,128]{2,1,0:T(8,128)(2,1)S(1)}, u32[]{:S(2)}, u32[]{:S(2)}) collective-permute-start(bf16[4,256,128]{2,1,0:T(8,128)(2,1)} %get-tuple-element.43), channel_id=1, source_target_pairs={{0,12},{4,8},{8,4},{12,0},{1,13},{5,9},{9,5},{13,1},{2,14},{6,10},... | collective-permute-start | bytes 786440 | tf_op jit(solution)/shard_map/ppermute | solution.py:348
  144.7 37.4 %collective-permute-start.21 = (bf16[4,256,128]{2,1,0:T(8,128)(2,1)}, bf16[4,256,128]{2,1,0:T(8,128)(2,1)S(1)}, u32[]{:S(2)}, u32[]{:S(2)}) collective-permute-start(bf16[4,256,128]{2,1,0:T(8,128)(2,1)} %get-tuple-element.44), channel_id=1, source_target_pairs={{0,4},{4,0},{8,12},{12,8},{1,5},{5,1},{9,13},{13,9},{2,6},{6,2},{1... | collective-permute-start | bytes 786440 | tf_op jit(solution)/shard_map/ppermute | solution.py:348
  145.8 22.2 %copy-start.15 = (bf16[4,32,1024]{2,1,0:T(8,128)(2,1)}, bf16[4,32,1024]{2,1,0:T(8,128)(2,1)S(1)}, u32[]{:S(2)}) copy-start(bf16[4,32,1024]{2,1,0:T(8,128)(2,1)S(1)} %collective-permute-done.25.row_low) | copy-start | bytes 786436
  149.1 18.9 %copy-start.16 = (bf16[4,32,1024]{2,1,0:T(8,128)(2,1)}, bf16[4,32,1024]{2,1,0:T(8,128)(2,1)S(1)}, u32[]{:S(2)}) copy-start(bf16[4,32,1024]{2,1,0:T(8,128)(2,1)S(1)} %collective-permute-done.26.row_high) | copy-start | bytes 786436
  149.1 18.8 %collective-permute-start.28 = (bf16[6,32,1024]{2,1,0:T(8,128)(2,1)S(1)}, bf16[6,32,1024]{2,1,0:T(8,128)(2,1)S(1)}, u32[]{:S(2)}, u32[]{:S(2)}) collective-permute-start(bf16[6,32,1024]{2,1,0:T(8,128)(2,1)S(1)} %pad_maximum_fusion.6), channel_id=1, source_target_pairs={{1,0},{2,1},{3,2},{5,4},{6,5},{7,6},{9,8},{10,9},{11,10},{13,12},{... | collective-permute-start | bytes 1179656 | tf_op jit(solution)/shard_map/ppermute | solution.py:396
  150.5 17.4 %collective-permute-start.27 = (bf16[6,32,1024]{2,1,0:T(8,128)(2,1)S(1)}, bf16[6,32,1024]{2,1,0:T(8,128)(2,1)S(1)}, u32[]{:S(2)}, u32[]{:S(2)}) collective-permute-start(bf16[6,32,1024]{2,1,0:T(8,128)(2,1)S(1)} %pad_maximum_fusion.5), channel_id=1, source_target_pairs={{0,1},{1,2},{2,3},{4,5},{5,6},{6,7},{8,9},{9,10},{10,11},{12,13},{... | collective-permute-start | bytes 1179656 | tf_op jit(solution)/shard_map/ppermute | solution.py:395
  167.9 0.7 copy-start.17
  167.9 0.9 copy-start.18
  179.8 21.6 %collective-permute-start.29 = (bf16[4,256,128]{2,1,0:T(8,128)(2,1)}, bf16[4,256,128]{2,1,0:T(8,128)(2,1)S(1)}, u32[]{:S(2)}, u32[]{:S(2)}) collective-permute-start(bf16[4,256,128]{2,1,0:T(8,128)(2,1)} %get-tuple-element.57), channel_id=1, source_target_pairs={{0,8},{4,12},{8,0},{12,4},{1,9},{5,13},{9,1},{13,5},{2,10},{6,14},... | collective-permute-start | bytes 786440 | tf_op jit(solution)/shard_map/ppermute | solution.py:348
  182.4 19.9 %copy-start.8 = (bf16[256,4,512]{2,1,0:T(4,128)(2,1)}, bf16[256,4,512]{2,1,0:T(4,128)(2,1)S(1)}, u32[]{:S(2)}) copy-start(bf16[256,4,512]{2,1,0:T(4,128)(2,1)S(1)} %copy_dynamic-update-slice_fusion.4) | copy-start | bytes 3145732
  182.4 19.3 %collective-permute-start.30 = (bf16[4,256,128]{2,1,0:T(8,128)(2,1)}, bf16[4,256,128]{2,1,0:T(8,128)(2,1)S(1)}, u32[]{:S(2)}, u32[]{:S(2)}) collective-permute-start(bf16[4,256,128]{2,1,0:T(8,128)(2,1)} %get-tuple-element.58), channel_id=1, source_target_pairs={{0,12},{4,8},{8,4},{12,0},{1,13},{5,9},{9,5},{13,1},{2,14},{6,10},... | collective-permute-start | bytes 786440 | tf_op jit(solution)/shard_map/ppermute | solution.py:348
  185.7 16.2 %collective-permute-start.31 = (bf16[4,256,128]{2,1,0:T(8,128)(2,1)}, bf16[4,256,128]{2,1,0:T(8,128)(2,1)S(1)}, u32[]{:S(2)}, u32[]{:S(2)}) collective-permute-start(bf16[4,256,128]{2,1,0:T(8,128)(2,1)} %get-tuple-element.59), channel_id=1, source_target_pairs={{0,4},{4,0},{8,12},{12,8},{1,5},{5,1},{9,13},{13,9},{2,6},{6,2},{1... | collective-permute-start | bytes 786440 | tf_op jit(solution)/shard_map/ppermute | solution.py:348
  202.3 1.0 copy-start.7

commit v7 on v6

--- a/solution.py
+++ b/solution.py
@@ -251,17 +251,24 @@
             turned[z * width : (z + 1) * width, pl.ds(start, own)] = block[z].T
 
 
-def put_with_rows(value, out, first, last):
+def put_with_edges(value, out, first, last, fore, back):
     out[...] = value
-    planes, extent = first.shape[:2]
+    planes, extent, width = first.shape
     plane = value.shape[0] // planes
+    rows = plane // extent
     for z in range(planes):
         first[z] = value[z * plane : z * plane + extent]
         last[z] = value[(z + 1) * plane - extent : (z + 1) * plane]
+    for edge, z in ((back, 0), (fore, planes - 1)):
+        edge[0] = jnp.zeros((extent, width), edge.dtype)
+        edge[rows + 1] = jnp.zeros((extent, width), edge.dtype)
+        for y in range(rows):
+            at = z * plane + y * extent
+            edge[y + 1] = value[at : at + extent]
 
 
 def hidden_kernel(here, mine, other, *rest, count):
-    inputs, (out, first, last, turned, weight, sems) = rest[:count], rest[count:]
+    inputs, (*outputs, turned, weight, sems) = rest[:count], rest[count:]
 
     @pl.when(pl.program_id(0) == 0)
     def _():
@@ -276,11 +283,11 @@
         (((1,), (1,)), ((), ())),
         preferred_element_type=jnp.float32,
     )
-    put_with_rows(value.astype(out.dtype), out, first, last)
+    put_with_edges(value.astype(turned.dtype), *outputs)
 
 
 def mix_kernel(here, mine, other, *rest, count):
-    inputs, (slope, out, first, last, turned, weight, sems) = rest[:count], rest[count:]
+    inputs, (slope, *outputs, turned, weight, sems) = rest[:count], rest[count:]
 
     @pl.when(pl.program_id(0) == 0)
     def _():
@@ -289,12 +296,12 @@
         turn_blocks(here, inputs, turned)
         wait_all(copies)
 
-    channels, width = turned.shape[1], out.shape[1]
+    channels, width = turned.shape[1], slope.shape[1]
     start = pl.multiple_of(pl.program_id(0) * width, width)
     columns = weight[:, :, :, pl.ds(start, width)].reshape(channels, width)
     grad = jnp.dot(turned[...], columns, preferred_element_type=jnp.float32)
-    grad = grad.astype(out.dtype).astype(jnp.float32)
-    put_with_rows((grad * slope[...]).astype(out.dtype), out, first, last)
+    grad = grad.astype(turned.dtype).astype(jnp.float32)
+    put_with_edges((grad * slope[...]).astype(turned.dtype), *outputs)
 
 
 def product_call(here, blocks, weight, slope=None):
@@ -304,23 +311,32 @@
     channels = own * count
     dtype = blocks[0].dtype
     columns = pl.BlockSpec((cells, own), lambda c, here: (0, c))
-    edge = pl.BlockSpec((planes, CX, own), lambda c, here: (0, 0, c))
+    room = width // CX + 2
+    row = pl.BlockSpec((planes, CX, own), lambda c, here: (0, 0, c))
+    plane = pl.BlockSpec((room, CX, own), lambda c, here: (0, 0, c))
     whole = pl.BlockSpec(
         blocks[0].shape, lambda c, here: (0, 0, 0), pipeline_mode=pl.Buffered(1)
     )
     anywhere = pl.BlockSpec(memory_space=pltpu.HBM)
     kernel, extra = (hidden_kernel, []) if slope is None else (mix_kernel, [slope])
-    edge_shape = jax.ShapeDtypeStruct((planes, CX, channels), dtype)
+    row_shape = jax.ShapeDtypeStruct((planes, CX, channels), dtype)
+    plane_shape = jax.ShapeDtypeStruct((room, CX, channels), dtype)
     return pl.pallas_call(
         lambda *refs: kernel(*refs, count=count),
         grid_spec=pltpu.PrefetchScalarGridSpec(
             num_scalar_prefetch=1,
             grid=(count,),
             in_specs=[anywhere] * 2 + [whole] * count + [columns] * len(extra),
-            out_specs=[columns, edge, edge],
+            out_specs=[columns, row, row, plane, plane],
             scratch_shapes=[pltpu.VMEM((cells, channels), dtype), *weight_scratch(weight[0])],
         ),
-        out_shape=[jax.ShapeDtypeStruct((cells, channels), dtype), edge_shape, edge_shape],
+        out_shape=[
+            jax.ShapeDtypeStruct((cells, channels), dtype),
+            row_shape,
+            row_shape,
+            plane_shape,
+            plane_shape,
+        ],
     )(here, *weight, *blocks, *extra)
 
 
@@ -348,9 +364,9 @@
         return lax.ppermute(part, axes, [(i, partner(i)) for i in range(count)])
 
     def exchange(blocks):
-        got = {0: blocks(0)}
+        got = {0: blocks[0]}
         for shift in shifts:
-            got[shift] = swap(blocks(shift), "chan", lambda i: i ^ shift)
+            got[shift] = swap(blocks[shift], "chan", lambda i: i ^ shift)
         return [got[shift] for shift in range(parts)]
 
     def cut(field):
@@ -359,7 +375,7 @@
             start = (place ^ shift) * width
             piece = lax.dynamic_slice_in_dim(field, start, width, axis=2).transpose(1, 0, 2)
             pieces[shift], place = lax.optimization_barrier((piece, place))
-        return lambda shift: pieces[shift]
+        return pieces
 
     def paste(pieces):
         field = jnp.zeros((own, planes, cells), pieces[0].dtype)
@@ -383,17 +399,18 @@
         mine = jnp.stack([column, over_x, over_y, far])
         return mine, swap(mine, others, lambda i: i ^ 1)
 
-    def halo_of(field, first, last):
+    def halo_of(first, last, fore, back):
         forward, backward = shift_pairs("chan")
         row_low = lax.ppermute(last, "chan", forward)
         row_high = lax.ppermute(first, "chan", backward)
         forward, backward = shift_pairs("space")
 
-        def plane(z):
-            return jnp.concatenate([row_low[z][None], field[z], row_high[z][None]], axis=0)
-
-        plane_low = lax.ppermute(plane(-1), "space", forward)
-        plane_high = lax.ppermute(plane(0), "space", backward)
+        def joined(plane, z):
+            plane = lax.dynamic_update_slice_in_dim(plane, row_low[z][None], 0, axis=0)
+            return lax.dynamic_update_slice_in_dim(plane, row_high[z][None], rows + 1, axis=0)
+
+        plane_low = lax.ppermute(joined(fore, planes - 1), "space", forward)
+        plane_high = lax.ppermute(joined(back, 0), "space", backward)
         return row_low, row_high, plane_low, plane_high
 
     grid = (planes, rows, CX, channels)
@@ -406,20 +423,24 @@
     full_out = gather_weight(column[:, share:])
     table = jnp.concatenate([filter_taps, filter_bias[:, None]], axis=1).T
     taps = gather_column(table)
-    vol_blocks = exchange(cut(volume))
-    grad_blocks = exchange(cut(out_grad))
-    hidden, first, last = product_call(here, vol_blocks, full_in)
-    hidden = hidden.reshape(grid)
-    halo = halo_of(hidden, first, last)
-    *out_blocks, slope = stencil(here, hidden, halo, taps, full_out, vol_blocks, True)
-    block_out = paste(exchange(lambda shift: out_blocks[shift]))
-    mix_grad, first, last = product_call(
+    vol_cut, grad_cut = cut(volume), cut(out_grad)
+    own_block, taps, grad_cut = lax.optimization_barrier((vol_cut[0], taps, grad_cut))
+    vol_blocks = exchange({**vol_cut, 0: own_block})
+    grad_blocks = exchange(grad_cut)
+    hidden, *edges = product_call(here, vol_blocks, full_in)
+    halo = halo_of(*edges)
+    *out_blocks, slope = stencil(here, hidden.reshape(grid), halo, taps, full_out, vol_blocks, True)
+    out_found = exchange(out_blocks)
+    mix_grad, *edges = product_call(
         here, grad_blocks, full_out, slope.reshape(planes * width, channels)
     )
-    mix_grad = mix_grad.reshape(grid)
-    halo = halo_of(mix_grad, first, last)
-    back_blocks = stencil(here, mix_grad, halo, taps, full_in, grad_blocks, False)
-    volume_grad = paste(exchange(lambda shift: back_blocks[shift]))
+    halo = halo_of(*edges)
+    back_blocks = list(
+        stencil(here, mix_grad.reshape(grid), halo, taps, full_in, grad_blocks, False)
+    )
+    out_found, back_blocks[0] = lax.optimization_barrier((out_found, back_blocks[0]))
+    block_out = paste(out_found)
+    volume_grad = paste(exchange(back_blocks))
     return block_out, volume_grad
 
 

time: 206 us -> 195 us (0.947)
  the two profiles are of different devices: /device:TPU:0 before, /device:TPU:12 now
where the time goes in v7:
time: 195 us; the launch traced here: 194 us
  waiting for transfers between devices  86.5 us (44%)
  starting transfers between devices  41.2 us (21%)
  Pallas kernels  37.5 us (19%)
  local copies, waits for them, and re-layouts  21.6 us (11%)
  other arithmetic  6.21 us (3%)
    ppermute x24, waiting for transfers between devices, swap(): return lax.ppermute(part, axes, [(i, partner(i)) for i in range(count)])  72.2 us
    ppermute x24, starting transfers between devices, swap(): return lax.ppermute(part, axes, [(i, partner(i)) for i in range(count)])  24.1 us
    pallas_call x2, Pallas kernels, stencil(): pl.pallas_call(forward_kernel if forward else backward_kernel, grid_spec=...  22.6 us
    pallas_call x2, Pallas kernels, product_call(): pl.pallas_call(lambda *refs: kernel(*refs, count=count), grid_spec=pltpu....  14.9 us
    unnamed x60, local copies, waits for them, and re-layouts  11.2 us
    ppermute x2, waiting for transfers between devices, halo_of(): row_low = lax.ppermute(last, 'chan', forward)  8.75 us
    ppermute x2, starting transfers between devices, halo_of(): row_low = lax.ppermute(last, 'chan', forward)  6.61 us
    ppermute x2, waiting for transfers between devices, halo_of(): row_high = lax.ppermute(first, 'chan', backward)  5.45 us
  transfers between devices with their start and end apart: 32, of which 20 were waited for; matrix products, arithmetic and copies ran while one was open for 10% of the time, Pallas kernels for 15%

profile of v7, /device:TPU:12, one launch (start us, length us, event | category | flops | bytes accessed | tf_op | source)
XLA Modules:
  0.0 194.1 jit_solution(8216623694435115002)
XLA Ops:
  0.7 1.0 constant_dynamic-slice_fusion.8
  1.7 1.6 collective-permute-start
  3.4 6.5 %collective-permute-done = bf16[1,64,1024]{2,1,0:T(8,128)(2,1)S(1)} collective-permute-done((bf16[1,64,1024]{2,1,0:T(8,128)(2,1)S(1)}, bf16[1,64,1024]{2,1,0:T(8,128)(2,1)S(1)}, u32[]{:S(2)}, u32[]{:S(2)}) %collective-permute-start) | collective-permute-done | bytes 131104 | tf_op jit(solution)/shard_map/ppermute | solution.py:364
  10.0 7.4 %collective-permute-done.1 = bf16[2,64,1024]{2,1,0:T(8,128)(2,1)S(1)} collective-permute-done((bf16[2,64,1024]{2,1,0:T(8,128)(2,1)S(1)}, bf16[2,64,1024]{2,1,0:T(8,128)(2,1)S(1)}, u32[]{:S(2)}, u32[]{:S(2)}) %collective-permute-start.1) | collective-permute-done | bytes 262176 | tf_op jit(solution)/shard_map/ppermute | solution.py:364
  17.4 0.9 slice_bitcast_fusion
  18.3 1.5 collective-permute-start.2
  21.1 0.7 copy.55
  21.9 2.9 %collective-permute-done.2 = bf16[4,32,1024]{2,1,0:T(8,128)(2,1)S(1)} collective-permute-done((bf16[4,32,1024]{2,1,0:T(8,128)(2,1)S(1)}, bf16[4,32,1024]{2,1,0:T(8,128)(2,1)S(1)}, u32[]{:S(2)}, u32[]{:S(2)}) %collective-permute-start.2) | collective-permute-done | bytes 262176 | tf_op jit(solution)/shard_map/ppermute | solution.py:364
  24.8 1.3 collective-permute-done.3
  26.2 0.7 broadcast_select_fusion.1
  27.5 0.7 copy.54
  28.3 0.7 copy.53
  29.5 0.7 copy.51
  30.3 1.5 collective-permute-start.15
  32.4 0.7 copy.50
  33.1 2.6 %collective-permute-done.4 = bf16[4,32,1024]{2,1,0:T(8,128)(2,1)} collective-permute-done((bf16[4,32,1024]{2,1,0:T(8,128)(2,1)}, bf16[4,32,1024]{2,1,0:T(8,128)(2,1)}, u32[]{:S(2)}, u32[]{:S(2)}) %collective-permute-start.4) | collective-permute-done | bytes 262176 | tf_op jit(solution)/shard_map/ppermute | solution.py:364
  35.7 1.1 pad_maximum_fusion.refs_1_.mine
  36.9 0.9 copy.49
  38.4 1.1 collective-permute-start.10
  39.5 1.7 broadcast_select_fusion
  41.8 1.0 constant_dynamic-slice_fusion.4
  42.9 0.7 copy.48
  43.6 0.8 copy.52
  44.4 2.4 %collective-permute-start.9 = (bf16[4,256,128]{2,1,0:T(8,128)(2,1)}, bf16[4,256,128]{2,1,0:T(8,128)(2,1)S(1)}, u32[]{:S(2)}, u32[]{:S(2)}) collective-permute-start(bf16[4,256,128]{2,1,0:T(8,128)(2,1)} %bitcast.74), channel_id=1, source_target_pairs={{0,8},{4,12},{8,0},{12,4},{1,9},{5,13},{9,1},{13,5},{2,10},{6,14},... | collective-permute-start | bytes 786440 | tf_op jit(solution)/shard_map/ppermute | solution.py:364
  46.8 1.1 collective-permute-done.17
  47.9 1.2 collective-permute-start.7
  49.1 1.3 pad_maximum_fusion.1.mine.refs_1_
  50.4 3.6 %collective-permute-done.7 = f32[2,28,256]{2,1,0:T(8,128)S(1)} collective-permute-done((f32[2,28,256]{2,1,0:T(8,128)S(1)}, f32[2,28,256]{2,1,0:T(8,128)S(1)}, u32[]{:S(2)}, u32[]{:S(2)}) %collective-permute-start.7) | collective-permute-done | bytes 57376 | tf_op jit(solution)/shard_map/ppermute | solution.py:364
  55.3 3.8 %collective-permute-done.10.refs_6_.rest_3_ = bf16[4,256,128]{2,1,0:T(8,128)(2,1)} collective-permute-done((bf16[4,256,128]{2,1,0:T(8,128)(2,1)}, bf16[4,256,128]{2,1,0:T(8,128)(2,1)}, u32[]{:S(2)}, u32[]{:S(2)}) %collective-permute-start.10) | collective-permute-done | bytes 262176 | tf_op jit(solution)/shard_map/ppermute | solution.py:364
  59.1 3.2 %collective-permute-done.9.refs_5_.rest_2_ = bf16[4,256,128]{2,1,0:T(8,128)(2,1)S(1)} collective-permute-done((bf16[4,256,128]{2,1,0:T(8,128)(2,1)}, bf16[4,256,128]{2,1,0:T(8,128)(2,1)S(1)}, u32[]{:S(2)}, u32[]{:S(2)}) %collective-permute-start.9) | collective-permute-done | bytes 262176 | tf_op jit(solution)/shard_map/ppermute | solution.py:364
  63.0 1.0 copy-done.2
  63.9 7.0 %shard_map.77 = (bf16[512,1024]{1,0:T(8,128)(2,1)}, bf16[4,32,1024]{2,1,0:T(8,128)(2,1)}, bf16[4,32,1024]{2,1,0:T(8,128)(2,1)}, bf16[6,32,1024]{2,1,0:T(8,128)(2,1)}, bf16[6,32,1024]{2,1,0:T(8,128)(2,1)}) custom-call(s32[2]{0:T(128)} %pad_add_fusion.refs_0_.here, bf16[4,4,32,1024]{3,2,1,0:T(8,128)(2,1)} %copy-done, bf16[4,4,32,1024]{3,2,1,0:T(8,128)(2,1)} %copy-done.2, ...), custom_call_target="tpu_custom_call" | custom-call | tf_op jit(solution)/shard_map/pallas_call | solution.py:324
  70.9 3.0 %collective-permute-start.11 = (bf16[4,32,1024]{2,1,0:T(8,128)(2,1)}, bf16[4,32,1024]{2,1,0:T(8,128)(2,1)S(1)}, u32[]{:S(2)}, u32[]{:S(2)}) collective-permute-start(bf16[4,32,1024]{2,1,0:T(8,128)(2,1)} %get-tuple-element.62), channel_id=1, source_target_pairs={{0,4},{4,8},{8,12},{1,5},{5,9},{9,13},{2,6},{6,10},{10,14},{3,7},{... | collective-permute-start | bytes 786440 | tf_op jit(solution)/shard_map/ppermute | solution.py:404
  73.9 2.9 %collective-permute-start.12 = (bf16[4,32,1024]{2,1,0:T(8,128)(2,1)}, bf16[4,32,1024]{2,1,0:T(8,128)(2,1)S(1)}, u32[]{:S(2)}, u32[]{:S(2)}) collective-permute-start(bf16[4,32,1024]{2,1,0:T(8,128)(2,1)} %get-tuple-element.63), channel_id=1, source_target_pairs={{4,0},{8,4},{12,8},{5,1},{9,5},{13,9},{6,2},{10,6},{14,10},{7,3},{... | collective-permute-start | bytes 786440 | tf_op jit(solution)/shard_map/ppermute | solution.py:405
  76.8 3.8 %collective-permute-done.11.row_low = bf16[4,32,1024]{2,1,0:T(8,128)(2,1)S(1)} collective-permute-done((bf16[4,32,1024]{2,1,0:T(8,128)(2,1)}, bf16[4,32,1024]{2,1,0:T(8,128)(2,1)S(1)}, u32[]{:S(2)}, u32[]{:S(2)}) %collective-permute-start.11) | collective-permute-done | bytes 262176 | tf_op jit(solution)/shard_map/ppermute | solution.py:404
  80.7 0.7 slice_dynamic-update-slice_fusion.5
  81.4 2.8 %collective-permute-done.12.row_high = bf16[4,32,1024]{2,1,0:T(8,128)(2,1)S(1)} collective-permute-done((bf16[4,32,1024]{2,1,0:T(8,128)(2,1)}, bf16[4,32,1024]{2,1,0:T(8,128)(2,1)S(1)}, u32[]{:S(2)}, u32[]{:S(2)}) %collective-permute-start.12) | collective-permute-done | bytes 262176 | tf_op jit(solution)/shard_map/ppermute | solution.py:405
  84.2 0.7 slice_dynamic-update-slice_fusion.4
  84.9 1.3 collective-permute-start.13
  86.2 1.3 collective-permute-start.14
  87.7 3.1 %collective-permute-start.23 = (bf16[4,256,128]{2,1,0:T(8,128)(2,1)}, bf16[4,256,128]{2,1,0:T(8,128)(2,1)S(1)}, u32[]{:S(2)}, u32[]{:S(2)}) collective-permute-start(bf16[4,256,128]{2,1,0:T(8,128)(2,1)} %bitcast.72), channel_id=1, source_target_pairs={{0,8},{4,12},{8,0},{12,4},{1,9},{5,13},{9,1},{13,5},{2,10},{6,14},... | collective-permute-start | bytes 786440 | tf_op jit(solution)/shard_map/ppermute | solution.py:364
  91.2 0.7 copy-done.18
  92.0 11.6 %shard_map.78 = (bf16[4,256,128]{2,1,0:T(8,128)(2,1)}, bf16[4,256,128]{2,1,0:T(8,128)(2,1)}, bf16[4,256,128]{2,1,0:T(8,128)(2,1)}, bf16[4,256,128]{2,1,0:T(8,128)(2,1)}, f32[4,4,32,1024]{3,2,1,0:T(8,128)}) custom-call(s32[2]{0:T(128)} %pad_add_fusion.refs_0_.here, bf16[4,4,32,1024]{3,2,1,0:T(8,128)(2,1)} %bitcast.60, bf16[4,32,1024]{2,1,0:T(8,128)(2,1)} %copy-done.14, ...), custom_call_target="tpu_custom_call" | custom-call | tf_op jit(solution)/shard_map/pallas_call | solution.py:229
  103.7 4.8 %collective-permute-done.23.refs_5_.rest_2_ = bf16[4,256,128]{2,1,0:T(8,128)(2,1)S(1)} collective-permute-done((bf16[4,256,128]{2,1,0:T(8,128)(2,1)}, bf16[4,256,128]{2,1,0:T(8,128)(2,1)S(1)}, u32[]{:S(2)}, u32[]{:S(2)}) %collective-permute-start.23) | collective-permute-done | bytes 262176 | tf_op jit(solution)/shard_map/ppermute | solution.py:364
  108.5 6.3 %collective-permute-done.24.refs_6_.rest_3_ = bf16[4,256,128]{2,1,0:T(8,128)(2,1)S(1)} collective-permute-done((bf16[4,256,128]{2,1,0:T(8,128)(2,1)}, bf16[4,256,128]{2,1,0:T(8,128)(2,1)S(1)}, u32[]{:S(2)}, u32[]{:S(2)}) %collective-permute-start.24) | collective-permute-done | bytes 262176 | tf_op jit(solution)/shard_map/ppermute | solution.py:364
  115.4 7.9 %shard_map.79 = (bf16[512,1024]{1,0:T(8,128)(2,1)}, bf16[4,32,1024]{2,1,0:T(8,128)(2,1)}, bf16[4,32,1024]{2,1,0:T(8,128)(2,1)}, bf16[6,32,1024]{2,1,0:T(8,128)(2,1)}, bf16[6,32,1024]{2,1,0:T(8,128)(2,1)}) custom-call(s32[2]{0:T(128)} %pad_add_fusion.refs_0_.here, bf16[4,4,32,1024]{3,2,1,0:T(8,128)(2,1)} %copy-done.1, ...), custom_call_target="tpu_custom_call" | custom-call | tf_op jit(solution)/shard_map/pallas_call | solution.py:324
  123.3 3.6 %collective-permute-start.25 = (bf16[4,32,1024]{2,1,0:T(8,128)(2,1)}, bf16[4,32,1024]{2,1,0:T(8,128)(2,1)S(1)}, u32[]{:S(2)}, u32[]{:S(2)}) collective-permute-start(bf16[4,32,1024]{2,1,0:T(8,128)(2,1)} %get-tuple-element.77), channel_id=1, source_target_pairs={{0,4},{4,8},{8,12},{1,5},{5,9},{9,13},{2,6},{6,10},{10,14},{3,7},{... | collective-permute-start | bytes 786440 | tf_op jit(solution)/shard_map/ppermute | solution.py:404
  127.0 2.2 %collective-permute-start.26 = (bf16[4,32,1024]{2,1,0:T(8,128)(2,1)}, bf16[4,32,1024]{2,1,0:T(8,128)(2,1)S(1)}, u32[]{:S(2)}, u32[]{:S(2)}) collective-permute-start(bf16[4,32,1024]{2,1,0:T(8,128)(2,1)} %get-tuple-element.78), channel_id=1, source_target_pairs={{4,0},{8,4},{12,8},{5,1},{9,5},{13,9},{6,2},{10,6},{14,10},{7,3},{... | collective-permute-start | bytes 786440 | tf_op jit(solution)/shard_map/ppermute | solution.py:405
  129.2 4.9 %collective-permute-done.25.row_low = bf16[4,32,1024]{2,1,0:T(8,128)(2,1)S(1)} collective-permute-done((bf16[4,32,1024]{2,1,0:T(8,128)(2,1)}, bf16[4,32,1024]{2,1,0:T(8,128)(2,1)S(1)}, u32[]{:S(2)}, u32[]{:S(2)}) %collective-permute-start.25) | collective-permute-done | bytes 262176 | tf_op jit(solution)/shard_map/ppermute | solution.py:404
  134.1 0.8 slice_dynamic-update-slice_fusion.1
  134.9 2.6 %collective-permute-done.26.row_high = bf16[4,32,1024]{2,1,0:T(8,128)(2,1)S(1)} collective-permute-done((bf16[4,32,1024]{2,1,0:T(8,128)(2,1)}, bf16[4,32,1024]{2,1,0:T(8,128)(2,1)S(1)}, u32[]{:S(2)}, u32[]{:S(2)}) %collective-permute-start.26) | collective-permute-done | bytes 262176 | tf_op jit(solution)/shard_map/ppermute | solution.py:405
  138.2 1.3 collective-permute-start.27
  139.5 1.5 collective-permute-start.28
  141.4 1.7 collective-permute-start.20
  143.0 1.5 collective-permute-start.21
  144.6 0.7 copy-done.16
  145.5 11.0 %shard_map.80 = (bf16[4,256,128]{2,1,0:T(8,128)(2,1)}, bf16[4,256,128]{2,1,0:T(8,128)(2,1)}, bf16[4,256,128]{2,1,0:T(8,128)(2,1)}, bf16[4,256,128]{2,1,0:T(8,128)(2,1)}) custom-call(s32[2]{0:T(128)} %pad_add_fusion.refs_0_.here, bf16[4,4,32,1024]{3,2,1,0:T(8,128)(2,1)} %bitcast.59, bf16[4,32,1024]{2,1,0:T(8,128)(2,1)} %copy-done.12, ...), custom_call_target="tpu_custom_call" | custom-call | tf_op jit(solution)/shard_map/pallas_call | solution.py:229
  156.5 4.4 %collective-permute-done.20 = bf16[4,256,128]{2,1,0:T(8,128)(2,1)S(1)} collective-permute-done((bf16[4,256,128]{2,1,0:T(8,128)(2,1)S(1)}, bf16[4,256,128]{2,1,0:T(8,128)(2,1)S(1)}, u32[]{:S(2)}, u32[]{:S(2)}) %collective-permute-start.20) | collective-permute-done | bytes 262176 | tf_op jit(solution)/shard_map/ppermute | solution.py:364
  160.9 7.6 %collective-permute-done.21 = bf16[4,256,128]{2,1,0:T(8,128)(2,1)S(1)} collective-permute-done((bf16[4,256,128]{2,1,0:T(8,128)(2,1)S(1)}, bf16[4,256,128]{2,1,0:T(8,128)(2,1)S(1)}, u32[]{:S(2)}, u32[]{:S(2)}) %collective-permute-start.21) | collective-permute-done | bytes 262176 | tf_op jit(solution)/shard_map/ppermute | solution.py:364
  169.0 3.9 %collective-permute-start.31 = (bf16[4,256,128]{2,1,0:T(8,128)(2,1)}, bf16[4,256,128]{2,1,0:T(8,128)(2,1)S(1)}, u32[]{:S(2)}, u32[]{:S(2)}) collective-permute-start(bf16[4,256,128]{2,1,0:T(8,128)(2,1)} %get-tuple-element.89), channel_id=1, source_target_pairs={{0,4},{4,0},{8,12},{12,8},{1,5},{5,1},{9,13},{13,9},{2,6},{6,2},{1... | collective-permute-start | bytes 786440 | tf_op jit(solution)/shard_map/ppermute | solution.py:364
  173.1 1.2 copy_dynamic-update-slice_fusion.3
  175.9 10.8 %collective-permute-done.29 = bf16[4,256,128]{2,1,0:T(8,128)(2,1)S(1)} collective-permute-done((bf16[4,256,128]{2,1,0:T(8,128)(2,1)}, bf16[4,256,128]{2,1,0:T(8,128)(2,1)S(1)}, u32[]{:S(2)}, u32[]{:S(2)}) %collective-permute-start.29) | collective-permute-done | bytes 262176 | tf_op jit(solution)/shard_map/ppermute | solution.py:364
  187.1 5.5 %collective-permute-done.30 = bf16[4,256,128]{2,1,0:T(8,128)(2,1)S(1)} collective-permute-done((bf16[4,256,128]{2,1,0:T(8,128)(2,1)}, bf16[4,256,128]{2,1,0:T(8,128)(2,1)S(1)}, u32[]{:S(2)}, u32[]{:S(2)}) %collective-permute-start.30) | collective-permute-done | bytes 262176 | tf_op jit(solution)/shard_map/ppermute | solution.py:364
  193.2 1.0 copy-done.6
  (98 shorter events, 12.3 us)
Async XLA Ops:
  0.6 19.7 %copy-start.22 = (f32[256]{0:T(256)S(1)}, f32[256]{0:T(256)}, u32[]{:S(2)}) copy-start(f32[256]{0:T(256)} %param.11) | copy-start | bytes 3076
  0.6 19.7 %copy-start.21 = (f32[256,27]{0,1:T(8,128)S(1)}, f32[256,27]{0,1:T(8,128)}, u32[]{:S(2)}) copy-start(f32[256,27]{0,1:T(8,128)} %param.10) | copy-start | bytes 82948
  0.7 20.3 %copy-start.4 = (bf16[256,4,512]{2,1,0:T(4,128)(2,1)S(1)}, bf16[256,4,512]{2,1,0:T(4,128)(2,1)}, u32[]{:S(2)}) copy-start(bf16[256,4,512]{2,1,0:T(4,128)(2,1)} %param.6) | copy-start | bytes 3145732
  0.7 20.3 %copy-start.3 = (bf16[256,4,512]{2,1,0:T(4,128)(2,1)S(1)}, bf16[256,4,512]{2,1,0:T(4,128)(2,1)}, u32[]{:S(2)}) copy-start(bf16[256,4,512]{2,1,0:T(4,128)(2,1)} %param.7) | copy-start | bytes 3145732
  1.7 8.1 %collective-permute-start = (bf16[1,64,1024]{2,1,0:T(8,128)(2,1)S(1)}, bf16[1,64,1024]{2,1,0:T(8,128)(2,1)S(1)}, u32[]{:S(2)}, u32[]{:S(2)}) collective-permute-start(bf16[1,64,1024]{2,1,0:T(8,128)(2,1)S(1)} %maximum_bitcast_fusion), channel_id=1, source_target_pairs={{0,12},{4,8},{8,4},{12,0},{1,13},{5,9},{9,5},{13,1},{2,14},{6,10},... | collective-permute-start | bytes 393224 | tf_op jit(solution)/shard_map/ppermute | solution.py:364
  9.9 7.4 %collective-permute-start.1 = (bf16[2,64,1024]{2,1,0:T(8,128)(2,1)S(1)}, bf16[2,64,1024]{2,1,0:T(8,128)(2,1)S(1)}, u32[]{:S(2)}, u32[]{:S(2)}) collective-permute-start(bf16[2,64,1024]{2,1,0:T(8,128)(2,1)S(1)} %pad_maximum_fusion.3), channel_id=1, source_target_pairs={{0,4},{4,0},{8,12},{12,8},{1,5},{5,1},{9,13},{13,9},{2,6},{6,2},{1... | collective-permute-start | bytes 786440 | tf_op jit(solution)/shard_map/ppermute | solution.py:364
  18.3 6.5 %collective-permute-start.2 = (bf16[4,32,1024]{2,1,0:T(8,128)(2,1)S(1)}, bf16[4,32,1024]{2,1,0:T(8,128)(2,1)S(1)}, u32[]{:S(2)}, u32[]{:S(2)}) collective-permute-start(bf16[4,32,1024]{2,1,0:T(8,128)(2,1)S(1)} %get-tuple-element.93), channel_id=1, source_target_pairs={{0,2},{1,3},{2,0},{3,1},{16,18},{17,19},{18,16},{19,17},{4,6},{5,7... | collective-permute-start | bytes 786440 | tf_op jit(solution)/shard_map/ppermute | solution.py:364
  19.8 6.4 %collective-permute-start.3 = (bf16[4,32,1024]{2,1,0:T(8,128)(2,1)S(1)}, bf16[4,32,1024]{2,1,0:T(8,128)(2,1)S(1)}, u32[]{:S(2)}, u32[]{:S(2)}) collective-permute-start(bf16[4,32,1024]{2,1,0:T(8,128)(2,1)S(1)} %get-tuple-element.93), channel_id=1, source_target_pairs={{0,16},{1,17},{2,18},{3,19},{16,0},{17,1},{18,2},{19,3},{4,20},{5,... | collective-permute-start | bytes 786440 | tf_op jit(solution)/shard_map/ppermute | solution.py:364
  20.3 24.1 %collective-permute-start.6 = (f32[1,28,256]{2,1,0:T(8,128)S(1)}, f32[1,28,256]{2,1,0:T(8,128)S(1)}, u32[]{:S(2)}, u32[]{:S(2)}) collective-permute-start(f32[1,28,256]{2,1,0:T(8,128)S(1)} %maximum_bitcast_fusion.1), channel_id=1, source_target_pairs={{0,12},{4,8},{8,4},{12,0},{1,13},{5,9},{9,5},{13,1},{2,14},{6,10},... | collective-permute-start | bytes 86024 | tf_op jit(solution)/shard_map/ppermute | solution.py:364
  26.9 8.8 %collective-permute-start.4 = (bf16[4,32,1024]{2,1,0:T(8,128)(2,1)}, bf16[4,32,1024]{2,1,0:T(8,128)(2,1)}, u32[]{:S(2)}, u32[]{:S(2)}) collective-permute-start(bf16[4,32,1024]{2,1,0:T(8,128)(2,1)} %broadcast_select_fusion.1), channel_id=1, source_target_pairs={{0,2},{1,17},{2,0},{3,19},{16,18},{17,1},{18,16},{19,3},{4,6},{5,2... | collective-permute-start | bytes 786440 | tf_op jit(solution)/shard_map/ppermute | solution.py:364
  29.1 26.2 %collective-permute-start.8 = (bf16[4,256,128]{2,1,0:T(8,128)(2,1)}, bf16[4,256,128]{2,1,0:T(8,128)(2,1)}, u32[]{:S(2)}, u32[]{:S(2)}) collective-permute-start(bf16[4,256,128]{2,1,0:T(8,128)(2,1)} %bitcast.51), channel_id=1, source_target_pairs={{0,4},{4,0},{8,12},{12,8},{1,5},{5,1},{9,13},{13,9},{2,6},{6,2},{1... | collective-permute-start | bytes 786440 | tf_op jit(solution)/shard_map/ppermute | solution.py:364
  30.3 8.1 %collective-permute-start.15 = (bf16[4,32,1024]{2,1,0:T(8,128)(2,1)}, bf16[4,32,1024]{2,1,0:T(8,128)(2,1)S(1)}, u32[]{:S(2)}, u32[]{:S(2)}) collective-permute-start(bf16[4,32,1024]{2,1,0:T(8,128)(2,1)} %get-tuple-element.92), channel_id=1, source_target_pairs={{0,2},{1,3},{2,0},{3,1},{16,18},{17,19},{18,16},{19,17},{4,6},{5,7... | collective-permute-start | bytes 786440 | tf_op jit(solution)/shard_map/ppermute | solution.py:364
  31.8 7.7 %collective-permute-start.16 = (bf16[4,32,1024]{2,1,0:T(8,128)(2,1)}, bf16[4,32,1024]{2,1,0:T(8,128)(2,1)}, u32[]{:S(2)}, u32[]{:S(2)}) collective-permute-start(bf16[4,32,1024]{2,1,0:T(8,128)(2,1)} %get-tuple-element.92), channel_id=1, source_target_pairs={{0,16},{1,17},{2,18},{3,19},{16,0},{17,1},{18,2},{19,3},{4,20},{5,... | collective-permute-start | bytes 786440 | tf_op jit(solution)/shard_map/ppermute | solution.py:364
  36.7 13.7 %copy-start = (bf16[4,4,32,1024]{3,2,1,0:T(8,128)(2,1)}, bf16[4,4,32,1024]{3,2,1,0:T(8,128)(2,1)S(1)}, u32[]{:S(2)}) copy-start(bf16[4,4,32,1024]{3,2,1,0:T(8,128)(2,1)S(1)} %pad_maximum_fusion.refs_1_.mine) | copy-start | bytes 3145732
  36.8 25.5 %collective-permute-start.5 = (bf16[4,4,32,1024]{3,2,1,0:T(8,128)(2,1)S(1)}, bf16[4,4,32,1024]{3,2,1,0:T(8,128)(2,1)S(1)}, u32[]{:S(2)}, u32[]{:S(2)}) collective-permute-start(bf16[4,4,32,1024]{3,2,1,0:T(8,128)(2,1)S(1)} %pad_maximum_fusion.refs_1_.mine), channel_id=1, source_target_pairs={{0,1},{1,0},{2,3},{3,2},{16,17},{17,16},{18,19},{19,18},{4,5},{5,4... | collective-permute-start | bytes 3145736 | tf_op jit(solution)/shard_map/ppermute | solution.py:364
  38.4 2.8 %copy-start.8 = (bf16[4,32,1024]{2,1,0:T(8,128)(2,1)}, bf16[4,32,1024]{2,1,0:T(8,128)(2,1)S(1)}, u32[]{:S(2)}) copy-start(bf16[4,32,1024]{2,1,0:T(8,128)(2,1)S(1)} %collective-permute-done.15) | copy-start | bytes 786436
  38.4 20.7 %collective-permute-start.10 = (bf16[4,256,128]{2,1,0:T(8,128)(2,1)}, bf16[4,256,128]{2,1,0:T(8,128)(2,1)}, u32[]{:S(2)}, u32[]{:S(2)}) collective-permute-start(bf16[4,256,128]{2,1,0:T(8,128)(2,1)} %bitcast.76), channel_id=1, source_target_pairs={{0,12},{4,8},{8,4},{12,0},{1,13},{5,9},{9,5},{13,1},{2,14},{6,10},... | collective-permute-start | bytes 786440 | tf_op jit(solution)/shard_map/ppermute | solution.py:364
  41.2 6.7 %collective-permute-start.17 = (bf16[4,32,1024]{2,1,0:T(8,128)(2,1)}, bf16[4,32,1024]{2,1,0:T(8,128)(2,1)}, u32[]{:S(2)}, u32[]{:S(2)}) collective-permute-start(bf16[4,32,1024]{2,1,0:T(8,128)(2,1)} %broadcast_select_fusion), channel_id=1, source_target_pairs={{0,2},{1,17},{2,0},{3,19},{16,18},{17,1},{18,16},{19,3},{4,6},{5,2... | collective-permute-start | bytes 786440 | tf_op jit(solution)/shard_map/ppermute | solution.py:364
  44.4 17.8 %collective-permute-start.9 = (bf16[4,256,128]{2,1,0:T(8,128)(2,1)}, bf16[4,256,128]{2,1,0:T(8,128)(2,1)S(1)}, u32[]{:S(2)}, u32[]{:S(2)}) collective-permute-start(bf16[4,256,128]{2,1,0:T(8,128)(2,1)} %bitcast.74), channel_id=1, source_target_pairs={{0,8},{4,12},{8,0},{12,4},{1,9},{5,13},{9,1},{13,5},{2,10},{6,14},... | collective-permute-start | bytes 786440 | tf_op jit(solution)/shard_map/ppermute | solution.py:364
  47.9 6.1 %collective-permute-start.7 = (f32[2,28,256]{2,1,0:T(8,128)S(1)}, f32[2,28,256]{2,1,0:T(8,128)S(1)}, u32[]{:S(2)}, u32[]{:S(2)}) collective-permute-start(f32[2,28,256]{2,1,0:T(8,128)S(1)} %pad_maximum_fusion.5), channel_id=1, source_target_pairs={{0,4},{4,0},{8,12},{12,8},{1,5},{5,1},{9,13},{13,9},{2,6},{6,2},{1... | collective-permute-start | bytes 172040 | tf_op jit(solution)/shard_map/ppermute | solution.py:364
  50.4 40.7 %copy-start.1 = (bf16[4,4,32,1024]{3,2,1,0:T(8,128)(2,1)}, bf16[4,4,32,1024]{3,2,1,0:T(8,128)(2,1)S(1)}, u32[]{:S(2)}) copy-start(bf16[4,4,32,1024]{3,2,1,0:T(8,128)(2,1)S(1)} %pad_maximum_fusion.1.mine.refs_1_) | copy-start | bytes 3145732
  54.0 36.8 %collective-permute-start.18 = (bf16[4,4,32,1024]{3,2,1,0:T(8,128)(2,1)S(1)}, bf16[4,4,32,1024]{3,2,1,0:T(8,128)(2,1)}, u32[]{:S(2)}, u32[]{:S(2)}) collective-permute-start(bf16[4,4,32,1024]{3,2,1,0:T(8,128)(2,1)S(1)} %pad_maximum_fusion.1.mine.refs_1_), channel_id=1, source_target_pairs={{0,1},{1,0},{2,3},{3,2},{16,17},{17,16},{18,19},{19,18},{4,5},{5,4... | collective-permute-start | bytes 3145736 | tf_op jit(solution)/shard_map/ppermute | solution.py:364
  62.2 0.7 copy-start.7
  63.0 1.0 copy-start.2
  70.9 9.7 %collective-permute-start.11 = (bf16[4,32,1024]{2,1,0:T(8,128)(2,1)}, bf16[4,32,1024]{2,1,0:T(8,128)(2,1)S(1)}, u32[]{:S(2)}, u32[]{:S(2)}) collective-permute-start(bf16[4,32,1024]{2,1,0:T(8,128)(2,1)} %get-tuple-element.62), channel_id=1, source_target_pairs={{0,4},{4,8},{8,12},{1,5},{5,9},{9,13},{2,6},{6,10},{10,14},{3,7},{... | collective-permute-start | bytes 786440 | tf_op jit(solution)/shard_map/ppermute | solution.py:404
  73.9 10.3 %collective-permute-start.12 = (bf16[4,32,1024]{2,1,0:T(8,128)(2,1)}, bf16[4,32,1024]{2,1,0:T(8,128)(2,1)S(1)}, u32[]{:S(2)}, u32[]{:S(2)}) collective-permute-start(bf16[4,32,1024]{2,1,0:T(8,128)(2,1)} %get-tuple-element.63), channel_id=1, source_target_pairs={{4,0},{8,4},{12,8},{5,1},{9,5},{13,9},{6,2},{10,6},{14,10},{7,3},{... | collective-permute-start | bytes 786440 | tf_op jit(solution)/shard_map/ppermute | solution.py:405
  80.6 10.5 %copy-start.14 = (bf16[4,32,1024]{2,1,0:T(8,128)(2,1)}, bf16[4,32,1024]{2,1,0:T(8,128)(2,1)S(1)}, u32[]{:S(2)}) copy-start(bf16[4,32,1024]{2,1,0:T(8,128)(2,1)S(1)} %collective-permute-done.11.row_low) | copy-start | bytes 786436
  84.2 6.9 %copy-start.15 = (bf16[4,32,1024]{2,1,0:T(8,128)(2,1)}, bf16[4,32,1024]{2,1,0:T(8,128)(2,1)S(1)}, u32[]{:S(2)}) copy-start(bf16[4,32,1024]{2,1,0:T(8,128)(2,1)S(1)} %collective-permute-done.12.row_high) | copy-start | bytes 786436
  84.9 6.2 %collective-permute-start.13 = (bf16[6,32,1024]{2,1,0:T(8,128)(2,1)}, bf16[6,32,1024]{2,1,0:T(8,128)(2,1)S(1)}, u32[]{:S(2)}, u32[]{:S(2)}) collective-permute-start(bf16[6,32,1024]{2,1,0:T(8,128)(2,1)} %get-tuple-element.99), channel_id=1, source_target_pairs={{0,1},{1,2},{2,3},{4,5},{5,6},{6,7},{8,9},{9,10},{10,11},{12,13},{... | collective-permute-start | bytes 1179656 | tf_op jit(solution)/shard_map/ppermute | solution.py:412
  86.2 4.9 %collective-permute-start.14 = (bf16[6,32,1024]{2,1,0:T(8,128)(2,1)}, bf16[6,32,1024]{2,1,0:T(8,128)(2,1)S(1)}, u32[]{:S(2)}, u32[]{:S(2)}) collective-permute-start(bf16[6,32,1024]{2,1,0:T(8,128)(2,1)} %get-tuple-element.98), channel_id=1, source_target_pairs={{1,0},{2,1},{3,2},{5,4},{6,5},{7,6},{9,8},{10,9},{11,10},{13,12},{... | collective-permute-start | bytes 1179656 | tf_op jit(solution)/shard_map/ppermute | solution.py:413
  87.5 16.1 %collective-permute-start.22 = (bf16[4,256,128]{2,1,0:T(8,128)(2,1)}, bf16[4,256,128]{2,1,0:T(8,128)(2,1)S(1)}, u32[]{:S(2)}, u32[]{:S(2)}) collective-permute-start(bf16[4,256,128]{2,1,0:T(8,128)(2,1)} %bitcast.75), channel_id=1, source_target_pairs={{0,4},{4,0},{8,12},{12,8},{1,5},{5,1},{9,13},{13,9},{2,6},{6,2},{1... | collective-permute-start | bytes 786440 | tf_op jit(solution)/shard_map/ppermute | solution.py:364
  87.7 20.8 %collective-permute-start.23 = (bf16[4,256,128]{2,1,0:T(8,128)(2,1)}, bf16[4,256,128]{2,1,0:T(8,128)(2,1)S(1)}, u32[]{:S(2)}, u32[]{:S(2)}) collective-permute-start(bf16[4,256,128]{2,1,0:T(8,128)(2,1)} %bitcast.72), channel_id=1, source_target_pairs={{0,8},{4,12},{8,0},{12,4},{1,9},{5,13},{9,1},{13,5},{2,10},{6,14},... | collective-permute-start | bytes 786440 | tf_op jit(solution)/shard_map/ppermute | solution.py:364
  90.8 23.9 %collective-permute-start.24 = (bf16[4,256,128]{2,1,0:T(8,128)(2,1)}, bf16[4,256,128]{2,1,0:T(8,128)(2,1)S(1)}, u32[]{:S(2)}, u32[]{:S(2)}) collective-permute-start(bf16[4,256,128]{2,1,0:T(8,128)(2,1)} %bitcast.73), channel_id=1, source_target_pairs={{0,12},{4,8},{8,4},{12,0},{1,13},{5,9},{9,5},{13,1},{2,14},{6,10},... | collective-permute-start | bytes 786440 | tf_op jit(solution)/shard_map/ppermute | solution.py:364
  91.1 0.8 copy-start.18
  91.1 0.9 copy-start.19
  103.6 11.1 %copy-start.9 = (bf16[4,256,128]{2,1,0:T(8,128)(2,1)}, bf16[4,256,128]{2,1,0:T(8,128)(2,1)S(1)}, u32[]{:S(2)}) copy-start(bf16[4,256,128]{2,1,0:T(8,128)(2,1)S(1)} %collective-permute-done.22.refs_4_.rest_1_) | copy-start | bytes 786436
  108.5 6.3 %copy-start.10 = (bf16[4,256,128]{2,1,0:T(8,128)(2,1)}, bf16[4,256,128]{2,1,0:T(8,128)(2,1)S(1)}, u32[]{:S(2)}) copy-start(bf16[4,256,128]{2,1,0:T(8,128)(2,1)S(1)} %collective-permute-done.23.refs_5_.rest_2_) | copy-start | bytes 786436
  114.7 0.7 copy-start.11
  115.4 25.5 %copy-start.25 = (bf16[4,256,128]{2,1,0:T(8,128)(2,1)S(1)}, bf16[4,256,128]{2,1,0:T(8,128)(2,1)}, u32[]{:S(2)}) copy-start(bf16[4,256,128]{2,1,0:T(8,128)(2,1)} %get-tuple-element.68) | copy-start | bytes 786436
  115.4 25.9 %copy-start.24 = (bf16[4,256,128]{2,1,0:T(8,128)(2,1)S(1)}, bf16[4,256,128]{2,1,0:T(8,128)(2,1)}, u32[]{:S(2)}) copy-start(bf16[4,256,128]{2,1,0:T(8,128)(2,1)} %get-tuple-element.69) | copy-start | bytes 786436
  115.4 27.6 %copy-start.23 = (bf16[4,256,128]{2,1,0:T(8,128)(2,1)S(1)}, bf16[4,256,128]{2,1,0:T(8,128)(2,1)}, u32[]{:S(2)}) copy-start(bf16[4,256,128]{2,1,0:T(8,128)(2,1)} %get-tuple-element.70) | copy-start | bytes 786436
  123.3 10.8 %collective-permute-start.25 = (bf16[4,32,1024]{2,1,0:T(8,128)(2,1)}, bf16[4,32,1024]{2,1,0:T(8,128)(2,1)S(1)}, u32[]{:S(2)}, u32[]{:S(2)}) collective-permute-start(bf16[4,32,1024]{2,1,0:T(8,128)(2,1)} %get-tuple-element.77), channel_id=1, source_target_pairs={{0,4},{4,8},{8,12},{1,5},{5,9},{9,13},{2,6},{6,10},{10,14},{3,7},{... | collective-permute-start | bytes 786440 | tf_op jit(solution)/shard_map/ppermute | solution.py:404
  127.0 10.5 %collective-permute-start.26 = (bf16[4,32,1024]{2,1,0:T(8,128)(2,1)}, bf16[4,32,1024]{2,1,0:T(8,128)(2,1)S(1)}, u32[]{:S(2)}, u32[]{:S(2)}) collective-permute-start(bf16[4,32,1024]{2,1,0:T(8,128)(2,1)} %get-tuple-element.78), channel_id=1, source_target_pairs={{4,0},{8,4},{12,8},{5,1},{9,5},{13,9},{6,2},{10,6},{14,10},{7,3},{... | collective-permute-start | bytes 786440 | tf_op jit(solution)/shard_map/ppermute | solution.py:405
  134.1 10.4 %copy-start.12 = (bf16[4,32,1024]{2,1,0:T(8,128)(2,1)}, bf16[4,32,1024]{2,1,0:T(8,128)(2,1)S(1)}, u32[]{:S(2)}) copy-start(bf16[4,32,1024]{2,1,0:T(8,128)(2,1)S(1)} %collective-permute-done.25.row_low) | copy-start | bytes 786436
  137.5 7.1 %copy-start.13 = (bf16[4,32,1024]{2,1,0:T(8,128)(2,1)}, bf16[4,32,1024]{2,1,0:T(8,128)(2,1)S(1)}, u32[]{:S(2)}) copy-start(bf16[4,32,1024]{2,1,0:T(8,128)(2,1)S(1)} %collective-permute-done.26.row_high) | copy-start | bytes 786436
  138.2 6.4 %collective-permute-start.27 = (bf16[6,32,1024]{2,1,0:T(8,128)(2,1)}, bf16[6,32,1024]{2,1,0:T(8,128)(2,1)S(1)}, u32[]{:S(2)}, u32[]{:S(2)}) collective-permute-start(bf16[6,32,1024]{2,1,0:T(8,128)(2,1)} %get-tuple-element.95), channel_id=1, source_target_pairs={{0,1},{1,2},{2,3},{4,5},{5,6},{6,7},{8,9},{9,10},{10,11},{12,13},{... | collective-permute-start | bytes 1179656 | tf_op jit(solution)/shard_map/ppermute | solution.py:412
  139.5 5.1 %collective-permute-start.28 = (bf16[6,32,1024]{2,1,0:T(8,128)(2,1)}, bf16[6,32,1024]{2,1,0:T(8,128)(2,1)S(1)}, u32[]{:S(2)}, u32[]{:S(2)}) collective-permute-start(bf16[6,32,1024]{2,1,0:T(8,128)(2,1)} %get-tuple-element.94), channel_id=1, source_target_pairs={{1,0},{2,1},{3,2},{5,4},{6,5},{7,6},{9,8},{10,9},{11,10},{13,12},{... | collective-permute-start | bytes 1179656 | tf_op jit(solution)/shard_map/ppermute | solution.py:413
  141.0 15.5 %collective-permute-start.19 = (bf16[4,256,128]{2,1,0:T(8,128)(2,1)S(1)}, bf16[4,256,128]{2,1,0:T(8,128)(2,1)S(1)}, u32[]{:S(2)}, u32[]{:S(2)}) collective-permute-start(bf16[4,256,128]{2,1,0:T(8,128)(2,1)S(1)} %copy-done.25), channel_id=1, source_target_pairs={{0,4},{4,0},{8,12},{12,8},{1,5},{5,1},{9,13},{13,9},{2,6},{6,2},{1... | collective-permute-start | bytes 786440 | tf_op jit(solution)/shard_map/ppermute | solution.py:364
  141.4 19.6 %collective-permute-start.20 = (bf16[4,256,128]{2,1,0:T(8,128)(2,1)S(1)}, bf16[4,256,128]{2,1,0:T(8,128)(2,1)S(1)}, u32[]{:S(2)}, u32[]{:S(2)}) collective-permute-start(bf16[4,256,128]{2,1,0:T(8,128)(2,1)S(1)} %copy-done.24), channel_id=1, source_target_pairs={{0,8},{4,12},{8,0},{12,4},{1,9},{5,13},{9,1},{13,5},{2,10},{6,14},... | collective-permute-start | bytes 786440 | tf_op jit(solution)/shard_map/ppermute | solution.py:364
  143.0 25.4 %collective-permute-start.21 = (bf16[4,256,128]{2,1,0:T(8,128)(2,1)S(1)}, bf16[4,256,128]{2,1,0:T(8,128)(2,1)S(1)}, u32[]{:S(2)}, u32[]{:S(2)}) collective-permute-start(bf16[4,256,128]{2,1,0:T(8,128)(2,1)S(1)} %copy-done.23), channel_id=1, source_target_pairs={{0,12},{4,8},{8,4},{12,0},{1,13},{5,9},{9,5},{13,1},{2,14},{6,10},... | collective-permute-start | bytes 786440 | tf_op jit(solution)/shard_map/ppermute | solution.py:364
  144.5 0.8 copy-start.16
  144.5 0.9 copy-start.17
  156.4 18.2 %copy-start.20 = (bf16[4,256,128]{2,1,0:T(8,128)(2,1)S(1)}, bf16[4,256,128]{2,1,0:T(8,128)(2,1)}, u32[]{:S(2)}) copy-start(bf16[4,256,128]{2,1,0:T(8,128)(2,1)} %get-tuple-element.82) | copy-start | bytes 786436
  168.5 18.3 %collective-permute-start.29 = (bf16[4,256,128]{2,1,0:T(8,128)(2,1)}, bf16[4,256,128]{2,1,0:T(8,128)(2,1)S(1)}, u32[]{:S(2)}, u32[]{:S(2)}) collective-permute-start(bf16[4,256,128]{2,1,0:T(8,128)(2,1)} %get-tuple-element.87), channel_id=1, source_target_pairs={{0,8},{4,12},{8,0},{12,4},{1,9},{5,13},{9,1},{13,5},{2,10},{6,14},... | collective-permute-start | bytes 786440 | tf_op jit(solution)/shard_map/ppermute | solution.py:364
  168.5 24.1 %collective-permute-start.30 = (bf16[4,256,128]{2,1,0:T(8,128)(2,1)}, bf16[4,256,128]{2,1,0:T(8,128)(2,1)S(1)}, u32[]{:S(2)}, u32[]{:S(2)}) collective-permute-start(bf16[4,256,128]{2,1,0:T(8,128)(2,1)} %get-tuple-element.88), channel_id=1, source_target_pairs={{0,12},{4,8},{8,4},{12,0},{1,13},{5,9},{9,5},{13,1},{2,14},{6,10},... | collective-permute-start | bytes 786440 | tf_op jit(solution)/shard_map/ppermute | solution.py:364
  169.0 23.9 %collective-permute-start.31 = (bf16[4,256,128]{2,1,0:T(8,128)(2,1)}, bf16[4,256,128]{2,1,0:T(8,128)(2,1)S(1)}, u32[]{:S(2)}, u32[]{:S(2)}) collective-permute-start(bf16[4,256,128]{2,1,0:T(8,128)(2,1)} %get-tuple-element.89), channel_id=1, source_target_pairs={{0,4},{4,0},{8,12},{12,8},{1,5},{5,1},{9,13},{13,9},{2,6},{6,2},{1... | collective-permute-start | bytes 786440 | tf_op jit(solution)/shard_map/ppermute | solution.py:364
  175.9 17.3 %copy-start.5 = (bf16[256,4,512]{2,1,0:T(4,128)(2,1)}, bf16[256,4,512]{2,1,0:T(4,128)(2,1)S(1)}, u32[]{:S(2)}) copy-start(bf16[256,4,512]{2,1,0:T(4,128)(2,1)S(1)} %copy_dynamic-update-slice_fusion.4) | copy-start | bytes 3145732
  193.2 1.0 copy-start.6

commit v8 on v7

--- a/solution.py
+++ b/solution.py
@@ -369,9 +369,9 @@
             got[shift] = swap(blocks[shift], "chan", lambda i: i ^ shift)
         return [got[shift] for shift in range(parts)]
 
-    def cut(field):
-        pieces, place = {}, chan
-        for shift in shifts + [0]:
+    def cut(field, order, place):
+        pieces = {}
+        for shift in order:
             start = (place ^ shift) * width
             piece = lax.dynamic_slice_in_dim(field, start, width, axis=2).transpose(1, 0, 2)
             pieces[shift], place = lax.optimization_barrier((piece, place))
@@ -384,12 +384,14 @@
             field = lax.dynamic_update_slice_in_dim(field, piece, (chan ^ shift) * width, axis=2)
         return field
 
-    def gather_column(piece):
+    def gather_column(piece, beside=None):
         column = piece[None]
         for mask in doubling(parts):
+            if mask == 1 and beside is not None:
+                column, beside = lax.optimization_barrier((column, beside))
             got = swap(column, "chan", lambda i: i ^ mask)
             column = jnp.concatenate([column, got])
-        return column
+        return column, beside
 
     def gather_weight(column):
         over_x = swap(column, others, lambda i: i ^ 2)
@@ -414,17 +416,21 @@
         return row_low, row_high, plane_low, plane_high
 
     grid = (planes, rows, CX, channels)
-    pieces = [
+    piece_in, piece_out = (
         lax.dynamic_slice_in_dim(weight, seat * share, share, axis=0)
         for weight in (weight_in, weight_out)
-    ]
-    column = gather_column(jnp.concatenate(pieces))
-    full_in = gather_weight(column[:, :share])
-    full_out = gather_weight(column[:, share:])
+    )
+    column, _ = gather_column(piece_in)
+    vol_cut = cut(volume, shifts, chan)
+    later, column = lax.optimization_barrier((chan, column))
+    own_cut = cut(volume, [0], later)
+    grad_cut = cut(out_grad, shifts + [0], later)
+    full_in = gather_weight(column)
+    column, (own_block, here, grad_cut) = gather_column(piece_out, (own_cut[0], here, grad_cut))
+    full_out = gather_weight(column)
     table = jnp.concatenate([filter_taps, filter_bias[:, None]], axis=1).T
-    taps = gather_column(table)
-    vol_cut, grad_cut = cut(volume), cut(out_grad)
-    own_block, taps, grad_cut = lax.optimization_barrier((vol_cut[0], taps, grad_cut))
+    taps, _ = gather_column(table)
+    own_block, taps = lax.optimization_barrier((own_block, taps))
     vol_blocks = exchange({**vol_cut, 0: own_block})
     grad_blocks = exchange(grad_cut)
     hidden, *edges = product_call(here, vol_blocks, full_in)

time: 195 us -> 192 us (0.985)
  the two profiles are of different devices: /device:TPU:12 before, /device:TPU:0 now
where the time goes in v8:
time: 192 us; the launch traced here: 189 us
  waiting for transfers between devices  74.5 us (39%)
  starting transfers between devices  55.6 us (29%)
  Pallas kernels  37 us (19%)
  local copies, waits for them, and re-layouts  19.2 us (10%)
    ppermute x26, waiting for transfers between devices, swap(): return lax.ppermute(part, axes, [(i, partner(i)) for i in range(count)])  59.7 us
    ppermute x26, starting transfers between devices, swap(): return lax.ppermute(part, axes, [(i, partner(i)) for i in range(count)])  37.5 us
    pallas_call x2, Pallas kernels, stencil(): pl.pallas_call(forward_kernel if forward else backward_kernel, grid_spec=...  22.7 us
    pallas_call x2, Pallas kernels, product_call(): pl.pallas_call(lambda *refs: kernel(*refs, count=count), grid_spec=pltpu....  14.3 us
    ppermute x2, starting transfers between devices, halo_of(): row_low = lax.ppermute(last, 'chan', forward)  9.45 us
    ppermute x2, waiting for transfers between devices, halo_of(): row_low = lax.ppermute(last, 'chan', forward)  7.57 us
    ppermute x2, waiting for transfers between devices, halo_of(): row_high = lax.ppermute(first, 'chan', backward)  7.16 us
    unnamed x51, local copies, waits for them, and re-layouts  7.16 us
  transfers between devices with their start and end apart: 34, of which 17 were waited for; matrix products, arithmetic and copies ran while one was open for 8% of the time, Pallas kernels for 15%

profile of v8, /device:TPU:0, one launch (start us, length us, event | category | flops | bytes accessed | tf_op | source)
XLA Modules:
  0.0 189.1 jit_solution(7585618932617689540)
XLA Ops:
  0.7 0.9 dynamic-slice_bitcast_fusion
  1.6 5.1 %collective-permute-start.1 = (bf16[1,32,1024]{2,1,0:T(8,128)(2,1)S(1)}, bf16[1,32,1024]{2,1,0:T(8,128)(2,1)S(1)}, u32[]{:S(2)}, u32[]{:S(2)}) collective-permute-start(bf16[1,32,1024]{2,1,0:T(8,128)(2,1)S(1)} %dynamic-slice_bitcast_fusion), channel_id=1, source_target_pairs={{0,12},{4,8},{8,4},{12,0},{1,13},{5,9},{9,5},{13,1},{2,14},{6,10},... | collective-permute-start | bytes 196616 | tf_op jit(solution)/shard_map/ppermute | solution.py:364
  6.7 0.8 dynamic-slice_bitcast_fusion.1
  7.5 1.0 constant_dynamic-slice_fusion.2
  8.6 0.7 copy.49
  9.3 1.1 constant_dynamic-slice_fusion.1
  10.5 1.0 collective-permute-start.2
  12.2 0.8 copy.48
  12.9 0.8 collective-permute-done
  13.7 2.5 %collective-permute-done.2 = bf16[2,32,1024]{2,1,0:T(8,128)(2,1)S(1)} collective-permute-done((bf16[2,32,1024]{2,1,0:T(8,128)(2,1)S(1)}, bf16[2,32,1024]{2,1,0:T(8,128)(2,1)S(1)}, u32[]{:S(2)}, u32[]{:S(2)}) %collective-permute-start.2) | collective-permute-done | bytes 131104 | tf_op jit(solution)/shard_map/ppermute | solution.py:364
  16.3 0.8 copy.53
  17.2 0.8 copy.52
  18.0 1.5 collective-permute-start.3
  19.4 1.5 collective-permute-start.4
  21.3 0.7 copy.51
  22.0 0.8 copy_bitcast_fusion
  22.8 2.8 %collective-permute-done.3 = bf16[4,32,1024]{2,1,0:T(8,128)(2,1)S(1)} collective-permute-done((bf16[4,32,1024]{2,1,0:T(8,128)(2,1)S(1)}, bf16[4,32,1024]{2,1,0:T(8,128)(2,1)S(1)}, u32[]{:S(2)}, u32[]{:S(2)}) %collective-permute-start.3) | collective-permute-done | bytes 262176 | tf_op jit(solution)/shard_map/ppermute | solution.py:364
  25.6 1.0 collective-permute-done.4
  26.6 0.8 collective-permute-start.5
  27.6 0.8 copy.50
  28.3 5.0 %collective-permute-done.16 = bf16[2,32,1024]{2,1,0:T(8,128)(2,1)S(1)} collective-permute-done((bf16[2,32,1024]{2,1,0:T(8,128)(2,1)S(1)}, bf16[2,32,1024]{2,1,0:T(8,128)(2,1)S(1)}, u32[]{:S(2)}, u32[]{:S(2)}) %collective-permute-start.16) | collective-permute-done | bytes 131104 | tf_op jit(solution)/shard_map/ppermute | solution.py:364
  33.3 1.3 collective-permute-start.17
  34.6 1.5 collective-permute-start.18
  36.4 3.3 %collective-permute-done.17 = bf16[4,32,1024]{2,1,0:T(8,128)(2,1)S(1)} collective-permute-done((bf16[4,32,1024]{2,1,0:T(8,128)(2,1)S(1)}, bf16[4,32,1024]{2,1,0:T(8,128)(2,1)S(1)}, u32[]{:S(2)}, u32[]{:S(2)}) %collective-permute-start.17) | collective-permute-done | bytes 262176 | tf_op jit(solution)/shard_map/ppermute | solution.py:364
  39.7 2.7 %collective-permute-done.18 = bf16[4,32,1024]{2,1,0:T(8,128)(2,1)S(1)} collective-permute-done((bf16[4,32,1024]{2,1,0:T(8,128)(2,1)S(1)}, bf16[4,32,1024]{2,1,0:T(8,128)(2,1)S(1)}, u32[]{:S(2)}, u32[]{:S(2)}) %collective-permute-start.18) | collective-permute-done | bytes 262176 | tf_op jit(solution)/shard_map/ppermute | solution.py:364
  42.9 3.0 %collective-permute-start.7 = (f32[1,28,256]{2,1,0:T(8,128)S(1)}, f32[1,28,256]{2,1,0:T(8,128)S(1)}, u32[]{:S(2)}, u32[]{:S(2)}) collective-permute-start(f32[1,28,256]{2,1,0:T(8,128)S(1)} %maximum_bitcast_fusion), channel_id=1, source_target_pairs={{0,12},{4,8},{8,4},{12,0},{1,13},{5,9},{9,5},{13,1},{2,14},{6,10},... | collective-permute-start | bytes 86024 | tf_op jit(solution)/shard_map/ppermute | solution.py:364
  45.9 0.9 collective-permute-start.11
  47.1 2.0 %collective-permute-done.7 = f32[1,28,256]{2,1,0:T(8,128)S(1)} collective-permute-done((f32[1,28,256]{2,1,0:T(8,128)S(1)}, f32[1,28,256]{2,1,0:T(8,128)S(1)}, u32[]{:S(2)}, u32[]{:S(2)}) %collective-permute-start.7) | collective-permute-done | bytes 28704 | tf_op jit(solution)/shard_map/ppermute | solution.py:364
  49.1 2.4 %collective-permute-start.8 = (f32[2,28,256]{2,1,0:T(8,128)S(1)}, f32[2,28,256]{2,1,0:T(8,128)S(1)}, u32[]{:S(2)}, u32[]{:S(2)}) collective-permute-start(f32[2,28,256]{2,1,0:T(8,128)S(1)} %pad_maximum_fusion.6), channel_id=1, source_target_pairs={{0,4},{4,0},{8,12},{12,8},{1,5},{5,1},{9,13},{13,9},{2,6},{6,2},{1... | collective-permute-start | bytes 172040 | tf_op jit(solution)/shard_map/ppermute | solution.py:364
  51.7 5.1 %collective-permute-done.8 = f32[2,28,256]{2,1,0:T(8,128)S(1)} collective-permute-done((f32[2,28,256]{2,1,0:T(8,128)S(1)}, f32[2,28,256]{2,1,0:T(8,128)S(1)}, u32[]{:S(2)}, u32[]{:S(2)}) %collective-permute-start.8) | collective-permute-done | bytes 57376 | tf_op jit(solution)/shard_map/ppermute | solution.py:364
  57.5 7.8 %collective-permute-done.10.refs_5_.rest_2_ = bf16[4,256,128]{2,1,0:T(8,128)(2,1)} collective-permute-done((bf16[4,256,128]{2,1,0:T(8,128)(2,1)S(1)}, bf16[4,256,128]{2,1,0:T(8,128)(2,1)}, u32[]{:S(2)}, u32[]{:S(2)}) %collective-permute-start.10) | collective-permute-done | bytes 262176 | tf_op jit(solution)/shard_map/ppermute | solution.py:364
  65.4 6.5 %shard_map.77 = (bf16[512,1024]{1,0:T(8,128)(2,1)}, bf16[4,32,1024]{2,1,0:T(8,128)(2,1)}, bf16[4,32,1024]{2,1,0:T(8,128)(2,1)}, bf16[6,32,1024]{2,1,0:T(8,128)(2,1)}, bf16[6,32,1024]{2,1,0:T(8,128)(2,1)}) custom-call(s32[2]{0:T(128)} %pad_add_fusion.refs_0_.here, bf16[4,4,32,1024]{3,2,1,0:T(8,128)(2,1)} %copy-done.1, ...), custom_call_target="tpu_custom_call" | custom-call | tf_op jit(solution)/shard_map/pallas_call | solution.py:324
  71.9 1.3 collective-permute-start.12
  73.2 1.3 collective-permute-start.13
  74.5 2.9 %collective-permute-done.12.row_low = bf16[4,32,1024]{2,1,0:T(8,128)(2,1)S(1)} collective-permute-done((bf16[4,32,1024]{2,1,0:T(8,128)(2,1)}, bf16[4,32,1024]{2,1,0:T(8,128)(2,1)S(1)}, u32[]{:S(2)}, u32[]{:S(2)}) %collective-permute-start.12) | collective-permute-done | bytes 262176 | tf_op jit(solution)/shard_map/ppermute | solution.py:406
  77.4 0.7 slice_dynamic-update-slice_fusion.5
  78.1 3.6 %collective-permute-done.13.row_high = bf16[4,32,1024]{2,1,0:T(8,128)(2,1)S(1)} collective-permute-done((bf16[4,32,1024]{2,1,0:T(8,128)(2,1)}, bf16[4,32,1024]{2,1,0:T(8,128)(2,1)S(1)}, u32[]{:S(2)}, u32[]{:S(2)}) %collective-permute-start.13) | collective-permute-done | bytes 262176 | tf_op jit(solution)/shard_map/ppermute | solution.py:407
  82.4 2.0 %collective-permute-start.14 = (bf16[6,32,1024]{2,1,0:T(8,128)(2,1)}, bf16[6,32,1024]{2,1,0:T(8,128)(2,1)}, u32[]{:S(2)}, u32[]{:S(2)}) collective-permute-start(bf16[6,32,1024]{2,1,0:T(8,128)(2,1)} %get-tuple-element.105), channel_id=1, source_target_pairs={{0,1},{1,2},{2,3},{4,5},{5,6},{6,7},{8,9},{9,10},{10,11},{12,13},{... | collective-permute-start | bytes 1179656 | tf_op jit(solution)/shard_map/ppermute | solution.py:414
  84.5 1.3 collective-permute-start.15
  85.7 1.8 collective-permute-start.24
  87.5 1.5 collective-permute-start.25
  89.0 1.4 collective-permute-start.26
  90.4 11.7 %shard_map.78 = (bf16[4,256,128]{2,1,0:T(8,128)(2,1)}, bf16[4,256,128]{2,1,0:T(8,128)(2,1)}, bf16[4,256,128]{2,1,0:T(8,128)(2,1)}, bf16[4,256,128]{2,1,0:T(8,128)(2,1)}, f32[4,4,32,1024]{3,2,1,0:T(8,128)}) custom-call(s32[2]{0:T(128)} %pad_add_fusion.refs_0_.here, bf16[4,4,32,1024]{3,2,1,0:T(8,128)(2,1)} %bitcast.56, bf16[4,32,1024]{2,1,0:T(8,128)(2,1)} %copy-done.12, ...), custom_call_target="tpu_custom_call" | custom-call | tf_op jit(solution)/shard_map/pallas_call | solution.py:229
  102.1 6.8 %collective-permute-done.26.refs_6_.rest_3_ = bf16[4,256,128]{2,1,0:T(8,128)(2,1)S(1)} collective-permute-done((bf16[4,256,128]{2,1,0:T(8,128)(2,1)}, bf16[4,256,128]{2,1,0:T(8,128)(2,1)S(1)}, u32[]{:S(2)}, u32[]{:S(2)}) %collective-permute-start.26) | collective-permute-done | bytes 262176 | tf_op jit(solution)/shard_map/ppermute | solution.py:364
  108.9 0.7 copy-done.9
  109.6 7.8 %shard_map.79 = (bf16[512,1024]{1,0:T(8,128)(2,1)}, bf16[4,32,1024]{2,1,0:T(8,128)(2,1)}, bf16[4,32,1024]{2,1,0:T(8,128)(2,1)}, bf16[6,32,1024]{2,1,0:T(8,128)(2,1)}, bf16[6,32,1024]{2,1,0:T(8,128)(2,1)}) custom-call(s32[2]{0:T(128)} %pad_add_fusion.refs_0_.here, bf16[4,4,32,1024]{3,2,1,0:T(8,128)(2,1)} %copy-done.2, ...), custom_call_target="tpu_custom_call" | custom-call | tf_op jit(solution)/shard_map/pallas_call | solution.py:324
  117.4 8.1 %collective-permute-start.27 = (bf16[4,32,1024]{2,1,0:T(8,128)(2,1)}, bf16[4,32,1024]{2,1,0:T(8,128)(2,1)S(1)}, u32[]{:S(2)}, u32[]{:S(2)}) collective-permute-start(bf16[4,32,1024]{2,1,0:T(8,128)(2,1)} %get-tuple-element.85), channel_id=1, source_target_pairs={{0,4},{4,8},{8,12},{1,5},{5,9},{9,13},{2,6},{6,10},{10,14},{3,7},{... | collective-permute-start | bytes 786440 | tf_op jit(solution)/shard_map/ppermute | solution.py:406
  125.6 1.3 collective-permute-start.28
  126.9 4.7 %collective-permute-done.27.row_low = bf16[4,32,1024]{2,1,0:T(8,128)(2,1)S(1)} collective-permute-done((bf16[4,32,1024]{2,1,0:T(8,128)(2,1)}, bf16[4,32,1024]{2,1,0:T(8,128)(2,1)S(1)}, u32[]{:S(2)}, u32[]{:S(2)}) %collective-permute-start.27) | collective-permute-done | bytes 262176 | tf_op jit(solution)/shard_map/ppermute | solution.py:406
  131.6 0.7 slice_dynamic-update-slice_fusion.1
  132.3 3.6 %collective-permute-done.28.row_high = bf16[4,32,1024]{2,1,0:T(8,128)(2,1)S(1)} collective-permute-done((bf16[4,32,1024]{2,1,0:T(8,128)(2,1)}, bf16[4,32,1024]{2,1,0:T(8,128)(2,1)S(1)}, u32[]{:S(2)}, u32[]{:S(2)}) %collective-permute-start.28) | collective-permute-done | bytes 262176 | tf_op jit(solution)/shard_map/ppermute | solution.py:407
  135.9 0.7 slice_dynamic-update-slice_fusion
  136.6 1.3 collective-permute-start.29
  137.9 1.5 collective-permute-start.30
  139.4 1.8 collective-permute-start.21
  141.2 2.7 %collective-permute-start.23 = (bf16[4,256,128]{2,1,0:T(8,128)(2,1)S(1)}, bf16[4,256,128]{2,1,0:T(8,128)(2,1)S(1)}, u32[]{:S(2)}, u32[]{:S(2)}) collective-permute-start(bf16[4,256,128]{2,1,0:T(8,128)(2,1)S(1)} %copy-done.21), channel_id=1, source_target_pairs={{0,12},{4,8},{8,4},{12,0},{1,13},{5,9},{9,5},{13,1},{2,14},{6,10},... | collective-permute-start | bytes 786440 | tf_op jit(solution)/shard_map/ppermute | solution.py:364
  143.9 0.7 copy-done.14
  144.8 11.0 %shard_map.80 = (bf16[4,256,128]{2,1,0:T(8,128)(2,1)}, bf16[4,256,128]{2,1,0:T(8,128)(2,1)}, bf16[4,256,128]{2,1,0:T(8,128)(2,1)}, bf16[4,256,128]{2,1,0:T(8,128)(2,1)}) custom-call(s32[2]{0:T(128)} %pad_add_fusion.refs_0_.here, bf16[4,4,32,1024]{3,2,1,0:T(8,128)(2,1)} %bitcast.55, bf16[4,32,1024]{2,1,0:T(8,128)(2,1)} %copy-done.10, ...), custom_call_target="tpu_custom_call" | custom-call | tf_op jit(solution)/shard_map/pallas_call | solution.py:229
  155.8 7.0 %collective-permute-done.22 = bf16[4,256,128]{2,1,0:T(8,128)(2,1)S(1)} collective-permute-done((bf16[4,256,128]{2,1,0:T(8,128)(2,1)}, bf16[4,256,128]{2,1,0:T(8,128)(2,1)S(1)}, u32[]{:S(2)}, u32[]{:S(2)}) %collective-permute-start.22) | collective-permute-done | bytes 262176 | tf_op jit(solution)/shard_map/ppermute | solution.py:364
  162.8 5.8 %collective-permute-start.31 = (bf16[4,256,128]{2,1,0:T(8,128)(2,1)}, bf16[4,256,128]{2,1,0:T(8,128)(2,1)S(1)}, u32[]{:S(2)}, u32[]{:S(2)}) collective-permute-start(bf16[4,256,128]{2,1,0:T(8,128)(2,1)} %get-tuple-element.95), channel_id=1, source_target_pairs={{0,8},{4,12},{8,0},{12,4},{1,9},{5,13},{9,1},{13,5},{2,10},{6,14},... | collective-permute-start | bytes 786440 | tf_op jit(solution)/shard_map/ppermute | solution.py:364
  168.5 2.6 %collective-permute-start.32 = (bf16[4,256,128]{2,1,0:T(8,128)(2,1)}, bf16[4,256,128]{2,1,0:T(8,128)(2,1)S(1)}, u32[]{:S(2)}, u32[]{:S(2)}) collective-permute-start(bf16[4,256,128]{2,1,0:T(8,128)(2,1)} %get-tuple-element.96), channel_id=1, source_target_pairs={{0,12},{4,8},{8,4},{12,0},{1,13},{5,9},{9,5},{13,1},{2,14},{6,10},... | collective-permute-start | bytes 786440 | tf_op jit(solution)/shard_map/ppermute | solution.py:364
  171.5 1.2 copy_dynamic-update-slice_fusion.3
  174.2 12.9 %collective-permute-done.31 = bf16[4,256,128]{2,1,0:T(8,128)(2,1)S(1)} collective-permute-done((bf16[4,256,128]{2,1,0:T(8,128)(2,1)}, bf16[4,256,128]{2,1,0:T(8,128)(2,1)S(1)}, u32[]{:S(2)}, u32[]{:S(2)}) %collective-permute-start.31) | collective-permute-done | bytes 262176 | tf_op jit(solution)/shard_map/ppermute | solution.py:364
  188.1 1.0 copy-done.5
  (95 shorter events, 6.9 us)
Async XLA Ops:
  0.6 15.6 %copy-start = (bf16[256,4,512]{2,1,0:T(4,128)(2,1)S(1)}, bf16[256,4,512]{2,1,0:T(4,128)(2,1)}, u32[]{:S(2)}) copy-start(bf16[256,4,512]{2,1,0:T(4,128)(2,1)} %param.7) | copy-start | bytes 3145732
  1.6 8.8 %collective-permute-start.1 = (bf16[1,32,1024]{2,1,0:T(8,128)(2,1)S(1)}, bf16[1,32,1024]{2,1,0:T(8,128)(2,1)S(1)}, u32[]{:S(2)}, u32[]{:S(2)}) collective-permute-start(bf16[1,32,1024]{2,1,0:T(8,128)(2,1)S(1)} %dynamic-slice_bitcast_fusion), channel_id=1, source_target_pairs={{0,12},{4,8},{8,4},{12,0},{1,13},{5,9},{9,5},{13,1},{2,14},{6,10},... | collective-permute-start | bytes 196616 | tf_op jit(solution)/shard_map/ppermute | solution.py:364
  7.5 6.2 %collective-permute-start = (bf16[1,32,1024]{2,1,0:T(8,128)(2,1)S(1)}, bf16[1,32,1024]{2,1,0:T(8,128)(2,1)S(1)}, u32[]{:S(2)}, u32[]{:S(2)}) collective-permute-start(bf16[1,32,1024]{2,1,0:T(8,128)(2,1)S(1)} %dynamic-slice_bitcast_fusion.1), channel_id=1, source_target_pairs={{0,12},{4,8},{8,4},{12,0},{1,13},{5,9},{9,5},{13,1},{2,14},{6,10},... | collective-permute-start | bytes 196616 | tf_op jit(solution)/shard_map/ppermute | solution.py:364
  9.3 11.7 %copy-start.3 = (bf16[256,4,512]{2,1,0:T(4,128)(2,1)S(1)}, bf16[256,4,512]{2,1,0:T(4,128)(2,1)}, u32[]{:S(2)}) copy-start(bf16[256,4,512]{2,1,0:T(4,128)(2,1)} %param.6) | copy-start | bytes 3145732
  10.5 5.7 %collective-permute-start.2 = (bf16[2,32,1024]{2,1,0:T(8,128)(2,1)S(1)}, bf16[2,32,1024]{2,1,0:T(8,128)(2,1)S(1)}, u32[]{:S(2)}, u32[]{:S(2)}) collective-permute-start(bf16[2,32,1024]{2,1,0:T(8,128)(2,1)S(1)} %pad_maximum_fusion.4), channel_id=1, source_target_pairs={{0,4},{4,0},{8,12},{12,8},{1,5},{5,1},{9,13},{13,9},{2,6},{6,2},{1... | collective-permute-start | bytes 393224 | tf_op jit(solution)/shard_map/ppermute | solution.py:364
  18.0 7.6 %collective-permute-start.3 = (bf16[4,32,1024]{2,1,0:T(8,128)(2,1)S(1)}, bf16[4,32,1024]{2,1,0:T(8,128)(2,1)S(1)}, u32[]{:S(2)}, u32[]{:S(2)}) collective-permute-start(bf16[4,32,1024]{2,1,0:T(8,128)(2,1)S(1)} %pad_maximum_fusion.2), channel_id=1, source_target_pairs={{0,2},{1,3},{2,0},{3,1},{16,18},{17,19},{18,16},{19,17},{4,6},{5,7... | collective-permute-start | bytes 786440 | tf_op jit(solution)/shard_map/ppermute | solution.py:364
  19.4 7.1 %collective-permute-start.4 = (bf16[4,32,1024]{2,1,0:T(8,128)(2,1)S(1)}, bf16[4,32,1024]{2,1,0:T(8,128)(2,1)S(1)}, u32[]{:S(2)}, u32[]{:S(2)}) collective-permute-start(bf16[4,32,1024]{2,1,0:T(8,128)(2,1)S(1)} %pad_maximum_fusion.2), channel_id=1, source_target_pairs={{0,16},{1,17},{2,18},{3,19},{16,0},{17,1},{18,2},{19,3},{4,20},{5,... | collective-permute-start | bytes 786440 | tf_op jit(solution)/shard_map/ppermute | solution.py:364
  26.6 9.6 %collective-permute-start.5 = (bf16[4,32,1024]{2,1,0:T(8,128)(2,1)S(1)}, bf16[4,32,1024]{2,1,0:T(8,128)(2,1)S(1)}, u32[]{:S(2)}, u32[]{:S(2)}) collective-permute-start(bf16[4,32,1024]{2,1,0:T(8,128)(2,1)S(1)} %broadcast_select_fusion.1), channel_id=1, source_target_pairs={{0,2},{1,17},{2,0},{3,19},{16,18},{17,1},{18,16},{19,3},{4,6},{5,2... | collective-permute-start | bytes 786440 | tf_op jit(solution)/shard_map/ppermute | solution.py:364
  27.5 15.4 %copy-start.19 = (f32[256,27]{0,1:T(8,128)S(1)}, f32[256,27]{0,1:T(8,128)}, u32[]{:S(2)}) copy-start(f32[256,27]{0,1:T(8,128)} %param.10) | copy-start | bytes 82948
  27.5 15.4 %copy-start.20 = (f32[256]{0:T(256)S(1)}, f32[256]{0:T(256)}, u32[]{:S(2)}) copy-start(f32[256]{0:T(256)} %param.11) | copy-start | bytes 3076
  27.5 18.4 %copy-start.18 = (bf16[256,4,128]{2,0,1:T(8,128)(2,1)S(1)}, bf16[256,4,128]{2,0,1:T(8,128)(2,1)}, u32[]{:S(2)}) copy-start(bf16[256,4,128]{2,0,1:T(8,128)(2,1)} %copy.48) | copy-start | bytes 786436
  27.5 19.3 %copy-start.17 = (bf16[256,4,128]{2,0,1:T(8,128)(2,1)S(1)}, bf16[256,4,128]{2,0,1:T(8,128)(2,1)}, u32[]{:S(2)}) copy-start(bf16[256,4,128]{2,0,1:T(8,128)(2,1)} %copy.49) | copy-start | bytes 786436
  28.3 5.0 %collective-permute-start.16 = (bf16[2,32,1024]{2,1,0:T(8,128)(2,1)S(1)}, bf16[2,32,1024]{2,1,0:T(8,128)(2,1)S(1)}, u32[]{:S(2)}, u32[]{:S(2)}) collective-permute-start(bf16[2,32,1024]{2,1,0:T(8,128)(2,1)S(1)} %pad_maximum_fusion.3), channel_id=1, source_target_pairs={{0,4},{4,0},{8,12},{12,8},{1,5},{5,1},{9,13},{13,9},{2,6},{6,2},{1... | collective-permute-start | bytes 393224 | tf_op jit(solution)/shard_map/ppermute | solution.py:364
  33.3 6.4 %collective-permute-start.17 = (bf16[4,32,1024]{2,1,0:T(8,128)(2,1)S(1)}, bf16[4,32,1024]{2,1,0:T(8,128)(2,1)S(1)}, u32[]{:S(2)}, u32[]{:S(2)}) collective-permute-start(bf16[4,32,1024]{2,1,0:T(8,128)(2,1)S(1)} %constant_dynamic-update-slice_fusion), channel_id=1, source_target_pairs={{0,2},{1,3},{2,0},{3,1},{16,18},{17,19},{18,16},{19,17},{4,6},{5,7... | collective-permute-start | bytes 786440 | tf_op jit(solution)/shard_map/ppermute | solution.py:364
  34.6 7.8 %collective-permute-start.18 = (bf16[4,32,1024]{2,1,0:T(8,128)(2,1)S(1)}, bf16[4,32,1024]{2,1,0:T(8,128)(2,1)S(1)}, u32[]{:S(2)}, u32[]{:S(2)}) collective-permute-start(bf16[4,32,1024]{2,1,0:T(8,128)(2,1)S(1)} %constant_dynamic-update-slice_fusion), channel_id=1, source_target_pairs={{0,16},{1,17},{2,18},{3,19},{16,0},{17,1},{18,2},{19,3},{4,20},{5,... | collective-permute-start | bytes 786440 | tf_op jit(solution)/shard_map/ppermute | solution.py:364
  36.3 29.1 %copy-start.1 = (bf16[4,4,32,1024]{3,2,1,0:T(8,128)(2,1)}, bf16[4,4,32,1024]{3,2,1,0:T(8,128)(2,1)S(1)}, u32[]{:S(2)}) copy-start(bf16[4,4,32,1024]{3,2,1,0:T(8,128)(2,1)S(1)} %pad_maximum_fusion.refs_1_.mine) | copy-start | bytes 3145732
  36.3 29.1 %collective-permute-start.6 = (bf16[4,4,32,1024]{3,2,1,0:T(8,128)(2,1)S(1)}, bf16[4,4,32,1024]{3,2,1,0:T(8,128)(2,1)}, u32[]{:S(2)}, u32[]{:S(2)}) collective-permute-start(bf16[4,4,32,1024]{3,2,1,0:T(8,128)(2,1)S(1)} %pad_maximum_fusion.refs_1_.mine), channel_id=1, source_target_pairs={{0,1},{1,0},{2,3},{3,2},{16,17},{17,16},{18,19},{19,18},{4,5},{5,4... | collective-permute-start | bytes 3145736 | tf_op jit(solution)/shard_map/ppermute | solution.py:364
  42.5 9.0 %collective-permute-start.19 = (bf16[4,32,1024]{2,1,0:T(8,128)(2,1)S(1)}, bf16[4,32,1024]{2,1,0:T(8,128)(2,1)S(1)}, u32[]{:S(2)}, u32[]{:S(2)}) collective-permute-start(bf16[4,32,1024]{2,1,0:T(8,128)(2,1)S(1)} %broadcast_select_fusion), channel_id=1, source_target_pairs={{0,2},{1,17},{2,0},{3,19},{16,18},{17,1},{18,16},{19,3},{4,6},{5,2... | collective-permute-start | bytes 786440 | tf_op jit(solution)/shard_map/ppermute | solution.py:364
  42.9 6.2 %collective-permute-start.7 = (f32[1,28,256]{2,1,0:T(8,128)S(1)}, f32[1,28,256]{2,1,0:T(8,128)S(1)}, u32[]{:S(2)}, u32[]{:S(2)}) collective-permute-start(f32[1,28,256]{2,1,0:T(8,128)S(1)} %maximum_bitcast_fusion), channel_id=1, source_target_pairs={{0,12},{4,8},{8,4},{12,0},{1,13},{5,9},{9,5},{13,1},{2,14},{6,10},... | collective-permute-start | bytes 86024 | tf_op jit(solution)/shard_map/ppermute | solution.py:364
  45.9 11.6 %collective-permute-start.11 = (bf16[4,256,128]{2,1,0:T(8,128)(2,1)S(1)}, bf16[4,256,128]{2,1,0:T(8,128)(2,1)S(1)}, u32[]{:S(2)}, u32[]{:S(2)}) collective-permute-start(bf16[4,256,128]{2,1,0:T(8,128)(2,1)S(1)} %bitcast.75), channel_id=1, source_target_pairs={{0,12},{4,8},{8,4},{12,0},{1,13},{5,9},{9,5},{13,1},{2,14},{6,10},... | collective-permute-start | bytes 786440 | tf_op jit(solution)/shard_map/ppermute | solution.py:364
  46.8 18.6 %collective-permute-start.10 = (bf16[4,256,128]{2,1,0:T(8,128)(2,1)S(1)}, bf16[4,256,128]{2,1,0:T(8,128)(2,1)}, u32[]{:S(2)}, u32[]{:S(2)}) collective-permute-start(bf16[4,256,128]{2,1,0:T(8,128)(2,1)S(1)} %bitcast.73), channel_id=1, source_target_pairs={{0,8},{4,12},{8,0},{12,4},{1,9},{5,13},{9,1},{13,5},{2,10},{6,14},... | collective-permute-start | bytes 786440 | tf_op jit(solution)/shard_map/ppermute | solution.py:364
  49.1 7.7 %collective-permute-start.8 = (f32[2,28,256]{2,1,0:T(8,128)S(1)}, f32[2,28,256]{2,1,0:T(8,128)S(1)}, u32[]{:S(2)}, u32[]{:S(2)}) collective-permute-start(f32[2,28,256]{2,1,0:T(8,128)S(1)} %pad_maximum_fusion.6), channel_id=1, source_target_pairs={{0,4},{4,0},{8,12},{12,8},{1,5},{5,1},{9,13},{13,9},{2,6},{6,2},{1... | collective-permute-start | bytes 172040 | tf_op jit(solution)/shard_map/ppermute | solution.py:364
  51.5 13.9 %collective-permute-start.9 = (bf16[4,256,128]{2,1,0:T(8,128)(2,1)S(1)}, bf16[4,256,128]{2,1,0:T(8,128)(2,1)}, u32[]{:S(2)}, u32[]{:S(2)}) collective-permute-start(bf16[4,256,128]{2,1,0:T(8,128)(2,1)S(1)} %get-tuple-element.65), channel_id=1, source_target_pairs={{0,4},{4,0},{8,12},{12,8},{1,5},{5,1},{9,13},{13,9},{2,6},{6,2},{1... | collective-permute-start | bytes 786440 | tf_op jit(solution)/shard_map/ppermute | solution.py:364
  51.7 38.7 %copy-start.2 = (bf16[4,4,32,1024]{3,2,1,0:T(8,128)(2,1)}, bf16[4,4,32,1024]{3,2,1,0:T(8,128)(2,1)S(1)}, u32[]{:S(2)}) copy-start(bf16[4,4,32,1024]{3,2,1,0:T(8,128)(2,1)S(1)} %pad_maximum_fusion.1.mine.refs_1_) | copy-start | bytes 3145732
  56.9 32.1 %collective-permute-start.20 = (bf16[4,4,32,1024]{3,2,1,0:T(8,128)(2,1)S(1)}, bf16[4,4,32,1024]{3,2,1,0:T(8,128)(2,1)}, u32[]{:S(2)}, u32[]{:S(2)}) collective-permute-start(bf16[4,4,32,1024]{3,2,1,0:T(8,128)(2,1)S(1)} %pad_maximum_fusion.1.mine.refs_1_), channel_id=1, source_target_pairs={{0,1},{1,0},{2,3},{3,2},{16,17},{17,16},{18,19},{19,18},{4,5},{5,4... | collective-permute-start | bytes 3145736 | tf_op jit(solution)/shard_map/ppermute | solution.py:364
  57.5 7.9 %copy-start.6 = (bf16[4,256,128]{2,1,0:T(8,128)(2,1)}, bf16[4,256,128]{2,1,0:T(8,128)(2,1)S(1)}, u32[]{:S(2)}) copy-start(bf16[4,256,128]{2,1,0:T(8,128)(2,1)S(1)} %collective-permute-done.11.refs_6_.rest_3_) | copy-start | bytes 786436
  71.9 5.5 %collective-permute-start.12 = (bf16[4,32,1024]{2,1,0:T(8,128)(2,1)}, bf16[4,32,1024]{2,1,0:T(8,128)(2,1)S(1)}, u32[]{:S(2)}, u32[]{:S(2)}) collective-permute-start(bf16[4,32,1024]{2,1,0:T(8,128)(2,1)} %get-tuple-element.69), channel_id=1, source_target_pairs={{0,4},{4,8},{8,12},{1,5},{5,9},{9,13},{2,6},{6,10},{10,14},{3,7},{... | collective-permute-start | bytes 786440 | tf_op jit(solution)/shard_map/ppermute | solution.py:406
  73.2 8.5 %collective-permute-start.13 = (bf16[4,32,1024]{2,1,0:T(8,128)(2,1)}, bf16[4,32,1024]{2,1,0:T(8,128)(2,1)S(1)}, u32[]{:S(2)}, u32[]{:S(2)}) collective-permute-start(bf16[4,32,1024]{2,1,0:T(8,128)(2,1)} %get-tuple-element.70), channel_id=1, source_target_pairs={{4,0},{8,4},{12,8},{5,1},{9,5},{13,9},{6,2},{10,6},{14,10},{7,3},{... | collective-permute-start | bytes 786440 | tf_op jit(solution)/shard_map/ppermute | solution.py:407
  77.4 13.0 %copy-start.12 = (bf16[4,32,1024]{2,1,0:T(8,128)(2,1)}, bf16[4,32,1024]{2,1,0:T(8,128)(2,1)S(1)}, u32[]{:S(2)}) copy-start(bf16[4,32,1024]{2,1,0:T(8,128)(2,1)S(1)} %collective-permute-done.12.row_low) | copy-start | bytes 786436
  81.7 8.7 %copy-start.13 = (bf16[4,32,1024]{2,1,0:T(8,128)(2,1)}, bf16[4,32,1024]{2,1,0:T(8,128)(2,1)S(1)}, u32[]{:S(2)}) copy-start(bf16[4,32,1024]{2,1,0:T(8,128)(2,1)S(1)} %collective-permute-done.13.row_high) | copy-start | bytes 786436
  82.4 8.0 %collective-permute-start.14 = (bf16[6,32,1024]{2,1,0:T(8,128)(2,1)}, bf16[6,32,1024]{2,1,0:T(8,128)(2,1)}, u32[]{:S(2)}, u32[]{:S(2)}) collective-permute-start(bf16[6,32,1024]{2,1,0:T(8,128)(2,1)} %get-tuple-element.105), channel_id=1, source_target_pairs={{0,1},{1,2},{2,3},{4,5},{5,6},{6,7},{8,9},{9,10},{10,11},{12,13},{... | collective-permute-start | bytes 1179656 | tf_op jit(solution)/shard_map/ppermute | solution.py:414
  84.5 5.9 %collective-permute-start.15 = (bf16[6,32,1024]{2,1,0:T(8,128)(2,1)}, bf16[6,32,1024]{2,1,0:T(8,128)(2,1)}, u32[]{:S(2)}, u32[]{:S(2)}) collective-permute-start(bf16[6,32,1024]{2,1,0:T(8,128)(2,1)} %get-tuple-element.104), channel_id=1, source_target_pairs={{1,0},{2,1},{3,2},{5,4},{6,5},{7,6},{9,8},{10,9},{11,10},{13,12},{... | collective-permute-start | bytes 1179656 | tf_op jit(solution)/shard_map/ppermute | solution.py:415
  85.7 16.4 %collective-permute-start.24 = (bf16[4,256,128]{2,1,0:T(8,128)(2,1)}, bf16[4,256,128]{2,1,0:T(8,128)(2,1)S(1)}, u32[]{:S(2)}, u32[]{:S(2)}) collective-permute-start(bf16[4,256,128]{2,1,0:T(8,128)(2,1)} %bitcast.74), channel_id=1, source_target_pairs={{0,4},{4,0},{8,12},{12,8},{1,5},{5,1},{9,13},{13,9},{2,6},{6,2},{1... | collective-permute-start | bytes 786440 | tf_op jit(solution)/shard_map/ppermute | solution.py:364
  87.5 14.6 %collective-permute-start.25 = (bf16[4,256,128]{2,1,0:T(8,128)(2,1)}, bf16[4,256,128]{2,1,0:T(8,128)(2,1)S(1)}, u32[]{:S(2)}, u32[]{:S(2)}) collective-permute-start(bf16[4,256,128]{2,1,0:T(8,128)(2,1)} %bitcast.71), channel_id=1, source_target_pairs={{0,8},{4,12},{8,0},{12,4},{1,9},{5,13},{9,1},{13,5},{2,10},{6,14},... | collective-permute-start | bytes 786440 | tf_op jit(solution)/shard_map/ppermute | solution.py:364
  89.0 19.9 %collective-permute-start.26 = (bf16[4,256,128]{2,1,0:T(8,128)(2,1)}, bf16[4,256,128]{2,1,0:T(8,128)(2,1)S(1)}, u32[]{:S(2)}, u32[]{:S(2)}) collective-permute-start(bf16[4,256,128]{2,1,0:T(8,128)(2,1)} %bitcast.72), channel_id=1, source_target_pairs={{0,12},{4,8},{8,4},{12,0},{1,13},{5,9},{9,5},{13,1},{2,14},{6,10},... | collective-permute-start | bytes 786440 | tf_op jit(solution)/shard_map/ppermute | solution.py:364
  102.1 6.8 %copy-start.7 = (bf16[4,256,128]{2,1,0:T(8,128)(2,1)}, bf16[4,256,128]{2,1,0:T(8,128)(2,1)S(1)}, u32[]{:S(2)}) copy-start(bf16[4,256,128]{2,1,0:T(8,128)(2,1)S(1)} %collective-permute-done.24.refs_4_.rest_1_) | copy-start | bytes 786436
  102.1 6.8 %copy-start.8 = (bf16[4,256,128]{2,1,0:T(8,128)(2,1)}, bf16[4,256,128]{2,1,0:T(8,128)(2,1)S(1)}, u32[]{:S(2)}) copy-start(bf16[4,256,128]{2,1,0:T(8,128)(2,1)S(1)} %collective-permute-done.25.refs_5_.rest_2_) | copy-start | bytes 786436
  108.9 0.7 copy-start.9
  109.6 31.6 %copy-start.21 = (bf16[4,256,128]{2,1,0:T(8,128)(2,1)S(1)}, bf16[4,256,128]{2,1,0:T(8,128)(2,1)}, u32[]{:S(2)}) copy-start(bf16[4,256,128]{2,1,0:T(8,128)(2,1)} %get-tuple-element.78) | copy-start | bytes 786436
  117.4 14.2 %collective-permute-start.27 = (bf16[4,32,1024]{2,1,0:T(8,128)(2,1)}, bf16[4,32,1024]{2,1,0:T(8,128)(2,1)S(1)}, u32[]{:S(2)}, u32[]{:S(2)}) collective-permute-start(bf16[4,32,1024]{2,1,0:T(8,128)(2,1)} %get-tuple-element.85), channel_id=1, source_target_pairs={{0,4},{4,8},{8,12},{1,5},{5,9},{9,13},{2,6},{6,10},{10,14},{3,7},{... | collective-permute-start | bytes 786440 | tf_op jit(solution)/shard_map/ppermute | solution.py:406
  125.6 10.3 %collective-permute-start.28 = (bf16[4,32,1024]{2,1,0:T(8,128)(2,1)}, bf16[4,32,1024]{2,1,0:T(8,128)(2,1)S(1)}, u32[]{:S(2)}, u32[]{:S(2)}) collective-permute-start(bf16[4,32,1024]{2,1,0:T(8,128)(2,1)} %get-tuple-element.86), channel_id=1, source_target_pairs={{4,0},{8,4},{12,8},{5,1},{9,5},{13,9},{6,2},{10,6},{14,10},{7,3},{... | collective-permute-start | bytes 786440 | tf_op jit(solution)/shard_map/ppermute | solution.py:407
  131.6 12.3 %copy-start.10 = (bf16[4,32,1024]{2,1,0:T(8,128)(2,1)}, bf16[4,32,1024]{2,1,0:T(8,128)(2,1)S(1)}, u32[]{:S(2)}) copy-start(bf16[4,32,1024]{2,1,0:T(8,128)(2,1)S(1)} %collective-permute-done.27.row_low) | copy-start | bytes 786436
  135.9 8.0 %copy-start.11 = (bf16[4,32,1024]{2,1,0:T(8,128)(2,1)}, bf16[4,32,1024]{2,1,0:T(8,128)(2,1)S(1)}, u32[]{:S(2)}) copy-start(bf16[4,32,1024]{2,1,0:T(8,128)(2,1)S(1)} %collective-permute-done.28.row_high) | copy-start | bytes 786436
  136.6 7.2 %collective-permute-start.29 = (bf16[6,32,1024]{2,1,0:T(8,128)(2,1)}, bf16[6,32,1024]{2,1,0:T(8,128)(2,1)S(1)}, u32[]{:S(2)}, u32[]{:S(2)}) collective-permute-start(bf16[6,32,1024]{2,1,0:T(8,128)(2,1)} %get-tuple-element.101), channel_id=1, source_target_pairs={{0,1},{1,2},{2,3},{4,5},{5,6},{6,7},{8,9},{9,10},{10,11},{12,13},{... | collective-permute-start | bytes 1179656 | tf_op jit(solution)/shard_map/ppermute | solution.py:414
  137.9 5.9 %collective-permute-start.30 = (bf16[6,32,1024]{2,1,0:T(8,128)(2,1)}, bf16[6,32,1024]{2,1,0:T(8,128)(2,1)S(1)}, u32[]{:S(2)}, u32[]{:S(2)}) collective-permute-start(bf16[6,32,1024]{2,1,0:T(8,128)(2,1)} %get-tuple-element.100), channel_id=1, source_target_pairs={{1,0},{2,1},{3,2},{5,4},{6,5},{7,6},{9,8},{10,9},{11,10},{13,12},{... | collective-permute-start | bytes 1179656 | tf_op jit(solution)/shard_map/ppermute | solution.py:415
  139.4 16.4 %collective-permute-start.21 = (bf16[4,256,128]{2,1,0:T(8,128)(2,1)}, bf16[4,256,128]{2,1,0:T(8,128)(2,1)S(1)}, u32[]{:S(2)}, u32[]{:S(2)}) collective-permute-start(bf16[4,256,128]{2,1,0:T(8,128)(2,1)} %get-tuple-element.76), channel_id=1, source_target_pairs={{0,4},{4,0},{8,12},{12,8},{1,5},{5,1},{9,13},{13,9},{2,6},{6,2},{1... | collective-permute-start | bytes 786440 | tf_op jit(solution)/shard_map/ppermute | solution.py:364
  141.2 21.6 %collective-permute-start.22 = (bf16[4,256,128]{2,1,0:T(8,128)(2,1)}, bf16[4,256,128]{2,1,0:T(8,128)(2,1)S(1)}, u32[]{:S(2)}, u32[]{:S(2)}) collective-permute-start(bf16[4,256,128]{2,1,0:T(8,128)(2,1)} %get-tuple-element.77), channel_id=1, source_target_pairs={{0,8},{4,12},{8,0},{12,4},{1,9},{5,13},{9,1},{13,5},{2,10},{6,14},... | collective-permute-start | bytes 786440 | tf_op jit(solution)/shard_map/ppermute | solution.py:364
  141.2 21.6 %collective-permute-start.23 = (bf16[4,256,128]{2,1,0:T(8,128)(2,1)S(1)}, bf16[4,256,128]{2,1,0:T(8,128)(2,1)S(1)}, u32[]{:S(2)}, u32[]{:S(2)}) collective-permute-start(bf16[4,256,128]{2,1,0:T(8,128)(2,1)S(1)} %copy-done.21), channel_id=1, source_target_pairs={{0,12},{4,8},{8,4},{12,0},{1,13},{5,9},{9,5},{13,1},{2,14},{6,10},... | collective-permute-start | bytes 786440 | tf_op jit(solution)/shard_map/ppermute | solution.py:364
  143.8 0.8 copy-start.14
  143.8 0.9 copy-start.15
  155.8 17.2 %copy-start.16 = (bf16[4,256,128]{2,1,0:T(8,128)(2,1)S(1)}, bf16[4,256,128]{2,1,0:T(8,128)(2,1)}, u32[]{:S(2)}) copy-start(bf16[4,256,128]{2,1,0:T(8,128)(2,1)} %get-tuple-element.90) | copy-start | bytes 786436
  162.8 24.4 %collective-permute-start.31 = (bf16[4,256,128]{2,1,0:T(8,128)(2,1)}, bf16[4,256,128]{2,1,0:T(8,128)(2,1)S(1)}, u32[]{:S(2)}, u32[]{:S(2)}) collective-permute-start(bf16[4,256,128]{2,1,0:T(8,128)(2,1)} %get-tuple-element.95), channel_id=1, source_target_pairs={{0,8},{4,12},{8,0},{12,4},{1,9},{5,13},{9,1},{13,5},{2,10},{6,14},... | collective-permute-start | bytes 786440 | tf_op jit(solution)/shard_map/ppermute | solution.py:364
  168.5 18.9 %collective-permute-start.32 = (bf16[4,256,128]{2,1,0:T(8,128)(2,1)}, bf16[4,256,128]{2,1,0:T(8,128)(2,1)S(1)}, u32[]{:S(2)}, u32[]{:S(2)}) collective-permute-start(bf16[4,256,128]{2,1,0:T(8,128)(2,1)} %get-tuple-element.96), channel_id=1, source_target_pairs={{0,12},{4,8},{8,4},{12,0},{1,13},{5,9},{9,5},{13,1},{2,14},{6,10},... | collective-permute-start | bytes 786440 | tf_op jit(solution)/shard_map/ppermute | solution.py:364
  171.2 16.6 %collective-permute-start.33 = (bf16[4,256,128]{2,1,0:T(8,128)(2,1)}, bf16[4,256,128]{2,1,0:T(8,128)(2,1)S(1)}, u32[]{:S(2)}, u32[]{:S(2)}) collective-permute-start(bf16[4,256,128]{2,1,0:T(8,128)(2,1)} %get-tuple-element.97), channel_id=1, source_target_pairs={{0,4},{4,0},{8,12},{12,8},{1,5},{5,1},{9,13},{13,9},{2,6},{6,2},{1... | collective-permute-start | bytes 786440 | tf_op jit(solution)/shard_map/ppermute | solution.py:364
  174.2 13.9 %copy-start.4 = (bf16[256,4,512]{2,1,0:T(4,128)(2,1)}, bf16[256,4,512]{2,1,0:T(4,128)(2,1)S(1)}, u32[]{:S(2)}) copy-start(bf16[256,4,512]{2,1,0:T(4,128)(2,1)S(1)} %copy_dynamic-update-slice_fusion.4) | copy-start | bytes 3145732
  188.1 1.0 copy-start.5

commit v9 on v8

--- a/solution.py
+++ b/solution.py
@@ -384,22 +384,21 @@
             field = lax.dynamic_update_slice_in_dim(field, piece, (chan ^ shift) * width, axis=2)
         return field
 
-    def gather_column(piece, beside=None):
+    def gather_column(piece):
         column = piece[None]
         for mask in doubling(parts):
-            if mask == 1 and beside is not None:
-                column, beside = lax.optimization_barrier((column, beside))
             got = swap(column, "chan", lambda i: i ^ mask)
             column = jnp.concatenate([column, got])
-        return column, beside
-
-    def gather_weight(column):
+        return column
+
+    def gather_weight(column, beside=None):
         over_x = swap(column, others, lambda i: i ^ 2)
         over_y = swap(column, others, lambda i: i ^ 4)
         mixed = jnp.where(seat & 1 == 0, over_y, over_x)
+        mixed, beside = lax.optimization_barrier((mixed, beside))
         far = swap(mixed, others, lambda i: i ^ (4 if i & 1 else 2))
         mine = jnp.stack([column, over_x, over_y, far])
-        return mine, swap(mine, others, lambda i: i ^ 1)
+        return (mine, swap(mine, others, lambda i: i ^ 1)), beside
 
     def halo_of(first, last, fore, back):
         forward, backward = shift_pairs("chan")
@@ -420,16 +419,15 @@
         lax.dynamic_slice_in_dim(weight, seat * share, share, axis=0)
         for weight in (weight_in, weight_out)
     )
-    column, _ = gather_column(piece_in)
+    column = gather_column(piece_in)
     vol_cut = cut(volume, shifts, chan)
     later, column = lax.optimization_barrier((chan, column))
     own_cut = cut(volume, [0], later)
     grad_cut = cut(out_grad, shifts + [0], later)
-    full_in = gather_weight(column)
-    column, (own_block, here, grad_cut) = gather_column(piece_out, (own_cut[0], here, grad_cut))
-    full_out = gather_weight(column)
+    full_in, (own_block, here, grad_cut) = gather_weight(column, (own_cut[0], here, grad_cut))
+    full_out, _ = gather_weight(gather_column(piece_out))
     table = jnp.concatenate([filter_taps, filter_bias[:, None]], axis=1).T
-    taps, _ = gather_column(table)
+    taps = gather_column(table)
     own_block, taps = lax.optimization_barrier((own_block, taps))
     vol_blocks = exchange({**vol_cut, 0: own_block})
     grad_blocks = exchange(grad_cut)

time: 192 us -> 193 us (level)
    ppermute x26, waiting for transfers between devices: 59.7 us -> 57.8 us  [swap(): return lax.ppermute(part, axes, [(i, partner(i)) for i in range(count)])]
    unnamed x51 -> x50, local copies, waits for them, and re-layouts: 7.16 us -> 7.18 us
  transfers between devices with their start and end apart: 34 -> 34, of which waited for: 17 -> 17; matrix products, arithmetic and copies ran while one was open for 8% -> 9% of each run, Pallas kernels for 15% -> 15%
where the time goes in v9:
time: 193 us; the launch traced here: 189 us
  waiting for transfers between devices  73.8 us (38%)
  starting transfers between devices  56.6 us (29%)
  Pallas kernels  37 us (19%)
  local copies, waits for them, and re-layouts  19.2 us (10%)
    ppermute x26, waiting for transfers between devices, swap(): return lax.ppermute(part, axes, [(i, partner(i)) for i in range(count)])  57.8 us
    ppermute x26, starting transfers between devices, swap(): return lax.ppermute(part, axes, [(i, partner(i)) for i in range(count)])  37.9 us
    pallas_call x2, Pallas kernels, stencil(): pl.pallas_call(forward_kernel if forward else backward_kernel, grid_spec=...  22.7 us
    pallas_call x2, Pallas kernels, product_call(): pl.pallas_call(lambda *refs: kernel(*refs, count=count), grid_spec=pltpu....  14.3 us
    ppermute x2, starting transfers between devices, halo_of(): row_low = lax.ppermute(last, 'chan', forward)  9.53 us
    ppermute x2, waiting for transfers between devices, halo_of(): row_low = lax.ppermute(last, 'chan', forward)  9.12 us
    unnamed x50, local copies, waits for them, and re-layouts  7.18 us
    ppermute x2, waiting for transfers between devices, halo_of(): row_high = lax.ppermute(first, 'chan', backward)  6.89 us
  transfers between devices with their start and end apart: 34, of which 17 were waited for; matrix products, arithmetic and copies ran while one was open for 9% of the time, Pallas kernels for 15%

profile of v9, /device:TPU:0, one launch (start us, length us, event | category | flops | bytes accessed | tf_op | source)
XLA Modules:
  0.0 189.4 jit_solution(14285539122625906646)
XLA Ops:
  0.7 0.9 dynamic-slice_bitcast_fusion.1
  1.6 5.1 %collective-permute-start = (bf16[1,32,1024]{2,1,0:T(8,128)(2,1)S(1)}, bf16[1,32,1024]{2,1,0:T(8,128)(2,1)S(1)}, u32[]{:S(2)}, u32[]{:S(2)}) collective-permute-start(bf16[1,32,1024]{2,1,0:T(8,128)(2,1)S(1)} %dynamic-slice_bitcast_fusion.1), channel_id=1, source_target_pairs={{0,12},{4,8},{8,4},{12,0},{1,13},{5,9},{9,5},{13,1},{2,14},{6,10},... | collective-permute-start | bytes 196616 | tf_op jit(solution)/shard_map/ppermute | solution.py:364
  6.7 0.8 dynamic-slice_bitcast_fusion
  7.5 1.0 constant_dynamic-slice_fusion.2
  8.6 0.7 copy.49
  9.3 2.1 %collective-permute-start.1 = (bf16[2,32,1024]{2,1,0:T(8,128)(2,1)S(1)}, bf16[2,32,1024]{2,1,0:T(8,128)(2,1)S(1)}, u32[]{:S(2)}, u32[]{:S(2)}) collective-permute-start(bf16[2,32,1024]{2,1,0:T(8,128)(2,1)S(1)} %pad_maximum_fusion.4), channel_id=1, source_target_pairs={{0,4},{4,0},{8,12},{12,8},{1,5},{5,1},{9,13},{13,9},{2,6},{6,2},{1... | collective-permute-start | bytes 393224 | tf_op jit(solution)/shard_map/ppermute | solution.py:364
  11.5 1.0 constant_dynamic-slice_fusion.1
  12.5 0.8 copy.48
  13.9 1.8 collective-permute-done.1
  15.8 0.8 copy.53
  16.7 0.8 copy.52
  17.5 0.7 copy.51
  18.3 1.5 collective-permute-start.2
  19.8 1.5 collective-permute-start.3
  21.6 0.8 copy.50
  22.4 0.8 copy_bitcast_fusion
  23.2 2.7 %collective-permute-done.2 = bf16[4,32,1024]{2,1,0:T(8,128)(2,1)S(1)} collective-permute-done((bf16[4,32,1024]{2,1,0:T(8,128)(2,1)S(1)}, bf16[4,32,1024]{2,1,0:T(8,128)(2,1)S(1)}, u32[]{:S(2)}, u32[]{:S(2)}) %collective-permute-start.2) | collective-permute-done | bytes 262176 | tf_op jit(solution)/shard_map/ppermute | solution.py:364
  25.8 1.2 collective-permute-done.3
  27.1 1.6 collective-permute-start.4
  28.8 5.0 %collective-permute-done.16 = bf16[2,32,1024]{2,1,0:T(8,128)(2,1)S(1)} collective-permute-done((bf16[2,32,1024]{2,1,0:T(8,128)(2,1)S(1)}, bf16[2,32,1024]{2,1,0:T(8,128)(2,1)S(1)}, u32[]{:S(2)}, u32[]{:S(2)}) %collective-permute-start.16) | collective-permute-done | bytes 131104 | tf_op jit(solution)/shard_map/ppermute | solution.py:364
  35.1 5.1 %collective-permute-done.17 = bf16[4,32,1024]{2,1,0:T(8,128)(2,1)S(1)} collective-permute-done((bf16[4,32,1024]{2,1,0:T(8,128)(2,1)S(1)}, bf16[4,32,1024]{2,1,0:T(8,128)(2,1)S(1)}, u32[]{:S(2)}, u32[]{:S(2)}) %collective-permute-start.17) | collective-permute-done | bytes 262176 | tf_op jit(solution)/shard_map/ppermute | solution.py:364
  40.2 2.4 %collective-permute-done.18 = bf16[4,32,1024]{2,1,0:T(8,128)(2,1)S(1)} collective-permute-done((bf16[4,32,1024]{2,1,0:T(8,128)(2,1)S(1)}, bf16[4,32,1024]{2,1,0:T(8,128)(2,1)S(1)}, u32[]{:S(2)}, u32[]{:S(2)}) %collective-permute-start.18) | collective-permute-done | bytes 262176 | tf_op jit(solution)/shard_map/ppermute | solution.py:364
  42.6 1.6 collective-permute-start.19
  44.2 1.1 collective-permute-start.6
  45.3 2.8 %collective-permute-start.10 = (bf16[4,256,128]{2,1,0:T(8,128)(2,1)S(1)}, bf16[4,256,128]{2,1,0:T(8,128)(2,1)S(1)}, u32[]{:S(2)}, u32[]{:S(2)}) collective-permute-start(bf16[4,256,128]{2,1,0:T(8,128)(2,1)S(1)} %bitcast.75), channel_id=1, source_target_pairs={{0,12},{4,8},{8,4},{12,0},{1,13},{5,9},{9,5},{13,1},{2,14},{6,10},... | collective-permute-start | bytes 786440 | tf_op jit(solution)/shard_map/ppermute | solution.py:364
  48.1 2.2 %collective-permute-done.6 = f32[1,28,256]{2,1,0:T(8,128)S(1)} collective-permute-done((f32[1,28,256]{2,1,0:T(8,128)S(1)}, f32[1,28,256]{2,1,0:T(8,128)S(1)}, u32[]{:S(2)}, u32[]{:S(2)}) %collective-permute-start.6) | collective-permute-done | bytes 28704 | tf_op jit(solution)/shard_map/ppermute | solution.py:364
  50.4 2.0 %collective-permute-start.8 = (bf16[4,256,128]{2,1,0:T(8,128)(2,1)S(1)}, bf16[4,256,128]{2,1,0:T(8,128)(2,1)}, u32[]{:S(2)}, u32[]{:S(2)}) collective-permute-start(bf16[4,256,128]{2,1,0:T(8,128)(2,1)S(1)} %get-tuple-element.66), channel_id=1, source_target_pairs={{0,4},{4,0},{8,12},{12,8},{1,5},{5,1},{9,13},{13,9},{2,6},{6,2},{1... | collective-permute-start | bytes 786440 | tf_op jit(solution)/shard_map/ppermute | solution.py:364
  52.5 4.5 %collective-permute-done.7 = f32[2,28,256]{2,1,0:T(8,128)S(1)} collective-permute-done((f32[2,28,256]{2,1,0:T(8,128)S(1)}, f32[2,28,256]{2,1,0:T(8,128)S(1)}, u32[]{:S(2)}, u32[]{:S(2)}) %collective-permute-start.7) | collective-permute-done | bytes 57376 | tf_op jit(solution)/shard_map/ppermute | solution.py:364
  57.1 0.7 pad_maximum_fusion.5.taps
  57.7 7.7 %collective-permute-done.9.refs_5_.rest_2_ = bf16[4,256,128]{2,1,0:T(8,128)(2,1)} collective-permute-done((bf16[4,256,128]{2,1,0:T(8,128)(2,1)S(1)}, bf16[4,256,128]{2,1,0:T(8,128)(2,1)}, u32[]{:S(2)}, u32[]{:S(2)}) %collective-permute-start.9) | collective-permute-done | bytes 262176 | tf_op jit(solution)/shard_map/ppermute | solution.py:364
  65.5 6.5 %shard_map.77 = (bf16[512,1024]{1,0:T(8,128)(2,1)}, bf16[4,32,1024]{2,1,0:T(8,128)(2,1)}, bf16[4,32,1024]{2,1,0:T(8,128)(2,1)}, bf16[6,32,1024]{2,1,0:T(8,128)(2,1)}, bf16[6,32,1024]{2,1,0:T(8,128)(2,1)}) custom-call(s32[2]{0:T(128)} %pad_add_fusion.refs_0_.here, bf16[4,4,32,1024]{3,2,1,0:T(8,128)(2,1)} %copy-done.1, ...), custom_call_target="tpu_custom_call" | custom-call | tf_op jit(solution)/shard_map/pallas_call | solution.py:324
  72.0 1.3 collective-permute-start.11
  73.3 1.3 collective-permute-start.12
  74.6 3.6 %collective-permute-done.11.row_low = bf16[4,32,1024]{2,1,0:T(8,128)(2,1)S(1)} collective-permute-done((bf16[4,32,1024]{2,1,0:T(8,128)(2,1)}, bf16[4,32,1024]{2,1,0:T(8,128)(2,1)S(1)}, u32[]{:S(2)}, u32[]{:S(2)}) %collective-permute-start.11) | collective-permute-done | bytes 262176 | tf_op jit(solution)/shard_map/ppermute | solution.py:405
  78.2 0.7 slice_dynamic-update-slice_fusion.5
  78.9 3.3 %collective-permute-done.12.row_high = bf16[4,32,1024]{2,1,0:T(8,128)(2,1)S(1)} collective-permute-done((bf16[4,32,1024]{2,1,0:T(8,128)(2,1)}, bf16[4,32,1024]{2,1,0:T(8,128)(2,1)S(1)}, u32[]{:S(2)}, u32[]{:S(2)}) %collective-permute-start.12) | collective-permute-done | bytes 262176 | tf_op jit(solution)/shard_map/ppermute | solution.py:406
  82.2 0.8 slice_dynamic-update-slice_fusion.4
  83.0 2.0 %collective-permute-start.13 = (bf16[6,32,1024]{2,1,0:T(8,128)(2,1)}, bf16[6,32,1024]{2,1,0:T(8,128)(2,1)}, u32[]{:S(2)}, u32[]{:S(2)}) collective-permute-start(bf16[6,32,1024]{2,1,0:T(8,128)(2,1)} %get-tuple-element.107), channel_id=1, source_target_pairs={{0,1},{1,2},{2,3},{4,5},{5,6},{6,7},{8,9},{9,10},{10,11},{12,13},{... | collective-permute-start | bytes 1179656 | tf_op jit(solution)/shard_map/ppermute | solution.py:413
  85.0 1.3 collective-permute-start.14
  86.3 1.1 collective-permute-start.24
  87.3 1.5 collective-permute-start.25
  88.9 1.9 collective-permute-start.26
  90.8 11.7 %shard_map.78 = (bf16[4,256,128]{2,1,0:T(8,128)(2,1)}, bf16[4,256,128]{2,1,0:T(8,128)(2,1)}, bf16[4,256,128]{2,1,0:T(8,128)(2,1)}, bf16[4,256,128]{2,1,0:T(8,128)(2,1)}, f32[4,4,32,1024]{3,2,1,0:T(8,128)}) custom-call(s32[2]{0:T(128)} %pad_add_fusion.refs_0_.here, bf16[4,4,32,1024]{3,2,1,0:T(8,128)(2,1)} %bitcast.57, bf16[4,32,1024]{2,1,0:T(8,128)(2,1)} %copy-done.12, ...), custom_call_target="tpu_custom_call" | custom-call | tf_op jit(solution)/shard_map/pallas_call | solution.py:229
  102.5 5.3 %collective-permute-done.26.refs_6_.rest_3_ = bf16[4,256,128]{2,1,0:T(8,128)(2,1)S(1)} collective-permute-done((bf16[4,256,128]{2,1,0:T(8,128)(2,1)}, bf16[4,256,128]{2,1,0:T(8,128)(2,1)S(1)}, u32[]{:S(2)}, u32[]{:S(2)}) %collective-permute-start.26) | collective-permute-done | bytes 262176 | tf_op jit(solution)/shard_map/ppermute | solution.py:364
  107.8 0.7 copy-done.9
  108.5 7.8 %shard_map.79 = (bf16[512,1024]{1,0:T(8,128)(2,1)}, bf16[4,32,1024]{2,1,0:T(8,128)(2,1)}, bf16[4,32,1024]{2,1,0:T(8,128)(2,1)}, bf16[6,32,1024]{2,1,0:T(8,128)(2,1)}, bf16[6,32,1024]{2,1,0:T(8,128)(2,1)}) custom-call(s32[2]{0:T(128)} %pad_add_fusion.refs_0_.here, bf16[4,4,32,1024]{3,2,1,0:T(8,128)(2,1)} %copy-done.2, ...), custom_call_target="tpu_custom_call" | custom-call | tf_op jit(solution)/shard_map/pallas_call | solution.py:324
  116.3 8.2 %collective-permute-start.27 = (bf16[4,32,1024]{2,1,0:T(8,128)(2,1)}, bf16[4,32,1024]{2,1,0:T(8,128)(2,1)S(1)}, u32[]{:S(2)}, u32[]{:S(2)}) collective-permute-start(bf16[4,32,1024]{2,1,0:T(8,128)(2,1)} %get-tuple-element.85), channel_id=1, source_target_pairs={{0,4},{4,8},{8,12},{1,5},{5,9},{9,13},{2,6},{6,10},{10,14},{3,7},{... | collective-permute-start | bytes 786440 | tf_op jit(solution)/shard_map/ppermute | solution.py:405
  124.6 1.3 collective-permute-start.28
  125.9 5.5 %collective-permute-done.27.row_low = bf16[4,32,1024]{2,1,0:T(8,128)(2,1)S(1)} collective-permute-done((bf16[4,32,1024]{2,1,0:T(8,128)(2,1)}, bf16[4,32,1024]{2,1,0:T(8,128)(2,1)S(1)}, u32[]{:S(2)}, u32[]{:S(2)}) %collective-permute-start.27) | collective-permute-done | bytes 262176 | tf_op jit(solution)/shard_map/ppermute | solution.py:405
  131.4 0.7 slice_dynamic-update-slice_fusion.1
  132.1 3.6 %collective-permute-done.28.row_high = bf16[4,32,1024]{2,1,0:T(8,128)(2,1)S(1)} collective-permute-done((bf16[4,32,1024]{2,1,0:T(8,128)(2,1)}, bf16[4,32,1024]{2,1,0:T(8,128)(2,1)S(1)}, u32[]{:S(2)}, u32[]{:S(2)}) %collective-permute-start.28) | collective-permute-done | bytes 262176 | tf_op jit(solution)/shard_map/ppermute | solution.py:406
  135.7 0.7 slice_dynamic-update-slice_fusion
  136.4 1.8 collective-permute-start.29
  138.1 1.5 collective-permute-start.30
  139.6 1.5 collective-permute-start.21
  141.2 2.8 %collective-permute-start.23 = (bf16[4,256,128]{2,1,0:T(8,128)(2,1)S(1)}, bf16[4,256,128]{2,1,0:T(8,128)(2,1)S(1)}, u32[]{:S(2)}, u32[]{:S(2)}) collective-permute-start(bf16[4,256,128]{2,1,0:T(8,128)(2,1)S(1)} %copy-done.21), channel_id=1, source_target_pairs={{0,12},{4,8},{8,4},{12,0},{1,13},{5,9},{9,5},{13,1},{2,14},{6,10},... | collective-permute-start | bytes 786440 | tf_op jit(solution)/shard_map/ppermute | solution.py:364
  144.1 0.7 copy-done.14
  145.0 11.0 %shard_map.80 = (bf16[4,256,128]{2,1,0:T(8,128)(2,1)}, bf16[4,256,128]{2,1,0:T(8,128)(2,1)}, bf16[4,256,128]{2,1,0:T(8,128)(2,1)}, bf16[4,256,128]{2,1,0:T(8,128)(2,1)}) custom-call(s32[2]{0:T(128)} %pad_add_fusion.refs_0_.here, bf16[4,4,32,1024]{3,2,1,0:T(8,128)(2,1)} %bitcast.56, bf16[4,32,1024]{2,1,0:T(8,128)(2,1)} %copy-done.10, ...), custom_call_target="tpu_custom_call" | custom-call | tf_op jit(solution)/shard_map/pallas_call | solution.py:229
  156.0 6.2 %collective-permute-done.22 = bf16[4,256,128]{2,1,0:T(8,128)(2,1)S(1)} collective-permute-done((bf16[4,256,128]{2,1,0:T(8,128)(2,1)}, bf16[4,256,128]{2,1,0:T(8,128)(2,1)S(1)}, u32[]{:S(2)}, u32[]{:S(2)}) %collective-permute-start.22) | collective-permute-done | bytes 262176 | tf_op jit(solution)/shard_map/ppermute | solution.py:364
  162.2 6.5 %collective-permute-start.31 = (bf16[4,256,128]{2,1,0:T(8,128)(2,1)}, bf16[4,256,128]{2,1,0:T(8,128)(2,1)S(1)}, u32[]{:S(2)}, u32[]{:S(2)}) collective-permute-start(bf16[4,256,128]{2,1,0:T(8,128)(2,1)} %get-tuple-element.95), channel_id=1, source_target_pairs={{0,8},{4,12},{8,0},{12,4},{1,9},{5,13},{9,1},{13,5},{2,10},{6,14},... | collective-permute-start | bytes 786440 | tf_op jit(solution)/shard_map/ppermute | solution.py:364
  168.8 2.0 %collective-permute-start.32 = (bf16[4,256,128]{2,1,0:T(8,128)(2,1)}, bf16[4,256,128]{2,1,0:T(8,128)(2,1)S(1)}, u32[]{:S(2)}, u32[]{:S(2)}) collective-permute-start(bf16[4,256,128]{2,1,0:T(8,128)(2,1)} %get-tuple-element.96), channel_id=1, source_target_pairs={{0,12},{4,8},{8,4},{12,0},{1,13},{5,9},{9,5},{13,1},{2,14},{6,10},... | collective-permute-start | bytes 786440 | tf_op jit(solution)/shard_map/ppermute | solution.py:364
  171.0 1.2 copy_dynamic-update-slice_fusion.3
  173.8 13.6 %collective-permute-done.31 = bf16[4,256,128]{2,1,0:T(8,128)(2,1)S(1)} collective-permute-done((bf16[4,256,128]{2,1,0:T(8,128)(2,1)}, bf16[4,256,128]{2,1,0:T(8,128)(2,1)S(1)}, u32[]{:S(2)}, u32[]{:S(2)}) %collective-permute-start.31) | collective-permute-done | bytes 262176 | tf_op jit(solution)/shard_map/ppermute | solution.py:364
  188.5 1.0 copy-done.5
  (94 shorter events, 6.1 us)
Async XLA Ops:
  0.6 15.1 %copy-start = (bf16[256,4,512]{2,1,0:T(4,128)(2,1)S(1)}, bf16[256,4,512]{2,1,0:T(4,128)(2,1)}, u32[]{:S(2)}) copy-start(bf16[256,4,512]{2,1,0:T(4,128)(2,1)} %param.7) | copy-start | bytes 3145732
  1.6 7.7 %collective-permute-start = (bf16[1,32,1024]{2,1,0:T(8,128)(2,1)S(1)}, bf16[1,32,1024]{2,1,0:T(8,128)(2,1)S(1)}, u32[]{:S(2)}, u32[]{:S(2)}) collective-permute-start(bf16[1,32,1024]{2,1,0:T(8,128)(2,1)S(1)} %dynamic-slice_bitcast_fusion.1), channel_id=1, source_target_pairs={{0,12},{4,8},{8,4},{12,0},{1,13},{5,9},{9,5},{13,1},{2,14},{6,10},... | collective-permute-start | bytes 196616 | tf_op jit(solution)/shard_map/ppermute | solution.py:364
  7.5 21.2 %collective-permute-start.15 = (bf16[1,32,1024]{2,1,0:T(8,128)(2,1)S(1)}, bf16[1,32,1024]{2,1,0:T(8,128)(2,1)S(1)}, u32[]{:S(2)}, u32[]{:S(2)}) collective-permute-start(bf16[1,32,1024]{2,1,0:T(8,128)(2,1)S(1)} %dynamic-slice_bitcast_fusion), channel_id=1, source_target_pairs={{0,12},{4,8},{8,4},{12,0},{1,13},{5,9},{9,5},{13,1},{2,14},{6,10},... | collective-permute-start | bytes 196616 | tf_op jit(solution)/shard_map/ppermute | solution.py:364
  9.3 6.4 %collective-permute-start.1 = (bf16[2,32,1024]{2,1,0:T(8,128)(2,1)S(1)}, bf16[2,32,1024]{2,1,0:T(8,128)(2,1)S(1)}, u32[]{:S(2)}, u32[]{:S(2)}) collective-permute-start(bf16[2,32,1024]{2,1,0:T(8,128)(2,1)S(1)} %pad_maximum_fusion.4), channel_id=1, source_target_pairs={{0,4},{4,0},{8,12},{12,8},{1,5},{5,1},{9,13},{13,9},{2,6},{6,2},{1... | collective-permute-start | bytes 393224 | tf_op jit(solution)/shard_map/ppermute | solution.py:364
  12.5 8.8 %copy-start.3 = (bf16[256,4,512]{2,1,0:T(4,128)(2,1)S(1)}, bf16[256,4,512]{2,1,0:T(4,128)(2,1)}, u32[]{:S(2)}) copy-start(bf16[256,4,512]{2,1,0:T(4,128)(2,1)} %param.6) | copy-start | bytes 3145732
  18.3 7.5 %collective-permute-start.2 = (bf16[4,32,1024]{2,1,0:T(8,128)(2,1)S(1)}, bf16[4,32,1024]{2,1,0:T(8,128)(2,1)S(1)}, u32[]{:S(2)}, u32[]{:S(2)}) collective-permute-start(bf16[4,32,1024]{2,1,0:T(8,128)(2,1)S(1)} %pad_maximum_fusion.2), channel_id=1, source_target_pairs={{0,16},{1,17},{2,18},{3,19},{16,0},{17,1},{18,2},{19,3},{4,20},{5,... | collective-permute-start | bytes 786440 | tf_op jit(solution)/shard_map/ppermute | solution.py:364
  19.8 7.2 %collective-permute-start.3 = (bf16[4,32,1024]{2,1,0:T(8,128)(2,1)S(1)}, bf16[4,32,1024]{2,1,0:T(8,128)(2,1)S(1)}, u32[]{:S(2)}, u32[]{:S(2)}) collective-permute-start(bf16[4,32,1024]{2,1,0:T(8,128)(2,1)S(1)} %pad_maximum_fusion.2), channel_id=1, source_target_pairs={{0,2},{1,3},{2,0},{3,1},{16,18},{17,19},{18,16},{19,17},{4,6},{5,7... | collective-permute-start | bytes 786440 | tf_op jit(solution)/shard_map/ppermute | solution.py:364
  27.1 17.1 %copy-start.19 = (f32[256,27]{0,1:T(8,128)S(1)}, f32[256,27]{0,1:T(8,128)}, u32[]{:S(2)}) copy-start(f32[256,27]{0,1:T(8,128)} %param.10) | copy-start | bytes 82948
  27.1 17.1 %copy-start.20 = (f32[256]{0:T(256)S(1)}, f32[256]{0:T(256)}, u32[]{:S(2)}) copy-start(f32[256]{0:T(256)} %param.11) | copy-start | bytes 3076
  27.1 18.2 %copy-start.18 = (bf16[256,4,128]{2,0,1:T(8,128)(2,1)S(1)}, bf16[256,4,128]{2,0,1:T(8,128)(2,1)}, u32[]{:S(2)}) copy-start(bf16[256,4,128]{2,0,1:T(8,128)(2,1)} %copy.48) | copy-start | bytes 786436
  27.1 21.0 %copy-start.17 = (bf16[256,4,128]{2,0,1:T(8,128)(2,1)S(1)}, bf16[256,4,128]{2,0,1:T(8,128)(2,1)}, u32[]{:S(2)}) copy-start(bf16[256,4,128]{2,0,1:T(8,128)(2,1)} %copy.49) | copy-start | bytes 786436
  27.1 7.8 %collective-permute-start.4 = (bf16[4,32,1024]{2,1,0:T(8,128)(2,1)S(1)}, bf16[4,32,1024]{2,1,0:T(8,128)(2,1)S(1)}, u32[]{:S(2)}, u32[]{:S(2)}) collective-permute-start(bf16[4,32,1024]{2,1,0:T(8,128)(2,1)S(1)} %broadcast_select_fusion.1), channel_id=1, source_target_pairs={{0,2},{1,17},{2,0},{3,19},{16,18},{17,1},{18,16},{19,3},{4,6},{5,2... | collective-permute-start | bytes 786440 | tf_op jit(solution)/shard_map/ppermute | solution.py:364
  28.7 5.0 %collective-permute-start.16 = (bf16[2,32,1024]{2,1,0:T(8,128)(2,1)S(1)}, bf16[2,32,1024]{2,1,0:T(8,128)(2,1)S(1)}, u32[]{:S(2)}, u32[]{:S(2)}) collective-permute-start(bf16[2,32,1024]{2,1,0:T(8,128)(2,1)S(1)} %pad_maximum_fusion.6), channel_id=1, source_target_pairs={{0,4},{4,0},{8,12},{12,8},{1,5},{5,1},{9,13},{13,9},{2,6},{6,2},{1... | collective-permute-start | bytes 393224 | tf_op jit(solution)/shard_map/ppermute | solution.py:364
  33.8 6.4 %collective-permute-start.17 = (bf16[4,32,1024]{2,1,0:T(8,128)(2,1)S(1)}, bf16[4,32,1024]{2,1,0:T(8,128)(2,1)S(1)}, u32[]{:S(2)}, u32[]{:S(2)}) collective-permute-start(bf16[4,32,1024]{2,1,0:T(8,128)(2,1)S(1)} %get-tuple-element.105), channel_id=1, source_target_pairs={{0,2},{1,3},{2,0},{3,1},{16,18},{17,19},{18,16},{19,17},{4,6},{5,7... | collective-permute-start | bytes 786440 | tf_op jit(solution)/shard_map/ppermute | solution.py:364
  34.4 8.2 %collective-permute-start.18 = (bf16[4,32,1024]{2,1,0:T(8,128)(2,1)S(1)}, bf16[4,32,1024]{2,1,0:T(8,128)(2,1)S(1)}, u32[]{:S(2)}, u32[]{:S(2)}) collective-permute-start(bf16[4,32,1024]{2,1,0:T(8,128)(2,1)S(1)} %get-tuple-element.105), channel_id=1, source_target_pairs={{0,16},{1,17},{2,18},{3,19},{16,0},{17,1},{18,2},{19,3},{4,20},{5,... | collective-permute-start | bytes 786440 | tf_op jit(solution)/shard_map/ppermute | solution.py:364
  35.0 30.4 %copy-start.1 = (bf16[4,4,32,1024]{3,2,1,0:T(8,128)(2,1)}, bf16[4,4,32,1024]{3,2,1,0:T(8,128)(2,1)S(1)}, u32[]{:S(2)}) copy-start(bf16[4,4,32,1024]{3,2,1,0:T(8,128)(2,1)S(1)} %pad_maximum_fusion.refs_1_.mine) | copy-start | bytes 3145732
  35.0 30.4 %collective-permute-start.5 = (bf16[4,4,32,1024]{3,2,1,0:T(8,128)(2,1)S(1)}, bf16[4,4,32,1024]{3,2,1,0:T(8,128)(2,1)}, u32[]{:S(2)}, u32[]{:S(2)}) collective-permute-start(bf16[4,4,32,1024]{3,2,1,0:T(8,128)(2,1)S(1)} %pad_maximum_fusion.refs_1_.mine), channel_id=1, source_target_pairs={{0,1},{1,0},{2,3},{3,2},{16,17},{17,16},{18,19},{19,18},{4,5},{5,4... | collective-permute-start | bytes 3145736 | tf_op jit(solution)/shard_map/ppermute | solution.py:364
  42.6 7.7 %collective-permute-start.19 = (bf16[4,32,1024]{2,1,0:T(8,128)(2,1)S(1)}, bf16[4,32,1024]{2,1,0:T(8,128)(2,1)S(1)}, u32[]{:S(2)}, u32[]{:S(2)}) collective-permute-start(bf16[4,32,1024]{2,1,0:T(8,128)(2,1)S(1)} %broadcast_select_fusion), channel_id=1, source_target_pairs={{0,2},{1,17},{2,0},{3,19},{16,18},{17,1},{18,16},{19,3},{4,6},{5,2... | collective-permute-start | bytes 786440 | tf_op jit(solution)/shard_map/ppermute | solution.py:364
  44.2 6.1 %collective-permute-start.6 = (f32[1,28,256]{2,1,0:T(8,128)S(1)}, f32[1,28,256]{2,1,0:T(8,128)S(1)}, u32[]{:S(2)}, u32[]{:S(2)}) collective-permute-start(f32[1,28,256]{2,1,0:T(8,128)S(1)} %maximum_bitcast_fusion), channel_id=1, source_target_pairs={{0,12},{4,8},{8,4},{12,0},{1,13},{5,9},{9,5},{13,1},{2,14},{6,10},... | collective-permute-start | bytes 86024 | tf_op jit(solution)/shard_map/ppermute | solution.py:364
  45.3 12.4 %collective-permute-start.10 = (bf16[4,256,128]{2,1,0:T(8,128)(2,1)S(1)}, bf16[4,256,128]{2,1,0:T(8,128)(2,1)S(1)}, u32[]{:S(2)}, u32[]{:S(2)}) collective-permute-start(bf16[4,256,128]{2,1,0:T(8,128)(2,1)S(1)} %bitcast.75), channel_id=1, source_target_pairs={{0,12},{4,8},{8,4},{12,0},{1,13},{5,9},{9,5},{13,1},{2,14},{6,10},... | collective-permute-start | bytes 786440 | tf_op jit(solution)/shard_map/ppermute | solution.py:364
  48.1 17.3 %collective-permute-start.9 = (bf16[4,256,128]{2,1,0:T(8,128)(2,1)S(1)}, bf16[4,256,128]{2,1,0:T(8,128)(2,1)}, u32[]{:S(2)}, u32[]{:S(2)}) collective-permute-start(bf16[4,256,128]{2,1,0:T(8,128)(2,1)S(1)} %bitcast.74), channel_id=1, source_target_pairs={{0,8},{4,12},{8,0},{12,4},{1,9},{5,13},{9,1},{13,5},{2,10},{6,14},... | collective-permute-start | bytes 786440 | tf_op jit(solution)/shard_map/ppermute | solution.py:364
  50.4 6.7 %collective-permute-start.7 = (f32[2,28,256]{2,1,0:T(8,128)S(1)}, f32[2,28,256]{2,1,0:T(8,128)S(1)}, u32[]{:S(2)}, u32[]{:S(2)}) collective-permute-start(f32[2,28,256]{2,1,0:T(8,128)S(1)} %pad_maximum_fusion.7), channel_id=1, source_target_pairs={{0,4},{4,0},{8,12},{12,8},{1,5},{5,1},{9,13},{13,9},{2,6},{6,2},{1... | collective-permute-start | bytes 172040 | tf_op jit(solution)/shard_map/ppermute | solution.py:364
  50.4 15.1 %collective-permute-start.8 = (bf16[4,256,128]{2,1,0:T(8,128)(2,1)S(1)}, bf16[4,256,128]{2,1,0:T(8,128)(2,1)}, u32[]{:S(2)}, u32[]{:S(2)}) collective-permute-start(bf16[4,256,128]{2,1,0:T(8,128)(2,1)S(1)} %get-tuple-element.66), channel_id=1, source_target_pairs={{0,4},{4,0},{8,12},{12,8},{1,5},{5,1},{9,13},{13,9},{2,6},{6,2},{1... | collective-permute-start | bytes 786440 | tf_op jit(solution)/shard_map/ppermute | solution.py:364
  52.5 38.2 %copy-start.2 = (bf16[4,4,32,1024]{3,2,1,0:T(8,128)(2,1)}, bf16[4,4,32,1024]{3,2,1,0:T(8,128)(2,1)S(1)}, u32[]{:S(2)}) copy-start(bf16[4,4,32,1024]{3,2,1,0:T(8,128)(2,1)S(1)} %pad_maximum_fusion.1.mine.refs_1_) | copy-start | bytes 3145732
  57.0 31.8 %collective-permute-start.20 = (bf16[4,4,32,1024]{3,2,1,0:T(8,128)(2,1)S(1)}, bf16[4,4,32,1024]{3,2,1,0:T(8,128)(2,1)}, u32[]{:S(2)}, u32[]{:S(2)}) collective-permute-start(bf16[4,4,32,1024]{3,2,1,0:T(8,128)(2,1)S(1)} %pad_maximum_fusion.1.mine.refs_1_), channel_id=1, source_target_pairs={{0,1},{1,0},{2,3},{3,2},{16,17},{17,16},{18,19},{19,18},{4,5},{5,4... | collective-permute-start | bytes 3145736 | tf_op jit(solution)/shard_map/ppermute | solution.py:364
  57.7 7.7 %copy-start.6 = (bf16[4,256,128]{2,1,0:T(8,128)(2,1)}, bf16[4,256,128]{2,1,0:T(8,128)(2,1)S(1)}, u32[]{:S(2)}) copy-start(bf16[4,256,128]{2,1,0:T(8,128)(2,1)S(1)} %collective-permute-done.10.refs_6_.rest_3_) | copy-start | bytes 786436
  72.0 6.2 %collective-permute-start.11 = (bf16[4,32,1024]{2,1,0:T(8,128)(2,1)}, bf16[4,32,1024]{2,1,0:T(8,128)(2,1)S(1)}, u32[]{:S(2)}, u32[]{:S(2)}) collective-permute-start(bf16[4,32,1024]{2,1,0:T(8,128)(2,1)} %get-tuple-element.70), channel_id=1, source_target_pairs={{0,4},{4,8},{8,12},{1,5},{5,9},{9,13},{2,6},{6,10},{10,14},{3,7},{... | collective-permute-start | bytes 786440 | tf_op jit(solution)/shard_map/ppermute | solution.py:405
  73.3 8.9 %collective-permute-start.12 = (bf16[4,32,1024]{2,1,0:T(8,128)(2,1)}, bf16[4,32,1024]{2,1,0:T(8,128)(2,1)S(1)}, u32[]{:S(2)}, u32[]{:S(2)}) collective-permute-start(bf16[4,32,1024]{2,1,0:T(8,128)(2,1)} %get-tuple-element.71), channel_id=1, source_target_pairs={{4,0},{8,4},{12,8},{5,1},{9,5},{13,9},{6,2},{10,6},{14,10},{7,3},{... | collective-permute-start | bytes 786440 | tf_op jit(solution)/shard_map/ppermute | solution.py:406
  78.2 12.6 %copy-start.12 = (bf16[4,32,1024]{2,1,0:T(8,128)(2,1)}, bf16[4,32,1024]{2,1,0:T(8,128)(2,1)S(1)}, u32[]{:S(2)}) copy-start(bf16[4,32,1024]{2,1,0:T(8,128)(2,1)S(1)} %collective-permute-done.11.row_low) | copy-start | bytes 786436
  82.2 8.6 %copy-start.13 = (bf16[4,32,1024]{2,1,0:T(8,128)(2,1)}, bf16[4,32,1024]{2,1,0:T(8,128)(2,1)S(1)}, u32[]{:S(2)}) copy-start(bf16[4,32,1024]{2,1,0:T(8,128)(2,1)S(1)} %collective-permute-done.12.row_high) | copy-start | bytes 786436
  83.0 7.8 %collective-permute-start.13 = (bf16[6,32,1024]{2,1,0:T(8,128)(2,1)}, bf16[6,32,1024]{2,1,0:T(8,128)(2,1)}, u32[]{:S(2)}, u32[]{:S(2)}) collective-permute-start(bf16[6,32,1024]{2,1,0:T(8,128)(2,1)} %get-tuple-element.107), channel_id=1, source_target_pairs={{0,1},{1,2},{2,3},{4,5},{5,6},{6,7},{8,9},{9,10},{10,11},{12,13},{... | collective-permute-start | bytes 1179656 | tf_op jit(solution)/shard_map/ppermute | solution.py:413
  85.0 5.8 %collective-permute-start.14 = (bf16[6,32,1024]{2,1,0:T(8,128)(2,1)}, bf16[6,32,1024]{2,1,0:T(8,128)(2,1)}, u32[]{:S(2)}, u32[]{:S(2)}) collective-permute-start(bf16[6,32,1024]{2,1,0:T(8,128)(2,1)} %get-tuple-element.106), channel_id=1, source_target_pairs={{1,0},{2,1},{3,2},{5,4},{6,5},{7,6},{9,8},{10,9},{11,10},{13,12},{... | collective-permute-start | bytes 1179656 | tf_op jit(solution)/shard_map/ppermute | solution.py:414
  86.3 16.2 %collective-permute-start.24 = (bf16[4,256,128]{2,1,0:T(8,128)(2,1)}, bf16[4,256,128]{2,1,0:T(8,128)(2,1)S(1)}, u32[]{:S(2)}, u32[]{:S(2)}) collective-permute-start(bf16[4,256,128]{2,1,0:T(8,128)(2,1)} %bitcast.73), channel_id=1, source_target_pairs={{0,4},{4,0},{8,12},{12,8},{1,5},{5,1},{9,13},{13,9},{2,6},{6,2},{1... | collective-permute-start | bytes 786440 | tf_op jit(solution)/shard_map/ppermute | solution.py:364
  87.3 15.2 %collective-permute-start.25 = (bf16[4,256,128]{2,1,0:T(8,128)(2,1)}, bf16[4,256,128]{2,1,0:T(8,128)(2,1)S(1)}, u32[]{:S(2)}, u32[]{:S(2)}) collective-permute-start(bf16[4,256,128]{2,1,0:T(8,128)(2,1)} %bitcast.71), channel_id=1, source_target_pairs={{0,8},{4,12},{8,0},{12,4},{1,9},{5,13},{9,1},{13,5},{2,10},{6,14},... | collective-permute-start | bytes 786440 | tf_op jit(solution)/shard_map/ppermute | solution.py:364
  88.9 18.9 %collective-permute-start.26 = (bf16[4,256,128]{2,1,0:T(8,128)(2,1)}, bf16[4,256,128]{2,1,0:T(8,128)(2,1)S(1)}, u32[]{:S(2)}, u32[]{:S(2)}) collective-permute-start(bf16[4,256,128]{2,1,0:T(8,128)(2,1)} %bitcast.72), channel_id=1, source_target_pairs={{0,12},{4,8},{8,4},{12,0},{1,13},{5,9},{9,5},{13,1},{2,14},{6,10},... | collective-permute-start | bytes 786440 | tf_op jit(solution)/shard_map/ppermute | solution.py:364
  102.5 5.3 %copy-start.7 = (bf16[4,256,128]{2,1,0:T(8,128)(2,1)}, bf16[4,256,128]{2,1,0:T(8,128)(2,1)S(1)}, u32[]{:S(2)}) copy-start(bf16[4,256,128]{2,1,0:T(8,128)(2,1)S(1)} %collective-permute-done.24.refs_4_.rest_1_) | copy-start | bytes 786436
  102.5 5.3 %copy-start.8 = (bf16[4,256,128]{2,1,0:T(8,128)(2,1)}, bf16[4,256,128]{2,1,0:T(8,128)(2,1)S(1)}, u32[]{:S(2)}) copy-start(bf16[4,256,128]{2,1,0:T(8,128)(2,1)S(1)} %collective-permute-done.25.refs_5_.rest_2_) | copy-start | bytes 786436
  107.8 0.7 copy-start.9
  108.5 32.7 %copy-start.21 = (bf16[4,256,128]{2,1,0:T(8,128)(2,1)S(1)}, bf16[4,256,128]{2,1,0:T(8,128)(2,1)}, u32[]{:S(2)}) copy-start(bf16[4,256,128]{2,1,0:T(8,128)(2,1)} %get-tuple-element.78) | copy-start | bytes 786436
  116.3 15.1 %collective-permute-start.27 = (bf16[4,32,1024]{2,1,0:T(8,128)(2,1)}, bf16[4,32,1024]{2,1,0:T(8,128)(2,1)S(1)}, u32[]{:S(2)}, u32[]{:S(2)}) collective-permute-start(bf16[4,32,1024]{2,1,0:T(8,128)(2,1)} %get-tuple-element.85), channel_id=1, source_target_pairs={{0,4},{4,8},{8,12},{1,5},{5,9},{9,13},{2,6},{6,10},{10,14},{3,7},{... | collective-permute-start | bytes 786440 | tf_op jit(solution)/shard_map/ppermute | solution.py:405
  124.6 11.1 %collective-permute-start.28 = (bf16[4,32,1024]{2,1,0:T(8,128)(2,1)}, bf16[4,32,1024]{2,1,0:T(8,128)(2,1)S(1)}, u32[]{:S(2)}, u32[]{:S(2)}) collective-permute-start(bf16[4,32,1024]{2,1,0:T(8,128)(2,1)} %get-tuple-element.86), channel_id=1, source_target_pairs={{4,0},{8,4},{12,8},{5,1},{9,5},{13,9},{6,2},{10,6},{14,10},{7,3},{... | collective-permute-start | bytes 786440 | tf_op jit(solution)/shard_map/ppermute | solution.py:406
  131.4 12.7 %copy-start.10 = (bf16[4,32,1024]{2,1,0:T(8,128)(2,1)}, bf16[4,32,1024]{2,1,0:T(8,128)(2,1)S(1)}, u32[]{:S(2)}) copy-start(bf16[4,32,1024]{2,1,0:T(8,128)(2,1)S(1)} %collective-permute-done.27.row_low) | copy-start | bytes 786436
  135.7 8.4 %copy-start.11 = (bf16[4,32,1024]{2,1,0:T(8,128)(2,1)}, bf16[4,32,1024]{2,1,0:T(8,128)(2,1)S(1)}, u32[]{:S(2)}) copy-start(bf16[4,32,1024]{2,1,0:T(8,128)(2,1)S(1)} %collective-permute-done.28.row_high) | copy-start | bytes 786436
  136.4 7.7 %collective-permute-start.29 = (bf16[6,32,1024]{2,1,0:T(8,128)(2,1)}, bf16[6,32,1024]{2,1,0:T(8,128)(2,1)S(1)}, u32[]{:S(2)}, u32[]{:S(2)}) collective-permute-start(bf16[6,32,1024]{2,1,0:T(8,128)(2,1)} %get-tuple-element.101), channel_id=1, source_target_pairs={{0,1},{1,2},{2,3},{4,5},{5,6},{6,7},{8,9},{9,10},{10,11},{12,13},{... | collective-permute-start | bytes 1179656 | tf_op jit(solution)/shard_map/ppermute | solution.py:413
  138.1 5.9 %collective-permute-start.30 = (bf16[6,32,1024]{2,1,0:T(8,128)(2,1)}, bf16[6,32,1024]{2,1,0:T(8,128)(2,1)S(1)}, u32[]{:S(2)}, u32[]{:S(2)}) collective-permute-start(bf16[6,32,1024]{2,1,0:T(8,128)(2,1)} %get-tuple-element.100), channel_id=1, source_target_pairs={{1,0},{2,1},{3,2},{5,4},{6,5},{7,6},{9,8},{10,9},{11,10},{13,12},{... | collective-permute-start | bytes 1179656 | tf_op jit(solution)/shard_map/ppermute | solution.py:414
  139.6 16.4 %collective-permute-start.21 = (bf16[4,256,128]{2,1,0:T(8,128)(2,1)}, bf16[4,256,128]{2,1,0:T(8,128)(2,1)S(1)}, u32[]{:S(2)}, u32[]{:S(2)}) collective-permute-start(bf16[4,256,128]{2,1,0:T(8,128)(2,1)} %get-tuple-element.76), channel_id=1, source_target_pairs={{0,4},{4,0},{8,12},{12,8},{1,5},{5,1},{9,13},{13,9},{2,6},{6,2},{1... | collective-permute-start | bytes 786440 | tf_op jit(solution)/shard_map/ppermute | solution.py:364
  141.1 21.1 %collective-permute-start.22 = (bf16[4,256,128]{2,1,0:T(8,128)(2,1)}, bf16[4,256,128]{2,1,0:T(8,128)(2,1)S(1)}, u32[]{:S(2)}, u32[]{:S(2)}) collective-permute-start(bf16[4,256,128]{2,1,0:T(8,128)(2,1)} %get-tuple-element.77), channel_id=1, source_target_pairs={{0,8},{4,12},{8,0},{12,4},{1,9},{5,13},{9,1},{13,5},{2,10},{6,14},... | collective-permute-start | bytes 786440 | tf_op jit(solution)/shard_map/ppermute | solution.py:364
  141.2 21.0 %collective-permute-start.23 = (bf16[4,256,128]{2,1,0:T(8,128)(2,1)S(1)}, bf16[4,256,128]{2,1,0:T(8,128)(2,1)S(1)}, u32[]{:S(2)}, u32[]{:S(2)}) collective-permute-start(bf16[4,256,128]{2,1,0:T(8,128)(2,1)S(1)} %copy-done.21), channel_id=1, source_target_pairs={{0,12},{4,8},{8,4},{12,0},{1,13},{5,9},{9,5},{13,1},{2,14},{6,10},... | collective-permute-start | bytes 786440 | tf_op jit(solution)/shard_map/ppermute | solution.py:364
  144.1 0.8 copy-start.14
  144.1 0.9 copy-start.15
  156.0 16.6 %copy-start.16 = (bf16[4,256,128]{2,1,0:T(8,128)(2,1)S(1)}, bf16[4,256,128]{2,1,0:T(8,128)(2,1)}, u32[]{:S(2)}) copy-start(bf16[4,256,128]{2,1,0:T(8,128)(2,1)} %get-tuple-element.90) | copy-start | bytes 786436
  162.2 25.2 %collective-permute-start.31 = (bf16[4,256,128]{2,1,0:T(8,128)(2,1)}, bf16[4,256,128]{2,1,0:T(8,128)(2,1)S(1)}, u32[]{:S(2)}, u32[]{:S(2)}) collective-permute-start(bf16[4,256,128]{2,1,0:T(8,128)(2,1)} %get-tuple-element.95), channel_id=1, source_target_pairs={{0,8},{4,12},{8,0},{12,4},{1,9},{5,13},{9,1},{13,5},{2,10},{6,14},... | collective-permute-start | bytes 786440 | tf_op jit(solution)/shard_map/ppermute | solution.py:364
  168.8 18.9 %collective-permute-start.32 = (bf16[4,256,128]{2,1,0:T(8,128)(2,1)}, bf16[4,256,128]{2,1,0:T(8,128)(2,1)S(1)}, u32[]{:S(2)}, u32[]{:S(2)}) collective-permute-start(bf16[4,256,128]{2,1,0:T(8,128)(2,1)} %get-tuple-element.96), channel_id=1, source_target_pairs={{0,12},{4,8},{8,4},{12,0},{1,13},{5,9},{9,5},{13,1},{2,14},{6,10},... | collective-permute-start | bytes 786440 | tf_op jit(solution)/shard_map/ppermute | solution.py:364
  170.8 17.4 %collective-permute-start.33 = (bf16[4,256,128]{2,1,0:T(8,128)(2,1)}, bf16[4,256,128]{2,1,0:T(8,128)(2,1)S(1)}, u32[]{:S(2)}, u32[]{:S(2)}) collective-permute-start(bf16[4,256,128]{2,1,0:T(8,128)(2,1)} %get-tuple-element.97), channel_id=1, source_target_pairs={{0,4},{4,0},{8,12},{12,8},{1,5},{5,1},{9,13},{13,9},{2,6},{6,2},{1... | collective-permute-start | bytes 786440 | tf_op jit(solution)/shard_map/ppermute | solution.py:364
  173.8 14.6 %copy-start.4 = (bf16[256,4,512]{2,1,0:T(4,128)(2,1)}, bf16[256,4,512]{2,1,0:T(4,128)(2,1)S(1)}, u32[]{:S(2)}) copy-start(bf16[256,4,512]{2,1,0:T(4,128)(2,1)S(1)} %copy_dynamic-update-slice_fusion.4) | copy-start | bytes 3145732
  188.5 1.0 copy-start.5

commit v10 on v9

--- a/solution.py
+++ b/solution.py
@@ -69,28 +69,31 @@
     return found
 
 
-def piece_copies(here, mine, other, full, sems):
+def slot_of(distance, count):
+    slot = 0
+    for place, held in enumerate(distances(count)):
+        slot = jnp.where(distance == held, place, slot)
+    return slot
+
+
+def piece_copies(here, mine, other, full, sems, blocks, columns=None):
     chan, seat = here[0], here[1]
     copies = []
-    for slot, distance in enumerate(distances(mine.shape[1])):
+    for index, block in enumerate(blocks):
+        slot = slot_of(chan ^ block, mine.shape[1])
         for side, pieces in enumerate((mine, other)):
             for turn in range(pieces.shape[0]):
+                source = pieces.at[turn, slot]
+                if columns is not None:
+                    source = source.at[:, columns]
                 copies.append(
                     pltpu.make_async_copy(
-                        pieces.at[turn, slot],
-                        full.at[chan ^ distance, seat ^ side ^ (2 * turn)],
-                        sems.at[chan ^ distance, 2 * turn + side],
+                        source,
+                        full.at[index, seat ^ side ^ (2 * turn)],
+                        sems.at[index, 2 * turn + side],
                     )
                 )
     return copies
-
-
-def wait_block(block, mine, other, full, sems):
-    for side, pieces in enumerate((mine, other)):
-        for turn in range(pieces.shape[0]):
-            pltpu.make_async_copy(
-                pieces.at[turn, 0], full.at[block, 2 * turn + side], sems.at[block, 2 * turn + side]
-            ).wait()
 
 
 def start_all(copies):
@@ -110,22 +113,9 @@
         out[z] = total.astype(out.dtype)
 
 
-def forward_kernel(
-    here, own, row_low, row_high, plane_low, plane_high, taps, mine, other, *rest
-):
-    count = (len(rest) - 5) // 2
-    inputs, outputs = rest[:count], rest[count : 2 * count]
-    slope, padded, active, weight, sems = rest[2 * count :]
-    step = pl.program_id(0)
-    planes, rows, extent = own.shape[:3]
-    copies = piece_copies(here, mine, other, weight, sems)
-
-    @pl.when(step == 0)
-    def _():
-        start_all(copies)
-
-    fill_padded(padded, own, row_low, row_high, plane_low, plane_high)
-    lanes = pl.ds(pl.multiple_of(step * LANES, LANES), LANES)
+def forward_cells(fields, taps, padded, active, lanes, slope):
+    planes, rows, extent = fields[0].shape[:3]
+    fill_padded(padded, *fields)
     for z in range(planes):
         for y in range(rows):
             mixed = stencil_row(padded, taps, z, y, False) + taps[0, 27][None, :]
@@ -134,66 +124,106 @@
             active[at : at + extent, lanes] = (mixed * half).astype(active.dtype)
             slope[z, y] = half + mixed * jnp.exp(-0.5 * mixed * mixed) * inv_root_two_pi
 
-    @pl.when(step == pl.num_programs(0) - 1)
-    def _():
-        wait_all(copies)
-        for shift in range(count):
-            rows_of = weight[here[0] ^ shift]
-            product = lax.dot_general(
-                rows_of.reshape(-1, rows_of.shape[-1]),
-                active[...],
-                (((1,), (1,)), ((), ())),
-                preferred_element_type=jnp.float32,
-            )
-            add_planes(inputs[shift], product, outputs[shift])
-
-
-def backward_kernel(
-    here, own, row_low, row_high, plane_low, plane_high, taps, mine, other, *rest
-):
-    count = (len(rest) - 4) // 2
-    inputs, outputs = rest[:count], rest[count : 2 * count]
-    padded, grads, weight, sems = rest[2 * count :]
-    step = pl.program_id(0)
-    planes, rows, extent = own.shape[:3]
-    copies = piece_copies(here, mine, other, weight, sems)
-
-    @pl.when(step == 0)
-    def _():
-        start_all(copies)
-
-    fill_padded(padded, own, row_low, row_high, plane_low, plane_high)
-    lanes = pl.ds(pl.multiple_of(step * LANES, LANES), LANES)
+
+def backward_cells(fields, taps, padded, grads, lanes):
+    planes, rows, extent = fields[0].shape[:3]
+    fill_padded(padded, *fields)
     for z in range(planes):
         for y in range(rows):
             at = (z * rows + y) * extent
             total = stencil_row(padded, taps, z, y, True)
             grads[at : at + extent, lanes] = total.astype(grads.dtype)
 
+
+def lane_block():
+    return pl.ds(pl.multiple_of(pl.program_id(0) * LANES, LANES), LANES)
+
+
+def forward_first(here, *refs):
+    fields, (taps, active, slope, padded) = refs[:5], refs[5:]
+    forward_cells(fields, taps, padded, active, slice(None), slope)
+
+
+def backward_first(here, *refs):
+    fields, (taps, grads, padded) = refs[:5], refs[5:]
+    backward_cells(fields, taps, padded, grads, slice(None))
+
+
+def forward_last(here, *refs, count):
+    fields, (taps, mine, other, before) = refs[:5], refs[5:9]
+    inputs, outputs = refs[9 : 9 + count], refs[9 + count : 9 + 2 * count]
+    slope, padded, active, weight, sems = refs[9 + 2 * count :]
+    step = pl.program_id(0)
+
+    @pl.when(step == 0)
+    def _():
+        start_all(piece_copies(here, mine, other, weight, sems, range(count)))
+
+    forward_cells(fields, taps, padded, active, lane_block(), slope)
+
     @pl.when(step == pl.num_programs(0) - 1)
     def _():
-        wait_all(copies)
-        channels = grads.shape[1]
+        wait_all(piece_copies(here, mine, other, weight, sems, range(count)))
+        half = active.shape[1]
+        for shift in range(count):
+            rows_of = weight[here[0] ^ shift]
+            rows_of = rows_of.reshape(-1, rows_of.shape[-1])
+            product = sum(
+                lax.dot_general(
+                    rows_of[:, part * half : (part + 1) * half],
+                    field[...],
+                    (((1,), (1,)), ((), ())),
+                    preferred_element_type=jnp.float32,
+                )
+                for part, field in enumerate((before, active))
+            )
+            add_planes(inputs[shift], product, outputs[shift])
+
+
+def backward_last(here, *refs, count):
+    fields, (taps, mine, other, before) = refs[:5], refs[5:9]
+    inputs, outputs = refs[9 : 9 + count], refs[9 + count : 9 + 2 * count]
+    padded, grads, weight, sems = refs[9 + 2 * count :]
+    step = pl.program_id(0)
+
+    @pl.when(step == 0)
+    def _():
+        start_all(piece_copies(here, mine, other, weight, sems, range(count)))
+
+    backward_cells(fields, taps, padded, grads, lane_block())
+
+    @pl.when(step == pl.num_programs(0) - 1)
+    def _():
+        wait_all(piece_copies(here, mine, other, weight, sems, range(count)))
+        half = grads.shape[1]
         width = inputs[0].shape[1]
         for shift in range(count):
             start = pl.multiple_of((here[0] ^ shift) * width, width)
-            columns = weight[:, :, :, pl.ds(start, width)].reshape(channels, width)
-            product = jnp.dot(grads[...], columns, preferred_element_type=jnp.float32)
+            columns = weight[:, :, :, pl.ds(start, width)].reshape(2 * half, width)
+            product = sum(
+                jnp.dot(
+                    field[...],
+                    columns[part * half : (part + 1) * half],
+                    preferred_element_type=jnp.float32,
+                )
+                for part, field in enumerate((before, grads))
+            )
             add_planes(inputs[shift], product.T, outputs[shift])
 
 
-def weight_scratch(mine):
-    turns, parts, share, channels = mine.shape
+def weight_scratch(mine, blocks, columns):
+    turns, _, share, _ = mine.shape
     return [
-        pltpu.VMEM((parts, 2 * turns, share, channels), mine.dtype),
-        pltpu.SemaphoreType.DMA((parts, 2 * turns)),
+        pltpu.VMEM((blocks, 2 * turns, share, columns), mine.dtype),
+        pltpu.SemaphoreType.DMA((blocks, 2 * turns)),
     ]
 
 
-def stencil(here, own, halo, taps, weight, blocks, forward):
+def stencil(here, own, halo, taps, part, forward, last=None):
     planes, rows, extent, channels = own.shape
     cells = planes * rows * extent
     per_table = taps.shape[2] // LANES
+    steps = channels // LANES
 
     def block(*lead):
         zeros = (0,) * len(lead)
@@ -203,13 +233,9 @@
         return pl.BlockSpec(shape, lambda c, here: (0,) * len(shape), pipeline_mode=pl.Buffered(1))
 
     def table_at(c, here):
-        away = (c // per_table) ^ here[0]
-        slot = 0
-        for place, distance in enumerate(distances(taps.shape[0])):
-            slot = jnp.where(away == distance, place, slot)
-        return slot, 0, c % per_table
-
-    anywhere = pl.BlockSpec(memory_space=pltpu.HBM)
+        away = ((part * steps + c) // per_table) ^ here[0]
+        return slot_of(away, taps.shape[0]), 0, (part * steps + c) % per_table
+
     in_specs = [
         block(planes, rows, extent),
         block(planes, extent),
@@ -217,30 +243,42 @@
         block(rows + 2, extent),
         block(rows + 2, extent),
         pl.BlockSpec((1, 28, LANES), table_at),
-        anywhere,
-        anywhere,
     ]
-    in_specs += [resident(piece.shape) for piece in blocks]
-    out_specs = [resident(piece.shape) for piece in blocks]
-    out_shape = [jax.ShapeDtypeStruct(piece.shape, piece.dtype) for piece in blocks]
-    if forward:
-        out_specs.append(block(planes, rows, extent))
-        out_shape.append(jax.ShapeDtypeStruct(own.shape, jnp.float32))
+    args = [own, *halo, taps]
+    scratch = [pltpu.VMEM((planes + 2, rows + 2, extent, LANES), jnp.float32)]
+    slope_spec = [block(planes, rows, extent)] if forward else []
+    slope_shape = [jax.ShapeDtypeStruct(own.shape, jnp.float32)] if forward else []
+    if last is None:
+        kernel = forward_first if forward else backward_first
+        out_specs = [block(cells)] + slope_spec
+        out_shape = [jax.ShapeDtypeStruct((cells, channels), own.dtype)] + slope_shape
+    else:
+        weight, before, blocks = last
+        body_of = forward_last if forward else backward_last
+
+        def kernel(*refs):
+            body_of(*refs, count=len(blocks))
+
+        anywhere = pl.BlockSpec(memory_space=pltpu.HBM)
+        in_specs += [anywhere, anywhere, resident(before.shape)]
+        in_specs += [resident(piece.shape) for piece in blocks]
+        args += [*weight, before, *blocks]
+        out_specs = [resident(piece.shape) for piece in blocks] + slope_spec
+        out_shape = [jax.ShapeDtypeStruct(piece.shape, piece.dtype) for piece in blocks]
+        out_shape += slope_shape
+        scratch.append(pltpu.VMEM((cells, channels), own.dtype))
+        scratch += weight_scratch(weight[0], len(blocks), weight[0].shape[3])
     return pl.pallas_call(
-        forward_kernel if forward else backward_kernel,
+        kernel,
         grid_spec=pltpu.PrefetchScalarGridSpec(
             num_scalar_prefetch=1,
-            grid=(channels // LANES,),
+            grid=(steps,),
             in_specs=in_specs,
             out_specs=out_specs,
-            scratch_shapes=[
-                pltpu.VMEM((planes + 2, rows + 2, extent, LANES), jnp.float32),
-                pltpu.VMEM((cells, channels), own.dtype),
-                *weight_scratch(weight[0]),
-            ],
+            scratch_shapes=scratch,
         ),
         out_shape=out_shape,
-    )(here, own, *halo, taps, *weight, *blocks)
+    )(here, *args)
 
 
 def turn_blocks(here, inputs, turned):
@@ -267,15 +305,19 @@
             edge[y + 1] = value[at : at + extent]
 
 
-def hidden_kernel(here, mine, other, *rest, count):
+def hidden_kernel(here, mine, other, *rest, count, part):
     inputs, (*outputs, turned, weight, sems) = rest[:count], rest[count:]
+    half = count // 2
+    copies = piece_copies(
+        here, mine, other, weight, sems, range(part * half, (part + 1) * half)
+    )
 
     @pl.when(pl.program_id(0) == 0)
     def _():
-        start_all(piece_copies(here, mine, other, weight, sems))
+        start_all(copies)
         turn_blocks(here, inputs, turned)
-
-    wait_block(pl.program_id(0), mine, other, weight, sems)
+        wait_all(copies)
+
     rows_of = weight[pl.program_id(0)]
     value = lax.dot_general(
         turned[...],
@@ -286,17 +328,19 @@
     put_with_edges(value.astype(turned.dtype), *outputs)
 
 
-def mix_kernel(here, mine, other, *rest, count):
+def mix_kernel(here, mine, other, *rest, count, part):
     inputs, (slope, *outputs, turned, weight, sems) = rest[:count], rest[count:]
+    channels, width = turned.shape[1], slope.shape[1]
+    half = channels // 2
 
     @pl.when(pl.program_id(0) == 0)
     def _():
-        copies = piece_copies(here, mine, other, weight, sems)
+        columns = slice(part * half, (part + 1) * half)
+        copies = piece_copies(here, mine, other, weight, sems, range(count), columns)
         start_all(copies)
         turn_blocks(here, inputs, turned)
         wait_all(copies)
 
-    channels, width = turned.shape[1], slope.shape[1]
     start = pl.multiple_of(pl.program_id(0) * width, width)
     columns = weight[:, :, :, pl.ds(start, width)].reshape(channels, width)
     grad = jnp.dot(turned[...], columns, preferred_element_type=jnp.float32)
@@ -304,11 +348,12 @@
     put_with_edges((grad * slope[...]).astype(turned.dtype), *outputs)
 
 
-def product_call(here, blocks, weight, slope=None):
+def product_call(here, blocks, weight, part, slope=None):
     planes, own, width = blocks[0].shape
     cells = planes * width
     count = len(blocks)
     channels = own * count
+    half = channels // 2
     dtype = blocks[0].dtype
     columns = pl.BlockSpec((cells, own), lambda c, here: (0, c))
     room = width // CX + 2
@@ -318,20 +363,25 @@
         blocks[0].shape, lambda c, here: (0, 0, 0), pipeline_mode=pl.Buffered(1)
     )
     anywhere = pl.BlockSpec(memory_space=pltpu.HBM)
-    kernel, extra = (hidden_kernel, []) if slope is None else (mix_kernel, [slope])
-    row_shape = jax.ShapeDtypeStruct((planes, CX, channels), dtype)
-    plane_shape = jax.ShapeDtypeStruct((room, CX, channels), dtype)
+    if slope is None:
+        kernel, extra = hidden_kernel, []
+        scratch = weight_scratch(weight[0], count // 2, channels)
+    else:
+        kernel, extra = mix_kernel, [slope]
+        scratch = weight_scratch(weight[0], count, half)
+    row_shape = jax.ShapeDtypeStruct((planes, CX, half), dtype)
+    plane_shape = jax.ShapeDtypeStruct((room, CX, half), dtype)
     return pl.pallas_call(
-        lambda *refs: kernel(*refs, count=count),
+        lambda *refs: kernel(*refs, count=count, part=part),
         grid_spec=pltpu.PrefetchScalarGridSpec(
             num_scalar_prefetch=1,
-            grid=(count,),
+            grid=(count // 2,),
             in_specs=[anywhere] * 2 + [whole] * count + [columns] * len(extra),
             out_specs=[columns, row, row, plane, plane],
-            scratch_shapes=[pltpu.VMEM((cells, channels), dtype), *weight_scratch(weight[0])],
+            scratch_shapes=[pltpu.VMEM((cells, channels), dtype), *scratch],
         ),
         out_shape=[
-            jax.ShapeDtypeStruct((cells, channels), dtype),
+            jax.ShapeDtypeStruct((cells, half), dtype),
             row_shape,
             row_shape,
             plane_shape,
@@ -414,7 +464,6 @@
         plane_high = lax.ppermute(joined(back, 0), "space", backward)
         return row_low, row_high, plane_low, plane_high
 
-    grid = (planes, rows, CX, channels)
     piece_in, piece_out = (
         lax.dynamic_slice_in_dim(weight, seat * share, share, axis=0)
         for weight in (weight_in, weight_out)
@@ -431,16 +480,28 @@
     own_block, taps = lax.optimization_barrier((own_block, taps))
     vol_blocks = exchange({**vol_cut, 0: own_block})
     grad_blocks = exchange(grad_cut)
-    hidden, *edges = product_call(here, vol_blocks, full_in)
-    halo = halo_of(*edges)
-    *out_blocks, slope = stencil(here, hidden.reshape(grid), halo, taps, full_out, vol_blocks, True)
+    halves = range(2)
+    grid = (planes, rows, CX, channels // 2)
+    hidden, halos = [], []
+    for part in halves:
+        field, *edges = product_call(here, vol_blocks, full_in, part)
+        hidden.append(field.reshape(grid))
+        halos.append(halo_of(*edges))
+    active, slope0 = stencil(here, hidden[0], halos[0], taps, 0, True)
+    *out_blocks, slope1 = stencil(
+        here, hidden[1], halos[1], taps, 1, True, (full_out, active, vol_blocks)
+    )
     out_found = exchange(out_blocks)
-    mix_grad, *edges = product_call(
-        here, grad_blocks, full_out, slope.reshape(planes * width, channels)
-    )
-    halo = halo_of(*edges)
+    mixed, halos = [], []
+    for part, slope in enumerate((slope0, slope1)):
+        field, *edges = product_call(
+            here, grad_blocks, full_out, part, slope.reshape(planes * width, channels // 2)
+        )
+        mixed.append(field.reshape(grid))
+        halos.append(halo_of(*edges))
+    (grads,) = stencil(here, mixed[0], halos[0], taps, 0, False)
     back_blocks = list(
-        stencil(here, mix_grad.reshape(grid), halo, taps, full_in, grad_blocks, False)
+        stencil(here, mixed[1], halos[1], taps, 1, False, (full_in, grads, grad_blocks))
     )
     out_found, back_blocks[0] = lax.optimization_barrier((out_found, back_blocks[0]))
     block_out = paste(out_found)
@@ -533,7 +594,7 @@
     own = volume.shape[0]
     parts = lax.axis_size("chan")
     groups, space = lax.axis_size("groups"), lax.axis_size("space")
-    whole_rows = CY % parts == 0 and (CY // parts * CX) % LANES == 0 and parts & (parts - 1) == 0
+    whole_rows = CY % parts == 0 and (CY // parts * CX) % LANES == 0 and parts > 1 and parts & (parts - 1) == 0
     whole_shares = own % LANES == 0 and own % (16 * groups * space) == 0
     split = whole_rows and whole_shares and (groups, space) == (2, 4)
     chosen = split_cells_body if split else exchange_body

time: 193 us -> 224 us (1.16)
  the two profiles are of different devices: /device:TPU:0 before, /device:TPU:11 now
where the time goes in v10:
time: 224 us; the launch traced here: 223 us
  starting transfers between devices  80.6 us (36%)
  waiting for transfers between devices  64.9 us (29%)
  Pallas kernels  48.8 us (22%)
  local copies, waits for them, and re-layouts  23.8 us (11%)
  other arithmetic  3.33 us (1%)
    ppermute x26, waiting for transfers between devices, swap(): return lax.ppermute(part, axes, [(i, partner(i)) for i in range(count)])  44.3 us
    ppermute x26, starting transfers between devices, swap(): return lax.ppermute(part, axes, [(i, partner(i)) for i in range(count)])  36 us
    pallas_call x4, Pallas kernels, stencil(): pl.pallas_call(kernel, grid_spec=pltpu.PrefetchScalarGridSpec(num_scalar_...  27.1 us
    pallas_call x4, Pallas kernels, product_call(): pl.pallas_call(lambda *refs: kernel(*refs, count=count, part=part), grid_...  21.8 us
    ppermute x4, starting transfers between devices, halo_of(): plane_high = lax.ppermute(joined(back, 0), 'space', backward)  19.9 us
    ppermute x4, waiting for transfers between devices, halo_of(): row_high = lax.ppermute(first, 'chan', backward)  17.5 us
    unnamed x78, local copies, waits for them, and re-layouts  11.6 us
    ppermute x4, starting transfers between devices, halo_of(): row_high = lax.ppermute(first, 'chan', backward)  10 us
  transfers between devices with their start and end apart: 42, of which 14 were waited for; matrix products, arithmetic and copies ran while one was open for 7% of the time, Pallas kernels for 22%

profile of v10, /device:TPU:11, one launch (start us, length us, event | category | flops | bytes accessed | tf_op | source)
XLA Modules:
  0.0 222.9 jit_solution(2316691237257820624)
XLA Ops:
  0.7 1.0 dynamic-slice_bitcast_fusion.1
  1.7 1.3 collective-permute-start
  3.0 1.0 constant_dynamic-slice_fusion.2
  4.8 2.2 collective-permute-start.1
  8.4 0.9 collective-permute-done.1
  9.5 0.8 copy.53
  11.2 0.8 copy.51
  12.0 1.2 collective-permute-start.2
  14.5 0.8 copy_bitcast_fusion
  15.3 1.9 collective-permute-done.2
  17.2 1.5 collective-permute-done.3
  18.8 0.9 dynamic-slice_bitcast_fusion
  19.7 2.2 %collective-permute-start.15 = (bf16[1,32,1024]{2,1,0:T(8,128)(2,1)S(1)}, bf16[1,32,1024]{2,1,0:T(8,128)(2,1)S(1)}, u32[]{:S(2)}, u32[]{:S(2)}) collective-permute-start(bf16[1,32,1024]{2,1,0:T(8,128)(2,1)S(1)} %dynamic-slice_bitcast_fusion), channel_id=1, source_target_pairs={{0,12},{4,8},{8,4},{12,0},{1,13},{5,9},{9,5},{13,1},{2,14},{6,10},... | collective-permute-start | bytes 196616 | tf_op jit(solution)/shard_map/ppermute | solution.py:414
  21.9 2.1 collective-permute-done.4
  24.2 5.7 %collective-permute-start.5 = (bf16[4,4,32,1024]{3,2,1,0:T(8,128)(2,1)S(1)}, bf16[4,4,32,1024]{3,2,1,0:T(8,128)(2,1)S(1)}, u32[]{:S(2)}, u32[]{:S(2)}) collective-permute-start(bf16[4,4,32,1024]{3,2,1,0:T(8,128)(2,1)S(1)} %pad_maximum_fusion.refs_1_.refs_7_), channel_id=1, source_target_pairs={{0,1},{1,0},{2,3},{3,2},{16,17},{17,16},{18,19},{19,18},{4,5},{5,4... | collective-permute-start | bytes 3145736 | tf_op jit(solution)/shard_map/ppermute | solution.py:414
  30.0 0.9 collective-permute-start.16
  30.9 4.2 %collective-permute-done.16 = bf16[2,32,1024]{2,1,0:T(8,128)(2,1)S(1)} collective-permute-done((bf16[2,32,1024]{2,1,0:T(8,128)(2,1)S(1)}, bf16[2,32,1024]{2,1,0:T(8,128)(2,1)S(1)}, u32[]{:S(2)}, u32[]{:S(2)}) %collective-permute-start.16) | collective-permute-done | bytes 131104 | tf_op jit(solution)/shard_map/ppermute | solution.py:414
  35.2 0.8 collective-permute-start.18
  36.1 1.0 collective-permute-start.6
  37.6 1.3 collective-permute-done.6
  38.9 3.8 %collective-permute-start.9 = (bf16[4,256,128]{2,1,0:T(8,128)(2,1)S(1)}, bf16[4,256,128]{2,1,0:T(8,128)(2,1)S(1)}, u32[]{:S(2)}, u32[]{:S(2)}) collective-permute-start(bf16[4,256,128]{2,1,0:T(8,128)(2,1)S(1)} %bitcast.78), channel_id=1, source_target_pairs={{0,8},{4,12},{8,0},{12,4},{1,9},{5,13},{9,1},{13,5},{2,10},{6,14},... | collective-permute-start | bytes 786440 | tf_op jit(solution)/shard_map/ppermute | solution.py:414
  42.8 1.4 collective-permute-start.8
  45.0 5.0 %collective-permute-done.7 = f32[2,28,256]{2,1,0:T(8,128)S(1)} collective-permute-done((f32[2,28,256]{2,1,0:T(8,128)S(1)}, f32[2,28,256]{2,1,0:T(8,128)S(1)}, u32[]{:S(2)}, u32[]{:S(2)}) %collective-permute-start.7) | collective-permute-done | bytes 57376 | tf_op jit(solution)/shard_map/ppermute | solution.py:414
  49.9 0.9 collective-permute-start.19
  52.1 7.7 %collective-permute-done.9.refs_5_.refs_12_ = bf16[4,256,128]{2,1,0:T(8,128)(2,1)S(1)} collective-permute-done((bf16[4,256,128]{2,1,0:T(8,128)(2,1)S(1)}, bf16[4,256,128]{2,1,0:T(8,128)(2,1)S(1)}, u32[]{:S(2)}, u32[]{:S(2)}) %collective-permute-start.9) | collective-permute-done | bytes 262176 | tf_op jit(solution)/shard_map/ppermute | solution.py:414
  61.3 1.0 copy-done.4
  62.2 5.3 %shard_map.78 = (bf16[512,512]{1,0:T(8,128)(2,1)}, bf16[4,32,512]{2,1,0:T(8,128)(2,1)}, bf16[4,32,512]{2,1,0:T(8,128)(2,1)}, bf16[6,32,512]{2,1,0:T(8,128)(2,1)}, bf16[6,32,512]{2,1,0:T(8,128)(2,1)}) custom-call(s32[2]{0:T(128)} %pad_add_fusion.refs_0_.here, bf16[4,4,32,1024]{3,2,1,0:T(8,128)(2,1)} %copy-done.2, bf16[4,4,32,1024]{3,2,1,0:T(8,128)(2,1)} %copy-done.4, ...), custom_call_target="tpu_custom_call" | custom-call | tf_op jit(solution)/shard_map/pallas_call | solution.py:374
  67.6 1.9 collective-permute-start.21
  69.5 1.1 pad_maximum_fusion.1.refs_7_.refs_1_
  70.6 3.2 %collective-permute-start.20 = (bf16[4,4,32,1024]{3,2,1,0:T(8,128)(2,1)S(1)}, bf16[4,4,32,1024]{3,2,1,0:T(8,128)(2,1)S(1)}, u32[]{:S(2)}, u32[]{:S(2)}) collective-permute-start(bf16[4,4,32,1024]{3,2,1,0:T(8,128)(2,1)S(1)} %pad_maximum_fusion.1.refs_7_.refs_1_), channel_id=1, source_target_pairs={{0,1},{1,0},{2,3},{3,2},{16,17},{17,16},{18,19},{19,18},{4,5},{5,4... | collective-permute-start | bytes 3145736 | tf_op jit(solution)/shard_map/ppermute | solution.py:414
  73.8 1.1 collective-permute-start.28
  74.8 2.8 %collective-permute-start.29 = (bf16[4,256,128]{2,1,0:T(8,128)(2,1)}, bf16[4,256,128]{2,1,0:T(8,128)(2,1)}, u32[]{:S(2)}, u32[]{:S(2)}) collective-permute-start(bf16[4,256,128]{2,1,0:T(8,128)(2,1)} %bitcast.55), channel_id=1, source_target_pairs={{0,8},{4,12},{8,0},{12,4},{1,9},{5,13},{9,1},{13,5},{2,10},{6,14},... | collective-permute-start | bytes 786440 | tf_op jit(solution)/shard_map/ppermute | solution.py:414
  77.7 5.3 %shard_map.77 = (bf16[512,512]{1,0:T(8,128)(2,1)}, bf16[4,32,512]{2,1,0:T(8,128)(2,1)}, bf16[4,32,512]{2,1,0:T(8,128)(2,1)}, bf16[6,32,512]{2,1,0:T(8,128)(2,1)}, bf16[6,32,512]{2,1,0:T(8,128)(2,1)}) custom-call(s32[2]{0:T(128)} %pad_add_fusion.refs_0_.here, bf16[4,4,32,1024]{3,2,1,0:T(8,128)(2,1)} %copy-done.2, bf16[4,4,32,1024]{3,2,1,0:T(8,128)(2,1)} %copy-done.4, ...), custom_call_target="tpu_custom_call" | custom-call | tf_op jit(solution)/shard_map/pallas_call | solution.py:374
  83.0 3.2 %collective-permute-start.22 = (bf16[4,32,512]{2,1,0:T(8,128)(2,1)}, bf16[4,32,512]{2,1,0:T(8,128)(2,1)S(1)}, u32[]{:S(2)}, u32[]{:S(2)}) collective-permute-start(bf16[4,32,512]{2,1,0:T(8,128)(2,1)} %get-tuple-element.89), channel_id=1, source_target_pairs={{4,0},{8,4},{12,8},{5,1},{9,5},{13,9},{6,2},{10,6},{14,10},{7,3},{... | collective-permute-start | bytes 393224 | tf_op jit(solution)/shard_map/ppermute | solution.py:456
  86.9 15.6 %collective-permute-done.22.refs_2_ = bf16[4,32,512]{2,1,0:T(8,128)(2,1)S(1)} collective-permute-done((bf16[4,32,512]{2,1,0:T(8,128)(2,1)}, bf16[4,32,512]{2,1,0:T(8,128)(2,1)S(1)}, u32[]{:S(2)}, u32[]{:S(2)}) %collective-permute-start.22) | collective-permute-done | bytes 131104 | tf_op jit(solution)/shard_map/ppermute | solution.py:456
  102.5 1.9 collective-permute-start.11
  105.1 3.1 %collective-permute-done.11.refs_2_ = bf16[4,32,512]{2,1,0:T(8,128)(2,1)S(1)} collective-permute-done((bf16[4,32,512]{2,1,0:T(8,128)(2,1)S(1)}, bf16[4,32,512]{2,1,0:T(8,128)(2,1)S(1)}, u32[]{:S(2)}, u32[]{:S(2)}) %collective-permute-start.11) | collective-permute-done | bytes 131104 | tf_op jit(solution)/shard_map/ppermute | solution.py:455
  108.2 1.9 collective-permute-start.12
  110.8 1.3 collective-permute-start.23
  112.1 1.9 collective-permute-done.12.refs_3_
  113.9 6.0 %collective-permute-start.24 = (bf16[6,32,512]{2,1,0:T(8,128)(2,1)}, bf16[6,32,512]{2,1,0:T(8,128)(2,1)}, u32[]{:S(2)}, u32[]{:S(2)}) collective-permute-start(bf16[6,32,512]{2,1,0:T(8,128)(2,1)} %get-tuple-element.134), channel_id=1, source_target_pairs={{1,0},{2,1},{3,2},{5,4},{6,5},{7,6},{9,8},{10,9},{11,10},{13,12},{... | collective-permute-start | bytes 589832 | tf_op jit(solution)/shard_map/ppermute | solution.py:464
  121.2 1.3 collective-permute-start.13
  122.5 3.7 %collective-permute-start.14 = (bf16[6,32,512]{2,1,0:T(8,128)(2,1)}, bf16[6,32,512]{2,1,0:T(8,128)(2,1)}, u32[]{:S(2)}, u32[]{:S(2)}) collective-permute-start(bf16[6,32,512]{2,1,0:T(8,128)(2,1)} %get-tuple-element.138), channel_id=1, source_target_pairs={{1,0},{2,1},{3,2},{5,4},{6,5},{7,6},{9,8},{10,9},{11,10},{13,12},{... | collective-permute-start | bytes 589832 | tf_op jit(solution)/shard_map/ppermute | solution.py:464
  126.3 5.6 %shard_map.79 = (bf16[512,512]{1,0:T(8,128)(2,1)}, f32[4,4,32,512]{3,2,1,0:T(8,128)}) custom-call(s32[2]{0:T(128)} %pad_add_fusion.refs_0_.here, bf16[4,4,32,512]{3,2,1,0:T(8,128)(2,1)} %bitcast.68, bf16[4,32,512]{2,1,0:T(8,128)(2,1)} %copy-done.14, bf16[4,32,512]{2,1,0:T(8,128)(2,1)} %copy-done.17, bf16[6,32,512]{2,1,0:T(8,128)(2,1)} %copy-done.26, ...), custom_call_target="tpu_custom_call" | custom-call | tf_op jit(solution)/shard_map/pallas_call | solution.py:271
  131.9 1.0 copy-done.3
  132.9 5.5 %shard_map.82 = (bf16[512,512]{1,0:T(8,128)(2,1)}, bf16[4,32,512]{2,1,0:T(8,128)(2,1)}, bf16[4,32,512]{2,1,0:T(8,128)(2,1)}, bf16[6,32,512]{2,1,0:T(8,128)(2,1)}, bf16[6,32,512]{2,1,0:T(8,128)(2,1)}) custom-call(s32[2]{0:T(128)} %pad_add_fusion.refs_0_.here, bf16[4,4,32,1024]{3,2,1,0:T(8,128)(2,1)} %copy-done.1, bf16[4,4,32,1024]{3,2,1,0:T(8,128)(2,1)} %copy-done.3, ...), custom_call_target="tpu_custom_call" | custom-call | tf_op jit(solution)/shard_map/pallas_call | solution.py:374
  138.4 2.8 %collective-permute-start.35 = (bf16[4,32,512]{2,1,0:T(8,128)(2,1)}, bf16[4,32,512]{2,1,0:T(8,128)(2,1)S(1)}, u32[]{:S(2)}, u32[]{:S(2)}) collective-permute-start(bf16[4,32,512]{2,1,0:T(8,128)(2,1)} %get-tuple-element.109), channel_id=1, source_target_pairs={{0,4},{4,8},{8,12},{1,5},{5,9},{9,13},{2,6},{6,10},{10,14},{3,7},{... | collective-permute-start | bytes 393224 | tf_op jit(solution)/shard_map/ppermute | solution.py:455
  141.2 2.4 %collective-permute-start.36 = (bf16[4,32,512]{2,1,0:T(8,128)(2,1)}, bf16[4,32,512]{2,1,0:T(8,128)(2,1)S(1)}, u32[]{:S(2)}, u32[]{:S(2)}) collective-permute-start(bf16[4,32,512]{2,1,0:T(8,128)(2,1)} %get-tuple-element.110), channel_id=1, source_target_pairs={{4,0},{8,4},{12,8},{5,1},{9,5},{13,9},{6,2},{10,6},{14,10},{7,3},{... | collective-permute-start | bytes 393224 | tf_op jit(solution)/shard_map/ppermute | solution.py:456
  143.7 8.4 %shard_map.80 = (bf16[4,256,128]{2,1,0:T(8,128)(2,1)}, bf16[4,256,128]{2,1,0:T(8,128)(2,1)}, bf16[4,256,128]{2,1,0:T(8,128)(2,1)}, bf16[4,256,128]{2,1,0:T(8,128)(2,1)}, f32[4,4,32,512]{3,2,1,0:T(8,128)}) custom-call(s32[2]{0:T(128)} %pad_add_fusion.refs_0_.here, bf16[4,4,32,512]{3,2,1,0:T(8,128)(2,1)} %bitcast.67, bf16[4,32,512]{2,1,0:T(8,128)(2,1)} %copy-done.15, ...), custom_call_target="tpu_custom_call" | custom-call | tf_op jit(solution)/shard_map/pallas_call | solution.py:271
  152.1 5.6 %shard_map.81 = (bf16[512,512]{1,0:T(8,128)(2,1)}, bf16[4,32,512]{2,1,0:T(8,128)(2,1)}, bf16[4,32,512]{2,1,0:T(8,128)(2,1)}, bf16[6,32,512]{2,1,0:T(8,128)(2,1)}, bf16[6,32,512]{2,1,0:T(8,128)(2,1)}) custom-call(s32[2]{0:T(128)} %pad_add_fusion.refs_0_.here, bf16[4,4,32,1024]{3,2,1,0:T(8,128)(2,1)} %copy-done.1, bf16[4,4,32,1024]{3,2,1,0:T(8,128)(2,1)} %copy-done.3, ...), custom_call_target="tpu_custom_call" | custom-call | tf_op jit(solution)/shard_map/pallas_call | solution.py:374
  157.8 2.8 %collective-permute-start.31 = (bf16[4,32,512]{2,1,0:T(8,128)(2,1)}, bf16[4,32,512]{2,1,0:T(8,128)(2,1)S(1)}, u32[]{:S(2)}, u32[]{:S(2)}) collective-permute-start(bf16[4,32,512]{2,1,0:T(8,128)(2,1)} %get-tuple-element.103), channel_id=1, source_target_pairs={{0,4},{4,8},{8,12},{1,5},{5,9},{9,13},{2,6},{6,10},{10,14},{3,7},{... | collective-permute-start | bytes 393224 | tf_op jit(solution)/shard_map/ppermute | solution.py:455
  160.6 2.4 %collective-permute-start.32 = (bf16[4,32,512]{2,1,0:T(8,128)(2,1)}, bf16[4,32,512]{2,1,0:T(8,128)(2,1)S(1)}, u32[]{:S(2)}, u32[]{:S(2)}) collective-permute-start(bf16[4,32,512]{2,1,0:T(8,128)(2,1)} %get-tuple-element.104), channel_id=1, source_target_pairs={{4,0},{8,4},{12,8},{5,1},{9,5},{13,9},{6,2},{10,6},{14,10},{7,3},{... | collective-permute-start | bytes 393224 | tf_op jit(solution)/shard_map/ppermute | solution.py:456
  163.2 2.1 collective-permute-start.26
  167.1 1.3 collective-permute-start.37
  169.1 4.9 %collective-permute-start.38 = (bf16[6,32,512]{2,1,0:T(8,128)(2,1)}, bf16[6,32,512]{2,1,0:T(8,128)(2,1)S(1)}, u32[]{:S(2)}, u32[]{:S(2)}) collective-permute-start(bf16[6,32,512]{2,1,0:T(8,128)(2,1)} %get-tuple-element.126), channel_id=1, source_target_pairs={{1,0},{2,1},{3,2},{5,4},{6,5},{7,6},{9,8},{10,9},{11,10},{13,12},{... | collective-permute-start | bytes 589832 | tf_op jit(solution)/shard_map/ppermute | solution.py:464
  174.6 1.3 collective-permute-start.33
  175.9 5.2 %collective-permute-start.34 = (bf16[6,32,512]{2,1,0:T(8,128)(2,1)}, bf16[6,32,512]{2,1,0:T(8,128)(2,1)S(1)}, u32[]{:S(2)}, u32[]{:S(2)}) collective-permute-start(bf16[6,32,512]{2,1,0:T(8,128)(2,1)} %get-tuple-element.130), channel_id=1, source_target_pairs={{1,0},{2,1},{3,2},{5,4},{6,5},{7,6},{9,8},{10,9},{11,10},{13,12},{... | collective-permute-start | bytes 589832 | tf_op jit(solution)/shard_map/ppermute | solution.py:464
  181.2 5.0 %shard_map.83.refs_9_ = bf16[512,512]{1,0:T(8,128)(2,1)} custom-call(s32[2]{0:T(128)} %pad_add_fusion.refs_0_.here, bf16[4,4,32,512]{3,2,1,0:T(8,128)(2,1)} %bitcast.69, bf16[4,32,512]{2,1,0:T(8,128)(2,1)} %copy-done.18, bf16[4,32,512]{2,1,0:T(8,128)(2,1)} %copy-done.19, bf16[6,32,512]{2,1,0:T(8,128)(2,1)} %copy-done.27, bf16[6,32,512]{2,1,0:T(8,128)(2,1)} %copy-done.28, ...), custom_call_target="tpu_custom_call" | custom-call | tf_op jit(solution)/shard_map/pallas_call | solution.py:271
  187.0 8.1 %shard_map.84 = (bf16[4,256,128]{2,1,0:T(8,128)(2,1)}, bf16[4,256,128]{2,1,0:T(8,128)(2,1)}, bf16[4,256,128]{2,1,0:T(8,128)(2,1)}, bf16[4,256,128]{2,1,0:T(8,128)(2,1)}) custom-call(s32[2]{0:T(128)} %pad_add_fusion.refs_0_.here, bf16[4,4,32,512]{3,2,1,0:T(8,128)(2,1)} %bitcast.66, bf16[4,32,512]{2,1,0:T(8,128)(2,1)} %copy-done.12, ...), custom_call_target="tpu_custom_call" | custom-call | tf_op jit(solution)/shard_map/pallas_call | solution.py:271
  195.1 2.2 collective-permute-start.39
  197.5 1.3 collective-permute-start.41
  202.2 12.3 %collective-permute-done.39 = bf16[4,256,128]{2,1,0:T(8,128)(2,1)S(1)} collective-permute-done((bf16[4,256,128]{2,1,0:T(8,128)(2,1)}, bf16[4,256,128]{2,1,0:T(8,128)(2,1)S(1)}, u32[]{:S(2)}, u32[]{:S(2)}) %collective-permute-start.39) | collective-permute-done | bytes 262176 | tf_op jit(solution)/shard_map/ppermute | solution.py:414
  214.7 6.5 %collective-permute-done.40 = bf16[4,256,128]{2,1,0:T(8,128)(2,1)S(1)} collective-permute-done((bf16[4,256,128]{2,1,0:T(8,128)(2,1)}, bf16[4,256,128]{2,1,0:T(8,128)(2,1)S(1)}, u32[]{:S(2)}, u32[]{:S(2)}) %collective-permute-start.40) | collective-permute-done | bytes 262176 | tf_op jit(solution)/shard_map/ppermute | solution.py:414
  221.9 1.0 copy-done.11
  (146 shorter events, 20.6 us)
Async XLA Ops:
  0.6 8.8 %copy-start = (bf16[256,4,512]{2,1,0:T(4,128)(2,1)S(1)}, bf16[256,4,512]{2,1,0:T(4,128)(2,1)}, u32[]{:S(2)}) copy-start(bf16[256,4,512]{2,1,0:T(4,128)(2,1)} %param.7) | copy-start | bytes 3145732
  0.6 6.4 %copy-start.9 = (bf16[256,4,512]{2,1,0:T(4,128)(2,1)S(1)}, bf16[256,4,512]{2,1,0:T(4,128)(2,1)}, u32[]{:S(2)}) copy-start(bf16[256,4,512]{2,1,0:T(4,128)(2,1)} %param.6) | copy-start | bytes 3145732
  1.7 3.1 %collective-permute-start = (bf16[1,32,1024]{2,1,0:T(8,128)(2,1)S(1)}, bf16[1,32,1024]{2,1,0:T(8,128)(2,1)S(1)}, u32[]{:S(2)}, u32[]{:S(2)}) collective-permute-start(bf16[1,32,1024]{2,1,0:T(8,128)(2,1)S(1)} %dynamic-slice_bitcast_fusion.1), channel_id=1, source_target_pairs={{0,12},{4,8},{8,4},{12,0},{1,13},{5,9},{9,5},{13,1},{2,14},{6,10},... | collective-permute-start | bytes 196616 | tf_op jit(solution)/shard_map/ppermute | solution.py:414
  4.8 4.6 %collective-permute-start.1 = (bf16[2,32,1024]{2,1,0:T(8,128)(2,1)S(1)}, bf16[2,32,1024]{2,1,0:T(8,128)(2,1)S(1)}, u32[]{:S(2)}, u32[]{:S(2)}) collective-permute-start(bf16[2,32,1024]{2,1,0:T(8,128)(2,1)S(1)} %pad_maximum_fusion.4), channel_id=1, source_target_pairs={{0,4},{4,0},{8,12},{12,8},{1,5},{5,1},{9,13},{13,9},{2,6},{6,2},{1... | collective-permute-start | bytes 393224 | tf_op jit(solution)/shard_map/ppermute | solution.py:414
  12.0 5.2 %collective-permute-start.2 = (bf16[4,32,1024]{2,1,0:T(8,128)(2,1)S(1)}, bf16[4,32,1024]{2,1,0:T(8,128)(2,1)S(1)}, u32[]{:S(2)}, u32[]{:S(2)}) collective-permute-start(bf16[4,32,1024]{2,1,0:T(8,128)(2,1)S(1)} %pad_maximum_fusion.2), channel_id=1, source_target_pairs={{0,16},{1,17},{2,18},{3,19},{16,0},{17,1},{18,2},{19,3},{4,20},{5,... | collective-permute-start | bytes 786440 | tf_op jit(solution)/shard_map/ppermute | solution.py:414
  13.2 5.5 %collective-permute-start.3 = (bf16[4,32,1024]{2,1,0:T(8,128)(2,1)S(1)}, bf16[4,32,1024]{2,1,0:T(8,128)(2,1)S(1)}, u32[]{:S(2)}, u32[]{:S(2)}) collective-permute-start(bf16[4,32,1024]{2,1,0:T(8,128)(2,1)S(1)} %pad_maximum_fusion.2), channel_id=1, source_target_pairs={{0,2},{1,3},{2,0},{3,1},{16,18},{17,19},{18,16},{19,17},{4,6},{5,7... | collective-permute-start | bytes 786440 | tf_op jit(solution)/shard_map/ppermute | solution.py:414
  18.8 5.3 %collective-permute-start.4 = (bf16[4,32,1024]{2,1,0:T(8,128)(2,1)S(1)}, bf16[4,32,1024]{2,1,0:T(8,128)(2,1)S(1)}, u32[]{:S(2)}, u32[]{:S(2)}) collective-permute-start(bf16[4,32,1024]{2,1,0:T(8,128)(2,1)S(1)} %broadcast_select_fusion.1), channel_id=1, source_target_pairs={{0,2},{1,17},{2,0},{3,19},{16,18},{17,1},{18,16},{19,3},{4,6},{5,2... | collective-permute-start | bytes 786440 | tf_op jit(solution)/shard_map/ppermute | solution.py:414
  19.7 10.2 %collective-permute-start.15 = (bf16[1,32,1024]{2,1,0:T(8,128)(2,1)S(1)}, bf16[1,32,1024]{2,1,0:T(8,128)(2,1)S(1)}, u32[]{:S(2)}, u32[]{:S(2)}) collective-permute-start(bf16[1,32,1024]{2,1,0:T(8,128)(2,1)S(1)} %dynamic-slice_bitcast_fusion), channel_id=1, source_target_pairs={{0,12},{4,8},{8,4},{12,0},{1,13},{5,9},{9,5},{13,1},{2,14},{6,10},... | collective-permute-start | bytes 196616 | tf_op jit(solution)/shard_map/ppermute | solution.py:414
  24.2 27.3 %copy-start.2 = (bf16[4,4,32,1024]{3,2,1,0:T(8,128)(2,1)}, bf16[4,4,32,1024]{3,2,1,0:T(8,128)(2,1)S(1)}, u32[]{:S(2)}) copy-start(bf16[4,4,32,1024]{3,2,1,0:T(8,128)(2,1)S(1)} %pad_maximum_fusion.refs_1_.refs_7_) | copy-start | bytes 3145732
  24.2 37.1 %collective-permute-start.5 = (bf16[4,4,32,1024]{3,2,1,0:T(8,128)(2,1)S(1)}, bf16[4,4,32,1024]{3,2,1,0:T(8,128)(2,1)S(1)}, u32[]{:S(2)}, u32[]{:S(2)}) collective-permute-start(bf16[4,4,32,1024]{3,2,1,0:T(8,128)(2,1)S(1)} %pad_maximum_fusion.refs_1_.refs_7_), channel_id=1, source_target_pairs={{0,1},{1,0},{2,3},{3,2},{16,17},{17,16},{18,19},{19,18},{4,5},{5,4... | collective-permute-start | bytes 3145736 | tf_op jit(solution)/shard_map/ppermute | solution.py:414
  30.0 6.1 %copy-start.29 = (f32[256,27]{0,1:T(8,128)S(1)}, f32[256,27]{0,1:T(8,128)}, u32[]{:S(2)}) copy-start(f32[256,27]{0,1:T(8,128)} %param.10) | copy-start | bytes 82948
  30.0 7.1 %copy-start.23 = (bf16[256,4,128]{2,0,1:T(8,128)(2,1)S(1)}, bf16[256,4,128]{2,0,1:T(8,128)(2,1)}, u32[]{:S(2)}) copy-start(bf16[256,4,128]{2,0,1:T(8,128)(2,1)} %copy.48) | copy-start | bytes 786436
  30.0 8.9 %copy-start.22 = (bf16[256,4,128]{2,0,1:T(8,128)(2,1)S(1)}, bf16[256,4,128]{2,0,1:T(8,128)(2,1)}, u32[]{:S(2)}) copy-start(bf16[256,4,128]{2,0,1:T(8,128)(2,1)} %copy.49) | copy-start | bytes 786436
  30.0 5.1 %collective-permute-start.16 = (bf16[2,32,1024]{2,1,0:T(8,128)(2,1)S(1)}, bf16[2,32,1024]{2,1,0:T(8,128)(2,1)S(1)}, u32[]{:S(2)}, u32[]{:S(2)}) collective-permute-start(bf16[2,32,1024]{2,1,0:T(8,128)(2,1)S(1)} %pad_maximum_fusion.6), channel_id=1, source_target_pairs={{0,4},{4,0},{8,12},{12,8},{1,5},{5,1},{9,13},{13,9},{2,6},{6,2},{1... | collective-permute-start | bytes 393224 | tf_op jit(solution)/shard_map/ppermute | solution.py:414
  35.1 7.5 %collective-permute-start.17 = (bf16[4,32,1024]{2,1,0:T(8,128)(2,1)S(1)}, bf16[4,32,1024]{2,1,0:T(8,128)(2,1)S(1)}, u32[]{:S(2)}, u32[]{:S(2)}) collective-permute-start(bf16[4,32,1024]{2,1,0:T(8,128)(2,1)S(1)} %get-tuple-element.125), channel_id=1, source_target_pairs={{0,2},{1,3},{2,0},{3,1},{16,18},{17,19},{18,16},{19,17},{4,6},{5,7... | collective-permute-start | bytes 786440 | tf_op jit(solution)/shard_map/ppermute | solution.py:414
  35.2 7.5 %collective-permute-start.18 = (bf16[4,32,1024]{2,1,0:T(8,128)(2,1)S(1)}, bf16[4,32,1024]{2,1,0:T(8,128)(2,1)S(1)}, u32[]{:S(2)}, u32[]{:S(2)}) collective-permute-start(bf16[4,32,1024]{2,1,0:T(8,128)(2,1)S(1)} %get-tuple-element.125), channel_id=1, source_target_pairs={{0,16},{1,17},{2,18},{3,19},{16,0},{17,1},{18,2},{19,3},{4,20},{5,... | collective-permute-start | bytes 786440 | tf_op jit(solution)/shard_map/ppermute | solution.py:414
  36.1 2.8 %collective-permute-start.6 = (f32[1,28,256]{2,1,0:T(8,128)S(1)}, f32[1,28,256]{2,1,0:T(8,128)S(1)}, u32[]{:S(2)}, u32[]{:S(2)}) collective-permute-start(f32[1,28,256]{2,1,0:T(8,128)S(1)} %maximum_bitcast_fusion), channel_id=1, source_target_pairs={{0,12},{4,8},{8,4},{12,0},{1,13},{5,9},{9,5},{13,1},{2,14},{6,10},... | collective-permute-start | bytes 86024 | tf_op jit(solution)/shard_map/ppermute | solution.py:414
  37.1 15.0 %collective-permute-start.10 = (bf16[4,256,128]{2,1,0:T(8,128)(2,1)S(1)}, bf16[4,256,128]{2,1,0:T(8,128)(2,1)S(1)}, u32[]{:S(2)}, u32[]{:S(2)}) collective-permute-start(bf16[4,256,128]{2,1,0:T(8,128)(2,1)S(1)} %bitcast.79), channel_id=1, source_target_pairs={{0,12},{4,8},{8,4},{12,0},{1,13},{5,9},{9,5},{13,1},{2,14},{6,10},... | collective-permute-start | bytes 786440 | tf_op jit(solution)/shard_map/ppermute | solution.py:414
  38.9 21.0 %collective-permute-start.9 = (bf16[4,256,128]{2,1,0:T(8,128)(2,1)S(1)}, bf16[4,256,128]{2,1,0:T(8,128)(2,1)S(1)}, u32[]{:S(2)}, u32[]{:S(2)}) collective-permute-start(bf16[4,256,128]{2,1,0:T(8,128)(2,1)S(1)} %bitcast.78), channel_id=1, source_target_pairs={{0,8},{4,12},{8,0},{12,4},{1,9},{5,13},{9,1},{13,5},{2,10},{6,14},... | collective-permute-start | bytes 786440 | tf_op jit(solution)/shard_map/ppermute | solution.py:414
  42.7 7.2 %collective-permute-start.7 = (f32[2,28,256]{2,1,0:T(8,128)S(1)}, f32[2,28,256]{2,1,0:T(8,128)S(1)}, u32[]{:S(2)}, u32[]{:S(2)}) collective-permute-start(f32[2,28,256]{2,1,0:T(8,128)S(1)} %pad_maximum_fusion.7), channel_id=1, source_target_pairs={{0,4},{4,0},{8,12},{12,8},{1,5},{5,1},{9,13},{13,9},{2,6},{6,2},{1... | collective-permute-start | bytes 172040 | tf_op jit(solution)/shard_map/ppermute | solution.py:414
  42.8 17.8 %collective-permute-start.8 = (bf16[4,256,128]{2,1,0:T(8,128)(2,1)S(1)}, bf16[4,256,128]{2,1,0:T(8,128)(2,1)S(1)}, u32[]{:S(2)}, u32[]{:S(2)}) collective-permute-start(bf16[4,256,128]{2,1,0:T(8,128)(2,1)S(1)} %get-tuple-element.78), channel_id=1, source_target_pairs={{0,4},{4,0},{8,12},{12,8},{1,5},{5,1},{9,13},{13,9},{2,6},{6,2},{1... | collective-permute-start | bytes 786440 | tf_op jit(solution)/shard_map/ppermute | solution.py:414
  49.9 19.6 %collective-permute-start.19 = (bf16[4,32,1024]{2,1,0:T(8,128)(2,1)}, bf16[4,32,1024]{2,1,0:T(8,128)(2,1)}, u32[]{:S(2)}, u32[]{:S(2)}) collective-permute-start(bf16[4,32,1024]{2,1,0:T(8,128)(2,1)} %broadcast_select_fusion), channel_id=1, source_target_pairs={{0,2},{1,17},{2,0},{3,19},{16,18},{17,1},{18,16},{19,3},{4,6},{5,2... | collective-permute-start | bytes 786440 | tf_op jit(solution)/shard_map/ppermute | solution.py:414
  52.1 9.1 %copy-start.6 = (bf16[4,256,128]{2,1,0:T(8,128)(2,1)}, bf16[4,256,128]{2,1,0:T(8,128)(2,1)S(1)}, u32[]{:S(2)}) copy-start(bf16[4,256,128]{2,1,0:T(8,128)(2,1)S(1)} %collective-permute-done.10.refs_6_.refs_13_) | copy-start | bytes 786436
  67.6 15.5 %collective-permute-start.21 = (bf16[4,32,512]{2,1,0:T(8,128)(2,1)}, bf16[4,32,512]{2,1,0:T(8,128)(2,1)S(1)}, u32[]{:S(2)}, u32[]{:S(2)}) collective-permute-start(bf16[4,32,512]{2,1,0:T(8,128)(2,1)} %get-tuple-element.88), channel_id=1, source_target_pairs={{0,4},{4,8},{8,12},{1,5},{5,9},{9,13},{2,6},{6,10},{10,14},{3,7},{... | collective-permute-start | bytes 393224 | tf_op jit(solution)/shard_map/ppermute | solution.py:455
  70.6 12.4 %copy-start.1 = (bf16[4,4,32,1024]{3,2,1,0:T(8,128)(2,1)}, bf16[4,4,32,1024]{3,2,1,0:T(8,128)(2,1)S(1)}, u32[]{:S(2)}) copy-start(bf16[4,4,32,1024]{3,2,1,0:T(8,128)(2,1)S(1)} %pad_maximum_fusion.1.refs_7_.refs_1_) | copy-start | bytes 3145732
  70.6 61.3 %collective-permute-start.20 = (bf16[4,4,32,1024]{3,2,1,0:T(8,128)(2,1)S(1)}, bf16[4,4,32,1024]{3,2,1,0:T(8,128)(2,1)S(1)}, u32[]{:S(2)}, u32[]{:S(2)}) collective-permute-start(bf16[4,4,32,1024]{3,2,1,0:T(8,128)(2,1)S(1)} %pad_maximum_fusion.1.refs_7_.refs_1_), channel_id=1, source_target_pairs={{0,1},{1,0},{2,3},{3,2},{16,17},{17,16},{18,19},{19,18},{4,5},{5,4... | collective-permute-start | bytes 3145736 | tf_op jit(solution)/shard_map/ppermute | solution.py:414
  73.8 37.0 %collective-permute-start.28 = (bf16[4,256,128]{2,1,0:T(8,128)(2,1)}, bf16[4,256,128]{2,1,0:T(8,128)(2,1)S(1)}, u32[]{:S(2)}, u32[]{:S(2)}) collective-permute-start(bf16[4,256,128]{2,1,0:T(8,128)(2,1)} %bitcast.53), channel_id=1, source_target_pairs={{0,4},{4,0},{8,12},{12,8},{1,5},{5,1},{9,13},{13,9},{2,6},{6,2},{1... | collective-permute-start | bytes 786440 | tf_op jit(solution)/shard_map/ppermute | solution.py:414
  74.8 57.0 %collective-permute-start.29 = (bf16[4,256,128]{2,1,0:T(8,128)(2,1)}, bf16[4,256,128]{2,1,0:T(8,128)(2,1)}, u32[]{:S(2)}, u32[]{:S(2)}) collective-permute-start(bf16[4,256,128]{2,1,0:T(8,128)(2,1)} %bitcast.55), channel_id=1, source_target_pairs={{0,8},{4,12},{8,0},{12,4},{1,9},{5,13},{9,1},{13,5},{2,10},{6,14},... | collective-permute-start | bytes 786440 | tf_op jit(solution)/shard_map/ppermute | solution.py:414
  77.7 54.2 %collective-permute-start.30 = (bf16[4,256,128]{2,1,0:T(8,128)(2,1)}, bf16[4,256,128]{2,1,0:T(8,128)(2,1)}, u32[]{:S(2)}, u32[]{:S(2)}) collective-permute-start(bf16[4,256,128]{2,1,0:T(8,128)(2,1)} %bitcast.54), channel_id=1, source_target_pairs={{0,12},{4,8},{8,4},{12,0},{1,13},{5,9},{9,5},{13,1},{2,14},{6,10},... | collective-permute-start | bytes 786440 | tf_op jit(solution)/shard_map/ppermute | solution.py:414
  83.0 19.5 %copy-start.35 = (bf16[4,32,512]{2,1,0:T(8,128)(2,1)S(1)}, bf16[4,32,512]{2,1,0:T(8,128)(2,1)}, u32[]{:S(2)}) copy-start(bf16[4,32,512]{2,1,0:T(8,128)(2,1)} %get-tuple-element.82) | copy-start | bytes 393220
  83.0 22.0 %copy-start.14 = (bf16[4,32,512]{2,1,0:T(8,128)(2,1)}, bf16[4,32,512]{2,1,0:T(8,128)(2,1)S(1)}, u32[]{:S(2)}) copy-start(bf16[4,32,512]{2,1,0:T(8,128)(2,1)S(1)} %collective-permute-done.21.refs_1_) | copy-start | bytes 393220
  83.0 19.5 %collective-permute-start.22 = (bf16[4,32,512]{2,1,0:T(8,128)(2,1)}, bf16[4,32,512]{2,1,0:T(8,128)(2,1)S(1)}, u32[]{:S(2)}, u32[]{:S(2)}) collective-permute-start(bf16[4,32,512]{2,1,0:T(8,128)(2,1)} %get-tuple-element.89), channel_id=1, source_target_pairs={{4,0},{8,4},{12,8},{5,1},{9,5},{13,9},{6,2},{10,6},{14,10},{7,3},{... | collective-permute-start | bytes 393224 | tf_op jit(solution)/shard_map/ppermute | solution.py:456
  86.3 21.9 %copy-start.34 = (bf16[4,32,512]{2,1,0:T(8,128)(2,1)S(1)}, bf16[4,32,512]{2,1,0:T(8,128)(2,1)}, u32[]{:S(2)}) copy-start(bf16[4,32,512]{2,1,0:T(8,128)(2,1)} %get-tuple-element.83) | copy-start | bytes 393220
  102.5 8.3 %copy-start.17 = (bf16[4,32,512]{2,1,0:T(8,128)(2,1)}, bf16[4,32,512]{2,1,0:T(8,128)(2,1)S(1)}, u32[]{:S(2)}) copy-start(bf16[4,32,512]{2,1,0:T(8,128)(2,1)S(1)} %collective-permute-done.22.refs_2_) | copy-start | bytes 393220
  102.5 5.7 %collective-permute-start.11 = (bf16[4,32,512]{2,1,0:T(8,128)(2,1)S(1)}, bf16[4,32,512]{2,1,0:T(8,128)(2,1)S(1)}, u32[]{:S(2)}, u32[]{:S(2)}) collective-permute-start(bf16[4,32,512]{2,1,0:T(8,128)(2,1)S(1)} %copy-done.35), channel_id=1, source_target_pairs={{0,4},{4,8},{8,12},{1,5},{5,9},{9,13},{2,6},{6,10},{10,14},{3,7},{... | collective-permute-start | bytes 393224 | tf_op jit(solution)/shard_map/ppermute | solution.py:455
  108.2 12.3 %copy-start.15 = (bf16[4,32,512]{2,1,0:T(8,128)(2,1)}, bf16[4,32,512]{2,1,0:T(8,128)(2,1)S(1)}, u32[]{:S(2)}) copy-start(bf16[4,32,512]{2,1,0:T(8,128)(2,1)S(1)} %collective-permute-done.11.refs_2_) | copy-start | bytes 393220
  108.2 5.7 %collective-permute-start.12 = (bf16[4,32,512]{2,1,0:T(8,128)(2,1)S(1)}, bf16[4,32,512]{2,1,0:T(8,128)(2,1)S(1)}, u32[]{:S(2)}, u32[]{:S(2)}) collective-permute-start(bf16[4,32,512]{2,1,0:T(8,128)(2,1)S(1)} %copy-done.34), channel_id=1, source_target_pairs={{4,0},{8,4},{12,8},{5,1},{9,5},{13,9},{6,2},{10,6},{14,10},{7,3},{... | collective-permute-start | bytes 393224 | tf_op jit(solution)/shard_map/ppermute | solution.py:456
  110.8 21.1 %copy-start.5 = (bf16[4,256,128]{2,1,0:T(8,128)(2,1)}, bf16[4,256,128]{2,1,0:T(8,128)(2,1)S(1)}, u32[]{:S(2)}) copy-start(bf16[4,256,128]{2,1,0:T(8,128)(2,1)S(1)} %collective-permute-done.28.refs_4_.refs_11_) | copy-start | bytes 786436
  110.8 9.8 %collective-permute-start.23 = (bf16[6,32,512]{2,1,0:T(8,128)(2,1)}, bf16[6,32,512]{2,1,0:T(8,128)(2,1)S(1)}, u32[]{:S(2)}, u32[]{:S(2)}) collective-permute-start(bf16[6,32,512]{2,1,0:T(8,128)(2,1)} %get-tuple-element.135), channel_id=1, source_target_pairs={{0,1},{1,2},{2,3},{4,5},{5,6},{6,7},{8,9},{9,10},{10,11},{12,13},{... | collective-permute-start | bytes 589832 | tf_op jit(solution)/shard_map/ppermute | solution.py:463
  113.9 17.9 %copy-start.16 = (bf16[4,32,512]{2,1,0:T(8,128)(2,1)}, bf16[4,32,512]{2,1,0:T(8,128)(2,1)S(1)}, u32[]{:S(2)}) copy-start(bf16[4,32,512]{2,1,0:T(8,128)(2,1)S(1)} %collective-permute-done.12.refs_3_) | copy-start | bytes 393220
  113.9 8.6 %collective-permute-start.24 = (bf16[6,32,512]{2,1,0:T(8,128)(2,1)}, bf16[6,32,512]{2,1,0:T(8,128)(2,1)}, u32[]{:S(2)}, u32[]{:S(2)}) collective-permute-start(bf16[6,32,512]{2,1,0:T(8,128)(2,1)} %get-tuple-element.134), channel_id=1, source_target_pairs={{1,0},{2,1},{3,2},{5,4},{6,5},{7,6},{9,8},{10,9},{11,10},{13,12},{... | collective-permute-start | bytes 589832 | tf_op jit(solution)/shard_map/ppermute | solution.py:464
  121.2 22.4 %collective-permute-start.13 = (bf16[6,32,512]{2,1,0:T(8,128)(2,1)}, bf16[6,32,512]{2,1,0:T(8,128)(2,1)}, u32[]{:S(2)}, u32[]{:S(2)}) collective-permute-start(bf16[6,32,512]{2,1,0:T(8,128)(2,1)} %get-tuple-element.139), channel_id=1, source_target_pairs={{0,1},{1,2},{2,3},{4,5},{5,6},{6,7},{8,9},{9,10},{10,11},{12,13},{... | collective-permute-start | bytes 589832 | tf_op jit(solution)/shard_map/ppermute | solution.py:463
  122.5 21.1 %collective-permute-start.14 = (bf16[6,32,512]{2,1,0:T(8,128)(2,1)}, bf16[6,32,512]{2,1,0:T(8,128)(2,1)}, u32[]{:S(2)}, u32[]{:S(2)}) collective-permute-start(bf16[6,32,512]{2,1,0:T(8,128)(2,1)} %get-tuple-element.138), channel_id=1, source_target_pairs={{1,0},{2,1},{3,2},{5,4},{6,5},{7,6},{9,8},{10,9},{11,10},{13,12},{... | collective-permute-start | bytes 589832 | tf_op jit(solution)/shard_map/ppermute | solution.py:464
  138.4 24.8 %collective-permute-start.35 = (bf16[4,32,512]{2,1,0:T(8,128)(2,1)}, bf16[4,32,512]{2,1,0:T(8,128)(2,1)S(1)}, u32[]{:S(2)}, u32[]{:S(2)}) collective-permute-start(bf16[4,32,512]{2,1,0:T(8,128)(2,1)} %get-tuple-element.109), channel_id=1, source_target_pairs={{0,4},{4,8},{8,12},{1,5},{5,9},{9,13},{2,6},{6,10},{10,14},{3,7},{... | collective-permute-start | bytes 393224 | tf_op jit(solution)/shard_map/ppermute | solution.py:455
  141.2 24.7 %collective-permute-start.36 = (bf16[4,32,512]{2,1,0:T(8,128)(2,1)}, bf16[4,32,512]{2,1,0:T(8,128)(2,1)S(1)}, u32[]{:S(2)}, u32[]{:S(2)}) collective-permute-start(bf16[4,32,512]{2,1,0:T(8,128)(2,1)} %get-tuple-element.110), channel_id=1, source_target_pairs={{4,0},{8,4},{12,8},{5,1},{9,5},{13,9},{6,2},{10,6},{14,10},{7,3},{... | collective-permute-start | bytes 393224 | tf_op jit(solution)/shard_map/ppermute | solution.py:456
  152.1 11.1 %copy-start.32 = (bf16[4,256,128]{2,1,0:T(8,128)(2,1)S(1)}, bf16[4,256,128]{2,1,0:T(8,128)(2,1)}, u32[]{:S(2)}) copy-start(bf16[4,256,128]{2,1,0:T(8,128)(2,1)} %get-tuple-element.95) | copy-start | bytes 786436
  152.1 13.2 %copy-start.33 = (bf16[6,32,512]{2,1,0:T(8,128)(2,1)S(1)}, bf16[6,32,512]{2,1,0:T(8,128)(2,1)}, u32[]{:S(2)}) copy-start(bf16[6,32,512]{2,1,0:T(8,128)(2,1)} %get-tuple-element.111) | copy-start | bytes 589828
  152.1 13.8 %copy-start.31 = (bf16[4,256,128]{2,1,0:T(8,128)(2,1)S(1)}, bf16[4,256,128]{2,1,0:T(8,128)(2,1)}, u32[]{:S(2)}) copy-start(bf16[4,256,128]{2,1,0:T(8,128)(2,1)} %get-tuple-element.96) | copy-start | bytes 786436
  157.8 9.4 %collective-permute-start.31 = (bf16[4,32,512]{2,1,0:T(8,128)(2,1)}, bf16[4,32,512]{2,1,0:T(8,128)(2,1)S(1)}, u32[]{:S(2)}, u32[]{:S(2)}) collective-permute-start(bf16[4,32,512]{2,1,0:T(8,128)(2,1)} %get-tuple-element.103), channel_id=1, source_target_pairs={{0,4},{4,8},{8,12},{1,5},{5,9},{9,13},{2,6},{6,10},{10,14},{3,7},{... | collective-permute-start | bytes 393224 | tf_op jit(solution)/shard_map/ppermute | solution.py:455
  160.6 8.5 %collective-permute-start.32 = (bf16[4,32,512]{2,1,0:T(8,128)(2,1)}, bf16[4,32,512]{2,1,0:T(8,128)(2,1)S(1)}, u32[]{:S(2)}, u32[]{:S(2)}) collective-permute-start(bf16[4,32,512]{2,1,0:T(8,128)(2,1)} %get-tuple-element.104), channel_id=1, source_target_pairs={{4,0},{8,4},{12,8},{5,1},{9,5},{13,9},{6,2},{10,6},{14,10},{7,3},{... | collective-permute-start | bytes 393224 | tf_op jit(solution)/shard_map/ppermute | solution.py:456
  163.1 32.0 %collective-permute-start.25 = (bf16[4,256,128]{2,1,0:T(8,128)(2,1)}, bf16[4,256,128]{2,1,0:T(8,128)(2,1)S(1)}, u32[]{:S(2)}, u32[]{:S(2)}) collective-permute-start(bf16[4,256,128]{2,1,0:T(8,128)(2,1)} %get-tuple-element.94), channel_id=1, source_target_pairs={{0,4},{4,0},{8,12},{12,8},{1,5},{5,1},{9,13},{13,9},{2,6},{6,2},{1... | collective-permute-start | bytes 786440 | tf_op jit(solution)/shard_map/ppermute | solution.py:414
  163.2 31.9 %collective-permute-start.26 = (bf16[4,256,128]{2,1,0:T(8,128)(2,1)S(1)}, bf16[4,256,128]{2,1,0:T(8,128)(2,1)S(1)}, u32[]{:S(2)}, u32[]{:S(2)}) collective-permute-start(bf16[4,256,128]{2,1,0:T(8,128)(2,1)S(1)} %copy-done.32), channel_id=1, source_target_pairs={{0,8},{4,12},{8,0},{12,4},{1,9},{5,13},{9,1},{13,5},{2,10},{6,14},... | collective-permute-start | bytes 786440 | tf_op jit(solution)/shard_map/ppermute | solution.py:414
  165.9 29.2 %collective-permute-start.27 = (bf16[4,256,128]{2,1,0:T(8,128)(2,1)S(1)}, bf16[4,256,128]{2,1,0:T(8,128)(2,1)S(1)}, u32[]{:S(2)}, u32[]{:S(2)}) collective-permute-start(bf16[4,256,128]{2,1,0:T(8,128)(2,1)S(1)} %copy-done.31), channel_id=1, source_target_pairs={{0,12},{4,8},{8,4},{12,0},{1,13},{5,9},{9,5},{13,1},{2,14},{6,10},... | collective-permute-start | bytes 786440 | tf_op jit(solution)/shard_map/ppermute | solution.py:414
  167.1 7.5 %copy-start.12 = (bf16[4,32,512]{2,1,0:T(8,128)(2,1)}, bf16[4,32,512]{2,1,0:T(8,128)(2,1)S(1)}, u32[]{:S(2)}) copy-start(bf16[4,32,512]{2,1,0:T(8,128)(2,1)S(1)} %collective-permute-done.31.refs_2_) | copy-start | bytes 393220
  167.1 7.5 %collective-permute-start.37 = (bf16[6,32,512]{2,1,0:T(8,128)(2,1)S(1)}, bf16[6,32,512]{2,1,0:T(8,128)(2,1)S(1)}, u32[]{:S(2)}, u32[]{:S(2)}) collective-permute-start(bf16[6,32,512]{2,1,0:T(8,128)(2,1)S(1)} %get-tuple-element.127), channel_id=1, source_target_pairs={{0,1},{1,2},{2,3},{4,5},{5,6},{6,7},{8,9},{9,10},{10,11},{12,13},{... | collective-permute-start | bytes 589832 | tf_op jit(solution)/shard_map/ppermute | solution.py:463
  169.1 17.2 %copy-start.13 = (bf16[4,32,512]{2,1,0:T(8,128)(2,1)}, bf16[4,32,512]{2,1,0:T(8,128)(2,1)S(1)}, u32[]{:S(2)}) copy-start(bf16[4,32,512]{2,1,0:T(8,128)(2,1)S(1)} %collective-permute-done.32.refs_3_) | copy-start | bytes 393220
  169.1 6.9 %collective-permute-start.38 = (bf16[6,32,512]{2,1,0:T(8,128)(2,1)}, bf16[6,32,512]{2,1,0:T(8,128)(2,1)S(1)}, u32[]{:S(2)}, u32[]{:S(2)}) collective-permute-start(bf16[6,32,512]{2,1,0:T(8,128)(2,1)} %get-tuple-element.126), channel_id=1, source_target_pairs={{1,0},{2,1},{3,2},{5,4},{6,5},{7,6},{9,8},{10,9},{11,10},{13,12},{... | collective-permute-start | bytes 589832 | tf_op jit(solution)/shard_map/ppermute | solution.py:464
  174.6 6.6 %copy-start.27 = (bf16[6,32,512]{2,1,0:T(8,128)(2,1)}, bf16[6,32,512]{2,1,0:T(8,128)(2,1)S(1)}, u32[]{:S(2)}) copy-start(bf16[6,32,512]{2,1,0:T(8,128)(2,1)S(1)} %collective-permute-done.37.refs_3_) | copy-start | bytes 589828
  174.6 11.7 %collective-permute-start.33 = (bf16[6,32,512]{2,1,0:T(8,128)(2,1)}, bf16[6,32,512]{2,1,0:T(8,128)(2,1)S(1)}, u32[]{:S(2)}, u32[]{:S(2)}) collective-permute-start(bf16[6,32,512]{2,1,0:T(8,128)(2,1)} %get-tuple-element.131), channel_id=1, source_target_pairs={{0,1},{1,2},{2,3},{4,5},{5,6},{6,7},{8,9},{9,10},{10,11},{12,13},{... | collective-permute-start | bytes 589832 | tf_op jit(solution)/shard_map/ppermute | solution.py:463
  175.9 10.4 %collective-permute-start.34 = (bf16[6,32,512]{2,1,0:T(8,128)(2,1)}, bf16[6,32,512]{2,1,0:T(8,128)(2,1)S(1)}, u32[]{:S(2)}, u32[]{:S(2)}) collective-permute-start(bf16[6,32,512]{2,1,0:T(8,128)(2,1)} %get-tuple-element.130), channel_id=1, source_target_pairs={{1,0},{2,1},{3,2},{5,4},{6,5},{7,6},{9,8},{10,9},{11,10},{13,12},{... | collective-permute-start | bytes 589832 | tf_op jit(solution)/shard_map/ppermute | solution.py:464
  195.1 19.3 %collective-permute-start.39 = (bf16[4,256,128]{2,1,0:T(8,128)(2,1)}, bf16[4,256,128]{2,1,0:T(8,128)(2,1)S(1)}, u32[]{:S(2)}, u32[]{:S(2)}) collective-permute-start(bf16[4,256,128]{2,1,0:T(8,128)(2,1)} %get-tuple-element.119), channel_id=1, source_target_pairs={{0,8},{4,12},{8,0},{12,4},{1,9},{5,13},{9,1},{13,5},{2,10},{6,14},... | collective-permute-start | bytes 786440 | tf_op jit(solution)/shard_map/ppermute | solution.py:414
  197.3 24.0 %collective-permute-start.40 = (bf16[4,256,128]{2,1,0:T(8,128)(2,1)}, bf16[4,256,128]{2,1,0:T(8,128)(2,1)S(1)}, u32[]{:S(2)}, u32[]{:S(2)}) collective-permute-start(bf16[4,256,128]{2,1,0:T(8,128)(2,1)} %get-tuple-element.120), channel_id=1, source_target_pairs={{0,12},{4,8},{8,4},{12,0},{1,13},{5,9},{9,5},{13,1},{2,14},{6,10},... | collective-permute-start | bytes 786440 | tf_op jit(solution)/shard_map/ppermute | solution.py:414
  197.5 24.1 %collective-permute-start.41 = (bf16[4,256,128]{2,1,0:T(8,128)(2,1)}, bf16[4,256,128]{2,1,0:T(8,128)(2,1)S(1)}, u32[]{:S(2)}, u32[]{:S(2)}) collective-permute-start(bf16[4,256,128]{2,1,0:T(8,128)(2,1)} %get-tuple-element.121), channel_id=1, source_target_pairs={{0,4},{4,0},{8,12},{12,8},{1,5},{5,1},{9,13},{13,9},{2,6},{6,2},{1... | collective-permute-start | bytes 786440 | tf_op jit(solution)/shard_map/ppermute | solution.py:414
  202.2 19.7 %copy-start.10 = (bf16[256,4,512]{2,1,0:T(4,128)(2,1)}, bf16[256,4,512]{2,1,0:T(4,128)(2,1)S(1)}, u32[]{:S(2)}) copy-start(bf16[256,4,512]{2,1,0:T(4,128)(2,1)S(1)} %copy_dynamic-update-slice_fusion.4) | copy-start | bytes 3145732
  (14 other events, 21.6 us)

commit v11 on v9

--- a/solution.py
+++ b/solution.py
@@ -415,17 +415,19 @@
         return row_low, row_high, plane_low, plane_high
 
     grid = (planes, rows, CX, channels)
-    piece_in, piece_out = (
+    pieces = [
         lax.dynamic_slice_in_dim(weight, seat * share, share, axis=0)
         for weight in (weight_in, weight_out)
-    )
-    column = gather_column(piece_in)
+    ]
+    column = gather_column(jnp.concatenate(pieces))
     vol_cut = cut(volume, shifts, chan)
     later, column = lax.optimization_barrier((chan, column))
     own_cut = cut(volume, [0], later)
     grad_cut = cut(out_grad, shifts + [0], later)
-    full_in, (own_block, here, grad_cut) = gather_weight(column, (own_cut[0], here, grad_cut))
-    full_out, _ = gather_weight(gather_column(piece_out))
+    full_in, (own_block, here, grad_cut) = gather_weight(
+        column[:, :share], (own_cut[0], here, grad_cut)
+    )
+    full_out, _ = gather_weight(column[:, share:])
     table = jnp.concatenate([filter_taps, filter_bias[:, None]], axis=1).T
     taps = gather_column(table)
     own_block, taps = lax.optimization_barrier((own_block, taps))

time: 193 us -> 194 us (level)
  the two profiles are of different devices: /device:TPU:0 before, /device:TPU:17 now
where the time goes in v11:
time: 194 us; the launch traced here: 193 us
  waiting for transfers between devices  69.8 us (36%)
  starting transfers between devices  64.3 us (33%)
  Pallas kernels  37.5 us (19%)
  local copies, waits for them, and re-layouts  18.1 us (9%)
    ppermute x24, waiting for transfers between devices, swap(): return lax.ppermute(part, axes, [(i, partner(i)) for i in range(count)])  49.8 us
    ppermute x24, starting transfers between devices, swap(): return lax.ppermute(part, axes, [(i, partner(i)) for i in range(count)])  36.5 us
    pallas_call x2, Pallas kernels, stencil(): pl.pallas_call(forward_kernel if forward else backward_kernel, grid_spec=...  22.7 us
    pallas_call x2, Pallas kernels, product_call(): pl.pallas_call(lambda *refs: kernel(*refs, count=count), grid_spec=pltpu....  14.8 us
    ppermute x2, starting transfers between devices, halo_of(): plane_low = lax.ppermute(joined(fore, planes - 1), 'space', forward)  11.9 us
    ppermute x2, waiting for transfers between devices, halo_of(): plane_high = lax.ppermute(joined(back, 0), 'space', backward)  9.17 us
    unnamed x54, local copies, waits for them, and re-layouts  7.79 us
    ppermute x2, starting transfers between devices, halo_of(): row_low = lax.ppermute(last, 'chan', forward)  6.55 us
  transfers between devices with their start and end apart: 32, of which 20 were waited for; matrix products, arithmetic and copies ran while one was open for 7% of the time, Pallas kernels for 15%

profile of v11, /device:TPU:17, one launch (start us, length us, event | category | flops | bytes accessed | tf_op | source)
XLA Modules:
  0.0 192.7 jit_solution(16554758063578059507)
XLA Ops:
  0.7 1.0 constant_dynamic-slice_fusion.8
  2.0 5.2 %collective-permute-done = bf16[1,64,1024]{2,1,0:T(8,128)(2,1)S(1)} collective-permute-done((bf16[1,64,1024]{2,1,0:T(8,128)(2,1)S(1)}, bf16[1,64,1024]{2,1,0:T(8,128)(2,1)S(1)}, u32[]{:S(2)}, u32[]{:S(2)}) %collective-permute-start) | collective-permute-done | bytes 131104 | tf_op jit(solution)/shard_map/ppermute | solution.py:364
  7.2 2.3 %collective-permute-start.1 = (bf16[2,64,1024]{2,1,0:T(8,128)(2,1)S(1)}, bf16[2,64,1024]{2,1,0:T(8,128)(2,1)S(1)}, u32[]{:S(2)}, u32[]{:S(2)}) collective-permute-start(bf16[2,64,1024]{2,1,0:T(8,128)(2,1)S(1)} %pad_maximum_fusion.3), channel_id=1, source_target_pairs={{0,4},{4,0},{8,12},{12,8},{1,5},{5,1},{9,13},{13,9},{2,6},{6,2},{1... | collective-permute-start | bytes 786440 | tf_op jit(solution)/shard_map/ppermute | solution.py:364
  9.4 1.0 constant_dynamic-slice_fusion.2
  10.5 0.8 copy.50
  11.3 0.7 copy.49
  12.7 0.8 collective-permute-done.1
  13.7 0.8 copy.54
  14.6 0.8 copy.53
  15.4 0.9 slice_bitcast_fusion
  16.3 1.2 collective-permute-start.2
  17.5 1.2 collective-permute-start.3
  18.8 0.7 copy.52
  19.7 0.8 copy.51
  20.7 0.8 copy.55
  21.7 1.5 collective-permute-done.3
  23.4 1.3 collective-permute-start.15
  24.7 1.4 collective-permute-start.16
  26.0 2.5 %collective-permute-done.4 = bf16[4,32,1024]{2,1,0:T(8,128)(2,1)S(1)} collective-permute-done((bf16[4,32,1024]{2,1,0:T(8,128)(2,1)S(1)}, bf16[4,32,1024]{2,1,0:T(8,128)(2,1)S(1)}, u32[]{:S(2)}, u32[]{:S(2)}) %collective-permute-start.4) | collective-permute-done | bytes 262176 | tf_op jit(solution)/shard_map/ppermute | solution.py:364
  28.7 6.8 %collective-permute-start.5 = (bf16[4,4,32,1024]{3,2,1,0:T(8,128)(2,1)S(1)}, bf16[4,4,32,1024]{3,2,1,0:T(8,128)(2,1)}, u32[]{:S(2)}, u32[]{:S(2)}) collective-permute-start(bf16[4,4,32,1024]{3,2,1,0:T(8,128)(2,1)S(1)} %pad_maximum_fusion.refs_1_.mine), channel_id=1, source_target_pairs={{0,1},{1,0},{2,3},{3,2},{16,17},{17,16},{18,19},{19,18},{4,5},{5,4... | collective-permute-start | bytes 3145736 | tf_op jit(solution)/shard_map/ppermute | solution.py:364
  35.7 0.9 collective-permute-start.6
  36.5 0.7 collective-permute-start.10
  37.2 2.7 %collective-permute-start.9 = (bf16[4,256,128]{2,1,0:T(8,128)(2,1)S(1)}, bf16[4,256,128]{2,1,0:T(8,128)(2,1)}, u32[]{:S(2)}, u32[]{:S(2)}) collective-permute-start(bf16[4,256,128]{2,1,0:T(8,128)(2,1)S(1)} %bitcast.76), channel_id=1, source_target_pairs={{0,8},{4,12},{8,0},{12,4},{1,9},{5,13},{9,1},{13,5},{2,10},{6,14},... | collective-permute-start | bytes 786440 | tf_op jit(solution)/shard_map/ppermute | solution.py:364
  40.0 1.1 collective-permute-start.7
  41.8 8.3 %collective-permute-done.7 = f32[2,28,256]{2,1,0:T(8,128)S(1)} collective-permute-done((f32[2,28,256]{2,1,0:T(8,128)S(1)}, f32[2,28,256]{2,1,0:T(8,128)S(1)}, u32[]{:S(2)}, u32[]{:S(2)}) %collective-permute-start.7) | collective-permute-done | bytes 57376 | tf_op jit(solution)/shard_map/ppermute | solution.py:364
  50.1 7.1 %collective-permute-start.18 = (bf16[4,4,32,1024]{3,2,1,0:T(8,128)(2,1)S(1)}, bf16[4,4,32,1024]{3,2,1,0:T(8,128)(2,1)}, u32[]{:S(2)}, u32[]{:S(2)}) collective-permute-start(bf16[4,4,32,1024]{3,2,1,0:T(8,128)(2,1)S(1)} %pad_maximum_fusion.1.mine.refs_1_), channel_id=1, source_target_pairs={{0,1},{1,0},{2,3},{3,2},{16,17},{17,16},{18,19},{19,18},{4,5},{5,4... | collective-permute-start | bytes 3145736 | tf_op jit(solution)/shard_map/ppermute | solution.py:364
  57.2 0.7 pad_maximum_fusion.4.taps
  57.8 1.2 collective-permute-done.9.refs_5_.rest_2_
  59.1 7.0 %shard_map.77 = (bf16[512,1024]{1,0:T(8,128)(2,1)}, bf16[4,32,1024]{2,1,0:T(8,128)(2,1)}, bf16[4,32,1024]{2,1,0:T(8,128)(2,1)}, bf16[6,32,1024]{2,1,0:T(8,128)(2,1)}, bf16[6,32,1024]{2,1,0:T(8,128)(2,1)}) custom-call(s32[2]{0:T(128)} %pad_add_fusion.refs_0_.here, bf16[4,4,32,1024]{3,2,1,0:T(8,128)(2,1)} %copy-done.1, ...), custom_call_target="tpu_custom_call" | custom-call | tf_op jit(solution)/shard_map/pallas_call | solution.py:324
  66.1 4.6 %collective-permute-start.11 = (bf16[4,32,1024]{2,1,0:T(8,128)(2,1)}, bf16[4,32,1024]{2,1,0:T(8,128)(2,1)S(1)}, u32[]{:S(2)}, u32[]{:S(2)}) collective-permute-start(bf16[4,32,1024]{2,1,0:T(8,128)(2,1)} %get-tuple-element.70), channel_id=1, source_target_pairs={{0,4},{4,8},{8,12},{1,5},{5,9},{9,13},{2,6},{6,10},{10,14},{3,7},{... | collective-permute-start | bytes 786440 | tf_op jit(solution)/shard_map/ppermute | solution.py:405
  70.7 1.9 collective-permute-start.12
  72.6 1.7 collective-permute-done.11.row_low
  74.3 0.7 slice_dynamic-update-slice_fusion.5
  75.0 3.0 %collective-permute-done.12.row_high = bf16[4,32,1024]{2,1,0:T(8,128)(2,1)S(1)} collective-permute-done((bf16[4,32,1024]{2,1,0:T(8,128)(2,1)}, bf16[4,32,1024]{2,1,0:T(8,128)(2,1)S(1)}, u32[]{:S(2)}, u32[]{:S(2)}) %collective-permute-start.12) | collective-permute-done | bytes 262176 | tf_op jit(solution)/shard_map/ppermute | solution.py:406
  78.0 0.7 slice_dynamic-update-slice_fusion.4
  78.7 8.0 %collective-permute-start.13 = (bf16[6,32,1024]{2,1,0:T(8,128)(2,1)}, bf16[6,32,1024]{2,1,0:T(8,128)(2,1)}, u32[]{:S(2)}, u32[]{:S(2)}) collective-permute-start(bf16[6,32,1024]{2,1,0:T(8,128)(2,1)} %get-tuple-element.109), channel_id=1, source_target_pairs={{0,1},{1,2},{2,3},{4,5},{5,6},{6,7},{8,9},{9,10},{10,11},{12,13},{... | collective-permute-start | bytes 1179656 | tf_op jit(solution)/shard_map/ppermute | solution.py:413
  86.8 1.9 collective-permute-start.14
  88.8 0.9 collective-permute-start.23
  89.7 1.7 collective-permute-start.24
  91.8 4.6 %collective-permute-done.14.plane_high = bf16[6,32,1024]{2,1,0:T(8,128)(2,1)} collective-permute-done((bf16[6,32,1024]{2,1,0:T(8,128)(2,1)}, bf16[6,32,1024]{2,1,0:T(8,128)(2,1)}, u32[]{:S(2)}, u32[]{:S(2)}) %collective-permute-start.14) | collective-permute-done | bytes 393248 | tf_op jit(solution)/shard_map/ppermute | solution.py:414
  96.4 11.7 %shard_map.78 = (bf16[4,256,128]{2,1,0:T(8,128)(2,1)}, bf16[4,256,128]{2,1,0:T(8,128)(2,1)}, bf16[4,256,128]{2,1,0:T(8,128)(2,1)}, bf16[4,256,128]{2,1,0:T(8,128)(2,1)}, f32[4,4,32,1024]{3,2,1,0:T(8,128)}) custom-call(s32[2]{0:T(128)} %pad_add_fusion.refs_0_.here, bf16[4,4,32,1024]{3,2,1,0:T(8,128)(2,1)} %bitcast.60, bf16[4,32,1024]{2,1,0:T(8,128)(2,1)} %copy-done.13, ...), custom_call_target="tpu_custom_call" | custom-call | tf_op jit(solution)/shard_map/pallas_call | solution.py:229
  108.1 5.4 %collective-permute-done.24.refs_6_.rest_3_ = bf16[4,256,128]{2,1,0:T(8,128)(2,1)S(1)} collective-permute-done((bf16[4,256,128]{2,1,0:T(8,128)(2,1)}, bf16[4,256,128]{2,1,0:T(8,128)(2,1)S(1)}, u32[]{:S(2)}, u32[]{:S(2)}) %collective-permute-start.24) | collective-permute-done | bytes 262176 | tf_op jit(solution)/shard_map/ppermute | solution.py:364
  113.5 0.7 copy-done.10
  114.2 7.8 %shard_map.79 = (bf16[512,1024]{1,0:T(8,128)(2,1)}, bf16[4,32,1024]{2,1,0:T(8,128)(2,1)}, bf16[4,32,1024]{2,1,0:T(8,128)(2,1)}, bf16[6,32,1024]{2,1,0:T(8,128)(2,1)}, bf16[6,32,1024]{2,1,0:T(8,128)(2,1)}) custom-call(s32[2]{0:T(128)} %pad_add_fusion.refs_0_.here, bf16[4,4,32,1024]{3,2,1,0:T(8,128)(2,1)} %copy-done.2, ...), custom_call_target="tpu_custom_call" | custom-call | tf_op jit(solution)/shard_map/pallas_call | solution.py:324
  122.0 1.9 collective-permute-start.25
  123.9 3.4 %collective-permute-start.26 = (bf16[4,32,1024]{2,1,0:T(8,128)(2,1)}, bf16[4,32,1024]{2,1,0:T(8,128)(2,1)S(1)}, u32[]{:S(2)}, u32[]{:S(2)}) collective-permute-start(bf16[4,32,1024]{2,1,0:T(8,128)(2,1)} %get-tuple-element.86), channel_id=1, source_target_pairs={{4,0},{8,4},{12,8},{5,1},{9,5},{13,9},{6,2},{10,6},{14,10},{7,3},{... | collective-permute-start | bytes 786440 | tf_op jit(solution)/shard_map/ppermute | solution.py:406
  127.3 4.7 %collective-permute-done.25.row_low = bf16[4,32,1024]{2,1,0:T(8,128)(2,1)S(1)} collective-permute-done((bf16[4,32,1024]{2,1,0:T(8,128)(2,1)}, bf16[4,32,1024]{2,1,0:T(8,128)(2,1)S(1)}, u32[]{:S(2)}, u32[]{:S(2)}) %collective-permute-start.25) | collective-permute-done | bytes 262176 | tf_op jit(solution)/shard_map/ppermute | solution.py:405
  132.0 0.7 slice_dynamic-update-slice_fusion.1
  132.7 0.9 collective-permute-done.26.row_high
  133.6 0.7 slice_dynamic-update-slice_fusion
  134.4 3.9 %collective-permute-start.27 = (bf16[6,32,1024]{2,1,0:T(8,128)(2,1)}, bf16[6,32,1024]{2,1,0:T(8,128)(2,1)S(1)}, u32[]{:S(2)}, u32[]{:S(2)}) collective-permute-start(bf16[6,32,1024]{2,1,0:T(8,128)(2,1)} %get-tuple-element.105), channel_id=1, source_target_pairs={{0,1},{1,2},{2,3},{4,5},{5,6},{6,7},{8,9},{9,10},{10,11},{12,13},{... | collective-permute-start | bytes 1179656 | tf_op jit(solution)/shard_map/ppermute | solution.py:413
  138.3 2.1 %collective-permute-start.28 = (bf16[6,32,1024]{2,1,0:T(8,128)(2,1)}, bf16[6,32,1024]{2,1,0:T(8,128)(2,1)S(1)}, u32[]{:S(2)}, u32[]{:S(2)}) collective-permute-start(bf16[6,32,1024]{2,1,0:T(8,128)(2,1)} %get-tuple-element.104), channel_id=1, source_target_pairs={{1,0},{2,1},{3,2},{5,4},{6,5},{7,6},{9,8},{10,9},{11,10},{13,12},{... | collective-permute-start | bytes 1179656 | tf_op jit(solution)/shard_map/ppermute | solution.py:414
  140.4 2.7 %collective-permute-start.20 = (bf16[4,256,128]{2,1,0:T(8,128)(2,1)}, bf16[4,256,128]{2,1,0:T(8,128)(2,1)S(1)}, u32[]{:S(2)}, u32[]{:S(2)}) collective-permute-start(bf16[4,256,128]{2,1,0:T(8,128)(2,1)} %get-tuple-element.77), channel_id=1, source_target_pairs={{0,8},{4,12},{8,0},{12,4},{1,9},{5,13},{9,1},{13,5},{2,10},{6,14},... | collective-permute-start | bytes 786440 | tf_op jit(solution)/shard_map/ppermute | solution.py:364
  143.3 4.6 %collective-permute-done.28.plane_high = bf16[6,32,1024]{2,1,0:T(8,128)(2,1)S(1)} collective-permute-done((bf16[6,32,1024]{2,1,0:T(8,128)(2,1)}, bf16[6,32,1024]{2,1,0:T(8,128)(2,1)S(1)}, u32[]{:S(2)}, u32[]{:S(2)}) %collective-permute-start.28) | collective-permute-done | bytes 393248 | tf_op jit(solution)/shard_map/ppermute | solution.py:414
  147.9 0.7 copy-done.16
  148.6 11.0 %shard_map.80 = (bf16[4,256,128]{2,1,0:T(8,128)(2,1)}, bf16[4,256,128]{2,1,0:T(8,128)(2,1)}, bf16[4,256,128]{2,1,0:T(8,128)(2,1)}, bf16[4,256,128]{2,1,0:T(8,128)(2,1)}) custom-call(s32[2]{0:T(128)} %pad_add_fusion.refs_0_.here, bf16[4,4,32,1024]{3,2,1,0:T(8,128)(2,1)} %bitcast.59, bf16[4,32,1024]{2,1,0:T(8,128)(2,1)} %copy-done.11, ...), custom_call_target="tpu_custom_call" | custom-call | tf_op jit(solution)/shard_map/pallas_call | solution.py:229
  159.6 1.2 collective-permute-done.20
  160.8 4.6 %collective-permute-done.21 = bf16[4,256,128]{2,1,0:T(8,128)(2,1)S(1)} collective-permute-done((bf16[4,256,128]{2,1,0:T(8,128)(2,1)S(1)}, bf16[4,256,128]{2,1,0:T(8,128)(2,1)S(1)}, u32[]{:S(2)}, u32[]{:S(2)}) %collective-permute-start.21) | collective-permute-done | bytes 262176 | tf_op jit(solution)/shard_map/ppermute | solution.py:364
  165.4 1.9 collective-permute-start.30
  167.3 1.7 collective-permute-start.31
  169.2 1.2 copy_dynamic-update-slice_fusion.3
  172.0 11.1 %collective-permute-done.29 = bf16[4,256,128]{2,1,0:T(8,128)(2,1)S(1)} collective-permute-done((bf16[4,256,128]{2,1,0:T(8,128)(2,1)}, bf16[4,256,128]{2,1,0:T(8,128)(2,1)S(1)}, u32[]{:S(2)}, u32[]{:S(2)}) %collective-permute-start.29) | collective-permute-done | bytes 262176 | tf_op jit(solution)/shard_map/ppermute | solution.py:364
  183.4 7.6 %collective-permute-done.30 = bf16[4,256,128]{2,1,0:T(8,128)(2,1)S(1)} collective-permute-done((bf16[4,256,128]{2,1,0:T(8,128)(2,1)}, bf16[4,256,128]{2,1,0:T(8,128)(2,1)S(1)}, u32[]{:S(2)}, u32[]{:S(2)}) %collective-permute-start.30) | collective-permute-done | bytes 262176 | tf_op jit(solution)/shard_map/ppermute | solution.py:364
  191.7 1.0 copy-done.5
  (92 shorter events, 6.4 us)
Async XLA Ops:
  0.6 13.0 %copy-start = (bf16[256,4,512]{2,1,0:T(4,128)(2,1)S(1)}, bf16[256,4,512]{2,1,0:T(4,128)(2,1)}, u32[]{:S(2)}) copy-start(bf16[256,4,512]{2,1,0:T(4,128)(2,1)} %param.7) | copy-start | bytes 3145732
  0.6 10.6 %copy-start.3 = (bf16[256,4,512]{2,1,0:T(4,128)(2,1)S(1)}, bf16[256,4,512]{2,1,0:T(4,128)(2,1)}, u32[]{:S(2)}) copy-start(bf16[256,4,512]{2,1,0:T(4,128)(2,1)} %param.6) | copy-start | bytes 3145732
  1.7 5.4 %collective-permute-start = (bf16[1,64,1024]{2,1,0:T(8,128)(2,1)S(1)}, bf16[1,64,1024]{2,1,0:T(8,128)(2,1)S(1)}, u32[]{:S(2)}, u32[]{:S(2)}) collective-permute-start(bf16[1,64,1024]{2,1,0:T(8,128)(2,1)S(1)} %maximum_bitcast_fusion), channel_id=1, source_target_pairs={{0,12},{4,8},{8,4},{12,0},{1,13},{5,9},{9,5},{13,1},{2,14},{6,10},... | collective-permute-start | bytes 393224 | tf_op jit(solution)/shard_map/ppermute | solution.py:364
  7.2 6.4 %collective-permute-start.1 = (bf16[2,64,1024]{2,1,0:T(8,128)(2,1)S(1)}, bf16[2,64,1024]{2,1,0:T(8,128)(2,1)S(1)}, u32[]{:S(2)}, u32[]{:S(2)}) collective-permute-start(bf16[2,64,1024]{2,1,0:T(8,128)(2,1)S(1)} %pad_maximum_fusion.3), channel_id=1, source_target_pairs={{0,4},{4,0},{8,12},{12,8},{1,5},{5,1},{9,13},{13,9},{2,6},{6,2},{1... | collective-permute-start | bytes 786440 | tf_op jit(solution)/shard_map/ppermute | solution.py:364
  16.3 5.4 %collective-permute-start.2 = (bf16[4,32,1024]{2,1,0:T(8,128)(2,1)}, bf16[4,32,1024]{2,1,0:T(8,128)(2,1)S(1)}, u32[]{:S(2)}, u32[]{:S(2)}) collective-permute-start(bf16[4,32,1024]{2,1,0:T(8,128)(2,1)} %get-tuple-element.103), channel_id=1, source_target_pairs={{0,16},{1,17},{2,18},{3,19},{16,0},{17,1},{18,2},{19,3},{4,20},{5,... | collective-permute-start | bytes 786440 | tf_op jit(solution)/shard_map/ppermute | solution.py:364
  17.5 5.7 %collective-permute-start.3 = (bf16[4,32,1024]{2,1,0:T(8,128)(2,1)}, bf16[4,32,1024]{2,1,0:T(8,128)(2,1)S(1)}, u32[]{:S(2)}, u32[]{:S(2)}) collective-permute-start(bf16[4,32,1024]{2,1,0:T(8,128)(2,1)} %get-tuple-element.103), channel_id=1, source_target_pairs={{0,2},{1,3},{2,0},{3,1},{16,18},{17,19},{18,16},{19,17},{4,6},{5,7... | collective-permute-start | bytes 786440 | tf_op jit(solution)/shard_map/ppermute | solution.py:364
  20.6 15.0 %copy-start.20 = (f32[256,27]{0,1:T(8,128)S(1)}, f32[256,27]{0,1:T(8,128)}, u32[]{:S(2)}) copy-start(f32[256,27]{0,1:T(8,128)} %param.10) | copy-start | bytes 82948
  20.6 15.0 %copy-start.21 = (f32[256]{0:T(256)S(1)}, f32[256]{0:T(256)}, u32[]{:S(2)}) copy-start(f32[256]{0:T(256)} %param.11) | copy-start | bytes 3076
  20.6 15.9 %copy-start.19 = (bf16[256,4,128]{2,0,1:T(8,128)(2,1)S(1)}, bf16[256,4,128]{2,0,1:T(8,128)(2,1)}, u32[]{:S(2)}) copy-start(bf16[256,4,128]{2,0,1:T(8,128)(2,1)} %copy.49) | copy-start | bytes 786436
  20.7 16.6 %copy-start.18 = (bf16[256,4,128]{2,0,1:T(8,128)(2,1)S(1)}, bf16[256,4,128]{2,0,1:T(8,128)(2,1)}, u32[]{:S(2)}) copy-start(bf16[256,4,128]{2,0,1:T(8,128)(2,1)} %copy.50) | copy-start | bytes 786436
  21.4 20.2 %copy-start.7 = (bf16[1,4,32,1024]{3,2,1,0:T(8,128)(2,1)S(1)}, bf16[1,4,32,1024]{3,2,1,0:T(8,128)(2,1)}, u32[]{:S(2)}) copy-start(bf16[1,4,32,1024]{3,2,1,0:T(8,128)(2,1)} %get-tuple-element.100) | copy-start | bytes 786436
  23.3 5.3 %collective-permute-start.4 = (bf16[4,32,1024]{2,1,0:T(8,128)(2,1)S(1)}, bf16[4,32,1024]{2,1,0:T(8,128)(2,1)S(1)}, u32[]{:S(2)}, u32[]{:S(2)}) collective-permute-start(bf16[4,32,1024]{2,1,0:T(8,128)(2,1)S(1)} %broadcast_select_fusion.1), channel_id=1, source_target_pairs={{0,2},{1,17},{2,0},{3,19},{16,18},{17,1},{18,16},{19,3},{4,6},{5,2... | collective-permute-start | bytes 786440 | tf_op jit(solution)/shard_map/ppermute | solution.py:364
  23.4 12.2 %collective-permute-start.15 = (bf16[4,32,1024]{2,1,0:T(8,128)(2,1)}, bf16[4,32,1024]{2,1,0:T(8,128)(2,1)S(1)}, u32[]{:S(2)}, u32[]{:S(2)}) collective-permute-start(bf16[4,32,1024]{2,1,0:T(8,128)(2,1)} %get-tuple-element.102), channel_id=1, source_target_pairs={{0,2},{1,3},{2,0},{3,1},{16,18},{17,19},{18,16},{19,17},{4,6},{5,7... | collective-permute-start | bytes 786440 | tf_op jit(solution)/shard_map/ppermute | solution.py:364
  24.7 10.9 %collective-permute-start.16 = (bf16[4,32,1024]{2,1,0:T(8,128)(2,1)}, bf16[4,32,1024]{2,1,0:T(8,128)(2,1)S(1)}, u32[]{:S(2)}, u32[]{:S(2)}) collective-permute-start(bf16[4,32,1024]{2,1,0:T(8,128)(2,1)} %get-tuple-element.102), channel_id=1, source_target_pairs={{0,16},{1,17},{2,18},{3,19},{16,0},{17,1},{18,2},{19,3},{4,20},{5,... | collective-permute-start | bytes 786440 | tf_op jit(solution)/shard_map/ppermute | solution.py:364
  28.7 30.3 %copy-start.1 = (bf16[4,4,32,1024]{3,2,1,0:T(8,128)(2,1)}, bf16[4,4,32,1024]{3,2,1,0:T(8,128)(2,1)S(1)}, u32[]{:S(2)}) copy-start(bf16[4,4,32,1024]{3,2,1,0:T(8,128)(2,1)S(1)} %pad_maximum_fusion.refs_1_.mine) | copy-start | bytes 3145732
  28.7 30.3 %collective-permute-start.5 = (bf16[4,4,32,1024]{3,2,1,0:T(8,128)(2,1)S(1)}, bf16[4,4,32,1024]{3,2,1,0:T(8,128)(2,1)}, u32[]{:S(2)}, u32[]{:S(2)}) collective-permute-start(bf16[4,4,32,1024]{3,2,1,0:T(8,128)(2,1)S(1)} %pad_maximum_fusion.refs_1_.mine), channel_id=1, source_target_pairs={{0,1},{1,0},{2,3},{3,2},{16,17},{17,16},{18,19},{19,18},{4,5},{5,4... | collective-permute-start | bytes 3145736 | tf_op jit(solution)/shard_map/ppermute | solution.py:364
  35.6 5.5 %collective-permute-start.17 = (bf16[4,32,1024]{2,1,0:T(8,128)(2,1)S(1)}, bf16[4,32,1024]{2,1,0:T(8,128)(2,1)S(1)}, u32[]{:S(2)}, u32[]{:S(2)}) collective-permute-start(bf16[4,32,1024]{2,1,0:T(8,128)(2,1)S(1)} %broadcast_select_fusion), channel_id=1, source_target_pairs={{0,2},{1,17},{2,0},{3,19},{16,18},{17,1},{18,16},{19,3},{4,6},{5,2... | collective-permute-start | bytes 786440 | tf_op jit(solution)/shard_map/ppermute | solution.py:364
  35.7 4.3 %collective-permute-start.6 = (f32[1,28,256]{2,1,0:T(8,128)S(1)}, f32[1,28,256]{2,1,0:T(8,128)S(1)}, u32[]{:S(2)}, u32[]{:S(2)}) collective-permute-start(f32[1,28,256]{2,1,0:T(8,128)S(1)} %maximum_bitcast_fusion.1), channel_id=1, source_target_pairs={{0,12},{4,8},{8,4},{12,0},{1,13},{5,9},{9,5},{13,1},{2,14},{6,10},... | collective-permute-start | bytes 86024 | tf_op jit(solution)/shard_map/ppermute | solution.py:364
  36.5 21.3 %collective-permute-start.10 = (bf16[4,256,128]{2,1,0:T(8,128)(2,1)S(1)}, bf16[4,256,128]{2,1,0:T(8,128)(2,1)S(1)}, u32[]{:S(2)}, u32[]{:S(2)}) collective-permute-start(bf16[4,256,128]{2,1,0:T(8,128)(2,1)S(1)} %bitcast.77), channel_id=1, source_target_pairs={{0,12},{4,8},{8,4},{12,0},{1,13},{5,9},{9,5},{13,1},{2,14},{6,10},... | collective-permute-start | bytes 786440 | tf_op jit(solution)/shard_map/ppermute | solution.py:364
  37.2 21.8 %collective-permute-start.9 = (bf16[4,256,128]{2,1,0:T(8,128)(2,1)S(1)}, bf16[4,256,128]{2,1,0:T(8,128)(2,1)}, u32[]{:S(2)}, u32[]{:S(2)}) collective-permute-start(bf16[4,256,128]{2,1,0:T(8,128)(2,1)S(1)} %bitcast.76), channel_id=1, source_target_pairs={{0,8},{4,12},{8,0},{12,4},{1,9},{5,13},{9,1},{13,5},{2,10},{6,14},... | collective-permute-start | bytes 786440 | tf_op jit(solution)/shard_map/ppermute | solution.py:364
  40.0 10.1 %collective-permute-start.7 = (f32[2,28,256]{2,1,0:T(8,128)S(1)}, f32[2,28,256]{2,1,0:T(8,128)S(1)}, u32[]{:S(2)}, u32[]{:S(2)}) collective-permute-start(f32[2,28,256]{2,1,0:T(8,128)S(1)} %pad_maximum_fusion.5), channel_id=1, source_target_pairs={{0,4},{4,0},{8,12},{12,8},{1,5},{5,1},{9,13},{13,9},{2,6},{6,2},{1... | collective-permute-start | bytes 172040 | tf_op jit(solution)/shard_map/ppermute | solution.py:364
  41.1 17.9 %collective-permute-start.8 = (bf16[4,256,128]{2,1,0:T(8,128)(2,1)S(1)}, bf16[4,256,128]{2,1,0:T(8,128)(2,1)}, u32[]{:S(2)}, u32[]{:S(2)}) collective-permute-start(bf16[4,256,128]{2,1,0:T(8,128)(2,1)S(1)} %bitcast.78), channel_id=1, source_target_pairs={{0,4},{4,0},{8,12},{12,8},{1,5},{5,1},{9,13},{13,9},{2,6},{6,2},{1... | collective-permute-start | bytes 786440 | tf_op jit(solution)/shard_map/ppermute | solution.py:364
  41.8 54.6 %copy-start.2 = (bf16[4,4,32,1024]{3,2,1,0:T(8,128)(2,1)}, bf16[4,4,32,1024]{3,2,1,0:T(8,128)(2,1)S(1)}, u32[]{:S(2)}) copy-start(bf16[4,4,32,1024]{3,2,1,0:T(8,128)(2,1)S(1)} %pad_maximum_fusion.1.mine.refs_1_) | copy-start | bytes 3145732
  50.1 39.6 %collective-permute-start.18 = (bf16[4,4,32,1024]{3,2,1,0:T(8,128)(2,1)S(1)}, bf16[4,4,32,1024]{3,2,1,0:T(8,128)(2,1)}, u32[]{:S(2)}, u32[]{:S(2)}) collective-permute-start(bf16[4,4,32,1024]{3,2,1,0:T(8,128)(2,1)S(1)} %pad_maximum_fusion.1.mine.refs_1_), channel_id=1, source_target_pairs={{0,1},{1,0},{2,3},{3,2},{16,17},{17,16},{18,19},{19,18},{4,5},{5,4... | collective-permute-start | bytes 3145736 | tf_op jit(solution)/shard_map/ppermute | solution.py:364
  57.8 1.2 copy-start.6
  66.1 8.3 %collective-permute-start.11 = (bf16[4,32,1024]{2,1,0:T(8,128)(2,1)}, bf16[4,32,1024]{2,1,0:T(8,128)(2,1)S(1)}, u32[]{:S(2)}, u32[]{:S(2)}) collective-permute-start(bf16[4,32,1024]{2,1,0:T(8,128)(2,1)} %get-tuple-element.70), channel_id=1, source_target_pairs={{0,4},{4,8},{8,12},{1,5},{5,9},{9,13},{2,6},{6,10},{10,14},{3,7},{... | collective-permute-start | bytes 786440 | tf_op jit(solution)/shard_map/ppermute | solution.py:405
  70.7 7.3 %collective-permute-start.12 = (bf16[4,32,1024]{2,1,0:T(8,128)(2,1)}, bf16[4,32,1024]{2,1,0:T(8,128)(2,1)S(1)}, u32[]{:S(2)}, u32[]{:S(2)}) collective-permute-start(bf16[4,32,1024]{2,1,0:T(8,128)(2,1)} %get-tuple-element.71), channel_id=1, source_target_pairs={{4,0},{8,4},{12,8},{5,1},{9,5},{13,9},{6,2},{10,6},{14,10},{7,3},{... | collective-permute-start | bytes 786440 | tf_op jit(solution)/shard_map/ppermute | solution.py:406
  74.3 22.1 %copy-start.13 = (bf16[4,32,1024]{2,1,0:T(8,128)(2,1)}, bf16[4,32,1024]{2,1,0:T(8,128)(2,1)S(1)}, u32[]{:S(2)}) copy-start(bf16[4,32,1024]{2,1,0:T(8,128)(2,1)S(1)} %collective-permute-done.11.row_low) | copy-start | bytes 786436
  78.0 18.3 %copy-start.14 = (bf16[4,32,1024]{2,1,0:T(8,128)(2,1)}, bf16[4,32,1024]{2,1,0:T(8,128)(2,1)S(1)}, u32[]{:S(2)}) copy-start(bf16[4,32,1024]{2,1,0:T(8,128)(2,1)S(1)} %collective-permute-done.12.row_high) | copy-start | bytes 786436
  78.7 13.1 %collective-permute-start.13 = (bf16[6,32,1024]{2,1,0:T(8,128)(2,1)}, bf16[6,32,1024]{2,1,0:T(8,128)(2,1)}, u32[]{:S(2)}, u32[]{:S(2)}) collective-permute-start(bf16[6,32,1024]{2,1,0:T(8,128)(2,1)} %get-tuple-element.109), channel_id=1, source_target_pairs={{0,1},{1,2},{2,3},{4,5},{5,6},{6,7},{8,9},{9,10},{10,11},{12,13},{... | collective-permute-start | bytes 1179656 | tf_op jit(solution)/shard_map/ppermute | solution.py:413
  86.8 9.6 %collective-permute-start.14 = (bf16[6,32,1024]{2,1,0:T(8,128)(2,1)}, bf16[6,32,1024]{2,1,0:T(8,128)(2,1)}, u32[]{:S(2)}, u32[]{:S(2)}) collective-permute-start(bf16[6,32,1024]{2,1,0:T(8,128)(2,1)} %get-tuple-element.108), channel_id=1, source_target_pairs={{1,0},{2,1},{3,2},{5,4},{6,5},{7,6},{9,8},{10,9},{11,10},{13,12},{... | collective-permute-start | bytes 1179656 | tf_op jit(solution)/shard_map/ppermute | solution.py:414
  88.7 19.4 %collective-permute-start.22 = (bf16[4,256,128]{2,1,0:T(8,128)(2,1)}, bf16[4,256,128]{2,1,0:T(8,128)(2,1)S(1)}, u32[]{:S(2)}, u32[]{:S(2)}) collective-permute-start(bf16[4,256,128]{2,1,0:T(8,128)(2,1)} %bitcast.75), channel_id=1, source_target_pairs={{0,4},{4,0},{8,12},{12,8},{1,5},{5,1},{9,13},{13,9},{2,6},{6,2},{1... | collective-permute-start | bytes 786440 | tf_op jit(solution)/shard_map/ppermute | solution.py:364
  88.8 19.3 %collective-permute-start.23 = (bf16[4,256,128]{2,1,0:T(8,128)(2,1)}, bf16[4,256,128]{2,1,0:T(8,128)(2,1)S(1)}, u32[]{:S(2)}, u32[]{:S(2)}) collective-permute-start(bf16[4,256,128]{2,1,0:T(8,128)(2,1)} %bitcast.73), channel_id=1, source_target_pairs={{0,8},{4,12},{8,0},{12,4},{1,9},{5,13},{9,1},{13,5},{2,10},{6,14},... | collective-permute-start | bytes 786440 | tf_op jit(solution)/shard_map/ppermute | solution.py:364
  89.7 23.8 %collective-permute-start.24 = (bf16[4,256,128]{2,1,0:T(8,128)(2,1)}, bf16[4,256,128]{2,1,0:T(8,128)(2,1)S(1)}, u32[]{:S(2)}, u32[]{:S(2)}) collective-permute-start(bf16[4,256,128]{2,1,0:T(8,128)(2,1)} %bitcast.74), channel_id=1, source_target_pairs={{0,12},{4,8},{8,4},{12,0},{1,13},{5,9},{9,5},{13,1},{2,14},{6,10},... | collective-permute-start | bytes 786440 | tf_op jit(solution)/shard_map/ppermute | solution.py:364
  108.1 5.4 %copy-start.8 = (bf16[4,256,128]{2,1,0:T(8,128)(2,1)}, bf16[4,256,128]{2,1,0:T(8,128)(2,1)S(1)}, u32[]{:S(2)}) copy-start(bf16[4,256,128]{2,1,0:T(8,128)(2,1)S(1)} %collective-permute-done.22.refs_4_.rest_1_) | copy-start | bytes 786436
  108.1 5.4 %copy-start.9 = (bf16[4,256,128]{2,1,0:T(8,128)(2,1)}, bf16[4,256,128]{2,1,0:T(8,128)(2,1)S(1)}, u32[]{:S(2)}) copy-start(bf16[4,256,128]{2,1,0:T(8,128)(2,1)S(1)} %collective-permute-done.23.refs_5_.rest_2_) | copy-start | bytes 786436
  113.5 0.7 copy-start.10
  114.2 28.9 %copy-start.22 = (bf16[4,256,128]{2,1,0:T(8,128)(2,1)S(1)}, bf16[4,256,128]{2,1,0:T(8,128)(2,1)}, u32[]{:S(2)}) copy-start(bf16[4,256,128]{2,1,0:T(8,128)(2,1)} %get-tuple-element.78) | copy-start | bytes 786436
  122.0 10.0 %collective-permute-start.25 = (bf16[4,32,1024]{2,1,0:T(8,128)(2,1)}, bf16[4,32,1024]{2,1,0:T(8,128)(2,1)S(1)}, u32[]{:S(2)}, u32[]{:S(2)}) collective-permute-start(bf16[4,32,1024]{2,1,0:T(8,128)(2,1)} %get-tuple-element.85), channel_id=1, source_target_pairs={{0,4},{4,8},{8,12},{1,5},{5,9},{9,13},{2,6},{6,10},{10,14},{3,7},{... | collective-permute-start | bytes 786440 | tf_op jit(solution)/shard_map/ppermute | solution.py:405
  123.9 9.7 %collective-permute-start.26 = (bf16[4,32,1024]{2,1,0:T(8,128)(2,1)}, bf16[4,32,1024]{2,1,0:T(8,128)(2,1)S(1)}, u32[]{:S(2)}, u32[]{:S(2)}) collective-permute-start(bf16[4,32,1024]{2,1,0:T(8,128)(2,1)} %get-tuple-element.86), channel_id=1, source_target_pairs={{4,0},{8,4},{12,8},{5,1},{9,5},{13,9},{6,2},{10,6},{14,10},{7,3},{... | collective-permute-start | bytes 786440 | tf_op jit(solution)/shard_map/ppermute | solution.py:406
  132.0 15.9 %copy-start.11 = (bf16[4,32,1024]{2,1,0:T(8,128)(2,1)}, bf16[4,32,1024]{2,1,0:T(8,128)(2,1)S(1)}, u32[]{:S(2)}) copy-start(bf16[4,32,1024]{2,1,0:T(8,128)(2,1)S(1)} %collective-permute-done.25.row_low) | copy-start | bytes 786436
  133.6 14.2 %copy-start.12 = (bf16[4,32,1024]{2,1,0:T(8,128)(2,1)}, bf16[4,32,1024]{2,1,0:T(8,128)(2,1)S(1)}, u32[]{:S(2)}) copy-start(bf16[4,32,1024]{2,1,0:T(8,128)(2,1)S(1)} %collective-permute-done.26.row_high) | copy-start | bytes 786436
  134.4 8.9 %collective-permute-start.27 = (bf16[6,32,1024]{2,1,0:T(8,128)(2,1)}, bf16[6,32,1024]{2,1,0:T(8,128)(2,1)S(1)}, u32[]{:S(2)}, u32[]{:S(2)}) collective-permute-start(bf16[6,32,1024]{2,1,0:T(8,128)(2,1)} %get-tuple-element.105), channel_id=1, source_target_pairs={{0,1},{1,2},{2,3},{4,5},{5,6},{6,7},{8,9},{9,10},{10,11},{12,13},{... | collective-permute-start | bytes 1179656 | tf_op jit(solution)/shard_map/ppermute | solution.py:413
  138.3 9.6 %collective-permute-start.28 = (bf16[6,32,1024]{2,1,0:T(8,128)(2,1)}, bf16[6,32,1024]{2,1,0:T(8,128)(2,1)S(1)}, u32[]{:S(2)}, u32[]{:S(2)}) collective-permute-start(bf16[6,32,1024]{2,1,0:T(8,128)(2,1)} %get-tuple-element.104), channel_id=1, source_target_pairs={{1,0},{2,1},{3,2},{5,4},{6,5},{7,6},{9,8},{10,9},{11,10},{13,12},{... | collective-permute-start | bytes 1179656 | tf_op jit(solution)/shard_map/ppermute | solution.py:414
  140.4 19.3 %collective-permute-start.19 = (bf16[4,256,128]{2,1,0:T(8,128)(2,1)}, bf16[4,256,128]{2,1,0:T(8,128)(2,1)S(1)}, u32[]{:S(2)}, u32[]{:S(2)}) collective-permute-start(bf16[4,256,128]{2,1,0:T(8,128)(2,1)} %get-tuple-element.76), channel_id=1, source_target_pairs={{0,4},{4,0},{8,12},{12,8},{1,5},{5,1},{9,13},{13,9},{2,6},{6,2},{1... | collective-permute-start | bytes 786440 | tf_op jit(solution)/shard_map/ppermute | solution.py:364
  140.4 20.4 %collective-permute-start.20 = (bf16[4,256,128]{2,1,0:T(8,128)(2,1)}, bf16[4,256,128]{2,1,0:T(8,128)(2,1)S(1)}, u32[]{:S(2)}, u32[]{:S(2)}) collective-permute-start(bf16[4,256,128]{2,1,0:T(8,128)(2,1)} %get-tuple-element.77), channel_id=1, source_target_pairs={{0,8},{4,12},{8,0},{12,4},{1,9},{5,13},{9,1},{13,5},{2,10},{6,14},... | collective-permute-start | bytes 786440 | tf_op jit(solution)/shard_map/ppermute | solution.py:364
  143.1 22.3 %collective-permute-start.21 = (bf16[4,256,128]{2,1,0:T(8,128)(2,1)S(1)}, bf16[4,256,128]{2,1,0:T(8,128)(2,1)S(1)}, u32[]{:S(2)}, u32[]{:S(2)}) collective-permute-start(bf16[4,256,128]{2,1,0:T(8,128)(2,1)S(1)} %copy-done.22), channel_id=1, source_target_pairs={{0,12},{4,8},{8,4},{12,0},{1,13},{5,9},{9,5},{13,1},{2,14},{6,10},... | collective-permute-start | bytes 786440 | tf_op jit(solution)/shard_map/ppermute | solution.py:364
  143.3 4.6 %copy-start.15 = (bf16[6,32,1024]{2,1,0:T(8,128)(2,1)}, bf16[6,32,1024]{2,1,0:T(8,128)(2,1)S(1)}, u32[]{:S(2)}) copy-start(bf16[6,32,1024]{2,1,0:T(8,128)(2,1)S(1)} %collective-permute-done.27.plane_low) | copy-start | bytes 1179652
  147.9 0.7 copy-start.16
  159.6 11.2 %copy-start.17 = (bf16[4,256,128]{2,1,0:T(8,128)(2,1)S(1)}, bf16[4,256,128]{2,1,0:T(8,128)(2,1)}, u32[]{:S(2)}) copy-start(bf16[4,256,128]{2,1,0:T(8,128)(2,1)} %get-tuple-element.90) | copy-start | bytes 786436
  165.4 17.7 %collective-permute-start.29 = (bf16[4,256,128]{2,1,0:T(8,128)(2,1)}, bf16[4,256,128]{2,1,0:T(8,128)(2,1)S(1)}, u32[]{:S(2)}, u32[]{:S(2)}) collective-permute-start(bf16[4,256,128]{2,1,0:T(8,128)(2,1)} %get-tuple-element.95), channel_id=1, source_target_pairs={{0,8},{4,12},{8,0},{12,4},{1,9},{5,13},{9,1},{13,5},{2,10},{6,14},... | collective-permute-start | bytes 786440 | tf_op jit(solution)/shard_map/ppermute | solution.py:364
  165.4 25.7 %collective-permute-start.30 = (bf16[4,256,128]{2,1,0:T(8,128)(2,1)}, bf16[4,256,128]{2,1,0:T(8,128)(2,1)S(1)}, u32[]{:S(2)}, u32[]{:S(2)}) collective-permute-start(bf16[4,256,128]{2,1,0:T(8,128)(2,1)} %get-tuple-element.96), channel_id=1, source_target_pairs={{0,12},{4,8},{8,4},{12,0},{1,13},{5,9},{9,5},{13,1},{2,14},{6,10},... | collective-permute-start | bytes 786440 | tf_op jit(solution)/shard_map/ppermute | solution.py:364
  167.3 24.1 %collective-permute-start.31 = (bf16[4,256,128]{2,1,0:T(8,128)(2,1)}, bf16[4,256,128]{2,1,0:T(8,128)(2,1)S(1)}, u32[]{:S(2)}, u32[]{:S(2)}) collective-permute-start(bf16[4,256,128]{2,1,0:T(8,128)(2,1)} %get-tuple-element.97), channel_id=1, source_target_pairs={{0,4},{4,0},{8,12},{12,8},{1,5},{5,1},{9,13},{13,9},{2,6},{6,2},{1... | collective-permute-start | bytes 786440 | tf_op jit(solution)/shard_map/ppermute | solution.py:364
  172.0 19.7 %copy-start.4 = (bf16[256,4,512]{2,1,0:T(4,128)(2,1)}, bf16[256,4,512]{2,1,0:T(4,128)(2,1)S(1)}, u32[]{:S(2)}) copy-start(bf16[256,4,512]{2,1,0:T(4,128)(2,1)S(1)} %copy_dynamic-update-slice_fusion.4) | copy-start | bytes 3145732
  191.7 1.0 copy-start.5

commit v12 on v9

--- a/solution.py
+++ b/solution.py
@@ -25,33 +25,57 @@
     )
 
 
-def fill_padded(padded, own, row_low, row_high, plane_low, plane_high):
-    planes, rows = own.shape[0], own.shape[1]
-    for z in range(planes):
-        padded[z + 1, 0] = row_low[z].astype(jnp.float32)
-        padded[z + 1, rows + 1] = row_high[z].astype(jnp.float32)
-        for y in range(rows):
-            padded[z + 1, y + 1] = own[z, y].astype(jnp.float32)
-    for y in range(rows + 2):
-        padded[0, y] = plane_low[y].astype(jnp.float32)
-        padded[planes + 1, y] = plane_high[y].astype(jnp.float32)
-
-
-def stencil_row(padded, taps, z, y, flip):
-    sums = [None, None, None]
+def fill_pairs(pairs, own, row_low, row_high, plane_low, plane_high):
+    planes, rows = own.shape[:2]
+    for p in range(planes + 2):
+        if p == 0:
+            fields = [plane_low[y] for y in range(rows + 2)]
+        elif p == planes + 1:
+            fields = [plane_high[y] for y in range(rows + 2)]
+        else:
+            fields = [row_low[p - 1]] + [own[p - 1, y] for y in range(rows)] + [row_high[p - 1]]
+        fields = [field.astype(jnp.float32) for field in fields]
+        for t in range(rows // 2):
+            d0, d1, d2, d3 = fields[2 * t : 2 * t + 4]
+            pairs[p, t, 0] = d0 - d2
+            pairs[p, t, 1] = d1 + d2
+            pairs[p, t, 2] = d2 - d1
+            pairs[p, t, 3] = d1 - d3
+
+
+def fill_factors(factors, taps, flip):
     for a in range(3):
-        for b in range(3):
-            row = padded[z + a, y + b]
-            for e in range(3):
+        for e in range(3):
+            g = []
+            for b in range(3):
                 index = (a * 3 + b) * 3 + e
-                tap = taps[0, 26 - index if flip else index]
-                term = row * tap[None, :]
-                sums[e] = term if sums[e] is None else sums[e] + term
-    x = lax.broadcasted_iota(jnp.int32, sums[0].shape, 0)
-    extent = sums[0].shape[0]
-    before = jnp.where(x == 0, 0.0, pltpu.roll(sums[0], 1, 0))
-    after = jnp.where(x == extent - 1, 0.0, pltpu.roll(sums[2], extent - 1, 0))
-    return sums[1] + (before + after)
+                g.append(taps[0, 26 - index if flip else index])
+            ends = g[0] + g[2]
+            at = (a * 3 + e) * 4
+            factors[at] = g[0]
+            factors[at + 1] = 0.5 * (ends + g[1])
+            factors[at + 2] = 0.5 * (ends - g[1])
+            factors[at + 3] = g[2]
+
+
+def stencil_pair(pairs, factors, z, t):
+    sums = ([], [])
+    for e in range(3):
+        terms = []
+        for i in range(4):
+            total = None
+            for a in range(3):
+                term = pairs[z + a, t, i] * factors[(a * 3 + e) * 4 + i][None, :]
+                total = term if total is None else total + term
+            terms.append(total)
+        sums[0].append(terms[0] + terms[1] + terms[2])
+        sums[1].append(terms[1] - terms[2] - terms[3])
+    extent = sums[0][0].shape[0]
+    x = lax.broadcasted_iota(jnp.int32, sums[0][0].shape, 0)
+    for left, here, right in sums:
+        before = jnp.where(x == 0, 0.0, pltpu.roll(left, 1, 0))
+        after = jnp.where(x == extent - 1, 0.0, pltpu.roll(right, extent - 1, 0))
+        yield here + (before + after)
 
 
 def doubling(count):
@@ -113,9 +137,9 @@
 def forward_kernel(
     here, own, row_low, row_high, plane_low, plane_high, taps, mine, other, *rest
 ):
-    count = (len(rest) - 5) // 2
+    count = (len(rest) - 6) // 2
     inputs, outputs = rest[:count], rest[count : 2 * count]
-    slope, padded, active, weight, sems = rest[2 * count :]
+    slope, pairs, factors, active, weight, sems = rest[2 * count :]
     step = pl.program_id(0)
     planes, rows, extent = own.shape[:3]
     copies = piece_copies(here, mine, other, weight, sems)
@@ -124,15 +148,18 @@
     def _():
         start_all(copies)
 
-    fill_padded(padded, own, row_low, row_high, plane_low, plane_high)
+    fill_pairs(pairs, own, row_low, row_high, plane_low, plane_high)
+    fill_factors(factors, taps, False)
     lanes = pl.ds(pl.multiple_of(step * LANES, LANES), LANES)
     for z in range(planes):
-        for y in range(rows):
-            mixed = stencil_row(padded, taps, z, y, False) + taps[0, 27][None, :]
-            half = 0.5 * (1.0 + lax.erf(mixed * root_half))
-            at = (z * rows + y) * extent
-            active[at : at + extent, lanes] = (mixed * half).astype(active.dtype)
-            slope[z, y] = half + mixed * jnp.exp(-0.5 * mixed * mixed) * inv_root_two_pi
+        for t in range(rows // 2):
+            for odd, mixed in enumerate(stencil_pair(pairs, factors, z, t)):
+                y = 2 * t + odd
+                mixed = mixed + taps[0, 27][None, :]
+                half = 0.5 * (1.0 + lax.erf(mixed * root_half))
+                at = (z * rows + y) * extent
+                active[at : at + extent, lanes] = (mixed * half).astype(active.dtype)
+                slope[z, y] = half + mixed * jnp.exp(-0.5 * mixed * mixed) * inv_root_two_pi
 
     @pl.when(step == pl.num_programs(0) - 1)
     def _():
@@ -151,9 +178,9 @@
 def backward_kernel(
     here, own, row_low, row_high, plane_low, plane_high, taps, mine, other, *rest
 ):
-    count = (len(rest) - 4) // 2
+    count = (len(rest) - 5) // 2
     inputs, outputs = rest[:count], rest[count : 2 * count]
-    padded, grads, weight, sems = rest[2 * count :]
+    pairs, factors, grads, weight, sems = rest[2 * count :]
     step = pl.program_id(0)
     planes, rows, extent = own.shape[:3]
     copies = piece_copies(here, mine, other, weight, sems)
@@ -162,13 +189,14 @@
     def _():
         start_all(copies)
 
-    fill_padded(padded, own, row_low, row_high, plane_low, plane_high)
+    fill_pairs(pairs, own, row_low, row_high, plane_low, plane_high)
+    fill_factors(factors, taps, True)
     lanes = pl.ds(pl.multiple_of(step * LANES, LANES), LANES)
     for z in range(planes):
-        for y in range(rows):
-            at = (z * rows + y) * extent
-            total = stencil_row(padded, taps, z, y, True)
-            grads[at : at + extent, lanes] = total.astype(grads.dtype)
+        for t in range(rows // 2):
+            for odd, total in enumerate(stencil_pair(pairs, factors, z, t)):
+                at = (z * rows + 2 * t + odd) * extent
+                grads[at : at + extent, lanes] = total.astype(grads.dtype)
 
     @pl.when(step == pl.num_programs(0) - 1)
     def _():
@@ -234,7 +262,8 @@
             in_specs=in_specs,
             out_specs=out_specs,
             scratch_shapes=[
-                pltpu.VMEM((planes + 2, rows + 2, extent, LANES), jnp.float32),
+                pltpu.VMEM((planes + 2, rows // 2, 4, extent, LANES), jnp.float32),
+                pltpu.VMEM((36, LANES), jnp.float32),
                 pltpu.VMEM((cells, channels), own.dtype),
                 *weight_scratch(weight[0]),
             ],
@@ -243,9 +272,18 @@
     )(here, own, *halo, taps, *weight, *blocks)
 
 
-def turn_blocks(here, inputs, turned):
-    planes, own, width = inputs[0].shape
-    for shift, block in enumerate(inputs):
+def block_copies(inputs, held, sems):
+    return [
+        pltpu.make_async_copy(block, held.at[shift], sems.at[shift])
+        for shift, block in enumerate(inputs)
+    ]
+
+
+def turn_blocks(here, copies, held, turned):
+    _, planes, own, width = held.shape
+    for shift, copy in enumerate(copies):
+        copy.wait()
+        block = held.at[shift]
         start = pl.multiple_of((here[0] ^ shift) * own, own)
         for z in range(planes):
             turned[z * width : (z + 1) * width, pl.ds(start, own)] = block[z].T
@@ -268,12 +306,14 @@
 
 
 def hidden_kernel(here, mine, other, *rest, count):
-    inputs, (*outputs, turned, weight, sems) = rest[:count], rest[count:]
+    inputs, (*outputs, turned, held, arrived, weight, sems) = rest[:count], rest[count:]
 
     @pl.when(pl.program_id(0) == 0)
     def _():
+        blocks = block_copies(inputs, held, arrived)
+        start_all(blocks)
         start_all(piece_copies(here, mine, other, weight, sems))
-        turn_blocks(here, inputs, turned)
+        turn_blocks(here, blocks, held, turned)
 
     wait_block(pl.program_id(0), mine, other, weight, sems)
     rows_of = weight[pl.program_id(0)]
@@ -287,13 +327,15 @@
 
 
 def mix_kernel(here, mine, other, *rest, count):
-    inputs, (slope, *outputs, turned, weight, sems) = rest[:count], rest[count:]
+    inputs, (slope, *outputs, turned, held, arrived, weight, sems) = rest[:count], rest[count:]
 
     @pl.when(pl.program_id(0) == 0)
     def _():
+        blocks = block_copies(inputs, held, arrived)
+        start_all(blocks)
         copies = piece_copies(here, mine, other, weight, sems)
         start_all(copies)
-        turn_blocks(here, inputs, turned)
+        turn_blocks(here, blocks, held, turned)
         wait_all(copies)
 
     channels, width = turned.shape[1], slope.shape[1]
@@ -314,9 +356,6 @@
     room = width // CX + 2
     row = pl.BlockSpec((planes, CX, own), lambda c, here: (0, 0, c))
     plane = pl.BlockSpec((room, CX, own), lambda c, here: (0, 0, c))
-    whole = pl.BlockSpec(
-        blocks[0].shape, lambda c, here: (0, 0, 0), pipeline_mode=pl.Buffered(1)
-    )
     anywhere = pl.BlockSpec(memory_space=pltpu.HBM)
     kernel, extra = (hidden_kernel, []) if slope is None else (mix_kernel, [slope])
     row_shape = jax.ShapeDtypeStruct((planes, CX, channels), dtype)
@@ -326,9 +365,14 @@
         grid_spec=pltpu.PrefetchScalarGridSpec(
             num_scalar_prefetch=1,
             grid=(count,),
-            in_specs=[anywhere] * 2 + [whole] * count + [columns] * len(extra),
+            in_specs=[anywhere] * (2 + count) + [columns] * len(extra),
             out_specs=[columns, row, row, plane, plane],
-            scratch_shapes=[pltpu.VMEM((cells, channels), dtype), *weight_scratch(weight[0])],
+            scratch_shapes=[
+                pltpu.VMEM((cells, channels), dtype),
+                pltpu.VMEM((count, planes, own, width), dtype),
+                pltpu.SemaphoreType.DMA((count,)),
+                *weight_scratch(weight[0]),
+            ],
         ),
         out_shape=[
             jax.ShapeDtypeStruct((cells, channels), dtype),
@@ -533,7 +577,8 @@
     own = volume.shape[0]
     parts = lax.axis_size("chan")
     groups, space = lax.axis_size("groups"), lax.axis_size("space")
-    whole_rows = CY % parts == 0 and (CY // parts * CX) % LANES == 0 and parts & (parts - 1) == 0
+    whole_rows = CY % (2 * parts) == 0 and (CY // parts * CX) % LANES == 0
+    whole_rows = whole_rows and parts & (parts - 1) == 0
     whole_shares = own % LANES == 0 and own % (16 * groups * space) == 0
     split = whole_rows and whole_shares and (groups, space) == (2, 4)
     chosen = split_cells_body if split else exchange_body

time: 193 us -> 192 us (level)
  no operation moved by 1% of the time
where the time goes in v12:
time: 192 us; the launch traced here: 189 us
  waiting for transfers between devices  74.1 us (39%)
  starting transfers between devices  56.6 us (29%)
  Pallas kernels  36.2 us (19%)
  local copies, waits for them, and re-layouts  19.2 us (10%)
    ppermute x26, waiting for transfers between devices, swap(): return lax.ppermute(part, axes, [(i, partner(i)) for i in range(count)])  58.1 us
    ppermute x26, starting transfers between devices, swap(): return lax.ppermute(part, axes, [(i, partner(i)) for i in range(count)])  37.9 us
    pallas_call x2, Pallas kernels, stencil(): pl.pallas_call(forward_kernel if forward else backward_kernel, grid_spec=...  22.2 us
    pallas_call x2, Pallas kernels, product_call(): pl.pallas_call(lambda *refs: kernel(*refs, count=count), grid_spec=pltpu....  14.1 us
    ppermute x2, starting transfers between devices, halo_of(): row_low = lax.ppermute(last, 'chan', forward)  9.55 us
    ppermute x2, waiting for transfers between devices, halo_of(): row_low = lax.ppermute(last, 'chan', forward)  9.07 us
    unnamed x50, local copies, waits for them, and re-layouts  7.18 us
    ppermute x2, waiting for transfers between devices, halo_of(): row_high = lax.ppermute(first, 'chan', backward)  6.88 us
  transfers between devices with their start and end apart: 34, of which 17 were waited for; matrix products, arithmetic and copies ran while one was open for 9% of the time, Pallas kernels for 15%

profile of v12, /device:TPU:0, one launch (start us, length us, event | category | flops | bytes accessed | tf_op | source)
XLA Modules:
  0.0 189.0 jit_solution(3579017168811733808)
XLA Ops:
  0.7 0.9 dynamic-slice_bitcast_fusion.1
  1.6 5.1 %collective-permute-start = (bf16[1,32,1024]{2,1,0:T(8,128)(2,1)S(1)}, bf16[1,32,1024]{2,1,0:T(8,128)(2,1)S(1)}, u32[]{:S(2)}, u32[]{:S(2)}) collective-permute-start(bf16[1,32,1024]{2,1,0:T(8,128)(2,1)S(1)} %dynamic-slice_bitcast_fusion.1), channel_id=1, source_target_pairs={{0,12},{4,8},{8,4},{12,0},{1,13},{5,9},{9,5},{13,1},{2,14},{6,10},... | collective-permute-start | bytes 196616 | tf_op jit(solution)/shard_map/ppermute | solution.py:408
  6.7 0.8 dynamic-slice_bitcast_fusion
  7.5 1.0 constant_dynamic-slice_fusion.2
  8.6 0.7 copy.49
  9.3 2.1 %collective-permute-start.1 = (bf16[2,32,1024]{2,1,0:T(8,128)(2,1)S(1)}, bf16[2,32,1024]{2,1,0:T(8,128)(2,1)S(1)}, u32[]{:S(2)}, u32[]{:S(2)}) collective-permute-start(bf16[2,32,1024]{2,1,0:T(8,128)(2,1)S(1)} %pad_maximum_fusion.4), channel_id=1, source_target_pairs={{0,4},{4,0},{8,12},{12,8},{1,5},{5,1},{9,13},{13,9},{2,6},{6,2},{1... | collective-permute-start | bytes 393224 | tf_op jit(solution)/shard_map/ppermute | solution.py:408
  11.5 1.0 constant_dynamic-slice_fusion.1
  12.5 0.8 copy.48
  13.9 1.8 collective-permute-done.1
  15.8 0.8 copy.53
  16.7 0.8 copy.52
  17.5 0.7 copy.51
  18.3 1.5 collective-permute-start.2
  19.8 1.5 collective-permute-start.3
  21.6 0.8 copy.50
  22.4 0.8 copy_bitcast_fusion
  23.2 2.7 %collective-permute-done.2 = bf16[4,32,1024]{2,1,0:T(8,128)(2,1)S(1)} collective-permute-done((bf16[4,32,1024]{2,1,0:T(8,128)(2,1)S(1)}, bf16[4,32,1024]{2,1,0:T(8,128)(2,1)S(1)}, u32[]{:S(2)}, u32[]{:S(2)}) %collective-permute-start.2) | collective-permute-done | bytes 262176 | tf_op jit(solution)/shard_map/ppermute | solution.py:408
  25.8 1.2 collective-permute-done.3
  27.1 1.6 collective-permute-start.4
  28.8 5.0 %collective-permute-done.16 = bf16[2,32,1024]{2,1,0:T(8,128)(2,1)S(1)} collective-permute-done((bf16[2,32,1024]{2,1,0:T(8,128)(2,1)S(1)}, bf16[2,32,1024]{2,1,0:T(8,128)(2,1)S(1)}, u32[]{:S(2)}, u32[]{:S(2)}) %collective-permute-start.16) | collective-permute-done | bytes 131104 | tf_op jit(solution)/shard_map/ppermute | solution.py:408
  35.1 5.1 %collective-permute-done.17 = bf16[4,32,1024]{2,1,0:T(8,128)(2,1)S(1)} collective-permute-done((bf16[4,32,1024]{2,1,0:T(8,128)(2,1)S(1)}, bf16[4,32,1024]{2,1,0:T(8,128)(2,1)S(1)}, u32[]{:S(2)}, u32[]{:S(2)}) %collective-permute-start.17) | collective-permute-done | bytes 262176 | tf_op jit(solution)/shard_map/ppermute | solution.py:408
  40.2 2.4 %collective-permute-done.18 = bf16[4,32,1024]{2,1,0:T(8,128)(2,1)S(1)} collective-permute-done((bf16[4,32,1024]{2,1,0:T(8,128)(2,1)S(1)}, bf16[4,32,1024]{2,1,0:T(8,128)(2,1)S(1)}, u32[]{:S(2)}, u32[]{:S(2)}) %collective-permute-start.18) | collective-permute-done | bytes 262176 | tf_op jit(solution)/shard_map/ppermute | solution.py:408
  42.6 1.6 collective-permute-start.19
  44.2 1.1 collective-permute-start.6
  45.3 2.8 %collective-permute-start.10 = (bf16[4,256,128]{2,1,0:T(8,128)(2,1)S(1)}, bf16[4,256,128]{2,1,0:T(8,128)(2,1)S(1)}, u32[]{:S(2)}, u32[]{:S(2)}) collective-permute-start(bf16[4,256,128]{2,1,0:T(8,128)(2,1)S(1)} %bitcast.75), channel_id=1, source_target_pairs={{0,12},{4,8},{8,4},{12,0},{1,13},{5,9},{9,5},{13,1},{2,14},{6,10},... | collective-permute-start | bytes 786440 | tf_op jit(solution)/shard_map/ppermute | solution.py:408
  48.1 2.2 %collective-permute-done.6 = f32[1,28,256]{2,1,0:T(8,128)S(1)} collective-permute-done((f32[1,28,256]{2,1,0:T(8,128)S(1)}, f32[1,28,256]{2,1,0:T(8,128)S(1)}, u32[]{:S(2)}, u32[]{:S(2)}) %collective-permute-start.6) | collective-permute-done | bytes 28704 | tf_op jit(solution)/shard_map/ppermute | solution.py:408
  50.4 2.0 %collective-permute-start.8 = (bf16[4,256,128]{2,1,0:T(8,128)(2,1)S(1)}, bf16[4,256,128]{2,1,0:T(8,128)(2,1)}, u32[]{:S(2)}, u32[]{:S(2)}) collective-permute-start(bf16[4,256,128]{2,1,0:T(8,128)(2,1)S(1)} %get-tuple-element.66), channel_id=1, source_target_pairs={{0,4},{4,0},{8,12},{12,8},{1,5},{5,1},{9,13},{13,9},{2,6},{6,2},{1... | collective-permute-start | bytes 786440 | tf_op jit(solution)/shard_map/ppermute | solution.py:408
  52.5 4.5 %collective-permute-done.7 = f32[2,28,256]{2,1,0:T(8,128)S(1)} collective-permute-done((f32[2,28,256]{2,1,0:T(8,128)S(1)}, f32[2,28,256]{2,1,0:T(8,128)S(1)}, u32[]{:S(2)}, u32[]{:S(2)}) %collective-permute-start.7) | collective-permute-done | bytes 57376 | tf_op jit(solution)/shard_map/ppermute | solution.py:408
  57.1 0.7 pad_maximum_fusion.5.taps
  57.7 7.7 %collective-permute-done.9.refs_5_.rest_2_ = bf16[4,256,128]{2,1,0:T(8,128)(2,1)} collective-permute-done((bf16[4,256,128]{2,1,0:T(8,128)(2,1)S(1)}, bf16[4,256,128]{2,1,0:T(8,128)(2,1)}, u32[]{:S(2)}, u32[]{:S(2)}) %collective-permute-start.9) | collective-permute-done | bytes 262176 | tf_op jit(solution)/shard_map/ppermute | solution.py:408
  65.5 6.2 %shard_map.77 = (bf16[512,1024]{1,0:T(8,128)(2,1)}, bf16[4,32,1024]{2,1,0:T(8,128)(2,1)}, bf16[4,32,1024]{2,1,0:T(8,128)(2,1)}, bf16[6,32,1024]{2,1,0:T(8,128)(2,1)}, bf16[6,32,1024]{2,1,0:T(8,128)(2,1)}) custom-call(s32[2]{0:T(128)} %pad_add_fusion.refs_0_.here, bf16[4,4,32,1024]{3,2,1,0:T(8,128)(2,1)} %copy-done.1, ...), custom_call_target="tpu_custom_call" | custom-call | tf_op jit(solution)/shard_map/pallas_call | solution.py:363
  71.7 1.3 collective-permute-start.11
  73.0 1.3 collective-permute-start.12
  74.3 3.6 %collective-permute-done.11.row_low = bf16[4,32,1024]{2,1,0:T(8,128)(2,1)S(1)} collective-permute-done((bf16[4,32,1024]{2,1,0:T(8,128)(2,1)}, bf16[4,32,1024]{2,1,0:T(8,128)(2,1)S(1)}, u32[]{:S(2)}, u32[]{:S(2)}) %collective-permute-start.11) | collective-permute-done | bytes 262176 | tf_op jit(solution)/shard_map/ppermute | solution.py:449
  77.9 0.7 slice_dynamic-update-slice_fusion.5
  78.6 3.3 %collective-permute-done.12.row_high = bf16[4,32,1024]{2,1,0:T(8,128)(2,1)S(1)} collective-permute-done((bf16[4,32,1024]{2,1,0:T(8,128)(2,1)}, bf16[4,32,1024]{2,1,0:T(8,128)(2,1)S(1)}, u32[]{:S(2)}, u32[]{:S(2)}) %collective-permute-start.12) | collective-permute-done | bytes 262176 | tf_op jit(solution)/shard_map/ppermute | solution.py:450
  81.9 0.8 slice_dynamic-update-slice_fusion.4
  82.7 2.0 %collective-permute-start.13 = (bf16[6,32,1024]{2,1,0:T(8,128)(2,1)}, bf16[6,32,1024]{2,1,0:T(8,128)(2,1)}, u32[]{:S(2)}, u32[]{:S(2)}) collective-permute-start(bf16[6,32,1024]{2,1,0:T(8,128)(2,1)} %get-tuple-element.107), channel_id=1, source_target_pairs={{0,1},{1,2},{2,3},{4,5},{5,6},{6,7},{8,9},{9,10},{10,11},{12,13},{... | collective-permute-start | bytes 1179656 | tf_op jit(solution)/shard_map/ppermute | solution.py:457
  84.7 1.3 collective-permute-start.14
  86.0 0.9 collective-permute-start.24
  86.9 1.5 collective-permute-start.25
  88.4 2.0 %collective-permute-start.26 = (bf16[4,256,128]{2,1,0:T(8,128)(2,1)}, bf16[4,256,128]{2,1,0:T(8,128)(2,1)S(1)}, u32[]{:S(2)}, u32[]{:S(2)}) collective-permute-start(bf16[4,256,128]{2,1,0:T(8,128)(2,1)} %bitcast.72), channel_id=1, source_target_pairs={{0,12},{4,8},{8,4},{12,0},{1,13},{5,9},{9,5},{13,1},{2,14},{6,10},... | collective-permute-start | bytes 786440 | tf_op jit(solution)/shard_map/ppermute | solution.py:408
  90.5 11.3 %shard_map.78 = (bf16[4,256,128]{2,1,0:T(8,128)(2,1)}, bf16[4,256,128]{2,1,0:T(8,128)(2,1)}, bf16[4,256,128]{2,1,0:T(8,128)(2,1)}, bf16[4,256,128]{2,1,0:T(8,128)(2,1)}, f32[4,4,32,1024]{3,2,1,0:T(8,128)}) custom-call(s32[2]{0:T(128)} %pad_add_fusion.refs_0_.here, bf16[4,4,32,1024]{3,2,1,0:T(8,128)(2,1)} %bitcast.57, bf16[4,32,1024]{2,1,0:T(8,128)(2,1)} %copy-done.12, ...), custom_call_target="tpu_custom_call" | custom-call | tf_op jit(solution)/shard_map/pallas_call | solution.py:257
  101.8 5.5 %collective-permute-done.26.refs_6_.rest_3_ = bf16[4,256,128]{2,1,0:T(8,128)(2,1)S(1)} collective-permute-done((bf16[4,256,128]{2,1,0:T(8,128)(2,1)}, bf16[4,256,128]{2,1,0:T(8,128)(2,1)S(1)}, u32[]{:S(2)}, u32[]{:S(2)}) %collective-permute-start.26) | collective-permute-done | bytes 262176 | tf_op jit(solution)/shard_map/ppermute | solution.py:408
  107.3 0.7 copy-done.9
  108.1 7.8 %shard_map.79 = (bf16[512,1024]{1,0:T(8,128)(2,1)}, bf16[4,32,1024]{2,1,0:T(8,128)(2,1)}, bf16[4,32,1024]{2,1,0:T(8,128)(2,1)}, bf16[6,32,1024]{2,1,0:T(8,128)(2,1)}, bf16[6,32,1024]{2,1,0:T(8,128)(2,1)}) custom-call(s32[2]{0:T(128)} %pad_add_fusion.refs_0_.here, bf16[4,4,32,1024]{3,2,1,0:T(8,128)(2,1)} %copy-done.2, ...), custom_call_target="tpu_custom_call" | custom-call | tf_op jit(solution)/shard_map/pallas_call | solution.py:363
  115.9 8.2 %collective-permute-start.27 = (bf16[4,32,1024]{2,1,0:T(8,128)(2,1)}, bf16[4,32,1024]{2,1,0:T(8,128)(2,1)S(1)}, u32[]{:S(2)}, u32[]{:S(2)}) collective-permute-start(bf16[4,32,1024]{2,1,0:T(8,128)(2,1)} %get-tuple-element.85), channel_id=1, source_target_pairs={{0,4},{4,8},{8,12},{1,5},{5,9},{9,13},{2,6},{6,10},{10,14},{3,7},{... | collective-permute-start | bytes 786440 | tf_op jit(solution)/shard_map/ppermute | solution.py:449
  124.2 1.3 collective-permute-start.28
  125.5 5.5 %collective-permute-done.27.row_low = bf16[4,32,1024]{2,1,0:T(8,128)(2,1)S(1)} collective-permute-done((bf16[4,32,1024]{2,1,0:T(8,128)(2,1)}, bf16[4,32,1024]{2,1,0:T(8,128)(2,1)S(1)}, u32[]{:S(2)}, u32[]{:S(2)}) %collective-permute-start.27) | collective-permute-done | bytes 262176 | tf_op jit(solution)/shard_map/ppermute | solution.py:449
  131.0 0.7 slice_dynamic-update-slice_fusion.1
  131.7 3.6 %collective-permute-done.28.row_high = bf16[4,32,1024]{2,1,0:T(8,128)(2,1)S(1)} collective-permute-done((bf16[4,32,1024]{2,1,0:T(8,128)(2,1)}, bf16[4,32,1024]{2,1,0:T(8,128)(2,1)S(1)}, u32[]{:S(2)}, u32[]{:S(2)}) %collective-permute-start.28) | collective-permute-done | bytes 262176 | tf_op jit(solution)/shard_map/ppermute | solution.py:450
  135.3 0.7 slice_dynamic-update-slice_fusion
  136.0 1.8 collective-permute-start.29
  137.7 1.5 collective-permute-start.30
  139.2 1.5 collective-permute-start.21
  140.8 2.8 %collective-permute-start.23 = (bf16[4,256,128]{2,1,0:T(8,128)(2,1)S(1)}, bf16[4,256,128]{2,1,0:T(8,128)(2,1)S(1)}, u32[]{:S(2)}, u32[]{:S(2)}) collective-permute-start(bf16[4,256,128]{2,1,0:T(8,128)(2,1)S(1)} %copy-done.21), channel_id=1, source_target_pairs={{0,12},{4,8},{8,4},{12,0},{1,13},{5,9},{9,5},{13,1},{2,14},{6,10},... | collective-permute-start | bytes 786440 | tf_op jit(solution)/shard_map/ppermute | solution.py:408
  143.7 0.7 copy-done.14
  144.6 10.9 %shard_map.80 = (bf16[4,256,128]{2,1,0:T(8,128)(2,1)}, bf16[4,256,128]{2,1,0:T(8,128)(2,1)}, bf16[4,256,128]{2,1,0:T(8,128)(2,1)}, bf16[4,256,128]{2,1,0:T(8,128)(2,1)}) custom-call(s32[2]{0:T(128)} %pad_add_fusion.refs_0_.here, bf16[4,4,32,1024]{3,2,1,0:T(8,128)(2,1)} %bitcast.56, bf16[4,32,1024]{2,1,0:T(8,128)(2,1)} %copy-done.10, ...), custom_call_target="tpu_custom_call" | custom-call | tf_op jit(solution)/shard_map/pallas_call | solution.py:257
  155.5 6.3 %collective-permute-done.22 = bf16[4,256,128]{2,1,0:T(8,128)(2,1)S(1)} collective-permute-done((bf16[4,256,128]{2,1,0:T(8,128)(2,1)}, bf16[4,256,128]{2,1,0:T(8,128)(2,1)S(1)}, u32[]{:S(2)}, u32[]{:S(2)}) %collective-permute-start.22) | collective-permute-done | bytes 262176 | tf_op jit(solution)/shard_map/ppermute | solution.py:408
  161.8 6.5 %collective-permute-start.31 = (bf16[4,256,128]{2,1,0:T(8,128)(2,1)}, bf16[4,256,128]{2,1,0:T(8,128)(2,1)S(1)}, u32[]{:S(2)}, u32[]{:S(2)}) collective-permute-start(bf16[4,256,128]{2,1,0:T(8,128)(2,1)} %get-tuple-element.95), channel_id=1, source_target_pairs={{0,8},{4,12},{8,0},{12,4},{1,9},{5,13},{9,1},{13,5},{2,10},{6,14},... | collective-permute-start | bytes 786440 | tf_op jit(solution)/shard_map/ppermute | solution.py:408
  168.3 2.0 %collective-permute-start.32 = (bf16[4,256,128]{2,1,0:T(8,128)(2,1)}, bf16[4,256,128]{2,1,0:T(8,128)(2,1)S(1)}, u32[]{:S(2)}, u32[]{:S(2)}) collective-permute-start(bf16[4,256,128]{2,1,0:T(8,128)(2,1)} %get-tuple-element.96), channel_id=1, source_target_pairs={{0,12},{4,8},{8,4},{12,0},{1,13},{5,9},{9,5},{13,1},{2,14},{6,10},... | collective-permute-start | bytes 786440 | tf_op jit(solution)/shard_map/ppermute | solution.py:408
  170.6 1.2 copy_dynamic-update-slice_fusion.3
  173.4 13.6 %collective-permute-done.31 = bf16[4,256,128]{2,1,0:T(8,128)(2,1)S(1)} collective-permute-done((bf16[4,256,128]{2,1,0:T(8,128)(2,1)}, bf16[4,256,128]{2,1,0:T(8,128)(2,1)S(1)}, u32[]{:S(2)}, u32[]{:S(2)}) %collective-permute-start.31) | collective-permute-done | bytes 262176 | tf_op jit(solution)/shard_map/ppermute | solution.py:408
  188.0 1.0 copy-done.5
  (94 shorter events, 6.1 us)
Async XLA Ops:
  0.6 15.1 %copy-start = (bf16[256,4,512]{2,1,0:T(4,128)(2,1)S(1)}, bf16[256,4,512]{2,1,0:T(4,128)(2,1)}, u32[]{:S(2)}) copy-start(bf16[256,4,512]{2,1,0:T(4,128)(2,1)} %param.7) | copy-start | bytes 3145732
  1.6 7.7 %collective-permute-start = (bf16[1,32,1024]{2,1,0:T(8,128)(2,1)S(1)}, bf16[1,32,1024]{2,1,0:T(8,128)(2,1)S(1)}, u32[]{:S(2)}, u32[]{:S(2)}) collective-permute-start(bf16[1,32,1024]{2,1,0:T(8,128)(2,1)S(1)} %dynamic-slice_bitcast_fusion.1), channel_id=1, source_target_pairs={{0,12},{4,8},{8,4},{12,0},{1,13},{5,9},{9,5},{13,1},{2,14},{6,10},... | collective-permute-start | bytes 196616 | tf_op jit(solution)/shard_map/ppermute | solution.py:408
  7.5 21.2 %collective-permute-start.15 = (bf16[1,32,1024]{2,1,0:T(8,128)(2,1)S(1)}, bf16[1,32,1024]{2,1,0:T(8,128)(2,1)S(1)}, u32[]{:S(2)}, u32[]{:S(2)}) collective-permute-start(bf16[1,32,1024]{2,1,0:T(8,128)(2,1)S(1)} %dynamic-slice_bitcast_fusion), channel_id=1, source_target_pairs={{0,12},{4,8},{8,4},{12,0},{1,13},{5,9},{9,5},{13,1},{2,14},{6,10},... | collective-permute-start | bytes 196616 | tf_op jit(solution)/shard_map/ppermute | solution.py:408
  9.3 6.4 %collective-permute-start.1 = (bf16[2,32,1024]{2,1,0:T(8,128)(2,1)S(1)}, bf16[2,32,1024]{2,1,0:T(8,128)(2,1)S(1)}, u32[]{:S(2)}, u32[]{:S(2)}) collective-permute-start(bf16[2,32,1024]{2,1,0:T(8,128)(2,1)S(1)} %pad_maximum_fusion.4), channel_id=1, source_target_pairs={{0,4},{4,0},{8,12},{12,8},{1,5},{5,1},{9,13},{13,9},{2,6},{6,2},{1... | collective-permute-start | bytes 393224 | tf_op jit(solution)/shard_map/ppermute | solution.py:408
  12.5 8.8 %copy-start.3 = (bf16[256,4,512]{2,1,0:T(4,128)(2,1)S(1)}, bf16[256,4,512]{2,1,0:T(4,128)(2,1)}, u32[]{:S(2)}) copy-start(bf16[256,4,512]{2,1,0:T(4,128)(2,1)} %param.6) | copy-start | bytes 3145732
  18.3 7.5 %collective-permute-start.2 = (bf16[4,32,1024]{2,1,0:T(8,128)(2,1)S(1)}, bf16[4,32,1024]{2,1,0:T(8,128)(2,1)S(1)}, u32[]{:S(2)}, u32[]{:S(2)}) collective-permute-start(bf16[4,32,1024]{2,1,0:T(8,128)(2,1)S(1)} %pad_maximum_fusion.2), channel_id=1, source_target_pairs={{0,16},{1,17},{2,18},{3,19},{16,0},{17,1},{18,2},{19,3},{4,20},{5,... | collective-permute-start | bytes 786440 | tf_op jit(solution)/shard_map/ppermute | solution.py:408
  19.8 7.2 %collective-permute-start.3 = (bf16[4,32,1024]{2,1,0:T(8,128)(2,1)S(1)}, bf16[4,32,1024]{2,1,0:T(8,128)(2,1)S(1)}, u32[]{:S(2)}, u32[]{:S(2)}) collective-permute-start(bf16[4,32,1024]{2,1,0:T(8,128)(2,1)S(1)} %pad_maximum_fusion.2), channel_id=1, source_target_pairs={{0,2},{1,3},{2,0},{3,1},{16,18},{17,19},{18,16},{19,17},{4,6},{5,7... | collective-permute-start | bytes 786440 | tf_op jit(solution)/shard_map/ppermute | solution.py:408
  27.1 17.1 %copy-start.19 = (f32[256,27]{0,1:T(8,128)S(1)}, f32[256,27]{0,1:T(8,128)}, u32[]{:S(2)}) copy-start(f32[256,27]{0,1:T(8,128)} %param.10) | copy-start | bytes 82948
  27.1 17.1 %copy-start.20 = (f32[256]{0:T(256)S(1)}, f32[256]{0:T(256)}, u32[]{:S(2)}) copy-start(f32[256]{0:T(256)} %param.11) | copy-start | bytes 3076
  27.1 18.2 %copy-start.18 = (bf16[256,4,128]{2,0,1:T(8,128)(2,1)S(1)}, bf16[256,4,128]{2,0,1:T(8,128)(2,1)}, u32[]{:S(2)}) copy-start(bf16[256,4,128]{2,0,1:T(8,128)(2,1)} %copy.48) | copy-start | bytes 786436
  27.1 21.0 %copy-start.17 = (bf16[256,4,128]{2,0,1:T(8,128)(2,1)S(1)}, bf16[256,4,128]{2,0,1:T(8,128)(2,1)}, u32[]{:S(2)}) copy-start(bf16[256,4,128]{2,0,1:T(8,128)(2,1)} %copy.49) | copy-start | bytes 786436
  27.1 7.8 %collective-permute-start.4 = (bf16[4,32,1024]{2,1,0:T(8,128)(2,1)S(1)}, bf16[4,32,1024]{2,1,0:T(8,128)(2,1)S(1)}, u32[]{:S(2)}, u32[]{:S(2)}) collective-permute-start(bf16[4,32,1024]{2,1,0:T(8,128)(2,1)S(1)} %broadcast_select_fusion.1), channel_id=1, source_target_pairs={{0,2},{1,17},{2,0},{3,19},{16,18},{17,1},{18,16},{19,3},{4,6},{5,2... | collective-permute-start | bytes 786440 | tf_op jit(solution)/shard_map/ppermute | solution.py:408
  28.7 5.0 %collective-permute-start.16 = (bf16[2,32,1024]{2,1,0:T(8,128)(2,1)S(1)}, bf16[2,32,1024]{2,1,0:T(8,128)(2,1)S(1)}, u32[]{:S(2)}, u32[]{:S(2)}) collective-permute-start(bf16[2,32,1024]{2,1,0:T(8,128)(2,1)S(1)} %pad_maximum_fusion.6), channel_id=1, source_target_pairs={{0,4},{4,0},{8,12},{12,8},{1,5},{5,1},{9,13},{13,9},{2,6},{6,2},{1... | collective-permute-start | bytes 393224 | tf_op jit(solution)/shard_map/ppermute | solution.py:408
  33.8 6.4 %collective-permute-start.17 = (bf16[4,32,1024]{2,1,0:T(8,128)(2,1)S(1)}, bf16[4,32,1024]{2,1,0:T(8,128)(2,1)S(1)}, u32[]{:S(2)}, u32[]{:S(2)}) collective-permute-start(bf16[4,32,1024]{2,1,0:T(8,128)(2,1)S(1)} %get-tuple-element.105), channel_id=1, source_target_pairs={{0,2},{1,3},{2,0},{3,1},{16,18},{17,19},{18,16},{19,17},{4,6},{5,7... | collective-permute-start | bytes 786440 | tf_op jit(solution)/shard_map/ppermute | solution.py:408
  34.4 8.2 %collective-permute-start.18 = (bf16[4,32,1024]{2,1,0:T(8,128)(2,1)S(1)}, bf16[4,32,1024]{2,1,0:T(8,128)(2,1)S(1)}, u32[]{:S(2)}, u32[]{:S(2)}) collective-permute-start(bf16[4,32,1024]{2,1,0:T(8,128)(2,1)S(1)} %get-tuple-element.105), channel_id=1, source_target_pairs={{0,16},{1,17},{2,18},{3,19},{16,0},{17,1},{18,2},{19,3},{4,20},{5,... | collective-permute-start | bytes 786440 | tf_op jit(solution)/shard_map/ppermute | solution.py:408
  35.0 30.4 %copy-start.1 = (bf16[4,4,32,1024]{3,2,1,0:T(8,128)(2,1)}, bf16[4,4,32,1024]{3,2,1,0:T(8,128)(2,1)S(1)}, u32[]{:S(2)}) copy-start(bf16[4,4,32,1024]{3,2,1,0:T(8,128)(2,1)S(1)} %pad_maximum_fusion.refs_1_.mine) | copy-start | bytes 3145732
  35.0 30.4 %collective-permute-start.5 = (bf16[4,4,32,1024]{3,2,1,0:T(8,128)(2,1)S(1)}, bf16[4,4,32,1024]{3,2,1,0:T(8,128)(2,1)}, u32[]{:S(2)}, u32[]{:S(2)}) collective-permute-start(bf16[4,4,32,1024]{3,2,1,0:T(8,128)(2,1)S(1)} %pad_maximum_fusion.refs_1_.mine), channel_id=1, source_target_pairs={{0,1},{1,0},{2,3},{3,2},{16,17},{17,16},{18,19},{19,18},{4,5},{5,4... | collective-permute-start | bytes 3145736 | tf_op jit(solution)/shard_map/ppermute | solution.py:408
  42.6 7.7 %collective-permute-start.19 = (bf16[4,32,1024]{2,1,0:T(8,128)(2,1)S(1)}, bf16[4,32,1024]{2,1,0:T(8,128)(2,1)S(1)}, u32[]{:S(2)}, u32[]{:S(2)}) collective-permute-start(bf16[4,32,1024]{2,1,0:T(8,128)(2,1)S(1)} %broadcast_select_fusion), channel_id=1, source_target_pairs={{0,2},{1,17},{2,0},{3,19},{16,18},{17,1},{18,16},{19,3},{4,6},{5,2... | collective-permute-start | bytes 786440 | tf_op jit(solution)/shard_map/ppermute | solution.py:408
  44.2 6.1 %collective-permute-start.6 = (f32[1,28,256]{2,1,0:T(8,128)S(1)}, f32[1,28,256]{2,1,0:T(8,128)S(1)}, u32[]{:S(2)}, u32[]{:S(2)}) collective-permute-start(f32[1,28,256]{2,1,0:T(8,128)S(1)} %maximum_bitcast_fusion), channel_id=1, source_target_pairs={{0,12},{4,8},{8,4},{12,0},{1,13},{5,9},{9,5},{13,1},{2,14},{6,10},... | collective-permute-start | bytes 86024 | tf_op jit(solution)/shard_map/ppermute | solution.py:408
  45.3 12.4 %collective-permute-start.10 = (bf16[4,256,128]{2,1,0:T(8,128)(2,1)S(1)}, bf16[4,256,128]{2,1,0:T(8,128)(2,1)S(1)}, u32[]{:S(2)}, u32[]{:S(2)}) collective-permute-start(bf16[4,256,128]{2,1,0:T(8,128)(2,1)S(1)} %bitcast.75), channel_id=1, source_target_pairs={{0,12},{4,8},{8,4},{12,0},{1,13},{5,9},{9,5},{13,1},{2,14},{6,10},... | collective-permute-start | bytes 786440 | tf_op jit(solution)/shard_map/ppermute | solution.py:408
  48.1 17.3 %collective-permute-start.9 = (bf16[4,256,128]{2,1,0:T(8,128)(2,1)S(1)}, bf16[4,256,128]{2,1,0:T(8,128)(2,1)}, u32[]{:S(2)}, u32[]{:S(2)}) collective-permute-start(bf16[4,256,128]{2,1,0:T(8,128)(2,1)S(1)} %bitcast.74), channel_id=1, source_target_pairs={{0,8},{4,12},{8,0},{12,4},{1,9},{5,13},{9,1},{13,5},{2,10},{6,14},... | collective-permute-start | bytes 786440 | tf_op jit(solution)/shard_map/ppermute | solution.py:408
  50.4 6.7 %collective-permute-start.7 = (f32[2,28,256]{2,1,0:T(8,128)S(1)}, f32[2,28,256]{2,1,0:T(8,128)S(1)}, u32[]{:S(2)}, u32[]{:S(2)}) collective-permute-start(f32[2,28,256]{2,1,0:T(8,128)S(1)} %pad_maximum_fusion.7), channel_id=1, source_target_pairs={{0,4},{4,0},{8,12},{12,8},{1,5},{5,1},{9,13},{13,9},{2,6},{6,2},{1... | collective-permute-start | bytes 172040 | tf_op jit(solution)/shard_map/ppermute | solution.py:408
  50.4 15.1 %collective-permute-start.8 = (bf16[4,256,128]{2,1,0:T(8,128)(2,1)S(1)}, bf16[4,256,128]{2,1,0:T(8,128)(2,1)}, u32[]{:S(2)}, u32[]{:S(2)}) collective-permute-start(bf16[4,256,128]{2,1,0:T(8,128)(2,1)S(1)} %get-tuple-element.66), channel_id=1, source_target_pairs={{0,4},{4,0},{8,12},{12,8},{1,5},{5,1},{9,13},{13,9},{2,6},{6,2},{1... | collective-permute-start | bytes 786440 | tf_op jit(solution)/shard_map/ppermute | solution.py:408
  52.5 37.9 %copy-start.2 = (bf16[4,4,32,1024]{3,2,1,0:T(8,128)(2,1)}, bf16[4,4,32,1024]{3,2,1,0:T(8,128)(2,1)S(1)}, u32[]{:S(2)}) copy-start(bf16[4,4,32,1024]{3,2,1,0:T(8,128)(2,1)S(1)} %pad_maximum_fusion.1.mine.refs_1_) | copy-start | bytes 3145732
  57.0 31.3 %collective-permute-start.20 = (bf16[4,4,32,1024]{3,2,1,0:T(8,128)(2,1)S(1)}, bf16[4,4,32,1024]{3,2,1,0:T(8,128)(2,1)}, u32[]{:S(2)}, u32[]{:S(2)}) collective-permute-start(bf16[4,4,32,1024]{3,2,1,0:T(8,128)(2,1)S(1)} %pad_maximum_fusion.1.mine.refs_1_), channel_id=1, source_target_pairs={{0,1},{1,0},{2,3},{3,2},{16,17},{17,16},{18,19},{19,18},{4,5},{5,4... | collective-permute-start | bytes 3145736 | tf_op jit(solution)/shard_map/ppermute | solution.py:408
  57.7 7.7 %copy-start.6 = (bf16[4,256,128]{2,1,0:T(8,128)(2,1)}, bf16[4,256,128]{2,1,0:T(8,128)(2,1)S(1)}, u32[]{:S(2)}) copy-start(bf16[4,256,128]{2,1,0:T(8,128)(2,1)S(1)} %collective-permute-done.10.refs_6_.rest_3_) | copy-start | bytes 786436
  71.7 6.2 %collective-permute-start.11 = (bf16[4,32,1024]{2,1,0:T(8,128)(2,1)}, bf16[4,32,1024]{2,1,0:T(8,128)(2,1)S(1)}, u32[]{:S(2)}, u32[]{:S(2)}) collective-permute-start(bf16[4,32,1024]{2,1,0:T(8,128)(2,1)} %get-tuple-element.70), channel_id=1, source_target_pairs={{0,4},{4,8},{8,12},{1,5},{5,9},{9,13},{2,6},{6,10},{10,14},{3,7},{... | collective-permute-start | bytes 786440 | tf_op jit(solution)/shard_map/ppermute | solution.py:449
  73.0 8.9 %collective-permute-start.12 = (bf16[4,32,1024]{2,1,0:T(8,128)(2,1)}, bf16[4,32,1024]{2,1,0:T(8,128)(2,1)S(1)}, u32[]{:S(2)}, u32[]{:S(2)}) collective-permute-start(bf16[4,32,1024]{2,1,0:T(8,128)(2,1)} %get-tuple-element.71), channel_id=1, source_target_pairs={{4,0},{8,4},{12,8},{5,1},{9,5},{13,9},{6,2},{10,6},{14,10},{7,3},{... | collective-permute-start | bytes 786440 | tf_op jit(solution)/shard_map/ppermute | solution.py:450
  77.9 12.6 %copy-start.12 = (bf16[4,32,1024]{2,1,0:T(8,128)(2,1)}, bf16[4,32,1024]{2,1,0:T(8,128)(2,1)S(1)}, u32[]{:S(2)}) copy-start(bf16[4,32,1024]{2,1,0:T(8,128)(2,1)S(1)} %collective-permute-done.11.row_low) | copy-start | bytes 786436
  81.9 8.6 %copy-start.13 = (bf16[4,32,1024]{2,1,0:T(8,128)(2,1)}, bf16[4,32,1024]{2,1,0:T(8,128)(2,1)S(1)}, u32[]{:S(2)}) copy-start(bf16[4,32,1024]{2,1,0:T(8,128)(2,1)S(1)} %collective-permute-done.12.row_high) | copy-start | bytes 786436
  82.7 7.8 %collective-permute-start.13 = (bf16[6,32,1024]{2,1,0:T(8,128)(2,1)}, bf16[6,32,1024]{2,1,0:T(8,128)(2,1)}, u32[]{:S(2)}, u32[]{:S(2)}) collective-permute-start(bf16[6,32,1024]{2,1,0:T(8,128)(2,1)} %get-tuple-element.107), channel_id=1, source_target_pairs={{0,1},{1,2},{2,3},{4,5},{5,6},{6,7},{8,9},{9,10},{10,11},{12,13},{... | collective-permute-start | bytes 1179656 | tf_op jit(solution)/shard_map/ppermute | solution.py:457
  84.7 5.8 %collective-permute-start.14 = (bf16[6,32,1024]{2,1,0:T(8,128)(2,1)}, bf16[6,32,1024]{2,1,0:T(8,128)(2,1)}, u32[]{:S(2)}, u32[]{:S(2)}) collective-permute-start(bf16[6,32,1024]{2,1,0:T(8,128)(2,1)} %get-tuple-element.106), channel_id=1, source_target_pairs={{1,0},{2,1},{3,2},{5,4},{6,5},{7,6},{9,8},{10,9},{11,10},{13,12},{... | collective-permute-start | bytes 1179656 | tf_op jit(solution)/shard_map/ppermute | solution.py:458
  86.0 15.8 %collective-permute-start.24 = (bf16[4,256,128]{2,1,0:T(8,128)(2,1)}, bf16[4,256,128]{2,1,0:T(8,128)(2,1)S(1)}, u32[]{:S(2)}, u32[]{:S(2)}) collective-permute-start(bf16[4,256,128]{2,1,0:T(8,128)(2,1)} %bitcast.73), channel_id=1, source_target_pairs={{0,4},{4,0},{8,12},{12,8},{1,5},{5,1},{9,13},{13,9},{2,6},{6,2},{1... | collective-permute-start | bytes 786440 | tf_op jit(solution)/shard_map/ppermute | solution.py:408
  86.9 15.0 %collective-permute-start.25 = (bf16[4,256,128]{2,1,0:T(8,128)(2,1)}, bf16[4,256,128]{2,1,0:T(8,128)(2,1)S(1)}, u32[]{:S(2)}, u32[]{:S(2)}) collective-permute-start(bf16[4,256,128]{2,1,0:T(8,128)(2,1)} %bitcast.71), channel_id=1, source_target_pairs={{0,8},{4,12},{8,0},{12,4},{1,9},{5,13},{9,1},{13,5},{2,10},{6,14},... | collective-permute-start | bytes 786440 | tf_op jit(solution)/shard_map/ppermute | solution.py:408
  88.4 18.9 %collective-permute-start.26 = (bf16[4,256,128]{2,1,0:T(8,128)(2,1)}, bf16[4,256,128]{2,1,0:T(8,128)(2,1)S(1)}, u32[]{:S(2)}, u32[]{:S(2)}) collective-permute-start(bf16[4,256,128]{2,1,0:T(8,128)(2,1)} %bitcast.72), channel_id=1, source_target_pairs={{0,12},{4,8},{8,4},{12,0},{1,13},{5,9},{9,5},{13,1},{2,14},{6,10},... | collective-permute-start | bytes 786440 | tf_op jit(solution)/shard_map/ppermute | solution.py:408
  101.8 5.5 %copy-start.7 = (bf16[4,256,128]{2,1,0:T(8,128)(2,1)}, bf16[4,256,128]{2,1,0:T(8,128)(2,1)S(1)}, u32[]{:S(2)}) copy-start(bf16[4,256,128]{2,1,0:T(8,128)(2,1)S(1)} %collective-permute-done.24.refs_4_.rest_1_) | copy-start | bytes 786436
  101.8 5.5 %copy-start.8 = (bf16[4,256,128]{2,1,0:T(8,128)(2,1)}, bf16[4,256,128]{2,1,0:T(8,128)(2,1)S(1)}, u32[]{:S(2)}) copy-start(bf16[4,256,128]{2,1,0:T(8,128)(2,1)S(1)} %collective-permute-done.25.refs_5_.rest_2_) | copy-start | bytes 786436
  107.3 0.7 copy-start.9
  108.1 32.7 %copy-start.21 = (bf16[4,256,128]{2,1,0:T(8,128)(2,1)S(1)}, bf16[4,256,128]{2,1,0:T(8,128)(2,1)}, u32[]{:S(2)}) copy-start(bf16[4,256,128]{2,1,0:T(8,128)(2,1)} %get-tuple-element.78) | copy-start | bytes 786436
  115.9 15.1 %collective-permute-start.27 = (bf16[4,32,1024]{2,1,0:T(8,128)(2,1)}, bf16[4,32,1024]{2,1,0:T(8,128)(2,1)S(1)}, u32[]{:S(2)}, u32[]{:S(2)}) collective-permute-start(bf16[4,32,1024]{2,1,0:T(8,128)(2,1)} %get-tuple-element.85), channel_id=1, source_target_pairs={{0,4},{4,8},{8,12},{1,5},{5,9},{9,13},{2,6},{6,10},{10,14},{3,7},{... | collective-permute-start | bytes 786440 | tf_op jit(solution)/shard_map/ppermute | solution.py:449
  124.2 11.1 %collective-permute-start.28 = (bf16[4,32,1024]{2,1,0:T(8,128)(2,1)}, bf16[4,32,1024]{2,1,0:T(8,128)(2,1)S(1)}, u32[]{:S(2)}, u32[]{:S(2)}) collective-permute-start(bf16[4,32,1024]{2,1,0:T(8,128)(2,1)} %get-tuple-element.86), channel_id=1, source_target_pairs={{4,0},{8,4},{12,8},{5,1},{9,5},{13,9},{6,2},{10,6},{14,10},{7,3},{... | collective-permute-start | bytes 786440 | tf_op jit(solution)/shard_map/ppermute | solution.py:450
  131.0 12.7 %copy-start.10 = (bf16[4,32,1024]{2,1,0:T(8,128)(2,1)}, bf16[4,32,1024]{2,1,0:T(8,128)(2,1)S(1)}, u32[]{:S(2)}) copy-start(bf16[4,32,1024]{2,1,0:T(8,128)(2,1)S(1)} %collective-permute-done.27.row_low) | copy-start | bytes 786436
  135.2 8.4 %copy-start.11 = (bf16[4,32,1024]{2,1,0:T(8,128)(2,1)}, bf16[4,32,1024]{2,1,0:T(8,128)(2,1)S(1)}, u32[]{:S(2)}) copy-start(bf16[4,32,1024]{2,1,0:T(8,128)(2,1)S(1)} %collective-permute-done.28.row_high) | copy-start | bytes 786436
  136.0 7.7 %collective-permute-start.29 = (bf16[6,32,1024]{2,1,0:T(8,128)(2,1)}, bf16[6,32,1024]{2,1,0:T(8,128)(2,1)S(1)}, u32[]{:S(2)}, u32[]{:S(2)}) collective-permute-start(bf16[6,32,1024]{2,1,0:T(8,128)(2,1)} %get-tuple-element.101), channel_id=1, source_target_pairs={{0,1},{1,2},{2,3},{4,5},{5,6},{6,7},{8,9},{9,10},{10,11},{12,13},{... | collective-permute-start | bytes 1179656 | tf_op jit(solution)/shard_map/ppermute | solution.py:457
  137.7 5.9 %collective-permute-start.30 = (bf16[6,32,1024]{2,1,0:T(8,128)(2,1)}, bf16[6,32,1024]{2,1,0:T(8,128)(2,1)S(1)}, u32[]{:S(2)}, u32[]{:S(2)}) collective-permute-start(bf16[6,32,1024]{2,1,0:T(8,128)(2,1)} %get-tuple-element.100), channel_id=1, source_target_pairs={{1,0},{2,1},{3,2},{5,4},{6,5},{7,6},{9,8},{10,9},{11,10},{13,12},{... | collective-permute-start | bytes 1179656 | tf_op jit(solution)/shard_map/ppermute | solution.py:458
  139.2 16.2 %collective-permute-start.21 = (bf16[4,256,128]{2,1,0:T(8,128)(2,1)}, bf16[4,256,128]{2,1,0:T(8,128)(2,1)S(1)}, u32[]{:S(2)}, u32[]{:S(2)}) collective-permute-start(bf16[4,256,128]{2,1,0:T(8,128)(2,1)} %get-tuple-element.76), channel_id=1, source_target_pairs={{0,4},{4,0},{8,12},{12,8},{1,5},{5,1},{9,13},{13,9},{2,6},{6,2},{1... | collective-permute-start | bytes 786440 | tf_op jit(solution)/shard_map/ppermute | solution.py:408
  140.7 21.1 %collective-permute-start.22 = (bf16[4,256,128]{2,1,0:T(8,128)(2,1)}, bf16[4,256,128]{2,1,0:T(8,128)(2,1)S(1)}, u32[]{:S(2)}, u32[]{:S(2)}) collective-permute-start(bf16[4,256,128]{2,1,0:T(8,128)(2,1)} %get-tuple-element.77), channel_id=1, source_target_pairs={{0,8},{4,12},{8,0},{12,4},{1,9},{5,13},{9,1},{13,5},{2,10},{6,14},... | collective-permute-start | bytes 786440 | tf_op jit(solution)/shard_map/ppermute | solution.py:408
  140.8 21.0 %collective-permute-start.23 = (bf16[4,256,128]{2,1,0:T(8,128)(2,1)S(1)}, bf16[4,256,128]{2,1,0:T(8,128)(2,1)S(1)}, u32[]{:S(2)}, u32[]{:S(2)}) collective-permute-start(bf16[4,256,128]{2,1,0:T(8,128)(2,1)S(1)} %copy-done.21), channel_id=1, source_target_pairs={{0,12},{4,8},{8,4},{12,0},{1,13},{5,9},{9,5},{13,1},{2,14},{6,10},... | collective-permute-start | bytes 786440 | tf_op jit(solution)/shard_map/ppermute | solution.py:408
  143.7 0.8 copy-start.14
  143.7 0.9 copy-start.15
  155.4 16.7 %copy-start.16 = (bf16[4,256,128]{2,1,0:T(8,128)(2,1)S(1)}, bf16[4,256,128]{2,1,0:T(8,128)(2,1)}, u32[]{:S(2)}) copy-start(bf16[4,256,128]{2,1,0:T(8,128)(2,1)} %get-tuple-element.90) | copy-start | bytes 786436
  161.8 25.2 %collective-permute-start.31 = (bf16[4,256,128]{2,1,0:T(8,128)(2,1)}, bf16[4,256,128]{2,1,0:T(8,128)(2,1)S(1)}, u32[]{:S(2)}, u32[]{:S(2)}) collective-permute-start(bf16[4,256,128]{2,1,0:T(8,128)(2,1)} %get-tuple-element.95), channel_id=1, source_target_pairs={{0,8},{4,12},{8,0},{12,4},{1,9},{5,13},{9,1},{13,5},{2,10},{6,14},... | collective-permute-start | bytes 786440 | tf_op jit(solution)/shard_map/ppermute | solution.py:408
  168.3 18.9 %collective-permute-start.32 = (bf16[4,256,128]{2,1,0:T(8,128)(2,1)}, bf16[4,256,128]{2,1,0:T(8,128)(2,1)S(1)}, u32[]{:S(2)}, u32[]{:S(2)}) collective-permute-start(bf16[4,256,128]{2,1,0:T(8,128)(2,1)} %get-tuple-element.96), channel_id=1, source_target_pairs={{0,12},{4,8},{8,4},{12,0},{1,13},{5,9},{9,5},{13,1},{2,14},{6,10},... | collective-permute-start | bytes 786440 | tf_op jit(solution)/shard_map/ppermute | solution.py:408
  170.3 17.4 %collective-permute-start.33 = (bf16[4,256,128]{2,1,0:T(8,128)(2,1)}, bf16[4,256,128]{2,1,0:T(8,128)(2,1)S(1)}, u32[]{:S(2)}, u32[]{:S(2)}) collective-permute-start(bf16[4,256,128]{2,1,0:T(8,128)(2,1)} %get-tuple-element.97), channel_id=1, source_target_pairs={{0,4},{4,0},{8,12},{12,8},{1,5},{5,1},{9,13},{13,9},{2,6},{6,2},{1... | collective-permute-start | bytes 786440 | tf_op jit(solution)/shard_map/ppermute | solution.py:408
  173.4 14.6 %copy-start.4 = (bf16[256,4,512]{2,1,0:T(4,128)(2,1)}, bf16[256,4,512]{2,1,0:T(4,128)(2,1)S(1)}, u32[]{:S(2)}) copy-start(bf16[256,4,512]{2,1,0:T(4,128)(2,1)S(1)} %copy_dynamic-update-slice_fusion.4) | copy-start | bytes 3145732
  188.0 1.0 copy-start.5

commit v13 on v12

--- a/solution.py
+++ b/solution.py
@@ -134,12 +134,17 @@
         out[z] = total.astype(out.dtype)
 
 
+def put_copy(shift, ready, outputs, left):
+    return pltpu.make_async_copy(ready.at[shift], outputs[shift], left.at[shift])
+
+
 def forward_kernel(
     here, own, row_low, row_high, plane_low, plane_high, taps, mine, other, *rest
 ):
-    count = (len(rest) - 6) // 2
+    count = (len(rest) - 10) // 2
     inputs, outputs = rest[:count], rest[count : 2 * count]
-    slope, pairs, factors, active, weight, sems = rest[2 * count :]
+    slope, pairs, factors, active, *blocks, weight, sems = rest[2 * count :]
+    held, ready, arrived, left = blocks
     step = pl.program_id(0)
     planes, rows, extent = own.shape[:3]
     copies = piece_copies(here, mine, other, weight, sems)
@@ -147,6 +152,7 @@
     @pl.when(step == 0)
     def _():
         start_all(copies)
+        start_all(block_copies(inputs, held, arrived))
 
     fill_pairs(pairs, own, row_low, row_high, plane_low, plane_high)
     fill_factors(factors, taps, False)
@@ -159,11 +165,13 @@
                 half = 0.5 * (1.0 + lax.erf(mixed * root_half))
                 at = (z * rows + y) * extent
                 active[at : at + extent, lanes] = (mixed * half).astype(active.dtype)
-                slope[z, y] = half + mixed * jnp.exp(-0.5 * mixed * mixed) * inv_root_two_pi
+                bell = jnp.exp(-0.5 * mixed * mixed) * inv_root_two_pi
+                slope[z, y] = (half + mixed * bell).astype(slope.dtype)
 
     @pl.when(step == pl.num_programs(0) - 1)
     def _():
         wait_all(copies)
+        wait_all(block_copies(inputs, held, arrived))
         for shift in range(count):
             rows_of = weight[here[0] ^ shift]
             product = lax.dot_general(
@@ -172,15 +180,19 @@
                 (((1,), (1,)), ((), ())),
                 preferred_element_type=jnp.float32,
             )
-            add_planes(inputs[shift], product, outputs[shift])
+            add_planes(held.at[shift], product, ready.at[shift])
+            put_copy(shift, ready, outputs, left).start()
+        for shift in range(count):
+            put_copy(shift, ready, outputs, left).wait()
 
 
 def backward_kernel(
     here, own, row_low, row_high, plane_low, plane_high, taps, mine, other, *rest
 ):
-    count = (len(rest) - 5) // 2
+    count = (len(rest) - 9) // 2
     inputs, outputs = rest[:count], rest[count : 2 * count]
-    pairs, factors, grads, weight, sems = rest[2 * count :]
+    pairs, factors, grads, *blocks, weight, sems = rest[2 * count :]
+    held, ready, arrived, left = blocks
     step = pl.program_id(0)
     planes, rows, extent = own.shape[:3]
     copies = piece_copies(here, mine, other, weight, sems)
@@ -188,6 +200,7 @@
     @pl.when(step == 0)
     def _():
         start_all(copies)
+        start_all(block_copies(inputs, held, arrived))
 
     fill_pairs(pairs, own, row_low, row_high, plane_low, plane_high)
     fill_factors(factors, taps, True)
@@ -201,13 +214,17 @@
     @pl.when(step == pl.num_programs(0) - 1)
     def _():
         wait_all(copies)
+        wait_all(block_copies(inputs, held, arrived))
         channels = grads.shape[1]
-        width = inputs[0].shape[1]
+        width = held.shape[2]
         for shift in range(count):
             start = pl.multiple_of((here[0] ^ shift) * width, width)
             columns = weight[:, :, :, pl.ds(start, width)].reshape(channels, width)
             product = jnp.dot(grads[...], columns, preferred_element_type=jnp.float32)
-            add_planes(inputs[shift], product.T, outputs[shift])
+            add_planes(held.at[shift], product.T, ready.at[shift])
+            put_copy(shift, ready, outputs, left).start()
+        for shift in range(count):
+            put_copy(shift, ready, outputs, left).wait()
 
 
 def weight_scratch(mine):
@@ -226,9 +243,6 @@
     def block(*lead):
         zeros = (0,) * len(lead)
         return pl.BlockSpec(lead + (LANES,), lambda c, here: zeros + (c,))
-
-    def resident(shape):
-        return pl.BlockSpec(shape, lambda c, here: (0,) * len(shape), pipeline_mode=pl.Buffered(1))
 
     def table_at(c, here):
         away = (c // per_table) ^ here[0]
@@ -248,12 +262,12 @@
         anywhere,
         anywhere,
     ]
-    in_specs += [resident(piece.shape) for piece in blocks]
-    out_specs = [resident(piece.shape) for piece in blocks]
+    in_specs += [anywhere for _ in blocks]
+    out_specs = [anywhere for _ in blocks]
     out_shape = [jax.ShapeDtypeStruct(piece.shape, piece.dtype) for piece in blocks]
     if forward:
         out_specs.append(block(planes, rows, extent))
-        out_shape.append(jax.ShapeDtypeStruct(own.shape, jnp.float32))
+        out_shape.append(jax.ShapeDtypeStruct(own.shape, own.dtype))
     return pl.pallas_call(
         forward_kernel if forward else backward_kernel,
         grid_spec=pltpu.PrefetchScalarGridSpec(
@@ -265,6 +279,10 @@
                 pltpu.VMEM((planes + 2, rows // 2, 4, extent, LANES), jnp.float32),
                 pltpu.VMEM((36, LANES), jnp.float32),
                 pltpu.VMEM((cells, channels), own.dtype),
+                pltpu.VMEM((len(blocks),) + blocks[0].shape, own.dtype),
+                pltpu.VMEM((len(blocks),) + blocks[0].shape, own.dtype),
+                pltpu.SemaphoreType.DMA((len(blocks),)),
+                pltpu.SemaphoreType.DMA((len(blocks),)),
                 *weight_scratch(weight[0]),
             ],
         ),
@@ -343,7 +361,7 @@
     columns = weight[:, :, :, pl.ds(start, width)].reshape(channels, width)
     grad = jnp.dot(turned[...], columns, preferred_element_type=jnp.float32)
     grad = grad.astype(turned.dtype).astype(jnp.float32)
-    put_with_edges((grad * slope[...]).astype(turned.dtype), *outputs)
+    put_with_edges((grad * slope[...].astype(jnp.float32)).astype(turned.dtype), *outputs)
 
 
 def product_call(here, blocks, weight, slope=None):

time: 192 us -> 192 us (level)
  the two profiles are of different devices: /device:TPU:0 before, /device:TPU:17 now
where the time goes in v13:
time: 192 us; the launch traced here: 191 us
  starting transfers between devices  68.5 us (36%)
  waiting for transfers between devices  64.9 us (34%)
  Pallas kernels  35.5 us (18%)
  local copies, waits for them, and re-layouts  19 us (10%)
    ppermute x26, waiting for transfers between devices, swap(): return lax.ppermute(part, axes, [(i, partner(i)) for i in range(count)])  44.8 us
    ppermute x26, starting transfers between devices, swap(): return lax.ppermute(part, axes, [(i, partner(i)) for i in range(count)])  42.7 us
    pallas_call x2, Pallas kernels, stencil(): pl.pallas_call(forward_kernel if forward else backward_kernel, grid_spec=...  21.7 us
    pallas_call x2, Pallas kernels, product_call(): pl.pallas_call(lambda *refs: kernel(*refs, count=count), grid_spec=pltpu....  13.8 us
    ppermute x2, starting transfers between devices, halo_of(): plane_low = lax.ppermute(joined(fore, planes - 1), 'space', forward)  10.9 us
    ppermute x2, waiting for transfers between devices, halo_of(): plane_high = lax.ppermute(joined(back, 0), 'space', backward)  9.17 us
    unnamed x64, local copies, waits for them, and re-layouts  8.96 us
    ppermute x2, waiting for transfers between devices, halo_of(): row_low = lax.ppermute(last, 'chan', forward)  6.94 us
  transfers between devices with their start and end apart: 34, of which 20 were waited for; matrix products, arithmetic and copies ran while one was open for 7% of the time, Pallas kernels for 15%

profile of v13, /device:TPU:17, one launch (start us, length us, event | category | flops | bytes accessed | tf_op | source)
XLA Modules:
  0.0 190.8 jit_solution(7334050145094062111)
XLA Ops:
  0.7 1.0 dynamic-slice_bitcast_fusion.1
  1.8 0.8 dynamic-slice_bitcast_fusion
  2.7 1.3 collective-permute-start.15
  4.0 1.0 constant_dynamic-slice_fusion.2
  5.0 0.7 copy.49
  5.8 3.2 %collective-permute-start.1 = (bf16[2,32,1024]{2,1,0:T(8,128)(2,1)S(1)}, bf16[2,32,1024]{2,1,0:T(8,128)(2,1)S(1)}, u32[]{:S(2)}, u32[]{:S(2)}) collective-permute-start(bf16[2,32,1024]{2,1,0:T(8,128)(2,1)S(1)} %pad_maximum_fusion.4), channel_id=1, source_target_pairs={{0,4},{4,0},{8,12},{12,8},{1,5},{5,1},{9,13},{13,9},{2,6},{6,2},{1... | collective-permute-start | bytes 393224 | tf_op jit(solution)/shard_map/ppermute | solution.py:426
  9.0 0.8 copy.48
  10.4 1.1 collective-permute-done.1
  11.7 0.8 copy.53
  12.5 0.7 copy.52
  13.4 0.7 copy.51
  14.1 1.2 collective-permute-start.2
  15.3 1.2 collective-permute-start.3
  16.9 0.7 copy.50
  17.6 0.8 copy_bitcast_fusion
  18.4 0.9 collective-permute-done.2
  19.3 1.5 collective-permute-done.3
  21.6 1.5 collective-permute-start.16
  23.1 2.4 %collective-permute-done.16 = bf16[2,32,1024]{2,1,0:T(8,128)(2,1)S(1)} collective-permute-done((bf16[2,32,1024]{2,1,0:T(8,128)(2,1)S(1)}, bf16[2,32,1024]{2,1,0:T(8,128)(2,1)S(1)}, u32[]{:S(2)}, u32[]{:S(2)}) %collective-permute-start.16) | collective-permute-done | bytes 131104 | tf_op jit(solution)/shard_map/ppermute | solution.py:426
  25.5 1.3 collective-permute-start.17
  26.8 1.5 collective-permute-start.18
  28.5 6.1 %collective-permute-start.5 = (bf16[4,4,32,1024]{3,2,1,0:T(8,128)(2,1)S(1)}, bf16[4,4,32,1024]{3,2,1,0:T(8,128)(2,1)}, u32[]{:S(2)}, u32[]{:S(2)}) collective-permute-start(bf16[4,4,32,1024]{3,2,1,0:T(8,128)(2,1)S(1)} %pad_maximum_fusion.refs_1_.mine), channel_id=1, source_target_pairs={{0,1},{1,0},{2,3},{3,2},{16,17},{17,16},{18,19},{19,18},{4,5},{5,4... | collective-permute-start | bytes 3145736 | tf_op jit(solution)/shard_map/ppermute | solution.py:426
  34.6 1.4 collective-permute-start.19
  36.2 1.4 collective-permute-start.10
  37.6 2.5 %collective-permute-start.9 = (bf16[4,256,128]{2,1,0:T(8,128)(2,1)S(1)}, bf16[4,256,128]{2,1,0:T(8,128)(2,1)}, u32[]{:S(2)}, u32[]{:S(2)}) collective-permute-start(bf16[4,256,128]{2,1,0:T(8,128)(2,1)S(1)} %bitcast.71), channel_id=1, source_target_pairs={{0,8},{4,12},{8,0},{12,4},{1,9},{5,13},{9,1},{13,5},{2,10},{6,14},... | collective-permute-start | bytes 786440 | tf_op jit(solution)/shard_map/ppermute | solution.py:426
  40.1 0.8 collective-permute-start.7
  40.9 1.0 collective-permute-done.19
  42.2 5.0 %collective-permute-done.7 = f32[2,28,256]{2,1,0:T(8,128)S(1)} collective-permute-done((f32[2,28,256]{2,1,0:T(8,128)S(1)}, f32[2,28,256]{2,1,0:T(8,128)S(1)}, u32[]{:S(2)}, u32[]{:S(2)}) %collective-permute-start.7) | collective-permute-done | bytes 57376 | tf_op jit(solution)/shard_map/ppermute | solution.py:426
  47.2 9.9 %collective-permute-start.20 = (bf16[4,4,32,1024]{3,2,1,0:T(8,128)(2,1)S(1)}, bf16[4,4,32,1024]{3,2,1,0:T(8,128)(2,1)}, u32[]{:S(2)}, u32[]{:S(2)}) collective-permute-start(bf16[4,4,32,1024]{3,2,1,0:T(8,128)(2,1)S(1)} %pad_maximum_fusion.1.mine.refs_1_), channel_id=1, source_target_pairs={{0,1},{1,0},{2,3},{3,2},{16,17},{17,16},{18,19},{19,18},{4,5},{5,4... | collective-permute-start | bytes 3145736 | tf_op jit(solution)/shard_map/ppermute | solution.py:426
  57.7 2.2 %collective-permute-done.9.refs_5_.rest_2_ = bf16[4,256,128]{2,1,0:T(8,128)(2,1)} collective-permute-done((bf16[4,256,128]{2,1,0:T(8,128)(2,1)S(1)}, bf16[4,256,128]{2,1,0:T(8,128)(2,1)}, u32[]{:S(2)}, u32[]{:S(2)}) %collective-permute-start.9) | collective-permute-done | bytes 262176 | tf_op jit(solution)/shard_map/ppermute | solution.py:426
  59.9 6.2 %shard_map.77 = (bf16[512,1024]{1,0:T(8,128)(2,1)}, bf16[4,32,1024]{2,1,0:T(8,128)(2,1)}, bf16[4,32,1024]{2,1,0:T(8,128)(2,1)}, bf16[6,32,1024]{2,1,0:T(8,128)(2,1)}, bf16[6,32,1024]{2,1,0:T(8,128)(2,1)}) custom-call(s32[2]{0:T(128)} %pad_add_fusion.refs_0_.here, bf16[4,4,32,1024]{3,2,1,0:T(8,128)(2,1)} %copy-done.2, ...), custom_call_target="tpu_custom_call" | custom-call | tf_op jit(solution)/shard_map/pallas_call | solution.py:381
  66.2 3.7 %collective-permute-start.11 = (bf16[4,32,1024]{2,1,0:T(8,128)(2,1)}, bf16[4,32,1024]{2,1,0:T(8,128)(2,1)S(1)}, u32[]{:S(2)}, u32[]{:S(2)}) collective-permute-start(bf16[4,32,1024]{2,1,0:T(8,128)(2,1)} %get-tuple-element.70), channel_id=1, source_target_pairs={{0,4},{4,8},{8,12},{1,5},{5,9},{9,13},{2,6},{6,10},{10,14},{3,7},{... | collective-permute-start | bytes 786440 | tf_op jit(solution)/shard_map/ppermute | solution.py:467
  70.0 1.9 %collective-permute-start.12 = (bf16[4,32,1024]{2,1,0:T(8,128)(2,1)}, bf16[4,32,1024]{2,1,0:T(8,128)(2,1)S(1)}, u32[]{:S(2)}, u32[]{:S(2)}) collective-permute-start(bf16[4,32,1024]{2,1,0:T(8,128)(2,1)} %get-tuple-element.71), channel_id=1, source_target_pairs={{4,0},{8,4},{12,8},{5,1},{9,5},{13,9},{6,2},{10,6},{14,10},{7,3},{... | collective-permute-start | bytes 786440 | tf_op jit(solution)/shard_map/ppermute | solution.py:468
  71.9 2.2 %collective-permute-done.11.row_low = bf16[4,32,1024]{2,1,0:T(8,128)(2,1)S(1)} collective-permute-done((bf16[4,32,1024]{2,1,0:T(8,128)(2,1)}, bf16[4,32,1024]{2,1,0:T(8,128)(2,1)S(1)}, u32[]{:S(2)}, u32[]{:S(2)}) %collective-permute-start.11) | collective-permute-done | bytes 262176 | tf_op jit(solution)/shard_map/ppermute | solution.py:467
  74.1 0.7 slice_dynamic-update-slice_fusion.5
  74.8 2.5 %collective-permute-done.12.row_high = bf16[4,32,1024]{2,1,0:T(8,128)(2,1)S(1)} collective-permute-done((bf16[4,32,1024]{2,1,0:T(8,128)(2,1)}, bf16[4,32,1024]{2,1,0:T(8,128)(2,1)S(1)}, u32[]{:S(2)}, u32[]{:S(2)}) %collective-permute-start.12) | collective-permute-done | bytes 262176 | tf_op jit(solution)/shard_map/ppermute | solution.py:468
  77.3 0.7 slice_dynamic-update-slice_fusion.4
  78.0 7.1 %collective-permute-start.13 = (bf16[6,32,1024]{2,1,0:T(8,128)(2,1)}, bf16[6,32,1024]{2,1,0:T(8,128)(2,1)S(1)}, u32[]{:S(2)}, u32[]{:S(2)}) collective-permute-start(bf16[6,32,1024]{2,1,0:T(8,128)(2,1)} %get-tuple-element.107), channel_id=1, source_target_pairs={{0,1},{1,2},{2,3},{4,5},{5,6},{6,7},{8,9},{9,10},{10,11},{12,13},{... | collective-permute-start | bytes 1179656 | tf_op jit(solution)/shard_map/ppermute | solution.py:475
  85.1 1.9 %collective-permute-start.14 = (bf16[6,32,1024]{2,1,0:T(8,128)(2,1)}, bf16[6,32,1024]{2,1,0:T(8,128)(2,1)}, u32[]{:S(2)}, u32[]{:S(2)}) collective-permute-start(bf16[6,32,1024]{2,1,0:T(8,128)(2,1)} %get-tuple-element.106), channel_id=1, source_target_pairs={{1,0},{2,1},{3,2},{5,4},{6,5},{7,6},{9,8},{10,9},{11,10},{13,12},{... | collective-permute-start | bytes 1179656 | tf_op jit(solution)/shard_map/ppermute | solution.py:476
  87.1 1.0 collective-permute-start.25
  88.1 1.6 collective-permute-start.26
  90.1 4.6 %collective-permute-done.14.plane_high = bf16[6,32,1024]{2,1,0:T(8,128)(2,1)} collective-permute-done((bf16[6,32,1024]{2,1,0:T(8,128)(2,1)}, bf16[6,32,1024]{2,1,0:T(8,128)(2,1)}, u32[]{:S(2)}, u32[]{:S(2)}) %collective-permute-start.14) | collective-permute-done | bytes 393248 | tf_op jit(solution)/shard_map/ppermute | solution.py:476
  94.7 11.3 %shard_map.78 = (bf16[4,256,128]{2,1,0:T(8,128)(2,1)}, bf16[4,256,128]{2,1,0:T(8,128)(2,1)}, bf16[4,256,128]{2,1,0:T(8,128)(2,1)}, bf16[4,256,128]{2,1,0:T(8,128)(2,1)}, bf16[4,4,32,1024]{3,2,1,0:T(8,128)(2,1)}) custom-call(s32[2]{0:T(128)} %pad_add_fusion.refs_0_.here, bf16[4,4,32,1024]{3,2,1,0:T(8,128)(2,1)} %bitcast.57, bf16[4,32,1024]{2,1,0:T(8,128)(2,1)} %copy-done.16, ...), custom_call_target="tpu_custom_call" | custom-call | tf_op jit(solution)/shard_map/pallas_call | solution.py:271
  106.0 5.8 %collective-permute-done.26.refs_6_.rest_3_ = bf16[4,256,128]{2,1,0:T(8,128)(2,1)S(1)} collective-permute-done((bf16[4,256,128]{2,1,0:T(8,128)(2,1)}, bf16[4,256,128]{2,1,0:T(8,128)(2,1)S(1)}, u32[]{:S(2)}, u32[]{:S(2)}) %collective-permute-start.26) | collective-permute-done | bytes 262176 | tf_op jit(solution)/shard_map/ppermute | solution.py:426
  111.8 0.7 copy-done.5
  112.5 7.5 %shard_map.79 = (bf16[512,1024]{1,0:T(8,128)(2,1)}, bf16[4,32,1024]{2,1,0:T(8,128)(2,1)}, bf16[4,32,1024]{2,1,0:T(8,128)(2,1)}, bf16[6,32,1024]{2,1,0:T(8,128)(2,1)}, bf16[6,32,1024]{2,1,0:T(8,128)(2,1)}) custom-call(s32[2]{0:T(128)} %pad_add_fusion.refs_0_.here, bf16[4,4,32,1024]{3,2,1,0:T(8,128)(2,1)} %copy-done.1, ...), custom_call_target="tpu_custom_call" | custom-call | tf_op jit(solution)/shard_map/pallas_call | solution.py:381
  120.0 1.9 %collective-permute-start.27 = (bf16[4,32,1024]{2,1,0:T(8,128)(2,1)}, bf16[4,32,1024]{2,1,0:T(8,128)(2,1)S(1)}, u32[]{:S(2)}, u32[]{:S(2)}) collective-permute-start(bf16[4,32,1024]{2,1,0:T(8,128)(2,1)} %get-tuple-element.85), channel_id=1, source_target_pairs={{0,4},{4,8},{8,12},{1,5},{5,9},{9,13},{2,6},{6,10},{10,14},{3,7},{... | collective-permute-start | bytes 786440 | tf_op jit(solution)/shard_map/ppermute | solution.py:467
  122.0 3.4 %collective-permute-start.28 = (bf16[4,32,1024]{2,1,0:T(8,128)(2,1)}, bf16[4,32,1024]{2,1,0:T(8,128)(2,1)S(1)}, u32[]{:S(2)}, u32[]{:S(2)}) collective-permute-start(bf16[4,32,1024]{2,1,0:T(8,128)(2,1)} %get-tuple-element.86), channel_id=1, source_target_pairs={{4,0},{8,4},{12,8},{5,1},{9,5},{13,9},{6,2},{10,6},{14,10},{7,3},{... | collective-permute-start | bytes 786440 | tf_op jit(solution)/shard_map/ppermute | solution.py:468
  125.3 4.8 %collective-permute-done.27.row_low = bf16[4,32,1024]{2,1,0:T(8,128)(2,1)S(1)} collective-permute-done((bf16[4,32,1024]{2,1,0:T(8,128)(2,1)}, bf16[4,32,1024]{2,1,0:T(8,128)(2,1)S(1)}, u32[]{:S(2)}, u32[]{:S(2)}) %collective-permute-start.27) | collective-permute-done | bytes 262176 | tf_op jit(solution)/shard_map/ppermute | solution.py:467
  130.7 1.0 collective-permute-done.28.row_high
  131.7 0.7 slice_dynamic-update-slice_fusion
  132.4 3.8 %collective-permute-start.29 = (bf16[6,32,1024]{2,1,0:T(8,128)(2,1)}, bf16[6,32,1024]{2,1,0:T(8,128)(2,1)S(1)}, u32[]{:S(2)}, u32[]{:S(2)}) collective-permute-start(bf16[6,32,1024]{2,1,0:T(8,128)(2,1)} %get-tuple-element.101), channel_id=1, source_target_pairs={{0,1},{1,2},{2,3},{4,5},{5,6},{6,7},{8,9},{9,10},{10,11},{12,13},{... | collective-permute-start | bytes 1179656 | tf_op jit(solution)/shard_map/ppermute | solution.py:475
  136.2 2.1 %collective-permute-start.30 = (bf16[6,32,1024]{2,1,0:T(8,128)(2,1)}, bf16[6,32,1024]{2,1,0:T(8,128)(2,1)S(1)}, u32[]{:S(2)}, u32[]{:S(2)}) collective-permute-start(bf16[6,32,1024]{2,1,0:T(8,128)(2,1)} %get-tuple-element.100), channel_id=1, source_target_pairs={{1,0},{2,1},{3,2},{5,4},{6,5},{7,6},{9,8},{10,9},{11,10},{13,12},{... | collective-permute-start | bytes 1179656 | tf_op jit(solution)/shard_map/ppermute | solution.py:476
  138.4 2.7 %collective-permute-start.22 = (bf16[4,256,128]{2,1,0:T(8,128)(2,1)S(1)}, bf16[4,256,128]{2,1,0:T(8,128)(2,1)S(1)}, u32[]{:S(2)}, u32[]{:S(2)}) collective-permute-start(bf16[4,256,128]{2,1,0:T(8,128)(2,1)S(1)} %copy-done.28), channel_id=1, source_target_pairs={{0,8},{4,12},{8,0},{12,4},{1,9},{5,13},{9,1},{13,5},{2,10},{6,14},... | collective-permute-start | bytes 786440 | tf_op jit(solution)/shard_map/ppermute | solution.py:426
  141.3 4.6 %collective-permute-done.30.plane_high = bf16[6,32,1024]{2,1,0:T(8,128)(2,1)S(1)} collective-permute-done((bf16[6,32,1024]{2,1,0:T(8,128)(2,1)}, bf16[6,32,1024]{2,1,0:T(8,128)(2,1)S(1)}, u32[]{:S(2)}, u32[]{:S(2)}) %collective-permute-start.30) | collective-permute-done | bytes 393248 | tf_op jit(solution)/shard_map/ppermute | solution.py:476
  145.9 0.7 copy-done.19
  146.6 10.4 %shard_map.80 = (bf16[4,256,128]{2,1,0:T(8,128)(2,1)}, bf16[4,256,128]{2,1,0:T(8,128)(2,1)}, bf16[4,256,128]{2,1,0:T(8,128)(2,1)}, bf16[4,256,128]{2,1,0:T(8,128)(2,1)}) custom-call(s32[2]{0:T(128)} %pad_add_fusion.refs_0_.here, bf16[4,4,32,1024]{3,2,1,0:T(8,128)(2,1)} %bitcast.56, bf16[4,32,1024]{2,1,0:T(8,128)(2,1)} %copy-done.14, ...), custom_call_target="tpu_custom_call" | custom-call | tf_op jit(solution)/shard_map/pallas_call | solution.py:271
  157.1 1.5 collective-permute-done.22
  158.5 4.8 %collective-permute-done.23 = bf16[4,256,128]{2,1,0:T(8,128)(2,1)S(1)} collective-permute-done((bf16[4,256,128]{2,1,0:T(8,128)(2,1)S(1)}, bf16[4,256,128]{2,1,0:T(8,128)(2,1)S(1)}, u32[]{:S(2)}, u32[]{:S(2)}) %collective-permute-start.23) | collective-permute-done | bytes 262176 | tf_op jit(solution)/shard_map/ppermute | solution.py:426
  163.3 1.9 collective-permute-start.32
  165.2 1.6 collective-permute-start.33
  170.3 10.8 %collective-permute-done.31 = bf16[4,256,128]{2,1,0:T(8,128)(2,1)S(1)} collective-permute-done((bf16[4,256,128]{2,1,0:T(8,128)(2,1)}, bf16[4,256,128]{2,1,0:T(8,128)(2,1)S(1)}, u32[]{:S(2)}, u32[]{:S(2)}) %collective-permute-start.31) | collective-permute-done | bytes 262176 | tf_op jit(solution)/shard_map/ppermute | solution.py:426
  181.3 7.8 %collective-permute-done.32 = bf16[4,256,128]{2,1,0:T(8,128)(2,1)S(1)} collective-permute-done((bf16[4,256,128]{2,1,0:T(8,128)(2,1)}, bf16[4,256,128]{2,1,0:T(8,128)(2,1)S(1)}, u32[]{:S(2)}, u32[]{:S(2)}) %collective-permute-start.32) | collective-permute-done | bytes 262176 | tf_op jit(solution)/shard_map/ppermute | solution.py:426
  189.8 1.0 copy-done.8
  (108 shorter events, 9.2 us)
Async XLA Ops:
  0.6 10.9 %copy-start = (bf16[256,4,512]{2,1,0:T(4,128)(2,1)S(1)}, bf16[256,4,512]{2,1,0:T(4,128)(2,1)}, u32[]{:S(2)}) copy-start(bf16[256,4,512]{2,1,0:T(4,128)(2,1)} %param.7) | copy-start | bytes 3145732
  0.6 8.3 %copy-start.6 = (bf16[256,4,512]{2,1,0:T(4,128)(2,1)S(1)}, bf16[256,4,512]{2,1,0:T(4,128)(2,1)}, u32[]{:S(2)}) copy-start(bf16[256,4,512]{2,1,0:T(4,128)(2,1)} %param.6) | copy-start | bytes 3145732
  1.7 4.1 %collective-permute-start = (bf16[1,32,1024]{2,1,0:T(8,128)(2,1)S(1)}, bf16[1,32,1024]{2,1,0:T(8,128)(2,1)S(1)}, u32[]{:S(2)}, u32[]{:S(2)}) collective-permute-start(bf16[1,32,1024]{2,1,0:T(8,128)(2,1)S(1)} %dynamic-slice_bitcast_fusion.1), channel_id=1, source_target_pairs={{0,12},{4,8},{8,4},{12,0},{1,13},{5,9},{9,5},{13,1},{2,14},{6,10},... | collective-permute-start | bytes 196616 | tf_op jit(solution)/shard_map/ppermute | solution.py:426
  2.7 18.9 %collective-permute-start.15 = (bf16[1,32,1024]{2,1,0:T(8,128)(2,1)S(1)}, bf16[1,32,1024]{2,1,0:T(8,128)(2,1)S(1)}, u32[]{:S(2)}, u32[]{:S(2)}) collective-permute-start(bf16[1,32,1024]{2,1,0:T(8,128)(2,1)S(1)} %dynamic-slice_bitcast_fusion), channel_id=1, source_target_pairs={{0,12},{4,8},{8,4},{12,0},{1,13},{5,9},{9,5},{13,1},{2,14},{6,10},... | collective-permute-start | bytes 196616 | tf_op jit(solution)/shard_map/ppermute | solution.py:426
  5.8 5.8 %collective-permute-start.1 = (bf16[2,32,1024]{2,1,0:T(8,128)(2,1)S(1)}, bf16[2,32,1024]{2,1,0:T(8,128)(2,1)S(1)}, u32[]{:S(2)}, u32[]{:S(2)}) collective-permute-start(bf16[2,32,1024]{2,1,0:T(8,128)(2,1)S(1)} %pad_maximum_fusion.4), channel_id=1, source_target_pairs={{0,4},{4,0},{8,12},{12,8},{1,5},{5,1},{9,13},{13,9},{2,6},{6,2},{1... | collective-permute-start | bytes 393224 | tf_op jit(solution)/shard_map/ppermute | solution.py:426
  14.1 5.2 %collective-permute-start.2 = (bf16[4,32,1024]{2,1,0:T(8,128)(2,1)S(1)}, bf16[4,32,1024]{2,1,0:T(8,128)(2,1)S(1)}, u32[]{:S(2)}, u32[]{:S(2)}) collective-permute-start(bf16[4,32,1024]{2,1,0:T(8,128)(2,1)S(1)} %pad_maximum_fusion.2), channel_id=1, source_target_pairs={{0,16},{1,17},{2,18},{3,19},{16,0},{17,1},{18,2},{19,3},{4,20},{5,... | collective-permute-start | bytes 786440 | tf_op jit(solution)/shard_map/ppermute | solution.py:426
  15.3 5.5 %collective-permute-start.3 = (bf16[4,32,1024]{2,1,0:T(8,128)(2,1)S(1)}, bf16[4,32,1024]{2,1,0:T(8,128)(2,1)S(1)}, u32[]{:S(2)}, u32[]{:S(2)}) collective-permute-start(bf16[4,32,1024]{2,1,0:T(8,128)(2,1)S(1)} %pad_maximum_fusion.2), channel_id=1, source_target_pairs={{0,2},{1,3},{2,0},{3,1},{16,18},{17,19},{18,16},{19,17},{4,6},{5,7... | collective-permute-start | bytes 786440 | tf_op jit(solution)/shard_map/ppermute | solution.py:426
  19.3 1.6 copy-start.10
  20.9 0.7 copy-start.12
  21.6 6.7 %collective-permute-start.4 = (bf16[4,32,1024]{2,1,0:T(8,128)(2,1)S(1)}, bf16[4,32,1024]{2,1,0:T(8,128)(2,1)S(1)}, u32[]{:S(2)}, u32[]{:S(2)}) collective-permute-start(bf16[4,32,1024]{2,1,0:T(8,128)(2,1)S(1)} %broadcast_select_fusion.1), channel_id=1, source_target_pairs={{0,2},{1,17},{2,0},{3,19},{16,18},{17,1},{18,16},{19,3},{4,6},{5,2... | collective-permute-start | bytes 786440 | tf_op jit(solution)/shard_map/ppermute | solution.py:426
  21.6 6.7 %copy-start.11 = (bf16[4,32,1024]{2,1,0:T(8,128)(2,1)S(1)}, bf16[4,32,1024]{2,1,0:T(8,128)(2,1)}, u32[]{:S(2)}) copy-start(bf16[4,32,1024]{2,1,0:T(8,128)(2,1)} %copy-done.10) | copy-start | bytes 786436
  21.6 6.7 %copy-start.13 = (bf16[4,32,1024]{2,1,0:T(8,128)(2,1)S(1)}, bf16[4,32,1024]{2,1,0:T(8,128)(2,1)}, u32[]{:S(2)}) copy-start(bf16[4,32,1024]{2,1,0:T(8,128)(2,1)} %copy-done.12) | copy-start | bytes 786436
  21.6 3.9 %collective-permute-start.16 = (bf16[2,32,1024]{2,1,0:T(8,128)(2,1)S(1)}, bf16[2,32,1024]{2,1,0:T(8,128)(2,1)S(1)}, u32[]{:S(2)}, u32[]{:S(2)}) collective-permute-start(bf16[2,32,1024]{2,1,0:T(8,128)(2,1)S(1)} %pad_maximum_fusion.6), channel_id=1, source_target_pairs={{0,4},{4,0},{8,12},{12,8},{1,5},{5,1},{9,13},{13,9},{2,6},{6,2},{1... | collective-permute-start | bytes 393224 | tf_op jit(solution)/shard_map/ppermute | solution.py:426
  25.5 9.0 %collective-permute-start.17 = (bf16[4,32,1024]{2,1,0:T(8,128)(2,1)S(1)}, bf16[4,32,1024]{2,1,0:T(8,128)(2,1)S(1)}, u32[]{:S(2)}, u32[]{:S(2)}) collective-permute-start(bf16[4,32,1024]{2,1,0:T(8,128)(2,1)S(1)} %get-tuple-element.105), channel_id=1, source_target_pairs={{0,2},{1,3},{2,0},{3,1},{16,18},{17,19},{18,16},{19,17},{4,6},{5,7... | collective-permute-start | bytes 786440 | tf_op jit(solution)/shard_map/ppermute | solution.py:426
  26.8 7.8 %collective-permute-start.18 = (bf16[4,32,1024]{2,1,0:T(8,128)(2,1)S(1)}, bf16[4,32,1024]{2,1,0:T(8,128)(2,1)S(1)}, u32[]{:S(2)}, u32[]{:S(2)}) collective-permute-start(bf16[4,32,1024]{2,1,0:T(8,128)(2,1)S(1)} %get-tuple-element.105), channel_id=1, source_target_pairs={{0,16},{1,17},{2,18},{3,19},{16,0},{17,1},{18,2},{19,3},{4,20},{5,... | collective-permute-start | bytes 786440 | tf_op jit(solution)/shard_map/ppermute | solution.py:426
  28.4 13.7 %copy-start.2 = (bf16[4,4,32,1024]{3,2,1,0:T(8,128)(2,1)}, bf16[4,4,32,1024]{3,2,1,0:T(8,128)(2,1)S(1)}, u32[]{:S(2)}) copy-start(bf16[4,4,32,1024]{3,2,1,0:T(8,128)(2,1)S(1)} %pad_maximum_fusion.refs_1_.mine) | copy-start | bytes 3145732
  28.4 7.6 %copy-start.25 = (f32[256,27]{0,1:T(8,128)S(1)}, f32[256,27]{0,1:T(8,128)}, u32[]{:S(2)}) copy-start(f32[256,27]{0,1:T(8,128)} %param.10) | copy-start | bytes 82948
  28.5 7.8 %copy-start.24 = (bf16[256,4,128]{2,0,1:T(8,128)(2,1)S(1)}, bf16[256,4,128]{2,0,1:T(8,128)(2,1)}, u32[]{:S(2)}) copy-start(bf16[256,4,128]{2,0,1:T(8,128)(2,1)} %copy.48) | copy-start | bytes 786436
  28.5 9.1 %copy-start.23 = (bf16[256,4,128]{2,0,1:T(8,128)(2,1)S(1)}, bf16[256,4,128]{2,0,1:T(8,128)(2,1)}, u32[]{:S(2)}) copy-start(bf16[256,4,128]{2,0,1:T(8,128)(2,1)} %copy.49) | copy-start | bytes 786436
  28.5 31.5 %collective-permute-start.5 = (bf16[4,4,32,1024]{3,2,1,0:T(8,128)(2,1)S(1)}, bf16[4,4,32,1024]{3,2,1,0:T(8,128)(2,1)}, u32[]{:S(2)}, u32[]{:S(2)}) collective-permute-start(bf16[4,4,32,1024]{3,2,1,0:T(8,128)(2,1)S(1)} %pad_maximum_fusion.refs_1_.mine), channel_id=1, source_target_pairs={{0,1},{1,0},{2,3},{3,2},{16,17},{17,16},{18,19},{19,18},{4,5},{5,4... | collective-permute-start | bytes 3145736 | tf_op jit(solution)/shard_map/ppermute | solution.py:426
  34.6 1.4 copy-start.26
  34.6 7.3 %collective-permute-start.19 = (bf16[4,32,1024]{2,1,0:T(8,128)(2,1)S(1)}, bf16[4,32,1024]{2,1,0:T(8,128)(2,1)S(1)}, u32[]{:S(2)}, u32[]{:S(2)}) collective-permute-start(bf16[4,32,1024]{2,1,0:T(8,128)(2,1)S(1)} %broadcast_select_fusion), channel_id=1, source_target_pairs={{0,2},{1,17},{2,0},{3,19},{16,18},{17,1},{18,16},{19,3},{4,6},{5,2... | collective-permute-start | bytes 786440 | tf_op jit(solution)/shard_map/ppermute | solution.py:426
  36.1 4.0 %collective-permute-start.6 = (f32[1,28,256]{2,1,0:T(8,128)S(1)}, f32[1,28,256]{2,1,0:T(8,128)S(1)}, u32[]{:S(2)}, u32[]{:S(2)}) collective-permute-start(f32[1,28,256]{2,1,0:T(8,128)S(1)} %maximum_bitcast_fusion), channel_id=1, source_target_pairs={{0,12},{4,8},{8,4},{12,0},{1,13},{5,9},{9,5},{13,1},{2,14},{6,10},... | collective-permute-start | bytes 86024 | tf_op jit(solution)/shard_map/ppermute | solution.py:426
  36.2 21.5 %collective-permute-start.10 = (bf16[4,256,128]{2,1,0:T(8,128)(2,1)S(1)}, bf16[4,256,128]{2,1,0:T(8,128)(2,1)S(1)}, u32[]{:S(2)}, u32[]{:S(2)}) collective-permute-start(bf16[4,256,128]{2,1,0:T(8,128)(2,1)S(1)} %bitcast.72), channel_id=1, source_target_pairs={{0,12},{4,8},{8,4},{12,0},{1,13},{5,9},{9,5},{13,1},{2,14},{6,10},... | collective-permute-start | bytes 786440 | tf_op jit(solution)/shard_map/ppermute | solution.py:426
  37.6 22.3 %collective-permute-start.9 = (bf16[4,256,128]{2,1,0:T(8,128)(2,1)S(1)}, bf16[4,256,128]{2,1,0:T(8,128)(2,1)}, u32[]{:S(2)}, u32[]{:S(2)}) collective-permute-start(bf16[4,256,128]{2,1,0:T(8,128)(2,1)S(1)} %bitcast.71), channel_id=1, source_target_pairs={{0,8},{4,12},{8,0},{12,4},{1,9},{5,13},{9,1},{13,5},{2,10},{6,14},... | collective-permute-start | bytes 786440 | tf_op jit(solution)/shard_map/ppermute | solution.py:426
  40.1 7.1 %collective-permute-start.7 = (f32[2,28,256]{2,1,0:T(8,128)S(1)}, f32[2,28,256]{2,1,0:T(8,128)S(1)}, u32[]{:S(2)}, u32[]{:S(2)}) collective-permute-start(f32[2,28,256]{2,1,0:T(8,128)S(1)} %pad_maximum_fusion.7), channel_id=1, source_target_pairs={{0,4},{4,0},{8,12},{12,8},{1,5},{5,1},{9,13},{13,9},{2,6},{6,2},{1... | collective-permute-start | bytes 172040 | tf_op jit(solution)/shard_map/ppermute | solution.py:426
  41.9 18.0 %collective-permute-start.8 = (bf16[4,256,128]{2,1,0:T(8,128)(2,1)S(1)}, bf16[4,256,128]{2,1,0:T(8,128)(2,1)}, u32[]{:S(2)}, u32[]{:S(2)}) collective-permute-start(bf16[4,256,128]{2,1,0:T(8,128)(2,1)S(1)} %get-tuple-element.66), channel_id=1, source_target_pairs={{0,4},{4,0},{8,12},{12,8},{1,5},{5,1},{9,13},{13,9},{2,6},{6,2},{1... | collective-permute-start | bytes 786440 | tf_op jit(solution)/shard_map/ppermute | solution.py:426
  42.2 24.0 %copy-start.1 = (bf16[4,4,32,1024]{3,2,1,0:T(8,128)(2,1)}, bf16[4,4,32,1024]{3,2,1,0:T(8,128)(2,1)S(1)}, u32[]{:S(2)}) copy-start(bf16[4,4,32,1024]{3,2,1,0:T(8,128)(2,1)S(1)} %pad_maximum_fusion.1.mine.refs_1_) | copy-start | bytes 3145732
  47.2 40.9 %collective-permute-start.20 = (bf16[4,4,32,1024]{3,2,1,0:T(8,128)(2,1)S(1)}, bf16[4,4,32,1024]{3,2,1,0:T(8,128)(2,1)}, u32[]{:S(2)}, u32[]{:S(2)}) collective-permute-start(bf16[4,4,32,1024]{3,2,1,0:T(8,128)(2,1)S(1)} %pad_maximum_fusion.1.mine.refs_1_), channel_id=1, source_target_pairs={{0,1},{1,0},{2,3},{3,2},{16,17},{17,16},{18,19},{19,18},{4,5},{5,4... | collective-permute-start | bytes 3145736 | tf_op jit(solution)/shard_map/ppermute | solution.py:426
  57.7 2.2 %copy-start.9 = (bf16[4,256,128]{2,1,0:T(8,128)(2,1)}, bf16[4,256,128]{2,1,0:T(8,128)(2,1)S(1)}, u32[]{:S(2)}) copy-start(bf16[4,256,128]{2,1,0:T(8,128)(2,1)S(1)} %collective-permute-done.10.refs_6_.rest_3_) | copy-start | bytes 786436
  66.2 7.9 %collective-permute-start.11 = (bf16[4,32,1024]{2,1,0:T(8,128)(2,1)}, bf16[4,32,1024]{2,1,0:T(8,128)(2,1)S(1)}, u32[]{:S(2)}, u32[]{:S(2)}) collective-permute-start(bf16[4,32,1024]{2,1,0:T(8,128)(2,1)} %get-tuple-element.70), channel_id=1, source_target_pairs={{0,4},{4,8},{8,12},{1,5},{5,9},{9,13},{2,6},{6,10},{10,14},{3,7},{... | collective-permute-start | bytes 786440 | tf_op jit(solution)/shard_map/ppermute | solution.py:467
  70.0 7.3 %collective-permute-start.12 = (bf16[4,32,1024]{2,1,0:T(8,128)(2,1)}, bf16[4,32,1024]{2,1,0:T(8,128)(2,1)S(1)}, u32[]{:S(2)}, u32[]{:S(2)}) collective-permute-start(bf16[4,32,1024]{2,1,0:T(8,128)(2,1)} %get-tuple-element.71), channel_id=1, source_target_pairs={{4,0},{8,4},{12,8},{5,1},{9,5},{13,9},{6,2},{10,6},{14,10},{7,3},{... | collective-permute-start | bytes 786440 | tf_op jit(solution)/shard_map/ppermute | solution.py:468
  74.1 3.9 %copy-start.16 = (bf16[4,32,1024]{2,1,0:T(8,128)(2,1)}, bf16[4,32,1024]{2,1,0:T(8,128)(2,1)S(1)}, u32[]{:S(2)}) copy-start(bf16[4,32,1024]{2,1,0:T(8,128)(2,1)S(1)} %collective-permute-done.11.row_low) | copy-start | bytes 786436
  77.3 17.4 %copy-start.17 = (bf16[4,32,1024]{2,1,0:T(8,128)(2,1)}, bf16[4,32,1024]{2,1,0:T(8,128)(2,1)S(1)}, u32[]{:S(2)}) copy-start(bf16[4,32,1024]{2,1,0:T(8,128)(2,1)S(1)} %collective-permute-done.12.row_high) | copy-start | bytes 786436
  78.0 12.1 %collective-permute-start.13 = (bf16[6,32,1024]{2,1,0:T(8,128)(2,1)}, bf16[6,32,1024]{2,1,0:T(8,128)(2,1)S(1)}, u32[]{:S(2)}, u32[]{:S(2)}) collective-permute-start(bf16[6,32,1024]{2,1,0:T(8,128)(2,1)} %get-tuple-element.107), channel_id=1, source_target_pairs={{0,1},{1,2},{2,3},{4,5},{5,6},{6,7},{8,9},{9,10},{10,11},{12,13},{... | collective-permute-start | bytes 1179656 | tf_op jit(solution)/shard_map/ppermute | solution.py:475
  85.1 9.6 %collective-permute-start.14 = (bf16[6,32,1024]{2,1,0:T(8,128)(2,1)}, bf16[6,32,1024]{2,1,0:T(8,128)(2,1)}, u32[]{:S(2)}, u32[]{:S(2)}) collective-permute-start(bf16[6,32,1024]{2,1,0:T(8,128)(2,1)} %get-tuple-element.106), channel_id=1, source_target_pairs={{1,0},{2,1},{3,2},{5,4},{6,5},{7,6},{9,8},{10,9},{11,10},{13,12},{... | collective-permute-start | bytes 1179656 | tf_op jit(solution)/shard_map/ppermute | solution.py:476
  87.0 19.0 %collective-permute-start.24 = (bf16[4,256,128]{2,1,0:T(8,128)(2,1)}, bf16[4,256,128]{2,1,0:T(8,128)(2,1)S(1)}, u32[]{:S(2)}, u32[]{:S(2)}) collective-permute-start(bf16[4,256,128]{2,1,0:T(8,128)(2,1)} %bitcast.50), channel_id=1, source_target_pairs={{0,4},{4,0},{8,12},{12,8},{1,5},{5,1},{9,13},{13,9},{2,6},{6,2},{1... | collective-permute-start | bytes 786440 | tf_op jit(solution)/shard_map/ppermute | solution.py:426
  87.1 18.9 %collective-permute-start.25 = (bf16[4,256,128]{2,1,0:T(8,128)(2,1)}, bf16[4,256,128]{2,1,0:T(8,128)(2,1)S(1)}, u32[]{:S(2)}, u32[]{:S(2)}) collective-permute-start(bf16[4,256,128]{2,1,0:T(8,128)(2,1)} %bitcast.52), channel_id=1, source_target_pairs={{0,8},{4,12},{8,0},{12,4},{1,9},{5,13},{9,1},{13,5},{2,10},{6,14},... | collective-permute-start | bytes 786440 | tf_op jit(solution)/shard_map/ppermute | solution.py:426
  88.1 23.7 %collective-permute-start.26 = (bf16[4,256,128]{2,1,0:T(8,128)(2,1)}, bf16[4,256,128]{2,1,0:T(8,128)(2,1)S(1)}, u32[]{:S(2)}, u32[]{:S(2)}) collective-permute-start(bf16[4,256,128]{2,1,0:T(8,128)(2,1)} %bitcast.51), channel_id=1, source_target_pairs={{0,12},{4,8},{8,4},{12,0},{1,13},{5,9},{9,5},{13,1},{2,14},{6,10},... | collective-permute-start | bytes 786440 | tf_op jit(solution)/shard_map/ppermute | solution.py:426
  90.1 4.6 %copy-start.20 = (bf16[6,32,1024]{2,1,0:T(8,128)(2,1)}, bf16[6,32,1024]{2,1,0:T(8,128)(2,1)S(1)}, u32[]{:S(2)}) copy-start(bf16[6,32,1024]{2,1,0:T(8,128)(2,1)S(1)} %collective-permute-done.13.plane_low) | copy-start | bytes 1179652
  106.0 5.8 %copy-start.3 = (bf16[4,256,128]{2,1,0:T(8,128)(2,1)}, bf16[4,256,128]{2,1,0:T(8,128)(2,1)S(1)}, u32[]{:S(2)}) copy-start(bf16[4,256,128]{2,1,0:T(8,128)(2,1)S(1)} %collective-permute-done.24.refs_4_.rest_1_) | copy-start | bytes 786436
  106.0 5.8 %copy-start.4 = (bf16[4,256,128]{2,1,0:T(8,128)(2,1)}, bf16[4,256,128]{2,1,0:T(8,128)(2,1)S(1)}, u32[]{:S(2)}) copy-start(bf16[4,256,128]{2,1,0:T(8,128)(2,1)S(1)} %collective-permute-done.25.refs_5_.rest_2_) | copy-start | bytes 786436
  111.8 0.7 copy-start.5
  120.0 10.1 %collective-permute-start.27 = (bf16[4,32,1024]{2,1,0:T(8,128)(2,1)}, bf16[4,32,1024]{2,1,0:T(8,128)(2,1)S(1)}, u32[]{:S(2)}, u32[]{:S(2)}) collective-permute-start(bf16[4,32,1024]{2,1,0:T(8,128)(2,1)} %get-tuple-element.85), channel_id=1, source_target_pairs={{0,4},{4,8},{8,12},{1,5},{5,9},{9,13},{2,6},{6,10},{10,14},{3,7},{... | collective-permute-start | bytes 786440 | tf_op jit(solution)/shard_map/ppermute | solution.py:467
  122.0 9.8 %collective-permute-start.28 = (bf16[4,32,1024]{2,1,0:T(8,128)(2,1)}, bf16[4,32,1024]{2,1,0:T(8,128)(2,1)S(1)}, u32[]{:S(2)}, u32[]{:S(2)}) collective-permute-start(bf16[4,32,1024]{2,1,0:T(8,128)(2,1)} %get-tuple-element.86), channel_id=1, source_target_pairs={{4,0},{8,4},{12,8},{5,1},{9,5},{13,9},{6,2},{10,6},{14,10},{7,3},{... | collective-permute-start | bytes 786440 | tf_op jit(solution)/shard_map/ppermute | solution.py:468
  130.1 2.3 %copy-start.14 = (bf16[4,32,1024]{2,1,0:T(8,128)(2,1)}, bf16[4,32,1024]{2,1,0:T(8,128)(2,1)S(1)}, u32[]{:S(2)}) copy-start(bf16[4,32,1024]{2,1,0:T(8,128)(2,1)S(1)} %collective-permute-done.27.row_low) | copy-start | bytes 786436
  130.1 8.3 %copy-start.28 = (bf16[4,256,128]{2,1,0:T(8,128)(2,1)S(1)}, bf16[4,256,128]{2,1,0:T(8,128)(2,1)}, u32[]{:S(2)}) copy-start(bf16[4,256,128]{2,1,0:T(8,128)(2,1)} %get-tuple-element.77) | copy-start | bytes 786436
  130.1 11.0 %copy-start.27 = (bf16[4,256,128]{2,1,0:T(8,128)(2,1)S(1)}, bf16[4,256,128]{2,1,0:T(8,128)(2,1)}, u32[]{:S(2)}) copy-start(bf16[4,256,128]{2,1,0:T(8,128)(2,1)} %get-tuple-element.78) | copy-start | bytes 786436
  131.7 14.1 %copy-start.15 = (bf16[4,32,1024]{2,1,0:T(8,128)(2,1)}, bf16[4,32,1024]{2,1,0:T(8,128)(2,1)S(1)}, u32[]{:S(2)}) copy-start(bf16[4,32,1024]{2,1,0:T(8,128)(2,1)S(1)} %collective-permute-done.28.row_high) | copy-start | bytes 786436
  132.4 8.8 %collective-permute-start.29 = (bf16[6,32,1024]{2,1,0:T(8,128)(2,1)}, bf16[6,32,1024]{2,1,0:T(8,128)(2,1)S(1)}, u32[]{:S(2)}, u32[]{:S(2)}) collective-permute-start(bf16[6,32,1024]{2,1,0:T(8,128)(2,1)} %get-tuple-element.101), channel_id=1, source_target_pairs={{0,1},{1,2},{2,3},{4,5},{5,6},{6,7},{8,9},{9,10},{10,11},{12,13},{... | collective-permute-start | bytes 1179656 | tf_op jit(solution)/shard_map/ppermute | solution.py:475
  136.2 9.6 %collective-permute-start.30 = (bf16[6,32,1024]{2,1,0:T(8,128)(2,1)}, bf16[6,32,1024]{2,1,0:T(8,128)(2,1)S(1)}, u32[]{:S(2)}, u32[]{:S(2)}) collective-permute-start(bf16[6,32,1024]{2,1,0:T(8,128)(2,1)} %get-tuple-element.100), channel_id=1, source_target_pairs={{1,0},{2,1},{3,2},{5,4},{6,5},{7,6},{9,8},{10,9},{11,10},{13,12},{... | collective-permute-start | bytes 1179656 | tf_op jit(solution)/shard_map/ppermute | solution.py:476
  138.4 18.7 %collective-permute-start.21 = (bf16[4,256,128]{2,1,0:T(8,128)(2,1)}, bf16[4,256,128]{2,1,0:T(8,128)(2,1)S(1)}, u32[]{:S(2)}, u32[]{:S(2)}) collective-permute-start(bf16[4,256,128]{2,1,0:T(8,128)(2,1)} %get-tuple-element.76), channel_id=1, source_target_pairs={{0,4},{4,0},{8,12},{12,8},{1,5},{5,1},{9,13},{13,9},{2,6},{6,2},{1... | collective-permute-start | bytes 786440 | tf_op jit(solution)/shard_map/ppermute | solution.py:426
  138.4 20.1 %collective-permute-start.22 = (bf16[4,256,128]{2,1,0:T(8,128)(2,1)S(1)}, bf16[4,256,128]{2,1,0:T(8,128)(2,1)S(1)}, u32[]{:S(2)}, u32[]{:S(2)}) collective-permute-start(bf16[4,256,128]{2,1,0:T(8,128)(2,1)S(1)} %copy-done.28), channel_id=1, source_target_pairs={{0,8},{4,12},{8,0},{12,4},{1,9},{5,13},{9,1},{13,5},{2,10},{6,14},... | collective-permute-start | bytes 786440 | tf_op jit(solution)/shard_map/ppermute | solution.py:426
  141.1 22.2 %collective-permute-start.23 = (bf16[4,256,128]{2,1,0:T(8,128)(2,1)S(1)}, bf16[4,256,128]{2,1,0:T(8,128)(2,1)S(1)}, u32[]{:S(2)}, u32[]{:S(2)}) collective-permute-start(bf16[4,256,128]{2,1,0:T(8,128)(2,1)S(1)} %copy-done.27), channel_id=1, source_target_pairs={{0,12},{4,8},{8,4},{12,0},{1,13},{5,9},{9,5},{13,1},{2,14},{6,10},... | collective-permute-start | bytes 786440 | tf_op jit(solution)/shard_map/ppermute | solution.py:426
  141.3 4.6 %copy-start.18 = (bf16[6,32,1024]{2,1,0:T(8,128)(2,1)}, bf16[6,32,1024]{2,1,0:T(8,128)(2,1)S(1)}, u32[]{:S(2)}) copy-start(bf16[6,32,1024]{2,1,0:T(8,128)(2,1)S(1)} %collective-permute-done.29.plane_low) | copy-start | bytes 1179652
  145.8 0.8 copy-start.19
  163.3 17.7 %collective-permute-start.31 = (bf16[4,256,128]{2,1,0:T(8,128)(2,1)}, bf16[4,256,128]{2,1,0:T(8,128)(2,1)S(1)}, u32[]{:S(2)}, u32[]{:S(2)}) collective-permute-start(bf16[4,256,128]{2,1,0:T(8,128)(2,1)} %get-tuple-element.95), channel_id=1, source_target_pairs={{0,8},{4,12},{8,0},{12,4},{1,9},{5,13},{9,1},{13,5},{2,10},{6,14},... | collective-permute-start | bytes 786440 | tf_op jit(solution)/shard_map/ppermute | solution.py:426
  163.3 25.8 %collective-permute-start.32 = (bf16[4,256,128]{2,1,0:T(8,128)(2,1)}, bf16[4,256,128]{2,1,0:T(8,128)(2,1)S(1)}, u32[]{:S(2)}, u32[]{:S(2)}) collective-permute-start(bf16[4,256,128]{2,1,0:T(8,128)(2,1)} %get-tuple-element.96), channel_id=1, source_target_pairs={{0,12},{4,8},{8,4},{12,0},{1,13},{5,9},{9,5},{13,1},{2,14},{6,10},... | collective-permute-start | bytes 786440 | tf_op jit(solution)/shard_map/ppermute | solution.py:426
  165.2 24.2 %collective-permute-start.33 = (bf16[4,256,128]{2,1,0:T(8,128)(2,1)}, bf16[4,256,128]{2,1,0:T(8,128)(2,1)S(1)}, u32[]{:S(2)}, u32[]{:S(2)}) collective-permute-start(bf16[4,256,128]{2,1,0:T(8,128)(2,1)} %get-tuple-element.97), channel_id=1, source_target_pairs={{0,4},{4,0},{8,12},{12,8},{1,5},{5,1},{9,13},{13,9},{2,6},{6,2},{1... | collective-permute-start | bytes 786440 | tf_op jit(solution)/shard_map/ppermute | solution.py:426
  166.9 0.9 copy-start.22
  168.1 1.0 copy-start.21
  170.3 19.5 %copy-start.7 = (bf16[256,4,512]{2,1,0:T(4,128)(2,1)}, bf16[256,4,512]{2,1,0:T(4,128)(2,1)S(1)}, u32[]{:S(2)}) copy-start(bf16[256,4,512]{2,1,0:T(4,128)(2,1)S(1)} %copy_dynamic-update-slice_fusion.4) | copy-start | bytes 3145732
  189.8 1.0 copy-start.8

commit v14 on v13

--- a/solution.py
+++ b/solution.py
@@ -8,6 +8,7 @@
 CX = 32
 CY = 16
 LANES = 128
+BLOCK = 2 * LANES
 
 
 root_half = 0.7071067811865476
@@ -134,6 +135,11 @@
         out[z] = total.astype(out.dtype)
 
 
+def part_of(ref, sub):
+    lanes = slice(sub * LANES, (sub + 1) * LANES)
+    return ref.at[(slice(None),) * (len(ref.shape) - 1) + (lanes,)]
+
+
 def put_copy(shift, ready, outputs, left):
     return pltpu.make_async_copy(ready.at[shift], outputs[shift], left.at[shift])
 
@@ -154,19 +160,22 @@
         start_all(copies)
         start_all(block_copies(inputs, held, arrived))
 
-    fill_pairs(pairs, own, row_low, row_high, plane_low, plane_high)
-    fill_factors(factors, taps, False)
-    lanes = pl.ds(pl.multiple_of(step * LANES, LANES), LANES)
-    for z in range(planes):
-        for t in range(rows // 2):
-            for odd, mixed in enumerate(stencil_pair(pairs, factors, z, t)):
-                y = 2 * t + odd
-                mixed = mixed + taps[0, 27][None, :]
-                half = 0.5 * (1.0 + lax.erf(mixed * root_half))
-                at = (z * rows + y) * extent
-                active[at : at + extent, lanes] = (mixed * half).astype(active.dtype)
-                bell = jnp.exp(-0.5 * mixed * mixed) * inv_root_two_pi
-                slope[z, y] = (half + mixed * bell).astype(slope.dtype)
+    for sub in range(BLOCK // LANES):
+        fields = [part_of(f, sub) for f in (own, row_low, row_high, plane_low, plane_high)]
+        table, result = part_of(taps, sub), part_of(slope, sub)
+        fill_pairs(pairs, *fields)
+        fill_factors(factors, table, False)
+        lanes = pl.ds(pl.multiple_of(step * BLOCK + sub * LANES, LANES), LANES)
+        for z in range(planes):
+            for t in range(rows // 2):
+                for odd, mixed in enumerate(stencil_pair(pairs, factors, z, t)):
+                    y = 2 * t + odd
+                    mixed = mixed + table[0, 27][None, :]
+                    half = 0.5 * (1.0 + lax.erf(mixed * root_half))
+                    at = (z * rows + y) * extent
+                    active[at : at + extent, lanes] = (mixed * half).astype(active.dtype)
+                    bell = jnp.exp(-0.5 * mixed * mixed) * inv_root_two_pi
+                    result[z, y] = (half + mixed * bell).astype(result.dtype)
 
     @pl.when(step == pl.num_programs(0) - 1)
     def _():
@@ -202,14 +211,16 @@
         start_all(copies)
         start_all(block_copies(inputs, held, arrived))
 
-    fill_pairs(pairs, own, row_low, row_high, plane_low, plane_high)
-    fill_factors(factors, taps, True)
-    lanes = pl.ds(pl.multiple_of(step * LANES, LANES), LANES)
-    for z in range(planes):
-        for t in range(rows // 2):
-            for odd, total in enumerate(stencil_pair(pairs, factors, z, t)):
-                at = (z * rows + 2 * t + odd) * extent
-                grads[at : at + extent, lanes] = total.astype(grads.dtype)
+    for sub in range(BLOCK // LANES):
+        fields = [part_of(f, sub) for f in (own, row_low, row_high, plane_low, plane_high)]
+        fill_pairs(pairs, *fields)
+        fill_factors(factors, part_of(taps, sub), True)
+        lanes = pl.ds(pl.multiple_of(step * BLOCK + sub * LANES, LANES), LANES)
+        for z in range(planes):
+            for t in range(rows // 2):
+                for odd, total in enumerate(stencil_pair(pairs, factors, z, t)):
+                    at = (z * rows + 2 * t + odd) * extent
+                    grads[at : at + extent, lanes] = total.astype(grads.dtype)
 
     @pl.when(step == pl.num_programs(0) - 1)
     def _():
@@ -238,11 +249,11 @@
 def stencil(here, own, halo, taps, weight, blocks, forward):
     planes, rows, extent, channels = own.shape
     cells = planes * rows * extent
-    per_table = taps.shape[2] // LANES
+    per_table = taps.shape[2] // BLOCK
 
     def block(*lead):
         zeros = (0,) * len(lead)
-        return pl.BlockSpec(lead + (LANES,), lambda c, here: zeros + (c,))
+        return pl.BlockSpec(lead + (BLOCK,), lambda c, here: zeros + (c,))
 
     def table_at(c, here):
         away = (c // per_table) ^ here[0]
@@ -258,7 +269,7 @@
         block(planes, extent),
         block(rows + 2, extent),
         block(rows + 2, extent),
-        pl.BlockSpec((1, 28, LANES), table_at),
+        pl.BlockSpec((1, 28, BLOCK), table_at),
         anywhere,
         anywhere,
     ]
@@ -272,7 +283,7 @@
         forward_kernel if forward else backward_kernel,
         grid_spec=pltpu.PrefetchScalarGridSpec(
             num_scalar_prefetch=1,
-            grid=(channels // LANES,),
+            grid=(channels // BLOCK,),
             in_specs=in_specs,
             out_specs=out_specs,
             scratch_shapes=[
@@ -459,7 +470,8 @@
         mixed = jnp.where(seat & 1 == 0, over_y, over_x)
         mixed, beside = lax.optimization_barrier((mixed, beside))
         far = swap(mixed, others, lambda i: i ^ (4 if i & 1 else 2))
-        mine = jnp.stack([column, over_x, over_y, far])
+        base = lax.optimization_barrier(jnp.stack([column, over_x, over_y, over_y]))
+        mine = lax.dynamic_update_slice_in_dim(base, far[None], 3, axis=0)
         return (mine, swap(mine, others, lambda i: i ^ 1)), beside
 
     def halo_of(first, last, fore, back):
@@ -597,7 +609,7 @@
     groups, space = lax.axis_size("groups"), lax.axis_size("space")
     whole_rows = CY % (2 * parts) == 0 and (CY // parts * CX) % LANES == 0
     whole_rows = whole_rows and parts & (parts - 1) == 0
-    whole_shares = own % LANES == 0 and own % (16 * groups * space) == 0
+    whole_shares = own % BLOCK == 0 and own % (16 * groups * space) == 0
     split = whole_rows and whole_shares and (groups, space) == (2, 4)
     chosen = split_cells_body if split else exchange_body
     return chosen(volume, out_grad, weight_in, weight_out, filter_taps, filter_bias)

time: 192 us -> 189 us (0.984)
  starting transfers between devices: 68.5 us -> 65 us
  Pallas kernels: 35.5 us -> 32.3 us
  waiting for transfers between devices: 64.9 us -> 67.7 us
    pallas_call x2, Pallas kernels: 21.7 us -> 18.5 us  [stencil(): pl.pallas_call(forward_kernel if forward else backward_kernel, grid_spec=...]
    ppermute x26, starting transfers between devices: 42.7 us -> 39.5 us  [swap(): return lax.ppermute(part, axes, [(i, partner(i)) for i in range(count)])]
    ppermute x26, waiting for transfers between devices: 44.8 us -> 48 us  [swap(): return lax.ppermute(part, axes, [(i, partner(i)) for i in range(count)])]
  transfers between devices with their start and end apart: 34 -> 34, of which waited for: 20 -> 20; matrix products, arithmetic and copies ran while one was open for 7% -> 8% of each run, Pallas kernels for 15% -> 13%
where the time goes in v14:
time: 189 us
  waiting for transfers between devices  67.7 us (36%)
  starting transfers between devices  65 us (34%)
  Pallas kernels  32.3 us (17%)
  local copies, waits for them, and re-layouts  19.1 us (10%)
  other arithmetic  3.39 us (2%)
    ppermute x26, waiting for transfers between devices, swap(): return lax.ppermute(part, axes, [(i, partner(i)) for i in range(count)])  48 us
    ppermute x26, starting transfers between devices, swap(): return lax.ppermute(part, axes, [(i, partner(i)) for i in range(count)])  39.5 us
    pallas_call x2, Pallas kernels, stencil(): pl.pallas_call(forward_kernel if forward else backward_kernel, grid_spec=...  18.5 us
    pallas_call x2, Pallas kernels, product_call(): pl.pallas_call(lambda *refs: kernel(*refs, count=count), grid_spec=pltpu....  13.8 us
    ppermute x2, starting transfers between devices, halo_of(): plane_low = lax.ppermute(joined(fore, planes - 1), 'space', forward)  10.9 us
    ppermute x2, waiting for transfers between devices, halo_of(): plane_high = lax.ppermute(joined(back, 0), 'space', backward)  9.17 us
    unnamed x64, local copies, waits for them, and re-layouts  9.08 us
    ppermute x2, waiting for transfers between devices, halo_of(): row_low = lax.ppermute(last, 'chan', forward)  8.06 us
  transfers between devices with their start and end apart: 34, of which 20 were waited for; matrix products, arithmetic and copies ran while one was open for 8% of the time, Pallas kernels for 13%

profile of v14, /device:TPU:17, one launch (start us, length us, event | category | flops | bytes accessed | tf_op | source)
XLA Modules:
  0.0 188.6 jit_solution(357325417424728197)
XLA Ops:
  0.7 1.0 dynamic-slice_bitcast_fusion.1
  1.8 0.8 dynamic-slice_bitcast_fusion
  2.7 1.3 collective-permute-start.15
  4.0 1.0 constant_dynamic-slice_fusion.2
  5.0 0.7 copy.49
  5.9 3.2 %collective-permute-start.1 = (bf16[2,32,1024]{2,1,0:T(8,128)(2,1)S(1)}, bf16[2,32,1024]{2,1,0:T(8,128)(2,1)S(1)}, u32[]{:S(2)}, u32[]{:S(2)}) collective-permute-start(bf16[2,32,1024]{2,1,0:T(8,128)(2,1)S(1)} %pad_maximum_fusion.4), channel_id=1, source_target_pairs={{0,4},{4,0},{8,12},{12,8},{1,5},{5,1},{9,13},{13,9},{2,6},{6,2},{1... | collective-permute-start | bytes 393224 | tf_op jit(solution)/shard_map/ppermute | solution.py:437
  9.7 0.7 copy.48
  10.5 0.7 pad_maximum_fusion.6
  11.7 0.8 copy.53
  12.5 0.7 copy.52
  13.4 0.7 copy.51
  14.1 1.2 collective-permute-start.2
  15.3 1.2 collective-permute-start.3
  16.9 0.7 copy.50
  17.6 0.8 copy_bitcast_fusion
  18.3 1.0 collective-permute-done.2
  19.3 1.2 collective-permute-done.3
  21.5 1.0 fusion
  22.5 1.3 collective-permute-start.17
  23.8 1.2 collective-permute-start.18
  25.2 1.5 collective-permute-done.4
  26.7 7.0 %collective-permute-start.5 = (bf16[4,4,32,1024]{3,2,1,0:T(8,128)(2,1)S(1)}, bf16[4,4,32,1024]{3,2,1,0:T(8,128)(2,1)}, u32[]{:S(2)}, u32[]{:S(2)}) collective-permute-start(bf16[4,4,32,1024]{3,2,1,0:T(8,128)(2,1)S(1)} %bitcast_dynamic-update-slice_fusion.1.refs_1_.mine), channel_id=1, source_target_pairs={{0,1},{1,0},{2,3},{3,2},{16,17},{17,16},{18,19},{19,18},{4,5},{5,4... | collective-permute-start | bytes 3145736 | tf_op jit(solution)/shard_map/ppermute | solution.py:437
  34.7 1.3 collective-permute-start.10
  36.0 3.4 %collective-permute-start.9 = (bf16[4,256,128]{2,1,0:T(8,128)(2,1)S(1)}, bf16[4,256,128]{2,1,0:T(8,128)(2,1)}, u32[]{:S(2)}, u32[]{:S(2)}) collective-permute-start(bf16[4,256,128]{2,1,0:T(8,128)(2,1)S(1)} %bitcast.73), channel_id=1, source_target_pairs={{0,8},{4,12},{8,0},{12,4},{1,9},{5,13},{9,1},{13,5},{2,10},{6,14},... | collective-permute-start | bytes 786440 | tf_op jit(solution)/shard_map/ppermute | solution.py:437
  39.6 2.1 %collective-permute-start.8 = (bf16[4,256,128]{2,1,0:T(8,128)(2,1)S(1)}, bf16[4,256,128]{2,1,0:T(8,128)(2,1)}, u32[]{:S(2)}, u32[]{:S(2)}) collective-permute-start(bf16[4,256,128]{2,1,0:T(8,128)(2,1)S(1)} %get-tuple-element.66), channel_id=1, source_target_pairs={{0,4},{4,0},{8,12},{12,8},{1,5},{5,1},{9,13},{13,9},{2,6},{6,2},{1... | collective-permute-start | bytes 786440 | tf_op jit(solution)/shard_map/ppermute | solution.py:437
  41.7 7.0 %collective-permute-done.7 = f32[2,28,256]{2,1,0:T(8,128)S(1)} collective-permute-done((f32[2,28,256]{2,1,0:T(8,128)S(1)}, f32[2,28,256]{2,1,0:T(8,128)S(1)}, u32[]{:S(2)}, u32[]{:S(2)}) %collective-permute-start.7) | collective-permute-done | bytes 57376 | tf_op jit(solution)/shard_map/ppermute | solution.py:437
  48.7 6.1 %collective-permute-start.20 = (bf16[4,4,32,1024]{3,2,1,0:T(8,128)(2,1)S(1)}, bf16[4,4,32,1024]{3,2,1,0:T(8,128)(2,1)}, u32[]{:S(2)}, u32[]{:S(2)}) collective-permute-start(bf16[4,4,32,1024]{3,2,1,0:T(8,128)(2,1)S(1)} %bitcast_dynamic-update-slice_fusion.mine.refs_1_), channel_id=1, source_target_pairs={{0,1},{1,0},{2,3},{3,2},{16,17},{17,16},{18,19},{19,18},{4,5},{5,4... | collective-permute-start | bytes 3145736 | tf_op jit(solution)/shard_map/ppermute | solution.py:437
  55.5 3.0 %collective-permute-done.9.refs_5_.rest_2_ = bf16[4,256,128]{2,1,0:T(8,128)(2,1)} collective-permute-done((bf16[4,256,128]{2,1,0:T(8,128)(2,1)S(1)}, bf16[4,256,128]{2,1,0:T(8,128)(2,1)}, u32[]{:S(2)}, u32[]{:S(2)}) %collective-permute-start.9) | collective-permute-done | bytes 262176 | tf_op jit(solution)/shard_map/ppermute | solution.py:437
  58.5 6.2 %shard_map.77 = (bf16[512,1024]{1,0:T(8,128)(2,1)}, bf16[4,32,1024]{2,1,0:T(8,128)(2,1)}, bf16[4,32,1024]{2,1,0:T(8,128)(2,1)}, bf16[6,32,1024]{2,1,0:T(8,128)(2,1)}, bf16[6,32,1024]{2,1,0:T(8,128)(2,1)}) custom-call(s32[2]{0:T(128)} %pad_add_fusion.refs_0_.here, bf16[4,4,32,1024]{3,2,1,0:T(8,128)(2,1)} %copy-done.2, ...), custom_call_target="tpu_custom_call" | custom-call | tf_op jit(solution)/shard_map/pallas_call | solution.py:392
  64.8 2.7 %collective-permute-start.11 = (bf16[4,32,1024]{2,1,0:T(8,128)(2,1)}, bf16[4,32,1024]{2,1,0:T(8,128)(2,1)S(1)}, u32[]{:S(2)}, u32[]{:S(2)}) collective-permute-start(bf16[4,32,1024]{2,1,0:T(8,128)(2,1)} %get-tuple-element.70), channel_id=1, source_target_pairs={{0,4},{4,8},{8,12},{1,5},{5,9},{9,13},{2,6},{6,10},{10,14},{3,7},{... | collective-permute-start | bytes 786440 | tf_op jit(solution)/shard_map/ppermute | solution.py:479
  67.5 2.6 %collective-permute-start.12 = (bf16[4,32,1024]{2,1,0:T(8,128)(2,1)}, bf16[4,32,1024]{2,1,0:T(8,128)(2,1)S(1)}, u32[]{:S(2)}, u32[]{:S(2)}) collective-permute-start(bf16[4,32,1024]{2,1,0:T(8,128)(2,1)} %get-tuple-element.71), channel_id=1, source_target_pairs={{4,0},{8,4},{12,8},{5,1},{9,5},{13,9},{6,2},{10,6},{14,10},{7,3},{... | collective-permute-start | bytes 786440 | tf_op jit(solution)/shard_map/ppermute | solution.py:480
  70.1 3.3 %collective-permute-done.11.row_low = bf16[4,32,1024]{2,1,0:T(8,128)(2,1)S(1)} collective-permute-done((bf16[4,32,1024]{2,1,0:T(8,128)(2,1)}, bf16[4,32,1024]{2,1,0:T(8,128)(2,1)S(1)}, u32[]{:S(2)}, u32[]{:S(2)}) %collective-permute-start.11) | collective-permute-done | bytes 262176 | tf_op jit(solution)/shard_map/ppermute | solution.py:479
  73.4 0.7 slice_dynamic-update-slice_fusion.5
  74.1 1.0 collective-permute-done.12.row_high
  75.2 0.7 slice_dynamic-update-slice_fusion.4
  75.9 7.1 %collective-permute-start.13 = (bf16[6,32,1024]{2,1,0:T(8,128)(2,1)}, bf16[6,32,1024]{2,1,0:T(8,128)(2,1)S(1)}, u32[]{:S(2)}, u32[]{:S(2)}) collective-permute-start(bf16[6,32,1024]{2,1,0:T(8,128)(2,1)} %get-tuple-element.107), channel_id=1, source_target_pairs={{0,1},{1,2},{2,3},{4,5},{5,6},{6,7},{8,9},{9,10},{10,11},{12,13},{... | collective-permute-start | bytes 1179656 | tf_op jit(solution)/shard_map/ppermute | solution.py:487
  83.0 1.9 %collective-permute-start.14 = (bf16[6,32,1024]{2,1,0:T(8,128)(2,1)}, bf16[6,32,1024]{2,1,0:T(8,128)(2,1)}, u32[]{:S(2)}, u32[]{:S(2)}) collective-permute-start(bf16[6,32,1024]{2,1,0:T(8,128)(2,1)} %get-tuple-element.106), channel_id=1, source_target_pairs={{1,0},{2,1},{3,2},{5,4},{6,5},{7,6},{9,8},{10,9},{11,10},{13,12},{... | collective-permute-start | bytes 1179656 | tf_op jit(solution)/shard_map/ppermute | solution.py:488
  85.0 1.0 collective-permute-start.25
  85.9 1.7 collective-permute-start.26
  88.0 4.6 %collective-permute-done.14.plane_high = bf16[6,32,1024]{2,1,0:T(8,128)(2,1)} collective-permute-done((bf16[6,32,1024]{2,1,0:T(8,128)(2,1)}, bf16[6,32,1024]{2,1,0:T(8,128)(2,1)}, u32[]{:S(2)}, u32[]{:S(2)}) %collective-permute-start.14) | collective-permute-done | bytes 393248 | tf_op jit(solution)/shard_map/ppermute | solution.py:488
  92.6 9.8 %shard_map.78 = (bf16[4,256,128]{2,1,0:T(8,128)(2,1)}, bf16[4,256,128]{2,1,0:T(8,128)(2,1)}, bf16[4,256,128]{2,1,0:T(8,128)(2,1)}, bf16[4,256,128]{2,1,0:T(8,128)(2,1)}, bf16[4,4,32,1024]{3,2,1,0:T(8,128)(2,1)}) custom-call(s32[2]{0:T(128)} %pad_add_fusion.refs_0_.here, bf16[4,4,32,1024]{3,2,1,0:T(8,128)(2,1)} %bitcast.64, bf16[4,32,1024]{2,1,0:T(8,128)(2,1)} %copy-done.16, ...), custom_call_target="tpu_custom_call" | custom-call | tf_op jit(solution)/shard_map/pallas_call | solution.py:282
  102.4 1.3 collective-permute-done.25.refs_5_.rest_2_
  103.6 6.1 %collective-permute-done.26.refs_6_.rest_3_ = bf16[4,256,128]{2,1,0:T(8,128)(2,1)S(1)} collective-permute-done((bf16[4,256,128]{2,1,0:T(8,128)(2,1)}, bf16[4,256,128]{2,1,0:T(8,128)(2,1)S(1)}, u32[]{:S(2)}, u32[]{:S(2)}) %collective-permute-start.26) | collective-permute-done | bytes 262176 | tf_op jit(solution)/shard_map/ppermute | solution.py:437
  109.7 0.7 copy-done.5
  110.4 7.5 %shard_map.79 = (bf16[512,1024]{1,0:T(8,128)(2,1)}, bf16[4,32,1024]{2,1,0:T(8,128)(2,1)}, bf16[4,32,1024]{2,1,0:T(8,128)(2,1)}, bf16[6,32,1024]{2,1,0:T(8,128)(2,1)}, bf16[6,32,1024]{2,1,0:T(8,128)(2,1)}) custom-call(s32[2]{0:T(128)} %pad_add_fusion.refs_0_.here, bf16[4,4,32,1024]{3,2,1,0:T(8,128)(2,1)} %copy-done.1, ...), custom_call_target="tpu_custom_call" | custom-call | tf_op jit(solution)/shard_map/pallas_call | solution.py:392
  117.9 1.9 %collective-permute-start.27 = (bf16[4,32,1024]{2,1,0:T(8,128)(2,1)}, bf16[4,32,1024]{2,1,0:T(8,128)(2,1)S(1)}, u32[]{:S(2)}, u32[]{:S(2)}) collective-permute-start(bf16[4,32,1024]{2,1,0:T(8,128)(2,1)} %get-tuple-element.85), channel_id=1, source_target_pairs={{0,4},{4,8},{8,12},{1,5},{5,9},{9,13},{2,6},{6,10},{10,14},{3,7},{... | collective-permute-start | bytes 786440 | tf_op jit(solution)/shard_map/ppermute | solution.py:479
  119.9 3.4 %collective-permute-start.28 = (bf16[4,32,1024]{2,1,0:T(8,128)(2,1)}, bf16[4,32,1024]{2,1,0:T(8,128)(2,1)S(1)}, u32[]{:S(2)}, u32[]{:S(2)}) collective-permute-start(bf16[4,32,1024]{2,1,0:T(8,128)(2,1)} %get-tuple-element.86), channel_id=1, source_target_pairs={{4,0},{8,4},{12,8},{5,1},{9,5},{13,9},{6,2},{10,6},{14,10},{7,3},{... | collective-permute-start | bytes 786440 | tf_op jit(solution)/shard_map/ppermute | solution.py:480
  123.2 4.7 %collective-permute-done.27.row_low = bf16[4,32,1024]{2,1,0:T(8,128)(2,1)S(1)} collective-permute-done((bf16[4,32,1024]{2,1,0:T(8,128)(2,1)}, bf16[4,32,1024]{2,1,0:T(8,128)(2,1)S(1)}, u32[]{:S(2)}, u32[]{:S(2)}) %collective-permute-start.27) | collective-permute-done | bytes 262176 | tf_op jit(solution)/shard_map/ppermute | solution.py:479
  128.6 1.0 collective-permute-done.28.row_high
  129.6 0.7 slice_dynamic-update-slice_fusion
  130.3 3.8 %collective-permute-start.29 = (bf16[6,32,1024]{2,1,0:T(8,128)(2,1)}, bf16[6,32,1024]{2,1,0:T(8,128)(2,1)S(1)}, u32[]{:S(2)}, u32[]{:S(2)}) collective-permute-start(bf16[6,32,1024]{2,1,0:T(8,128)(2,1)} %get-tuple-element.101), channel_id=1, source_target_pairs={{0,1},{1,2},{2,3},{4,5},{5,6},{6,7},{8,9},{9,10},{10,11},{12,13},{... | collective-permute-start | bytes 1179656 | tf_op jit(solution)/shard_map/ppermute | solution.py:487
  134.1 2.1 %collective-permute-start.30 = (bf16[6,32,1024]{2,1,0:T(8,128)(2,1)}, bf16[6,32,1024]{2,1,0:T(8,128)(2,1)S(1)}, u32[]{:S(2)}, u32[]{:S(2)}) collective-permute-start(bf16[6,32,1024]{2,1,0:T(8,128)(2,1)} %get-tuple-element.100), channel_id=1, source_target_pairs={{1,0},{2,1},{3,2},{5,4},{6,5},{7,6},{9,8},{10,9},{11,10},{13,12},{... | collective-permute-start | bytes 1179656 | tf_op jit(solution)/shard_map/ppermute | solution.py:488
  136.3 2.7 %collective-permute-start.22 = (bf16[4,256,128]{2,1,0:T(8,128)(2,1)S(1)}, bf16[4,256,128]{2,1,0:T(8,128)(2,1)S(1)}, u32[]{:S(2)}, u32[]{:S(2)}) collective-permute-start(bf16[4,256,128]{2,1,0:T(8,128)(2,1)S(1)} %copy-done.28), channel_id=1, source_target_pairs={{0,8},{4,12},{8,0},{12,4},{1,9},{5,13},{9,1},{13,5},{2,10},{6,14},... | collective-permute-start | bytes 786440 | tf_op jit(solution)/shard_map/ppermute | solution.py:437
  139.2 4.6 %collective-permute-done.30.plane_high = bf16[6,32,1024]{2,1,0:T(8,128)(2,1)S(1)} collective-permute-done((bf16[6,32,1024]{2,1,0:T(8,128)(2,1)}, bf16[6,32,1024]{2,1,0:T(8,128)(2,1)S(1)}, u32[]{:S(2)}, u32[]{:S(2)}) %collective-permute-start.30) | collective-permute-done | bytes 393248 | tf_op jit(solution)/shard_map/ppermute | solution.py:488
  143.8 0.7 copy-done.19
  144.5 8.7 %shard_map.80 = (bf16[4,256,128]{2,1,0:T(8,128)(2,1)}, bf16[4,256,128]{2,1,0:T(8,128)(2,1)}, bf16[4,256,128]{2,1,0:T(8,128)(2,1)}, bf16[4,256,128]{2,1,0:T(8,128)(2,1)}) custom-call(s32[2]{0:T(128)} %pad_add_fusion.refs_0_.here, bf16[4,4,32,1024]{3,2,1,0:T(8,128)(2,1)} %bitcast.63, bf16[4,32,1024]{2,1,0:T(8,128)(2,1)} %copy-done.14, ...), custom_call_target="tpu_custom_call" | custom-call | tf_op jit(solution)/shard_map/pallas_call | solution.py:282
  153.3 3.2 %collective-permute-done.22 = bf16[4,256,128]{2,1,0:T(8,128)(2,1)S(1)} collective-permute-done((bf16[4,256,128]{2,1,0:T(8,128)(2,1)S(1)}, bf16[4,256,128]{2,1,0:T(8,128)(2,1)S(1)}, u32[]{:S(2)}, u32[]{:S(2)}) %collective-permute-start.22) | collective-permute-done | bytes 262176 | tf_op jit(solution)/shard_map/ppermute | solution.py:437
  156.4 4.7 %collective-permute-done.23 = bf16[4,256,128]{2,1,0:T(8,128)(2,1)S(1)} collective-permute-done((bf16[4,256,128]{2,1,0:T(8,128)(2,1)S(1)}, bf16[4,256,128]{2,1,0:T(8,128)(2,1)S(1)}, u32[]{:S(2)}, u32[]{:S(2)}) %collective-permute-start.23) | collective-permute-done | bytes 262176 | tf_op jit(solution)/shard_map/ppermute | solution.py:437
  161.2 1.9 %collective-permute-start.32 = (bf16[4,256,128]{2,1,0:T(8,128)(2,1)}, bf16[4,256,128]{2,1,0:T(8,128)(2,1)S(1)}, u32[]{:S(2)}, u32[]{:S(2)}) collective-permute-start(bf16[4,256,128]{2,1,0:T(8,128)(2,1)} %get-tuple-element.96), channel_id=1, source_target_pairs={{0,12},{4,8},{8,4},{12,0},{1,13},{5,9},{9,5},{13,1},{2,14},{6,10},... | collective-permute-start | bytes 786440 | tf_op jit(solution)/shard_map/ppermute | solution.py:437
  163.1 1.6 collective-permute-start.33
  165.0 0.7 copy-done.22
  168.1 10.8 %collective-permute-done.31 = bf16[4,256,128]{2,1,0:T(8,128)(2,1)S(1)} collective-permute-done((bf16[4,256,128]{2,1,0:T(8,128)(2,1)}, bf16[4,256,128]{2,1,0:T(8,128)(2,1)S(1)}, u32[]{:S(2)}, u32[]{:S(2)}) %collective-permute-start.31) | collective-permute-done | bytes 262176 | tf_op jit(solution)/shard_map/ppermute | solution.py:437
  179.2 7.8 %collective-permute-done.32 = bf16[4,256,128]{2,1,0:T(8,128)(2,1)S(1)} collective-permute-done((bf16[4,256,128]{2,1,0:T(8,128)(2,1)}, bf16[4,256,128]{2,1,0:T(8,128)(2,1)S(1)}, u32[]{:S(2)}, u32[]{:S(2)}) %collective-permute-start.32) | collective-permute-done | bytes 262176 | tf_op jit(solution)/shard_map/ppermute | solution.py:437
  187.6 1.0 copy-done.8
  (110 shorter events, 9.8 us)
Async XLA Ops:
  0.6 10.9 %copy-start = (bf16[256,4,512]{2,1,0:T(4,128)(2,1)S(1)}, bf16[256,4,512]{2,1,0:T(4,128)(2,1)}, u32[]{:S(2)}) copy-start(bf16[256,4,512]{2,1,0:T(4,128)(2,1)} %param.7) | copy-start | bytes 3145732
  0.6 5.1 %copy-start.6 = (bf16[256,4,512]{2,1,0:T(4,128)(2,1)S(1)}, bf16[256,4,512]{2,1,0:T(4,128)(2,1)}, u32[]{:S(2)}) copy-start(bf16[256,4,512]{2,1,0:T(4,128)(2,1)} %param.6) | copy-start | bytes 3145732
  1.7 4.2 %collective-permute-start = (bf16[1,32,1024]{2,1,0:T(8,128)(2,1)S(1)}, bf16[1,32,1024]{2,1,0:T(8,128)(2,1)S(1)}, u32[]{:S(2)}, u32[]{:S(2)}) collective-permute-start(bf16[1,32,1024]{2,1,0:T(8,128)(2,1)S(1)} %dynamic-slice_bitcast_fusion.1), channel_id=1, source_target_pairs={{0,12},{4,8},{8,4},{12,0},{1,13},{5,9},{9,5},{13,1},{2,14},{6,10},... | collective-permute-start | bytes 196616 | tf_op jit(solution)/shard_map/ppermute | solution.py:437
  2.7 7.8 %collective-permute-start.15 = (bf16[1,32,1024]{2,1,0:T(8,128)(2,1)S(1)}, bf16[1,32,1024]{2,1,0:T(8,128)(2,1)S(1)}, u32[]{:S(2)}, u32[]{:S(2)}) collective-permute-start(bf16[1,32,1024]{2,1,0:T(8,128)(2,1)S(1)} %dynamic-slice_bitcast_fusion), channel_id=1, source_target_pairs={{0,12},{4,8},{8,4},{12,0},{1,13},{5,9},{9,5},{13,1},{2,14},{6,10},... | collective-permute-start | bytes 196616 | tf_op jit(solution)/shard_map/ppermute | solution.py:437
  5.9 5.7 %collective-permute-start.1 = (bf16[2,32,1024]{2,1,0:T(8,128)(2,1)S(1)}, bf16[2,32,1024]{2,1,0:T(8,128)(2,1)S(1)}, u32[]{:S(2)}, u32[]{:S(2)}) collective-permute-start(bf16[2,32,1024]{2,1,0:T(8,128)(2,1)S(1)} %pad_maximum_fusion.4), channel_id=1, source_target_pairs={{0,4},{4,0},{8,12},{12,8},{1,5},{5,1},{9,13},{13,9},{2,6},{6,2},{1... | collective-permute-start | bytes 393224 | tf_op jit(solution)/shard_map/ppermute | solution.py:437
  11.1 10.4 %collective-permute-start.16 = (bf16[2,32,1024]{2,1,0:T(8,128)(2,1)}, bf16[2,32,1024]{2,1,0:T(8,128)(2,1)}, u32[]{:S(2)}, u32[]{:S(2)}) collective-permute-start(bf16[2,32,1024]{2,1,0:T(8,128)(2,1)} %pad_maximum_fusion.6), channel_id=1, source_target_pairs={{0,4},{4,0},{8,12},{12,8},{1,5},{5,1},{9,13},{13,9},{2,6},{6,2},{1... | collective-permute-start | bytes 393224 | tf_op jit(solution)/shard_map/ppermute | solution.py:437
  14.1 5.2 %collective-permute-start.2 = (bf16[4,32,1024]{2,1,0:T(8,128)(2,1)S(1)}, bf16[4,32,1024]{2,1,0:T(8,128)(2,1)S(1)}, u32[]{:S(2)}, u32[]{:S(2)}) collective-permute-start(bf16[4,32,1024]{2,1,0:T(8,128)(2,1)S(1)} %pad_maximum_fusion.2), channel_id=1, source_target_pairs={{0,16},{1,17},{2,18},{3,19},{16,0},{17,1},{18,2},{19,3},{4,20},{5,... | collective-permute-start | bytes 786440 | tf_op jit(solution)/shard_map/ppermute | solution.py:437
  15.3 5.2 %collective-permute-start.3 = (bf16[4,32,1024]{2,1,0:T(8,128)(2,1)S(1)}, bf16[4,32,1024]{2,1,0:T(8,128)(2,1)S(1)}, u32[]{:S(2)}, u32[]{:S(2)}) collective-permute-start(bf16[4,32,1024]{2,1,0:T(8,128)(2,1)S(1)} %pad_maximum_fusion.2), channel_id=1, source_target_pairs={{0,2},{1,3},{2,0},{3,1},{16,18},{17,19},{18,16},{19,17},{4,6},{5,7... | collective-permute-start | bytes 786440 | tf_op jit(solution)/shard_map/ppermute | solution.py:437
  19.3 1.3 copy-start.9
  20.6 0.7 copy-start.11
  21.3 5.4 %collective-permute-start.4 = (bf16[4,32,1024]{2,1,0:T(8,128)(2,1)S(1)}, bf16[4,32,1024]{2,1,0:T(8,128)(2,1)S(1)}, u32[]{:S(2)}, u32[]{:S(2)}) collective-permute-start(bf16[4,32,1024]{2,1,0:T(8,128)(2,1)S(1)} %broadcast_select_fusion.1), channel_id=1, source_target_pairs={{0,2},{1,17},{2,0},{3,19},{16,18},{17,1},{18,16},{19,3},{4,6},{5,2... | collective-permute-start | bytes 786440 | tf_op jit(solution)/shard_map/ppermute | solution.py:437
  21.5 3.5 %copy-start.10 = (bf16[4,32,1024]{2,1,0:T(8,128)(2,1)S(1)}, bf16[4,32,1024]{2,1,0:T(8,128)(2,1)}, u32[]{:S(2)}) copy-start(bf16[4,32,1024]{2,1,0:T(8,128)(2,1)} %copy-done.9) | copy-start | bytes 786436
  21.5 3.5 %copy-start.12 = (bf16[4,32,1024]{2,1,0:T(8,128)(2,1)S(1)}, bf16[4,32,1024]{2,1,0:T(8,128)(2,1)}, u32[]{:S(2)}) copy-start(bf16[4,32,1024]{2,1,0:T(8,128)(2,1)} %copy-done.11) | copy-start | bytes 786436
  22.5 11.3 %collective-permute-start.17 = (bf16[4,32,1024]{2,1,0:T(8,128)(2,1)S(1)}, bf16[4,32,1024]{2,1,0:T(8,128)(2,1)S(1)}, u32[]{:S(2)}, u32[]{:S(2)}) collective-permute-start(bf16[4,32,1024]{2,1,0:T(8,128)(2,1)S(1)} %get-tuple-element.105), channel_id=1, source_target_pairs={{0,2},{1,3},{2,0},{3,1},{16,18},{17,19},{18,16},{19,17},{4,6},{5,7... | collective-permute-start | bytes 786440 | tf_op jit(solution)/shard_map/ppermute | solution.py:437
  23.8 10.0 %collective-permute-start.18 = (bf16[4,32,1024]{2,1,0:T(8,128)(2,1)S(1)}, bf16[4,32,1024]{2,1,0:T(8,128)(2,1)S(1)}, u32[]{:S(2)}, u32[]{:S(2)}) collective-permute-start(bf16[4,32,1024]{2,1,0:T(8,128)(2,1)S(1)} %get-tuple-element.105), channel_id=1, source_target_pairs={{0,16},{1,17},{2,18},{3,19},{16,0},{17,1},{18,2},{19,3},{4,20},{5,... | collective-permute-start | bytes 786440 | tf_op jit(solution)/shard_map/ppermute | solution.py:437
  25.2 8.5 %copy-start.25 = (f32[256,27]{0,1:T(8,128)S(1)}, f32[256,27]{0,1:T(8,128)}, u32[]{:S(2)}) copy-start(f32[256,27]{0,1:T(8,128)} %param.10) | copy-start | bytes 82948
  26.7 12.9 %copy-start.2 = (bf16[4,4,32,1024]{3,2,1,0:T(8,128)(2,1)}, bf16[4,4,32,1024]{3,2,1,0:T(8,128)(2,1)S(1)}, u32[]{:S(2)}) copy-start(bf16[4,4,32,1024]{3,2,1,0:T(8,128)(2,1)S(1)} %bitcast_dynamic-update-slice_fusion.1.refs_1_.mine) | copy-start | bytes 3145732
  26.7 7.0 %copy-start.26 = (f32[256]{0:T(256)S(1)}, f32[256]{0:T(256)}, u32[]{:S(2)}) copy-start(f32[256]{0:T(256)} %param.11) | copy-start | bytes 3076
  26.7 31.8 %collective-permute-start.5 = (bf16[4,4,32,1024]{3,2,1,0:T(8,128)(2,1)S(1)}, bf16[4,4,32,1024]{3,2,1,0:T(8,128)(2,1)}, u32[]{:S(2)}, u32[]{:S(2)}) collective-permute-start(bf16[4,4,32,1024]{3,2,1,0:T(8,128)(2,1)S(1)} %bitcast_dynamic-update-slice_fusion.1.refs_1_.mine), channel_id=1, source_target_pairs={{0,1},{1,0},{2,3},{3,2},{16,17},{17,16},{18,19},{19,18},{4,5},{5,4... | collective-permute-start | bytes 3145736 | tf_op jit(solution)/shard_map/ppermute | solution.py:437
  33.7 1.0 copy-start.24
  33.7 2.3 %copy-start.23 = (bf16[256,4,128]{2,0,1:T(8,128)(2,1)S(1)}, bf16[256,4,128]{2,0,1:T(8,128)(2,1)}, u32[]{:S(2)}) copy-start(bf16[256,4,128]{2,0,1:T(8,128)(2,1)} %copy.49) | copy-start | bytes 786436
  33.7 5.6 %collective-permute-start.6 = (f32[1,28,256]{2,1,0:T(8,128)S(1)}, f32[1,28,256]{2,1,0:T(8,128)S(1)}, u32[]{:S(2)}, u32[]{:S(2)}) collective-permute-start(f32[1,28,256]{2,1,0:T(8,128)S(1)} %maximum_bitcast_fusion), channel_id=1, source_target_pairs={{0,12},{4,8},{8,4},{12,0},{1,13},{5,9},{9,5},{13,1},{2,14},{6,10},... | collective-permute-start | bytes 86024 | tf_op jit(solution)/shard_map/ppermute | solution.py:437
  33.9 5.8 %collective-permute-start.19 = (bf16[4,32,1024]{2,1,0:T(8,128)(2,1)S(1)}, bf16[4,32,1024]{2,1,0:T(8,128)(2,1)S(1)}, u32[]{:S(2)}, u32[]{:S(2)}) collective-permute-start(bf16[4,32,1024]{2,1,0:T(8,128)(2,1)S(1)} %broadcast_select_fusion), channel_id=1, source_target_pairs={{0,2},{1,17},{2,0},{3,19},{16,18},{17,1},{18,16},{19,3},{4,6},{5,2... | collective-permute-start | bytes 786440 | tf_op jit(solution)/shard_map/ppermute | solution.py:437
  34.7 20.8 %collective-permute-start.10 = (bf16[4,256,128]{2,1,0:T(8,128)(2,1)S(1)}, bf16[4,256,128]{2,1,0:T(8,128)(2,1)S(1)}, u32[]{:S(2)}, u32[]{:S(2)}) collective-permute-start(bf16[4,256,128]{2,1,0:T(8,128)(2,1)S(1)} %bitcast.74), channel_id=1, source_target_pairs={{0,12},{4,8},{8,4},{12,0},{1,13},{5,9},{9,5},{13,1},{2,14},{6,10},... | collective-permute-start | bytes 786440 | tf_op jit(solution)/shard_map/ppermute | solution.py:437
  36.0 22.5 %collective-permute-start.9 = (bf16[4,256,128]{2,1,0:T(8,128)(2,1)S(1)}, bf16[4,256,128]{2,1,0:T(8,128)(2,1)}, u32[]{:S(2)}, u32[]{:S(2)}) collective-permute-start(bf16[4,256,128]{2,1,0:T(8,128)(2,1)S(1)} %bitcast.73), channel_id=1, source_target_pairs={{0,8},{4,12},{8,0},{12,4},{1,9},{5,13},{9,1},{13,5},{2,10},{6,14},... | collective-permute-start | bytes 786440 | tf_op jit(solution)/shard_map/ppermute | solution.py:437
  39.4 9.3 %collective-permute-start.7 = (f32[2,28,256]{2,1,0:T(8,128)S(1)}, f32[2,28,256]{2,1,0:T(8,128)S(1)}, u32[]{:S(2)}, u32[]{:S(2)}) collective-permute-start(f32[2,28,256]{2,1,0:T(8,128)S(1)} %pad_maximum_fusion.7), channel_id=1, source_target_pairs={{0,4},{4,0},{8,12},{12,8},{1,5},{5,1},{9,13},{13,9},{2,6},{6,2},{1... | collective-permute-start | bytes 172040 | tf_op jit(solution)/shard_map/ppermute | solution.py:437
  39.6 18.9 %collective-permute-start.8 = (bf16[4,256,128]{2,1,0:T(8,128)(2,1)S(1)}, bf16[4,256,128]{2,1,0:T(8,128)(2,1)}, u32[]{:S(2)}, u32[]{:S(2)}) collective-permute-start(bf16[4,256,128]{2,1,0:T(8,128)(2,1)S(1)} %get-tuple-element.66), channel_id=1, source_target_pairs={{0,4},{4,0},{8,12},{12,8},{1,5},{5,1},{9,13},{13,9},{2,6},{6,2},{1... | collective-permute-start | bytes 786440 | tf_op jit(solution)/shard_map/ppermute | solution.py:437
  41.7 23.1 %copy-start.1 = (bf16[4,4,32,1024]{3,2,1,0:T(8,128)(2,1)}, bf16[4,4,32,1024]{3,2,1,0:T(8,128)(2,1)S(1)}, u32[]{:S(2)}) copy-start(bf16[4,4,32,1024]{3,2,1,0:T(8,128)(2,1)S(1)} %bitcast_dynamic-update-slice_fusion.mine.refs_1_) | copy-start | bytes 3145732
  48.7 37.2 %collective-permute-start.20 = (bf16[4,4,32,1024]{3,2,1,0:T(8,128)(2,1)S(1)}, bf16[4,4,32,1024]{3,2,1,0:T(8,128)(2,1)}, u32[]{:S(2)}, u32[]{:S(2)}) collective-permute-start(bf16[4,4,32,1024]{3,2,1,0:T(8,128)(2,1)S(1)} %bitcast_dynamic-update-slice_fusion.mine.refs_1_), channel_id=1, source_target_pairs={{0,1},{1,0},{2,3},{3,2},{16,17},{17,16},{18,19},{19,18},{4,5},{5,4... | collective-permute-start | bytes 3145736 | tf_op jit(solution)/shard_map/ppermute | solution.py:437
  55.5 3.0 %copy-start.13 = (bf16[4,256,128]{2,1,0:T(8,128)(2,1)}, bf16[4,256,128]{2,1,0:T(8,128)(2,1)S(1)}, u32[]{:S(2)}) copy-start(bf16[4,256,128]{2,1,0:T(8,128)(2,1)S(1)} %collective-permute-done.10.refs_6_.rest_3_) | copy-start | bytes 786436
  64.8 8.6 %collective-permute-start.11 = (bf16[4,32,1024]{2,1,0:T(8,128)(2,1)}, bf16[4,32,1024]{2,1,0:T(8,128)(2,1)S(1)}, u32[]{:S(2)}, u32[]{:S(2)}) collective-permute-start(bf16[4,32,1024]{2,1,0:T(8,128)(2,1)} %get-tuple-element.70), channel_id=1, source_target_pairs={{0,4},{4,8},{8,12},{1,5},{5,9},{9,13},{2,6},{6,10},{10,14},{3,7},{... | collective-permute-start | bytes 786440 | tf_op jit(solution)/shard_map/ppermute | solution.py:479
  67.5 7.6 %collective-permute-start.12 = (bf16[4,32,1024]{2,1,0:T(8,128)(2,1)}, bf16[4,32,1024]{2,1,0:T(8,128)(2,1)S(1)}, u32[]{:S(2)}, u32[]{:S(2)}) collective-permute-start(bf16[4,32,1024]{2,1,0:T(8,128)(2,1)} %get-tuple-element.71), channel_id=1, source_target_pairs={{4,0},{8,4},{12,8},{5,1},{9,5},{13,9},{6,2},{10,6},{14,10},{7,3},{... | collective-permute-start | bytes 786440 | tf_op jit(solution)/shard_map/ppermute | solution.py:480
  73.4 2.4 %copy-start.16 = (bf16[4,32,1024]{2,1,0:T(8,128)(2,1)}, bf16[4,32,1024]{2,1,0:T(8,128)(2,1)S(1)}, u32[]{:S(2)}) copy-start(bf16[4,32,1024]{2,1,0:T(8,128)(2,1)S(1)} %collective-permute-done.11.row_low) | copy-start | bytes 786436
  75.2 17.4 %copy-start.17 = (bf16[4,32,1024]{2,1,0:T(8,128)(2,1)}, bf16[4,32,1024]{2,1,0:T(8,128)(2,1)S(1)}, u32[]{:S(2)}) copy-start(bf16[4,32,1024]{2,1,0:T(8,128)(2,1)S(1)} %collective-permute-done.12.row_high) | copy-start | bytes 786436
  75.9 12.1 %collective-permute-start.13 = (bf16[6,32,1024]{2,1,0:T(8,128)(2,1)}, bf16[6,32,1024]{2,1,0:T(8,128)(2,1)S(1)}, u32[]{:S(2)}, u32[]{:S(2)}) collective-permute-start(bf16[6,32,1024]{2,1,0:T(8,128)(2,1)} %get-tuple-element.107), channel_id=1, source_target_pairs={{0,1},{1,2},{2,3},{4,5},{5,6},{6,7},{8,9},{9,10},{10,11},{12,13},{... | collective-permute-start | bytes 1179656 | tf_op jit(solution)/shard_map/ppermute | solution.py:487
  83.0 9.6 %collective-permute-start.14 = (bf16[6,32,1024]{2,1,0:T(8,128)(2,1)}, bf16[6,32,1024]{2,1,0:T(8,128)(2,1)}, u32[]{:S(2)}, u32[]{:S(2)}) collective-permute-start(bf16[6,32,1024]{2,1,0:T(8,128)(2,1)} %get-tuple-element.106), channel_id=1, source_target_pairs={{1,0},{2,1},{3,2},{5,4},{6,5},{7,6},{9,8},{10,9},{11,10},{13,12},{... | collective-permute-start | bytes 1179656 | tf_op jit(solution)/shard_map/ppermute | solution.py:488
  84.9 17.4 %collective-permute-start.24 = (bf16[4,256,128]{2,1,0:T(8,128)(2,1)}, bf16[4,256,128]{2,1,0:T(8,128)(2,1)S(1)}, u32[]{:S(2)}, u32[]{:S(2)}) collective-permute-start(bf16[4,256,128]{2,1,0:T(8,128)(2,1)} %bitcast.52), channel_id=1, source_target_pairs={{0,4},{4,0},{8,12},{12,8},{1,5},{5,1},{9,13},{13,9},{2,6},{6,2},{1... | collective-permute-start | bytes 786440 | tf_op jit(solution)/shard_map/ppermute | solution.py:437
  85.0 18.6 %collective-permute-start.25 = (bf16[4,256,128]{2,1,0:T(8,128)(2,1)}, bf16[4,256,128]{2,1,0:T(8,128)(2,1)S(1)}, u32[]{:S(2)}, u32[]{:S(2)}) collective-permute-start(bf16[4,256,128]{2,1,0:T(8,128)(2,1)} %bitcast.54), channel_id=1, source_target_pairs={{0,8},{4,12},{8,0},{12,4},{1,9},{5,13},{9,1},{13,5},{2,10},{6,14},... | collective-permute-start | bytes 786440 | tf_op jit(solution)/shard_map/ppermute | solution.py:437
  85.9 23.8 %collective-permute-start.26 = (bf16[4,256,128]{2,1,0:T(8,128)(2,1)}, bf16[4,256,128]{2,1,0:T(8,128)(2,1)S(1)}, u32[]{:S(2)}, u32[]{:S(2)}) collective-permute-start(bf16[4,256,128]{2,1,0:T(8,128)(2,1)} %bitcast.53), channel_id=1, source_target_pairs={{0,12},{4,8},{8,4},{12,0},{1,13},{5,9},{9,5},{13,1},{2,14},{6,10},... | collective-permute-start | bytes 786440 | tf_op jit(solution)/shard_map/ppermute | solution.py:437
  88.0 4.6 %copy-start.20 = (bf16[6,32,1024]{2,1,0:T(8,128)(2,1)}, bf16[6,32,1024]{2,1,0:T(8,128)(2,1)S(1)}, u32[]{:S(2)}) copy-start(bf16[6,32,1024]{2,1,0:T(8,128)(2,1)S(1)} %collective-permute-done.13.plane_low) | copy-start | bytes 1179652
  102.4 7.3 %copy-start.3 = (bf16[4,256,128]{2,1,0:T(8,128)(2,1)}, bf16[4,256,128]{2,1,0:T(8,128)(2,1)S(1)}, u32[]{:S(2)}) copy-start(bf16[4,256,128]{2,1,0:T(8,128)(2,1)S(1)} %collective-permute-done.24.refs_4_.rest_1_) | copy-start | bytes 786436
  103.6 6.1 %copy-start.4 = (bf16[4,256,128]{2,1,0:T(8,128)(2,1)}, bf16[4,256,128]{2,1,0:T(8,128)(2,1)S(1)}, u32[]{:S(2)}) copy-start(bf16[4,256,128]{2,1,0:T(8,128)(2,1)S(1)} %collective-permute-done.25.refs_5_.rest_2_) | copy-start | bytes 786436
  109.7 0.7 copy-start.5
  117.9 10.0 %collective-permute-start.27 = (bf16[4,32,1024]{2,1,0:T(8,128)(2,1)}, bf16[4,32,1024]{2,1,0:T(8,128)(2,1)S(1)}, u32[]{:S(2)}, u32[]{:S(2)}) collective-permute-start(bf16[4,32,1024]{2,1,0:T(8,128)(2,1)} %get-tuple-element.85), channel_id=1, source_target_pairs={{0,4},{4,8},{8,12},{1,5},{5,9},{9,13},{2,6},{6,10},{10,14},{3,7},{... | collective-permute-start | bytes 786440 | tf_op jit(solution)/shard_map/ppermute | solution.py:479
  119.9 9.7 %collective-permute-start.28 = (bf16[4,32,1024]{2,1,0:T(8,128)(2,1)}, bf16[4,32,1024]{2,1,0:T(8,128)(2,1)S(1)}, u32[]{:S(2)}, u32[]{:S(2)}) collective-permute-start(bf16[4,32,1024]{2,1,0:T(8,128)(2,1)} %get-tuple-element.86), channel_id=1, source_target_pairs={{4,0},{8,4},{12,8},{5,1},{9,5},{13,9},{6,2},{10,6},{14,10},{7,3},{... | collective-permute-start | bytes 786440 | tf_op jit(solution)/shard_map/ppermute | solution.py:480
  128.0 2.3 %copy-start.14 = (bf16[4,32,1024]{2,1,0:T(8,128)(2,1)}, bf16[4,32,1024]{2,1,0:T(8,128)(2,1)S(1)}, u32[]{:S(2)}) copy-start(bf16[4,32,1024]{2,1,0:T(8,128)(2,1)S(1)} %collective-permute-done.27.row_low) | copy-start | bytes 786436
  128.0 8.4 %copy-start.28 = (bf16[4,256,128]{2,1,0:T(8,128)(2,1)S(1)}, bf16[4,256,128]{2,1,0:T(8,128)(2,1)}, u32[]{:S(2)}) copy-start(bf16[4,256,128]{2,1,0:T(8,128)(2,1)} %get-tuple-element.77) | copy-start | bytes 786436
  128.0 11.0 %copy-start.27 = (bf16[4,256,128]{2,1,0:T(8,128)(2,1)S(1)}, bf16[4,256,128]{2,1,0:T(8,128)(2,1)}, u32[]{:S(2)}) copy-start(bf16[4,256,128]{2,1,0:T(8,128)(2,1)} %get-tuple-element.78) | copy-start | bytes 786436
  129.6 14.1 %copy-start.15 = (bf16[4,32,1024]{2,1,0:T(8,128)(2,1)}, bf16[4,32,1024]{2,1,0:T(8,128)(2,1)S(1)}, u32[]{:S(2)}) copy-start(bf16[4,32,1024]{2,1,0:T(8,128)(2,1)S(1)} %collective-permute-done.28.row_high) | copy-start | bytes 786436
  130.3 8.9 %collective-permute-start.29 = (bf16[6,32,1024]{2,1,0:T(8,128)(2,1)}, bf16[6,32,1024]{2,1,0:T(8,128)(2,1)S(1)}, u32[]{:S(2)}, u32[]{:S(2)}) collective-permute-start(bf16[6,32,1024]{2,1,0:T(8,128)(2,1)} %get-tuple-element.101), channel_id=1, source_target_pairs={{0,1},{1,2},{2,3},{4,5},{5,6},{6,7},{8,9},{9,10},{10,11},{12,13},{... | collective-permute-start | bytes 1179656 | tf_op jit(solution)/shard_map/ppermute | solution.py:487
  134.1 9.6 %collective-permute-start.30 = (bf16[6,32,1024]{2,1,0:T(8,128)(2,1)}, bf16[6,32,1024]{2,1,0:T(8,128)(2,1)S(1)}, u32[]{:S(2)}, u32[]{:S(2)}) collective-permute-start(bf16[6,32,1024]{2,1,0:T(8,128)(2,1)} %get-tuple-element.100), channel_id=1, source_target_pairs={{1,0},{2,1},{3,2},{5,4},{6,5},{7,6},{9,8},{10,9},{11,10},{13,12},{... | collective-permute-start | bytes 1179656 | tf_op jit(solution)/shard_map/ppermute | solution.py:488
  136.2 17.0 %collective-permute-start.21 = (bf16[4,256,128]{2,1,0:T(8,128)(2,1)}, bf16[4,256,128]{2,1,0:T(8,128)(2,1)S(1)}, u32[]{:S(2)}, u32[]{:S(2)}) collective-permute-start(bf16[4,256,128]{2,1,0:T(8,128)(2,1)} %get-tuple-element.76), channel_id=1, source_target_pairs={{0,4},{4,0},{8,12},{12,8},{1,5},{5,1},{9,13},{13,9},{2,6},{6,2},{1... | collective-permute-start | bytes 786440 | tf_op jit(solution)/shard_map/ppermute | solution.py:437
  136.3 20.1 %collective-permute-start.22 = (bf16[4,256,128]{2,1,0:T(8,128)(2,1)S(1)}, bf16[4,256,128]{2,1,0:T(8,128)(2,1)S(1)}, u32[]{:S(2)}, u32[]{:S(2)}) collective-permute-start(bf16[4,256,128]{2,1,0:T(8,128)(2,1)S(1)} %copy-done.28), channel_id=1, source_target_pairs={{0,8},{4,12},{8,0},{12,4},{1,9},{5,13},{9,1},{13,5},{2,10},{6,14},... | collective-permute-start | bytes 786440 | tf_op jit(solution)/shard_map/ppermute | solution.py:437
  139.0 22.1 %collective-permute-start.23 = (bf16[4,256,128]{2,1,0:T(8,128)(2,1)S(1)}, bf16[4,256,128]{2,1,0:T(8,128)(2,1)S(1)}, u32[]{:S(2)}, u32[]{:S(2)}) collective-permute-start(bf16[4,256,128]{2,1,0:T(8,128)(2,1)S(1)} %copy-done.27), channel_id=1, source_target_pairs={{0,12},{4,8},{8,4},{12,0},{1,13},{5,9},{9,5},{13,1},{2,14},{6,10},... | collective-permute-start | bytes 786440 | tf_op jit(solution)/shard_map/ppermute | solution.py:437
  139.2 4.6 %copy-start.18 = (bf16[6,32,1024]{2,1,0:T(8,128)(2,1)}, bf16[6,32,1024]{2,1,0:T(8,128)(2,1)S(1)}, u32[]{:S(2)}) copy-start(bf16[6,32,1024]{2,1,0:T(8,128)(2,1)S(1)} %collective-permute-done.29.plane_low) | copy-start | bytes 1179652
  143.7 0.8 copy-start.19
  161.2 17.7 %collective-permute-start.31 = (bf16[4,256,128]{2,1,0:T(8,128)(2,1)}, bf16[4,256,128]{2,1,0:T(8,128)(2,1)S(1)}, u32[]{:S(2)}, u32[]{:S(2)}) collective-permute-start(bf16[4,256,128]{2,1,0:T(8,128)(2,1)} %get-tuple-element.95), channel_id=1, source_target_pairs={{0,8},{4,12},{8,0},{12,4},{1,9},{5,13},{9,1},{13,5},{2,10},{6,14},... | collective-permute-start | bytes 786440 | tf_op jit(solution)/shard_map/ppermute | solution.py:437
  161.2 25.8 %collective-permute-start.32 = (bf16[4,256,128]{2,1,0:T(8,128)(2,1)}, bf16[4,256,128]{2,1,0:T(8,128)(2,1)S(1)}, u32[]{:S(2)}, u32[]{:S(2)}) collective-permute-start(bf16[4,256,128]{2,1,0:T(8,128)(2,1)} %get-tuple-element.96), channel_id=1, source_target_pairs={{0,12},{4,8},{8,4},{12,0},{1,13},{5,9},{9,5},{13,1},{2,14},{6,10},... | collective-permute-start | bytes 786440 | tf_op jit(solution)/shard_map/ppermute | solution.py:437
  163.1 24.2 %collective-permute-start.33 = (bf16[4,256,128]{2,1,0:T(8,128)(2,1)}, bf16[4,256,128]{2,1,0:T(8,128)(2,1)S(1)}, u32[]{:S(2)}, u32[]{:S(2)}) collective-permute-start(bf16[4,256,128]{2,1,0:T(8,128)(2,1)} %get-tuple-element.97), channel_id=1, source_target_pairs={{0,4},{4,0},{8,12},{12,8},{1,5},{5,1},{9,13},{13,9},{2,6},{6,2},{1... | collective-permute-start | bytes 786440 | tf_op jit(solution)/shard_map/ppermute | solution.py:437
  164.7 0.9 copy-start.22
  165.9 1.0 copy-start.21
  168.1 19.5 %copy-start.7 = (bf16[256,4,512]{2,1,0:T(4,128)(2,1)}, bf16[256,4,512]{2,1,0:T(4,128)(2,1)S(1)}, u32[]{:S(2)}) copy-start(bf16[256,4,512]{2,1,0:T(4,128)(2,1)S(1)} %copy_dynamic-update-slice_fusion.4) | copy-start | bytes 3145732
  187.6 1.0 copy-start.8

commit v15 on v14

--- a/solution.py
+++ b/solution.py
@@ -365,12 +365,19 @@
         copies = piece_copies(here, mine, other, weight, sems)
         start_all(copies)
         turn_blocks(here, blocks, held, turned)
-        wait_all(copies)
-
-    channels, width = turned.shape[1], slope.shape[1]
+
+    width = slope.shape[1]
     start = pl.multiple_of(pl.program_id(0) * width, width)
-    columns = weight[:, :, :, pl.ds(start, width)].reshape(channels, width)
-    grad = jnp.dot(turned[...], columns, preferred_element_type=jnp.float32)
+    grad = 0.0
+    for block in range(count):
+
+        @pl.when(pl.program_id(0) == 0)
+        def _():
+            wait_block(block, mine, other, weight, sems)
+
+        columns = weight[block, :, :, pl.ds(start, width)].reshape(-1, width)
+        rows_of = turned[:, block * columns.shape[0] : (block + 1) * columns.shape[0]]
+        grad = grad + jnp.dot(rows_of, columns, preferred_element_type=jnp.float32)
     grad = grad.astype(turned.dtype).astype(jnp.float32)
     put_with_edges((grad * slope[...].astype(jnp.float32)).astype(turned.dtype), *outputs)
 

time: 189 us -> 191 us (1.011)
  no operation moved by 1% of the time
where the time goes in v15:
time: 191 us; the launch traced here: 190 us
  waiting for transfers between devices  67.6 us (35%)
  starting transfers between devices  65 us (34%)
  Pallas kernels  33.6 us (18%)
  local copies, waits for them, and re-layouts  19.1 us (10%)
  other arithmetic  3.39 us (2%)
    ppermute x26, waiting for transfers between devices, swap(): return lax.ppermute(part, axes, [(i, partner(i)) for i in range(count)])  47.9 us
    ppermute x26, starting transfers between devices, swap(): return lax.ppermute(part, axes, [(i, partner(i)) for i in range(count)])  39.5 us
    pallas_call x2, Pallas kernels, stencil(): pl.pallas_call(forward_kernel if forward else backward_kernel, grid_spec=...  18.5 us
    pallas_call x2, Pallas kernels, product_call(): pl.pallas_call(lambda *refs: kernel(*refs, count=count), grid_spec=pltpu....  15.1 us
    ppermute x2, starting transfers between devices, halo_of(): plane_low = lax.ppermute(joined(fore, planes - 1), 'space', forward)  10.9 us
    ppermute x2, waiting for transfers between devices, halo_of(): plane_high = lax.ppermute(joined(back, 0), 'space', backward)  9.17 us
    unnamed x64, local copies, waits for them, and re-layouts  9.08 us
    ppermute x2, waiting for transfers between devices, halo_of(): row_low = lax.ppermute(last, 'chan', forward)  8.05 us
  transfers between devices with their start and end apart: 34, of which 20 were waited for; matrix products, arithmetic and copies ran while one was open for 8% of the time, Pallas kernels for 13%

profile of v15, /device:TPU:17, one launch (start us, length us, event | category | flops | bytes accessed | tf_op | source)
XLA Modules:
  0.0 189.9 jit_solution(2496982525902220349)
XLA Ops:
  0.7 1.0 dynamic-slice_bitcast_fusion.1
  1.8 0.8 dynamic-slice_bitcast_fusion
  2.7 1.3 collective-permute-start.15
  4.0 1.0 constant_dynamic-slice_fusion.2
  5.0 0.7 copy.49
  5.9 3.2 %collective-permute-start.1 = (bf16[2,32,1024]{2,1,0:T(8,128)(2,1)S(1)}, bf16[2,32,1024]{2,1,0:T(8,128)(2,1)S(1)}, u32[]{:S(2)}, u32[]{:S(2)}) collective-permute-start(bf16[2,32,1024]{2,1,0:T(8,128)(2,1)S(1)} %pad_maximum_fusion.4), channel_id=1, source_target_pairs={{0,4},{4,0},{8,12},{12,8},{1,5},{5,1},{9,13},{13,9},{2,6},{6,2},{1... | collective-permute-start | bytes 393224 | tf_op jit(solution)/shard_map/ppermute | solution.py:444
  9.7 0.7 copy.48
  10.5 0.7 pad_maximum_fusion.6
  11.7 0.8 copy.53
  12.5 0.7 copy.52
  13.4 0.7 copy.51
  14.1 1.2 collective-permute-start.2
  15.3 1.2 collective-permute-start.3
  16.9 0.7 copy.50
  17.6 0.8 copy_bitcast_fusion
  18.3 1.0 collective-permute-done.2
  19.3 1.2 collective-permute-done.3
  21.5 1.0 fusion
  22.5 1.3 collective-permute-start.17
  23.8 1.2 collective-permute-start.18
  25.2 1.5 collective-permute-done.4
  26.7 7.0 %collective-permute-start.5 = (bf16[4,4,32,1024]{3,2,1,0:T(8,128)(2,1)S(1)}, bf16[4,4,32,1024]{3,2,1,0:T(8,128)(2,1)}, u32[]{:S(2)}, u32[]{:S(2)}) collective-permute-start(bf16[4,4,32,1024]{3,2,1,0:T(8,128)(2,1)S(1)} %bitcast_dynamic-update-slice_fusion.1.refs_1_.mine), channel_id=1, source_target_pairs={{0,1},{1,0},{2,3},{3,2},{16,17},{17,16},{18,19},{19,18},{4,5},{5,4... | collective-permute-start | bytes 3145736 | tf_op jit(solution)/shard_map/ppermute | solution.py:444
  34.7 1.3 collective-permute-start.10
  36.0 3.4 %collective-permute-start.9 = (bf16[4,256,128]{2,1,0:T(8,128)(2,1)S(1)}, bf16[4,256,128]{2,1,0:T(8,128)(2,1)}, u32[]{:S(2)}, u32[]{:S(2)}) collective-permute-start(bf16[4,256,128]{2,1,0:T(8,128)(2,1)S(1)} %bitcast.73), channel_id=1, source_target_pairs={{0,8},{4,12},{8,0},{12,4},{1,9},{5,13},{9,1},{13,5},{2,10},{6,14},... | collective-permute-start | bytes 786440 | tf_op jit(solution)/shard_map/ppermute | solution.py:444
  39.6 2.1 %collective-permute-start.8 = (bf16[4,256,128]{2,1,0:T(8,128)(2,1)S(1)}, bf16[4,256,128]{2,1,0:T(8,128)(2,1)}, u32[]{:S(2)}, u32[]{:S(2)}) collective-permute-start(bf16[4,256,128]{2,1,0:T(8,128)(2,1)S(1)} %get-tuple-element.66), channel_id=1, source_target_pairs={{0,4},{4,0},{8,12},{12,8},{1,5},{5,1},{9,13},{13,9},{2,6},{6,2},{1... | collective-permute-start | bytes 786440 | tf_op jit(solution)/shard_map/ppermute | solution.py:444
  41.7 7.0 %collective-permute-done.7 = f32[2,28,256]{2,1,0:T(8,128)S(1)} collective-permute-done((f32[2,28,256]{2,1,0:T(8,128)S(1)}, f32[2,28,256]{2,1,0:T(8,128)S(1)}, u32[]{:S(2)}, u32[]{:S(2)}) %collective-permute-start.7) | collective-permute-done | bytes 57376 | tf_op jit(solution)/shard_map/ppermute | solution.py:444
  48.7 6.1 %collective-permute-start.20 = (bf16[4,4,32,1024]{3,2,1,0:T(8,128)(2,1)S(1)}, bf16[4,4,32,1024]{3,2,1,0:T(8,128)(2,1)}, u32[]{:S(2)}, u32[]{:S(2)}) collective-permute-start(bf16[4,4,32,1024]{3,2,1,0:T(8,128)(2,1)S(1)} %bitcast_dynamic-update-slice_fusion.mine.refs_1_), channel_id=1, source_target_pairs={{0,1},{1,0},{2,3},{3,2},{16,17},{17,16},{18,19},{19,18},{4,5},{5,4... | collective-permute-start | bytes 3145736 | tf_op jit(solution)/shard_map/ppermute | solution.py:444
  55.5 3.0 %collective-permute-done.9.refs_5_.rest_2_ = bf16[4,256,128]{2,1,0:T(8,128)(2,1)} collective-permute-done((bf16[4,256,128]{2,1,0:T(8,128)(2,1)S(1)}, bf16[4,256,128]{2,1,0:T(8,128)(2,1)}, u32[]{:S(2)}, u32[]{:S(2)}) %collective-permute-start.9) | collective-permute-done | bytes 262176 | tf_op jit(solution)/shard_map/ppermute | solution.py:444
  58.5 6.2 %shard_map.77 = (bf16[512,1024]{1,0:T(8,128)(2,1)}, bf16[4,32,1024]{2,1,0:T(8,128)(2,1)}, bf16[4,32,1024]{2,1,0:T(8,128)(2,1)}, bf16[6,32,1024]{2,1,0:T(8,128)(2,1)}, bf16[6,32,1024]{2,1,0:T(8,128)(2,1)}) custom-call(s32[2]{0:T(128)} %pad_add_fusion.refs_0_.here, bf16[4,4,32,1024]{3,2,1,0:T(8,128)(2,1)} %copy-done.2, ...), custom_call_target="tpu_custom_call" | custom-call | tf_op jit(solution)/shard_map/pallas_call | solution.py:399
  64.8 2.7 %collective-permute-start.11 = (bf16[4,32,1024]{2,1,0:T(8,128)(2,1)}, bf16[4,32,1024]{2,1,0:T(8,128)(2,1)S(1)}, u32[]{:S(2)}, u32[]{:S(2)}) collective-permute-start(bf16[4,32,1024]{2,1,0:T(8,128)(2,1)} %get-tuple-element.70), channel_id=1, source_target_pairs={{0,4},{4,8},{8,12},{1,5},{5,9},{9,13},{2,6},{6,10},{10,14},{3,7},{... | collective-permute-start | bytes 786440 | tf_op jit(solution)/shard_map/ppermute | solution.py:486
  67.5 2.6 %collective-permute-start.12 = (bf16[4,32,1024]{2,1,0:T(8,128)(2,1)}, bf16[4,32,1024]{2,1,0:T(8,128)(2,1)S(1)}, u32[]{:S(2)}, u32[]{:S(2)}) collective-permute-start(bf16[4,32,1024]{2,1,0:T(8,128)(2,1)} %get-tuple-element.71), channel_id=1, source_target_pairs={{4,0},{8,4},{12,8},{5,1},{9,5},{13,9},{6,2},{10,6},{14,10},{7,3},{... | collective-permute-start | bytes 786440 | tf_op jit(solution)/shard_map/ppermute | solution.py:487
  70.1 3.3 %collective-permute-done.11.row_low = bf16[4,32,1024]{2,1,0:T(8,128)(2,1)S(1)} collective-permute-done((bf16[4,32,1024]{2,1,0:T(8,128)(2,1)}, bf16[4,32,1024]{2,1,0:T(8,128)(2,1)S(1)}, u32[]{:S(2)}, u32[]{:S(2)}) %collective-permute-start.11) | collective-permute-done | bytes 262176 | tf_op jit(solution)/shard_map/ppermute | solution.py:486
  73.4 0.7 slice_dynamic-update-slice_fusion.5
  74.1 1.0 collective-permute-done.12.row_high
  75.2 0.7 slice_dynamic-update-slice_fusion.4
  75.9 7.1 %collective-permute-start.13 = (bf16[6,32,1024]{2,1,0:T(8,128)(2,1)}, bf16[6,32,1024]{2,1,0:T(8,128)(2,1)S(1)}, u32[]{:S(2)}, u32[]{:S(2)}) collective-permute-start(bf16[6,32,1024]{2,1,0:T(8,128)(2,1)} %get-tuple-element.107), channel_id=1, source_target_pairs={{0,1},{1,2},{2,3},{4,5},{5,6},{6,7},{8,9},{9,10},{10,11},{12,13},{... | collective-permute-start | bytes 1179656 | tf_op jit(solution)/shard_map/ppermute | solution.py:494
  83.0 1.9 %collective-permute-start.14 = (bf16[6,32,1024]{2,1,0:T(8,128)(2,1)}, bf16[6,32,1024]{2,1,0:T(8,128)(2,1)}, u32[]{:S(2)}, u32[]{:S(2)}) collective-permute-start(bf16[6,32,1024]{2,1,0:T(8,128)(2,1)} %get-tuple-element.106), channel_id=1, source_target_pairs={{1,0},{2,1},{3,2},{5,4},{6,5},{7,6},{9,8},{10,9},{11,10},{13,12},{... | collective-permute-start | bytes 1179656 | tf_op jit(solution)/shard_map/ppermute | solution.py:495
  85.0 1.0 collective-permute-start.25
  85.9 1.7 collective-permute-start.26
  88.0 4.6 %collective-permute-done.14.plane_high = bf16[6,32,1024]{2,1,0:T(8,128)(2,1)} collective-permute-done((bf16[6,32,1024]{2,1,0:T(8,128)(2,1)}, bf16[6,32,1024]{2,1,0:T(8,128)(2,1)}, u32[]{:S(2)}, u32[]{:S(2)}) %collective-permute-start.14) | collective-permute-done | bytes 393248 | tf_op jit(solution)/shard_map/ppermute | solution.py:495
  92.6 9.8 %shard_map.78 = (bf16[4,256,128]{2,1,0:T(8,128)(2,1)}, bf16[4,256,128]{2,1,0:T(8,128)(2,1)}, bf16[4,256,128]{2,1,0:T(8,128)(2,1)}, bf16[4,256,128]{2,1,0:T(8,128)(2,1)}, bf16[4,4,32,1024]{3,2,1,0:T(8,128)(2,1)}) custom-call(s32[2]{0:T(128)} %pad_add_fusion.refs_0_.here, bf16[4,4,32,1024]{3,2,1,0:T(8,128)(2,1)} %bitcast.64, bf16[4,32,1024]{2,1,0:T(8,128)(2,1)} %copy-done.16, ...), custom_call_target="tpu_custom_call" | custom-call | tf_op jit(solution)/shard_map/pallas_call | solution.py:282
  102.4 1.3 collective-permute-done.25.refs_5_.rest_2_
  103.6 6.1 %collective-permute-done.26.refs_6_.rest_3_ = bf16[4,256,128]{2,1,0:T(8,128)(2,1)S(1)} collective-permute-done((bf16[4,256,128]{2,1,0:T(8,128)(2,1)}, bf16[4,256,128]{2,1,0:T(8,128)(2,1)S(1)}, u32[]{:S(2)}, u32[]{:S(2)}) %collective-permute-start.26) | collective-permute-done | bytes 262176 | tf_op jit(solution)/shard_map/ppermute | solution.py:444
  109.7 0.7 copy-done.5
  110.4 8.9 %shard_map.79 = (bf16[512,1024]{1,0:T(8,128)(2,1)}, bf16[4,32,1024]{2,1,0:T(8,128)(2,1)}, bf16[4,32,1024]{2,1,0:T(8,128)(2,1)}, bf16[6,32,1024]{2,1,0:T(8,128)(2,1)}, bf16[6,32,1024]{2,1,0:T(8,128)(2,1)}) custom-call(s32[2]{0:T(128)} %pad_add_fusion.refs_0_.here, bf16[4,4,32,1024]{3,2,1,0:T(8,128)(2,1)} %copy-done.1, ...), custom_call_target="tpu_custom_call" | custom-call | tf_op jit(solution)/shard_map/pallas_call | solution.py:399
  119.3 1.9 %collective-permute-start.27 = (bf16[4,32,1024]{2,1,0:T(8,128)(2,1)}, bf16[4,32,1024]{2,1,0:T(8,128)(2,1)S(1)}, u32[]{:S(2)}, u32[]{:S(2)}) collective-permute-start(bf16[4,32,1024]{2,1,0:T(8,128)(2,1)} %get-tuple-element.85), channel_id=1, source_target_pairs={{0,4},{4,8},{8,12},{1,5},{5,9},{9,13},{2,6},{6,10},{10,14},{3,7},{... | collective-permute-start | bytes 786440 | tf_op jit(solution)/shard_map/ppermute | solution.py:486
  121.2 3.4 %collective-permute-start.28 = (bf16[4,32,1024]{2,1,0:T(8,128)(2,1)}, bf16[4,32,1024]{2,1,0:T(8,128)(2,1)S(1)}, u32[]{:S(2)}, u32[]{:S(2)}) collective-permute-start(bf16[4,32,1024]{2,1,0:T(8,128)(2,1)} %get-tuple-element.86), channel_id=1, source_target_pairs={{4,0},{8,4},{12,8},{5,1},{9,5},{13,9},{6,2},{10,6},{14,10},{7,3},{... | collective-permute-start | bytes 786440 | tf_op jit(solution)/shard_map/ppermute | solution.py:487
  124.6 4.7 %collective-permute-done.27.row_low = bf16[4,32,1024]{2,1,0:T(8,128)(2,1)S(1)} collective-permute-done((bf16[4,32,1024]{2,1,0:T(8,128)(2,1)}, bf16[4,32,1024]{2,1,0:T(8,128)(2,1)S(1)}, u32[]{:S(2)}, u32[]{:S(2)}) %collective-permute-start.27) | collective-permute-done | bytes 262176 | tf_op jit(solution)/shard_map/ppermute | solution.py:486
  130.0 1.0 collective-permute-done.28.row_high
  131.0 0.7 slice_dynamic-update-slice_fusion
  131.7 3.8 %collective-permute-start.29 = (bf16[6,32,1024]{2,1,0:T(8,128)(2,1)}, bf16[6,32,1024]{2,1,0:T(8,128)(2,1)S(1)}, u32[]{:S(2)}, u32[]{:S(2)}) collective-permute-start(bf16[6,32,1024]{2,1,0:T(8,128)(2,1)} %get-tuple-element.101), channel_id=1, source_target_pairs={{0,1},{1,2},{2,3},{4,5},{5,6},{6,7},{8,9},{9,10},{10,11},{12,13},{... | collective-permute-start | bytes 1179656 | tf_op jit(solution)/shard_map/ppermute | solution.py:494
  135.5 2.1 %collective-permute-start.30 = (bf16[6,32,1024]{2,1,0:T(8,128)(2,1)}, bf16[6,32,1024]{2,1,0:T(8,128)(2,1)S(1)}, u32[]{:S(2)}, u32[]{:S(2)}) collective-permute-start(bf16[6,32,1024]{2,1,0:T(8,128)(2,1)} %get-tuple-element.100), channel_id=1, source_target_pairs={{1,0},{2,1},{3,2},{5,4},{6,5},{7,6},{9,8},{10,9},{11,10},{13,12},{... | collective-permute-start | bytes 1179656 | tf_op jit(solution)/shard_map/ppermute | solution.py:495
  137.7 2.7 %collective-permute-start.22 = (bf16[4,256,128]{2,1,0:T(8,128)(2,1)S(1)}, bf16[4,256,128]{2,1,0:T(8,128)(2,1)S(1)}, u32[]{:S(2)}, u32[]{:S(2)}) collective-permute-start(bf16[4,256,128]{2,1,0:T(8,128)(2,1)S(1)} %copy-done.28), channel_id=1, source_target_pairs={{0,8},{4,12},{8,0},{12,4},{1,9},{5,13},{9,1},{13,5},{2,10},{6,14},... | collective-permute-start | bytes 786440 | tf_op jit(solution)/shard_map/ppermute | solution.py:444
  140.5 4.6 %collective-permute-done.30.plane_high = bf16[6,32,1024]{2,1,0:T(8,128)(2,1)S(1)} collective-permute-done((bf16[6,32,1024]{2,1,0:T(8,128)(2,1)}, bf16[6,32,1024]{2,1,0:T(8,128)(2,1)S(1)}, u32[]{:S(2)}, u32[]{:S(2)}) %collective-permute-start.30) | collective-permute-done | bytes 393248 | tf_op jit(solution)/shard_map/ppermute | solution.py:495
  145.1 0.7 copy-done.19
  145.9 8.7 %shard_map.80 = (bf16[4,256,128]{2,1,0:T(8,128)(2,1)}, bf16[4,256,128]{2,1,0:T(8,128)(2,1)}, bf16[4,256,128]{2,1,0:T(8,128)(2,1)}, bf16[4,256,128]{2,1,0:T(8,128)(2,1)}) custom-call(s32[2]{0:T(128)} %pad_add_fusion.refs_0_.here, bf16[4,4,32,1024]{3,2,1,0:T(8,128)(2,1)} %bitcast.63, bf16[4,32,1024]{2,1,0:T(8,128)(2,1)} %copy-done.14, ...), custom_call_target="tpu_custom_call" | custom-call | tf_op jit(solution)/shard_map/pallas_call | solution.py:282
  154.6 3.2 %collective-permute-done.22 = bf16[4,256,128]{2,1,0:T(8,128)(2,1)S(1)} collective-permute-done((bf16[4,256,128]{2,1,0:T(8,128)(2,1)S(1)}, bf16[4,256,128]{2,1,0:T(8,128)(2,1)S(1)}, u32[]{:S(2)}, u32[]{:S(2)}) %collective-permute-start.22) | collective-permute-done | bytes 262176 | tf_op jit(solution)/shard_map/ppermute | solution.py:444
  157.8 4.7 %collective-permute-done.23 = bf16[4,256,128]{2,1,0:T(8,128)(2,1)S(1)} collective-permute-done((bf16[4,256,128]{2,1,0:T(8,128)(2,1)S(1)}, bf16[4,256,128]{2,1,0:T(8,128)(2,1)S(1)}, u32[]{:S(2)}, u32[]{:S(2)}) %collective-permute-start.23) | collective-permute-done | bytes 262176 | tf_op jit(solution)/shard_map/ppermute | solution.py:444
  162.5 1.9 %collective-permute-start.32 = (bf16[4,256,128]{2,1,0:T(8,128)(2,1)}, bf16[4,256,128]{2,1,0:T(8,128)(2,1)S(1)}, u32[]{:S(2)}, u32[]{:S(2)}) collective-permute-start(bf16[4,256,128]{2,1,0:T(8,128)(2,1)} %get-tuple-element.96), channel_id=1, source_target_pairs={{0,12},{4,8},{8,4},{12,0},{1,13},{5,9},{9,5},{13,1},{2,14},{6,10},... | collective-permute-start | bytes 786440 | tf_op jit(solution)/shard_map/ppermute | solution.py:444
  164.4 1.6 collective-permute-start.33
  166.3 0.7 copy-done.22
  169.5 10.8 %collective-permute-done.31 = bf16[4,256,128]{2,1,0:T(8,128)(2,1)S(1)} collective-permute-done((bf16[4,256,128]{2,1,0:T(8,128)(2,1)}, bf16[4,256,128]{2,1,0:T(8,128)(2,1)S(1)}, u32[]{:S(2)}, u32[]{:S(2)}) %collective-permute-start.31) | collective-permute-done | bytes 262176 | tf_op jit(solution)/shard_map/ppermute | solution.py:444
  180.5 7.8 %collective-permute-done.32 = bf16[4,256,128]{2,1,0:T(8,128)(2,1)S(1)} collective-permute-done((bf16[4,256,128]{2,1,0:T(8,128)(2,1)}, bf16[4,256,128]{2,1,0:T(8,128)(2,1)S(1)}, u32[]{:S(2)}, u32[]{:S(2)}) %collective-permute-start.32) | collective-permute-done | bytes 262176 | tf_op jit(solution)/shard_map/ppermute | solution.py:444
  189.0 1.0 copy-done.8
  (110 shorter events, 9.8 us)
Async XLA Ops:
  0.6 10.9 %copy-start = (bf16[256,4,512]{2,1,0:T(4,128)(2,1)S(1)}, bf16[256,4,512]{2,1,0:T(4,128)(2,1)}, u32[]{:S(2)}) copy-start(bf16[256,4,512]{2,1,0:T(4,128)(2,1)} %param.7) | copy-start | bytes 3145732
  0.6 5.1 %copy-start.6 = (bf16[256,4,512]{2,1,0:T(4,128)(2,1)S(1)}, bf16[256,4,512]{2,1,0:T(4,128)(2,1)}, u32[]{:S(2)}) copy-start(bf16[256,4,512]{2,1,0:T(4,128)(2,1)} %param.6) | copy-start | bytes 3145732
  1.7 4.2 %collective-permute-start = (bf16[1,32,1024]{2,1,0:T(8,128)(2,1)S(1)}, bf16[1,32,1024]{2,1,0:T(8,128)(2,1)S(1)}, u32[]{:S(2)}, u32[]{:S(2)}) collective-permute-start(bf16[1,32,1024]{2,1,0:T(8,128)(2,1)S(1)} %dynamic-slice_bitcast_fusion.1), channel_id=1, source_target_pairs={{0,12},{4,8},{8,4},{12,0},{1,13},{5,9},{9,5},{13,1},{2,14},{6,10},... | collective-permute-start | bytes 196616 | tf_op jit(solution)/shard_map/ppermute | solution.py:444
  2.7 7.8 %collective-permute-start.15 = (bf16[1,32,1024]{2,1,0:T(8,128)(2,1)S(1)}, bf16[1,32,1024]{2,1,0:T(8,128)(2,1)S(1)}, u32[]{:S(2)}, u32[]{:S(2)}) collective-permute-start(bf16[1,32,1024]{2,1,0:T(8,128)(2,1)S(1)} %dynamic-slice_bitcast_fusion), channel_id=1, source_target_pairs={{0,12},{4,8},{8,4},{12,0},{1,13},{5,9},{9,5},{13,1},{2,14},{6,10},... | collective-permute-start | bytes 196616 | tf_op jit(solution)/shard_map/ppermute | solution.py:444
  5.9 5.7 %collective-permute-start.1 = (bf16[2,32,1024]{2,1,0:T(8,128)(2,1)S(1)}, bf16[2,32,1024]{2,1,0:T(8,128)(2,1)S(1)}, u32[]{:S(2)}, u32[]{:S(2)}) collective-permute-start(bf16[2,32,1024]{2,1,0:T(8,128)(2,1)S(1)} %pad_maximum_fusion.4), channel_id=1, source_target_pairs={{0,4},{4,0},{8,12},{12,8},{1,5},{5,1},{9,13},{13,9},{2,6},{6,2},{1... | collective-permute-start | bytes 393224 | tf_op jit(solution)/shard_map/ppermute | solution.py:444
  11.1 10.4 %collective-permute-start.16 = (bf16[2,32,1024]{2,1,0:T(8,128)(2,1)}, bf16[2,32,1024]{2,1,0:T(8,128)(2,1)}, u32[]{:S(2)}, u32[]{:S(2)}) collective-permute-start(bf16[2,32,1024]{2,1,0:T(8,128)(2,1)} %pad_maximum_fusion.6), channel_id=1, source_target_pairs={{0,4},{4,0},{8,12},{12,8},{1,5},{5,1},{9,13},{13,9},{2,6},{6,2},{1... | collective-permute-start | bytes 393224 | tf_op jit(solution)/shard_map/ppermute | solution.py:444
  14.1 5.2 %collective-permute-start.2 = (bf16[4,32,1024]{2,1,0:T(8,128)(2,1)S(1)}, bf16[4,32,1024]{2,1,0:T(8,128)(2,1)S(1)}, u32[]{:S(2)}, u32[]{:S(2)}) collective-permute-start(bf16[4,32,1024]{2,1,0:T(8,128)(2,1)S(1)} %pad_maximum_fusion.2), channel_id=1, source_target_pairs={{0,16},{1,17},{2,18},{3,19},{16,0},{17,1},{18,2},{19,3},{4,20},{5,... | collective-permute-start | bytes 786440 | tf_op jit(solution)/shard_map/ppermute | solution.py:444
  15.3 5.2 %collective-permute-start.3 = (bf16[4,32,1024]{2,1,0:T(8,128)(2,1)S(1)}, bf16[4,32,1024]{2,1,0:T(8,128)(2,1)S(1)}, u32[]{:S(2)}, u32[]{:S(2)}) collective-permute-start(bf16[4,32,1024]{2,1,0:T(8,128)(2,1)S(1)} %pad_maximum_fusion.2), channel_id=1, source_target_pairs={{0,2},{1,3},{2,0},{3,1},{16,18},{17,19},{18,16},{19,17},{4,6},{5,7... | collective-permute-start | bytes 786440 | tf_op jit(solution)/shard_map/ppermute | solution.py:444
  19.3 1.3 copy-start.9
  20.6 0.7 copy-start.11
  21.3 5.4 %collective-permute-start.4 = (bf16[4,32,1024]{2,1,0:T(8,128)(2,1)S(1)}, bf16[4,32,1024]{2,1,0:T(8,128)(2,1)S(1)}, u32[]{:S(2)}, u32[]{:S(2)}) collective-permute-start(bf16[4,32,1024]{2,1,0:T(8,128)(2,1)S(1)} %broadcast_select_fusion.1), channel_id=1, source_target_pairs={{0,2},{1,17},{2,0},{3,19},{16,18},{17,1},{18,16},{19,3},{4,6},{5,2... | collective-permute-start | bytes 786440 | tf_op jit(solution)/shard_map/ppermute | solution.py:444
  21.5 3.5 %copy-start.10 = (bf16[4,32,1024]{2,1,0:T(8,128)(2,1)S(1)}, bf16[4,32,1024]{2,1,0:T(8,128)(2,1)}, u32[]{:S(2)}) copy-start(bf16[4,32,1024]{2,1,0:T(8,128)(2,1)} %copy-done.9) | copy-start | bytes 786436
  21.5 3.5 %copy-start.12 = (bf16[4,32,1024]{2,1,0:T(8,128)(2,1)S(1)}, bf16[4,32,1024]{2,1,0:T(8,128)(2,1)}, u32[]{:S(2)}) copy-start(bf16[4,32,1024]{2,1,0:T(8,128)(2,1)} %copy-done.11) | copy-start | bytes 786436
  22.5 11.3 %collective-permute-start.17 = (bf16[4,32,1024]{2,1,0:T(8,128)(2,1)S(1)}, bf16[4,32,1024]{2,1,0:T(8,128)(2,1)S(1)}, u32[]{:S(2)}, u32[]{:S(2)}) collective-permute-start(bf16[4,32,1024]{2,1,0:T(8,128)(2,1)S(1)} %get-tuple-element.105), channel_id=1, source_target_pairs={{0,2},{1,3},{2,0},{3,1},{16,18},{17,19},{18,16},{19,17},{4,6},{5,7... | collective-permute-start | bytes 786440 | tf_op jit(solution)/shard_map/ppermute | solution.py:444
  23.8 10.0 %collective-permute-start.18 = (bf16[4,32,1024]{2,1,0:T(8,128)(2,1)S(1)}, bf16[4,32,1024]{2,1,0:T(8,128)(2,1)S(1)}, u32[]{:S(2)}, u32[]{:S(2)}) collective-permute-start(bf16[4,32,1024]{2,1,0:T(8,128)(2,1)S(1)} %get-tuple-element.105), channel_id=1, source_target_pairs={{0,16},{1,17},{2,18},{3,19},{16,0},{17,1},{18,2},{19,3},{4,20},{5,... | collective-permute-start | bytes 786440 | tf_op jit(solution)/shard_map/ppermute | solution.py:444
  25.2 8.5 %copy-start.25 = (f32[256,27]{0,1:T(8,128)S(1)}, f32[256,27]{0,1:T(8,128)}, u32[]{:S(2)}) copy-start(f32[256,27]{0,1:T(8,128)} %param.10) | copy-start | bytes 82948
  26.7 12.9 %copy-start.2 = (bf16[4,4,32,1024]{3,2,1,0:T(8,128)(2,1)}, bf16[4,4,32,1024]{3,2,1,0:T(8,128)(2,1)S(1)}, u32[]{:S(2)}) copy-start(bf16[4,4,32,1024]{3,2,1,0:T(8,128)(2,1)S(1)} %bitcast_dynamic-update-slice_fusion.1.refs_1_.mine) | copy-start | bytes 3145732
  26.7 7.0 %copy-start.26 = (f32[256]{0:T(256)S(1)}, f32[256]{0:T(256)}, u32[]{:S(2)}) copy-start(f32[256]{0:T(256)} %param.11) | copy-start | bytes 3076
  26.7 31.8 %collective-permute-start.5 = (bf16[4,4,32,1024]{3,2,1,0:T(8,128)(2,1)S(1)}, bf16[4,4,32,1024]{3,2,1,0:T(8,128)(2,1)}, u32[]{:S(2)}, u32[]{:S(2)}) collective-permute-start(bf16[4,4,32,1024]{3,2,1,0:T(8,128)(2,1)S(1)} %bitcast_dynamic-update-slice_fusion.1.refs_1_.mine), channel_id=1, source_target_pairs={{0,1},{1,0},{2,3},{3,2},{16,17},{17,16},{18,19},{19,18},{4,5},{5,4... | collective-permute-start | bytes 3145736 | tf_op jit(solution)/shard_map/ppermute | solution.py:444
  33.7 1.0 copy-start.24
  33.7 2.3 %copy-start.23 = (bf16[256,4,128]{2,0,1:T(8,128)(2,1)S(1)}, bf16[256,4,128]{2,0,1:T(8,128)(2,1)}, u32[]{:S(2)}) copy-start(bf16[256,4,128]{2,0,1:T(8,128)(2,1)} %copy.49) | copy-start | bytes 786436
  33.7 5.6 %collective-permute-start.6 = (f32[1,28,256]{2,1,0:T(8,128)S(1)}, f32[1,28,256]{2,1,0:T(8,128)S(1)}, u32[]{:S(2)}, u32[]{:S(2)}) collective-permute-start(f32[1,28,256]{2,1,0:T(8,128)S(1)} %maximum_bitcast_fusion), channel_id=1, source_target_pairs={{0,12},{4,8},{8,4},{12,0},{1,13},{5,9},{9,5},{13,1},{2,14},{6,10},... | collective-permute-start | bytes 86024 | tf_op jit(solution)/shard_map/ppermute | solution.py:444
  33.9 5.8 %collective-permute-start.19 = (bf16[4,32,1024]{2,1,0:T(8,128)(2,1)S(1)}, bf16[4,32,1024]{2,1,0:T(8,128)(2,1)S(1)}, u32[]{:S(2)}, u32[]{:S(2)}) collective-permute-start(bf16[4,32,1024]{2,1,0:T(8,128)(2,1)S(1)} %broadcast_select_fusion), channel_id=1, source_target_pairs={{0,2},{1,17},{2,0},{3,19},{16,18},{17,1},{18,16},{19,3},{4,6},{5,2... | collective-permute-start | bytes 786440 | tf_op jit(solution)/shard_map/ppermute | solution.py:444
  34.7 20.8 %collective-permute-start.10 = (bf16[4,256,128]{2,1,0:T(8,128)(2,1)S(1)}, bf16[4,256,128]{2,1,0:T(8,128)(2,1)S(1)}, u32[]{:S(2)}, u32[]{:S(2)}) collective-permute-start(bf16[4,256,128]{2,1,0:T(8,128)(2,1)S(1)} %bitcast.74), channel_id=1, source_target_pairs={{0,12},{4,8},{8,4},{12,0},{1,13},{5,9},{9,5},{13,1},{2,14},{6,10},... | collective-permute-start | bytes 786440 | tf_op jit(solution)/shard_map/ppermute | solution.py:444
  36.0 22.5 %collective-permute-start.9 = (bf16[4,256,128]{2,1,0:T(8,128)(2,1)S(1)}, bf16[4,256,128]{2,1,0:T(8,128)(2,1)}, u32[]{:S(2)}, u32[]{:S(2)}) collective-permute-start(bf16[4,256,128]{2,1,0:T(8,128)(2,1)S(1)} %bitcast.73), channel_id=1, source_target_pairs={{0,8},{4,12},{8,0},{12,4},{1,9},{5,13},{9,1},{13,5},{2,10},{6,14},... | collective-permute-start | bytes 786440 | tf_op jit(solution)/shard_map/ppermute | solution.py:444
  39.4 9.3 %collective-permute-start.7 = (f32[2,28,256]{2,1,0:T(8,128)S(1)}, f32[2,28,256]{2,1,0:T(8,128)S(1)}, u32[]{:S(2)}, u32[]{:S(2)}) collective-permute-start(f32[2,28,256]{2,1,0:T(8,128)S(1)} %pad_maximum_fusion.7), channel_id=1, source_target_pairs={{0,4},{4,0},{8,12},{12,8},{1,5},{5,1},{9,13},{13,9},{2,6},{6,2},{1... | collective-permute-start | bytes 172040 | tf_op jit(solution)/shard_map/ppermute | solution.py:444
  39.6 18.9 %collective-permute-start.8 = (bf16[4,256,128]{2,1,0:T(8,128)(2,1)S(1)}, bf16[4,256,128]{2,1,0:T(8,128)(2,1)}, u32[]{:S(2)}, u32[]{:S(2)}) collective-permute-start(bf16[4,256,128]{2,1,0:T(8,128)(2,1)S(1)} %get-tuple-element.66), channel_id=1, source_target_pairs={{0,4},{4,0},{8,12},{12,8},{1,5},{5,1},{9,13},{13,9},{2,6},{6,2},{1... | collective-permute-start | bytes 786440 | tf_op jit(solution)/shard_map/ppermute | solution.py:444
  41.7 23.1 %copy-start.1 = (bf16[4,4,32,1024]{3,2,1,0:T(8,128)(2,1)}, bf16[4,4,32,1024]{3,2,1,0:T(8,128)(2,1)S(1)}, u32[]{:S(2)}) copy-start(bf16[4,4,32,1024]{3,2,1,0:T(8,128)(2,1)S(1)} %bitcast_dynamic-update-slice_fusion.mine.refs_1_) | copy-start | bytes 3145732
  48.7 37.2 %collective-permute-start.20 = (bf16[4,4,32,1024]{3,2,1,0:T(8,128)(2,1)S(1)}, bf16[4,4,32,1024]{3,2,1,0:T(8,128)(2,1)}, u32[]{:S(2)}, u32[]{:S(2)}) collective-permute-start(bf16[4,4,32,1024]{3,2,1,0:T(8,128)(2,1)S(1)} %bitcast_dynamic-update-slice_fusion.mine.refs_1_), channel_id=1, source_target_pairs={{0,1},{1,0},{2,3},{3,2},{16,17},{17,16},{18,19},{19,18},{4,5},{5,4... | collective-permute-start | bytes 3145736 | tf_op jit(solution)/shard_map/ppermute | solution.py:444
  55.5 3.0 %copy-start.13 = (bf16[4,256,128]{2,1,0:T(8,128)(2,1)}, bf16[4,256,128]{2,1,0:T(8,128)(2,1)S(1)}, u32[]{:S(2)}) copy-start(bf16[4,256,128]{2,1,0:T(8,128)(2,1)S(1)} %collective-permute-done.10.refs_6_.rest_3_) | copy-start | bytes 786436
  64.8 8.6 %collective-permute-start.11 = (bf16[4,32,1024]{2,1,0:T(8,128)(2,1)}, bf16[4,32,1024]{2,1,0:T(8,128)(2,1)S(1)}, u32[]{:S(2)}, u32[]{:S(2)}) collective-permute-start(bf16[4,32,1024]{2,1,0:T(8,128)(2,1)} %get-tuple-element.70), channel_id=1, source_target_pairs={{0,4},{4,8},{8,12},{1,5},{5,9},{9,13},{2,6},{6,10},{10,14},{3,7},{... | collective-permute-start | bytes 786440 | tf_op jit(solution)/shard_map/ppermute | solution.py:486
  67.5 7.6 %collective-permute-start.12 = (bf16[4,32,1024]{2,1,0:T(8,128)(2,1)}, bf16[4,32,1024]{2,1,0:T(8,128)(2,1)S(1)}, u32[]{:S(2)}, u32[]{:S(2)}) collective-permute-start(bf16[4,32,1024]{2,1,0:T(8,128)(2,1)} %get-tuple-element.71), channel_id=1, source_target_pairs={{4,0},{8,4},{12,8},{5,1},{9,5},{13,9},{6,2},{10,6},{14,10},{7,3},{... | collective-permute-start | bytes 786440 | tf_op jit(solution)/shard_map/ppermute | solution.py:487
  73.4 2.4 %copy-start.16 = (bf16[4,32,1024]{2,1,0:T(8,128)(2,1)}, bf16[4,32,1024]{2,1,0:T(8,128)(2,1)S(1)}, u32[]{:S(2)}) copy-start(bf16[4,32,1024]{2,1,0:T(8,128)(2,1)S(1)} %collective-permute-done.11.row_low) | copy-start | bytes 786436
  75.2 17.4 %copy-start.17 = (bf16[4,32,1024]{2,1,0:T(8,128)(2,1)}, bf16[4,32,1024]{2,1,0:T(8,128)(2,1)S(1)}, u32[]{:S(2)}) copy-start(bf16[4,32,1024]{2,1,0:T(8,128)(2,1)S(1)} %collective-permute-done.12.row_high) | copy-start | bytes 786436
  75.9 12.1 %collective-permute-start.13 = (bf16[6,32,1024]{2,1,0:T(8,128)(2,1)}, bf16[6,32,1024]{2,1,0:T(8,128)(2,1)S(1)}, u32[]{:S(2)}, u32[]{:S(2)}) collective-permute-start(bf16[6,32,1024]{2,1,0:T(8,128)(2,1)} %get-tuple-element.107), channel_id=1, source_target_pairs={{0,1},{1,2},{2,3},{4,5},{5,6},{6,7},{8,9},{9,10},{10,11},{12,13},{... | collective-permute-start | bytes 1179656 | tf_op jit(solution)/shard_map/ppermute | solution.py:494
  83.0 9.6 %collective-permute-start.14 = (bf16[6,32,1024]{2,1,0:T(8,128)(2,1)}, bf16[6,32,1024]{2,1,0:T(8,128)(2,1)}, u32[]{:S(2)}, u32[]{:S(2)}) collective-permute-start(bf16[6,32,1024]{2,1,0:T(8,128)(2,1)} %get-tuple-element.106), channel_id=1, source_target_pairs={{1,0},{2,1},{3,2},{5,4},{6,5},{7,6},{9,8},{10,9},{11,10},{13,12},{... | collective-permute-start | bytes 1179656 | tf_op jit(solution)/shard_map/ppermute | solution.py:495
  84.9 17.4 %collective-permute-start.24 = (bf16[4,256,128]{2,1,0:T(8,128)(2,1)}, bf16[4,256,128]{2,1,0:T(8,128)(2,1)S(1)}, u32[]{:S(2)}, u32[]{:S(2)}) collective-permute-start(bf16[4,256,128]{2,1,0:T(8,128)(2,1)} %bitcast.52), channel_id=1, source_target_pairs={{0,4},{4,0},{8,12},{12,8},{1,5},{5,1},{9,13},{13,9},{2,6},{6,2},{1... | collective-permute-start | bytes 786440 | tf_op jit(solution)/shard_map/ppermute | solution.py:444
  85.0 18.6 %collective-permute-start.25 = (bf16[4,256,128]{2,1,0:T(8,128)(2,1)}, bf16[4,256,128]{2,1,0:T(8,128)(2,1)S(1)}, u32[]{:S(2)}, u32[]{:S(2)}) collective-permute-start(bf16[4,256,128]{2,1,0:T(8,128)(2,1)} %bitcast.54), channel_id=1, source_target_pairs={{0,8},{4,12},{8,0},{12,4},{1,9},{5,13},{9,1},{13,5},{2,10},{6,14},... | collective-permute-start | bytes 786440 | tf_op jit(solution)/shard_map/ppermute | solution.py:444
  85.9 23.8 %collective-permute-start.26 = (bf16[4,256,128]{2,1,0:T(8,128)(2,1)}, bf16[4,256,128]{2,1,0:T(8,128)(2,1)S(1)}, u32[]{:S(2)}, u32[]{:S(2)}) collective-permute-start(bf16[4,256,128]{2,1,0:T(8,128)(2,1)} %bitcast.53), channel_id=1, source_target_pairs={{0,12},{4,8},{8,4},{12,0},{1,13},{5,9},{9,5},{13,1},{2,14},{6,10},... | collective-permute-start | bytes 786440 | tf_op jit(solution)/shard_map/ppermute | solution.py:444
  88.0 4.6 %copy-start.20 = (bf16[6,32,1024]{2,1,0:T(8,128)(2,1)}, bf16[6,32,1024]{2,1,0:T(8,128)(2,1)S(1)}, u32[]{:S(2)}) copy-start(bf16[6,32,1024]{2,1,0:T(8,128)(2,1)S(1)} %collective-permute-done.13.plane_low) | copy-start | bytes 1179652
  102.4 7.3 %copy-start.3 = (bf16[4,256,128]{2,1,0:T(8,128)(2,1)}, bf16[4,256,128]{2,1,0:T(8,128)(2,1)S(1)}, u32[]{:S(2)}) copy-start(bf16[4,256,128]{2,1,0:T(8,128)(2,1)S(1)} %collective-permute-done.24.refs_4_.rest_1_) | copy-start | bytes 786436
  103.6 6.1 %copy-start.4 = (bf16[4,256,128]{2,1,0:T(8,128)(2,1)}, bf16[4,256,128]{2,1,0:T(8,128)(2,1)S(1)}, u32[]{:S(2)}) copy-start(bf16[4,256,128]{2,1,0:T(8,128)(2,1)S(1)} %collective-permute-done.25.refs_5_.rest_2_) | copy-start | bytes 786436
  109.7 0.7 copy-start.5
  119.3 10.0 %collective-permute-start.27 = (bf16[4,32,1024]{2,1,0:T(8,128)(2,1)}, bf16[4,32,1024]{2,1,0:T(8,128)(2,1)S(1)}, u32[]{:S(2)}, u32[]{:S(2)}) collective-permute-start(bf16[4,32,1024]{2,1,0:T(8,128)(2,1)} %get-tuple-element.85), channel_id=1, source_target_pairs={{0,4},{4,8},{8,12},{1,5},{5,9},{9,13},{2,6},{6,10},{10,14},{3,7},{... | collective-permute-start | bytes 786440 | tf_op jit(solution)/shard_map/ppermute | solution.py:486
  121.2 9.7 %collective-permute-start.28 = (bf16[4,32,1024]{2,1,0:T(8,128)(2,1)}, bf16[4,32,1024]{2,1,0:T(8,128)(2,1)S(1)}, u32[]{:S(2)}, u32[]{:S(2)}) collective-permute-start(bf16[4,32,1024]{2,1,0:T(8,128)(2,1)} %get-tuple-element.86), channel_id=1, source_target_pairs={{4,0},{8,4},{12,8},{5,1},{9,5},{13,9},{6,2},{10,6},{14,10},{7,3},{... | collective-permute-start | bytes 786440 | tf_op jit(solution)/shard_map/ppermute | solution.py:487
  129.3 2.3 %copy-start.14 = (bf16[4,32,1024]{2,1,0:T(8,128)(2,1)}, bf16[4,32,1024]{2,1,0:T(8,128)(2,1)S(1)}, u32[]{:S(2)}) copy-start(bf16[4,32,1024]{2,1,0:T(8,128)(2,1)S(1)} %collective-permute-done.27.row_low) | copy-start | bytes 786436
  129.3 8.4 %copy-start.28 = (bf16[4,256,128]{2,1,0:T(8,128)(2,1)S(1)}, bf16[4,256,128]{2,1,0:T(8,128)(2,1)}, u32[]{:S(2)}) copy-start(bf16[4,256,128]{2,1,0:T(8,128)(2,1)} %get-tuple-element.77) | copy-start | bytes 786436
  129.3 11.0 %copy-start.27 = (bf16[4,256,128]{2,1,0:T(8,128)(2,1)S(1)}, bf16[4,256,128]{2,1,0:T(8,128)(2,1)}, u32[]{:S(2)}) copy-start(bf16[4,256,128]{2,1,0:T(8,128)(2,1)} %get-tuple-element.78) | copy-start | bytes 786436
  131.0 14.1 %copy-start.15 = (bf16[4,32,1024]{2,1,0:T(8,128)(2,1)}, bf16[4,32,1024]{2,1,0:T(8,128)(2,1)S(1)}, u32[]{:S(2)}) copy-start(bf16[4,32,1024]{2,1,0:T(8,128)(2,1)S(1)} %collective-permute-done.28.row_high) | copy-start | bytes 786436
  131.7 8.9 %collective-permute-start.29 = (bf16[6,32,1024]{2,1,0:T(8,128)(2,1)}, bf16[6,32,1024]{2,1,0:T(8,128)(2,1)S(1)}, u32[]{:S(2)}, u32[]{:S(2)}) collective-permute-start(bf16[6,32,1024]{2,1,0:T(8,128)(2,1)} %get-tuple-element.101), channel_id=1, source_target_pairs={{0,1},{1,2},{2,3},{4,5},{5,6},{6,7},{8,9},{9,10},{10,11},{12,13},{... | collective-permute-start | bytes 1179656 | tf_op jit(solution)/shard_map/ppermute | solution.py:494
  135.5 9.6 %collective-permute-start.30 = (bf16[6,32,1024]{2,1,0:T(8,128)(2,1)}, bf16[6,32,1024]{2,1,0:T(8,128)(2,1)S(1)}, u32[]{:S(2)}, u32[]{:S(2)}) collective-permute-start(bf16[6,32,1024]{2,1,0:T(8,128)(2,1)} %get-tuple-element.100), channel_id=1, source_target_pairs={{1,0},{2,1},{3,2},{5,4},{6,5},{7,6},{9,8},{10,9},{11,10},{13,12},{... | collective-permute-start | bytes 1179656 | tf_op jit(solution)/shard_map/ppermute | solution.py:495
  137.6 17.0 %collective-permute-start.21 = (bf16[4,256,128]{2,1,0:T(8,128)(2,1)}, bf16[4,256,128]{2,1,0:T(8,128)(2,1)S(1)}, u32[]{:S(2)}, u32[]{:S(2)}) collective-permute-start(bf16[4,256,128]{2,1,0:T(8,128)(2,1)} %get-tuple-element.76), channel_id=1, source_target_pairs={{0,4},{4,0},{8,12},{12,8},{1,5},{5,1},{9,13},{13,9},{2,6},{6,2},{1... | collective-permute-start | bytes 786440 | tf_op jit(solution)/shard_map/ppermute | solution.py:444
  137.7 20.1 %collective-permute-start.22 = (bf16[4,256,128]{2,1,0:T(8,128)(2,1)S(1)}, bf16[4,256,128]{2,1,0:T(8,128)(2,1)S(1)}, u32[]{:S(2)}, u32[]{:S(2)}) collective-permute-start(bf16[4,256,128]{2,1,0:T(8,128)(2,1)S(1)} %copy-done.28), channel_id=1, source_target_pairs={{0,8},{4,12},{8,0},{12,4},{1,9},{5,13},{9,1},{13,5},{2,10},{6,14},... | collective-permute-start | bytes 786440 | tf_op jit(solution)/shard_map/ppermute | solution.py:444
  140.4 22.1 %collective-permute-start.23 = (bf16[4,256,128]{2,1,0:T(8,128)(2,1)S(1)}, bf16[4,256,128]{2,1,0:T(8,128)(2,1)S(1)}, u32[]{:S(2)}, u32[]{:S(2)}) collective-permute-start(bf16[4,256,128]{2,1,0:T(8,128)(2,1)S(1)} %copy-done.27), channel_id=1, source_target_pairs={{0,12},{4,8},{8,4},{12,0},{1,13},{5,9},{9,5},{13,1},{2,14},{6,10},... | collective-permute-start | bytes 786440 | tf_op jit(solution)/shard_map/ppermute | solution.py:444
  140.5 4.6 %copy-start.18 = (bf16[6,32,1024]{2,1,0:T(8,128)(2,1)}, bf16[6,32,1024]{2,1,0:T(8,128)(2,1)S(1)}, u32[]{:S(2)}) copy-start(bf16[6,32,1024]{2,1,0:T(8,128)(2,1)S(1)} %collective-permute-done.29.plane_low) | copy-start | bytes 1179652
  145.1 0.8 copy-start.19
  162.5 17.7 %collective-permute-start.31 = (bf16[4,256,128]{2,1,0:T(8,128)(2,1)}, bf16[4,256,128]{2,1,0:T(8,128)(2,1)S(1)}, u32[]{:S(2)}, u32[]{:S(2)}) collective-permute-start(bf16[4,256,128]{2,1,0:T(8,128)(2,1)} %get-tuple-element.95), channel_id=1, source_target_pairs={{0,8},{4,12},{8,0},{12,4},{1,9},{5,13},{9,1},{13,5},{2,10},{6,14},... | collective-permute-start | bytes 786440 | tf_op jit(solution)/shard_map/ppermute | solution.py:444
  162.5 25.8 %collective-permute-start.32 = (bf16[4,256,128]{2,1,0:T(8,128)(2,1)}, bf16[4,256,128]{2,1,0:T(8,128)(2,1)S(1)}, u32[]{:S(2)}, u32[]{:S(2)}) collective-permute-start(bf16[4,256,128]{2,1,0:T(8,128)(2,1)} %get-tuple-element.96), channel_id=1, source_target_pairs={{0,12},{4,8},{8,4},{12,0},{1,13},{5,9},{9,5},{13,1},{2,14},{6,10},... | collective-permute-start | bytes 786440 | tf_op jit(solution)/shard_map/ppermute | solution.py:444
  164.4 24.2 %collective-permute-start.33 = (bf16[4,256,128]{2,1,0:T(8,128)(2,1)}, bf16[4,256,128]{2,1,0:T(8,128)(2,1)S(1)}, u32[]{:S(2)}, u32[]{:S(2)}) collective-permute-start(bf16[4,256,128]{2,1,0:T(8,128)(2,1)} %get-tuple-element.97), channel_id=1, source_target_pairs={{0,4},{4,0},{8,12},{12,8},{1,5},{5,1},{9,13},{13,9},{2,6},{6,2},{1... | collective-permute-start | bytes 786440 | tf_op jit(solution)/shard_map/ppermute | solution.py:444
  166.1 0.9 copy-start.22
  167.3 1.0 copy-start.21
  169.5 19.5 %copy-start.7 = (bf16[256,4,512]{2,1,0:T(4,128)(2,1)}, bf16[256,4,512]{2,1,0:T(4,128)(2,1)S(1)}, u32[]{:S(2)}) copy-start(bf16[256,4,512]{2,1,0:T(4,128)(2,1)S(1)} %copy_dynamic-update-slice_fusion.4) | copy-start | bytes 3145732
  188.9 1.0 copy-start.8
